TPU v7x, 256 devices: a whole 4x4x8 slice. The times are simulated.
256 devices in a mesh: rep: 2 (over z_hi), zero: 128 (over z_lo, y, x, core).
Axes of the slice: x: 4, y: 4, z: 8 (z_hi: 2, z_lo: 4; z = z_hi * 4 + z_lo), core: 2. Of those that a mesh axis runs over, the one named last changes fastest.
Arguments:
- acts: bfloat16 [256, 8192], P('rep', 'zero'), may hold values from -6 to 6
- grads_out: bfloat16 [256, 8192], P('rep', 'zero'), may hold values from -12 to 12
- act_inverse: bfloat16 [8192, 8192], P('zero'), as said below
- grad_inverse: bfloat16 [8192, 8192], P('zero'), as said below
Outputs:
- precond: float32 [8192, 8192], P('zero')
Inputs may be any that keep to these rules, and one draw needn't show every extreme that they name: act_inverse is symmetric. grad_inverse is symmetric.
All inputs are finite; a program needn't handle non-finite values.
Results may differ from a plain program's by a relative error of at most 0.004.
Values may be sent and summed in bfloat16 or wider, within the bound.
No kernel may reach another device: no remote copies, remote signals or barrier semaphores. Data moves between devices by JAX's collectives and lax.ppermute only.
A program may use at most 64 MiB of HBM per device.

v0:
```python
import jax
import jax.numpy as jnp
from jax import lax
from jax.sharding import Mesh
from jax.sharding import PartitionSpec as P

ZERO = ("zero_0", "zero_1", "zero_2", "zero_3")


def padded_to(lines, size):
    spare = -len(lines) % size
    return jnp.pad(lines, [(0, spare)] + [(0, 0)] * (lines.ndim - 1))


def sent_to_all(x, axis):
    copies = jnp.broadcast_to(x, (lax.axis_size(axis), *x.shape))
    return lax.all_to_all(copies, axis, split_axis=0, concat_axis=0, tiled=True)


def in_order(blocks, dim):
    blocks = jnp.moveaxis(blocks, 0, dim)
    shape = blocks.shape
    return blocks.reshape(*shape[:dim], shape[dim] * shape[dim + 1], *shape[dim + 2 :])


def gather_axes(x, axes, dim):
    far, near = axes
    leading = sent_to_all(x, far)
    blocks = jnp.swapaxes(sent_to_all(leading, near), 0, 1)
    return in_order(blocks.reshape(-1, *x.shape), dim)


def cut_along(x, dim, size):
    shape = x.shape
    blocks = x.reshape(*shape[:dim], size, shape[dim] // size, *shape[dim + 1 :])
    return jnp.moveaxis(blocks, dim, 0)


def sum_at_owner(x, axis, dim):
    size = lax.axis_size(axis)
    blocks = lax.all_to_all(cut_along(x, dim, size), axis, 0, 0, tiled=True)
    return jnp.sum(blocks, axis=0)


def sum_by_axis(x, axes, dim):
    far, near = axes
    blocks = cut_along(x, dim, lax.axis_size(far))
    nearer = sum_at_owner(blocks, near, dim + 1)
    arrived = lax.all_to_all(nearer, far, split_axis=0, concat_axis=0, tiled=True)
    return arrived.sum(axis=0)


def sum_by_parts(x, axes):
    lines = x.reshape(-1, x.shape[-1])
    padded = padded_to(lines, lax.axis_size(axes[0]) * lax.axis_size(axes[1]))
    whole = gather_axes(sum_by_axis(padded, axes, 0), axes, 0)
    return lax.slice_in_dim(whole, 0, len(lines)).reshape(x.shape)


def taken_together(x, axis):
    return sent_to_all(x, axis).sum(axis=0)


def on_device(acts, grads_out, act_inverse, grad_inverse):
    tok_group = acts.shape[0]
    total_tokens = tok_group * lax.axis_size("rep")
    term = jnp.dot(acts, act_inverse, preferred_element_type=jnp.float32)
    act_pre = sum_by_parts(term, (("zero_0", "zero_1", "zero_2"), "zero_3")).astype(jnp.bfloat16)
    grad_pre_t = lax.dot_general(
        grad_inverse,
        gather_axes(grads_out, (("zero_0", "zero_1", "zero_2"), "zero_3"), 1),
        (((1,), (1,)), ((), ())),
        preferred_element_type=jnp.float32,
    ).astype(jnp.bfloat16)
    partial_rows = jnp.dot(grad_pre_t, act_pre, preferred_element_type=jnp.float32) / jnp.float32(
        total_tokens
    )
    return taken_together(partial_rows, "rep")


def solution(mesh):
    finer = Mesh(
        mesh.devices.reshape(mesh.shape["rep"], 4, 4, 4, 2),
        ("rep", "zero_0", "zero_1", "zero_2", "zero_3"),
    )
    return jax.shard_map(
        on_device,
        mesh=finer,
        in_specs=(P("rep", ZERO), P("rep", ZERO), P(ZERO, None), P(ZERO, None)),
        out_specs=P(ZERO, None),
        check_vma=False,
    )
```

profile of v0, /device:TPU:64, one launch (start us, length us, event | category | flops | bytes accessed | tf_op | source)
XLA Modules:
  0.0 307.9 jit_solution(14298806756484301864)
XLA Ops:
  0.0 1.2 copy-done
  1.2 3.4 %fusion = f32[128,8192]{1,0:T(8,128)} fusion(bf16[128,64]{0,1:T(8,128)(2,1)} %param.4, bf16[64,8192]{1,0:T(8,128)(2,1)S(1)} %copy-done), kind=kOutput, calls=%fused_computation.5 | convolution fusion | flops 134217728 | bytes 5259264 | tf_op jit(solution)/shard_map/dot_general | solution.py:67
  4.6 5.8 %reshape_reshape.4 = f32[64,2,1,8192]{3,1,0,2:T(2,128)} reshape(f32[128,8192]{1,0:T(8,128)} %fusion) | data formatting | bytes 8388608 | tf_op jit(solution)/shard_map/reshape;reshape | solution.py:35
  10.4 4.6 %copy.15 = f32[64,2,1,8192]{3,0,2,1:T(8,128)S(1)} copy(f32[64,2,1,8192]{3,1,0,2:T(2,128)} %reshape_reshape.4) | data formatting | bytes 8388608 | tf_op jit(solution)/shard_map/reshape;reshape | solution.py:35
  15.0 0.0 copy-start.1
  15.0 8.2 %all_to_all.38 = f32[2,64,1,8192]{3,1,2,0:T(8,128)} all-to-all(f32[2,64,1,8192]{3,1,2,0:T(8,128)S(1)} %bitcast.23), channel_id=1, replica_groups=mesh['rep'=2,'zero_0'=4,'zero_1'=4,'zero_2'=4,'zero_3'=2] {'zero_3'}, dimensions={0} | all-to-all | bytes 8388608 | tf_op jit(solution)/shard_map/all_to_all | solution.py:41
  23.2 1.3 broadcast_in_dim.15
  24.5 11.5 %all-to-all-start = ((bf16[64,128,64]{1,2,0:T(8,128)(2,1)}), bf16[64,128,64]{1,2,0:T(8,128)(2,1)}, u32[]{:S(2)}, u32[]{:S(2)}) async-start(bf16[64,128,64]{1,2,0:T(8,128)(2,1)} %broadcast_in_dim.15), calls=%async_computation | async-start | bytes 2097152 | tf_op jit(solution)/shard_map/all_to_all | solution.py:17
  36.0 2.7 reduce_sum.29
  38.7 3.7 %reduce_sum.30 = f32[64,1,8192]{2,1,0:T(1,128)} reshape(f32[64,8192]{1,0:T(8,128)S(1)} %reduce_sum.29) | data formatting | bytes 4194304 | tf_op jit(solution)/shard_map/reduce_sum | solution.py:42
  42.4 21.3 %all-to-all-done = bf16[64,128,64]{1,2,0:T(8,128)(2,1)} async-done(((bf16[64,128,64]{1,2,0:T(8,128)(2,1)}), bf16[64,128,64]{1,2,0:T(8,128)(2,1)}, u32[]{:S(2)}, u32[]{:S(2)}) %all-to-all-start) | async-done | bytes 1048608 | tf_op jit(solution)/shard_map/all_to_all | solution.py:17
  63.6 55.4 %all_to_all.39 = f32[64,1,8192]{2,1,0:T(1,128)} all-to-all(f32[64,1,8192]{2,1,0:T(1,128)} %reduce_sum.30), channel_id=1, replica_groups=mesh['rep'=2,'zero_0'=4,'zero_1'=4,'zero_2'=4,'zero_3'=2] {'zero_0','zer..., dimensions={0} | all-to-all | bytes 4194304 | tf_op jit(solution)/shard_map/all_to_all | solution.py:49
  119.1 3.2 %broadcast_in_dim.16 = bf16[2,64,128,64]{2,3,1,0:T(8,128)(2,1)} broadcast(bf16[64,128,64]{1,2,0:T(8,128)(2,1)} %all-to-all-done), dimensions={1,2,3} | broadcast | bytes 3145728 | tf_op jit(solution)/shard_map/broadcast_in_dim | solution.py:16
  122.2 3.9 %all-to-all-start.1 = ((bf16[2,64,128,64]{2,3,1,0:T(8,128)(2,1)}), bf16[2,64,128,64]{2,3,1,0:T(8,128)(2,1)S(1)}, u32[]{:S(2)}, u32[]{:S(2)}) async-start(bf16[2,64,128,64]{2,3,1,0:T(8,128)(2,1)} %broadcast_in_dim.16), calls=%async_computation.1 | async-start | bytes 4194304 | tf_op jit(solution)/shard_map/all_to_all | solution.py:17
  126.2 3.4 %reduce_sum.31 = bf16[8192]{0:T(1024)(128)(2,1)S(1)} reduce(f32[64,1,8192]{2,1,0:T(1,128)} %all_to_all.39, f32[]{:T(128)} %constant.2.clone.1), dimensions={0,1}, to_apply=%region_1.2 | reduce | flops 516096 | bytes 2113540 | tf_op jit(solution)/shard_map/reduce_sum | solution.py:50
  129.6 3.3 %broadcast_in_dim.17 = bf16[64,1,8192]{2,1,0:T(2,128)(2,1)} broadcast(bf16[8192]{0:T(1024)(128)(2,1)S(1)} %reduce_sum.31), dimensions={2} | broadcast | bytes 1064960 | tf_op jit(solution)/shard_map/broadcast_in_dim | solution.py:16
  132.9 0.5 broadcast.4
  133.4 9.4 %reduce.2 = bf16[64,8192]{1,0:T(8,128)(2,1)} reduce(bf16[64,1,8192]{2,1,0:T(2,128)(2,1)} %broadcast_in_dim.17, bf16[]{:T(256)} %broadcast.4), dimensions={1}, to_apply=%broadcast_in_dim.17.reduce_sub_computation | reduce | bytes 2097154 | tf_op jit(solution)/shard_map/broadcast_in_dim | solution.py:16
  142.8 2.6 reshape.14
  145.4 6.7 %all-to-all-start.4 = ((bf16[64,2,4096]{2,1,0:T(2,128)(2,1)}), bf16[64,2,4096]{2,1,0:T(2,128)(2,1)}, u32[]{:S(2)}, u32[]{:S(2)}) async-start(bf16[64,2,4096]{2,1,0:T(2,128)(2,1)} %reshape.14), calls=%async_computation.4 | async-start | bytes 2097152 | tf_op jit(solution)/shard_map/all_to_all | solution.py:17
  152.1 1.6 copy.9
  153.7 26.4 %all-to-all-done.4 = bf16[64,2,4096]{2,1,0:T(2,128)(2,1)} async-done(((bf16[64,2,4096]{2,1,0:T(2,128)(2,1)}), bf16[64,2,4096]{2,1,0:T(2,128)(2,1)}, u32[]{:S(2)}, u32[]{:S(2)}) %all-to-all-start.4) | async-done | bytes 1048608 | tf_op jit(solution)/shard_map/all_to_all | solution.py:17
  180.1 6.5 %reshape.15 = bf16[64,1,8192]{2,1,0:T(2,128)(2,1)S(1)} reshape(bf16[64,2,4096]{2,1,0:T(2,128)(2,1)} %all-to-all-done.4) | data formatting | bytes 2097152
  186.6 1.1 copy.16
  187.7 0.2 broadcast_in_dim.18
  188.0 5.4 %all_to_all.40 = bf16[2,64,1,8192]{3,1,2,0:T(8,128)(2,1)S(1)} all-to-all(bf16[2,64,1,8192]{3,1,2,0:T(8,128)(2,1)S(1)} %broadcast_in_dim.18), channel_id=1, replica_groups=mesh['rep'=2,'zero_0'=4,'zero_1'=4,'zero_2'=4,'zero_3'=2] {'zero_3'}, dimensions={0} | all-to-all | bytes 4194304 | tf_op jit(solution)/shard_map/all_to_all | solution.py:17
  193.4 2.2 copy.11
  195.6 2.2 convert_element_type.15
  197.8 3.4 %convolution_multiply_fusion = f32[64,8192]{1,0:T(8,128)S(1)} fusion(bf16[128,8192]{1,0:T(8,128)(2,1)} %convert_element_type.15, bf16[64,8192]{1,0:T(8,128)(2,1)} %param.7, bf16[128,8192]{0,1:T(8,128)(2,1)} %bitcast.24), kind=kOutput, calls=%fused_computation | convolution fusion | flops 268967936 | bytes 7340032 | tf_op jit(solution)/shard_map/dot_general | solution.py:75
  201.2 0.4 broadcast_in_dim.19
  201.6 102.2 %all_to_all.41 = f32[2,64,8192]{2,1,0:T(8,128)} all-to-all(f32[2,64,8192]{2,1,0:T(8,128)S(1)} %broadcast_in_dim.19), channel_id=1, replica_groups=mesh['rep'=2,'zero_0'=4,'zero_1'=4,'zero_2'=4,'zero_3'=2] {'rep'}, dimensions={0} | all-to-all | bytes 8388608 | tf_op jit(solution)/shard_map/all_to_all | solution.py:17
  303.9 4.0 %reduce_sum.32 = f32[64,8192]{1,0:T(8,128)} reduce(f32[2,64,8192]{2,1,0:T(8,128)} %all_to_all.41, f32[]{:T(128)} %constant.2.clone.1), dimensions={0}, to_apply=%region_2.3 | reduce | flops 524288 | bytes 6291460 | tf_op jit(solution)/shard_map/reduce_sum | solution.py:61
  (3 shorter events, 0.0 us)
Async XLA Ops:
  0.0 1.2 copy-start
  15.0 8.2 %copy-start.1 = (bf16[128,64]{0,1:T(8,128)(2,1)S(1)}, bf16[128,64]{0,1:T(8,128)(2,1)}, u32[]{:S(2)}) copy-start(bf16[128,64]{0,1:T(8,128)(2,1)} %param.5) | copy-start | bytes 49156
  24.5 39.1 %all-to-all-start = ((bf16[64,128,64]{1,2,0:T(8,128)(2,1)}), bf16[64,128,64]{1,2,0:T(8,128)(2,1)}, u32[]{:S(2)}, u32[]{:S(2)}) async-start(bf16[64,128,64]{1,2,0:T(8,128)(2,1)} %broadcast_in_dim.15), calls=%async_computation | async-start | bytes 2097152 | tf_op jit(solution)/shard_map/all_to_all | solution.py:17
  122.2 23.2 %all-to-all-start.1 = ((bf16[2,64,128,64]{2,3,1,0:T(8,128)(2,1)}), bf16[2,64,128,64]{2,3,1,0:T(8,128)(2,1)S(1)}, u32[]{:S(2)}, u32[]{:S(2)}) async-start(bf16[2,64,128,64]{2,3,1,0:T(8,128)(2,1)} %broadcast_in_dim.16), calls=%async_computation.1 | async-start | bytes 4194304 | tf_op jit(solution)/shard_map/all_to_all | solution.py:17
  145.4 34.7 %all-to-all-start.4 = ((bf16[64,2,4096]{2,1,0:T(2,128)(2,1)}), bf16[64,2,4096]{2,1,0:T(2,128)(2,1)}, u32[]{:S(2)}, u32[]{:S(2)}) async-start(bf16[64,2,4096]{2,1,0:T(2,128)(2,1)} %reshape.14), calls=%async_computation.4 | async-start | bytes 2097152 | tf_op jit(solution)/shard_map/all_to_all | solution.py:17
where the time goes:
time: 309 us; the launch traced here: 308 us
  blocking collectives  171 us (55%)
  waiting for transfers between devices  47.7 us (15%)
  local copies, waits for them, and re-layouts  40.4 us (13%)
  starting transfers between devices  22.1 us (7%)
  other arithmetic  19.5 us (6%)
  matrix products  6.81 us (2%)
    all_to_all x2, blocking collectives, sent_to_all(): return lax.all_to_all(copies, axis, split_axis=0, concat_axis=0, tiled=True)  108 us
    all_to_all x1, blocking collectives, sum_by_axis(): lax.all_to_all(nearer, far, split_axis=0, concat_axis=0, tiled=True)  55.4 us
    all_to_all x3, waiting for transfers between devices, sent_to_all(): return lax.all_to_all(copies, axis, split_axis=0, concat_axis=0, tiled=True)  47.7 us
    all_to_all x3, starting transfers between devices, sent_to_all(): return lax.all_to_all(copies, axis, split_axis=0, concat_axis=0, tiled=True)  22.1 us
    unnamed x7, local copies, waits for them, and re-layouts  11.5 us
    another operation x2, local copies, waits for them, and re-layouts, cut_along(): blocks = x.reshape(*shape[:dim], size, shape[dim] // size, *shape[dim + 1:])  10.4 us
    broadcast_in_dim x1, other arithmetic, sent_to_all(): copies = jnp.broadcast_to(x, (lax.axis_size(axis), *x.shape))  9.4 us
    broadcast_in_dim x6, local copies, waits for them, and re-layouts, sent_to_all(): copies = jnp.broadcast_to(x, (lax.axis_size(axis), *x.shape))  8.88 us
  transfers between devices with their start and end apart: 3, of which 2 were waited for; matrix products, arithmetic and copies ran while one was open for 9% of the time, Pallas kernels for 0%

commit v1 on v0

v1 whole, which is shorter than its diff:
```python
import functools

import jax
import jax.numpy as jnp
from jax import lax
from jax.experimental import pallas as pl
from jax.experimental.pallas import tpu as pltpu
from jax.sharding import Mesh
from jax.sharding import PartitionSpec as P

AXES = ("rep", "zl", "y", "x", "c")
SIZES = (2, 4, 4, 4, 2)
ZERO = AXES[1:]
TOKENS = 256


def places():
    for r in range(2):
        for zl in range(4):
            for y in range(4):
                for x in range(4):
                    for c in range(2):
                        yield r, zl, y, x, c


def rank(r, zl, y, x, c):
    return (((r * 4 + zl % 4) * 4 + y % 4) * 4 + x % 4) * 2 + c


def send(value, target):
    pairs = [(rank(*place), rank(*target(*place))) for place in places()]
    return lax.ppermute(value, AXES, pairs)


def swap_cores(value):
    return send(value, lambda r, zl, y, x, c: (r, zl, y, x, 1 - c))


def along_line(value, k):
    return send(value, lambda r, zl, y, x, c: (r, zl + k, y, x, c))


def along_ring(value, k):
    return send(
        value,
        lambda r, zl, y, x, c: ((r * 4 + zl + k) // 4 % 2, zl + k, y, x, c),
    )


def first_turn(value, k):
    return send(
        value,
        lambda r, zl, y, x, c: (r, zl, y, x + k, c) if c else (r, zl, y + k, x, c),
    )


def second_turn(value, k):
    return send(
        value,
        lambda r, zl, y, x, c: (r, zl, y + k, x, c) if c else (r, zl, y, x + k, c),
    )


def block_of(where, core, k3, k2, kz):
    zl = lax.rem(where[0] + 4 - kz, 4)
    k_y = jnp.where(core == 0, k2, k3)
    k_x = jnp.where(core == 0, k3, k2)
    y = lax.rem(where[1] + 4 - k_y, 4)
    x = lax.rem(where[2] + 4 - k_x, 4)
    return pl.multiple_of(((zl * 4 + y) * 4 + x) * 128, 128)


def precondition(where, p0, p1, p2, p3, mine, theirs, pre):
    core = where[3]
    total = jnp.zeros((128, 128), jnp.float32)
    for k3, piece in enumerate((p0, p1, p2, p3)):
        for k2 in range(4):
            rows, cols = [], []
            for kz in range(4):
                at = block_of(where, core, k3, k2, kz)
                cols.append(piece[k2, kz])
                rows.append(
                    jnp.concatenate(
                        [mine[:, pl.ds(at, 128)], theirs[:, pl.ds(at, 128)]], axis=0
                    )
                )
            total += lax.dot_general(
                jnp.concatenate(cols, axis=1),
                jnp.concatenate(rows, axis=1),
                (((1,), (1,)), ((), ())),
                preferred_element_type=jnp.float32,
            )
    swapped = pltpu.roll(total, 64, 1)
    pre[...] = jnp.where(core == 0, total, swapped).astype(pre.dtype)


def outer(zs, where, g_own, g_other, *refs):
    pieces, out = refs[:-1], refs[-1]
    core = where[3]
    for side, grads in enumerate((g_own, g_other)):
        left = grads[...]
        held_by = core if side == 0 else 1 - core
        for k3 in range(4):
            piece = pieces[side * 4 + k3]
            for k2 in range(4):
                wide = jnp.concatenate([piece[k2, j] for j in range(4)], axis=1)
                part = lax.dot_general(
                    left,
                    wide,
                    (((1,), (0,)), ((), ())),
                    preferred_element_type=jnp.float32,
                ) * (1.0 / TOKENS)
                for j, kz in enumerate(zs):
                    at = block_of(where, held_by, k3, k2, kz)
                    block = part[:, j * 128 : (j + 1) * 128]
                    if side == 0:
                        out[:, pl.ds(at, 128)] = block
                    else:
                        out[:, pl.ds(at, 128)] += block


VMEM = pl.BlockSpec(memory_space=pltpu.VMEM)
SMEM = pl.BlockSpec(memory_space=pltpu.SMEM)
PARAMS = pltpu.CompilerParams(vmem_limit_bytes=40 * 1024 * 1024)


def on_device(acts, grads_out, act_inverse, grad_inverse):
    r, c = lax.axis_index("rep"), lax.axis_index("c")
    where = jnp.stack(
        [lax.axis_index("zl"), lax.axis_index("y"), lax.axis_index("x"), c]
    ).astype(jnp.int32)
    first = c == 0

    got = swap_cores(jnp.where(first, grads_out, acts))
    kept = jnp.where(first, acts, grads_out)
    block = jnp.concatenate(
        [jnp.where(first, kept, got), jnp.where(first, got, kept)], axis=1
    )
    theirs = swap_cores(jnp.where(first, grad_inverse, act_inverse))
    mine = jnp.where(first, act_inverse, grad_inverse)

    line = jnp.stack([block] + [along_line(block, k) for k in (1, 2, 3)])
    plane = jnp.stack([line] + [first_turn(line, k) for k in (1, 2, 3)])
    pieces = [plane] + [second_turn(plane, k) for k in (1, 2, 3)]
    pre = pl.pallas_call(
        precondition,
        out_shape=jax.ShapeDtypeStruct((128, 128), jnp.bfloat16),
        in_specs=[SMEM] + [VMEM] * 6,
        out_specs=VMEM,
        compiler_params=PARAMS,
        name="precondition",
    )(where, *pieces, mine, theirs)

    far = send(
        pre, lambda r, zl, y, x, c: (1 - r, zl, y, x, 1 - r if c else r)
    )
    near = swap_cores(pre)
    block = jnp.where(r != c, far, jnp.where(first, pre, near))
    passed = swap_cores(far)
    g_here = jnp.where(first, near, pre)
    g_there = jnp.where(r == c, far, passed)
    own_tokens = r == c
    g_own = jnp.where(own_tokens, g_here, g_there)
    g_other = jnp.where(own_tokens, g_there, g_here)
    g_own, g_other = (
        jnp.where(first, g[:, :64], g[:, 64:]).T for g in (g_own, g_other)
    )

    line = jnp.stack([block] + [along_ring(block, k) for k in (1, 7, 2)])
    plane = jnp.stack([line] + [first_turn(line, k) for k in (1, 2, 3)])
    pieces = [plane] + [second_turn(plane, k) for k in (1, 2, 3)]
    others = [swap_cores(piece) for piece in pieces]
    return pl.pallas_call(
        functools.partial(outer, (0, 1, 3, 2)),
        out_shape=jax.ShapeDtypeStruct((64, 8192), jnp.float32),
        in_specs=[SMEM] + [VMEM] * 10,
        out_specs=VMEM,
        compiler_params=PARAMS,
        name="outer",
    )(where, g_own, g_other, *pieces, *others)


def solution(mesh):
    finer = Mesh(mesh.devices.reshape(SIZES), AXES)
    return jax.shard_map(
        on_device,
        mesh=finer,
        in_specs=(P("rep", ZERO), P("rep", ZERO), P(ZERO, None), P(ZERO, None)),
        out_specs=P(ZERO, None),
        check_vma=False,
    )
```

time: 309 us -> 96.5 us (0.31)
  the two profiles are of different devices: /device:TPU:64 before, /device:TPU:1 now
where the time goes in v1:
time: 96.5 us; the launch traced here: 96.3 us
  waiting for transfers between devices  43.7 us (45%)
  starting transfers between devices  41.5 us (43%)
  Pallas kernels  5.96 us (6%)
  other arithmetic  3.12 us (3%)
  local copies, waits for them, and re-layouts  1.84 us (2%)
    ppermute x27, waiting for transfers between devices, send(): return lax.ppermute(value, AXES, pairs)  43.7 us
    ppermute x27, starting transfers between devices, send(): return lax.ppermute(value, AXES, pairs)  41.5 us
    pallas_call x1, Pallas kernels, on_device(): pl.pallas_call(functools.partial(outer, (0, 1, 3, 2)), out_shape=jax.Shap...  3.84 us
    select_n x1, other arithmetic, on_device(): theirs = swap_cores(jnp.where(first, grad_inverse, act_inverse))  2.65 us
    pallas_call x1, Pallas kernels, on_device(): pl.pallas_call(precondition, out_shape=jax.ShapeDtypeStruct((128, 128), j...  2.12 us
  transfers between devices with their start and end apart: 27, of which 15 were waited for; matrix products, arithmetic and copies ran while one was open for 3% of the time, Pallas kernels for 0%

profile of v1, /device:TPU:1, one launch (start us, length us, event | category | flops | bytes accessed | tf_op | source)
XLA Modules:
  0.0 96.3 jit_solution(11791694857295132295)
XLA Ops:
  0.0 0.8 copy.5
  0.8 0.8 copy.6
  1.7 3.3 %collective-permute-start = (bf16[128,64]{1,0:T(8,128)(2,1)S(1)}, bf16[128,64]{1,0:T(8,128)(2,1)S(1)}, u32[]{:S(2)}, u32[]{:S(2)}) collective-permute-start(bf16[128,64]{1,0:T(8,128)(2,1)S(1)} %broadcast_select_fusion.8), channel_id=1, source_target_pairs={{0,1},{1,0},{2,3},{3,2},{4,5},{5,4},{6,7},{7,6},{8,9},{9,8},{10,11... | collective-permute-start | bytes 49160 | tf_op jit(solution)/shard_map/ppermute | solution.py:32
  5.0 2.6 %broadcast_select_fusion = (bf16[64,8192]{1,0:T(8,128)(2,1)}, bf16[64,8192]{1,0:T(8,128)(2,1)S(1)}) fusion(bf16[64,8192]{1,0:T(8,128)(2,1)} %param.7, bf16[64,8192]{1,0:T(8,128)(2,1)} %param.6, pred[]{:T(512)S(6)} %eq.7), kind=kLoop, calls=%fused_computation | loop fusion | flops 1048576 | bytes 4194305 | tf_op jit(solution)/shard_map/jit(_where)/select_n | solution.py:139
  7.8 2.7 %collective-permute-start.3 = (bf16[128,128]{1,0:T(8,128)(2,1)S(1)}, bf16[128,128]{1,0:T(8,128)(2,1)S(1)}, u32[]{:S(2)}, u32[]{:S(2)}) collective-permute-start(bf16[128,128]{1,0:T(8,128)(2,1)S(1)} %pad_maximum_fusion.4), channel_id=1, source_target_pairs={{0,96},{1,97},{2,98},{3,99},{4,100},{5,101},{6,102},{7,103},{8,104... | collective-permute-start | bytes 98312 | tf_op jit(solution)/shard_map/ppermute | solution.py:32
  11.5 2.8 %collective-permute-done.2 = bf16[128,128]{1,0:T(8,128)(2,1)S(1)} collective-permute-done((bf16[128,128]{1,0:T(8,128)(2,1)S(1)}, bf16[128,128]{1,0:T(8,128)(2,1)S(1)}, u32[]{:S(2)}, u32[]{:S(2)}) %collective-permute-start.2) | collective-permute-done | bytes 32800 | tf_op jit(solution)/shard_map/ppermute | solution.py:32
  14.3 0.7 collective-permute-done.1
  15.1 2.8 %collective-permute-start.5 = (bf16[4,128,128]{2,1,0:T(8,128)(2,1)S(1)}, bf16[4,128,128]{2,1,0:T(8,128)(2,1)S(1)}, u32[]{:S(2)}, u32[]{:S(2)}) collective-permute-start(bf16[4,128,128]{2,1,0:T(8,128)(2,1)S(1)} %get-tuple-element.12), channel_id=1, source_target_pairs={{0,16},{1,5},{2,18},{3,7},{4,20},{5,1},{6,22},{7,3},{8,24},{9,13},... | collective-permute-start | bytes 393224 | tf_op jit(solution)/shard_map/ppermute | solution.py:32
  18.2 2.4 %collective-permute-start.6 = (bf16[4,128,128]{2,1,0:T(8,128)(2,1)S(1)}, bf16[4,128,128]{2,1,0:T(8,128)(2,1)S(1)}, u32[]{:S(2)}, u32[]{:S(2)}) collective-permute-start(bf16[4,128,128]{2,1,0:T(8,128)(2,1)S(1)} %get-tuple-element.12), channel_id=1, source_target_pairs={{0,24},{1,7},{2,26},{3,1},{4,28},{5,3},{6,30},{7,5},{8,0},{9,15},{... | collective-permute-start | bytes 393224 | tf_op jit(solution)/shard_map/ppermute | solution.py:32
  20.6 2.6 %collective-permute-done.4 = bf16[4,128,128]{2,1,0:T(8,128)(2,1)S(1)} collective-permute-done((bf16[4,128,128]{2,1,0:T(8,128)(2,1)S(1)}, bf16[4,128,128]{2,1,0:T(8,128)(2,1)S(1)}, u32[]{:S(2)}, u32[]{:S(2)}) %collective-permute-start.4) | collective-permute-done | bytes 131104 | tf_op jit(solution)/shard_map/ppermute | solution.py:32
  23.2 2.8 %collective-permute-start.9 = (bf16[4,4,128,128]{3,2,1,0:T(8,128)(2,1)S(1)}, bf16[4,4,128,128]{3,2,1,0:T(8,128)(2,1)S(1)}, u32[]{:S(2)}, u32[]{:S(2)}) collective-permute-start(bf16[4,4,128,128]{3,2,1,0:T(8,128)(2,1)S(1)} %pad_maximum_fusion.p0), channel_id=1, source_target_pairs={{0,6},{1,25},{2,0},{3,27},{4,2},{5,29},{6,4},{7,31},{8,14},{9,1},{... | collective-permute-start | bytes 1572872 | tf_op jit(solution)/shard_map/ppermute | solution.py:32
  27.1 10.7 %collective-permute-done.9.p3 = bf16[4,4,128,128]{3,2,1,0:T(8,128)(2,1)S(1)} collective-permute-done((bf16[4,4,128,128]{3,2,1,0:T(8,128)(2,1)S(1)}, bf16[4,4,128,128]{3,2,1,0:T(8,128)(2,1)S(1)}, u32[]{:S(2)}, u32[]{:S(2)}) %collective-permute-start.9) | collective-permute-done | bytes 524320 | tf_op jit(solution)/shard_map/ppermute | solution.py:32
  37.8 3.8 %collective-permute-done.7.p1 = bf16[4,4,128,128]{3,2,1,0:T(8,128)(2,1)} collective-permute-done((bf16[4,4,128,128]{3,2,1,0:T(8,128)(2,1)S(1)}, bf16[4,4,128,128]{3,2,1,0:T(8,128)(2,1)}, u32[]{:S(2)}, u32[]{:S(2)}) %collective-permute-start.7) | collective-permute-done | bytes 524320 | tf_op jit(solution)/shard_map/ppermute | solution.py:32
  41.6 2.1 %precondition.1 = bf16[128,128]{1,0:T(8,128)(2,1)S(1)} custom-call(s32[4]{0:T(128)S(1)} %pad_add_fusion.where, bf16[4,4,128,128]{3,2,1,0:T(8,128)(2,1)S(1)} %pad_maximum_fusion.p0, bf16[4,4,128,128]{3,2,1,0:T(8,128)(2,1)} %collective-permute-done.7.p1, bf16[4,4,128,128]{3,2,1,0:T(8,128)(2,1)} %collective-permute-done.8.p2, ...), custom_call_target="tpu_custom_call" | custom-call | tf_op jit(solution)/shard_map/precondition/pallas_call | solution.py:145
  43.7 4.6 %collective-permute-start.12 = (bf16[128,128]{1,0:T(8,128)(2,1)S(1)}, bf16[128,128]{1,0:T(8,128)(2,1)S(1)}, u32[]{:S(2)}, u32[]{:S(2)}) collective-permute-start(bf16[128,128]{1,0:T(8,128)(2,1)S(1)} %precondition.1), channel_id=1, source_target_pairs={{0,128},{1,129},{2,130},{3,131},{4,132},{5,133},{6,134},{7,135},{8... | collective-permute-start | bytes 98312 | tf_op jit(solution)/shard_map/ppermute | solution.py:32
  48.3 4.7 %collective-permute-start.11 = (bf16[128,128]{1,0:T(8,128)(2,1)S(1)}, bf16[128,128]{1,0:T(8,128)(2,1)S(1)}, u32[]{:S(2)}, u32[]{:S(2)}) collective-permute-start(bf16[128,128]{1,0:T(8,128)(2,1)S(1)} %precondition.1), channel_id=1, source_target_pairs={{0,1},{1,0},{2,3},{3,2},{4,5},{5,4},{6,7},{7,6},{8,9},{9,8},{10,11... | collective-permute-start | bytes 98312 | tf_op jit(solution)/shard_map/ppermute | solution.py:32
  53.0 1.5 %collective-permute-done.12 = bf16[128,128]{1,0:T(8,128)(2,1)S(1)} collective-permute-done((bf16[128,128]{1,0:T(8,128)(2,1)S(1)}, bf16[128,128]{1,0:T(8,128)(2,1)S(1)}, u32[]{:S(2)}, u32[]{:S(2)}) %collective-permute-start.12) | collective-permute-done | bytes 32800 | tf_op jit(solution)/shard_map/ppermute | solution.py:32
  55.3 0.9 collective-permute-done.13
  56.1 0.9 collective-permute-start.16
  57.0 1.6 %collective-permute-start.15 = (bf16[128,128]{1,0:T(8,128)(2,1)S(1)}, bf16[128,128]{1,0:T(8,128)(2,1)S(1)}, u32[]{:S(2)}, u32[]{:S(2)}) collective-permute-start(bf16[128,128]{1,0:T(8,128)(2,1)S(1)} %get-tuple-element.13), channel_id=1, source_target_pairs={{0,224},{1,225},{2,226},{3,227},{4,228},{5,229},{6,230},{7,231},{8... | collective-permute-start | bytes 98312 | tf_op jit(solution)/shard_map/ppermute | solution.py:32
  58.7 2.4 %collective-permute-done.16 = bf16[128,128]{1,0:T(8,128)(2,1)S(1)} collective-permute-done((bf16[128,128]{1,0:T(8,128)(2,1)S(1)}, bf16[128,128]{1,0:T(8,128)(2,1)S(1)}, u32[]{:S(2)}, u32[]{:S(2)}) %collective-permute-start.16) | collective-permute-done | bytes 32800 | tf_op jit(solution)/shard_map/ppermute | solution.py:32
  61.1 1.5 %collective-permute-done.14 = bf16[128,128]{1,0:T(8,128)(2,1)S(1)} collective-permute-done((bf16[128,128]{1,0:T(8,128)(2,1)S(1)}, bf16[128,128]{1,0:T(8,128)(2,1)S(1)}, u32[]{:S(2)}, u32[]{:S(2)}) %collective-permute-start.14) | collective-permute-done | bytes 32800 | tf_op jit(solution)/shard_map/ppermute | solution.py:32
  63.7 2.3 %collective-permute-start.19 = (bf16[4,128,128]{2,1,0:T(8,128)(2,1)S(1)}, bf16[4,128,128]{2,1,0:T(8,128)(2,1)S(1)}, u32[]{:S(2)}, u32[]{:S(2)}) collective-permute-start(bf16[4,128,128]{2,1,0:T(8,128)(2,1)S(1)} %get-tuple-element.8), channel_id=1, source_target_pairs={{0,24},{1,7},{2,26},{3,1},{4,28},{5,3},{6,30},{7,5},{8,0},{9,15},{... | collective-permute-start | bytes 393224 | tf_op jit(solution)/shard_map/ppermute | solution.py:32
  66.0 2.2 %collective-permute-done.18 = bf16[4,128,128]{2,1,0:T(8,128)(2,1)S(1)} collective-permute-done((bf16[4,128,128]{2,1,0:T(8,128)(2,1)S(1)}, bf16[4,128,128]{2,1,0:T(8,128)(2,1)S(1)}, u32[]{:S(2)}, u32[]{:S(2)}) %collective-permute-start.18) | collective-permute-done | bytes 131104 | tf_op jit(solution)/shard_map/ppermute | solution.py:32
  68.2 1.6 %collective-permute-done.17 = bf16[4,128,128]{2,1,0:T(8,128)(2,1)S(1)} collective-permute-done((bf16[4,128,128]{2,1,0:T(8,128)(2,1)S(1)}, bf16[4,128,128]{2,1,0:T(8,128)(2,1)S(1)}, u32[]{:S(2)}, u32[]{:S(2)}) %collective-permute-start.17) | collective-permute-done | bytes 131104 | tf_op jit(solution)/shard_map/ppermute | solution.py:32
  69.8 3.0 %collective-permute-start.22 = (bf16[4,4,128,128]{3,2,1,0:T(8,128)(2,1)S(1)}, bf16[4,4,128,128]{3,2,1,0:T(8,128)(2,1)S(1)}, u32[]{:S(2)}, u32[]{:S(2)}) collective-permute-start(bf16[4,4,128,128]{3,2,1,0:T(8,128)(2,1)S(1)} %pad_maximum_fusion.1.refs_0_), channel_id=1, source_target_pairs={{0,6},{1,25},{2,0},{3,27},{4,2},{5,29},{6,4},{7,31},{8,14},{9,1},{... | collective-permute-start | bytes 1572872 | tf_op jit(solution)/shard_map/ppermute | solution.py:32
  73.6 2.9 %collective-permute-start.23 = (bf16[4,4,128,128]{3,2,1,0:T(8,128)(2,1)S(1)}, bf16[4,4,128,128]{3,2,1,0:T(8,128)(2,1)S(1)}, u32[]{:S(2)}, u32[]{:S(2)}) collective-permute-start(bf16[4,4,128,128]{3,2,1,0:T(8,128)(2,1)S(1)} %pad_maximum_fusion.1.refs_0_), channel_id=1, source_target_pairs={{0,1},{1,0},{2,3},{3,2},{4,5},{5,4},{6,7},{7,6},{8,9},{9,8},{10,11... | collective-permute-start | bytes 1572872 | tf_op jit(solution)/shard_map/ppermute | solution.py:32
  76.5 8.1 %collective-permute-done.22.refs_3_ = bf16[4,4,128,128]{3,2,1,0:T(8,128)(2,1)S(1)} collective-permute-done((bf16[4,4,128,128]{3,2,1,0:T(8,128)(2,1)S(1)}, bf16[4,4,128,128]{3,2,1,0:T(8,128)(2,1)S(1)}, u32[]{:S(2)}, u32[]{:S(2)}) %collective-permute-start.22) | collective-permute-done | bytes 524320 | tf_op jit(solution)/shard_map/ppermute | solution.py:32
  85.2 2.8 %collective-permute-done.20.refs_1_ = bf16[4,4,128,128]{3,2,1,0:T(8,128)(2,1)S(1)} collective-permute-done((bf16[4,4,128,128]{3,2,1,0:T(8,128)(2,1)S(1)}, bf16[4,4,128,128]{3,2,1,0:T(8,128)(2,1)S(1)}, u32[]{:S(2)}, u32[]{:S(2)}) %collective-permute-start.20) | collective-permute-done | bytes 524320 | tf_op jit(solution)/shard_map/ppermute | solution.py:32
  88.0 2.7 %collective-permute-start.24 = (bf16[4,4,128,128]{3,2,1,0:T(8,128)(2,1)S(1)}, bf16[4,4,128,128]{3,2,1,0:T(8,128)(2,1)}, u32[]{:S(2)}, u32[]{:S(2)}) collective-permute-start(bf16[4,4,128,128]{3,2,1,0:T(8,128)(2,1)S(1)} %collective-permute-done.20.refs_1_), channel_id=1, source_target_pairs={{0,1},{1,0},{2,3},{3,2},{4,5},{5,4},{6,7},{7,6},{8,9},{9,8},{10,11... | collective-permute-start | bytes 1572872 | tf_op jit(solution)/shard_map/ppermute | solution.py:32
  91.1 1.4 %collective-permute-done.24.refs_5_ = bf16[4,4,128,128]{3,2,1,0:T(8,128)(2,1)} collective-permute-done((bf16[4,4,128,128]{3,2,1,0:T(8,128)(2,1)S(1)}, bf16[4,4,128,128]{3,2,1,0:T(8,128)(2,1)}, u32[]{:S(2)}, u32[]{:S(2)}) %collective-permute-start.24) | collective-permute-done | bytes 524320 | tf_op jit(solution)/shard_map/ppermute | solution.py:32
  92.4 3.8 %outer.1 = f32[64,8192]{1,0:T(8,128)} custom-call(s32[4]{0:T(128)S(1)} %pad_add_fusion.where, bf16[64,128]{1,0:T(8,128)(2,1)S(1)} %copy.9.g_own, bf16[64,128]{1,0:T(8,128)(2,1)S(1)} %copy.10.g_other, bf16[4,4,128,128]{3,2,1,0:T(8,128)(2,1)S(1)} %pad_maximum_fusion.1.refs_0_, bf16[4,4,128,128]{3,2,1,0:T(8,128)(2,1)S(1)} %collective-permute-done.20.refs_1_, ...), custom_call_target="tpu_custom_call" | custom-call | tf_op jit(solution)/shard_map/outer/pallas_call | solution.py:173
  (39 shorter events, 6.0 us)
Async XLA Ops:
  1.7 6.0 %collective-permute-start = (bf16[128,64]{1,0:T(8,128)(2,1)S(1)}, bf16[128,64]{1,0:T(8,128)(2,1)S(1)}, u32[]{:S(2)}, u32[]{:S(2)}) collective-permute-start(bf16[128,64]{1,0:T(8,128)(2,1)S(1)} %broadcast_select_fusion.8), channel_id=1, source_target_pairs={{0,1},{1,0},{2,3},{3,2},{4,5},{5,4},{6,7},{7,6},{8,9},{9,8},{10,11... | collective-permute-start | bytes 49160 | tf_op jit(solution)/shard_map/ppermute | solution.py:32
  7.7 33.9 %collective-permute-start.10 = (bf16[64,8192]{1,0:T(8,128)(2,1)}, bf16[64,8192]{1,0:T(8,128)(2,1)S(1)}, u32[]{:S(2)}, u32[]{:S(2)}) collective-permute-start(bf16[64,8192]{1,0:T(8,128)(2,1)} %get-tuple-element.5), channel_id=1, source_target_pairs={{0,1},{1,0},{2,3},{3,2},{4,5},{5,4},{6,7},{7,6},{8,9},{9,8},{10,11... | collective-permute-start | bytes 3145736 | tf_op jit(solution)/shard_map/ppermute | solution.py:32
  7.8 3.7 %collective-permute-start.3 = (bf16[128,128]{1,0:T(8,128)(2,1)S(1)}, bf16[128,128]{1,0:T(8,128)(2,1)S(1)}, u32[]{:S(2)}, u32[]{:S(2)}) collective-permute-start(bf16[128,128]{1,0:T(8,128)(2,1)S(1)} %pad_maximum_fusion.4), channel_id=1, source_target_pairs={{0,96},{1,97},{2,98},{3,99},{4,100},{5,101},{6,102},{7,103},{8,104... | collective-permute-start | bytes 98312 | tf_op jit(solution)/shard_map/ppermute | solution.py:32
  10.5 3.8 %collective-permute-start.2 = (bf16[128,128]{1,0:T(8,128)(2,1)S(1)}, bf16[128,128]{1,0:T(8,128)(2,1)S(1)}, u32[]{:S(2)}, u32[]{:S(2)}) collective-permute-start(bf16[128,128]{1,0:T(8,128)(2,1)S(1)} %pad_maximum_fusion.4), channel_id=1, source_target_pairs={{0,64},{1,65},{2,66},{3,67},{4,68},{5,69},{6,70},{7,71},{8,72},{9,... | collective-permute-start | bytes 98312 | tf_op jit(solution)/shard_map/ppermute | solution.py:32
  10.5 4.6 %collective-permute-start.1 = (bf16[128,128]{1,0:T(8,128)(2,1)S(1)}, bf16[128,128]{1,0:T(8,128)(2,1)S(1)}, u32[]{:S(2)}, u32[]{:S(2)}) collective-permute-start(bf16[128,128]{1,0:T(8,128)(2,1)S(1)} %pad_maximum_fusion.4), channel_id=1, source_target_pairs={{0,32},{1,33},{2,34},{3,35},{4,36},{5,37},{6,38},{7,39},{8,40},{9,... | collective-permute-start | bytes 98312 | tf_op jit(solution)/shard_map/ppermute | solution.py:32
  15.1 5.5 %collective-permute-start.5 = (bf16[4,128,128]{2,1,0:T(8,128)(2,1)S(1)}, bf16[4,128,128]{2,1,0:T(8,128)(2,1)S(1)}, u32[]{:S(2)}, u32[]{:S(2)}) collective-permute-start(bf16[4,128,128]{2,1,0:T(8,128)(2,1)S(1)} %get-tuple-element.12), channel_id=1, source_target_pairs={{0,16},{1,5},{2,18},{3,7},{4,20},{5,1},{6,22},{7,3},{8,24},{9,13},... | collective-permute-start | bytes 393224 | tf_op jit(solution)/shard_map/ppermute | solution.py:32
  17.9 5.3 %collective-permute-start.4 = (bf16[4,128,128]{2,1,0:T(8,128)(2,1)S(1)}, bf16[4,128,128]{2,1,0:T(8,128)(2,1)S(1)}, u32[]{:S(2)}, u32[]{:S(2)}) collective-permute-start(bf16[4,128,128]{2,1,0:T(8,128)(2,1)S(1)} %get-tuple-element.12), channel_id=1, source_target_pairs={{0,8},{1,3},{2,10},{3,5},{4,12},{5,7},{6,14},{7,1},{8,16},{9,11},{... | collective-permute-start | bytes 393224 | tf_op jit(solution)/shard_map/ppermute | solution.py:32
  18.2 4.9 %collective-permute-start.6 = (bf16[4,128,128]{2,1,0:T(8,128)(2,1)S(1)}, bf16[4,128,128]{2,1,0:T(8,128)(2,1)S(1)}, u32[]{:S(2)}, u32[]{:S(2)}) collective-permute-start(bf16[4,128,128]{2,1,0:T(8,128)(2,1)S(1)} %get-tuple-element.12), channel_id=1, source_target_pairs={{0,24},{1,7},{2,26},{3,1},{4,28},{5,3},{6,30},{7,5},{8,0},{9,15},{... | collective-permute-start | bytes 393224 | tf_op jit(solution)/shard_map/ppermute | solution.py:32
  23.2 14.6 %collective-permute-start.9 = (bf16[4,4,128,128]{3,2,1,0:T(8,128)(2,1)S(1)}, bf16[4,4,128,128]{3,2,1,0:T(8,128)(2,1)S(1)}, u32[]{:S(2)}, u32[]{:S(2)}) collective-permute-start(bf16[4,4,128,128]{3,2,1,0:T(8,128)(2,1)S(1)} %pad_maximum_fusion.p0), channel_id=1, source_target_pairs={{0,6},{1,25},{2,0},{3,27},{4,2},{5,29},{6,4},{7,31},{8,14},{9,1},{... | collective-permute-start | bytes 1572872 | tf_op jit(solution)/shard_map/ppermute | solution.py:32
  26.0 11.7 %collective-permute-start.8 = (bf16[4,4,128,128]{3,2,1,0:T(8,128)(2,1)S(1)}, bf16[4,4,128,128]{3,2,1,0:T(8,128)(2,1)}, u32[]{:S(2)}, u32[]{:S(2)}) collective-permute-start(bf16[4,4,128,128]{3,2,1,0:T(8,128)(2,1)S(1)} %pad_maximum_fusion.p0), channel_id=1, source_target_pairs={{0,4},{1,17},{2,6},{3,19},{4,0},{5,21},{6,2},{7,23},{8,12},{9,25},... | collective-permute-start | bytes 1572872 | tf_op jit(solution)/shard_map/ppermute | solution.py:32
  26.3 15.3 %collective-permute-start.7 = (bf16[4,4,128,128]{3,2,1,0:T(8,128)(2,1)S(1)}, bf16[4,4,128,128]{3,2,1,0:T(8,128)(2,1)}, u32[]{:S(2)}, u32[]{:S(2)}) collective-permute-start(bf16[4,4,128,128]{3,2,1,0:T(8,128)(2,1)S(1)} %pad_maximum_fusion.p0), channel_id=1, source_target_pairs={{0,2},{1,9},{2,4},{3,11},{4,6},{5,13},{6,0},{7,15},{8,10},{9,17},{... | collective-permute-start | bytes 1572872 | tf_op jit(solution)/shard_map/ppermute | solution.py:32
  43.7 10.9 %collective-permute-start.12 = (bf16[128,128]{1,0:T(8,128)(2,1)S(1)}, bf16[128,128]{1,0:T(8,128)(2,1)S(1)}, u32[]{:S(2)}, u32[]{:S(2)}) collective-permute-start(bf16[128,128]{1,0:T(8,128)(2,1)S(1)} %precondition.1), channel_id=1, source_target_pairs={{0,128},{1,129},{2,130},{3,131},{4,132},{5,133},{6,134},{7,135},{8... | collective-permute-start | bytes 98312 | tf_op jit(solution)/shard_map/ppermute | solution.py:32
  48.3 7.0 %collective-permute-start.11 = (bf16[128,128]{1,0:T(8,128)(2,1)S(1)}, bf16[128,128]{1,0:T(8,128)(2,1)S(1)}, u32[]{:S(2)}, u32[]{:S(2)}) collective-permute-start(bf16[128,128]{1,0:T(8,128)(2,1)S(1)} %precondition.1), channel_id=1, source_target_pairs={{0,1},{1,0},{2,3},{3,2},{4,5},{5,4},{6,7},{7,6},{8,9},{9,8},{10,11... | collective-permute-start | bytes 98312 | tf_op jit(solution)/shard_map/ppermute | solution.py:32
  54.5 1.6 %collective-permute-start.13 = (bf16[128,128]{1,0:T(8,128)(2,1)S(1)}, bf16[128,128]{1,0:T(8,128)(2,1)S(1)}, u32[]{:S(2)}, u32[]{:S(2)}) collective-permute-start(bf16[128,128]{1,0:T(8,128)(2,1)S(1)} %collective-permute-done.12), channel_id=1, source_target_pairs={{0,1},{1,0},{2,3},{3,2},{4,5},{5,4},{6,7},{7,6},{8,9},{9,8},{10,11... | collective-permute-start | bytes 98312 | tf_op jit(solution)/shard_map/ppermute | solution.py:32
  56.1 5.0 %collective-permute-start.16 = (bf16[128,128]{1,0:T(8,128)(2,1)S(1)}, bf16[128,128]{1,0:T(8,128)(2,1)S(1)}, u32[]{:S(2)}, u32[]{:S(2)}) collective-permute-start(bf16[128,128]{1,0:T(8,128)(2,1)S(1)} %get-tuple-element.13), channel_id=1, source_target_pairs={{0,64},{1,65},{2,66},{3,67},{4,68},{5,69},{6,70},{7,71},{8,72},{9,... | collective-permute-start | bytes 98312 | tf_op jit(solution)/shard_map/ppermute | solution.py:32
  57.0 4.1 %collective-permute-start.15 = (bf16[128,128]{1,0:T(8,128)(2,1)S(1)}, bf16[128,128]{1,0:T(8,128)(2,1)S(1)}, u32[]{:S(2)}, u32[]{:S(2)}) collective-permute-start(bf16[128,128]{1,0:T(8,128)(2,1)S(1)} %get-tuple-element.13), channel_id=1, source_target_pairs={{0,224},{1,225},{2,226},{3,227},{4,228},{5,229},{6,230},{7,231},{8... | collective-permute-start | bytes 98312 | tf_op jit(solution)/shard_map/ppermute | solution.py:32
  58.7 4.0 %collective-permute-start.14 = (bf16[128,128]{1,0:T(8,128)(2,1)S(1)}, bf16[128,128]{1,0:T(8,128)(2,1)S(1)}, u32[]{:S(2)}, u32[]{:S(2)}) collective-permute-start(bf16[128,128]{1,0:T(8,128)(2,1)S(1)} %get-tuple-element.13), channel_id=1, source_target_pairs={{0,32},{1,33},{2,34},{3,35},{4,36},{5,37},{6,38},{7,39},{8,40},{9,... | collective-permute-start | bytes 98312 | tf_op jit(solution)/shard_map/ppermute | solution.py:32
  62.7 5.5 %collective-permute-start.18 = (bf16[4,128,128]{2,1,0:T(8,128)(2,1)S(1)}, bf16[4,128,128]{2,1,0:T(8,128)(2,1)S(1)}, u32[]{:S(2)}, u32[]{:S(2)}) collective-permute-start(bf16[4,128,128]{2,1,0:T(8,128)(2,1)S(1)} %get-tuple-element.8), channel_id=1, source_target_pairs={{0,16},{1,5},{2,18},{3,7},{4,20},{5,1},{6,22},{7,3},{8,24},{9,13},... | collective-permute-start | bytes 393224 | tf_op jit(solution)/shard_map/ppermute | solution.py:32
  63.3 6.5 %collective-permute-start.17 = (bf16[4,128,128]{2,1,0:T(8,128)(2,1)S(1)}, bf16[4,128,128]{2,1,0:T(8,128)(2,1)S(1)}, u32[]{:S(2)}, u32[]{:S(2)}) collective-permute-start(bf16[4,128,128]{2,1,0:T(8,128)(2,1)S(1)} %get-tuple-element.8), channel_id=1, source_target_pairs={{0,8},{1,3},{2,10},{3,5},{4,12},{5,7},{6,14},{7,1},{8,16},{9,11},{... | collective-permute-start | bytes 393224 | tf_op jit(solution)/shard_map/ppermute | solution.py:32
  63.7 6.1 %collective-permute-start.19 = (bf16[4,128,128]{2,1,0:T(8,128)(2,1)S(1)}, bf16[4,128,128]{2,1,0:T(8,128)(2,1)S(1)}, u32[]{:S(2)}, u32[]{:S(2)}) collective-permute-start(bf16[4,128,128]{2,1,0:T(8,128)(2,1)S(1)} %get-tuple-element.8), channel_id=1, source_target_pairs={{0,24},{1,7},{2,26},{3,1},{4,28},{5,3},{6,30},{7,5},{8,0},{9,15},{... | collective-permute-start | bytes 393224 | tf_op jit(solution)/shard_map/ppermute | solution.py:32
  69.8 14.8 %collective-permute-start.22 = (bf16[4,4,128,128]{3,2,1,0:T(8,128)(2,1)S(1)}, bf16[4,4,128,128]{3,2,1,0:T(8,128)(2,1)S(1)}, u32[]{:S(2)}, u32[]{:S(2)}) collective-permute-start(bf16[4,4,128,128]{3,2,1,0:T(8,128)(2,1)S(1)} %pad_maximum_fusion.1.refs_0_), channel_id=1, source_target_pairs={{0,6},{1,25},{2,0},{3,27},{4,2},{5,29},{6,4},{7,31},{8,14},{9,1},{... | collective-permute-start | bytes 1572872 | tf_op jit(solution)/shard_map/ppermute | solution.py:32
  72.9 11.8 %collective-permute-start.21 = (bf16[4,4,128,128]{3,2,1,0:T(8,128)(2,1)S(1)}, bf16[4,4,128,128]{3,2,1,0:T(8,128)(2,1)S(1)}, u32[]{:S(2)}, u32[]{:S(2)}) collective-permute-start(bf16[4,4,128,128]{3,2,1,0:T(8,128)(2,1)S(1)} %pad_maximum_fusion.1.refs_0_), channel_id=1, source_target_pairs={{0,4},{1,17},{2,6},{3,19},{4,0},{5,21},{6,2},{7,23},{8,12},{9,25},... | collective-permute-start | bytes 1572872 | tf_op jit(solution)/shard_map/ppermute | solution.py:32
  72.9 15.2 %collective-permute-start.20 = (bf16[4,4,128,128]{3,2,1,0:T(8,128)(2,1)S(1)}, bf16[4,4,128,128]{3,2,1,0:T(8,128)(2,1)S(1)}, u32[]{:S(2)}, u32[]{:S(2)}) collective-permute-start(bf16[4,4,128,128]{3,2,1,0:T(8,128)(2,1)S(1)} %pad_maximum_fusion.1.refs_0_), channel_id=1, source_target_pairs={{0,2},{1,9},{2,4},{3,11},{4,6},{5,13},{6,0},{7,15},{8,10},{9,17},{... | collective-permute-start | bytes 1572872 | tf_op jit(solution)/shard_map/ppermute | solution.py:32
  73.6 17.5 %collective-permute-start.23 = (bf16[4,4,128,128]{3,2,1,0:T(8,128)(2,1)S(1)}, bf16[4,4,128,128]{3,2,1,0:T(8,128)(2,1)S(1)}, u32[]{:S(2)}, u32[]{:S(2)}) collective-permute-start(bf16[4,4,128,128]{3,2,1,0:T(8,128)(2,1)S(1)} %pad_maximum_fusion.1.refs_0_), channel_id=1, source_target_pairs={{0,1},{1,0},{2,3},{3,2},{4,5},{5,4},{6,7},{7,6},{8,9},{9,8},{10,11... | collective-permute-start | bytes 1572872 | tf_op jit(solution)/shard_map/ppermute | solution.py:32
  84.6 6.4 %collective-permute-start.26 = (bf16[4,4,128,128]{3,2,1,0:T(8,128)(2,1)S(1)}, bf16[4,4,128,128]{3,2,1,0:T(8,128)(2,1)S(1)}, u32[]{:S(2)}, u32[]{:S(2)}) collective-permute-start(bf16[4,4,128,128]{3,2,1,0:T(8,128)(2,1)S(1)} %collective-permute-done.22.refs_3_), channel_id=1, source_target_pairs={{0,1},{1,0},{2,3},{3,2},{4,5},{5,4},{6,7},{7,6},{8,9},{9,8},{10,11... | collective-permute-start | bytes 1572872 | tf_op jit(solution)/shard_map/ppermute | solution.py:32
  84.6 6.4 %collective-permute-start.25 = (bf16[4,4,128,128]{3,2,1,0:T(8,128)(2,1)S(1)}, bf16[4,4,128,128]{3,2,1,0:T(8,128)(2,1)}, u32[]{:S(2)}, u32[]{:S(2)}) collective-permute-start(bf16[4,4,128,128]{3,2,1,0:T(8,128)(2,1)S(1)} %collective-permute-done.21.refs_2_), channel_id=1, source_target_pairs={{0,1},{1,0},{2,3},{3,2},{4,5},{5,4},{6,7},{7,6},{8,9},{9,8},{10,11... | collective-permute-start | bytes 1572872 | tf_op jit(solution)/shard_map/ppermute | solution.py:32
  88.0 4.4 %collective-permute-start.24 = (bf16[4,4,128,128]{3,2,1,0:T(8,128)(2,1)S(1)}, bf16[4,4,128,128]{3,2,1,0:T(8,128)(2,1)}, u32[]{:S(2)}, u32[]{:S(2)}) collective-permute-start(bf16[4,4,128,128]{3,2,1,0:T(8,128)(2,1)S(1)} %collective-permute-done.20.refs_1_), channel_id=1, source_target_pairs={{0,1},{1,0},{2,3},{3,2},{4,5},{5,4},{6,7},{7,6},{8,9},{9,8},{10,11... | collective-permute-start | bytes 1572872 | tf_op jit(solution)/shard_map/ppermute | solution.py:32

commit v2 on v1

v2 whole, which is shorter than its diff:
```python
import jax
import jax.numpy as jnp
from jax import lax
from jax.experimental import pallas as pl
from jax.experimental.pallas import tpu as pltpu
from jax.sharding import Mesh
from jax.sharding import PartitionSpec as P

AXES = ("rep", "zl", "y", "x", "c")
SIZES = (2, 4, 4, 4, 2)
ZERO = AXES[1:]
TOKENS = 256


def places():
    for r in range(2):
        for zl in range(4):
            for y in range(4):
                for x in range(4):
                    for c in range(2):
                        yield r, zl, y, x, c


def rank(r, zl, y, x, c):
    return (((r * 4 + zl % 4) * 4 + y % 4) * 4 + x % 4) * 2 + c


def send(value, target):
    pairs = [(rank(*place), rank(*target(*place))) for place in places()]
    return lax.ppermute(value, AXES, pairs)


def swap_cores(value):
    return send(value, lambda r, zl, y, x, c: (r, zl, y, x, 1 - c))


def swap_reps(value):
    return send(value, lambda r, zl, y, x, c: (1 - r, zl, y, x, c))


def along_line(value, k):
    return send(value, lambda r, zl, y, x, c: (r, zl + k, y, x, c))


def first_turn(value, k):
    return send(
        value,
        lambda r, zl, y, x, c: (r, zl, y, x + k, c) if c else (r, zl, y + k, x, c),
    )


def second_turn(value, k):
    return send(
        value,
        lambda r, zl, y, x, c: (r, zl, y + k, x, c) if c else (r, zl, y, x + k, c),
    )


def to_parity(value, j, other_rep):
    def target(r, zl, y, x, c):
        return (
            r ^ other_rep,
            zl - 1 + 2 * j if c else zl - 2 * j,
            y,
            x,
            zl % 2,
        )

    return send(value, target)


def column(zl, y, x):
    return pl.multiple_of(((zl * 4 + y) * 4 + x) * 128, 128)


def back(at, k):
    return lax.rem(at + 4 - k, 4)


def arrange(where, act_rows, grad_rows, mine, other):
    zl, y, x, core = (where[i] for i in range(4))

    def write(rows, out, role):
        for k in range(4):
            for k2 in range(4):
                for kz in range(4):
                    if role == 0:
                        at = column(back(zl, kz), back(y, k2), lax.rem(x + k, 4))
                    else:
                        at = column(back(zl, kz), lax.rem(y + k, 4), back(x, k2))
                    b = (k2 * 4 + kz) * 128
                    out[k, :, b : b + 128] = rows[:, pl.ds(at, 128)]

    @pl.when(core == 0)
    def _():
        write(act_rows, mine, 0)
        write(grad_rows, other, 1)

    @pl.when(core == 1)
    def _():
        write(grad_rows, mine, 1)
        write(act_rows, other, 0)


def partials(w0, w1, w2, w3, plane, p0, p1, p2, p3):
    x = plane[...].reshape(2048, 128)
    for w, p in ((w0, p0), (w3, p1), (w2, p2), (w1, p3)):
        p[...] = jnp.dot(
            w[...].reshape(128, 2048), x, preferred_element_type=jnp.float32
        )


def tiles(g0, g1, g2, g3, plane, e0, e1, e2, e3):
    x = plane[...].reshape(1024, 256)
    for g, e in ((g0, e0), (g3, e1), (g2, e2), (g1, e3)):
        part = lax.dot_general(
            g[...], x, (((1,), (1,)), ((), ())), preferred_element_type=jnp.float32
        )
        e[...] = (part * (1.0 / TOKENS)).astype(e.dtype)


def assemble(where, own, sibling, out):
    zl, y, x, core = (where[i] for i in range(4))
    for side, piece in enumerate((own, sibling)):
        held_by = core if side == 0 else 1 - core
        match = lax.rem(zl + held_by, 2) == 0
        for k3 in range(4):
            for k2 in range(4):
                for j in range(2):
                    z = jnp.where(
                        match, lax.rem(zl + 2 * j, 4), lax.rem(zl + 5 - 2 * j, 4)
                    )
                    at = jnp.where(
                        held_by == 0,
                        column(z, back(y, k2), back(x, k3)),
                        column(z, back(y, k3), back(x, k2)),
                    )
                    b = (k2 * 2 + j) * 128
                    out[:, pl.ds(pl.multiple_of(at, 128), 128)] = piece[
                        k3, :, b : b + 128
                    ].astype(jnp.float32)


VMEM = pl.BlockSpec(memory_space=pltpu.VMEM)
SMEM = pl.BlockSpec(memory_space=pltpu.SMEM)
PARAMS = pltpu.CompilerParams(vmem_limit_bytes=40 * 1024 * 1024)


def call(body, name, shapes, ins):
    return pl.pallas_call(
        body,
        out_shape=shapes,
        in_specs=ins,
        out_specs=jax.tree.map(lambda _: VMEM, shapes),
        compiler_params=PARAMS,
        name=name,
    )


def on_device(acts, grads_out, act_inverse, grad_inverse):
    bf16, f32 = jnp.bfloat16, jnp.float32
    shape = jax.ShapeDtypeStruct
    c = lax.axis_index("c")
    where = jnp.stack(
        [lax.axis_index("zl"), lax.axis_index("y"), lax.axis_index("x"), c]
    ).astype(jnp.int32)
    first = c == 0

    acts_t, grads_t = acts.T, grads_out.T
    got = swap_cores(jnp.where(first, grads_t, acts_t))
    kept = jnp.where(first, acts_t, grads_t)
    block = jnp.concatenate(
        [jnp.where(first, kept, got), jnp.where(first, got, kept)], axis=0
    )
    mine, other = call(
        arrange, "arrange", [shape((4, 64, 2048), bf16)] * 2, [SMEM, VMEM, VMEM]
    )(where, act_inverse, grad_inverse)
    theirs = swap_cores(other)
    rows = [jnp.stack([mine[k], theirs[k]]) for k in range(4)]

    line = jnp.stack([block] + [along_line(block, k) for k in (1, 2, 3)])
    weights = [rows[0]] + [second_turn(rows[k], k) for k in (1, 2, 3)]
    plane = jnp.stack([line] + [first_turn(line, k) for k in (1, 2, 3)])
    parts = call(partials, "partials", [shape((128, 128), f32)] * 4, [VMEM] * 5)(
        *weights, plane
    )
    total = parts[0]
    for k in (1, 2, 3):
        total = total + second_turn(parts[k], k)
    pre = jnp.where(
        first, total, jnp.concatenate([total[64:], total[:64]], axis=0)
    ).astype(bf16)

    near = swap_cores(pre)
    act = jnp.where(first, pre, near)
    grad = jnp.where(first, near, pre)
    pair = jnp.stack(
        [
            jnp.concatenate([to_parity(act, j, 0), to_parity(act, j, 1)], axis=1)
            for j in (0, 1)
        ]
    )
    grad = jnp.concatenate([grad, swap_reps(grad)], axis=1)
    plane = jnp.stack([pair] + [first_turn(pair, k) for k in (1, 2, 3)])
    grads = [grad] + [second_turn(grad, k) for k in (1, 2, 3)]
    made = call(tiles, "tiles", [shape((128, 1024), bf16)] * 4, [VMEM] * 5)(
        *grads, plane
    )
    whole = [made[0]] + [second_turn(made[k], k) for k in (1, 2, 3)]
    low = jnp.stack([e[:64] for e in whole])
    high = jnp.stack([e[64:] for e in whole])
    own = jnp.where(first, low, high)
    sibling = swap_cores(jnp.where(first, high, low))
    return call(
        assemble, "assemble", shape((64, 8192), f32), [SMEM, VMEM, VMEM]
    )(where, own, sibling)


def solution(mesh):
    finer = Mesh(mesh.devices.reshape(SIZES), AXES)
    return jax.shard_map(
        on_device,
        mesh=finer,
        in_specs=(P("rep", ZERO), P("rep", ZERO), P(ZERO, None), P(ZERO, None)),
        out_specs=P(ZERO, None),
        check_vma=False,
    )
```

time: 96.5 us -> 92.7 us (0.961)
  waiting for transfers between devices: 43.7 us -> 39.1 us
  starting transfers between devices: 41.5 us -> 44.9 us
  other arithmetic: 3.12 us -> 0.7 us
  Pallas kernels: 5.96 us -> 4.85 us
    ppermute x27 -> x30, waiting for transfers between devices: 43.7 us -> 39.1 us  [send(): return lax.ppermute(value, AXES, pairs)]
    ppermute x27 -> x30, starting transfers between devices: 41.5 us -> 44.9 us  [send(): return lax.ppermute(value, AXES, pairs)]
    select_n x3, other arithmetic: 2.67 us -> 0.16 us  [the longest x1 0.15 us: on_device(): sibling = swap_cores(jnp.where(first, high, low))]
    pallas_call x2 -> x4, Pallas kernels: 5.96 us -> 4.85 us  [the longest x1 2.22 us: on_device(): call(assemble, 'assemble', shape((64, 8192), f32), [SMEM, VMEM, VMEM])]
    unnamed x2 -> x8, local copies, waits for them, and re-layouts: 1.66 us -> 2.46 us
  transfers between devices with their start and end apart: 27 -> 30, of which waited for: 15 -> 18; matrix products, arithmetic and copies ran while one was open for 3% -> 1% of each run, Pallas kernels for 0% -> 0%
where the time goes in v2:
time: 92.7 us; the launch traced here: 92.5 us
  starting transfers between devices  44.9 us (48%)
  waiting for transfers between devices  39.1 us (42%)
  Pallas kernels  4.85 us (5%)
  local copies, waits for them, and re-layouts  2.68 us (3%)
    ppermute x30, starting transfers between devices, send(): return lax.ppermute(value, AXES, pairs)  44.9 us
    ppermute x30, waiting for transfers between devices, send(): return lax.ppermute(value, AXES, pairs)  39.1 us
    unnamed x8, local copies, waits for them, and re-layouts  2.46 us
    pallas_call x1, Pallas kernels, on_device(): call(assemble, 'assemble', shape((64, 8192), f32), [SMEM, VMEM, VMEM])  2.22 us
  transfers between devices with their start and end apart: 30, of which 18 were waited for; matrix products, arithmetic and copies ran while one was open for 1% of the time, Pallas kernels for 0%

profile of v2, /device:TPU:1, one launch (start us, length us, event | category | flops | bytes accessed | tf_op | source)
XLA Modules:
  0.0 92.5 jit_solution(12931299966332814949)
XLA Ops:
  0.1 1.2 %copy-done = bf16[64,8192]{1,0:T(8,128)(2,1)S(1)} copy-done((bf16[64,8192]{1,0:T(8,128)(2,1)S(1)}, bf16[64,8192]{1,0:T(8,128)(2,1)}, u32[]{:S(2)}) %copy-start) | copy-done | bytes 1048600
  1.3 1.2 %copy-done.1 = bf16[64,8192]{1,0:T(8,128)(2,1)S(1)} copy-done((bf16[64,8192]{1,0:T(8,128)(2,1)S(1)}, bf16[64,8192]{1,0:T(8,128)(2,1)}, u32[]{:S(2)}) %copy-start.1) | copy-done | bytes 1048600
  3.7 3.3 %collective-permute-start = (bf16[4,64,2048]{2,1,0:T(8,128)(2,1)S(1)}, bf16[4,64,2048]{2,1,0:T(8,128)(2,1)S(1)}, u32[]{:S(2)}, u32[]{:S(2)}) collective-permute-start(bf16[4,64,2048]{2,1,0:T(8,128)(2,1)S(1)} %get-tuple-element.16), channel_id=1, source_target_pairs={{0,1},{1,0},{2,3},{3,2},{4,5},{5,4},{6,7},{7,6},{8,9},{9,8},{10,11... | collective-permute-start | bytes 3145736 | tf_op jit(solution)/shard_map/ppermute | solution.py:30
  7.1 2.2 %collective-permute-done.4 = bf16[64,128]{1,0:T(8,128)(2,1)S(1)} collective-permute-done((bf16[64,128]{1,0:T(8,128)(2,1)S(1)}, bf16[64,128]{1,0:T(8,128)(2,1)S(1)}, u32[]{:S(2)}, u32[]{:S(2)}) %collective-permute-start.4) | collective-permute-done | bytes 16416 | tf_op jit(solution)/shard_map/ppermute | solution.py:30
  9.3 2.7 %collective-permute-start.7 = (bf16[128,128]{1,0:T(8,128)(2,1)S(1)}, bf16[128,128]{1,0:T(8,128)(2,1)S(1)}, u32[]{:S(2)}, u32[]{:S(2)}) collective-permute-start(bf16[128,128]{1,0:T(8,128)(2,1)S(1)} %get-tuple-element.54), channel_id=1, source_target_pairs={{0,96},{1,97},{2,98},{3,99},{4,100},{5,101},{6,102},{7,103},{8,104... | collective-permute-start | bytes 98312 | tf_op jit(solution)/shard_map/ppermute | solution.py:30
  13.0 2.7 %collective-permute-done.6 = bf16[128,128]{1,0:T(8,128)(2,1)S(1)} collective-permute-done((bf16[128,128]{1,0:T(8,128)(2,1)S(1)}, bf16[128,128]{1,0:T(8,128)(2,1)S(1)}, u32[]{:S(2)}, u32[]{:S(2)}) %collective-permute-start.6) | collective-permute-done | bytes 32800 | tf_op jit(solution)/shard_map/ppermute | solution.py:30
  16.6 2.6 %collective-permute-start.10 = (bf16[4,128,128]{2,1,0:T(8,128)(2,1)S(1)}, bf16[4,128,128]{2,1,0:T(8,128)(2,1)S(1)}, u32[]{:S(2)}, u32[]{:S(2)}) collective-permute-start(bf16[4,128,128]{2,1,0:T(8,128)(2,1)S(1)} %get-tuple-element.46), channel_id=1, source_target_pairs={{0,24},{1,7},{2,26},{3,1},{4,28},{5,3},{6,30},{7,5},{8,0},{9,15},{... | collective-permute-start | bytes 393224 | tf_op jit(solution)/shard_map/ppermute | solution.py:30
  19.3 1.4 %collective-permute-start.1 = (bf16[2,64,2048]{2,1,0:T(8,128)(2,1)S(1)}, bf16[2,64,2048]{2,1,0:T(8,128)(2,1)S(1)}, u32[]{:S(2)}, u32[]{:S(2)}) collective-permute-start(bf16[2,64,2048]{2,1,0:T(8,128)(2,1)S(1)} %pad_maximum_fusion.1), channel_id=1, source_target_pairs={{0,2},{1,9},{2,4},{3,11},{4,6},{5,13},{6,0},{7,15},{8,10},{9,17},{... | collective-permute-start | bytes 1572872 | tf_op jit(solution)/shard_map/ppermute | solution.py:30
  20.7 2.7 %collective-permute-start.2 = (bf16[2,64,2048]{2,1,0:T(8,128)(2,1)S(1)}, bf16[2,64,2048]{2,1,0:T(8,128)(2,1)S(1)}, u32[]{:S(2)}, u32[]{:S(2)}) collective-permute-start(bf16[2,64,2048]{2,1,0:T(8,128)(2,1)S(1)} %pad_maximum_fusion.2), channel_id=1, source_target_pairs={{0,4},{1,17},{2,6},{3,19},{4,0},{5,21},{6,2},{7,23},{8,12},{9,25},... | collective-permute-start | bytes 1572872 | tf_op jit(solution)/shard_map/ppermute | solution.py:30
  23.5 1.1 %collective-permute-start.3 = (bf16[2,64,2048]{2,1,0:T(8,128)(2,1)S(1)}, bf16[2,64,2048]{2,1,0:T(8,128)(2,1)S(1)}, u32[]{:S(2)}, u32[]{:S(2)}) collective-permute-start(bf16[2,64,2048]{2,1,0:T(8,128)(2,1)S(1)} %pad_maximum_fusion.3), channel_id=1, source_target_pairs={{0,6},{1,25},{2,0},{3,27},{4,2},{5,29},{6,4},{7,31},{8,14},{9,1},{... | collective-permute-start | bytes 1572872 | tf_op jit(solution)/shard_map/ppermute | solution.py:30
  25.8 5.7 %collective-permute-done.9 = bf16[4,128,128]{2,1,0:T(8,128)(2,1)S(1)} collective-permute-done((bf16[4,128,128]{2,1,0:T(8,128)(2,1)S(1)}, bf16[4,128,128]{2,1,0:T(8,128)(2,1)S(1)}, u32[]{:S(2)}, u32[]{:S(2)}) %collective-permute-start.9) | collective-permute-done | bytes 131104 | tf_op jit(solution)/shard_map/ppermute | solution.py:30
  31.4 1.8 %collective-permute-done.8 = bf16[4,128,128]{2,1,0:T(8,128)(2,1)S(1)} collective-permute-done((bf16[4,128,128]{2,1,0:T(8,128)(2,1)S(1)}, bf16[4,128,128]{2,1,0:T(8,128)(2,1)S(1)}, u32[]{:S(2)}, u32[]{:S(2)}) %collective-permute-start.8) | collective-permute-done | bytes 131104 | tf_op jit(solution)/shard_map/ppermute | solution.py:30
  33.4 4.6 %collective-permute-done.2.w2 = bf16[2,64,2048]{2,1,0:T(8,128)(2,1)S(1)} collective-permute-done((bf16[2,64,2048]{2,1,0:T(8,128)(2,1)S(1)}, bf16[2,64,2048]{2,1,0:T(8,128)(2,1)S(1)}, u32[]{:S(2)}, u32[]{:S(2)}) %collective-permute-start.2) | collective-permute-done | bytes 524320 | tf_op jit(solution)/shard_map/ppermute | solution.py:30
  38.7 1.7 %collective-permute-start.13 = (f32[128,128]{1,0:T(8,128)S(1)}, f32[128,128]{1,0:T(8,128)S(1)}, u32[]{:S(2)}, u32[]{:S(2)}) collective-permute-start(f32[128,128]{1,0:T(8,128)S(1)} %get-tuple-element.20), channel_id=1, source_target_pairs={{0,6},{1,25},{2,0},{3,27},{4,2},{5,29},{6,4},{7,31},{8,14},{9,1},{... | collective-permute-start | bytes 196616 | tf_op jit(solution)/shard_map/ppermute | solution.py:30
  41.9 3.2 %collective-permute-done.12 = f32[128,128]{1,0:T(8,128)S(1)} collective-permute-done((f32[128,128]{1,0:T(8,128)S(1)}, f32[128,128]{1,0:T(8,128)S(1)}, u32[]{:S(2)}, u32[]{:S(2)}) %collective-permute-start.12) | collective-permute-done | bytes 65568 | tf_op jit(solution)/shard_map/ppermute | solution.py:30
  45.8 4.5 %collective-permute-start.14 = (bf16[128,128]{1,0:T(8,128)(2,1)S(1)}, bf16[128,128]{1,0:T(8,128)(2,1)S(1)}, u32[]{:S(2)}, u32[]{:S(2)}) collective-permute-start(bf16[128,128]{1,0:T(8,128)(2,1)S(1)} %fusion), channel_id=1, source_target_pairs={{0,1},{1,0},{2,3},{3,2},{4,5},{5,4},{6,7},{7,6},{8,9},{9,8},{10,11... | collective-permute-start | bytes 98312 | tf_op jit(solution)/shard_map/ppermute | solution.py:30
  51.2 2.9 %collective-permute-start.22 = (bf16[128,128]{1,0:T(8,128)(2,1)S(1)}, bf16[128,128]{1,0:T(8,128)(2,1)S(1)}, u32[]{:S(2)}, u32[]{:S(2)}) collective-permute-start(bf16[128,128]{1,0:T(8,128)(2,1)S(1)} %get-tuple-element.47), channel_id=1, source_target_pairs={{0,192},{1,160},{2,194},{3,162},{4,196},{5,164},{6,198},{7,166},{8... | collective-permute-start | bytes 98312 | tf_op jit(solution)/shard_map/ppermute | solution.py:30
  54.6 1.3 %collective-permute-start.20 = (bf16[128,128]{1,0:T(8,128)(2,1)S(1)}, bf16[128,128]{1,0:T(8,128)(2,1)S(1)}, u32[]{:S(2)}, u32[]{:S(2)}) collective-permute-start(bf16[128,128]{1,0:T(8,128)(2,1)S(1)} %get-tuple-element.47), channel_id=1, source_target_pairs={{0,128},{1,224},{2,130},{3,226},{4,132},{5,228},{6,134},{7,230},{8... | collective-permute-start | bytes 98312 | tf_op jit(solution)/shard_map/ppermute | solution.py:30
  55.9 5.4 %collective-permute-start.19 = (bf16[128,128]{1,0:T(8,128)(2,1)S(1)}, bf16[128,128]{1,0:T(8,128)(2,1)S(1)}, u32[]{:S(2)}, u32[]{:S(2)}) collective-permute-start(bf16[128,128]{1,0:T(8,128)(2,1)S(1)} %get-tuple-element.47), channel_id=1, source_target_pairs={{0,0},{1,96},{2,2},{3,98},{4,4},{5,100},{6,6},{7,102},{8,8},{9,104... | collective-permute-start | bytes 98312 | tf_op jit(solution)/shard_map/ppermute | solution.py:30
  61.4 3.6 %collective-permute-start.15 = (bf16[128,128]{1,0:T(8,128)(2,1)S(1)}, bf16[128,128]{1,0:T(8,128)(2,1)S(1)}, u32[]{:S(2)}, u32[]{:S(2)}) collective-permute-start(bf16[128,128]{1,0:T(8,128)(2,1)S(1)} %get-tuple-element.48), channel_id=1, source_target_pairs={{0,128},{1,129},{2,130},{3,131},{4,132},{5,133},{6,134},{7,135},{8... | collective-permute-start | bytes 98312 | tf_op jit(solution)/shard_map/ppermute | solution.py:30
  67.0 1.1 %collective-permute-done.15 = bf16[128,128]{1,0:T(8,128)(2,1)S(1)} collective-permute-done((bf16[128,128]{1,0:T(8,128)(2,1)S(1)}, bf16[128,128]{1,0:T(8,128)(2,1)S(1)}, u32[]{:S(2)}, u32[]{:S(2)}) %collective-permute-start.15) | collective-permute-done | bytes 32800 | tf_op jit(solution)/shard_map/ppermute | solution.py:30
  68.2 1.3 %collective-permute-start.17 = (bf16[128,256]{1,0:T(8,128)(2,1)S(1)}, bf16[128,256]{1,0:T(8,128)(2,1)S(1)}, u32[]{:S(2)}, u32[]{:S(2)}) collective-permute-start(bf16[128,256]{1,0:T(8,128)(2,1)S(1)} %pad_maximum_fusion.10.g0), channel_id=1, source_target_pairs={{0,4},{1,17},{2,6},{3,19},{4,0},{5,21},{6,2},{7,23},{8,12},{9,25},... | collective-permute-start | bytes 196616 | tf_op jit(solution)/shard_map/ppermute | solution.py:30
  69.6 1.3 %collective-permute-start.18 = (bf16[128,256]{1,0:T(8,128)(2,1)S(1)}, bf16[128,256]{1,0:T(8,128)(2,1)S(1)}, u32[]{:S(2)}, u32[]{:S(2)}) collective-permute-start(bf16[128,256]{1,0:T(8,128)(2,1)S(1)} %pad_maximum_fusion.10.g0), channel_id=1, source_target_pairs={{0,6},{1,25},{2,0},{3,27},{4,2},{5,29},{6,4},{7,31},{8,14},{9,1},{... | collective-permute-start | bytes 196616 | tf_op jit(solution)/shard_map/ppermute | solution.py:30
  70.9 1.3 %collective-permute-done.24 = bf16[2,128,256]{2,1,0:T(8,128)(2,1)S(1)} collective-permute-done((bf16[2,128,256]{2,1,0:T(8,128)(2,1)S(1)}, bf16[2,128,256]{2,1,0:T(8,128)(2,1)S(1)}, u32[]{:S(2)}, u32[]{:S(2)}) %collective-permute-start.24) | collective-permute-done | bytes 131104 | tf_op jit(solution)/shard_map/ppermute | solution.py:30
  72.2 2.3 %collective-permute-done.23 = bf16[2,128,256]{2,1,0:T(8,128)(2,1)S(1)} collective-permute-done((bf16[2,128,256]{2,1,0:T(8,128)(2,1)S(1)}, bf16[2,128,256]{2,1,0:T(8,128)(2,1)S(1)}, u32[]{:S(2)}, u32[]{:S(2)}) %collective-permute-start.23) | collective-permute-done | bytes 131104 | tf_op jit(solution)/shard_map/ppermute | solution.py:30
  75.5 1.4 %collective-permute-start.28 = (bf16[128,1024]{1,0:T(8,128)(2,1)S(1)}, bf16[128,1024]{1,0:T(8,128)(2,1)S(1)}, u32[]{:S(2)}, u32[]{:S(2)}) collective-permute-start(bf16[128,1024]{1,0:T(8,128)(2,1)S(1)} %get-tuple-element.24), channel_id=1, source_target_pairs={{0,6},{1,25},{2,0},{3,27},{4,2},{5,29},{6,4},{7,31},{8,14},{9,1},{... | collective-permute-start | bytes 786440 | tf_op jit(solution)/shard_map/ppermute | solution.py:30
  77.5 3.5 %collective-permute-done.28 = bf16[128,1024]{1,0:T(8,128)(2,1)S(1)} collective-permute-done((bf16[128,1024]{1,0:T(8,128)(2,1)S(1)}, bf16[128,1024]{1,0:T(8,128)(2,1)S(1)}, u32[]{:S(2)}, u32[]{:S(2)}) %collective-permute-start.28) | collective-permute-done | bytes 262176 | tf_op jit(solution)/shard_map/ppermute | solution.py:30
  81.1 2.8 %collective-permute-done.27 = bf16[128,1024]{1,0:T(8,128)(2,1)S(1)} collective-permute-done((bf16[128,1024]{1,0:T(8,128)(2,1)S(1)}, bf16[128,1024]{1,0:T(8,128)(2,1)S(1)}, u32[]{:S(2)}, u32[]{:S(2)}) %collective-permute-start.27) | collective-permute-done | bytes 262176 | tf_op jit(solution)/shard_map/ppermute | solution.py:30
  83.9 2.7 %collective-permute-done.26 = bf16[128,1024]{1,0:T(8,128)(2,1)S(1)} collective-permute-done((bf16[128,1024]{1,0:T(8,128)(2,1)S(1)}, bf16[128,1024]{1,0:T(8,128)(2,1)S(1)}, u32[]{:S(2)}, u32[]{:S(2)}) %collective-permute-start.26) | collective-permute-done | bytes 262176 | tf_op jit(solution)/shard_map/ppermute | solution.py:30
  86.8 1.9 %collective-permute-start.29 = (bf16[4,64,1024]{2,1,0:T(8,128)(2,1)S(1)}, bf16[4,64,1024]{2,1,0:T(8,128)(2,1)S(1)}, u32[]{:S(2)}, u32[]{:S(2)}) collective-permute-start(bf16[4,64,1024]{2,1,0:T(8,128)(2,1)S(1)} %get-tuple-element.25), channel_id=1, source_target_pairs={{0,1},{1,0},{2,3},{3,2},{4,5},{5,4},{6,7},{7,6},{8,9},{9,8},{10,11... | collective-permute-start | bytes 1572872 | tf_op jit(solution)/shard_map/ppermute | solution.py:30
  88.7 1.5 %collective-permute-done.29.sibling = bf16[4,64,1024]{2,1,0:T(8,128)(2,1)S(1)} collective-permute-done((bf16[4,64,1024]{2,1,0:T(8,128)(2,1)S(1)}, bf16[4,64,1024]{2,1,0:T(8,128)(2,1)S(1)}, u32[]{:S(2)}, u32[]{:S(2)}) %collective-permute-start.29) | collective-permute-done | bytes 524320 | tf_op jit(solution)/shard_map/ppermute | solution.py:30
  90.3 2.2 %assemble.1 = f32[64,8192]{1,0:T(8,128)} custom-call(s32[4]{0:T(128)S(1)} %pad_add_fusion.where, bf16[4,64,1024]{2,1,0:T(8,128)(2,1)S(1)} %get-tuple-element.26.own, bf16[4,64,1024]{2,1,0:T(8,128)(2,1)S(1)} %collective-permute-done.29.sibling), custom_call_target="tpu_custom_call" | custom-call | tf_op jit(solution)/shard_map/assemble/pallas_call | solution.py:214
  (66 shorter events, 13.0 us)
Async XLA Ops:
  0.0 7.0 %copy-start.2 = (bf16[128,64]{0,1:T(8,128)(2,1)S(1)}, bf16[128,64]{0,1:T(8,128)(2,1)}, u32[]{:S(2)}) copy-start(bf16[128,64]{0,1:T(8,128)(2,1)} %param.5) | copy-start | bytes 49156
  0.0 7.0 %copy-start.3 = (bf16[128,64]{0,1:T(8,128)(2,1)S(1)}, bf16[128,64]{0,1:T(8,128)(2,1)}, u32[]{:S(2)}) copy-start(bf16[128,64]{0,1:T(8,128)(2,1)} %param.4) | copy-start | bytes 49156
  3.7 15.5 %collective-permute-start = (bf16[4,64,2048]{2,1,0:T(8,128)(2,1)S(1)}, bf16[4,64,2048]{2,1,0:T(8,128)(2,1)S(1)}, u32[]{:S(2)}, u32[]{:S(2)}) collective-permute-start(bf16[4,64,2048]{2,1,0:T(8,128)(2,1)S(1)} %get-tuple-element.16), channel_id=1, source_target_pairs={{0,1},{1,0},{2,3},{3,2},{4,5},{5,4},{6,7},{7,6},{8,9},{9,8},{10,11... | collective-permute-start | bytes 3145736 | tf_op jit(solution)/shard_map/ppermute | solution.py:30
  7.0 2.3 %collective-permute-start.4 = (bf16[64,128]{1,0:T(8,128)(2,1)S(1)}, bf16[64,128]{1,0:T(8,128)(2,1)S(1)}, u32[]{:S(2)}, u32[]{:S(2)}) collective-permute-start(bf16[64,128]{1,0:T(8,128)(2,1)S(1)} %select_bitcast_fusion), channel_id=1, source_target_pairs={{0,1},{1,0},{2,3},{3,2},{4,5},{5,4},{6,7},{7,6},{8,9},{9,8},{10,11... | collective-permute-start | bytes 49160 | tf_op jit(solution)/shard_map/ppermute | solution.py:30
  9.3 3.7 %collective-permute-start.7 = (bf16[128,128]{1,0:T(8,128)(2,1)S(1)}, bf16[128,128]{1,0:T(8,128)(2,1)S(1)}, u32[]{:S(2)}, u32[]{:S(2)}) collective-permute-start(bf16[128,128]{1,0:T(8,128)(2,1)S(1)} %get-tuple-element.54), channel_id=1, source_target_pairs={{0,96},{1,97},{2,98},{3,99},{4,100},{5,101},{6,102},{7,103},{8,104... | collective-permute-start | bytes 98312 | tf_op jit(solution)/shard_map/ppermute | solution.py:30
  12.0 3.7 %collective-permute-start.6 = (bf16[128,128]{1,0:T(8,128)(2,1)S(1)}, bf16[128,128]{1,0:T(8,128)(2,1)S(1)}, u32[]{:S(2)}, u32[]{:S(2)}) collective-permute-start(bf16[128,128]{1,0:T(8,128)(2,1)S(1)} %get-tuple-element.54), channel_id=1, source_target_pairs={{0,64},{1,65},{2,66},{3,67},{4,68},{5,69},{6,70},{7,71},{8,72},{9,... | collective-permute-start | bytes 98312 | tf_op jit(solution)/shard_map/ppermute | solution.py:30
  12.0 4.6 %collective-permute-start.5 = (bf16[128,128]{1,0:T(8,128)(2,1)S(1)}, bf16[128,128]{1,0:T(8,128)(2,1)S(1)}, u32[]{:S(2)}, u32[]{:S(2)}) collective-permute-start(bf16[128,128]{1,0:T(8,128)(2,1)S(1)} %get-tuple-element.54), channel_id=1, source_target_pairs={{0,32},{1,33},{2,34},{3,35},{4,36},{5,37},{6,38},{7,39},{8,40},{9,... | collective-permute-start | bytes 98312 | tf_op jit(solution)/shard_map/ppermute | solution.py:30
  16.6 8.6 %collective-permute-start.10 = (bf16[4,128,128]{2,1,0:T(8,128)(2,1)S(1)}, bf16[4,128,128]{2,1,0:T(8,128)(2,1)S(1)}, u32[]{:S(2)}, u32[]{:S(2)}) collective-permute-start(bf16[4,128,128]{2,1,0:T(8,128)(2,1)S(1)} %get-tuple-element.46), channel_id=1, source_target_pairs={{0,24},{1,7},{2,26},{3,1},{4,28},{5,3},{6,30},{7,5},{8,0},{9,15},{... | collective-permute-start | bytes 393224 | tf_op jit(solution)/shard_map/ppermute | solution.py:30
  19.3 14.1 %collective-permute-start.1 = (bf16[2,64,2048]{2,1,0:T(8,128)(2,1)S(1)}, bf16[2,64,2048]{2,1,0:T(8,128)(2,1)S(1)}, u32[]{:S(2)}, u32[]{:S(2)}) collective-permute-start(bf16[2,64,2048]{2,1,0:T(8,128)(2,1)S(1)} %pad_maximum_fusion.1), channel_id=1, source_target_pairs={{0,2},{1,9},{2,4},{3,11},{4,6},{5,13},{6,0},{7,15},{8,10},{9,17},{... | collective-permute-start | bytes 1572872 | tf_op jit(solution)/shard_map/ppermute | solution.py:30
  20.7 17.2 %collective-permute-start.2 = (bf16[2,64,2048]{2,1,0:T(8,128)(2,1)S(1)}, bf16[2,64,2048]{2,1,0:T(8,128)(2,1)S(1)}, u32[]{:S(2)}, u32[]{:S(2)}) collective-permute-start(bf16[2,64,2048]{2,1,0:T(8,128)(2,1)S(1)} %pad_maximum_fusion.2), channel_id=1, source_target_pairs={{0,4},{1,17},{2,6},{3,19},{4,0},{5,21},{6,2},{7,23},{8,12},{9,25},... | collective-permute-start | bytes 1572872 | tf_op jit(solution)/shard_map/ppermute | solution.py:30
  23.5 14.5 %collective-permute-start.3 = (bf16[2,64,2048]{2,1,0:T(8,128)(2,1)S(1)}, bf16[2,64,2048]{2,1,0:T(8,128)(2,1)S(1)}, u32[]{:S(2)}, u32[]{:S(2)}) collective-permute-start(bf16[2,64,2048]{2,1,0:T(8,128)(2,1)S(1)} %pad_maximum_fusion.3), channel_id=1, source_target_pairs={{0,6},{1,25},{2,0},{3,27},{4,2},{5,29},{6,4},{7,31},{8,14},{9,1},{... | collective-permute-start | bytes 1572872 | tf_op jit(solution)/shard_map/ppermute | solution.py:30
  24.6 6.8 %collective-permute-start.9 = (bf16[4,128,128]{2,1,0:T(8,128)(2,1)S(1)}, bf16[4,128,128]{2,1,0:T(8,128)(2,1)S(1)}, u32[]{:S(2)}, u32[]{:S(2)}) collective-permute-start(bf16[4,128,128]{2,1,0:T(8,128)(2,1)S(1)} %get-tuple-element.46), channel_id=1, source_target_pairs={{0,16},{1,5},{2,18},{3,7},{4,20},{5,1},{6,22},{7,3},{8,24},{9,13},... | collective-permute-start | bytes 393224 | tf_op jit(solution)/shard_map/ppermute | solution.py:30
  25.2 8.1 %collective-permute-start.8 = (bf16[4,128,128]{2,1,0:T(8,128)(2,1)S(1)}, bf16[4,128,128]{2,1,0:T(8,128)(2,1)S(1)}, u32[]{:S(2)}, u32[]{:S(2)}) collective-permute-start(bf16[4,128,128]{2,1,0:T(8,128)(2,1)S(1)} %get-tuple-element.46), channel_id=1, source_target_pairs={{0,8},{1,3},{2,10},{3,5},{4,12},{5,7},{6,14},{7,1},{8,16},{9,11},{... | collective-permute-start | bytes 393224 | tf_op jit(solution)/shard_map/ppermute | solution.py:30
  38.7 3.2 %collective-permute-start.13 = (f32[128,128]{1,0:T(8,128)S(1)}, f32[128,128]{1,0:T(8,128)S(1)}, u32[]{:S(2)}, u32[]{:S(2)}) collective-permute-start(f32[128,128]{1,0:T(8,128)S(1)} %get-tuple-element.20), channel_id=1, source_target_pairs={{0,6},{1,25},{2,0},{3,27},{4,2},{5,29},{6,4},{7,31},{8,14},{9,1},{... | collective-permute-start | bytes 196616 | tf_op jit(solution)/shard_map/ppermute | solution.py:30
  40.4 4.7 %collective-permute-start.12 = (f32[128,128]{1,0:T(8,128)S(1)}, f32[128,128]{1,0:T(8,128)S(1)}, u32[]{:S(2)}, u32[]{:S(2)}) collective-permute-start(f32[128,128]{1,0:T(8,128)S(1)} %get-tuple-element.19), channel_id=1, source_target_pairs={{0,4},{1,17},{2,6},{3,19},{4,0},{5,21},{6,2},{7,23},{8,12},{9,25},... | collective-permute-start | bytes 196616 | tf_op jit(solution)/shard_map/ppermute | solution.py:30
  40.9 4.8 %collective-permute-start.11 = (f32[128,128]{1,0:T(8,128)S(1)}, f32[128,128]{1,0:T(8,128)S(1)}, u32[]{:S(2)}, u32[]{:S(2)}) collective-permute-start(f32[128,128]{1,0:T(8,128)S(1)} %get-tuple-element.18), channel_id=1, source_target_pairs={{0,2},{1,9},{2,4},{3,11},{4,6},{5,13},{6,0},{7,15},{8,10},{9,17},{... | collective-permute-start | bytes 196616 | tf_op jit(solution)/shard_map/ppermute | solution.py:30
  45.8 5.4 %collective-permute-start.14 = (bf16[128,128]{1,0:T(8,128)(2,1)S(1)}, bf16[128,128]{1,0:T(8,128)(2,1)S(1)}, u32[]{:S(2)}, u32[]{:S(2)}) collective-permute-start(bf16[128,128]{1,0:T(8,128)(2,1)S(1)} %fusion), channel_id=1, source_target_pairs={{0,1},{1,0},{2,3},{3,2},{4,5},{5,4},{6,7},{7,6},{8,9},{9,8},{10,11... | collective-permute-start | bytes 98312 | tf_op jit(solution)/shard_map/ppermute | solution.py:30
  51.2 13.8 %collective-permute-start.22 = (bf16[128,128]{1,0:T(8,128)(2,1)S(1)}, bf16[128,128]{1,0:T(8,128)(2,1)S(1)}, u32[]{:S(2)}, u32[]{:S(2)}) collective-permute-start(bf16[128,128]{1,0:T(8,128)(2,1)S(1)} %get-tuple-element.47), channel_id=1, source_target_pairs={{0,192},{1,160},{2,194},{3,162},{4,196},{5,164},{6,198},{7,166},{8... | collective-permute-start | bytes 98312 | tf_op jit(solution)/shard_map/ppermute | solution.py:30
  54.0 10.9 %collective-permute-start.21 = (bf16[128,128]{1,0:T(8,128)(2,1)S(1)}, bf16[128,128]{1,0:T(8,128)(2,1)S(1)}, u32[]{:S(2)}, u32[]{:S(2)}) collective-permute-start(bf16[128,128]{1,0:T(8,128)(2,1)S(1)} %get-tuple-element.47), channel_id=1, source_target_pairs={{0,64},{1,32},{2,66},{3,34},{4,68},{5,36},{6,70},{7,38},{8,72},{9,... | collective-permute-start | bytes 98312 | tf_op jit(solution)/shard_map/ppermute | solution.py:30
  54.6 10.3 %collective-permute-start.20 = (bf16[128,128]{1,0:T(8,128)(2,1)S(1)}, bf16[128,128]{1,0:T(8,128)(2,1)S(1)}, u32[]{:S(2)}, u32[]{:S(2)}) collective-permute-start(bf16[128,128]{1,0:T(8,128)(2,1)S(1)} %get-tuple-element.47), channel_id=1, source_target_pairs={{0,128},{1,224},{2,130},{3,226},{4,132},{5,228},{6,134},{7,230},{8... | collective-permute-start | bytes 98312 | tf_op jit(solution)/shard_map/ppermute | solution.py:30
  55.9 9.0 %collective-permute-start.19 = (bf16[128,128]{1,0:T(8,128)(2,1)S(1)}, bf16[128,128]{1,0:T(8,128)(2,1)S(1)}, u32[]{:S(2)}, u32[]{:S(2)}) collective-permute-start(bf16[128,128]{1,0:T(8,128)(2,1)S(1)} %get-tuple-element.47), channel_id=1, source_target_pairs={{0,0},{1,96},{2,2},{3,98},{4,4},{5,100},{6,6},{7,102},{8,8},{9,104... | collective-permute-start | bytes 98312 | tf_op jit(solution)/shard_map/ppermute | solution.py:30
  61.4 6.8 %collective-permute-start.15 = (bf16[128,128]{1,0:T(8,128)(2,1)S(1)}, bf16[128,128]{1,0:T(8,128)(2,1)S(1)}, u32[]{:S(2)}, u32[]{:S(2)}) collective-permute-start(bf16[128,128]{1,0:T(8,128)(2,1)S(1)} %get-tuple-element.48), channel_id=1, source_target_pairs={{0,128},{1,129},{2,130},{3,131},{4,132},{5,133},{6,134},{7,135},{8... | collective-permute-start | bytes 98312 | tf_op jit(solution)/shard_map/ppermute | solution.py:30
  65.0 4.6 %collective-permute-start.25 = (bf16[2,128,256]{2,1,0:T(8,128)(2,1)S(1)}, bf16[2,128,256]{2,1,0:T(8,128)(2,1)S(1)}, u32[]{:S(2)}, u32[]{:S(2)}) collective-permute-start(bf16[2,128,256]{2,1,0:T(8,128)(2,1)S(1)} %get-tuple-element.44), channel_id=1, source_target_pairs={{0,24},{1,7},{2,26},{3,1},{4,28},{5,3},{6,30},{7,5},{8,0},{9,15},{... | collective-permute-start | bytes 393224 | tf_op jit(solution)/shard_map/ppermute | solution.py:30
  66.1 6.1 %collective-permute-start.24 = (bf16[2,128,256]{2,1,0:T(8,128)(2,1)S(1)}, bf16[2,128,256]{2,1,0:T(8,128)(2,1)S(1)}, u32[]{:S(2)}, u32[]{:S(2)}) collective-permute-start(bf16[2,128,256]{2,1,0:T(8,128)(2,1)S(1)} %get-tuple-element.44), channel_id=1, source_target_pairs={{0,16},{1,5},{2,18},{3,7},{4,20},{5,1},{6,22},{7,3},{8,24},{9,13},... | collective-permute-start | bytes 393224 | tf_op jit(solution)/shard_map/ppermute | solution.py:30
  66.7 7.8 %collective-permute-start.23 = (bf16[2,128,256]{2,1,0:T(8,128)(2,1)S(1)}, bf16[2,128,256]{2,1,0:T(8,128)(2,1)S(1)}, u32[]{:S(2)}, u32[]{:S(2)}) collective-permute-start(bf16[2,128,256]{2,1,0:T(8,128)(2,1)S(1)} %get-tuple-element.44), channel_id=1, source_target_pairs={{0,8},{1,3},{2,10},{3,5},{4,12},{5,7},{6,14},{7,1},{8,16},{9,11},{... | collective-permute-start | bytes 393224 | tf_op jit(solution)/shard_map/ppermute | solution.py:30
  68.1 6.5 %collective-permute-start.16 = (bf16[128,256]{1,0:T(8,128)(2,1)S(1)}, bf16[128,256]{1,0:T(8,128)(2,1)S(1)}, u32[]{:S(2)}, u32[]{:S(2)}) collective-permute-start(bf16[128,256]{1,0:T(8,128)(2,1)S(1)} %pad_maximum_fusion.10.g0), channel_id=1, source_target_pairs={{0,2},{1,9},{2,4},{3,11},{4,6},{5,13},{6,0},{7,15},{8,10},{9,17},{... | collective-permute-start | bytes 196616 | tf_op jit(solution)/shard_map/ppermute | solution.py:30
  68.2 6.4 %collective-permute-start.17 = (bf16[128,256]{1,0:T(8,128)(2,1)S(1)}, bf16[128,256]{1,0:T(8,128)(2,1)S(1)}, u32[]{:S(2)}, u32[]{:S(2)}) collective-permute-start(bf16[128,256]{1,0:T(8,128)(2,1)S(1)} %pad_maximum_fusion.10.g0), channel_id=1, source_target_pairs={{0,4},{1,17},{2,6},{3,19},{4,0},{5,21},{6,2},{7,23},{8,12},{9,25},... | collective-permute-start | bytes 196616 | tf_op jit(solution)/shard_map/ppermute | solution.py:30
  69.6 5.0 %collective-permute-start.18 = (bf16[128,256]{1,0:T(8,128)(2,1)S(1)}, bf16[128,256]{1,0:T(8,128)(2,1)S(1)}, u32[]{:S(2)}, u32[]{:S(2)}) collective-permute-start(bf16[128,256]{1,0:T(8,128)(2,1)S(1)} %pad_maximum_fusion.10.g0), channel_id=1, source_target_pairs={{0,6},{1,25},{2,0},{3,27},{4,2},{5,29},{6,4},{7,31},{8,14},{9,1},{... | collective-permute-start | bytes 196616 | tf_op jit(solution)/shard_map/ppermute | solution.py:30
  75.5 5.6 %collective-permute-start.28 = (bf16[128,1024]{1,0:T(8,128)(2,1)S(1)}, bf16[128,1024]{1,0:T(8,128)(2,1)S(1)}, u32[]{:S(2)}, u32[]{:S(2)}) collective-permute-start(bf16[128,1024]{1,0:T(8,128)(2,1)S(1)} %get-tuple-element.24), channel_id=1, source_target_pairs={{0,6},{1,25},{2,0},{3,27},{4,2},{5,29},{6,4},{7,31},{8,14},{9,1},{... | collective-permute-start | bytes 786440 | tf_op jit(solution)/shard_map/ppermute | solution.py:30
  76.8 7.1 %collective-permute-start.27 = (bf16[128,1024]{1,0:T(8,128)(2,1)S(1)}, bf16[128,1024]{1,0:T(8,128)(2,1)S(1)}, u32[]{:S(2)}, u32[]{:S(2)}) collective-permute-start(bf16[128,1024]{1,0:T(8,128)(2,1)S(1)} %get-tuple-element.23), channel_id=1, source_target_pairs={{0,4},{1,17},{2,6},{3,19},{4,0},{5,21},{6,2},{7,23},{8,12},{9,25},... | collective-permute-start | bytes 786440 | tf_op jit(solution)/shard_map/ppermute | solution.py:30
  77.4 9.3 %collective-permute-start.26 = (bf16[128,1024]{1,0:T(8,128)(2,1)S(1)}, bf16[128,1024]{1,0:T(8,128)(2,1)S(1)}, u32[]{:S(2)}, u32[]{:S(2)}) collective-permute-start(bf16[128,1024]{1,0:T(8,128)(2,1)S(1)} %get-tuple-element.22), channel_id=1, source_target_pairs={{0,2},{1,9},{2,4},{3,11},{4,6},{5,13},{6,0},{7,15},{8,10},{9,17},{... | collective-permute-start | bytes 786440 | tf_op jit(solution)/shard_map/ppermute | solution.py:30
  86.8 3.4 %collective-permute-start.29 = (bf16[4,64,1024]{2,1,0:T(8,128)(2,1)S(1)}, bf16[4,64,1024]{2,1,0:T(8,128)(2,1)S(1)}, u32[]{:S(2)}, u32[]{:S(2)}) collective-permute-start(bf16[4,64,1024]{2,1,0:T(8,128)(2,1)S(1)} %get-tuple-element.25), channel_id=1, source_target_pairs={{0,1},{1,0},{2,3},{3,2},{4,5},{5,4},{6,7},{7,6},{8,9},{9,8},{10,11... | collective-permute-start | bytes 1572872 | tf_op jit(solution)/shard_map/ppermute | solution.py:30
  (2 other events, 2.5 us)

commit v3 on v2

--- a/solution.py
+++ b/solution.py
@@ -56,17 +56,19 @@
     )
 
 
-def to_parity(value, j, other_rep):
+def on_ring(value, shifts, cores):
     def target(r, zl, y, x, c):
-        return (
-            r ^ other_rep,
-            zl - 1 + 2 * j if c else zl - 2 * j,
-            y,
-            x,
-            zl % 2,
-        )
+        plane = (r * 4 + zl + shifts[c]) % 8
+        return plane // 4, plane, y, x, cores[c]
 
     return send(value, target)
+
+
+def third_pair(value, k):
+    return send(
+        value,
+        lambda r, zl, y, x, c: (r, zl, y ^ k, x, c) if c else (r, zl, y, x ^ k, c),
+    )
 
 
 def column(zl, y, x):
@@ -110,26 +112,30 @@
         )
 
 
-def tiles(g0, g1, g2, g3, plane, e0, e1, e2, e3):
+def tiles(where, g, plane, e0, e1, e2, e3):
     x = plane[...].reshape(1024, 256)
-    for g, e in ((g0, e0), (g3, e1), (g2, e2), (g1, e3)):
+    at = jnp.where(where[3] == 0, where[2], where[1])
+    for k, e in enumerate((e0, e1, e2, e3)):
+        apart = at ^ lax.rem(at + k, 4)
         part = lax.dot_general(
-            g[...], x, (((1,), (1,)), ((), ())), preferred_element_type=jnp.float32
+            g[apart ^ (apart >> 1)],
+            x,
+            (((1,), (1,)), ((), ())),
+            preferred_element_type=jnp.float32,
         )
         e[...] = (part * (1.0 / TOKENS)).astype(e.dtype)
 
 
-def assemble(where, own, sibling, out):
+def assemble(where, *refs):
     zl, y, x, core = (where[i] for i in range(4))
-    for side, piece in enumerate((own, sibling)):
+    out = refs[-1]
+    for side in range(2):
         held_by = core if side == 0 else 1 - core
-        match = lax.rem(zl + held_by, 2) == 0
         for k3 in range(4):
+            piece = refs[side * 4 + k3]
             for k2 in range(4):
                 for j in range(2):
-                    z = jnp.where(
-                        match, lax.rem(zl + 2 * j, 4), lax.rem(zl + 5 - 2 * j, 4)
-                    )
+                    z = lax.rem(jnp.where(held_by == 0, zl + 4 - j, zl + 1 + j), 4)
                     at = jnp.where(
                         held_by == 0,
                         column(z, back(y, k2), back(x, k3)),
@@ -137,7 +143,7 @@
                     )
                     b = (k2 * 2 + j) * 128
                     out[:, pl.ds(pl.multiple_of(at, 128), 128)] = piece[
-                        k3, :, b : b + 128
+                        :, b : b + 128
                     ].astype(jnp.float32)
 
 
@@ -167,7 +173,8 @@
     first = c == 0
 
     acts_t, grads_t = acts.T, grads_out.T
-    got = swap_cores(jnp.where(first, grads_t, acts_t))
+    to_swap = jnp.where(first, grads_t, acts_t)
+    got = swap_cores(to_swap)
     kept = jnp.where(first, acts_t, grads_t)
     block = jnp.concatenate(
         [jnp.where(first, kept, got), jnp.where(first, got, kept)], axis=0
@@ -177,9 +184,12 @@
     )(where, act_inverse, grad_inverse)
     theirs = swap_cores(other)
     rows = [jnp.stack([mine[k], theirs[k]]) for k in range(4)]
+    weights = [rows[0]] + [second_turn(rows[k], k) for k in (1, 2, 3)]
 
     line = jnp.stack([block] + [along_line(block, k) for k in (1, 2, 3)])
-    weights = [rows[0]] + [second_turn(rows[k], k) for k in (1, 2, 3)]
+    line, weights[1], weights[3] = lax.optimization_barrier(
+        (line, weights[1], weights[3])
+    )
     plane = jnp.stack([line] + [first_turn(line, k) for k in (1, 2, 3)])
     parts = call(partials, "partials", [shape((128, 128), f32)] * 4, [VMEM] * 5)(
         *weights, plane
@@ -191,29 +201,27 @@
         first, total, jnp.concatenate([total[64:], total[:64]], axis=0)
     ).astype(bf16)
 
-    near = swap_cores(pre)
-    act = jnp.where(first, pre, near)
-    grad = jnp.where(first, near, pre)
-    pair = jnp.stack(
-        [
-            jnp.concatenate([to_parity(act, j, 0), to_parity(act, j, 1)], axis=1)
-            for j in (0, 1)
-        ]
-    )
-    grad = jnp.concatenate([grad, swap_reps(grad)], axis=1)
+    far = swap_reps(pre)
+    low_rep = lax.axis_index("rep") == 0
+    pre = jnp.concatenate(
+        [jnp.where(low_rep, pre, far), jnp.where(low_rep, far, pre)], axis=1
+    )
+    got = on_ring(pre, (-1, 0), (1, 0))
+    act = jnp.where(first, pre, got)
+    grad = jnp.where(first, got, pre)
+    pair = jnp.stack([act, on_ring(act, (1, -1), (0, 1))])
+    grads = jnp.stack([grad, third_pair(grad, 1)])
     plane = jnp.stack([pair] + [first_turn(pair, k) for k in (1, 2, 3)])
-    grads = [grad] + [second_turn(grad, k) for k in (1, 2, 3)]
-    made = call(tiles, "tiles", [shape((128, 1024), bf16)] * 4, [VMEM] * 5)(
-        *grads, plane
-    )
+    grads = jnp.concatenate([grads, third_pair(grads, 3)], axis=0)
+    made = call(
+        tiles, "tiles", [shape((128, 1024), bf16)] * 4, [SMEM, VMEM, VMEM]
+    )(where, grads, plane)
     whole = [made[0]] + [second_turn(made[k], k) for k in (1, 2, 3)]
-    low = jnp.stack([e[:64] for e in whole])
-    high = jnp.stack([e[64:] for e in whole])
-    own = jnp.where(first, low, high)
-    sibling = swap_cores(jnp.where(first, high, low))
+    own = [jnp.where(first, e[:64], e[64:]) for e in whole]
+    sibling = [swap_cores(jnp.where(first, e[64:], e[:64])) for e in whole]
     return call(
-        assemble, "assemble", shape((64, 8192), f32), [SMEM, VMEM, VMEM]
-    )(where, own, sibling)
+        assemble, "assemble", shape((64, 8192), f32), [SMEM] + [VMEM] * 8
+    )(where, *own, *sibling)
 
 
 def solution(mesh):

time: 92.7 us -> 88.7 us (0.957)
  waiting for transfers between devices: 39.1 us -> 29.9 us
  starting transfers between devices: 44.9 us -> 49.7 us
    ppermute x30 -> x29, waiting for transfers between devices: 39.1 us -> 29.9 us  [send(): return lax.ppermute(value, AXES, pairs)]
    ppermute x30 -> x29, starting transfers between devices: 44.9 us -> 49.7 us  [send(): return lax.ppermute(value, AXES, pairs)]
  transfers between devices with their start and end apart: 30 -> 29, of which waited for: 18 -> 18; matrix products, arithmetic and copies ran while one was open for 1% -> 1% of each run, Pallas kernels for 0% -> 0%
where the time goes in v3:
time: 88.7 us; the launch traced here: 88.5 us
  starting transfers between devices  49.7 us (56%)
  waiting for transfers between devices  29.9 us (34%)
  Pallas kernels  5.39 us (6%)
  local copies, waits for them, and re-layouts  2.61 us (3%)
    ppermute x29, starting transfers between devices, send(): return lax.ppermute(value, AXES, pairs)  49.7 us
    ppermute x29, waiting for transfers between devices, send(): return lax.ppermute(value, AXES, pairs)  29.9 us
    unnamed x8, local copies, waits for them, and re-layouts  2.46 us
    pallas_call x1, Pallas kernels, on_device(): call(assemble, 'assemble', shape((64, 8192), f32), [SMEM] + [VMEM] * 8)  2.22 us
  transfers between devices with their start and end apart: 29, of which 18 were waited for; matrix products, arithmetic and copies ran while one was open for 1% of the time, Pallas kernels for 0%

profile of v3, /device:TPU:1, one launch (start us, length us, event | category | flops | bytes accessed | tf_op | source)
XLA Modules:
  0.0 88.5 jit_solution(1018462306069082691)
XLA Ops:
  0.1 1.2 %copy-done = bf16[64,8192]{1,0:T(8,128)(2,1)S(1)} copy-done((bf16[64,8192]{1,0:T(8,128)(2,1)S(1)}, bf16[64,8192]{1,0:T(8,128)(2,1)}, u32[]{:S(2)}) %copy-start) | copy-done | bytes 1048600
  1.3 1.2 %copy-done.1 = bf16[64,8192]{1,0:T(8,128)(2,1)S(1)} copy-done((bf16[64,8192]{1,0:T(8,128)(2,1)S(1)}, bf16[64,8192]{1,0:T(8,128)(2,1)}, u32[]{:S(2)}) %copy-start.1) | copy-done | bytes 1048600
  2.5 1.1 %arrange.1 = (bf16[4,64,2048]{2,1,0:T(8,128)(2,1)S(1)}, bf16[4,64,2048]{2,1,0:T(8,128)(2,1)S(1)}) custom-call(s32[4]{0:T(128)S(1)} %pad_add_fusion.where, bf16[64,8192]{1,0:T(8,128)(2,1)S(1)} %copy-done, bf16[64,8192]{1,0:T(8,128)(2,1)S(1)} %copy-done.1), custom_call_target="tpu_custom_call" | custom-call | tf_op jit(solution)/shard_map/arrange/pallas_call | solution.py:182
  3.7 3.3 %collective-permute-start = (bf16[4,64,2048]{2,1,0:T(8,128)(2,1)S(1)}, bf16[4,64,2048]{2,1,0:T(8,128)(2,1)S(1)}, u32[]{:S(2)}, u32[]{:S(2)}) collective-permute-start(bf16[4,64,2048]{2,1,0:T(8,128)(2,1)S(1)} %get-tuple-element.19), channel_id=1, source_target_pairs={{0,1},{1,0},{2,3},{3,2},{4,5},{5,4},{6,7},{7,6},{8,9},{9,8},{10,11... | collective-permute-start | bytes 3145736 | tf_op jit(solution)/shard_map/ppermute | solution.py:30
  7.2 2.1 %collective-permute-done = bf16[4,64,2048]{2,1,0:T(8,128)(2,1)S(1)} collective-permute-done((bf16[4,64,2048]{2,1,0:T(8,128)(2,1)S(1)}, bf16[4,64,2048]{2,1,0:T(8,128)(2,1)S(1)}, u32[]{:S(2)}, u32[]{:S(2)}) %collective-permute-start) | collective-permute-done | bytes 1048608 | tf_op jit(solution)/shard_map/ppermute | solution.py:30
  9.6 2.7 %collective-permute-start.6 = (bf16[2,64,2048]{2,1,0:T(8,128)(2,1)S(1)}, bf16[2,64,2048]{2,1,0:T(8,128)(2,1)S(1)}, u32[]{:S(2)}, u32[]{:S(2)}) collective-permute-start(bf16[2,64,2048]{2,1,0:T(8,128)(2,1)S(1)} %pad_maximum_fusion.2), channel_id=1, source_target_pairs={{0,6},{1,25},{2,0},{3,27},{4,2},{5,29},{6,4},{7,31},{8,14},{9,1},{... | collective-permute-start | bytes 1572872 | tf_op jit(solution)/shard_map/ppermute | solution.py:30
  12.3 2.8 %collective-permute-start.4 = (bf16[128,128]{1,0:T(8,128)(2,1)S(1)}, bf16[128,128]{1,0:T(8,128)(2,1)S(1)}, u32[]{:S(2)}, u32[]{:S(2)}) collective-permute-start(bf16[128,128]{1,0:T(8,128)(2,1)S(1)} %get-tuple-element.58), channel_id=1, source_target_pairs={{0,96},{1,97},{2,98},{3,99},{4,100},{5,101},{6,102},{7,103},{8,104... | collective-permute-start | bytes 98312 | tf_op jit(solution)/shard_map/ppermute | solution.py:30
  15.1 1.7 %collective-permute-start.7 = (bf16[2,64,2048]{2,1,0:T(8,128)(2,1)S(1)}, bf16[2,64,2048]{2,1,0:T(8,128)(2,1)S(1)}, u32[]{:S(2)}, u32[]{:S(2)}) collective-permute-start(bf16[2,64,2048]{2,1,0:T(8,128)(2,1)S(1)} %pad_maximum_fusion.3), channel_id=1, source_target_pairs={{0,4},{1,17},{2,6},{3,19},{4,0},{5,21},{6,2},{7,23},{8,12},{9,25},... | collective-permute-start | bytes 1572872 | tf_op jit(solution)/shard_map/ppermute | solution.py:30
  17.2 3.4 %collective-permute-done.3 = bf16[128,128]{1,0:T(8,128)(2,1)S(1)} collective-permute-done((bf16[128,128]{1,0:T(8,128)(2,1)S(1)}, bf16[128,128]{1,0:T(8,128)(2,1)S(1)}, u32[]{:S(2)}, u32[]{:S(2)}) %collective-permute-start.3) | collective-permute-done | bytes 32800 | tf_op jit(solution)/shard_map/ppermute | solution.py:30
  20.5 1.2 %collective-permute-done.2 = bf16[128,128]{1,0:T(8,128)(2,1)S(1)} collective-permute-done((bf16[128,128]{1,0:T(8,128)(2,1)S(1)}, bf16[128,128]{1,0:T(8,128)(2,1)S(1)}, u32[]{:S(2)}, u32[]{:S(2)}) %collective-permute-start.2) | collective-permute-done | bytes 32800 | tf_op jit(solution)/shard_map/ppermute | solution.py:30
  21.8 2.3 %collective-permute-done.6.w3 = bf16[2,64,2048]{2,1,0:T(8,128)(2,1)S(1)} collective-permute-done((bf16[2,64,2048]{2,1,0:T(8,128)(2,1)S(1)}, bf16[2,64,2048]{2,1,0:T(8,128)(2,1)S(1)}, u32[]{:S(2)}, u32[]{:S(2)}) %collective-permute-start.6) | collective-permute-done | bytes 524320 | tf_op jit(solution)/shard_map/ppermute | solution.py:30
  25.6 2.3 %collective-permute-done.10 = bf16[4,128,128]{2,1,0:T(8,128)(2,1)S(1)} collective-permute-done((bf16[4,128,128]{2,1,0:T(8,128)(2,1)S(1)}, bf16[4,128,128]{2,1,0:T(8,128)(2,1)S(1)}, u32[]{:S(2)}, u32[]{:S(2)}) %collective-permute-start.10) | collective-permute-done | bytes 131104 | tf_op jit(solution)/shard_map/ppermute | solution.py:30
  27.9 2.0 %collective-permute-done.9 = bf16[4,128,128]{2,1,0:T(8,128)(2,1)S(1)} collective-permute-done((bf16[4,128,128]{2,1,0:T(8,128)(2,1)S(1)}, bf16[4,128,128]{2,1,0:T(8,128)(2,1)S(1)}, u32[]{:S(2)}, u32[]{:S(2)}) %collective-permute-start.9) | collective-permute-done | bytes 131104 | tf_op jit(solution)/shard_map/ppermute | solution.py:30
  29.8 1.3 %collective-permute-done.8 = bf16[4,128,128]{2,1,0:T(8,128)(2,1)S(1)} collective-permute-done((bf16[4,128,128]{2,1,0:T(8,128)(2,1)S(1)}, bf16[4,128,128]{2,1,0:T(8,128)(2,1)S(1)}, u32[]{:S(2)}, u32[]{:S(2)}) %collective-permute-start.8) | collective-permute-done | bytes 131104 | tf_op jit(solution)/shard_map/ppermute | solution.py:30
  31.9 3.1 %collective-permute-start.13 = (f32[128,128]{1,0:T(8,128)S(1)}, f32[128,128]{1,0:T(8,128)S(1)}, u32[]{:S(2)}, u32[]{:S(2)}) collective-permute-start(f32[128,128]{1,0:T(8,128)S(1)} %get-tuple-element.26), channel_id=1, source_target_pairs={{0,6},{1,25},{2,0},{3,27},{4,2},{5,29},{6,4},{7,31},{8,14},{9,1},{... | collective-permute-start | bytes 196616 | tf_op jit(solution)/shard_map/ppermute | solution.py:30
  36.4 3.4 %collective-permute-done.12 = f32[128,128]{1,0:T(8,128)S(1)} collective-permute-done((f32[128,128]{1,0:T(8,128)S(1)}, f32[128,128]{1,0:T(8,128)S(1)}, u32[]{:S(2)}, u32[]{:S(2)}) %collective-permute-start.12) | collective-permute-done | bytes 65568 | tf_op jit(solution)/shard_map/ppermute | solution.py:30
  40.1 8.0 %collective-permute-start.14 = (bf16[128,128]{1,0:T(8,128)(2,1)S(1)}, bf16[128,128]{1,0:T(8,128)(2,1)S(1)}, u32[]{:S(2)}, u32[]{:S(2)}) collective-permute-start(bf16[128,128]{1,0:T(8,128)(2,1)S(1)} %fusion), channel_id=1, source_target_pairs={{0,128},{1,129},{2,130},{3,131},{4,132},{5,133},{6,134},{7,135},{8... | collective-permute-start | bytes 98312 | tf_op jit(solution)/shard_map/ppermute | solution.py:30
  48.1 1.3 %collective-permute-done.14 = bf16[128,128]{1,0:T(8,128)(2,1)S(1)} collective-permute-done((bf16[128,128]{1,0:T(8,128)(2,1)S(1)}, bf16[128,128]{1,0:T(8,128)(2,1)S(1)}, u32[]{:S(2)}, u32[]{:S(2)}) %collective-permute-start.14) | collective-permute-done | bytes 32800 | tf_op jit(solution)/shard_map/ppermute | solution.py:30
  49.5 5.3 %collective-permute-start.15 = (bf16[128,256]{1,0:T(8,128)(2,1)S(1)}, bf16[128,256]{1,0:T(8,128)(2,1)S(1)}, u32[]{:S(2)}, u32[]{:S(2)}) collective-permute-start(bf16[128,256]{1,0:T(8,128)(2,1)S(1)} %pad_maximum_fusion.10), channel_id=1, source_target_pairs={{0,225},{1,0},{2,227},{3,2},{4,229},{5,4},{6,231},{7,6},{8,233},{9... | collective-permute-start | bytes 196616 | tf_op jit(solution)/shard_map/ppermute | solution.py:30
  54.8 2.6 %collective-permute-done.15 = bf16[128,256]{1,0:T(8,128)(2,1)S(1)} collective-permute-done((bf16[128,256]{1,0:T(8,128)(2,1)S(1)}, bf16[128,256]{1,0:T(8,128)(2,1)S(1)}, u32[]{:S(2)}, u32[]{:S(2)}) %collective-permute-start.15) | collective-permute-done | bytes 65568 | tf_op jit(solution)/shard_map/ppermute | solution.py:30
  57.4 2.7 %collective-permute-start.18 = (bf16[128,256]{1,0:T(8,128)(2,1)S(1)}, bf16[128,256]{1,0:T(8,128)(2,1)S(1)}, u32[]{:S(2)}, u32[]{:S(2)}) collective-permute-start(bf16[128,256]{1,0:T(8,128)(2,1)S(1)} %get-tuple-element.49), channel_id=1, source_target_pairs={{0,32},{1,225},{2,34},{3,227},{4,36},{5,229},{6,38},{7,231},{8,40}... | collective-permute-start | bytes 196616 | tf_op jit(solution)/shard_map/ppermute | solution.py:30
  60.1 1.3 %collective-permute-done.18 = bf16[128,256]{1,0:T(8,128)(2,1)S(1)} collective-permute-done((bf16[128,256]{1,0:T(8,128)(2,1)S(1)}, bf16[128,256]{1,0:T(8,128)(2,1)S(1)}, u32[]{:S(2)}, u32[]{:S(2)}) %collective-permute-start.18) | collective-permute-done | bytes 65568 | tf_op jit(solution)/shard_map/ppermute | solution.py:30
  62.1 0.9 collective-permute-start.20
  64.3 1.1 %collective-permute-done.21 = bf16[2,128,256]{2,1,0:T(8,128)(2,1)S(1)} collective-permute-done((bf16[2,128,256]{2,1,0:T(8,128)(2,1)S(1)}, bf16[2,128,256]{2,1,0:T(8,128)(2,1)S(1)}, u32[]{:S(2)}, u32[]{:S(2)}) %collective-permute-start.21) | collective-permute-done | bytes 131104 | tf_op jit(solution)/shard_map/ppermute | solution.py:30
  65.4 2.2 %collective-permute-done.20 = bf16[2,128,256]{2,1,0:T(8,128)(2,1)S(1)} collective-permute-done((bf16[2,128,256]{2,1,0:T(8,128)(2,1)S(1)}, bf16[2,128,256]{2,1,0:T(8,128)(2,1)S(1)}, u32[]{:S(2)}, u32[]{:S(2)}) %collective-permute-start.20) | collective-permute-done | bytes 131104 | tf_op jit(solution)/shard_map/ppermute | solution.py:30
  67.5 1.6 %collective-permute-done.19 = bf16[2,128,256]{2,1,0:T(8,128)(2,1)S(1)} collective-permute-done((bf16[2,128,256]{2,1,0:T(8,128)(2,1)S(1)}, bf16[2,128,256]{2,1,0:T(8,128)(2,1)S(1)}, u32[]{:S(2)}, u32[]{:S(2)}) %collective-permute-start.19) | collective-permute-done | bytes 131104 | tf_op jit(solution)/shard_map/ppermute | solution.py:30
  69.2 1.4 %tiles.1 = (bf16[128,1024]{1,0:T(8,128)(2,1)S(1)}, bf16[128,1024]{1,0:T(8,128)(2,1)S(1)}, bf16[128,1024]{1,0:T(8,128)(2,1)S(1)}, bf16[128,1024]{1,0:T(8,128)(2,1)S(1)}) custom-call(s32[4]{0:T(128)S(1)} %pad_add_fusion.where, bf16[4,128,256]{2,1,0:T(8,128)(2,1)S(1)} %pad_maximum_fusion.6.g, bf16[4,2,128,256]{3,2,1,0:T(8,128)(2,1)S(1)} %pad_maximum_fusion.5.plane), custom_call_target="tpu_custom_call" | custom-call | tf_op jit(solution)/shard_map/tiles/pallas_call | solution.py:216
  70.7 2.7 %collective-permute-start.23 = (bf16[128,1024]{1,0:T(8,128)(2,1)S(1)}, bf16[128,1024]{1,0:T(8,128)(2,1)S(1)}, u32[]{:S(2)}, u32[]{:S(2)}) collective-permute-start(bf16[128,1024]{1,0:T(8,128)(2,1)S(1)} %get-tuple-element.29), channel_id=1, source_target_pairs={{0,4},{1,17},{2,6},{3,19},{4,0},{5,21},{6,2},{7,23},{8,12},{9,25},... | collective-permute-start | bytes 786440 | tf_op jit(solution)/shard_map/ppermute | solution.py:30
  73.5 6.1 %collective-permute-start.25 = (bf16[64,1024]{1,0:T(8,128)(2,1)S(1)}, bf16[64,1024]{1,0:T(8,128)(2,1)S(1)}, u32[]{:S(2)}, u32[]{:S(2)}) collective-permute-start(bf16[64,1024]{1,0:T(8,128)(2,1)S(1)} %get-tuple-element.45), channel_id=1, source_target_pairs={{0,1},{1,0},{2,3},{3,2},{4,5},{5,4},{6,7},{7,6},{8,9},{9,8},{10,11... | collective-permute-start | bytes 393224 | tf_op jit(solution)/shard_map/ppermute | solution.py:30
  79.7 1.9 %collective-permute-start.26 = (bf16[64,1024]{1,0:T(8,128)(2,1)S(1)}, bf16[64,1024]{1,0:T(8,128)(2,1)S(1)}, u32[]{:S(2)}, u32[]{:S(2)}) collective-permute-start(bf16[64,1024]{1,0:T(8,128)(2,1)S(1)} %get-tuple-element.43), channel_id=1, source_target_pairs={{0,1},{1,0},{2,3},{3,2},{4,5},{5,4},{6,7},{7,6},{8,9},{9,8},{10,11... | collective-permute-start | bytes 393224 | tf_op jit(solution)/shard_map/ppermute | solution.py:30
  81.7 3.2 %collective-permute-start.27 = (bf16[64,1024]{1,0:T(8,128)(2,1)S(1)}, bf16[64,1024]{1,0:T(8,128)(2,1)S(1)}, u32[]{:S(2)}, u32[]{:S(2)}) collective-permute-start(bf16[64,1024]{1,0:T(8,128)(2,1)S(1)} %get-tuple-element.41), channel_id=1, source_target_pairs={{0,1},{1,0},{2,3},{3,2},{4,5},{5,4},{6,7},{7,6},{8,9},{9,8},{10,11... | collective-permute-start | bytes 393224 | tf_op jit(solution)/shard_map/ppermute | solution.py:30
  86.3 2.2 %assemble.1 = f32[64,8192]{1,0:T(8,128)} custom-call(s32[4]{0:T(128)S(1)} %pad_add_fusion.where, bf16[64,1024]{1,0:T(8,128)(2,1)S(1)} %get-tuple-element.46.refs_0_, bf16[64,1024]{1,0:T(8,128)(2,1)S(1)} %get-tuple-element.44.refs_1_, bf16[64,1024]{1,0:T(8,128)(2,1)S(1)} %get-tuple-element.42.refs_2_, bf16[64,1024]{1,0:T(8,128)(2,1)S(1)} %get-tuple-element.40.refs_3_, ...), custom_call_target="tpu_custom_call" | custom-call | tf_op jit(solution)/shard_map/assemble/pallas_call | solution.py:222
  (64 shorter events, 8.7 us)
Async XLA Ops:
  0.0 7.0 %copy-start.2 = (bf16[128,64]{0,1:T(8,128)(2,1)S(1)}, bf16[128,64]{0,1:T(8,128)(2,1)}, u32[]{:S(2)}) copy-start(bf16[128,64]{0,1:T(8,128)(2,1)} %param.5) | copy-start | bytes 49156
  0.0 7.0 %copy-start.3 = (bf16[128,64]{0,1:T(8,128)(2,1)S(1)}, bf16[128,64]{0,1:T(8,128)(2,1)}, u32[]{:S(2)}) copy-start(bf16[128,64]{0,1:T(8,128)(2,1)} %param.4) | copy-start | bytes 49156
  0.1 1.2 %copy-start = (bf16[64,8192]{1,0:T(8,128)(2,1)S(1)}, bf16[64,8192]{1,0:T(8,128)(2,1)}, u32[]{:S(2)}) copy-start(bf16[64,8192]{1,0:T(8,128)(2,1)} %act_rows.1) | copy-start | bytes 3145732
  3.7 5.6 %collective-permute-start = (bf16[4,64,2048]{2,1,0:T(8,128)(2,1)S(1)}, bf16[4,64,2048]{2,1,0:T(8,128)(2,1)S(1)}, u32[]{:S(2)}, u32[]{:S(2)}) collective-permute-start(bf16[4,64,2048]{2,1,0:T(8,128)(2,1)S(1)} %get-tuple-element.19), channel_id=1, source_target_pairs={{0,1},{1,0},{2,3},{3,2},{4,5},{5,4},{6,7},{7,6},{8,9},{9,8},{10,11... | collective-permute-start | bytes 3145736 | tf_op jit(solution)/shard_map/ppermute | solution.py:30
  7.0 5.3 %collective-permute-start.1 = (bf16[64,128]{1,0:T(8,128)(2,1)S(1)}, bf16[64,128]{1,0:T(8,128)(2,1)S(1)}, u32[]{:S(2)}, u32[]{:S(2)}) collective-permute-start(bf16[64,128]{1,0:T(8,128)(2,1)S(1)} %select_bitcast_fusion), channel_id=1, source_target_pairs={{0,1},{1,0},{2,3},{3,2},{4,5},{5,4},{6,7},{7,6},{8,9},{9,8},{10,11... | collective-permute-start | bytes 49160 | tf_op jit(solution)/shard_map/ppermute | solution.py:30
  9.4 12.3 %collective-permute-start.5 = (bf16[2,64,2048]{2,1,0:T(8,128)(2,1)S(1)}, bf16[2,64,2048]{2,1,0:T(8,128)(2,1)S(1)}, u32[]{:S(2)}, u32[]{:S(2)}) collective-permute-start(bf16[2,64,2048]{2,1,0:T(8,128)(2,1)S(1)} %pad_maximum_fusion.1), channel_id=1, source_target_pairs={{0,2},{1,9},{2,4},{3,11},{4,6},{5,13},{6,0},{7,15},{8,10},{9,17},{... | collective-permute-start | bytes 1572872 | tf_op jit(solution)/shard_map/ppermute | solution.py:30
  9.6 14.5 %collective-permute-start.6 = (bf16[2,64,2048]{2,1,0:T(8,128)(2,1)S(1)}, bf16[2,64,2048]{2,1,0:T(8,128)(2,1)S(1)}, u32[]{:S(2)}, u32[]{:S(2)}) collective-permute-start(bf16[2,64,2048]{2,1,0:T(8,128)(2,1)S(1)} %pad_maximum_fusion.2), channel_id=1, source_target_pairs={{0,6},{1,25},{2,0},{3,27},{4,2},{5,29},{6,4},{7,31},{8,14},{9,1},{... | collective-permute-start | bytes 1572872 | tf_op jit(solution)/shard_map/ppermute | solution.py:30
  12.3 4.5 %collective-permute-start.4 = (bf16[128,128]{1,0:T(8,128)(2,1)S(1)}, bf16[128,128]{1,0:T(8,128)(2,1)S(1)}, u32[]{:S(2)}, u32[]{:S(2)}) collective-permute-start(bf16[128,128]{1,0:T(8,128)(2,1)S(1)} %get-tuple-element.58), channel_id=1, source_target_pairs={{0,96},{1,97},{2,98},{3,99},{4,100},{5,101},{6,102},{7,103},{8,104... | collective-permute-start | bytes 98312 | tf_op jit(solution)/shard_map/ppermute | solution.py:30
  15.1 16.1 %collective-permute-start.7 = (bf16[2,64,2048]{2,1,0:T(8,128)(2,1)S(1)}, bf16[2,64,2048]{2,1,0:T(8,128)(2,1)S(1)}, u32[]{:S(2)}, u32[]{:S(2)}) collective-permute-start(bf16[2,64,2048]{2,1,0:T(8,128)(2,1)S(1)} %pad_maximum_fusion.3), channel_id=1, source_target_pairs={{0,4},{1,17},{2,6},{3,19},{4,0},{5,21},{6,2},{7,23},{8,12},{9,25},... | collective-permute-start | bytes 1572872 | tf_op jit(solution)/shard_map/ppermute | solution.py:30
  16.9 3.7 %collective-permute-start.3 = (bf16[128,128]{1,0:T(8,128)(2,1)S(1)}, bf16[128,128]{1,0:T(8,128)(2,1)S(1)}, u32[]{:S(2)}, u32[]{:S(2)}) collective-permute-start(bf16[128,128]{1,0:T(8,128)(2,1)S(1)} %get-tuple-element.58), channel_id=1, source_target_pairs={{0,64},{1,65},{2,66},{3,67},{4,68},{5,69},{6,70},{7,71},{8,72},{9,... | collective-permute-start | bytes 98312 | tf_op jit(solution)/shard_map/ppermute | solution.py:30
  16.9 4.9 %collective-permute-start.2 = (bf16[128,128]{1,0:T(8,128)(2,1)S(1)}, bf16[128,128]{1,0:T(8,128)(2,1)S(1)}, u32[]{:S(2)}, u32[]{:S(2)}) collective-permute-start(bf16[128,128]{1,0:T(8,128)(2,1)S(1)} %get-tuple-element.58), channel_id=1, source_target_pairs={{0,32},{1,33},{2,34},{3,35},{4,36},{5,37},{6,38},{7,39},{8,40},{9,... | collective-permute-start | bytes 98312 | tf_op jit(solution)/shard_map/ppermute | solution.py:30
  24.0 3.8 %collective-permute-start.10 = (bf16[4,128,128]{2,1,0:T(8,128)(2,1)S(1)}, bf16[4,128,128]{2,1,0:T(8,128)(2,1)S(1)}, u32[]{:S(2)}, u32[]{:S(2)}) collective-permute-start(bf16[4,128,128]{2,1,0:T(8,128)(2,1)S(1)} %pad_maximum_fusion.7), channel_id=1, source_target_pairs={{0,24},{1,7},{2,26},{3,1},{4,28},{5,3},{6,30},{7,5},{8,0},{9,15},{... | collective-permute-start | bytes 393224 | tf_op jit(solution)/shard_map/ppermute | solution.py:30
  24.4 5.4 %collective-permute-start.9 = (bf16[4,128,128]{2,1,0:T(8,128)(2,1)S(1)}, bf16[4,128,128]{2,1,0:T(8,128)(2,1)S(1)}, u32[]{:S(2)}, u32[]{:S(2)}) collective-permute-start(bf16[4,128,128]{2,1,0:T(8,128)(2,1)S(1)} %pad_maximum_fusion.7), channel_id=1, source_target_pairs={{0,16},{1,5},{2,18},{3,7},{4,20},{5,1},{6,22},{7,3},{8,24},{9,13},... | collective-permute-start | bytes 393224 | tf_op jit(solution)/shard_map/ppermute | solution.py:30
  24.7 6.4 %collective-permute-start.8 = (bf16[4,128,128]{2,1,0:T(8,128)(2,1)S(1)}, bf16[4,128,128]{2,1,0:T(8,128)(2,1)S(1)}, u32[]{:S(2)}, u32[]{:S(2)}) collective-permute-start(bf16[4,128,128]{2,1,0:T(8,128)(2,1)S(1)} %pad_maximum_fusion.7), channel_id=1, source_target_pairs={{0,8},{1,3},{2,10},{3,5},{4,12},{5,7},{6,14},{7,1},{8,16},{9,11},{... | collective-permute-start | bytes 393224 | tf_op jit(solution)/shard_map/ppermute | solution.py:30
  31.9 4.5 %collective-permute-start.13 = (f32[128,128]{1,0:T(8,128)S(1)}, f32[128,128]{1,0:T(8,128)S(1)}, u32[]{:S(2)}, u32[]{:S(2)}) collective-permute-start(f32[128,128]{1,0:T(8,128)S(1)} %get-tuple-element.26), channel_id=1, source_target_pairs={{0,6},{1,25},{2,0},{3,27},{4,2},{5,29},{6,4},{7,31},{8,14},{9,1},{... | collective-permute-start | bytes 196616 | tf_op jit(solution)/shard_map/ppermute | solution.py:30
  35.0 4.7 %collective-permute-start.12 = (f32[128,128]{1,0:T(8,128)S(1)}, f32[128,128]{1,0:T(8,128)S(1)}, u32[]{:S(2)}, u32[]{:S(2)}) collective-permute-start(f32[128,128]{1,0:T(8,128)S(1)} %get-tuple-element.25), channel_id=1, source_target_pairs={{0,4},{1,17},{2,6},{3,19},{4,0},{5,21},{6,2},{7,23},{8,12},{9,25},... | collective-permute-start | bytes 196616 | tf_op jit(solution)/shard_map/ppermute | solution.py:30
  35.0 5.0 %collective-permute-start.11 = (f32[128,128]{1,0:T(8,128)S(1)}, f32[128,128]{1,0:T(8,128)S(1)}, u32[]{:S(2)}, u32[]{:S(2)}) collective-permute-start(f32[128,128]{1,0:T(8,128)S(1)} %get-tuple-element.24), channel_id=1, source_target_pairs={{0,2},{1,9},{2,4},{3,11},{4,6},{5,13},{6,0},{7,15},{8,10},{9,17},{... | collective-permute-start | bytes 196616 | tf_op jit(solution)/shard_map/ppermute | solution.py:30
  40.1 9.3 %collective-permute-start.14 = (bf16[128,128]{1,0:T(8,128)(2,1)S(1)}, bf16[128,128]{1,0:T(8,128)(2,1)S(1)}, u32[]{:S(2)}, u32[]{:S(2)}) collective-permute-start(bf16[128,128]{1,0:T(8,128)(2,1)S(1)} %fusion), channel_id=1, source_target_pairs={{0,128},{1,129},{2,130},{3,131},{4,132},{5,133},{6,134},{7,135},{8... | collective-permute-start | bytes 98312 | tf_op jit(solution)/shard_map/ppermute | solution.py:30
  49.5 7.9 %collective-permute-start.15 = (bf16[128,256]{1,0:T(8,128)(2,1)S(1)}, bf16[128,256]{1,0:T(8,128)(2,1)S(1)}, u32[]{:S(2)}, u32[]{:S(2)}) collective-permute-start(bf16[128,256]{1,0:T(8,128)(2,1)S(1)} %pad_maximum_fusion.10), channel_id=1, source_target_pairs={{0,225},{1,0},{2,227},{3,2},{4,229},{5,4},{6,231},{7,6},{8,233},{9... | collective-permute-start | bytes 196616 | tf_op jit(solution)/shard_map/ppermute | solution.py:30
  57.4 4.0 %collective-permute-start.18 = (bf16[128,256]{1,0:T(8,128)(2,1)S(1)}, bf16[128,256]{1,0:T(8,128)(2,1)S(1)}, u32[]{:S(2)}, u32[]{:S(2)}) collective-permute-start(bf16[128,256]{1,0:T(8,128)(2,1)S(1)} %get-tuple-element.49), channel_id=1, source_target_pairs={{0,32},{1,225},{2,34},{3,227},{4,36},{5,229},{6,38},{7,231},{8,40}... | collective-permute-start | bytes 196616 | tf_op jit(solution)/shard_map/ppermute | solution.py:30
  60.1 3.6 %collective-permute-start.16 = (bf16[128,256]{1,0:T(8,128)(2,1)S(1)}, bf16[128,256]{1,0:T(8,128)(2,1)S(1)}, u32[]{:S(2)}, u32[]{:S(2)}) collective-permute-start(bf16[128,256]{1,0:T(8,128)(2,1)S(1)} %get-tuple-element.50), channel_id=1, source_target_pairs={{0,2},{1,9},{2,0},{3,11},{4,6},{5,13},{6,4},{7,15},{8,10},{9,1},{1... | collective-permute-start | bytes 196616 | tf_op jit(solution)/shard_map/ppermute | solution.py:30
  61.5 3.9 %collective-permute-start.21 = (bf16[2,128,256]{2,1,0:T(8,128)(2,1)S(1)}, bf16[2,128,256]{2,1,0:T(8,128)(2,1)S(1)}, u32[]{:S(2)}, u32[]{:S(2)}) collective-permute-start(bf16[2,128,256]{2,1,0:T(8,128)(2,1)S(1)} %get-tuple-element.48), channel_id=1, source_target_pairs={{0,24},{1,7},{2,26},{3,1},{4,28},{5,3},{6,30},{7,5},{8,0},{9,15},{... | collective-permute-start | bytes 393224 | tf_op jit(solution)/shard_map/ppermute | solution.py:30
  62.1 5.4 %collective-permute-start.20 = (bf16[2,128,256]{2,1,0:T(8,128)(2,1)S(1)}, bf16[2,128,256]{2,1,0:T(8,128)(2,1)S(1)}, u32[]{:S(2)}, u32[]{:S(2)}) collective-permute-start(bf16[2,128,256]{2,1,0:T(8,128)(2,1)S(1)} %get-tuple-element.48), channel_id=1, source_target_pairs={{0,16},{1,5},{2,18},{3,7},{4,20},{5,1},{6,22},{7,3},{8,24},{9,13},... | collective-permute-start | bytes 393224 | tf_op jit(solution)/shard_map/ppermute | solution.py:30
  63.0 6.2 %collective-permute-start.19 = (bf16[2,128,256]{2,1,0:T(8,128)(2,1)S(1)}, bf16[2,128,256]{2,1,0:T(8,128)(2,1)S(1)}, u32[]{:S(2)}, u32[]{:S(2)}) collective-permute-start(bf16[2,128,256]{2,1,0:T(8,128)(2,1)S(1)} %get-tuple-element.48), channel_id=1, source_target_pairs={{0,8},{1,3},{2,10},{3,5},{4,12},{5,7},{6,14},{7,1},{8,16},{9,11},{... | collective-permute-start | bytes 393224 | tf_op jit(solution)/shard_map/ppermute | solution.py:30
  63.7 5.5 %collective-permute-start.17 = (bf16[2,128,256]{2,1,0:T(8,128)(2,1)S(1)}, bf16[2,128,256]{2,1,0:T(8,128)(2,1)S(1)}, u32[]{:S(2)}, u32[]{:S(2)}) collective-permute-start(bf16[2,128,256]{2,1,0:T(8,128)(2,1)S(1)} %pad_maximum_fusion.8), channel_id=1, source_target_pairs={{0,6},{1,25},{2,4},{3,27},{4,2},{5,29},{6,0},{7,31},{8,14},{9,17},... | collective-permute-start | bytes 393224 | tf_op jit(solution)/shard_map/ppermute | solution.py:30
  70.6 9.0 %collective-permute-start.22 = (bf16[128,1024]{1,0:T(8,128)(2,1)S(1)}, bf16[128,1024]{1,0:T(8,128)(2,1)S(1)}, u32[]{:S(2)}, u32[]{:S(2)}) collective-permute-start(bf16[128,1024]{1,0:T(8,128)(2,1)S(1)} %get-tuple-element.28), channel_id=1, source_target_pairs={{0,2},{1,9},{2,4},{3,11},{4,6},{5,13},{6,0},{7,15},{8,10},{9,17},{... | collective-permute-start | bytes 786440 | tf_op jit(solution)/shard_map/ppermute | solution.py:30
  70.7 10.9 %collective-permute-start.23 = (bf16[128,1024]{1,0:T(8,128)(2,1)S(1)}, bf16[128,1024]{1,0:T(8,128)(2,1)S(1)}, u32[]{:S(2)}, u32[]{:S(2)}) collective-permute-start(bf16[128,1024]{1,0:T(8,128)(2,1)S(1)} %get-tuple-element.29), channel_id=1, source_target_pairs={{0,4},{1,17},{2,6},{3,19},{4,0},{5,21},{6,2},{7,23},{8,12},{9,25},... | collective-permute-start | bytes 786440 | tf_op jit(solution)/shard_map/ppermute | solution.py:30
  73.4 11.4 %collective-permute-start.24 = (bf16[128,1024]{1,0:T(8,128)(2,1)S(1)}, bf16[128,1024]{1,0:T(8,128)(2,1)S(1)}, u32[]{:S(2)}, u32[]{:S(2)}) collective-permute-start(bf16[128,1024]{1,0:T(8,128)(2,1)S(1)} %get-tuple-element.30), channel_id=1, source_target_pairs={{0,6},{1,25},{2,0},{3,27},{4,2},{5,29},{6,4},{7,31},{8,14},{9,1},{... | collective-permute-start | bytes 786440 | tf_op jit(solution)/shard_map/ppermute | solution.py:30
  73.5 11.8 %collective-permute-start.25 = (bf16[64,1024]{1,0:T(8,128)(2,1)S(1)}, bf16[64,1024]{1,0:T(8,128)(2,1)S(1)}, u32[]{:S(2)}, u32[]{:S(2)}) collective-permute-start(bf16[64,1024]{1,0:T(8,128)(2,1)S(1)} %get-tuple-element.45), channel_id=1, source_target_pairs={{0,1},{1,0},{2,3},{3,2},{4,5},{5,4},{6,7},{7,6},{8,9},{9,8},{10,11... | collective-permute-start | bytes 393224 | tf_op jit(solution)/shard_map/ppermute | solution.py:30
  79.7 5.6 %collective-permute-start.26 = (bf16[64,1024]{1,0:T(8,128)(2,1)S(1)}, bf16[64,1024]{1,0:T(8,128)(2,1)S(1)}, u32[]{:S(2)}, u32[]{:S(2)}) collective-permute-start(bf16[64,1024]{1,0:T(8,128)(2,1)S(1)} %get-tuple-element.43), channel_id=1, source_target_pairs={{0,1},{1,0},{2,3},{3,2},{4,5},{5,4},{6,7},{7,6},{8,9},{9,8},{10,11... | collective-permute-start | bytes 393224 | tf_op jit(solution)/shard_map/ppermute | solution.py:30
  81.7 4.2 %collective-permute-start.27 = (bf16[64,1024]{1,0:T(8,128)(2,1)S(1)}, bf16[64,1024]{1,0:T(8,128)(2,1)S(1)}, u32[]{:S(2)}, u32[]{:S(2)}) collective-permute-start(bf16[64,1024]{1,0:T(8,128)(2,1)S(1)} %get-tuple-element.41), channel_id=1, source_target_pairs={{0,1},{1,0},{2,3},{3,2},{4,5},{5,4},{6,7},{7,6},{8,9},{9,8},{10,11... | collective-permute-start | bytes 393224 | tf_op jit(solution)/shard_map/ppermute | solution.py:30
  84.9 1.4 %collective-permute-start.28 = (bf16[64,1024]{1,0:T(8,128)(2,1)S(1)}, bf16[64,1024]{1,0:T(8,128)(2,1)S(1)}, u32[]{:S(2)}, u32[]{:S(2)}) collective-permute-start(bf16[64,1024]{1,0:T(8,128)(2,1)S(1)} %get-tuple-element.39), channel_id=1, source_target_pairs={{0,1},{1,0},{2,3},{3,2},{4,5},{5,4},{6,7},{7,6},{8,9},{9,8},{10,11... | collective-permute-start | bytes 393224 | tf_op jit(solution)/shard_map/ppermute | solution.py:30
  (1 other events, 1.2 us)

commit v4 on v3

--- a/solution.py
+++ b/solution.py
@@ -1,3 +1,5 @@
+import functools
+
 import jax
 import jax.numpy as jnp
 from jax import lax
@@ -34,12 +36,8 @@
     return send(value, lambda r, zl, y, x, c: (r, zl, y, x, 1 - c))
 
 
-def swap_reps(value):
-    return send(value, lambda r, zl, y, x, c: (1 - r, zl, y, x, c))
-
-
 def along_line(value, k):
-    return send(value, lambda r, zl, y, x, c: (r, zl + k, y, x, c))
+    return send(value, lambda r, zl, y, x, c: (r, zl ^ k, y, x, c))
 
 
 def first_turn(value, k):
@@ -64,6 +62,11 @@
     return send(value, target)
 
 
+def turned(turn, values):
+    got = {k: turn(values[k], k) for k in (1, 3, 2)}
+    return [values[0]] + [got[k] for k in (1, 2, 3)]
+
+
 def third_pair(value, k):
     return send(
         value,
@@ -79,17 +82,28 @@
     return lax.rem(at + 4 - k, 4)
 
 
-def arrange(where, act_rows, grad_rows, mine, other):
+def arrange(where, act_hbm, grad_hbm, mine, other, act_rows, grad_rows, sems):
     zl, y, x, core = (where[i] for i in range(4))
+    copies = []
+    for n, (far, near) in enumerate(((act_hbm, act_rows), (grad_hbm, grad_rows))):
+        for i in range(4):
+            part = pl.ds(i * 16, 16)
+            copies.append(
+                pltpu.make_async_copy(far.at[part], near.at[part], sems.at[n * 4 + i])
+            )
+    for copy in copies:
+        copy.start()
+    for copy in copies:
+        copy.wait()
 
     def write(rows, out, role):
         for k in range(4):
             for k2 in range(4):
                 for kz in range(4):
                     if role == 0:
-                        at = column(back(zl, kz), back(y, k2), lax.rem(x + k, 4))
+                        at = column(zl ^ kz, back(y, k2), lax.rem(x + k, 4))
                     else:
-                        at = column(back(zl, kz), lax.rem(y + k, 4), back(x, k2))
+                        at = column(zl ^ kz, lax.rem(y + k, 4), back(x, k2))
                     b = (k2 * 4 + kz) * 128
                     out[k, :, b : b + 128] = rows[:, pl.ds(at, 128)]
 
@@ -126,41 +140,68 @@
         e[...] = (part * (1.0 / TOKENS)).astype(e.dtype)
 
 
-def assemble(where, *refs):
+def place(sides, where, *refs):
     zl, y, x, core = (where[i] for i in range(4))
-    out = refs[-1]
-    for side in range(2):
+    pieces, (out, wide, sems) = refs[: len(sides)], refs[-3:]
+    copies = []
+    for (side, k3), piece in zip(sides, pieces):
         held_by = core if side == 0 else 1 - core
-        for k3 in range(4):
-            piece = refs[side * 4 + k3]
-            for k2 in range(4):
-                for j in range(2):
-                    z = lax.rem(jnp.where(held_by == 0, zl + 4 - j, zl + 1 + j), 4)
-                    at = jnp.where(
-                        held_by == 0,
-                        column(z, back(y, k2), back(x, k3)),
-                        column(z, back(y, k3), back(x, k2)),
-                    )
-                    b = (k2 * 2 + j) * 128
-                    out[:, pl.ds(pl.multiple_of(at, 128), 128)] = piece[
-                        :, b : b + 128
-                    ].astype(jnp.float32)
+        for k2 in range(4):
+            for j in range(2):
+                z = lax.rem(zl + 4 - j - 2 * held_by, 4)
+                at = jnp.where(
+                    held_by == 0,
+                    column(z, back(y, k2), back(x, k3)),
+                    column(z, back(y, k3), back(x, k2)),
+                )
+                b, n = (k2 * 2 + j) * 128, len(copies)
+                wide[n] = piece[:, b : b + 128].astype(jnp.float32)
+                copy = pltpu.make_async_copy(
+                    wide.at[n],
+                    out.at[:, pl.ds(pl.multiple_of(at, 128), 128)],
+                    sems.at[n],
+                )
+                copy.start()
+                copies.append(copy)
+    for copy in copies:
+        copy.wait()
 
 
 VMEM = pl.BlockSpec(memory_space=pltpu.VMEM)
 SMEM = pl.BlockSpec(memory_space=pltpu.SMEM)
+HBM = pl.BlockSpec(memory_space=pltpu.HBM)
 PARAMS = pltpu.CompilerParams(vmem_limit_bytes=40 * 1024 * 1024)
 
 
-def call(body, name, shapes, ins):
+def call(body, name, shapes, ins, scratch=()):
     return pl.pallas_call(
         body,
         out_shape=shapes,
         in_specs=ins,
         out_specs=jax.tree.map(lambda _: VMEM, shapes),
+        scratch_shapes=scratch,
         compiler_params=PARAMS,
         name=name,
     )
+
+
+def placed(where, out, pieces):
+    sides, values = list(pieces), list(pieces.values())
+    n = 8 * len(sides)
+    held = [] if out is None else [out]
+    return pl.pallas_call(
+        functools.partial(place, sides),
+        out_shape=jax.ShapeDtypeStruct((64, 8192), jnp.float32),
+        in_specs=[SMEM] + [VMEM] * len(sides) + [HBM] * len(held),
+        out_specs=HBM,
+        scratch_shapes=[
+            pltpu.VMEM((n, 64, 128), jnp.float32),
+            pltpu.SemaphoreType.DMA((n,)),
+        ],
+        input_output_aliases={1 + len(sides): 0} if held else {},
+        compiler_params=PARAMS,
+        name="place",
+    )(where, *values, *held)
 
 
 def on_device(acts, grads_out, act_inverse, grad_inverse):
@@ -180,48 +221,70 @@
         [jnp.where(first, kept, got), jnp.where(first, got, kept)], axis=0
     )
     mine, other = call(
-        arrange, "arrange", [shape((4, 64, 2048), bf16)] * 2, [SMEM, VMEM, VMEM]
+        arrange, "arrange", [shape((4, 64, 2048), bf16)] * 2, [SMEM, HBM, HBM],
+        [pltpu.VMEM((64, 8192), bf16)] * 2 + [pltpu.SemaphoreType.DMA((8,))],
     )(where, act_inverse, grad_inverse)
     theirs = swap_cores(other)
     rows = [jnp.stack([mine[k], theirs[k]]) for k in range(4)]
-    weights = [rows[0]] + [second_turn(rows[k], k) for k in (1, 2, 3)]
-
-    line = jnp.stack([block] + [along_line(block, k) for k in (1, 2, 3)])
+    weights = turned(second_turn, rows)
+
+    line = jnp.stack([block, along_line(block, 1)])
+    line = jnp.concatenate([line, along_line(line, 2)], axis=0)
     line, weights[1], weights[3] = lax.optimization_barrier(
         (line, weights[1], weights[3])
     )
-    plane = jnp.stack([line] + [first_turn(line, k) for k in (1, 2, 3)])
+    plane = jnp.stack(turned(first_turn, [line] * 4))
     parts = call(partials, "partials", [shape((128, 128), f32)] * 4, [VMEM] * 5)(
         *weights, plane
     )
-    total = parts[0]
-    for k in (1, 2, 3):
-        total = total + second_turn(parts[k], k)
+    total = sum(turned(second_turn, parts))
     pre = jnp.where(
         first, total, jnp.concatenate([total[64:], total[:64]], axis=0)
     ).astype(bf16)
 
-    far = swap_reps(pre)
-    low_rep = lax.axis_index("rep") == 0
-    pre = jnp.concatenate(
-        [jnp.where(low_rep, pre, far), jnp.where(low_rep, far, pre)], axis=1
-    )
-    got = on_ring(pre, (-1, 0), (1, 0))
+    r, zl = lax.axis_index("rep"), where[0]
+    got = on_ring(pre, (-1, 1), (1, 0))
     act = jnp.where(first, pre, got)
-    grad = jnp.where(first, got, pre)
-    pair = jnp.stack([act, on_ring(act, (1, -1), (0, 1))])
+    one = on_ring(jnp.stack([act, got]), (1, -1), (0, 1))
+    two = on_ring(jnp.concatenate([act[None], one], axis=0), (2, -2), (0, 1))
+    cross = swap_cores(
+        jnp.where(first, two, jnp.stack([two[1], two[0], pre]))
+    )
+    near = (jnp.where(first, act, cross[0]), jnp.where(first, one[0], cross[1]))
+    over = (jnp.where(first, cross[0], one[0]), jnp.where(first, cross[1], act))
+
+    def by_rep(low, a, b):
+        return jnp.concatenate([jnp.where(low, a, b), jnp.where(low, b, a)], axis=1)
+
+    pair = jnp.stack(
+        [by_rep((r == 0) == (zl >= j + 2 * c), near[j], over[j]) for j in (0, 1)]
+    )
+    grad = by_rep(
+        r == 0, jnp.where(first, cross[2], pre), jnp.where(first, two[2], cross[2])
+    )
     grads = jnp.stack([grad, third_pair(grad, 1)])
-    plane = jnp.stack([pair] + [first_turn(pair, k) for k in (1, 2, 3)])
+    plane = jnp.stack(turned(first_turn, [pair] * 4))
     grads = jnp.concatenate([grads, third_pair(grads, 3)], axis=0)
     made = call(
         tiles, "tiles", [shape((128, 1024), bf16)] * 4, [SMEM, VMEM, VMEM]
     )(where, grads, plane)
-    whole = [made[0]] + [second_turn(made[k], k) for k in (1, 2, 3)]
-    own = [jnp.where(first, e[:64], e[64:]) for e in whole]
-    sibling = [swap_cores(jnp.where(first, e[64:], e[:64])) for e in whole]
-    return call(
-        assemble, "assemble", shape((64, 8192), f32), [SMEM] + [VMEM] * 8
-    )(where, *own, *sibling)
+    whole = turned(second_turn, made)
+
+    def parted(e):
+        return jnp.where(first, e[:64], e[64:]), jnp.where(first, e[64:], e[:64])
+
+    own, give = zip(*(parted(e) for e in whole))
+    give, sibling = list(give), {}
+    sibling[0] = swap_cores(give[0])
+    out = placed(where, None, {(0, 0): own[0], (1, 0): sibling[0]})
+    sibling[3] = swap_cores(give[3])
+    give[2], out = lax.optimization_barrier((give[2], out))
+    sibling[2] = swap_cores(give[2])
+    out = placed(where, out, {(0, 3): own[3], (1, 3): sibling[3], (0, 2): own[2]})
+    give[1], out = lax.optimization_barrier((give[1], out))
+    sibling[1] = swap_cores(give[1])
+    out = placed(where, out, {(0, 1): own[1], (1, 2): sibling[2]})
+    return placed(where, out, {(1, 1): sibling[1]})
 
 
 def solution(mesh):

time: 88.7 us -> 97.7 us (1.10)
  waiting for transfers between devices: 29.9 us -> 34.4 us
  Pallas kernels: 5.39 us -> 9.46 us
    ppermute x29, waiting for transfers between devices: 29.9 us -> 34.4 us  [send(): return lax.ppermute(value, AXES, pairs)]
    pallas_call x2 -> x5, Pallas kernels: 3.34 us -> 7.41 us  [the longest x4 6.07 us: placed(): pl.pallas_call(functools.partial(place, sides), out_shape=jax.ShapeDtypeS...]
  transfers between devices with their start and end apart: 29 -> 29, of which waited for: 18 -> 20; matrix products, arithmetic and copies ran while one was open for 1% -> 1% of each run, Pallas kernels for 0% -> 5%
where the time goes in v4:
time: 97.7 us; the launch traced here: 97.6 us
  starting transfers between devices  50 us (51%)
  waiting for transfers between devices  34.4 us (35%)
  Pallas kernels  9.46 us (10%)
  local copies, waits for them, and re-layouts  2.61 us (3%)
    ppermute x29, starting transfers between devices, send(): return lax.ppermute(value, AXES, pairs)  50 us
    ppermute x29, waiting for transfers between devices, send(): return lax.ppermute(value, AXES, pairs)  34.4 us
    pallas_call x4, Pallas kernels, placed(): pl.pallas_call(functools.partial(place, sides), out_shape=jax.ShapeDtypeS...  6.07 us
    unnamed x8, local copies, waits for them, and re-layouts  2.46 us
  transfers between devices with their start and end apart: 29, of which 20 were waited for; matrix products, arithmetic and copies ran while one was open for 1% of the time, Pallas kernels for 5%

profile of v4, /device:TPU:1, one launch (start us, length us, event | category | flops | bytes accessed | tf_op | source)
XLA Modules:
  0.0 97.6 jit_solution(6601469557930374144)
XLA Ops:
  2.5 1.3 %arrange.1 = (bf16[4,64,2048]{2,1,0:T(8,128)(2,1)S(1)}, bf16[4,64,2048]{2,1,0:T(8,128)(2,1)S(1)}) custom-call(s32[4]{0:T(128)S(1)} %pad_add_fusion.where, bf16[64,8192]{1,0:T(8,128)(2,1)S(1)} %copy-done, bf16[64,8192]{1,0:T(8,128)(2,1)S(1)} %copy-done.1), custom_call_target="tpu_custom_call" | custom-call | tf_op jit(solution)/shard_map/arrange/pallas_call | solution.py:223
  3.9 3.3 %collective-permute-start = (bf16[4,64,2048]{2,1,0:T(8,128)(2,1)S(1)}, bf16[4,64,2048]{2,1,0:T(8,128)(2,1)S(1)}, u32[]{:S(2)}, u32[]{:S(2)}) collective-permute-start(bf16[4,64,2048]{2,1,0:T(8,128)(2,1)S(1)} %get-tuple-element.23), channel_id=1, source_target_pairs={{0,1},{1,0},{2,3},{3,2},{4,5},{5,4},{6,7},{7,6},{8,9},{9,8},{10,11... | collective-permute-start | bytes 3145736 | tf_op jit(solution)/shard_map/ppermute | solution.py:32
  7.4 2.1 %collective-permute-done.1 = bf16[64,128]{1,0:T(8,128)(2,1)S(1)} collective-permute-done((bf16[64,128]{1,0:T(8,128)(2,1)S(1)}, bf16[64,128]{1,0:T(8,128)(2,1)S(1)}, u32[]{:S(2)}, u32[]{:S(2)}) %collective-permute-start.1) | collective-permute-done | bytes 16416 | tf_op jit(solution)/shard_map/ppermute | solution.py:32
  11.1 1.6 %collective-permute-start.5 = (bf16[2,64,2048]{2,1,0:T(8,128)(2,1)S(1)}, bf16[2,64,2048]{2,1,0:T(8,128)(2,1)S(1)}, u32[]{:S(2)}, u32[]{:S(2)}) collective-permute-start(bf16[2,64,2048]{2,1,0:T(8,128)(2,1)S(1)} %pad_maximum_fusion.2), channel_id=1, source_target_pairs={{0,6},{1,25},{2,0},{3,27},{4,2},{5,29},{6,4},{7,31},{8,14},{9,1},{... | collective-permute-start | bytes 1572872 | tf_op jit(solution)/shard_map/ppermute | solution.py:32
  12.7 3.0 %collective-permute-start.3 = (bf16[2,128,128]{2,1,0:T(8,128)(2,1)S(1)}, bf16[2,128,128]{2,1,0:T(8,128)(2,1)S(1)}, u32[]{:S(2)}, u32[]{:S(2)}) collective-permute-start(bf16[2,128,128]{2,1,0:T(8,128)(2,1)S(1)} %pad_maximum_fusion.11), channel_id=1, source_target_pairs={{0,64},{1,65},{2,66},{3,67},{4,68},{5,69},{6,70},{7,71},{8,72},{9,... | collective-permute-start | bytes 196616 | tf_op jit(solution)/shard_map/ppermute | solution.py:32
  15.8 1.7 %collective-permute-start.6 = (bf16[2,64,2048]{2,1,0:T(8,128)(2,1)S(1)}, bf16[2,64,2048]{2,1,0:T(8,128)(2,1)S(1)}, u32[]{:S(2)}, u32[]{:S(2)}) collective-permute-start(bf16[2,64,2048]{2,1,0:T(8,128)(2,1)S(1)} %pad_maximum_fusion.3), channel_id=1, source_target_pairs={{0,4},{1,17},{2,6},{3,19},{4,0},{5,21},{6,2},{7,23},{8,12},{9,25},... | collective-permute-start | bytes 1572872 | tf_op jit(solution)/shard_map/ppermute | solution.py:32
  19.4 4.4 %collective-permute-done.5.w3 = bf16[2,64,2048]{2,1,0:T(8,128)(2,1)S(1)} collective-permute-done((bf16[2,64,2048]{2,1,0:T(8,128)(2,1)S(1)}, bf16[2,64,2048]{2,1,0:T(8,128)(2,1)S(1)}, u32[]{:S(2)}, u32[]{:S(2)}) %collective-permute-start.5) | collective-permute-done | bytes 524320 | tf_op jit(solution)/shard_map/ppermute | solution.py:32
  23.8 1.5 %collective-permute-start.7 = (bf16[4,128,128]{2,1,0:T(8,128)(2,1)S(1)}, bf16[4,128,128]{2,1,0:T(8,128)(2,1)S(1)}, u32[]{:S(2)}, u32[]{:S(2)}) collective-permute-start(bf16[4,128,128]{2,1,0:T(8,128)(2,1)S(1)} %pad_maximum_fusion.7), channel_id=1, source_target_pairs={{0,8},{1,3},{2,10},{3,5},{4,12},{5,7},{6,14},{7,1},{8,16},{9,11},{... | collective-permute-start | bytes 393224 | tf_op jit(solution)/shard_map/ppermute | solution.py:32
  25.3 2.3 %collective-permute-done.9 = bf16[4,128,128]{2,1,0:T(8,128)(2,1)S(1)} collective-permute-done((bf16[4,128,128]{2,1,0:T(8,128)(2,1)S(1)}, bf16[4,128,128]{2,1,0:T(8,128)(2,1)S(1)}, u32[]{:S(2)}, u32[]{:S(2)}) %collective-permute-start.9) | collective-permute-done | bytes 131104 | tf_op jit(solution)/shard_map/ppermute | solution.py:32
  27.6 1.8 %collective-permute-done.8 = bf16[4,128,128]{2,1,0:T(8,128)(2,1)S(1)} collective-permute-done((bf16[4,128,128]{2,1,0:T(8,128)(2,1)S(1)}, bf16[4,128,128]{2,1,0:T(8,128)(2,1)S(1)}, u32[]{:S(2)}, u32[]{:S(2)}) %collective-permute-start.8) | collective-permute-done | bytes 131104 | tf_op jit(solution)/shard_map/ppermute | solution.py:32
  29.4 1.4 %collective-permute-done.7 = bf16[4,128,128]{2,1,0:T(8,128)(2,1)S(1)} collective-permute-done((bf16[4,128,128]{2,1,0:T(8,128)(2,1)S(1)}, bf16[4,128,128]{2,1,0:T(8,128)(2,1)S(1)}, u32[]{:S(2)}, u32[]{:S(2)}) %collective-permute-start.7) | collective-permute-done | bytes 131104 | tf_op jit(solution)/shard_map/ppermute | solution.py:32
  32.2 6.5 %collective-permute-start.11 = (f32[128,128]{1,0:T(8,128)S(1)}, f32[128,128]{1,0:T(8,128)S(1)}, u32[]{:S(2)}, u32[]{:S(2)}) collective-permute-start(f32[128,128]{1,0:T(8,128)S(1)} %get-tuple-element.29), channel_id=1, source_target_pairs={{0,4},{1,17},{2,6},{3,19},{4,0},{5,21},{6,2},{7,23},{8,12},{9,25},... | collective-permute-start | bytes 196616 | tf_op jit(solution)/shard_map/ppermute | solution.py:32
  39.2 1.9 %collective-permute-done.11 = f32[128,128]{1,0:T(8,128)S(1)} collective-permute-done((f32[128,128]{1,0:T(8,128)S(1)}, f32[128,128]{1,0:T(8,128)S(1)}, u32[]{:S(2)}, u32[]{:S(2)}) %collective-permute-start.11) | collective-permute-done | bytes 65568 | tf_op jit(solution)/shard_map/ppermute | solution.py:32
  41.9 4.1 %collective-permute-start.13 = (bf16[128,128]{1,0:T(8,128)(2,1)S(1)}, bf16[128,128]{1,0:T(8,128)(2,1)S(1)}, u32[]{:S(2)}, u32[]{:S(2)}) collective-permute-start(bf16[128,128]{1,0:T(8,128)(2,1)S(1)} %fusion), channel_id=1, source_target_pairs={{0,225},{1,32},{2,227},{3,34},{4,229},{5,36},{6,231},{7,38},{8,233... | collective-permute-start | bytes 98312 | tf_op jit(solution)/shard_map/ppermute | solution.py:32
  46.1 1.6 %collective-permute-done.13 = bf16[128,128]{1,0:T(8,128)(2,1)S(1)} collective-permute-done((bf16[128,128]{1,0:T(8,128)(2,1)S(1)}, bf16[128,128]{1,0:T(8,128)(2,1)S(1)}, u32[]{:S(2)}, u32[]{:S(2)}) %collective-permute-start.13) | collective-permute-done | bytes 32800 | tf_op jit(solution)/shard_map/ppermute | solution.py:32
  47.7 3.9 %collective-permute-start.14 = (bf16[2,128,128]{2,1,0:T(8,128)(2,1)S(1)}, bf16[2,128,128]{2,1,0:T(8,128)(2,1)S(1)}, u32[]{:S(2)}, u32[]{:S(2)}) collective-permute-start(bf16[2,128,128]{2,1,0:T(8,128)(2,1)S(1)} %pad_maximum_fusion.12), channel_id=1, source_target_pairs={{0,32},{1,225},{2,34},{3,227},{4,36},{5,229},{6,38},{7,231},{8,40}... | collective-permute-start | bytes 196616 | tf_op jit(solution)/shard_map/ppermute | solution.py:32
  51.6 2.5 %collective-permute-done.14 = bf16[2,128,128]{2,1,0:T(8,128)(2,1)S(1)} collective-permute-done((bf16[2,128,128]{2,1,0:T(8,128)(2,1)S(1)}, bf16[2,128,128]{2,1,0:T(8,128)(2,1)S(1)}, u32[]{:S(2)}, u32[]{:S(2)}) %collective-permute-start.14) | collective-permute-done | bytes 65568 | tf_op jit(solution)/shard_map/ppermute | solution.py:32
  54.1 4.1 %collective-permute-start.15 = (bf16[3,128,128]{2,1,0:T(8,128)(2,1)S(1)}, bf16[3,128,128]{2,1,0:T(8,128)(2,1)S(1)}, u32[]{:S(2)}, u32[]{:S(2)}) collective-permute-start(bf16[3,128,128]{2,1,0:T(8,128)(2,1)S(1)} %pad_maximum_fusion.10), channel_id=1, source_target_pairs={{0,64},{1,193},{2,66},{3,195},{4,68},{5,197},{6,70},{7,199},{8,72}... | collective-permute-start | bytes 294920 | tf_op jit(solution)/shard_map/ppermute | solution.py:32
  58.2 2.6 %collective-permute-done.15 = bf16[3,128,128]{2,1,0:T(8,128)(2,1)S(1)} collective-permute-done((bf16[3,128,128]{2,1,0:T(8,128)(2,1)S(1)}, bf16[3,128,128]{2,1,0:T(8,128)(2,1)S(1)}, u32[]{:S(2)}, u32[]{:S(2)}) %collective-permute-start.15) | collective-permute-done | bytes 98336 | tf_op jit(solution)/shard_map/ppermute | solution.py:32
  60.8 5.4 %collective-permute-start.16 = (bf16[3,128,128]{2,1,0:T(8,128)(2,1)S(1)}, bf16[3,128,128]{2,1,0:T(8,128)(2,1)S(1)}, u32[]{:S(2)}, u32[]{:S(2)}) collective-permute-start(bf16[3,128,128]{2,1,0:T(8,128)(2,1)S(1)} %maximum_select_fusion), channel_id=1, source_target_pairs={{0,1},{1,0},{2,3},{3,2},{4,5},{5,4},{6,7},{7,6},{8,9},{9,8},{10,11... | collective-permute-start | bytes 294920 | tf_op jit(solution)/shard_map/ppermute | solution.py:32
  68.9 2.4 %collective-permute-start.21 = (bf16[2,128,256]{2,1,0:T(8,128)(2,1)S(1)}, bf16[2,128,256]{2,1,0:T(8,128)(2,1)S(1)}, u32[]{:S(2)}, u32[]{:S(2)}) collective-permute-start(bf16[2,128,256]{2,1,0:T(8,128)(2,1)S(1)} %get-tuple-element.62), channel_id=1, source_target_pairs={{0,24},{1,7},{2,26},{3,1},{4,28},{5,3},{6,30},{7,5},{8,0},{9,15},{... | collective-permute-start | bytes 393224 | tf_op jit(solution)/shard_map/ppermute | solution.py:32
  73.5 1.4 %collective-permute-done.19 = bf16[2,128,256]{2,1,0:T(8,128)(2,1)S(1)} collective-permute-done((bf16[2,128,256]{2,1,0:T(8,128)(2,1)S(1)}, bf16[2,128,256]{2,1,0:T(8,128)(2,1)S(1)}, u32[]{:S(2)}, u32[]{:S(2)}) %collective-permute-start.19) | collective-permute-done | bytes 131104 | tf_op jit(solution)/shard_map/ppermute | solution.py:32
  75.0 1.5 %collective-permute-done.18 = bf16[2,128,256]{2,1,0:T(8,128)(2,1)S(1)} collective-permute-done((bf16[2,128,256]{2,1,0:T(8,128)(2,1)S(1)}, bf16[2,128,256]{2,1,0:T(8,128)(2,1)S(1)}, u32[]{:S(2)}, u32[]{:S(2)}) %collective-permute-start.18) | collective-permute-done | bytes 131104 | tf_op jit(solution)/shard_map/ppermute | solution.py:32
  76.5 1.4 %tiles.1 = (bf16[128,1024]{1,0:T(8,128)(2,1)S(1)}, bf16[128,1024]{1,0:T(8,128)(2,1)S(1)}, bf16[128,1024]{1,0:T(8,128)(2,1)S(1)}, bf16[128,1024]{1,0:T(8,128)(2,1)S(1)}) custom-call(s32[4]{0:T(128)S(1)} %pad_add_fusion.where, bf16[4,128,256]{2,1,0:T(8,128)(2,1)S(1)} %pad_maximum_fusion.6.g, bf16[4,2,128,256]{3,2,1,0:T(8,128)(2,1)S(1)} %pad_maximum_fusion.5.plane), custom_call_target="tpu_custom_call" | custom-call | tf_op jit(solution)/shard_map/tiles/pallas_call | solution.py:268
  77.9 2.4 %collective-permute-start.23 = (bf16[128,1024]{1,0:T(8,128)(2,1)S(1)}, bf16[128,1024]{1,0:T(8,128)(2,1)S(1)}, u32[]{:S(2)}, u32[]{:S(2)}) collective-permute-start(bf16[128,1024]{1,0:T(8,128)(2,1)S(1)} %get-tuple-element.32), channel_id=1, source_target_pairs={{0,6},{1,25},{2,0},{3,27},{4,2},{5,29},{6,4},{7,31},{8,14},{9,1},{... | collective-permute-start | bytes 786440 | tf_op jit(solution)/shard_map/ppermute | solution.py:32
  80.3 1.7 %collective-permute-start.26 = (bf16[64,1024]{1,0:T(8,128)(2,1)S(1)}, bf16[64,1024]{1,0:T(8,128)(2,1)S(1)}, u32[]{:S(2)}, u32[]{:S(2)}) collective-permute-start(bf16[64,1024]{1,0:T(8,128)(2,1)S(1)} %get-tuple-element.49), channel_id=1, source_target_pairs={{0,1},{1,0},{2,3},{3,2},{4,5},{5,4},{6,7},{7,6},{8,9},{9,8},{10,11... | collective-permute-start | bytes 393224 | tf_op jit(solution)/shard_map/ppermute | solution.py:32
  83.0 1.5 %place.4.refs_3_ = f32[64,8192]{1,0:T(8,128)} custom-call(s32[4]{0:T(128)S(1)} %pad_add_fusion.where, bf16[64,1024]{1,0:T(8,128)(2,1)S(1)} %get-tuple-element.50.refs_0_, bf16[64,1024]{1,0:T(8,128)(2,1)S(1)} %collective-permute-done.26.refs_1_), custom_call_target="tpu_custom_call" | custom-call | tf_op jit(solution)/shard_map/place/pallas_call | solution.py:192
  84.5 1.9 %collective-permute-done.23 = bf16[128,1024]{1,0:T(8,128)(2,1)S(1)} collective-permute-done((bf16[128,1024]{1,0:T(8,128)(2,1)S(1)}, bf16[128,1024]{1,0:T(8,128)(2,1)S(1)}, u32[]{:S(2)}, u32[]{:S(2)}) %collective-permute-start.23) | collective-permute-done | bytes 262176 | tf_op jit(solution)/shard_map/ppermute | solution.py:32
  86.8 2.2 %collective-permute-done.25 = bf16[128,1024]{1,0:T(8,128)(2,1)S(1)} collective-permute-done((bf16[128,1024]{1,0:T(8,128)(2,1)S(1)}, bf16[128,1024]{1,0:T(8,128)(2,1)S(1)}, u32[]{:S(2)}, u32[]{:S(2)}) %collective-permute-start.25) | collective-permute-done | bytes 262176 | tf_op jit(solution)/shard_map/ppermute | solution.py:32
  90.1 1.6 %collective-permute-done.22 = bf16[128,1024]{1,0:T(8,128)(2,1)S(1)} collective-permute-done((bf16[128,1024]{1,0:T(8,128)(2,1)S(1)}, bf16[128,1024]{1,0:T(8,128)(2,1)S(1)}, u32[]{:S(2)}, u32[]{:S(2)}) %collective-permute-start.22) | collective-permute-done | bytes 262176 | tf_op jit(solution)/shard_map/ppermute | solution.py:32
  91.8 1.7 %place.5.refs_2_ = f32[64,8192]{1,0:T(8,128)} custom-call(s32[4]{0:T(128)S(1)} %pad_add_fusion.where, bf16[64,1024]{1,0:T(8,128)(2,1)S(1)} %get-tuple-element.54.refs_0_, bf16[64,1024]{1,0:T(8,128)(2,1)S(1)} %collective-permute-done.24.refs_1_, bf16[64,1024]{1,0:T(8,128)(2,1)S(1)} %get-tuple-element.52.refs_2_, ...), custom_call_target="tpu_custom_call", output_to_operand_aliasing={{}: (4, {})} | custom-call | tf_op jit(solution)/shard_map/place/pallas_call | solution.py:192
  94.6 1.5 %place.6.refs_1_ = f32[64,8192]{1,0:T(8,128)} custom-call(s32[4]{0:T(128)S(1)} %pad_add_fusion.where, bf16[64,1024]{1,0:T(8,128)(2,1)S(1)} %get-tuple-element.47.refs_0_, bf16[64,1024]{1,0:T(8,128)(2,1)S(1)} %collective-permute-done.28.refs_1_, f32[64,8192]{1,0:T(8,128)} %place.5.refs_2_), custom_call_target="tpu_custom_call", output_to_operand_aliasing={{}: (3, {})} | custom-call | tf_op jit(solution)/shard_map/place/pallas_call | solution.py:192
  (73 shorter events, 19.0 us)
Async XLA Ops:
  0.0 7.2 %copy-start.2 = (bf16[128,64]{0,1:T(8,128)(2,1)S(1)}, bf16[128,64]{0,1:T(8,128)(2,1)}, u32[]{:S(2)}) copy-start(bf16[128,64]{0,1:T(8,128)(2,1)} %param.5) | copy-start | bytes 49156
  0.0 7.2 %copy-start.3 = (bf16[128,64]{0,1:T(8,128)(2,1)S(1)}, bf16[128,64]{0,1:T(8,128)(2,1)}, u32[]{:S(2)}) copy-start(bf16[128,64]{0,1:T(8,128)(2,1)} %param.4) | copy-start | bytes 49156
  0.1 1.2 %copy-start = (bf16[64,8192]{1,0:T(8,128)(2,1)S(1)}, bf16[64,8192]{1,0:T(8,128)(2,1)}, u32[]{:S(2)}) copy-start(bf16[64,8192]{1,0:T(8,128)(2,1)} %act_hbm.1) | copy-start | bytes 3145732
  3.9 5.7 %collective-permute-start = (bf16[4,64,2048]{2,1,0:T(8,128)(2,1)S(1)}, bf16[4,64,2048]{2,1,0:T(8,128)(2,1)S(1)}, u32[]{:S(2)}, u32[]{:S(2)}) collective-permute-start(bf16[4,64,2048]{2,1,0:T(8,128)(2,1)S(1)} %get-tuple-element.23), channel_id=1, source_target_pairs={{0,1},{1,0},{2,3},{3,2},{4,5},{5,4},{6,7},{7,6},{8,9},{9,8},{10,11... | collective-permute-start | bytes 3145736 | tf_op jit(solution)/shard_map/ppermute | solution.py:32
  7.2 2.3 %collective-permute-start.1 = (bf16[64,128]{1,0:T(8,128)(2,1)S(1)}, bf16[64,128]{1,0:T(8,128)(2,1)S(1)}, u32[]{:S(2)}, u32[]{:S(2)}) collective-permute-start(bf16[64,128]{1,0:T(8,128)(2,1)S(1)} %select_bitcast_fusion), channel_id=1, source_target_pairs={{0,1},{1,0},{2,3},{3,2},{4,5},{5,4},{6,7},{7,6},{8,9},{9,8},{10,11... | collective-permute-start | bytes 49160 | tf_op jit(solution)/shard_map/ppermute | solution.py:32
  9.5 3.1 %collective-permute-start.2 = (bf16[128,128]{1,0:T(8,128)(2,1)S(1)}, bf16[128,128]{1,0:T(8,128)(2,1)S(1)}, u32[]{:S(2)}, u32[]{:S(2)}) collective-permute-start(bf16[128,128]{1,0:T(8,128)(2,1)S(1)} %get-tuple-element.74), channel_id=1, source_target_pairs={{0,32},{1,33},{2,34},{3,35},{4,36},{5,37},{6,38},{7,39},{8,40},{9,... | collective-permute-start | bytes 98312 | tf_op jit(solution)/shard_map/ppermute | solution.py:32
  9.8 9.6 %collective-permute-start.4 = (bf16[2,64,2048]{2,1,0:T(8,128)(2,1)S(1)}, bf16[2,64,2048]{2,1,0:T(8,128)(2,1)S(1)}, u32[]{:S(2)}, u32[]{:S(2)}) collective-permute-start(bf16[2,64,2048]{2,1,0:T(8,128)(2,1)S(1)} %pad_maximum_fusion.1), channel_id=1, source_target_pairs={{0,2},{1,9},{2,4},{3,11},{4,6},{5,13},{6,0},{7,15},{8,10},{9,17},{... | collective-permute-start | bytes 1572872 | tf_op jit(solution)/shard_map/ppermute | solution.py:32
  11.1 12.7 %collective-permute-start.5 = (bf16[2,64,2048]{2,1,0:T(8,128)(2,1)S(1)}, bf16[2,64,2048]{2,1,0:T(8,128)(2,1)S(1)}, u32[]{:S(2)}, u32[]{:S(2)}) collective-permute-start(bf16[2,64,2048]{2,1,0:T(8,128)(2,1)S(1)} %pad_maximum_fusion.2), channel_id=1, source_target_pairs={{0,6},{1,25},{2,0},{3,27},{4,2},{5,29},{6,4},{7,31},{8,14},{9,1},{... | collective-permute-start | bytes 1572872 | tf_op jit(solution)/shard_map/ppermute | solution.py:32
  12.7 5.7 %collective-permute-start.3 = (bf16[2,128,128]{2,1,0:T(8,128)(2,1)S(1)}, bf16[2,128,128]{2,1,0:T(8,128)(2,1)S(1)}, u32[]{:S(2)}, u32[]{:S(2)}) collective-permute-start(bf16[2,128,128]{2,1,0:T(8,128)(2,1)S(1)} %pad_maximum_fusion.11), channel_id=1, source_target_pairs={{0,64},{1,65},{2,66},{3,67},{4,68},{5,69},{6,70},{7,71},{8,72},{9,... | collective-permute-start | bytes 196616 | tf_op jit(solution)/shard_map/ppermute | solution.py:32
  15.8 15.2 %collective-permute-start.6 = (bf16[2,64,2048]{2,1,0:T(8,128)(2,1)S(1)}, bf16[2,64,2048]{2,1,0:T(8,128)(2,1)S(1)}, u32[]{:S(2)}, u32[]{:S(2)}) collective-permute-start(bf16[2,64,2048]{2,1,0:T(8,128)(2,1)S(1)} %pad_maximum_fusion.3), channel_id=1, source_target_pairs={{0,4},{1,17},{2,6},{3,19},{4,0},{5,21},{6,2},{7,23},{8,12},{9,25},... | collective-permute-start | bytes 1572872 | tf_op jit(solution)/shard_map/ppermute | solution.py:32
  23.8 3.8 %collective-permute-start.9 = (bf16[4,128,128]{2,1,0:T(8,128)(2,1)S(1)}, bf16[4,128,128]{2,1,0:T(8,128)(2,1)S(1)}, u32[]{:S(2)}, u32[]{:S(2)}) collective-permute-start(bf16[4,128,128]{2,1,0:T(8,128)(2,1)S(1)} %pad_maximum_fusion.7), channel_id=1, source_target_pairs={{0,24},{1,7},{2,26},{3,1},{4,28},{5,3},{6,30},{7,5},{8,0},{9,15},{... | collective-permute-start | bytes 393224 | tf_op jit(solution)/shard_map/ppermute | solution.py:32
  23.8 5.6 %collective-permute-start.8 = (bf16[4,128,128]{2,1,0:T(8,128)(2,1)S(1)}, bf16[4,128,128]{2,1,0:T(8,128)(2,1)S(1)}, u32[]{:S(2)}, u32[]{:S(2)}) collective-permute-start(bf16[4,128,128]{2,1,0:T(8,128)(2,1)S(1)} %pad_maximum_fusion.7), channel_id=1, source_target_pairs={{0,16},{1,5},{2,18},{3,7},{4,20},{5,1},{6,22},{7,3},{8,24},{9,13},... | collective-permute-start | bytes 393224 | tf_op jit(solution)/shard_map/ppermute | solution.py:32
  23.8 7.0 %collective-permute-start.7 = (bf16[4,128,128]{2,1,0:T(8,128)(2,1)S(1)}, bf16[4,128,128]{2,1,0:T(8,128)(2,1)S(1)}, u32[]{:S(2)}, u32[]{:S(2)}) collective-permute-start(bf16[4,128,128]{2,1,0:T(8,128)(2,1)S(1)} %pad_maximum_fusion.7), channel_id=1, source_target_pairs={{0,8},{1,3},{2,10},{3,5},{4,12},{5,7},{6,14},{7,1},{8,16},{9,11},{... | collective-permute-start | bytes 393224 | tf_op jit(solution)/shard_map/ppermute | solution.py:32
  31.6 7.6 %collective-permute-start.10 = (f32[128,128]{1,0:T(8,128)S(1)}, f32[128,128]{1,0:T(8,128)S(1)}, u32[]{:S(2)}, u32[]{:S(2)}) collective-permute-start(f32[128,128]{1,0:T(8,128)S(1)} %get-tuple-element.28), channel_id=1, source_target_pairs={{0,2},{1,9},{2,4},{3,11},{4,6},{5,13},{6,0},{7,15},{8,10},{9,17},{... | collective-permute-start | bytes 196616 | tf_op jit(solution)/shard_map/ppermute | solution.py:32
  32.2 8.8 %collective-permute-start.11 = (f32[128,128]{1,0:T(8,128)S(1)}, f32[128,128]{1,0:T(8,128)S(1)}, u32[]{:S(2)}, u32[]{:S(2)}) collective-permute-start(f32[128,128]{1,0:T(8,128)S(1)} %get-tuple-element.29), channel_id=1, source_target_pairs={{0,4},{1,17},{2,6},{3,19},{4,0},{5,21},{6,2},{7,23},{8,12},{9,25},... | collective-permute-start | bytes 196616 | tf_op jit(solution)/shard_map/ppermute | solution.py:32
  38.7 3.1 %collective-permute-start.12 = (f32[128,128]{1,0:T(8,128)S(1)}, f32[128,128]{1,0:T(8,128)S(1)}, u32[]{:S(2)}, u32[]{:S(2)}) collective-permute-start(f32[128,128]{1,0:T(8,128)S(1)} %get-tuple-element.30), channel_id=1, source_target_pairs={{0,6},{1,25},{2,0},{3,27},{4,2},{5,29},{6,4},{7,31},{8,14},{9,1},{... | collective-permute-start | bytes 196616 | tf_op jit(solution)/shard_map/ppermute | solution.py:32
  41.9 5.7 %collective-permute-start.13 = (bf16[128,128]{1,0:T(8,128)(2,1)S(1)}, bf16[128,128]{1,0:T(8,128)(2,1)S(1)}, u32[]{:S(2)}, u32[]{:S(2)}) collective-permute-start(bf16[128,128]{1,0:T(8,128)(2,1)S(1)} %fusion), channel_id=1, source_target_pairs={{0,225},{1,32},{2,227},{3,34},{4,229},{5,36},{6,231},{7,38},{8,233... | collective-permute-start | bytes 98312 | tf_op jit(solution)/shard_map/ppermute | solution.py:32
  47.7 6.4 %collective-permute-start.14 = (bf16[2,128,128]{2,1,0:T(8,128)(2,1)S(1)}, bf16[2,128,128]{2,1,0:T(8,128)(2,1)S(1)}, u32[]{:S(2)}, u32[]{:S(2)}) collective-permute-start(bf16[2,128,128]{2,1,0:T(8,128)(2,1)S(1)} %pad_maximum_fusion.12), channel_id=1, source_target_pairs={{0,32},{1,225},{2,34},{3,227},{4,36},{5,229},{6,38},{7,231},{8,40}... | collective-permute-start | bytes 196616 | tf_op jit(solution)/shard_map/ppermute | solution.py:32
  54.1 6.7 %collective-permute-start.15 = (bf16[3,128,128]{2,1,0:T(8,128)(2,1)S(1)}, bf16[3,128,128]{2,1,0:T(8,128)(2,1)S(1)}, u32[]{:S(2)}, u32[]{:S(2)}) collective-permute-start(bf16[3,128,128]{2,1,0:T(8,128)(2,1)S(1)} %pad_maximum_fusion.10), channel_id=1, source_target_pairs={{0,64},{1,193},{2,66},{3,195},{4,68},{5,197},{6,70},{7,199},{8,72}... | collective-permute-start | bytes 294920 | tf_op jit(solution)/shard_map/ppermute | solution.py:32
  60.8 6.3 %collective-permute-start.16 = (bf16[3,128,128]{2,1,0:T(8,128)(2,1)S(1)}, bf16[3,128,128]{2,1,0:T(8,128)(2,1)S(1)}, u32[]{:S(2)}, u32[]{:S(2)}) collective-permute-start(bf16[3,128,128]{2,1,0:T(8,128)(2,1)S(1)} %maximum_select_fusion), channel_id=1, source_target_pairs={{0,1},{1,0},{2,3},{3,2},{4,5},{5,4},{6,7},{7,6},{8,9},{9,8},{10,11... | collective-permute-start | bytes 294920 | tf_op jit(solution)/shard_map/ppermute | solution.py:32
  67.2 4.2 %collective-permute-start.17 = (bf16[128,256]{1,0:T(8,128)(2,1)S(1)}, bf16[128,256]{1,0:T(8,128)(2,1)S(1)}, u32[]{:S(2)}, u32[]{:S(2)}) collective-permute-start(bf16[128,256]{1,0:T(8,128)(2,1)S(1)} %get-tuple-element.68), channel_id=1, source_target_pairs={{0,2},{1,9},{2,0},{3,11},{4,6},{5,13},{6,4},{7,15},{8,10},{9,1},{1... | collective-permute-start | bytes 196616 | tf_op jit(solution)/shard_map/ppermute | solution.py:32
  67.3 6.2 %collective-permute-start.20 = (bf16[2,128,256]{2,1,0:T(8,128)(2,1)S(1)}, bf16[2,128,256]{2,1,0:T(8,128)(2,1)S(1)}, u32[]{:S(2)}, u32[]{:S(2)}) collective-permute-start(bf16[2,128,256]{2,1,0:T(8,128)(2,1)S(1)} %get-tuple-element.62), channel_id=1, source_target_pairs={{0,16},{1,5},{2,18},{3,7},{4,20},{5,1},{6,22},{7,3},{8,24},{9,13},... | collective-permute-start | bytes 393224 | tf_op jit(solution)/shard_map/ppermute | solution.py:32
  68.6 6.3 %collective-permute-start.19 = (bf16[2,128,256]{2,1,0:T(8,128)(2,1)S(1)}, bf16[2,128,256]{2,1,0:T(8,128)(2,1)S(1)}, u32[]{:S(2)}, u32[]{:S(2)}) collective-permute-start(bf16[2,128,256]{2,1,0:T(8,128)(2,1)S(1)} %get-tuple-element.62), channel_id=1, source_target_pairs={{0,8},{1,3},{2,10},{3,5},{4,12},{5,7},{6,14},{7,1},{8,16},{9,11},{... | collective-permute-start | bytes 393224 | tf_op jit(solution)/shard_map/ppermute | solution.py:32
  68.9 6.0 %collective-permute-start.21 = (bf16[2,128,256]{2,1,0:T(8,128)(2,1)S(1)}, bf16[2,128,256]{2,1,0:T(8,128)(2,1)S(1)}, u32[]{:S(2)}, u32[]{:S(2)}) collective-permute-start(bf16[2,128,256]{2,1,0:T(8,128)(2,1)S(1)} %get-tuple-element.62), channel_id=1, source_target_pairs={{0,24},{1,7},{2,26},{3,1},{4,28},{5,3},{6,30},{7,5},{8,0},{9,15},{... | collective-permute-start | bytes 393224 | tf_op jit(solution)/shard_map/ppermute | solution.py:32
  71.3 5.1 %collective-permute-start.18 = (bf16[2,128,256]{2,1,0:T(8,128)(2,1)S(1)}, bf16[2,128,256]{2,1,0:T(8,128)(2,1)S(1)}, u32[]{:S(2)}, u32[]{:S(2)}) collective-permute-start(bf16[2,128,256]{2,1,0:T(8,128)(2,1)S(1)} %pad_maximum_fusion.8), channel_id=1, source_target_pairs={{0,6},{1,25},{2,4},{3,27},{4,2},{5,29},{6,0},{7,31},{8,14},{9,17},... | collective-permute-start | bytes 393224 | tf_op jit(solution)/shard_map/ppermute | solution.py:32
  77.9 8.5 %collective-permute-start.23 = (bf16[128,1024]{1,0:T(8,128)(2,1)S(1)}, bf16[128,1024]{1,0:T(8,128)(2,1)S(1)}, u32[]{:S(2)}, u32[]{:S(2)}) collective-permute-start(bf16[128,1024]{1,0:T(8,128)(2,1)S(1)} %get-tuple-element.32), channel_id=1, source_target_pairs={{0,6},{1,25},{2,0},{3,27},{4,2},{5,29},{6,4},{7,31},{8,14},{9,1},{... | collective-permute-start | bytes 786440 | tf_op jit(solution)/shard_map/ppermute | solution.py:32
  80.3 2.7 %collective-permute-start.26 = (bf16[64,1024]{1,0:T(8,128)(2,1)S(1)}, bf16[64,1024]{1,0:T(8,128)(2,1)S(1)}, u32[]{:S(2)}, u32[]{:S(2)}) collective-permute-start(bf16[64,1024]{1,0:T(8,128)(2,1)S(1)} %get-tuple-element.49), channel_id=1, source_target_pairs={{0,1},{1,0},{2,3},{3,2},{4,5},{5,4},{6,7},{7,6},{8,9},{9,8},{10,11... | collective-permute-start | bytes 393224 | tf_op jit(solution)/shard_map/ppermute | solution.py:32
  81.9 7.1 %collective-permute-start.25 = (bf16[128,1024]{1,0:T(8,128)(2,1)S(1)}, bf16[128,1024]{1,0:T(8,128)(2,1)S(1)}, u32[]{:S(2)}, u32[]{:S(2)}) collective-permute-start(bf16[128,1024]{1,0:T(8,128)(2,1)S(1)} %get-tuple-element.33), channel_id=1, source_target_pairs={{0,4},{1,17},{2,6},{3,19},{4,0},{5,21},{6,2},{7,23},{8,12},{9,25},... | collective-permute-start | bytes 786440 | tf_op jit(solution)/shard_map/ppermute | solution.py:32
  83.0 8.8 %collective-permute-start.22 = (bf16[128,1024]{1,0:T(8,128)(2,1)S(1)}, bf16[128,1024]{1,0:T(8,128)(2,1)S(1)}, u32[]{:S(2)}, u32[]{:S(2)}) collective-permute-start(bf16[128,1024]{1,0:T(8,128)(2,1)S(1)} %get-tuple-element.31), channel_id=1, source_target_pairs={{0,2},{1,9},{2,4},{3,11},{4,6},{5,13},{6,0},{7,15},{8,10},{9,17},{... | collective-permute-start | bytes 786440 | tf_op jit(solution)/shard_map/ppermute | solution.py:32
  86.4 5.4 %collective-permute-start.24 = (bf16[64,1024]{1,0:T(8,128)(2,1)S(1)}, bf16[64,1024]{1,0:T(8,128)(2,1)S(1)}, u32[]{:S(2)}, u32[]{:S(2)}) collective-permute-start(bf16[64,1024]{1,0:T(8,128)(2,1)S(1)} %get-tuple-element.53), channel_id=1, source_target_pairs={{0,1},{1,0},{2,3},{3,2},{4,5},{5,4},{6,7},{7,6},{8,9},{9,8},{10,11... | collective-permute-start | bytes 393224 | tf_op jit(solution)/shard_map/ppermute | solution.py:32
  89.0 5.5 %collective-permute-start.28 = (bf16[64,1024]{1,0:T(8,128)(2,1)S(1)}, bf16[64,1024]{1,0:T(8,128)(2,1)S(1)}, u32[]{:S(2)}, u32[]{:S(2)}) collective-permute-start(bf16[64,1024]{1,0:T(8,128)(2,1)S(1)} %get-tuple-element.37), channel_id=1, source_target_pairs={{0,1},{1,0},{2,3},{3,2},{4,5},{5,4},{6,7},{7,6},{8,9},{9,8},{10,11... | collective-permute-start | bytes 393224 | tf_op jit(solution)/shard_map/ppermute | solution.py:32
  93.5 2.6 %collective-permute-start.27 = (bf16[64,1024]{1,0:T(8,128)(2,1)S(1)}, bf16[64,1024]{1,0:T(8,128)(2,1)S(1)}, u32[]{:S(2)}, u32[]{:S(2)}) collective-permute-start(bf16[64,1024]{1,0:T(8,128)(2,1)S(1)} %get-tuple-element.36), channel_id=1, source_target_pairs={{0,1},{1,0},{2,3},{3,2},{4,5},{5,4},{6,7},{7,6},{8,9},{9,8},{10,11... | collective-permute-start | bytes 393224 | tf_op jit(solution)/shard_map/ppermute | solution.py:32
  (1 other events, 1.2 us)

commit v5 on v3

v5 whole, which is shorter than its diff:
```python
import jax
import jax.numpy as jnp
from jax import lax
from jax.experimental import pallas as pl
from jax.experimental.pallas import tpu as pltpu
from jax.sharding import Mesh
from jax.sharding import PartitionSpec as P

AXES = ("rep", "zl", "y", "x", "c")
SIZES = (2, 4, 4, 4, 2)
ZERO = AXES[1:]
TOKENS = 256


def places():
    for r in range(2):
        for zl in range(4):
            for y in range(4):
                for x in range(4):
                    for c in range(2):
                        yield r, zl, y, x, c


def rank(r, zl, y, x, c):
    return (((r * 4 + zl) * 4 + y) * 4 + x) * 2 + c


def send(value, target):
    pairs = [(rank(*place), rank(*target(*place))) for place in places()]
    return lax.ppermute(value, AXES, pairs)


def swap_cores(value):
    return send(value, lambda r, zl, y, x, c: (r, zl, y, x, 1 - c))


def along_line(value, k):
    return send(value, lambda r, zl, y, x, c: (r, zl ^ k, y, x, c))


def first_turn(value, k):
    return send(
        value,
        lambda r, zl, y, x, c: (r, zl, y, x ^ k, c) if c else (r, zl, y ^ k, x, c),
    )


def second_turn(value, k):
    return send(
        value,
        lambda r, zl, y, x, c: (r, zl, y ^ k, x, c) if c else (r, zl, y, x ^ k, c),
    )


def turned(turn, values):
    got = {k: turn(values[k], k) for k in (1, 3, 2)}
    return [values[0]] + [got[k] for k in (1, 2, 3)]


def column(where, core, k3, k2, z):
    y = where[1] ^ jnp.where(core == 0, k2, k3)
    x = where[2] ^ jnp.where(core == 0, k3, k2)
    return pl.multiple_of(((z * 4 + y) * 4 + x) * 128, 128)


def product(where, turns, pieces, mine, theirs):
    total = jnp.zeros((128, 128), jnp.float32)
    for k3, piece in zip(turns, pieces):
        for k2 in range(4):
            at = [
                pl.ds(column(where, where[3], k3, k2, where[0] ^ kz), 128)
                for kz in range(4)
            ]
            rows = jnp.concatenate(
                [
                    jnp.concatenate([side[:, part] for part in at], axis=1)
                    for side in (mine, theirs)
                ],
                axis=0,
            )
            total += jnp.dot(
                rows,
                piece[k2].reshape(512, 128),
                preferred_element_type=jnp.float32,
            )
    return total


def sums_most(where, p0, p1, p2, mine, theirs, total):
    total[...] = product(where, EARLY, (p0, p1, p2), mine, theirs)


def sums_rest(where, p3, mine, theirs, most, pre):
    total = most[...] + product(where, LATE, (p3,), mine, theirs)
    crossed = jnp.concatenate([total[64:], total[:64]], axis=0)
    pre[...] = jnp.where(where[3] == 0, total, crossed).astype(pre.dtype)


EARLY, LATE = (0, 2, 3), (1,)


def tiles(g, plane, *made):
    x = plane[...].reshape(1024, 256)
    for k, e in enumerate(made):
        part = lax.dot_general(
            g[k ^ (k >> 1)],
            x,
            (((1,), (1,)), ((), ())),
            preferred_element_type=jnp.float32,
        )
        e[...] = (part * (1.0 / TOKENS)).astype(e.dtype)


def assemble(where, *refs):
    core, out = where[3], refs[-1]
    for side in range(2):
        held_by = core if side == 0 else 1 - core
        for k3 in range(4):
            piece = refs[side * 4 + k3]
            for k2 in range(4):
                for j in range(2):
                    at = column(where, held_by, k3, k2, j + 2 * held_by)
                    b = (k2 * 2 + j) * 128
                    out[:, pl.ds(at, 128)] = piece[:, b : b + 128].astype(jnp.float32)


VMEM = pl.BlockSpec(memory_space=pltpu.VMEM)
SMEM = pl.BlockSpec(memory_space=pltpu.SMEM)
PARAMS = pltpu.CompilerParams(vmem_limit_bytes=40 * 1024 * 1024)


def call(body, name, shapes, ins):
    return pl.pallas_call(
        body,
        out_shape=shapes,
        in_specs=ins,
        out_specs=jax.tree.map(lambda _: VMEM, shapes),
        compiler_params=PARAMS,
        name=name,
    )


def on_device(acts, grads_out, act_inverse, grad_inverse):
    bf16, f32 = jnp.bfloat16, jnp.float32
    shape = jax.ShapeDtypeStruct
    c = lax.axis_index("c")
    where = jnp.stack(
        [lax.axis_index("zl"), lax.axis_index("y"), lax.axis_index("x"), c]
    ).astype(jnp.int32)
    first = c == 0

    acts_t, grads_t = acts.T, grads_out.T
    got = swap_cores(jnp.where(first, grads_t, acts_t))
    kept = jnp.where(first, acts_t, grads_t)
    block = jnp.concatenate(
        [jnp.where(first, kept, got), jnp.where(first, got, kept)], axis=0
    )
    line = jnp.stack(turned(along_line, [block] * 4))
    rows = turned(first_turn, [line] * 4)
    rows[1], act_inverse, grad_inverse = lax.optimization_barrier(
        (rows[1], act_inverse, grad_inverse)
    )
    theirs = swap_cores(jnp.where(first, grad_inverse, act_inverse))
    mine = jnp.where(first, act_inverse, grad_inverse)
    plane = jnp.stack(rows)
    pieces = turned(second_turn, [plane] * 4)
    most = call(
        sums_most, "sums_most", shape((128, 128), f32), [SMEM] + [VMEM] * 5
    )(where, *(pieces[k] for k in EARLY), mine, theirs)
    pre = call(
        sums_rest, "sums_rest", shape((128, 128), bf16), [SMEM] + [VMEM] * 4
    )(where, *(pieces[k] for k in LATE), mine, theirs, most)

    sent = jnp.broadcast_to(pre, (8, 128, 128))
    all_planes = lax.all_to_all(sent, ("rep", "zl"), 0, 0, tiled=True)
    all_planes = all_planes.reshape(2, 4, 128, 128)
    here = lax.dynamic_slice_in_dim(all_planes, where[0], 1, axis=1)
    cross = swap_cores(
        jnp.where(first, all_planes[:, 2:], jnp.concatenate([here, here], axis=1))
    )
    pair = jnp.where(first, all_planes[:, :2], cross)
    pair = jnp.concatenate([pair[0], pair[1]], axis=2)
    grad = jnp.where(first, cross[:, 0], here[:, 0])
    grad = jnp.concatenate([grad[0], grad[1]], axis=1)

    grads = jnp.stack([grad, second_turn(grad, 1)])
    plane = jnp.stack(turned(first_turn, [pair] * 4))
    grads = jnp.concatenate([grads, second_turn(grads, 3)], axis=0)
    made = call(tiles, "tiles", [shape((128, 1024), bf16)] * 4, [VMEM] * 2)(
        grads, plane
    )
    whole = turned(second_turn, made)
    own = [jnp.where(first, e[:64], e[64:]) for e in whole]
    sibling = [swap_cores(jnp.where(first, e[64:], e[:64])) for e in whole]
    return call(
        assemble, "assemble", shape((64, 8192), f32), [SMEM] + [VMEM] * 8
    )(where, *own, *sibling)


def solution(mesh):
    finer = Mesh(mesh.devices.reshape(SIZES), AXES)
    return jax.shard_map(
        on_device,
        mesh=finer,
        in_specs=(P("rep", ZERO), P("rep", ZERO), P(ZERO, None), P(ZERO, None)),
        out_specs=P(ZERO, None),
        check_vma=False,
    )
```

time: 88.7 us -> 100 us (1.13)
  waiting for transfers between devices: 29.9 us -> 41.9 us
  other arithmetic: 0.68 us -> 4.55 us
  starting transfers between devices: 49.7 us -> 46.6 us
  local copies, waits for them, and re-layouts: 2.61 us -> 0.76 us
    all_to_all x0 -> x1, waiting for transfers between devices: none -> 9.44 us  [on_device(): all_planes = lax.all_to_all(sent, ('rep', 'zl'), 0, 0, tiled=True)]
    ppermute x29 -> x24, starting transfers between devices: 49.7 us -> 41.2 us  [send(): return lax.ppermute(value, AXES, pairs)]
    all_to_all x0 -> x1, starting transfers between devices: none -> 5.49 us  [on_device(): all_planes = lax.all_to_all(sent, ('rep', 'zl'), 0, 0, tiled=True)]
    select_n x3 -> x5, other arithmetic: 0.04 us -> 3.42 us  [the longest x1 2.65 us: on_device(): theirs = swap_cores(jnp.where(first, grad_inverse, act_inverse))]
    ppermute x29 -> x24, waiting for transfers between devices: 29.9 us -> 32.4 us  [send(): return lax.ppermute(value, AXES, pairs)]
    unnamed x8 -> x0, local copies, waits for them, and re-layouts: 2.46 us -> none
  transfers between devices with their start and end apart: 29 -> 25, of which waited for: 18 -> 15; matrix products, arithmetic and copies ran while one was open for 1% -> 0% of each run, Pallas kernels for 0% -> 2%
where the time goes in v5:
time: 100 us; the launch traced here: 99.7 us
  starting transfers between devices  46.6 us (47%)
  waiting for transfers between devices  41.9 us (42%)
  Pallas kernels  5.72 us (6%)
  other arithmetic  4.55 us (5%)
    ppermute x24, starting transfers between devices, send(): return lax.ppermute(value, AXES, pairs)  41.2 us
    ppermute x24, waiting for transfers between devices, send(): return lax.ppermute(value, AXES, pairs)  32.4 us
    all_to_all x1, waiting for transfers between devices, on_device(): all_planes = lax.all_to_all(sent, ('rep', 'zl'), 0, 0, tiled=True)  9.44 us
    all_to_all x1, starting transfers between devices, on_device(): all_planes = lax.all_to_all(sent, ('rep', 'zl'), 0, 0, tiled=True)  5.49 us
    select_n x1, other arithmetic, on_device(): theirs = swap_cores(jnp.where(first, grad_inverse, act_inverse))  2.65 us
    pallas_call x1, Pallas kernels, on_device(): call(assemble, 'assemble', shape((64, 8192), f32), [SMEM] + [VMEM] * 8)  2.24 us
  transfers between devices with their start and end apart: 25, of which 15 were waited for; matrix products, arithmetic and copies ran while one was open for 0% of the time, Pallas kernels for 2%

profile of v5, /device:TPU:1, one launch (start us, length us, event | category | flops | bytes accessed | tf_op | source)
XLA Modules:
  0.0 99.7 jit_solution(3926192536988109373)
XLA Ops:
  0.7 3.2 %collective-permute-start = (bf16[64,128]{1,0:T(8,128)(2,1)S(1)}, bf16[64,128]{1,0:T(8,128)(2,1)S(1)}, u32[]{:S(2)}, u32[]{:S(2)}) collective-permute-start(bf16[64,128]{1,0:T(8,128)(2,1)S(1)} %select_bitcast_fusion), channel_id=1, source_target_pairs={{0,1},{1,0},{2,3},{3,2},{4,5},{5,4},{6,7},{7,6},{8,9},{9,8},{10,11... | collective-permute-start | bytes 49160 | tf_op jit(solution)/shard_map/ppermute | solution.py:30
  5.6 2.9 %collective-permute-start.2 = (bf16[128,128]{1,0:T(8,128)(2,1)S(1)}, bf16[128,128]{1,0:T(8,128)(2,1)S(1)}, u32[]{:S(2)}, u32[]{:S(2)}) collective-permute-start(bf16[128,128]{1,0:T(8,128)(2,1)S(1)} %get-tuple-element.42), channel_id=1, source_target_pairs={{0,64},{1,65},{2,66},{3,67},{4,68},{5,69},{6,70},{7,71},{8,72},{9,... | collective-permute-start | bytes 98312 | tf_op jit(solution)/shard_map/ppermute | solution.py:30
  9.8 3.3 %collective-permute-done.3 = bf16[128,128]{1,0:T(8,128)(2,1)S(1)} collective-permute-done((bf16[128,128]{1,0:T(8,128)(2,1)S(1)}, bf16[128,128]{1,0:T(8,128)(2,1)S(1)}, u32[]{:S(2)}, u32[]{:S(2)}) %collective-permute-start.3) | collective-permute-done | bytes 32800 | tf_op jit(solution)/shard_map/ppermute | solution.py:30
  13.1 1.3 %collective-permute-start.4 = (bf16[4,128,128]{2,1,0:T(8,128)(2,1)S(1)}, bf16[4,128,128]{2,1,0:T(8,128)(2,1)S(1)}, u32[]{:S(2)}, u32[]{:S(2)}) collective-permute-start(bf16[4,128,128]{2,1,0:T(8,128)(2,1)S(1)} %get-tuple-element.34), channel_id=1, source_target_pairs={{0,8},{1,3},{2,10},{3,1},{4,12},{5,7},{6,14},{7,5},{8,0},{9,11},{1... | collective-permute-start | bytes 393224 | tf_op jit(solution)/shard_map/ppermute | solution.py:30
  14.4 2.6 %collective-permute-done.4 = bf16[4,128,128]{2,1,0:T(8,128)(2,1)S(1)} collective-permute-done((bf16[4,128,128]{2,1,0:T(8,128)(2,1)S(1)}, bf16[4,128,128]{2,1,0:T(8,128)(2,1)S(1)}, u32[]{:S(2)}, u32[]{:S(2)}) %collective-permute-start.4) | collective-permute-done | bytes 131104 | tf_op jit(solution)/shard_map/ppermute | solution.py:30
  17.0 2.6 %broadcast_select_fusion = (bf16[64,8192]{1,0:T(8,128)(2,1)}, bf16[64,8192]{1,0:T(8,128)(2,1)S(1)}) fusion(bf16[64,8192]{1,0:T(8,128)(2,1)} %param.7, bf16[64,8192]{1,0:T(8,128)(2,1)} %param.6, pred[]{:T(512)S(6)} %eq.3), kind=kLoop, calls=%fused_computation | loop fusion | flops 1048576 | bytes 4194305 | tf_op jit(solution)/shard_map/jit(_where)/select_n | solution.py:163
  19.7 3.2 %collective-permute-start.8 = (bf16[64,8192]{1,0:T(8,128)(2,1)}, bf16[64,8192]{1,0:T(8,128)(2,1)S(1)}, u32[]{:S(2)}, u32[]{:S(2)}) collective-permute-start(bf16[64,8192]{1,0:T(8,128)(2,1)} %get-tuple-element.19), channel_id=1, source_target_pairs={{0,1},{1,0},{2,3},{3,2},{4,5},{5,4},{6,7},{7,6},{8,9},{9,8},{10,11... | collective-permute-start | bytes 3145736 | tf_op jit(solution)/shard_map/ppermute | solution.py:30
  22.9 2.7 %collective-permute-start.5 = (bf16[4,128,128]{2,1,0:T(8,128)(2,1)S(1)}, bf16[4,128,128]{2,1,0:T(8,128)(2,1)S(1)}, u32[]{:S(2)}, u32[]{:S(2)}) collective-permute-start(bf16[4,128,128]{2,1,0:T(8,128)(2,1)S(1)} %get-tuple-element.34), channel_id=1, source_target_pairs={{0,16},{1,5},{2,18},{3,7},{4,20},{5,1},{6,22},{7,3},{8,24},{9,13},... | collective-permute-start | bytes 393224 | tf_op jit(solution)/shard_map/ppermute | solution.py:30
  26.5 2.0 %collective-permute-done.5 = bf16[4,128,128]{2,1,0:T(8,128)(2,1)S(1)} collective-permute-done((bf16[4,128,128]{2,1,0:T(8,128)(2,1)S(1)}, bf16[4,128,128]{2,1,0:T(8,128)(2,1)S(1)}, u32[]{:S(2)}, u32[]{:S(2)}) %collective-permute-start.5) | collective-permute-done | bytes 131104 | tf_op jit(solution)/shard_map/ppermute | solution.py:30
  28.5 2.5 %collective-permute-done.6 = bf16[4,128,128]{2,1,0:T(8,128)(2,1)S(1)} collective-permute-done((bf16[4,128,128]{2,1,0:T(8,128)(2,1)S(1)}, bf16[4,128,128]{2,1,0:T(8,128)(2,1)S(1)}, u32[]{:S(2)}, u32[]{:S(2)}) %collective-permute-start.6) | collective-permute-done | bytes 131104 | tf_op jit(solution)/shard_map/ppermute | solution.py:30
  31.0 2.5 %collective-permute-start.10 = (bf16[4,4,128,128]{3,2,1,0:T(8,128)(2,1)S(1)}, bf16[4,4,128,128]{3,2,1,0:T(8,128)(2,1)}, u32[]{:S(2)}, u32[]{:S(2)}) collective-permute-start(bf16[4,4,128,128]{3,2,1,0:T(8,128)(2,1)S(1)} %pad_maximum_fusion.p0), channel_id=1, source_target_pairs={{0,6},{1,25},{2,4},{3,27},{4,2},{5,29},{6,0},{7,31},{8,14},{9,17},... | collective-permute-start | bytes 1572872 | tf_op jit(solution)/shard_map/ppermute | solution.py:30
  34.4 11.9 %collective-permute-done.10.p2 = bf16[4,4,128,128]{3,2,1,0:T(8,128)(2,1)} collective-permute-done((bf16[4,4,128,128]{3,2,1,0:T(8,128)(2,1)S(1)}, bf16[4,4,128,128]{3,2,1,0:T(8,128)(2,1)}, u32[]{:S(2)}, u32[]{:S(2)}) %collective-permute-start.10) | collective-permute-done | bytes 524320 | tf_op jit(solution)/shard_map/ppermute | solution.py:30
  46.4 1.8 %sums_most.1.most = f32[128,128]{1,0:T(8,128)S(1)} custom-call(s32[4]{0:T(128)S(1)} %pad_add_fusion.where, bf16[4,4,128,128]{3,2,1,0:T(8,128)(2,1)S(1)} %pad_maximum_fusion.p0, bf16[4,4,128,128]{3,2,1,0:T(8,128)(2,1)} %collective-permute-done.9.p1, bf16[4,4,128,128]{3,2,1,0:T(8,128)(2,1)} %collective-permute-done.10.p2, ...), custom_call_target="tpu_custom_call" | custom-call | tf_op jit(solution)/shard_map/sums_most/pallas_call | solution.py:167
  49.8 5.5 %all-to-all-start = ((bf16[8,128,128]{2,1,0:T(8,128)(2,1)}), bf16[8,128,128]{2,1,0:T(8,128)(2,1)S(1)}, u32[]{:S(2)}, u32[]{:S(2)}) async-start(bf16[8,128,128]{2,1,0:T(8,128)(2,1)} %broadcast_in_dim.3), calls=%async_computation | async-start | bytes 524288 | tf_op jit(solution)/shard_map/all_to_all | solution.py:175
  55.3 9.4 %all-to-all-done = bf16[8,128,128]{2,1,0:T(8,128)(2,1)S(1)} async-done(((bf16[8,128,128]{2,1,0:T(8,128)(2,1)}), bf16[8,128,128]{2,1,0:T(8,128)(2,1)S(1)}, u32[]{:S(2)}, u32[]{:S(2)}) %all-to-all-start) | async-done | bytes 262176 | tf_op jit(solution)/shard_map/all_to_all | solution.py:175
  64.8 3.6 %collective-permute-start.11 = (bf16[2,2,128,128]{3,2,1,0:T(8,128)(2,1)S(1)}, bf16[2,2,128,128]{3,2,1,0:T(8,128)(2,1)S(1)}, u32[]{:S(2)}, u32[]{:S(2)}) collective-permute-start(bf16[2,2,128,128]{3,2,1,0:T(8,128)(2,1)S(1)} %slice_select_fusion.1), channel_id=1, source_target_pairs={{0,1},{1,0},{2,3},{3,2},{4,5},{5,4},{6,7},{7,6},{8,9},{9,8},{10,11... | collective-permute-start | bytes 393224 | tf_op jit(solution)/shard_map/ppermute | solution.py:30
  68.3 1.0 collective-permute-done.11
  69.8 3.5 %collective-permute-start.15 = (bf16[2,128,256]{2,1,0:T(8,128)(2,1)S(1)}, bf16[2,128,256]{2,1,0:T(8,128)(2,1)S(1)}, u32[]{:S(2)}, u32[]{:S(2)}) collective-permute-start(bf16[2,128,256]{2,1,0:T(8,128)(2,1)S(1)} %get-tuple-element.30), channel_id=1, source_target_pairs={{0,16},{1,5},{2,18},{3,7},{4,20},{5,1},{6,22},{7,3},{8,24},{9,13},... | collective-permute-start | bytes 393224 | tf_op jit(solution)/shard_map/ppermute | solution.py:30
  73.5 2.4 %collective-permute-start.13 = (bf16[2,128,256]{2,1,0:T(8,128)(2,1)S(1)}, bf16[2,128,256]{2,1,0:T(8,128)(2,1)S(1)}, u32[]{:S(2)}, u32[]{:S(2)}) collective-permute-start(bf16[2,128,256]{2,1,0:T(8,128)(2,1)S(1)} %pad_maximum_fusion.4), channel_id=1, source_target_pairs={{0,6},{1,25},{2,4},{3,27},{4,2},{5,29},{6,0},{7,31},{8,14},{9,17},... | collective-permute-start | bytes 393224 | tf_op jit(solution)/shard_map/ppermute | solution.py:30
  75.9 2.1 %collective-permute-done.15 = bf16[2,128,256]{2,1,0:T(8,128)(2,1)S(1)} collective-permute-done((bf16[2,128,256]{2,1,0:T(8,128)(2,1)S(1)}, bf16[2,128,256]{2,1,0:T(8,128)(2,1)S(1)}, u32[]{:S(2)}, u32[]{:S(2)}) %collective-permute-start.15) | collective-permute-done | bytes 131104 | tf_op jit(solution)/shard_map/ppermute | solution.py:30
  78.0 1.4 %collective-permute-done.16 = bf16[2,128,256]{2,1,0:T(8,128)(2,1)S(1)} collective-permute-done((bf16[2,128,256]{2,1,0:T(8,128)(2,1)S(1)}, bf16[2,128,256]{2,1,0:T(8,128)(2,1)S(1)}, u32[]{:S(2)}, u32[]{:S(2)}) %collective-permute-start.16) | collective-permute-done | bytes 131104 | tf_op jit(solution)/shard_map/ppermute | solution.py:30
  79.5 1.3 %collective-permute-done.13 = bf16[2,128,256]{2,1,0:T(8,128)(2,1)S(1)} collective-permute-done((bf16[2,128,256]{2,1,0:T(8,128)(2,1)S(1)}, bf16[2,128,256]{2,1,0:T(8,128)(2,1)S(1)}, u32[]{:S(2)}, u32[]{:S(2)}) %collective-permute-start.13) | collective-permute-done | bytes 131104 | tf_op jit(solution)/shard_map/ppermute | solution.py:30
  81.6 1.2 %collective-permute-start.17 = (bf16[128,1024]{1,0:T(8,128)(2,1)S(1)}, bf16[128,1024]{1,0:T(8,128)(2,1)S(1)}, u32[]{:S(2)}, u32[]{:S(2)}) collective-permute-start(bf16[128,1024]{1,0:T(8,128)(2,1)S(1)} %get-tuple-element.16), channel_id=1, source_target_pairs={{0,2},{1,9},{2,0},{3,11},{4,6},{5,13},{6,4},{7,15},{8,10},{9,1},{1... | collective-permute-start | bytes 786440 | tf_op jit(solution)/shard_map/ppermute | solution.py:30
  82.8 1.5 %collective-permute-start.18 = (bf16[128,1024]{1,0:T(8,128)(2,1)S(1)}, bf16[128,1024]{1,0:T(8,128)(2,1)S(1)}, u32[]{:S(2)}, u32[]{:S(2)}) collective-permute-start(bf16[128,1024]{1,0:T(8,128)(2,1)S(1)} %get-tuple-element.17), channel_id=1, source_target_pairs={{0,4},{1,17},{2,6},{3,19},{4,0},{5,21},{6,2},{7,23},{8,12},{9,25},... | collective-permute-start | bytes 786440 | tf_op jit(solution)/shard_map/ppermute | solution.py:30
  84.3 1.4 %collective-permute-start.19 = (bf16[128,1024]{1,0:T(8,128)(2,1)S(1)}, bf16[128,1024]{1,0:T(8,128)(2,1)S(1)}, u32[]{:S(2)}, u32[]{:S(2)}) collective-permute-start(bf16[128,1024]{1,0:T(8,128)(2,1)S(1)} %get-tuple-element.18), channel_id=1, source_target_pairs={{0,6},{1,25},{2,4},{3,27},{4,2},{5,29},{6,0},{7,31},{8,14},{9,17},... | collective-permute-start | bytes 786440 | tf_op jit(solution)/shard_map/ppermute | solution.py:30
  85.8 1.9 %collective-permute-start.20 = (bf16[64,1024]{1,0:T(8,128)(2,1)S(1)}, bf16[64,1024]{1,0:T(8,128)(2,1)S(1)}, u32[]{:S(2)}, u32[]{:S(2)}) collective-permute-start(bf16[64,1024]{1,0:T(8,128)(2,1)S(1)} %get-tuple-element.27), channel_id=1, source_target_pairs={{0,1},{1,0},{2,3},{3,2},{4,5},{5,4},{6,7},{7,6},{8,9},{9,8},{10,11... | collective-permute-start | bytes 393224 | tf_op jit(solution)/shard_map/ppermute | solution.py:30
  87.7 1.6 %collective-permute-start.21 = (bf16[64,1024]{1,0:T(8,128)(2,1)S(1)}, bf16[64,1024]{1,0:T(8,128)(2,1)S(1)}, u32[]{:S(2)}, u32[]{:S(2)}) collective-permute-start(bf16[64,1024]{1,0:T(8,128)(2,1)S(1)} %get-tuple-element.25), channel_id=1, source_target_pairs={{0,1},{1,0},{2,3},{3,2},{4,5},{5,4},{6,7},{7,6},{8,9},{9,8},{10,11... | collective-permute-start | bytes 393224 | tf_op jit(solution)/shard_map/ppermute | solution.py:30
  89.4 1.9 %collective-permute-done.18 = bf16[128,1024]{1,0:T(8,128)(2,1)S(1)} collective-permute-done((bf16[128,1024]{1,0:T(8,128)(2,1)S(1)}, bf16[128,1024]{1,0:T(8,128)(2,1)S(1)}, u32[]{:S(2)}, u32[]{:S(2)}) %collective-permute-start.18) | collective-permute-done | bytes 262176 | tf_op jit(solution)/shard_map/ppermute | solution.py:30
  91.2 2.5 %collective-permute-start.22 = (bf16[64,1024]{1,0:T(8,128)(2,1)S(1)}, bf16[64,1024]{1,0:T(8,128)(2,1)S(1)}, u32[]{:S(2)}, u32[]{:S(2)}) collective-permute-start(bf16[64,1024]{1,0:T(8,128)(2,1)S(1)} %get-tuple-element.23), channel_id=1, source_target_pairs={{0,1},{1,0},{2,3},{3,2},{4,5},{5,4},{6,7},{7,6},{8,9},{9,8},{10,11... | collective-permute-start | bytes 393224 | tf_op jit(solution)/shard_map/ppermute | solution.py:30
  93.9 2.6 %collective-permute-start.23 = (bf16[64,1024]{1,0:T(8,128)(2,1)S(1)}, bf16[64,1024]{1,0:T(8,128)(2,1)S(1)}, u32[]{:S(2)}, u32[]{:S(2)}) collective-permute-start(bf16[64,1024]{1,0:T(8,128)(2,1)S(1)} %get-tuple-element.21), channel_id=1, source_target_pairs={{0,1},{1,0},{2,3},{3,2},{4,5},{5,4},{6,7},{7,6},{8,9},{9,8},{10,11... | collective-permute-start | bytes 393224 | tf_op jit(solution)/shard_map/ppermute | solution.py:30
  96.5 1.0 collective-permute-done.23.refs_7_
  97.5 2.2 %assemble.1 = f32[64,8192]{1,0:T(8,128)} custom-call(s32[4]{0:T(128)S(1)} %pad_add_fusion.where, bf16[64,1024]{1,0:T(8,128)(2,1)S(1)} %get-tuple-element.28.refs_0_, bf16[64,1024]{1,0:T(8,128)(2,1)S(1)} %get-tuple-element.26.refs_1_, bf16[64,1024]{1,0:T(8,128)(2,1)S(1)} %get-tuple-element.24.refs_2_, bf16[64,1024]{1,0:T(8,128)(2,1)S(1)} %get-tuple-element.22.refs_3_, ...), custom_call_target="tpu_custom_call" | custom-call | tf_op jit(solution)/shard_map/assemble/pallas_call | solution.py:195
  (45 shorter events, 8.9 us)
Async XLA Ops:
  0.7 4.1 %collective-permute-start = (bf16[64,128]{1,0:T(8,128)(2,1)S(1)}, bf16[64,128]{1,0:T(8,128)(2,1)S(1)}, u32[]{:S(2)}, u32[]{:S(2)}) collective-permute-start(bf16[64,128]{1,0:T(8,128)(2,1)S(1)} %select_bitcast_fusion), channel_id=1, source_target_pairs={{0,1},{1,0},{2,3},{3,2},{4,5},{5,4},{6,7},{7,6},{8,9},{9,8},{10,11... | collective-permute-start | bytes 49160 | tf_op jit(solution)/shard_map/ppermute | solution.py:30
  5.5 3.6 %collective-permute-start.1 = (bf16[128,128]{1,0:T(8,128)(2,1)S(1)}, bf16[128,128]{1,0:T(8,128)(2,1)S(1)}, u32[]{:S(2)}, u32[]{:S(2)}) collective-permute-start(bf16[128,128]{1,0:T(8,128)(2,1)S(1)} %get-tuple-element.42), channel_id=1, source_target_pairs={{0,32},{1,33},{2,34},{3,35},{4,36},{5,37},{6,38},{7,39},{8,40},{9,... | collective-permute-start | bytes 98312 | tf_op jit(solution)/shard_map/ppermute | solution.py:30
  5.6 4.2 %collective-permute-start.2 = (bf16[128,128]{1,0:T(8,128)(2,1)S(1)}, bf16[128,128]{1,0:T(8,128)(2,1)S(1)}, u32[]{:S(2)}, u32[]{:S(2)}) collective-permute-start(bf16[128,128]{1,0:T(8,128)(2,1)S(1)} %get-tuple-element.42), channel_id=1, source_target_pairs={{0,64},{1,65},{2,66},{3,67},{4,68},{5,69},{6,70},{7,71},{8,72},{9,... | collective-permute-start | bytes 98312 | tf_op jit(solution)/shard_map/ppermute | solution.py:30
  8.5 4.6 %collective-permute-start.3 = (bf16[128,128]{1,0:T(8,128)(2,1)S(1)}, bf16[128,128]{1,0:T(8,128)(2,1)S(1)}, u32[]{:S(2)}, u32[]{:S(2)}) collective-permute-start(bf16[128,128]{1,0:T(8,128)(2,1)S(1)} %get-tuple-element.42), channel_id=1, source_target_pairs={{0,96},{1,97},{2,98},{3,99},{4,100},{5,101},{6,102},{7,103},{8,104... | collective-permute-start | bytes 98312 | tf_op jit(solution)/shard_map/ppermute | solution.py:30
  13.1 3.9 %collective-permute-start.4 = (bf16[4,128,128]{2,1,0:T(8,128)(2,1)S(1)}, bf16[4,128,128]{2,1,0:T(8,128)(2,1)S(1)}, u32[]{:S(2)}, u32[]{:S(2)}) collective-permute-start(bf16[4,128,128]{2,1,0:T(8,128)(2,1)S(1)} %get-tuple-element.34), channel_id=1, source_target_pairs={{0,8},{1,3},{2,10},{3,1},{4,12},{5,7},{6,14},{7,5},{8,0},{9,11},{1... | collective-permute-start | bytes 393224 | tf_op jit(solution)/shard_map/ppermute | solution.py:30
  19.7 26.7 %collective-permute-start.8 = (bf16[64,8192]{1,0:T(8,128)(2,1)}, bf16[64,8192]{1,0:T(8,128)(2,1)S(1)}, u32[]{:S(2)}, u32[]{:S(2)}) collective-permute-start(bf16[64,8192]{1,0:T(8,128)(2,1)} %get-tuple-element.19), channel_id=1, source_target_pairs={{0,1},{1,0},{2,3},{3,2},{4,5},{5,4},{6,7},{7,6},{8,9},{9,8},{10,11... | collective-permute-start | bytes 3145736 | tf_op jit(solution)/shard_map/ppermute | solution.py:30
  22.9 5.6 %collective-permute-start.5 = (bf16[4,128,128]{2,1,0:T(8,128)(2,1)S(1)}, bf16[4,128,128]{2,1,0:T(8,128)(2,1)S(1)}, u32[]{:S(2)}, u32[]{:S(2)}) collective-permute-start(bf16[4,128,128]{2,1,0:T(8,128)(2,1)S(1)} %get-tuple-element.34), channel_id=1, source_target_pairs={{0,16},{1,5},{2,18},{3,7},{4,20},{5,1},{6,22},{7,3},{8,24},{9,13},... | collective-permute-start | bytes 393224 | tf_op jit(solution)/shard_map/ppermute | solution.py:30
  25.6 5.3 %collective-permute-start.6 = (bf16[4,128,128]{2,1,0:T(8,128)(2,1)S(1)}, bf16[4,128,128]{2,1,0:T(8,128)(2,1)S(1)}, u32[]{:S(2)}, u32[]{:S(2)}) collective-permute-start(bf16[4,128,128]{2,1,0:T(8,128)(2,1)S(1)} %get-tuple-element.34), channel_id=1, source_target_pairs={{0,24},{1,7},{2,26},{3,5},{4,28},{5,3},{6,30},{7,1},{8,16},{9,15},... | collective-permute-start | bytes 393224 | tf_op jit(solution)/shard_map/ppermute | solution.py:30
  31.0 15.3 %collective-permute-start.10 = (bf16[4,4,128,128]{3,2,1,0:T(8,128)(2,1)S(1)}, bf16[4,4,128,128]{3,2,1,0:T(8,128)(2,1)}, u32[]{:S(2)}, u32[]{:S(2)}) collective-permute-start(bf16[4,4,128,128]{3,2,1,0:T(8,128)(2,1)S(1)} %pad_maximum_fusion.p0), channel_id=1, source_target_pairs={{0,6},{1,25},{2,4},{3,27},{4,2},{5,29},{6,0},{7,31},{8,14},{9,17},... | collective-permute-start | bytes 1572872 | tf_op jit(solution)/shard_map/ppermute | solution.py:30
  33.5 12.8 %collective-permute-start.9 = (bf16[4,4,128,128]{3,2,1,0:T(8,128)(2,1)S(1)}, bf16[4,4,128,128]{3,2,1,0:T(8,128)(2,1)}, u32[]{:S(2)}, u32[]{:S(2)}) collective-permute-start(bf16[4,4,128,128]{3,2,1,0:T(8,128)(2,1)S(1)} %pad_maximum_fusion.p0), channel_id=1, source_target_pairs={{0,4},{1,17},{2,6},{3,19},{4,0},{5,21},{6,2},{7,23},{8,12},{9,25},... | collective-permute-start | bytes 1572872 | tf_op jit(solution)/shard_map/ppermute | solution.py:30
  33.9 14.3 %collective-permute-start.7 = (bf16[4,4,128,128]{3,2,1,0:T(8,128)(2,1)S(1)}, bf16[4,4,128,128]{3,2,1,0:T(8,128)(2,1)S(1)}, u32[]{:S(2)}, u32[]{:S(2)}) collective-permute-start(bf16[4,4,128,128]{3,2,1,0:T(8,128)(2,1)S(1)} %pad_maximum_fusion.p0), channel_id=1, source_target_pairs={{0,2},{1,9},{2,0},{3,11},{4,6},{5,13},{6,4},{7,15},{8,10},{9,1},{1... | collective-permute-start | bytes 1572872 | tf_op jit(solution)/shard_map/ppermute | solution.py:30
  49.8 14.9 %all-to-all-start = ((bf16[8,128,128]{2,1,0:T(8,128)(2,1)}), bf16[8,128,128]{2,1,0:T(8,128)(2,1)S(1)}, u32[]{:S(2)}, u32[]{:S(2)}) async-start(bf16[8,128,128]{2,1,0:T(8,128)(2,1)} %broadcast_in_dim.3), calls=%async_computation | async-start | bytes 524288 | tf_op jit(solution)/shard_map/all_to_all | solution.py:175
  64.8 4.6 %collective-permute-start.11 = (bf16[2,2,128,128]{3,2,1,0:T(8,128)(2,1)S(1)}, bf16[2,2,128,128]{3,2,1,0:T(8,128)(2,1)S(1)}, u32[]{:S(2)}, u32[]{:S(2)}) collective-permute-start(bf16[2,2,128,128]{3,2,1,0:T(8,128)(2,1)S(1)} %slice_select_fusion.1), channel_id=1, source_target_pairs={{0,1},{1,0},{2,3},{3,2},{4,5},{5,4},{6,7},{7,6},{8,9},{9,8},{10,11... | collective-permute-start | bytes 393224 | tf_op jit(solution)/shard_map/ppermute | solution.py:30
  69.4 4.1 %collective-permute-start.12 = (bf16[128,256]{1,0:T(8,128)(2,1)S(1)}, bf16[128,256]{1,0:T(8,128)(2,1)S(1)}, u32[]{:S(2)}, u32[]{:S(2)}) collective-permute-start(bf16[128,256]{1,0:T(8,128)(2,1)S(1)} %get-tuple-element.36), channel_id=1, source_target_pairs={{0,2},{1,9},{2,0},{3,11},{4,6},{5,13},{6,4},{7,15},{8,10},{9,1},{1... | collective-permute-start | bytes 196616 | tf_op jit(solution)/shard_map/ppermute | solution.py:30
  69.5 6.4 %collective-permute-start.14 = (bf16[2,128,256]{2,1,0:T(8,128)(2,1)S(1)}, bf16[2,128,256]{2,1,0:T(8,128)(2,1)S(1)}, u32[]{:S(2)}, u32[]{:S(2)}) collective-permute-start(bf16[2,128,256]{2,1,0:T(8,128)(2,1)S(1)} %get-tuple-element.30), channel_id=1, source_target_pairs={{0,8},{1,3},{2,10},{3,1},{4,12},{5,7},{6,14},{7,5},{8,0},{9,11},{1... | collective-permute-start | bytes 393224 | tf_op jit(solution)/shard_map/ppermute | solution.py:30
  69.8 8.3 %collective-permute-start.15 = (bf16[2,128,256]{2,1,0:T(8,128)(2,1)S(1)}, bf16[2,128,256]{2,1,0:T(8,128)(2,1)S(1)}, u32[]{:S(2)}, u32[]{:S(2)}) collective-permute-start(bf16[2,128,256]{2,1,0:T(8,128)(2,1)S(1)} %get-tuple-element.30), channel_id=1, source_target_pairs={{0,16},{1,5},{2,18},{3,7},{4,20},{5,1},{6,22},{7,3},{8,24},{9,13},... | collective-permute-start | bytes 393224 | tf_op jit(solution)/shard_map/ppermute | solution.py:30
  73.3 6.2 %collective-permute-start.16 = (bf16[2,128,256]{2,1,0:T(8,128)(2,1)S(1)}, bf16[2,128,256]{2,1,0:T(8,128)(2,1)S(1)}, u32[]{:S(2)}, u32[]{:S(2)}) collective-permute-start(bf16[2,128,256]{2,1,0:T(8,128)(2,1)S(1)} %get-tuple-element.30), channel_id=1, source_target_pairs={{0,24},{1,7},{2,26},{3,5},{4,28},{5,3},{6,30},{7,1},{8,16},{9,15},... | collective-permute-start | bytes 393224 | tf_op jit(solution)/shard_map/ppermute | solution.py:30
  73.5 7.3 %collective-permute-start.13 = (bf16[2,128,256]{2,1,0:T(8,128)(2,1)S(1)}, bf16[2,128,256]{2,1,0:T(8,128)(2,1)S(1)}, u32[]{:S(2)}, u32[]{:S(2)}) collective-permute-start(bf16[2,128,256]{2,1,0:T(8,128)(2,1)S(1)} %pad_maximum_fusion.4), channel_id=1, source_target_pairs={{0,6},{1,25},{2,4},{3,27},{4,2},{5,29},{6,0},{7,31},{8,14},{9,17},... | collective-permute-start | bytes 393224 | tf_op jit(solution)/shard_map/ppermute | solution.py:30
  81.6 6.1 %collective-permute-start.17 = (bf16[128,1024]{1,0:T(8,128)(2,1)S(1)}, bf16[128,1024]{1,0:T(8,128)(2,1)S(1)}, u32[]{:S(2)}, u32[]{:S(2)}) collective-permute-start(bf16[128,1024]{1,0:T(8,128)(2,1)S(1)} %get-tuple-element.16), channel_id=1, source_target_pairs={{0,2},{1,9},{2,0},{3,11},{4,6},{5,13},{6,4},{7,15},{8,10},{9,1},{1... | collective-permute-start | bytes 786440 | tf_op jit(solution)/shard_map/ppermute | solution.py:30
  82.8 8.4 %collective-permute-start.18 = (bf16[128,1024]{1,0:T(8,128)(2,1)S(1)}, bf16[128,1024]{1,0:T(8,128)(2,1)S(1)}, u32[]{:S(2)}, u32[]{:S(2)}) collective-permute-start(bf16[128,1024]{1,0:T(8,128)(2,1)S(1)} %get-tuple-element.17), channel_id=1, source_target_pairs={{0,4},{1,17},{2,6},{3,19},{4,0},{5,21},{6,2},{7,23},{8,12},{9,25},... | collective-permute-start | bytes 786440 | tf_op jit(solution)/shard_map/ppermute | solution.py:30
  84.3 9.5 %collective-permute-start.19 = (bf16[128,1024]{1,0:T(8,128)(2,1)S(1)}, bf16[128,1024]{1,0:T(8,128)(2,1)S(1)}, u32[]{:S(2)}, u32[]{:S(2)}) collective-permute-start(bf16[128,1024]{1,0:T(8,128)(2,1)S(1)} %get-tuple-element.18), channel_id=1, source_target_pairs={{0,6},{1,25},{2,4},{3,27},{4,2},{5,29},{6,0},{7,31},{8,14},{9,17},... | collective-permute-start | bytes 786440 | tf_op jit(solution)/shard_map/ppermute | solution.py:30
  85.8 10.7 %collective-permute-start.20 = (bf16[64,1024]{1,0:T(8,128)(2,1)S(1)}, bf16[64,1024]{1,0:T(8,128)(2,1)S(1)}, u32[]{:S(2)}, u32[]{:S(2)}) collective-permute-start(bf16[64,1024]{1,0:T(8,128)(2,1)S(1)} %get-tuple-element.27), channel_id=1, source_target_pairs={{0,1},{1,0},{2,3},{3,2},{4,5},{5,4},{6,7},{7,6},{8,9},{9,8},{10,11... | collective-permute-start | bytes 393224 | tf_op jit(solution)/shard_map/ppermute | solution.py:30
  87.7 8.8 %collective-permute-start.21 = (bf16[64,1024]{1,0:T(8,128)(2,1)S(1)}, bf16[64,1024]{1,0:T(8,128)(2,1)S(1)}, u32[]{:S(2)}, u32[]{:S(2)}) collective-permute-start(bf16[64,1024]{1,0:T(8,128)(2,1)S(1)} %get-tuple-element.25), channel_id=1, source_target_pairs={{0,1},{1,0},{2,3},{3,2},{4,5},{5,4},{6,7},{7,6},{8,9},{9,8},{10,11... | collective-permute-start | bytes 393224 | tf_op jit(solution)/shard_map/ppermute | solution.py:30
  91.2 5.2 %collective-permute-start.22 = (bf16[64,1024]{1,0:T(8,128)(2,1)S(1)}, bf16[64,1024]{1,0:T(8,128)(2,1)S(1)}, u32[]{:S(2)}, u32[]{:S(2)}) collective-permute-start(bf16[64,1024]{1,0:T(8,128)(2,1)S(1)} %get-tuple-element.23), channel_id=1, source_target_pairs={{0,1},{1,0},{2,3},{3,2},{4,5},{5,4},{6,7},{7,6},{8,9},{9,8},{10,11... | collective-permute-start | bytes 393224 | tf_op jit(solution)/shard_map/ppermute | solution.py:30
  93.9 3.6 %collective-permute-start.23 = (bf16[64,1024]{1,0:T(8,128)(2,1)S(1)}, bf16[64,1024]{1,0:T(8,128)(2,1)S(1)}, u32[]{:S(2)}, u32[]{:S(2)}) collective-permute-start(bf16[64,1024]{1,0:T(8,128)(2,1)S(1)} %get-tuple-element.21), channel_id=1, source_target_pairs={{0,1},{1,0},{2,3},{3,2},{4,5},{5,4},{6,7},{7,6},{8,9},{9,8},{10,11... | collective-permute-start | bytes 393224 | tf_op jit(solution)/shard_map/ppermute | solution.py:30

commit v6 on v5

--- a/solution.py
+++ b/solution.py
@@ -52,51 +52,58 @@
     )
 
 
+def to_parity(value, j, other_rep):
+    def target(r, zl, y, x, c):
+        return r ^ other_rep, zl ^ (2 * j + c), y, x, zl % 2
+
+    return send(value, target)
+
+
 def turned(turn, values):
     got = {k: turn(values[k], k) for k in (1, 3, 2)}
     return [values[0]] + [got[k] for k in (1, 2, 3)]
 
 
 def column(where, core, k3, k2, z):
-    y = where[1] ^ jnp.where(core == 0, k2, k3)
-    x = where[2] ^ jnp.where(core == 0, k3, k2)
+    k_y, k_x = (k2, k3), (k3, k2)
+    if isinstance(core, int):
+        y, x = where[1] ^ k_y[core], where[2] ^ k_x[core]
+    else:
+        y = where[1] ^ jnp.where(core == 0, *k_y)
+        x = where[2] ^ jnp.where(core == 0, *k_x)
     return pl.multiple_of(((z * 4 + y) * 4 + x) * 128, 128)
 
 
-def product(where, turns, pieces, mine, theirs):
-    total = jnp.zeros((128, 128), jnp.float32)
-    for k3, piece in zip(turns, pieces):
-        for k2 in range(4):
-            at = [
-                pl.ds(column(where, where[3], k3, k2, where[0] ^ kz), 128)
-                for kz in range(4)
-            ]
-            rows = jnp.concatenate(
-                [
-                    jnp.concatenate([side[:, part] for part in at], axis=1)
-                    for side in (mine, theirs)
-                ],
-                axis=0,
-            )
-            total += jnp.dot(
-                rows,
-                piece[k2].reshape(512, 128),
-                preferred_element_type=jnp.float32,
-            )
-    return total
-
-
-def sums_most(where, p0, p1, p2, mine, theirs, total):
-    total[...] = product(where, EARLY, (p0, p1, p2), mine, theirs)
-
-
-def sums_rest(where, p3, mine, theirs, most, pre):
-    total = most[...] + product(where, LATE, (p3,), mine, theirs)
-    crossed = jnp.concatenate([total[64:], total[:64]], axis=0)
-    pre[...] = jnp.where(where[3] == 0, total, crossed).astype(pre.dtype)
-
-
-EARLY, LATE = (0, 2, 3), (1,)
+def precondition(where, p0, p1, p2, p3, act_rows, grad_rows, acts_there, grads_there, pre):
+    def product(core, mine, theirs):
+        total = jnp.zeros((128, 128), jnp.float32)
+        for k3, piece in enumerate((p0, p1, p2, p3)):
+            for k2 in range(4):
+                at = [
+                    pl.ds(column(where, core, k3, k2, where[0] ^ kz), 128)
+                    for kz in range(4)
+                ]
+                rows = jnp.concatenate(
+                    [
+                        jnp.concatenate([side[:, part] for part in at], axis=1)
+                        for side in (mine, theirs)
+                    ],
+                    axis=0,
+                )
+                total += jnp.dot(
+                    rows,
+                    piece[k2].reshape(512, 128),
+                    preferred_element_type=jnp.float32,
+                )
+        return total.astype(pre.dtype)
+
+    @pl.when(where[3] == 0)
+    def _():
+        pre[...] = product(0, act_rows, acts_there)
+
+    @pl.when(where[3] == 1)
+    def _():
+        pre[...] = product(1, grads_there, grad_rows)
 
 
 def tiles(g, plane, *made):
@@ -119,7 +126,8 @@
             piece = refs[side * 4 + k3]
             for k2 in range(4):
                 for j in range(2):
-                    at = column(where, held_by, k3, k2, j + 2 * held_by)
+                    z = where[0] ^ (2 * j + lax.rem(where[0] + held_by, 2))
+                    at = column(where, held_by, k3, k2, z)
                     b = (k2 * 2 + j) * 128
                     out[:, pl.ds(at, 128)] = piece[:, b : b + 128].astype(jnp.float32)
 
@@ -156,32 +164,30 @@
         [jnp.where(first, kept, got), jnp.where(first, got, kept)], axis=0
     )
     line = jnp.stack(turned(along_line, [block] * 4))
-    rows = turned(first_turn, [line] * 4)
-    rows[1], act_inverse, grad_inverse = lax.optimization_barrier(
-        (rows[1], act_inverse, grad_inverse)
-    )
-    theirs = swap_cores(jnp.where(first, grad_inverse, act_inverse))
-    mine = jnp.where(first, act_inverse, grad_inverse)
-    plane = jnp.stack(rows)
+    plane = jnp.stack(turned(first_turn, [line] * 4))
     pieces = turned(second_turn, [plane] * 4)
-    most = call(
-        sums_most, "sums_most", shape((128, 128), f32), [SMEM] + [VMEM] * 5
-    )(where, *(pieces[k] for k in EARLY), mine, theirs)
     pre = call(
-        sums_rest, "sums_rest", shape((128, 128), bf16), [SMEM] + [VMEM] * 4
-    )(where, *(pieces[k] for k in LATE), mine, theirs, most)
-
-    sent = jnp.broadcast_to(pre, (8, 128, 128))
-    all_planes = lax.all_to_all(sent, ("rep", "zl"), 0, 0, tiled=True)
-    all_planes = all_planes.reshape(2, 4, 128, 128)
-    here = lax.dynamic_slice_in_dim(all_planes, where[0], 1, axis=1)
-    cross = swap_cores(
-        jnp.where(first, all_planes[:, 2:], jnp.concatenate([here, here], axis=1))
-    )
-    pair = jnp.where(first, all_planes[:, :2], cross)
-    pair = jnp.concatenate([pair[0], pair[1]], axis=2)
-    grad = jnp.where(first, cross[:, 0], here[:, 0])
-    grad = jnp.concatenate([grad[0], grad[1]], axis=1)
+        precondition, "precondition", shape((128, 128), bf16), [SMEM] + [VMEM] * 8
+    )(
+        where,
+        *pieces,
+        act_inverse,
+        grad_inverse,
+        swap_cores(act_inverse),
+        swap_cores(grad_inverse),
+    )
+
+    near = swap_cores(pre)
+    act = jnp.where(first, pre, near)
+    grad = jnp.where(first, near, pre)
+    riding = to_parity(jnp.stack([act, grad]), 0, 1)
+    there = (riding[0], to_parity(act, 1, 1))
+    here = [to_parity(act, j, 0) for j in (1, 0)][::-1]
+    pair = jnp.stack([jnp.concatenate(p, axis=1) for p in zip(here, there)])
+    far = jnp.where(
+        lax.rem(where[0] + c, 2) == 0, riding[1], swap_cores(riding[1])
+    )
+    grad = jnp.concatenate([grad, far], axis=1)
 
     grads = jnp.stack([grad, second_turn(grad, 1)])
     plane = jnp.stack(turned(first_turn, [pair] * 4))

time: 100 us -> 93.8 us (0.938)
  waiting for transfers between devices: 41.9 us -> 37.9 us
  other arithmetic: 4.55 us -> 1.99 us
    all_to_all x1 -> x0, waiting for transfers between devices: 9.44 us -> none  [on_device(): all_planes = lax.all_to_all(sent, ('rep', 'zl'), 0, 0, tiled=True)]
    ppermute x24 -> x30, starting transfers between devices: 41.2 us -> 47 us  [send(): return lax.ppermute(value, AXES, pairs)]
    all_to_all x1 -> x0, starting transfers between devices: 5.49 us -> none  [on_device(): all_planes = lax.all_to_all(sent, ('rep', 'zl'), 0, 0, tiled=True)]
    ppermute x24 -> x30, waiting for transfers between devices: 32.4 us -> 37.9 us  [send(): return lax.ppermute(value, AXES, pairs)]
    select_n x4 -> x2, other arithmetic: 2.69 us -> 0.02 us  [the longest x1 0.01 us: on_device(): act = jnp.where(first, pre, near)]
    unnamed x0 -> x4, local copies, waits for them, and re-layouts: none -> 1.22 us
    pallas_call x2 -> x1, Pallas kernels: 2.67 us -> 2.36 us  [on_device(): call(precondition, 'precondition', shape((128, 128), bf16), [SMEM] + [VME...]
  transfers between devices with their start and end apart: 25 -> 30, of which waited for: 15 -> 19; matrix products, arithmetic and copies ran while one was open for 0% -> 1% of each run, Pallas kernels for 2% -> 0%
where the time goes in v6:
time: 93.8 us; the launch traced here: 93.5 us
  starting transfers between devices  47 us (50%)
  waiting for transfers between devices  37.9 us (40%)
  Pallas kernels  5.34 us (6%)
  other arithmetic  1.99 us (2%)
  local copies, waits for them, and re-layouts  1.23 us (1%)
    ppermute x30, starting transfers between devices, send(): return lax.ppermute(value, AXES, pairs)  47 us
    ppermute x30, waiting for transfers between devices, send(): return lax.ppermute(value, AXES, pairs)  37.9 us
    pallas_call x1, Pallas kernels, on_device(): call(precondition, 'precondition', shape((128, 128), bf16), [SMEM] + [VME...  2.36 us
    pallas_call x1, Pallas kernels, on_device(): call(assemble, 'assemble', shape((64, 8192), f32), [SMEM] + [VMEM] * 8)  2.16 us
  transfers between devices with their start and end apart: 30, of which 19 were waited for; matrix products, arithmetic and copies ran while one was open for 1% of the time, Pallas kernels for 0%

profile of v6, /device:TPU:1, one launch (start us, length us, event | category | flops | bytes accessed | tf_op | source)
XLA Modules:
  0.0 93.5 jit_solution(1877625321077285727)
XLA Ops:
  0.0 0.8 select_bitcast_fusion
  0.8 3.2 %collective-permute-start = (bf16[64,128]{1,0:T(8,128)(2,1)S(1)}, bf16[64,128]{1,0:T(8,128)(2,1)S(1)}, u32[]{:S(2)}, u32[]{:S(2)}) collective-permute-start(bf16[64,128]{1,0:T(8,128)(2,1)S(1)} %select_bitcast_fusion), channel_id=1, source_target_pairs={{0,1},{1,0},{2,3},{3,2},{4,5},{5,4},{6,7},{7,6},{8,9},{9,8},{10,11... | collective-permute-start | bytes 49160 | tf_op jit(solution)/shard_map/ppermute | solution.py:30
  4.9 0.7 bitcast_select_fusion.1
  5.6 1.3 %collective-permute-start.2 = (bf16[128,128]{1,0:T(8,128)(2,1)S(1)}, bf16[128,128]{1,0:T(8,128)(2,1)S(1)}, u32[]{:S(2)}, u32[]{:S(2)}) collective-permute-start(bf16[128,128]{1,0:T(8,128)(2,1)S(1)} %get-tuple-element.34), channel_id=1, source_target_pairs={{0,64},{1,65},{2,66},{3,67},{4,68},{5,69},{6,70},{7,71},{8,72},{9,... | collective-permute-start | bytes 98312 | tf_op jit(solution)/shard_map/ppermute | solution.py:30
  7.0 1.6 %collective-permute-start.1 = (bf16[128,128]{1,0:T(8,128)(2,1)S(1)}, bf16[128,128]{1,0:T(8,128)(2,1)S(1)}, u32[]{:S(2)}, u32[]{:S(2)}) collective-permute-start(bf16[128,128]{1,0:T(8,128)(2,1)S(1)} %get-tuple-element.34), channel_id=1, source_target_pairs={{0,32},{1,33},{2,34},{3,35},{4,36},{5,37},{6,38},{7,39},{8,40},{9,... | collective-permute-start | bytes 98312 | tf_op jit(solution)/shard_map/ppermute | solution.py:30
  9.9 3.3 %collective-permute-done.3 = bf16[128,128]{1,0:T(8,128)(2,1)S(1)} collective-permute-done((bf16[128,128]{1,0:T(8,128)(2,1)S(1)}, bf16[128,128]{1,0:T(8,128)(2,1)S(1)}, u32[]{:S(2)}, u32[]{:S(2)}) %collective-permute-start.3) | collective-permute-done | bytes 32800 | tf_op jit(solution)/shard_map/ppermute | solution.py:30
  13.2 2.8 %collective-permute-start.5 = (bf16[4,128,128]{2,1,0:T(8,128)(2,1)S(1)}, bf16[4,128,128]{2,1,0:T(8,128)(2,1)S(1)}, u32[]{:S(2)}, u32[]{:S(2)}) collective-permute-start(bf16[4,128,128]{2,1,0:T(8,128)(2,1)S(1)} %get-tuple-element.24), channel_id=1, source_target_pairs={{0,16},{1,5},{2,18},{3,7},{4,20},{5,1},{6,22},{7,3},{8,24},{9,13},... | collective-permute-start | bytes 393224 | tf_op jit(solution)/shard_map/ppermute | solution.py:30
  16.9 1.7 %collective-permute-done.5 = bf16[4,128,128]{2,1,0:T(8,128)(2,1)S(1)} collective-permute-done((bf16[4,128,128]{2,1,0:T(8,128)(2,1)S(1)}, bf16[4,128,128]{2,1,0:T(8,128)(2,1)S(1)}, u32[]{:S(2)}, u32[]{:S(2)}) %collective-permute-start.5) | collective-permute-done | bytes 131104 | tf_op jit(solution)/shard_map/ppermute | solution.py:30
  18.6 1.8 %collective-permute-done.4 = bf16[4,128,128]{2,1,0:T(8,128)(2,1)S(1)} collective-permute-done((bf16[4,128,128]{2,1,0:T(8,128)(2,1)S(1)}, bf16[4,128,128]{2,1,0:T(8,128)(2,1)S(1)}, u32[]{:S(2)}, u32[]{:S(2)}) %collective-permute-start.4) | collective-permute-done | bytes 131104 | tf_op jit(solution)/shard_map/ppermute | solution.py:30
  20.4 1.0 %collective-permute-done.6 = bf16[4,128,128]{2,1,0:T(8,128)(2,1)S(1)} collective-permute-done((bf16[4,128,128]{2,1,0:T(8,128)(2,1)S(1)}, bf16[4,128,128]{2,1,0:T(8,128)(2,1)S(1)}, u32[]{:S(2)}, u32[]{:S(2)}) %collective-permute-start.6) | collective-permute-done | bytes 131104 | tf_op jit(solution)/shard_map/ppermute | solution.py:30
  21.5 3.1 %collective-permute-start.9 = (bf16[4,4,128,128]{3,2,1,0:T(8,128)(2,1)S(1)}, bf16[4,4,128,128]{3,2,1,0:T(8,128)(2,1)S(1)}, u32[]{:S(2)}, u32[]{:S(2)}) collective-permute-start(bf16[4,4,128,128]{3,2,1,0:T(8,128)(2,1)S(1)} %pad_maximum_fusion.p0), channel_id=1, source_target_pairs={{0,6},{1,25},{2,4},{3,27},{4,2},{5,29},{6,0},{7,31},{8,14},{9,17},... | collective-permute-start | bytes 1572872 | tf_op jit(solution)/shard_map/ppermute | solution.py:30
  25.3 11.8 %collective-permute-done.9.p3 = bf16[4,4,128,128]{3,2,1,0:T(8,128)(2,1)S(1)} collective-permute-done((bf16[4,4,128,128]{3,2,1,0:T(8,128)(2,1)S(1)}, bf16[4,4,128,128]{3,2,1,0:T(8,128)(2,1)S(1)}, u32[]{:S(2)}, u32[]{:S(2)}) %collective-permute-start.9) | collective-permute-done | bytes 524320 | tf_op jit(solution)/shard_map/ppermute | solution.py:30
  37.9 1.2 %copy-done.1 = bf16[64,8192]{1,0:T(8,128)(2,1)S(1)} copy-done((bf16[64,8192]{1,0:T(8,128)(2,1)S(1)}, bf16[64,8192]{1,0:T(8,128)(2,1)}, u32[]{:S(2)}) %copy-start.1) | copy-done | bytes 1048600
  39.1 2.4 %precondition.1 = bf16[128,128]{1,0:T(8,128)(2,1)S(1)} custom-call(s32[4]{0:T(128)S(1)} %pad_add_fusion.where, bf16[4,4,128,128]{3,2,1,0:T(8,128)(2,1)S(1)} %pad_maximum_fusion.p0, bf16[4,4,128,128]{3,2,1,0:T(8,128)(2,1)} %collective-permute-done.7.p1, bf16[4,4,128,128]{3,2,1,0:T(8,128)(2,1)} %collective-permute-done.8.p2, ...), custom_call_target="tpu_custom_call" | custom-call | tf_op jit(solution)/shard_map/precondition/pallas_call | solution.py:169
  41.5 5.0 %collective-permute-start.12 = (bf16[128,128]{1,0:T(8,128)(2,1)S(1)}, bf16[128,128]{1,0:T(8,128)(2,1)S(1)}, u32[]{:S(2)}, u32[]{:S(2)}) collective-permute-start(bf16[128,128]{1,0:T(8,128)(2,1)S(1)} %precondition.1), channel_id=1, source_target_pairs={{0,1},{1,0},{2,3},{3,2},{4,5},{5,4},{6,7},{7,6},{8,9},{9,8},{10,11... | collective-permute-start | bytes 98312 | tf_op jit(solution)/shard_map/ppermute | solution.py:30
  46.5 0.9 collective-permute-done.12
  47.3 3.1 %collective-permute-start.19 = (bf16[128,128]{1,0:T(8,128)(2,1)S(1)}, bf16[128,128]{1,0:T(8,128)(2,1)S(1)}, u32[]{:S(2)}, u32[]{:S(2)}) collective-permute-start(bf16[128,128]{1,0:T(8,128)(2,1)S(1)} %get-tuple-element.29), channel_id=1, source_target_pairs={{0,192},{1,224},{2,194},{3,226},{4,196},{5,228},{6,198},{7,230},{8... | collective-permute-start | bytes 98312 | tf_op jit(solution)/shard_map/ppermute | solution.py:30
  51.0 3.3 %collective-permute-start.17 = (bf16[128,128]{1,0:T(8,128)(2,1)S(1)}, bf16[128,128]{1,0:T(8,128)(2,1)S(1)}, u32[]{:S(2)}, u32[]{:S(2)}) collective-permute-start(bf16[128,128]{1,0:T(8,128)(2,1)S(1)} %get-tuple-element.29), channel_id=1, source_target_pairs={{0,0},{1,32},{2,2},{3,34},{4,4},{5,36},{6,6},{7,38},{8,8},{9,40},{... | collective-permute-start | bytes 98312 | tf_op jit(solution)/shard_map/ppermute | solution.py:30
  55.0 6.9 %collective-permute-done.13 = bf16[2,128,128]{2,1,0:T(8,128)(2,1)S(1)} collective-permute-done((bf16[2,128,128]{2,1,0:T(8,128)(2,1)S(1)}, bf16[2,128,128]{2,1,0:T(8,128)(2,1)S(1)}, u32[]{:S(2)}, u32[]{:S(2)}) %collective-permute-start.13) | collective-permute-done | bytes 65568 | tf_op jit(solution)/shard_map/ppermute | solution.py:30
  62.0 1.1 %collective-permute-done.14 = bf16[128,128]{1,0:T(8,128)(2,1)S(1)} collective-permute-done((bf16[128,128]{1,0:T(8,128)(2,1)S(1)}, bf16[128,128]{1,0:T(8,128)(2,1)S(1)}, u32[]{:S(2)}, u32[]{:S(2)}) %collective-permute-start.14) | collective-permute-done | bytes 32800 | tf_op jit(solution)/shard_map/ppermute | solution.py:30
  63.3 3.2 %collective-permute-start.21 = (bf16[2,128,256]{2,1,0:T(8,128)(2,1)S(1)}, bf16[2,128,256]{2,1,0:T(8,128)(2,1)S(1)}, u32[]{:S(2)}, u32[]{:S(2)}) collective-permute-start(bf16[2,128,256]{2,1,0:T(8,128)(2,1)S(1)} %get-tuple-element.22), channel_id=1, source_target_pairs={{0,16},{1,5},{2,18},{3,7},{4,20},{5,1},{6,22},{7,3},{8,24},{9,13},... | collective-permute-start | bytes 393224 | tf_op jit(solution)/shard_map/ppermute | solution.py:30
  68.0 0.9 collective-permute-done.21
  68.9 2.0 %collective-permute-done.20 = bf16[2,128,256]{2,1,0:T(8,128)(2,1)S(1)} collective-permute-done((bf16[2,128,256]{2,1,0:T(8,128)(2,1)S(1)}, bf16[2,128,256]{2,1,0:T(8,128)(2,1)S(1)}, u32[]{:S(2)}, u32[]{:S(2)}) %collective-permute-start.20) | collective-permute-done | bytes 131104 | tf_op jit(solution)/shard_map/ppermute | solution.py:30
  70.9 1.3 %collective-permute-done.22 = bf16[2,128,256]{2,1,0:T(8,128)(2,1)S(1)} collective-permute-done((bf16[2,128,256]{2,1,0:T(8,128)(2,1)S(1)}, bf16[2,128,256]{2,1,0:T(8,128)(2,1)S(1)}, u32[]{:S(2)}, u32[]{:S(2)}) %collective-permute-start.22) | collective-permute-done | bytes 131104 | tf_op jit(solution)/shard_map/ppermute | solution.py:30
  72.2 2.0 %collective-permute-done.16 = bf16[2,128,256]{2,1,0:T(8,128)(2,1)S(1)} collective-permute-done((bf16[2,128,256]{2,1,0:T(8,128)(2,1)S(1)}, bf16[2,128,256]{2,1,0:T(8,128)(2,1)S(1)}, u32[]{:S(2)}, u32[]{:S(2)}) %collective-permute-start.16) | collective-permute-done | bytes 131104 | tf_op jit(solution)/shard_map/ppermute | solution.py:30
  74.2 0.8 tiles.1
  75.6 4.8 %collective-permute-start.26 = (bf16[64,1024]{1,0:T(8,128)(2,1)S(1)}, bf16[64,1024]{1,0:T(8,128)(2,1)S(1)}, u32[]{:S(2)}, u32[]{:S(2)}) collective-permute-start(bf16[64,1024]{1,0:T(8,128)(2,1)S(1)} %get-tuple-element.19), channel_id=1, source_target_pairs={{0,1},{1,0},{2,3},{3,2},{4,5},{5,4},{6,7},{7,6},{8,9},{9,8},{10,11... | collective-permute-start | bytes 393224 | tf_op jit(solution)/shard_map/ppermute | solution.py:30
  80.7 2.4 %collective-permute-start.27 = (bf16[64,1024]{1,0:T(8,128)(2,1)S(1)}, bf16[64,1024]{1,0:T(8,128)(2,1)S(1)}, u32[]{:S(2)}, u32[]{:S(2)}) collective-permute-start(bf16[64,1024]{1,0:T(8,128)(2,1)S(1)} %get-tuple-element.17), channel_id=1, source_target_pairs={{0,1},{1,0},{2,3},{3,2},{4,5},{5,4},{6,7},{7,6},{8,9},{9,8},{10,11... | collective-permute-start | bytes 393224 | tf_op jit(solution)/shard_map/ppermute | solution.py:30
  83.1 4.5 %collective-permute-start.28 = (bf16[64,1024]{1,0:T(8,128)(2,1)S(1)}, bf16[64,1024]{1,0:T(8,128)(2,1)S(1)}, u32[]{:S(2)}, u32[]{:S(2)}) collective-permute-start(bf16[64,1024]{1,0:T(8,128)(2,1)S(1)} %get-tuple-element.15), channel_id=1, source_target_pairs={{0,1},{1,0},{2,3},{3,2},{4,5},{5,4},{6,7},{7,6},{8,9},{9,8},{10,11... | collective-permute-start | bytes 393224 | tf_op jit(solution)/shard_map/ppermute | solution.py:30
  87.7 2.7 %collective-permute-start.29 = (bf16[64,1024]{1,0:T(8,128)(2,1)S(1)}, bf16[64,1024]{1,0:T(8,128)(2,1)S(1)}, u32[]{:S(2)}, u32[]{:S(2)}) collective-permute-start(bf16[64,1024]{1,0:T(8,128)(2,1)S(1)} %get-tuple-element.13), channel_id=1, source_target_pairs={{0,1},{1,0},{2,3},{3,2},{4,5},{5,4},{6,7},{7,6},{8,9},{9,8},{10,11... | collective-permute-start | bytes 393224 | tf_op jit(solution)/shard_map/ppermute | solution.py:30
  90.4 1.0 %collective-permute-done.29.refs_7_ = bf16[64,1024]{1,0:T(8,128)(2,1)S(1)} collective-permute-done((bf16[64,1024]{1,0:T(8,128)(2,1)S(1)}, bf16[64,1024]{1,0:T(8,128)(2,1)S(1)}, u32[]{:S(2)}, u32[]{:S(2)}) %collective-permute-start.29) | collective-permute-done | bytes 131104 | tf_op jit(solution)/shard_map/ppermute | solution.py:30
  91.3 2.2 %assemble.1 = f32[64,8192]{1,0:T(8,128)} custom-call(s32[4]{0:T(128)S(1)} %pad_add_fusion.where, bf16[64,1024]{1,0:T(8,128)(2,1)S(1)} %get-tuple-element.20.refs_0_, bf16[64,1024]{1,0:T(8,128)(2,1)S(1)} %get-tuple-element.18.refs_1_, bf16[64,1024]{1,0:T(8,128)(2,1)S(1)} %get-tuple-element.16.refs_2_, bf16[64,1024]{1,0:T(8,128)(2,1)S(1)} %get-tuple-element.14.refs_3_, ...), custom_call_target="tpu_custom_call" | custom-call | tf_op jit(solution)/shard_map/assemble/pallas_call | solution.py:201
  (56 shorter events, 8.5 us)
Async XLA Ops:
  0.0 37.9 %copy-start = (bf16[64,8192]{1,0:T(8,128)(2,1)S(1)}, bf16[64,8192]{1,0:T(8,128)(2,1)}, u32[]{:S(2)}) copy-start(bf16[64,8192]{1,0:T(8,128)(2,1)} %act_rows.1) | copy-start | bytes 3145732
  0.8 4.1 %collective-permute-start = (bf16[64,128]{1,0:T(8,128)(2,1)S(1)}, bf16[64,128]{1,0:T(8,128)(2,1)S(1)}, u32[]{:S(2)}, u32[]{:S(2)}) collective-permute-start(bf16[64,128]{1,0:T(8,128)(2,1)S(1)} %select_bitcast_fusion), channel_id=1, source_target_pairs={{0,1},{1,0},{2,3},{3,2},{4,5},{5,4},{6,7},{7,6},{8,9},{9,8},{10,11... | collective-permute-start | bytes 49160 | tf_op jit(solution)/shard_map/ppermute | solution.py:30
  4.1 33.8 %collective-permute-start.10 = (bf16[64,8192]{1,0:T(8,128)(2,1)}, bf16[64,8192]{1,0:T(8,128)(2,1)S(1)}, u32[]{:S(2)}, u32[]{:S(2)}) collective-permute-start(bf16[64,8192]{1,0:T(8,128)(2,1)} %act_rows.1), channel_id=1, source_target_pairs={{0,1},{1,0},{2,3},{3,2},{4,5},{5,4},{6,7},{7,6},{8,9},{9,8},{10,11... | collective-permute-start | bytes 3145736 | tf_op jit(solution)/shard_map/ppermute | solution.py:30
  4.2 33.7 %collective-permute-start.11 = (bf16[64,8192]{1,0:T(8,128)(2,1)}, bf16[64,8192]{1,0:T(8,128)(2,1)}, u32[]{:S(2)}, u32[]{:S(2)}) collective-permute-start(bf16[64,8192]{1,0:T(8,128)(2,1)} %grad_rows.1), channel_id=1, source_target_pairs={{0,1},{1,0},{2,3},{3,2},{4,5},{5,4},{6,7},{7,6},{8,9},{9,8},{10,11... | collective-permute-start | bytes 3145736 | tf_op jit(solution)/shard_map/ppermute | solution.py:30
  5.6 3.8 %collective-permute-start.2 = (bf16[128,128]{1,0:T(8,128)(2,1)S(1)}, bf16[128,128]{1,0:T(8,128)(2,1)S(1)}, u32[]{:S(2)}, u32[]{:S(2)}) collective-permute-start(bf16[128,128]{1,0:T(8,128)(2,1)S(1)} %get-tuple-element.34), channel_id=1, source_target_pairs={{0,64},{1,65},{2,66},{3,67},{4,68},{5,69},{6,70},{7,71},{8,72},{9,... | collective-permute-start | bytes 98312 | tf_op jit(solution)/shard_map/ppermute | solution.py:30
  7.0 2.9 %collective-permute-start.1 = (bf16[128,128]{1,0:T(8,128)(2,1)S(1)}, bf16[128,128]{1,0:T(8,128)(2,1)S(1)}, u32[]{:S(2)}, u32[]{:S(2)}) collective-permute-start(bf16[128,128]{1,0:T(8,128)(2,1)S(1)} %get-tuple-element.34), channel_id=1, source_target_pairs={{0,32},{1,33},{2,34},{3,35},{4,36},{5,37},{6,38},{7,39},{8,40},{9,... | collective-permute-start | bytes 98312 | tf_op jit(solution)/shard_map/ppermute | solution.py:30
  8.6 4.6 %collective-permute-start.3 = (bf16[128,128]{1,0:T(8,128)(2,1)S(1)}, bf16[128,128]{1,0:T(8,128)(2,1)S(1)}, u32[]{:S(2)}, u32[]{:S(2)}) collective-permute-start(bf16[128,128]{1,0:T(8,128)(2,1)S(1)} %get-tuple-element.34), channel_id=1, source_target_pairs={{0,96},{1,97},{2,98},{3,99},{4,100},{5,101},{6,102},{7,103},{8,104... | collective-permute-start | bytes 98312 | tf_op jit(solution)/shard_map/ppermute | solution.py:30
  13.2 5.4 %collective-permute-start.5 = (bf16[4,128,128]{2,1,0:T(8,128)(2,1)S(1)}, bf16[4,128,128]{2,1,0:T(8,128)(2,1)S(1)}, u32[]{:S(2)}, u32[]{:S(2)}) collective-permute-start(bf16[4,128,128]{2,1,0:T(8,128)(2,1)S(1)} %get-tuple-element.24), channel_id=1, source_target_pairs={{0,16},{1,5},{2,18},{3,7},{4,20},{5,1},{6,22},{7,3},{8,24},{9,13},... | collective-permute-start | bytes 393224 | tf_op jit(solution)/shard_map/ppermute | solution.py:30
  16.0 4.4 %collective-permute-start.4 = (bf16[4,128,128]{2,1,0:T(8,128)(2,1)S(1)}, bf16[4,128,128]{2,1,0:T(8,128)(2,1)S(1)}, u32[]{:S(2)}, u32[]{:S(2)}) collective-permute-start(bf16[4,128,128]{2,1,0:T(8,128)(2,1)S(1)} %get-tuple-element.24), channel_id=1, source_target_pairs={{0,8},{1,3},{2,10},{3,1},{4,12},{5,7},{6,14},{7,5},{8,0},{9,11},{1... | collective-permute-start | bytes 393224 | tf_op jit(solution)/shard_map/ppermute | solution.py:30
  16.3 5.1 %collective-permute-start.6 = (bf16[4,128,128]{2,1,0:T(8,128)(2,1)S(1)}, bf16[4,128,128]{2,1,0:T(8,128)(2,1)S(1)}, u32[]{:S(2)}, u32[]{:S(2)}) collective-permute-start(bf16[4,128,128]{2,1,0:T(8,128)(2,1)S(1)} %get-tuple-element.24), channel_id=1, source_target_pairs={{0,24},{1,7},{2,26},{3,5},{4,28},{5,3},{6,30},{7,1},{8,16},{9,15},... | collective-permute-start | bytes 393224 | tf_op jit(solution)/shard_map/ppermute | solution.py:30
  21.5 15.7 %collective-permute-start.9 = (bf16[4,4,128,128]{3,2,1,0:T(8,128)(2,1)S(1)}, bf16[4,4,128,128]{3,2,1,0:T(8,128)(2,1)S(1)}, u32[]{:S(2)}, u32[]{:S(2)}) collective-permute-start(bf16[4,4,128,128]{3,2,1,0:T(8,128)(2,1)S(1)} %pad_maximum_fusion.p0), channel_id=1, source_target_pairs={{0,6},{1,25},{2,4},{3,27},{4,2},{5,29},{6,0},{7,31},{8,14},{9,17},... | collective-permute-start | bytes 1572872 | tf_op jit(solution)/shard_map/ppermute | solution.py:30
  24.6 12.6 %collective-permute-start.8 = (bf16[4,4,128,128]{3,2,1,0:T(8,128)(2,1)S(1)}, bf16[4,4,128,128]{3,2,1,0:T(8,128)(2,1)}, u32[]{:S(2)}, u32[]{:S(2)}) collective-permute-start(bf16[4,4,128,128]{3,2,1,0:T(8,128)(2,1)S(1)} %pad_maximum_fusion.p0), channel_id=1, source_target_pairs={{0,4},{1,17},{2,6},{3,19},{4,0},{5,21},{6,2},{7,23},{8,12},{9,25},... | collective-permute-start | bytes 1572872 | tf_op jit(solution)/shard_map/ppermute | solution.py:30
  24.7 13.2 %collective-permute-start.7 = (bf16[4,4,128,128]{3,2,1,0:T(8,128)(2,1)S(1)}, bf16[4,4,128,128]{3,2,1,0:T(8,128)(2,1)}, u32[]{:S(2)}, u32[]{:S(2)}) collective-permute-start(bf16[4,4,128,128]{3,2,1,0:T(8,128)(2,1)S(1)} %pad_maximum_fusion.p0), channel_id=1, source_target_pairs={{0,2},{1,9},{2,0},{3,11},{4,6},{5,13},{6,4},{7,15},{8,10},{9,1},{1... | collective-permute-start | bytes 1572872 | tf_op jit(solution)/shard_map/ppermute | solution.py:30
  37.9 1.2 %copy-start.1 = (bf16[64,8192]{1,0:T(8,128)(2,1)S(1)}, bf16[64,8192]{1,0:T(8,128)(2,1)}, u32[]{:S(2)}) copy-start(bf16[64,8192]{1,0:T(8,128)(2,1)} %grad_rows.1) | copy-start | bytes 3145732
  41.5 5.8 %collective-permute-start.12 = (bf16[128,128]{1,0:T(8,128)(2,1)S(1)}, bf16[128,128]{1,0:T(8,128)(2,1)S(1)}, u32[]{:S(2)}, u32[]{:S(2)}) collective-permute-start(bf16[128,128]{1,0:T(8,128)(2,1)S(1)} %precondition.1), channel_id=1, source_target_pairs={{0,1},{1,0},{2,3},{3,2},{4,5},{5,4},{6,7},{7,6},{8,9},{9,8},{10,11... | collective-permute-start | bytes 98312 | tf_op jit(solution)/shard_map/ppermute | solution.py:30
  47.3 7.4 %collective-permute-start.19 = (bf16[128,128]{1,0:T(8,128)(2,1)S(1)}, bf16[128,128]{1,0:T(8,128)(2,1)S(1)}, u32[]{:S(2)}, u32[]{:S(2)}) collective-permute-start(bf16[128,128]{1,0:T(8,128)(2,1)S(1)} %get-tuple-element.29), channel_id=1, source_target_pairs={{0,192},{1,224},{2,194},{3,226},{4,196},{5,228},{6,198},{7,230},{8... | collective-permute-start | bytes 98312 | tf_op jit(solution)/shard_map/ppermute | solution.py:30
  50.4 4.6 %collective-permute-start.18 = (bf16[128,128]{1,0:T(8,128)(2,1)S(1)}, bf16[128,128]{1,0:T(8,128)(2,1)S(1)}, u32[]{:S(2)}, u32[]{:S(2)}) collective-permute-start(bf16[128,128]{1,0:T(8,128)(2,1)S(1)} %get-tuple-element.29), channel_id=1, source_target_pairs={{0,64},{1,96},{2,66},{3,98},{4,68},{5,100},{6,70},{7,102},{8,72},{... | collective-permute-start | bytes 98312 | tf_op jit(solution)/shard_map/ppermute | solution.py:30
  51.0 11.0 %collective-permute-start.17 = (bf16[128,128]{1,0:T(8,128)(2,1)S(1)}, bf16[128,128]{1,0:T(8,128)(2,1)S(1)}, u32[]{:S(2)}, u32[]{:S(2)}) collective-permute-start(bf16[128,128]{1,0:T(8,128)(2,1)S(1)} %get-tuple-element.29), channel_id=1, source_target_pairs={{0,0},{1,32},{2,2},{3,34},{4,4},{5,36},{6,6},{7,38},{8,8},{9,40},{... | collective-permute-start | bytes 98312 | tf_op jit(solution)/shard_map/ppermute | solution.py:30
  54.3 7.6 %collective-permute-start.13 = (bf16[2,128,128]{2,1,0:T(8,128)(2,1)S(1)}, bf16[2,128,128]{2,1,0:T(8,128)(2,1)S(1)}, u32[]{:S(2)}, u32[]{:S(2)}) collective-permute-start(bf16[2,128,128]{2,1,0:T(8,128)(2,1)S(1)} %pad_maximum_fusion.6), channel_id=1, source_target_pairs={{0,128},{1,160},{2,130},{3,162},{4,132},{5,164},{6,134},{7,166},{8... | collective-permute-start | bytes 196616 | tf_op jit(solution)/shard_map/ppermute | solution.py:30
  61.9 1.2 %collective-permute-start.14 = (bf16[128,128]{1,0:T(8,128)(2,1)S(1)}, bf16[128,128]{1,0:T(8,128)(2,1)S(1)}, u32[]{:S(2)}, u32[]{:S(2)}) collective-permute-start(bf16[128,128]{1,0:T(8,128)(2,1)S(1)} %get-tuple-element.26), channel_id=1, source_target_pairs={{0,1},{1,0},{2,3},{3,2},{4,5},{5,4},{6,7},{7,6},{8,9},{9,8},{10,11... | collective-permute-start | bytes 98312 | tf_op jit(solution)/shard_map/ppermute | solution.py:30
  63.2 4.1 %collective-permute-start.15 = (bf16[128,256]{1,0:T(8,128)(2,1)S(1)}, bf16[128,256]{1,0:T(8,128)(2,1)S(1)}, u32[]{:S(2)}, u32[]{:S(2)}) collective-permute-start(bf16[128,256]{1,0:T(8,128)(2,1)S(1)} %get-tuple-element.28), channel_id=1, source_target_pairs={{0,2},{1,9},{2,0},{3,11},{4,6},{5,13},{6,4},{7,15},{8,10},{9,1},{1... | collective-permute-start | bytes 196616 | tf_op jit(solution)/shard_map/ppermute | solution.py:30
  63.3 5.6 %collective-permute-start.21 = (bf16[2,128,256]{2,1,0:T(8,128)(2,1)S(1)}, bf16[2,128,256]{2,1,0:T(8,128)(2,1)S(1)}, u32[]{:S(2)}, u32[]{:S(2)}) collective-permute-start(bf16[2,128,256]{2,1,0:T(8,128)(2,1)S(1)} %get-tuple-element.22), channel_id=1, source_target_pairs={{0,16},{1,5},{2,18},{3,7},{4,20},{5,1},{6,22},{7,3},{8,24},{9,13},... | collective-permute-start | bytes 393224 | tf_op jit(solution)/shard_map/ppermute | solution.py:30
  66.5 4.4 %collective-permute-start.20 = (bf16[2,128,256]{2,1,0:T(8,128)(2,1)S(1)}, bf16[2,128,256]{2,1,0:T(8,128)(2,1)S(1)}, u32[]{:S(2)}, u32[]{:S(2)}) collective-permute-start(bf16[2,128,256]{2,1,0:T(8,128)(2,1)S(1)} %get-tuple-element.22), channel_id=1, source_target_pairs={{0,8},{1,3},{2,10},{3,1},{4,12},{5,7},{6,14},{7,5},{8,0},{9,11},{1... | collective-permute-start | bytes 393224 | tf_op jit(solution)/shard_map/ppermute | solution.py:30
  66.8 5.3 %collective-permute-start.22 = (bf16[2,128,256]{2,1,0:T(8,128)(2,1)S(1)}, bf16[2,128,256]{2,1,0:T(8,128)(2,1)S(1)}, u32[]{:S(2)}, u32[]{:S(2)}) collective-permute-start(bf16[2,128,256]{2,1,0:T(8,128)(2,1)S(1)} %get-tuple-element.22), channel_id=1, source_target_pairs={{0,24},{1,7},{2,26},{3,5},{4,28},{5,3},{6,30},{7,1},{8,16},{9,15},... | collective-permute-start | bytes 393224 | tf_op jit(solution)/shard_map/ppermute | solution.py:30
  67.3 6.9 %collective-permute-start.16 = (bf16[2,128,256]{2,1,0:T(8,128)(2,1)S(1)}, bf16[2,128,256]{2,1,0:T(8,128)(2,1)S(1)}, u32[]{:S(2)}, u32[]{:S(2)}) collective-permute-start(bf16[2,128,256]{2,1,0:T(8,128)(2,1)S(1)} %pad_maximum_fusion.4), channel_id=1, source_target_pairs={{0,6},{1,25},{2,4},{3,27},{4,2},{5,29},{6,0},{7,31},{8,14},{9,17},... | collective-permute-start | bytes 393224 | tf_op jit(solution)/shard_map/ppermute | solution.py:30
  75.0 5.6 %collective-permute-start.23 = (bf16[128,1024]{1,0:T(8,128)(2,1)S(1)}, bf16[128,1024]{1,0:T(8,128)(2,1)S(1)}, u32[]{:S(2)}, u32[]{:S(2)}) collective-permute-start(bf16[128,1024]{1,0:T(8,128)(2,1)S(1)} %get-tuple-element.10), channel_id=1, source_target_pairs={{0,2},{1,9},{2,0},{3,11},{4,6},{5,13},{6,4},{7,15},{8,10},{9,1},{1... | collective-permute-start | bytes 786440 | tf_op jit(solution)/shard_map/ppermute | solution.py:30
  75.1 8.0 %collective-permute-start.24 = (bf16[128,1024]{1,0:T(8,128)(2,1)S(1)}, bf16[128,1024]{1,0:T(8,128)(2,1)S(1)}, u32[]{:S(2)}, u32[]{:S(2)}) collective-permute-start(bf16[128,1024]{1,0:T(8,128)(2,1)S(1)} %get-tuple-element.11), channel_id=1, source_target_pairs={{0,4},{1,17},{2,6},{3,19},{4,0},{5,21},{6,2},{7,23},{8,12},{9,25},... | collective-permute-start | bytes 786440 | tf_op jit(solution)/shard_map/ppermute | solution.py:30
  75.6 14.7 %collective-permute-start.26 = (bf16[64,1024]{1,0:T(8,128)(2,1)S(1)}, bf16[64,1024]{1,0:T(8,128)(2,1)S(1)}, u32[]{:S(2)}, u32[]{:S(2)}) collective-permute-start(bf16[64,1024]{1,0:T(8,128)(2,1)S(1)} %get-tuple-element.19), channel_id=1, source_target_pairs={{0,1},{1,0},{2,3},{3,2},{4,5},{5,4},{6,7},{7,6},{8,9},{9,8},{10,11... | collective-permute-start | bytes 393224 | tf_op jit(solution)/shard_map/ppermute | solution.py:30
  80.4 7.3 %collective-permute-start.25 = (bf16[128,1024]{1,0:T(8,128)(2,1)S(1)}, bf16[128,1024]{1,0:T(8,128)(2,1)S(1)}, u32[]{:S(2)}, u32[]{:S(2)}) collective-permute-start(bf16[128,1024]{1,0:T(8,128)(2,1)S(1)} %get-tuple-element.12), channel_id=1, source_target_pairs={{0,6},{1,25},{2,4},{3,27},{4,2},{5,29},{6,0},{7,31},{8,14},{9,17},... | collective-permute-start | bytes 786440 | tf_op jit(solution)/shard_map/ppermute | solution.py:30
  80.7 9.7 %collective-permute-start.27 = (bf16[64,1024]{1,0:T(8,128)(2,1)S(1)}, bf16[64,1024]{1,0:T(8,128)(2,1)S(1)}, u32[]{:S(2)}, u32[]{:S(2)}) collective-permute-start(bf16[64,1024]{1,0:T(8,128)(2,1)S(1)} %get-tuple-element.17), channel_id=1, source_target_pairs={{0,1},{1,0},{2,3},{3,2},{4,5},{5,4},{6,7},{7,6},{8,9},{9,8},{10,11... | collective-permute-start | bytes 393224 | tf_op jit(solution)/shard_map/ppermute | solution.py:30
  83.1 7.2 %collective-permute-start.28 = (bf16[64,1024]{1,0:T(8,128)(2,1)S(1)}, bf16[64,1024]{1,0:T(8,128)(2,1)S(1)}, u32[]{:S(2)}, u32[]{:S(2)}) collective-permute-start(bf16[64,1024]{1,0:T(8,128)(2,1)S(1)} %get-tuple-element.15), channel_id=1, source_target_pairs={{0,1},{1,0},{2,3},{3,2},{4,5},{5,4},{6,7},{7,6},{8,9},{9,8},{10,11... | collective-permute-start | bytes 393224 | tf_op jit(solution)/shard_map/ppermute | solution.py:30
  87.7 3.7 %collective-permute-start.29 = (bf16[64,1024]{1,0:T(8,128)(2,1)S(1)}, bf16[64,1024]{1,0:T(8,128)(2,1)S(1)}, u32[]{:S(2)}, u32[]{:S(2)}) collective-permute-start(bf16[64,1024]{1,0:T(8,128)(2,1)S(1)} %get-tuple-element.13), channel_id=1, source_target_pairs={{0,1},{1,0},{2,3},{3,2},{4,5},{5,4},{6,7},{7,6},{8,9},{9,8},{10,11... | collective-permute-start | bytes 393224 | tf_op jit(solution)/shard_map/ppermute | solution.py:30

commit v7 on v5

--- a/solution.py
+++ b/solution.py
@@ -34,6 +34,10 @@
     return send(value, lambda r, zl, y, x, c: (r, zl, y, x, 1 - c))
 
 
+def swap_reps(value):
+    return send(value, lambda r, zl, y, x, c: (1 - r, zl, y, x, c))
+
+
 def along_line(value, k):
     return send(value, lambda r, zl, y, x, c: (r, zl ^ k, y, x, c))
 
@@ -52,6 +56,13 @@
     )
 
 
+def to_parity(value, j, other_rep):
+    def target(r, zl, y, x, c):
+        return r ^ other_rep, zl ^ (2 * j + c), y, x, zl % 2
+
+    return send(value, target)
+
+
 def turned(turn, values):
     got = {k: turn(values[k], k) for k in (1, 3, 2)}
     return [values[0]] + [got[k] for k in (1, 2, 3)]
@@ -63,9 +74,9 @@
     return pl.multiple_of(((z * 4 + y) * 4 + x) * 128, 128)
 
 
-def product(where, turns, pieces, mine, theirs):
+def precondition(where, p0, p1, p2, p3, mine, theirs, pre):
     total = jnp.zeros((128, 128), jnp.float32)
-    for k3, piece in zip(turns, pieces):
+    for k3, piece in enumerate((p0, p1, p2, p3)):
         for k2 in range(4):
             at = [
                 pl.ds(column(where, where[3], k3, k2, where[0] ^ kz), 128)
@@ -83,20 +94,8 @@
                 piece[k2].reshape(512, 128),
                 preferred_element_type=jnp.float32,
             )
-    return total
-
-
-def sums_most(where, p0, p1, p2, mine, theirs, total):
-    total[...] = product(where, EARLY, (p0, p1, p2), mine, theirs)
-
-
-def sums_rest(where, p3, mine, theirs, most, pre):
-    total = most[...] + product(where, LATE, (p3,), mine, theirs)
     crossed = jnp.concatenate([total[64:], total[:64]], axis=0)
     pre[...] = jnp.where(where[3] == 0, total, crossed).astype(pre.dtype)
-
-
-EARLY, LATE = (0, 2, 3), (1,)
 
 
 def tiles(g, plane, *made):
@@ -111,22 +110,35 @@
         e[...] = (part * (1.0 / TOKENS)).astype(e.dtype)
 
 
+FIRST = 1
+
+
 def assemble(where, *refs):
-    core, out = where[3], refs[-1]
+    pieces, (out, wide, sems) = refs[:8], refs[8:]
+    core = where[3]
+    places = []
     for side in range(2):
         held_by = core if side == 0 else 1 - core
         for k3 in range(4):
-            piece = refs[side * 4 + k3]
             for k2 in range(4):
                 for j in range(2):
-                    at = column(where, held_by, k3, k2, j + 2 * held_by)
-                    b = (k2 * 2 + j) * 128
-                    out[:, pl.ds(at, 128)] = piece[:, b : b + 128].astype(jnp.float32)
+                    z = where[0] ^ (2 * j + lax.rem(where[0] + held_by, 2))
+                    at = column(where, held_by, k3, k2, z)
+                    places.append((pieces[side * 4 + k3], (k2 * 2 + j) * 128, at))
+    copies = []
+    for i in range(4):
+        rows = slice(i * 16, i * 16 + 16)
+        for piece, b, at in places:
+            wide[rows, pl.ds(at, 128)] = piece[rows, b : b + 128].astype(jnp.float32)
+        copies.append(pltpu.make_async_copy(wide.at[rows], out.at[rows], sems.at[i]))
+        copies[-1].start()
+    for copy in copies:
+        copy.wait()
 
 
 VMEM = pl.BlockSpec(memory_space=pltpu.VMEM)
 SMEM = pl.BlockSpec(memory_space=pltpu.SMEM)
-PARAMS = pltpu.CompilerParams(vmem_limit_bytes=40 * 1024 * 1024)
+PARAMS = pltpu.CompilerParams(vmem_limit_bytes=12 * 1024 * 1024)
 
 
 def call(body, name, shapes, ins):
@@ -150,38 +162,29 @@
     first = c == 0
 
     acts_t, grads_t = acts.T, grads_out.T
-    got = swap_cores(jnp.where(first, grads_t, acts_t))
-    kept = jnp.where(first, acts_t, grads_t)
+    kept, given = lax.optimization_barrier(
+        (jnp.where(first, acts_t, grads_t), jnp.where(first, grads_t, acts_t))
+    )
+    got = swap_cores(given)
     block = jnp.concatenate(
         [jnp.where(first, kept, got), jnp.where(first, got, kept)], axis=0
     )
+    mine = jnp.where(first, act_inverse, grad_inverse)
+    theirs = jnp.where(first, swap_cores(act_inverse), swap_cores(grad_inverse))
     line = jnp.stack(turned(along_line, [block] * 4))
-    rows = turned(first_turn, [line] * 4)
-    rows[1], act_inverse, grad_inverse = lax.optimization_barrier(
-        (rows[1], act_inverse, grad_inverse)
-    )
-    theirs = swap_cores(jnp.where(first, grad_inverse, act_inverse))
-    mine = jnp.where(first, act_inverse, grad_inverse)
-    plane = jnp.stack(rows)
+    plane = jnp.stack(turned(first_turn, [line] * 4))
     pieces = turned(second_turn, [plane] * 4)
-    most = call(
-        sums_most, "sums_most", shape((128, 128), f32), [SMEM] + [VMEM] * 5
-    )(where, *(pieces[k] for k in EARLY), mine, theirs)
     pre = call(
-        sums_rest, "sums_rest", shape((128, 128), bf16), [SMEM] + [VMEM] * 4
-    )(where, *(pieces[k] for k in LATE), mine, theirs, most)
-
-    sent = jnp.broadcast_to(pre, (8, 128, 128))
-    all_planes = lax.all_to_all(sent, ("rep", "zl"), 0, 0, tiled=True)
-    all_planes = all_planes.reshape(2, 4, 128, 128)
-    here = lax.dynamic_slice_in_dim(all_planes, where[0], 1, axis=1)
-    cross = swap_cores(
-        jnp.where(first, all_planes[:, 2:], jnp.concatenate([here, here], axis=1))
-    )
-    pair = jnp.where(first, all_planes[:, :2], cross)
-    pair = jnp.concatenate([pair[0], pair[1]], axis=2)
-    grad = jnp.where(first, cross[:, 0], here[:, 0])
-    grad = jnp.concatenate([grad[0], grad[1]], axis=1)
+        precondition, "precondition", shape((128, 128), bf16), [SMEM] + [VMEM] * 6
+    )(where, *pieces, mine, theirs)
+
+    near = swap_cores(pre)
+    act = jnp.where(first, pre, near)
+    grad = jnp.where(first, near, pre)
+    here = [to_parity(act, j, 0) for j in (0, 1)]
+    there = [to_parity(act, j, 1) for j in (0, 1)]
+    pair = jnp.stack([jnp.concatenate(p, axis=1) for p in zip(here, there)])
+    grad = jnp.concatenate([grad, swap_reps(grad)], axis=1)
 
     grads = jnp.stack([grad, second_turn(grad, 1)])
     plane = jnp.stack(turned(first_turn, [pair] * 4))
@@ -191,10 +194,21 @@
     )
     whole = turned(second_turn, made)
     own = [jnp.where(first, e[:64], e[64:]) for e in whole]
-    sibling = [swap_cores(jnp.where(first, e[64:], e[:64])) for e in whole]
-    return call(
-        assemble, "assemble", shape((64, 8192), f32), [SMEM] + [VMEM] * 8
-    )(where, *own, *sibling)
+    give = [jnp.where(first, e[64:], e[:64]) for e in whole]
+    one = swap_cores(jnp.stack([give[0], give[FIRST]]))
+    sibling = {0: one[0], FIRST: one[1]}
+    for k in (1, 2, 3):
+        if k != FIRST:
+            sibling[k] = swap_cores(give[k])
+    return pl.pallas_call(
+        assemble,
+        out_shape=shape((64, 8192), f32),
+        in_specs=[SMEM] + [VMEM] * 8,
+        out_specs=pl.BlockSpec(memory_space=pltpu.HBM),
+        scratch_shapes=[pltpu.VMEM((64, 8192), f32), pltpu.SemaphoreType.DMA((4,))],
+        compiler_params=PARAMS,
+        name="assemble",
+    )(where, *own, *(sibling[k] for k in range(4)))
 
 
 def solution(mesh):

time: 100 us -> 90.9 us (0.909)
  waiting for transfers between devices: 41.9 us -> 37.4 us
  starting transfers between devices: 46.6 us -> 45 us
  Pallas kernels: 5.72 us -> 4.25 us
    all_to_all x1 -> x0, waiting for transfers between devices: 9.44 us -> none  [on_device(): all_planes = lax.all_to_all(sent, ('rep', 'zl'), 0, 0, tiled=True)]
    all_to_all x1 -> x0, starting transfers between devices: 5.49 us -> none  [on_device(): all_planes = lax.all_to_all(sent, ('rep', 'zl'), 0, 0, tiled=True)]
    ppermute x24 -> x29, waiting for transfers between devices: 32.4 us -> 37.4 us  [send(): return lax.ppermute(value, AXES, pairs)]
    ppermute x24 -> x29, starting transfers between devices: 41.2 us -> 45 us  [send(): return lax.ppermute(value, AXES, pairs)]
    pallas_call x3 -> x2, Pallas kernels: 4.91 us -> 3.44 us  [the longest x1 2.1 us: on_device(): pl.pallas_call(assemble, out_shape=shape((64, 8192), f32), in_specs=[SMEM...]
    select_n x9 -> x6, other arithmetic: 3.51 us -> 2.24 us  [the longest x1 1.34 us: on_device(): mine = jnp.where(first, act_inverse, grad_inverse)]
    another operation x2 -> x7, other arithmetic: 0.09 us -> 1.15 us  [the longest x2 1.06 us: on_device(): plane = jnp.stack(turned(first_turn, [line] * 4))]
  transfers between devices with their start and end apart: 25 -> 29, of which waited for: 15 -> 17; matrix products, arithmetic and copies ran while one was open for 0% -> 3% of each run, Pallas kernels for 2% -> 0%
where the time goes in v7:
time: 90.9 us; the launch traced here: 90.6 us
  starting transfers between devices  45 us (50%)
  waiting for transfers between devices  37.4 us (41%)
  Pallas kernels  4.25 us (5%)
  other arithmetic  3.63 us (4%)
    ppermute x29, starting transfers between devices, send(): return lax.ppermute(value, AXES, pairs)  45 us
    ppermute x29, waiting for transfers between devices, send(): return lax.ppermute(value, AXES, pairs)  37.4 us
    pallas_call x1, Pallas kernels, on_device(): pl.pallas_call(assemble, out_shape=shape((64, 8192), f32), in_specs=[SMEM...  2.1 us
  transfers between devices with their start and end apart: 29, of which 17 were waited for; matrix products, arithmetic and copies ran while one was open for 3% of the time, Pallas kernels for 0%

profile of v7, /device:TPU:1, one launch (start us, length us, event | category | flops | bytes accessed | tf_op | source)
XLA Modules:
  0.0 90.6 jit_solution(13430205194134984795)
XLA Ops:
  0.7 3.2 %collective-permute-start = (bf16[64,128]{1,0:T(8,128)(2,1)S(1)}, bf16[64,128]{1,0:T(8,128)(2,1)S(1)}, u32[]{:S(2)}, u32[]{:S(2)}) collective-permute-start(bf16[64,128]{1,0:T(8,128)(2,1)S(1)} %get-tuple-element.12), channel_id=1, source_target_pairs={{0,1},{1,0},{2,3},{3,2},{4,5},{5,4},{6,7},{7,6},{8,9},{9,8},{10,11... | collective-permute-start | bytes 49160 | tf_op jit(solution)/shard_map/ppermute | solution.py:30
  4.9 2.9 %collective-permute-start.2 = (bf16[128,128]{1,0:T(8,128)(2,1)S(1)}, bf16[128,128]{1,0:T(8,128)(2,1)S(1)}, u32[]{:S(2)}, u32[]{:S(2)}) collective-permute-start(bf16[128,128]{1,0:T(8,128)(2,1)S(1)} %get-tuple-element.36), channel_id=1, source_target_pairs={{0,64},{1,65},{2,66},{3,67},{4,68},{5,69},{6,70},{7,71},{8,72},{9,... | collective-permute-start | bytes 98312 | tf_op jit(solution)/shard_map/ppermute | solution.py:30
  8.5 1.2 %collective-permute-start.10 = (bf16[64,8192]{1,0:T(8,128)(2,1)}, bf16[64,8192]{1,0:T(8,128)(2,1)S(1)}, u32[]{:S(2)}, u32[]{:S(2)}) collective-permute-start(bf16[64,8192]{1,0:T(8,128)(2,1)} %param.6), channel_id=1, source_target_pairs={{0,1},{1,0},{2,3},{3,2},{4,5},{5,4},{6,7},{7,6},{8,9},{9,8},{10,11... | collective-permute-start | bytes 3145736 | tf_op jit(solution)/shard_map/ppermute | solution.py:30
  9.7 2.7 %collective-permute-done.3 = bf16[128,128]{1,0:T(8,128)(2,1)S(1)} collective-permute-done((bf16[128,128]{1,0:T(8,128)(2,1)S(1)}, bf16[128,128]{1,0:T(8,128)(2,1)S(1)}, u32[]{:S(2)}, u32[]{:S(2)}) %collective-permute-start.3) | collective-permute-done | bytes 32800 | tf_op jit(solution)/shard_map/ppermute | solution.py:30
  12.4 1.3 %collective-permute-start.4 = (bf16[4,128,128]{2,1,0:T(8,128)(2,1)S(1)}, bf16[4,128,128]{2,1,0:T(8,128)(2,1)S(1)}, u32[]{:S(2)}, u32[]{:S(2)}) collective-permute-start(bf16[4,128,128]{2,1,0:T(8,128)(2,1)S(1)} %get-tuple-element.30), channel_id=1, source_target_pairs={{0,8},{1,3},{2,10},{3,1},{4,12},{5,7},{6,14},{7,5},{8,0},{9,11},{1... | collective-permute-start | bytes 393224 | tf_op jit(solution)/shard_map/ppermute | solution.py:30
  13.7 2.5 %collective-permute-start.5 = (bf16[4,128,128]{2,1,0:T(8,128)(2,1)S(1)}, bf16[4,128,128]{2,1,0:T(8,128)(2,1)}, u32[]{:S(2)}, u32[]{:S(2)}) collective-permute-start(bf16[4,128,128]{2,1,0:T(8,128)(2,1)S(1)} %get-tuple-element.30), channel_id=1, source_target_pairs={{0,16},{1,5},{2,18},{3,7},{4,20},{5,1},{6,22},{7,3},{8,24},{9,13},... | collective-permute-start | bytes 393224 | tf_op jit(solution)/shard_map/ppermute | solution.py:30
  16.4 1.3 %broadcast_select_fusion.1.mine = bf16[64,8192]{1,0:T(8,128)(2,1)S(1)} fusion(bf16[64,8192]{1,0:T(8,128)(2,1)} %param.6, bf16[64,8192]{1,0:T(8,128)(2,1)} %param.7, pred[]{:T(512)S(6)} %eq.3), kind=kLoop, calls=%fused_computation.1 | loop fusion | flops 524288 | bytes 3145729 | tf_op jit(solution)/shard_map/jit(_where)/select_n | solution.py:172
  17.8 2.2 %collective-permute-done.5 = bf16[4,128,128]{2,1,0:T(8,128)(2,1)} collective-permute-done((bf16[4,128,128]{2,1,0:T(8,128)(2,1)S(1)}, bf16[4,128,128]{2,1,0:T(8,128)(2,1)}, u32[]{:S(2)}, u32[]{:S(2)}) %collective-permute-start.5) | collective-permute-done | bytes 131104 | tf_op jit(solution)/shard_map/ppermute | solution.py:30
  20.0 1.7 %collective-permute-done.6 = bf16[4,128,128]{2,1,0:T(8,128)(2,1)} collective-permute-done((bf16[4,128,128]{2,1,0:T(8,128)(2,1)S(1)}, bf16[4,128,128]{2,1,0:T(8,128)(2,1)}, u32[]{:S(2)}, u32[]{:S(2)}) %collective-permute-start.6) | collective-permute-done | bytes 131104 | tf_op jit(solution)/shard_map/ppermute | solution.py:30
  22.8 1.2 %collective-permute-start.7 = (bf16[4,4,128,128]{3,2,1,0:T(8,128)(2,1)S(1)}, bf16[4,4,128,128]{3,2,1,0:T(8,128)(2,1)S(1)}, u32[]{:S(2)}, u32[]{:S(2)}) collective-permute-start(bf16[4,4,128,128]{3,2,1,0:T(8,128)(2,1)S(1)} %pad_maximum_fusion.p0), channel_id=1, source_target_pairs={{0,2},{1,9},{2,0},{3,11},{4,6},{5,13},{6,4},{7,15},{8,10},{9,1},{1... | collective-permute-start | bytes 1572872 | tf_op jit(solution)/shard_map/ppermute | solution.py:30
  24.0 2.8 %collective-permute-start.8 = (bf16[4,4,128,128]{3,2,1,0:T(8,128)(2,1)S(1)}, bf16[4,4,128,128]{3,2,1,0:T(8,128)(2,1)S(1)}, u32[]{:S(2)}, u32[]{:S(2)}) collective-permute-start(bf16[4,4,128,128]{3,2,1,0:T(8,128)(2,1)S(1)} %pad_maximum_fusion.p0), channel_id=1, source_target_pairs={{0,4},{1,17},{2,6},{3,19},{4,0},{5,21},{6,2},{7,23},{8,12},{9,25},... | collective-permute-start | bytes 1572872 | tf_op jit(solution)/shard_map/ppermute | solution.py:30
  26.9 4.3 %collective-permute-done.7.p1 = bf16[4,4,128,128]{3,2,1,0:T(8,128)(2,1)S(1)} collective-permute-done((bf16[4,4,128,128]{3,2,1,0:T(8,128)(2,1)S(1)}, bf16[4,4,128,128]{3,2,1,0:T(8,128)(2,1)S(1)}, u32[]{:S(2)}, u32[]{:S(2)}) %collective-permute-start.7) | collective-permute-done | bytes 524320 | tf_op jit(solution)/shard_map/ppermute | solution.py:30
  31.2 8.1 %collective-permute-done.8.p2 = bf16[4,4,128,128]{3,2,1,0:T(8,128)(2,1)S(1)} collective-permute-done((bf16[4,4,128,128]{3,2,1,0:T(8,128)(2,1)S(1)}, bf16[4,4,128,128]{3,2,1,0:T(8,128)(2,1)S(1)}, u32[]{:S(2)}, u32[]{:S(2)}) %collective-permute-start.8) | collective-permute-done | bytes 524320 | tf_op jit(solution)/shard_map/ppermute | solution.py:30
  39.3 2.6 %collective-permute-done.9.p3 = bf16[4,4,128,128]{3,2,1,0:T(8,128)(2,1)S(1)} collective-permute-done((bf16[4,4,128,128]{3,2,1,0:T(8,128)(2,1)S(1)}, bf16[4,4,128,128]{3,2,1,0:T(8,128)(2,1)S(1)}, u32[]{:S(2)}, u32[]{:S(2)}) %collective-permute-start.9) | collective-permute-done | bytes 524320 | tf_op jit(solution)/shard_map/ppermute | solution.py:30
  41.9 1.3 %precondition.1 = bf16[128,128]{1,0:T(8,128)(2,1)S(1)} custom-call(s32[4]{0:T(128)S(1)} %pad_add_fusion.where, bf16[4,4,128,128]{3,2,1,0:T(8,128)(2,1)S(1)} %pad_maximum_fusion.p0, bf16[4,4,128,128]{3,2,1,0:T(8,128)(2,1)S(1)} %collective-permute-done.7.p1, bf16[4,4,128,128]{3,2,1,0:T(8,128)(2,1)S(1)} %collective-permute-done.8.p2, ...), custom_call_target="tpu_custom_call" | custom-call | tf_op jit(solution)/shard_map/precondition/pallas_call | solution.py:177
  43.3 4.8 %collective-permute-start.12 = (bf16[128,128]{1,0:T(8,128)(2,1)S(1)}, bf16[128,128]{1,0:T(8,128)(2,1)S(1)}, u32[]{:S(2)}, u32[]{:S(2)}) collective-permute-start(bf16[128,128]{1,0:T(8,128)(2,1)S(1)} %precondition.1), channel_id=1, source_target_pairs={{0,1},{1,0},{2,3},{3,2},{4,5},{5,4},{6,7},{7,6},{8,9},{9,8},{10,11... | collective-permute-start | bytes 98312 | tf_op jit(solution)/shard_map/ppermute | solution.py:30
  49.0 4.3 %collective-permute-start.13 = (bf16[128,128]{1,0:T(8,128)(2,1)S(1)}, bf16[128,128]{1,0:T(8,128)(2,1)S(1)}, u32[]{:S(2)}, u32[]{:S(2)}) collective-permute-start(bf16[128,128]{1,0:T(8,128)(2,1)S(1)} %get-tuple-element.32), channel_id=1, source_target_pairs={{0,128},{1,129},{2,130},{3,131},{4,132},{5,133},{6,134},{7,135},{8... | collective-permute-start | bytes 98312 | tf_op jit(solution)/shard_map/ppermute | solution.py:30
  53.3 1.9 %collective-permute-start.16 = (bf16[128,128]{1,0:T(8,128)(2,1)S(1)}, bf16[128,128]{1,0:T(8,128)(2,1)S(1)}, u32[]{:S(2)}, u32[]{:S(2)}) collective-permute-start(bf16[128,128]{1,0:T(8,128)(2,1)S(1)} %get-tuple-element.31), channel_id=1, source_target_pairs={{0,0},{1,32},{2,2},{3,34},{4,4},{5,36},{6,6},{7,38},{8,8},{9,40},{... | collective-permute-start | bytes 98312 | tf_op jit(solution)/shard_map/ppermute | solution.py:30
  55.3 2.2 %collective-permute-start.18 = (bf16[128,128]{1,0:T(8,128)(2,1)S(1)}, bf16[128,128]{1,0:T(8,128)(2,1)S(1)}, u32[]{:S(2)}, u32[]{:S(2)}) collective-permute-start(bf16[128,128]{1,0:T(8,128)(2,1)S(1)} %get-tuple-element.31), channel_id=1, source_target_pairs={{0,64},{1,96},{2,66},{3,98},{4,68},{5,100},{6,70},{7,102},{8,72},{... | collective-permute-start | bytes 98312 | tf_op jit(solution)/shard_map/ppermute | solution.py:30
  57.5 2.8 %collective-permute-start.19 = (bf16[128,128]{1,0:T(8,128)(2,1)S(1)}, bf16[128,128]{1,0:T(8,128)(2,1)S(1)}, u32[]{:S(2)}, u32[]{:S(2)}) collective-permute-start(bf16[128,128]{1,0:T(8,128)(2,1)S(1)} %get-tuple-element.31), channel_id=1, source_target_pairs={{0,192},{1,224},{2,194},{3,226},{4,196},{5,228},{6,198},{7,230},{8... | collective-permute-start | bytes 98312 | tf_op jit(solution)/shard_map/ppermute | solution.py:30
  61.2 2.0 %collective-permute-done.19 = bf16[128,128]{1,0:T(8,128)(2,1)S(1)} collective-permute-done((bf16[128,128]{1,0:T(8,128)(2,1)S(1)}, bf16[128,128]{1,0:T(8,128)(2,1)S(1)}, u32[]{:S(2)}, u32[]{:S(2)}) %collective-permute-start.19) | collective-permute-done | bytes 32800 | tf_op jit(solution)/shard_map/ppermute | solution.py:30
  63.5 1.4 %collective-permute-start.21 = (bf16[2,128,256]{2,1,0:T(8,128)(2,1)S(1)}, bf16[2,128,256]{2,1,0:T(8,128)(2,1)S(1)}, u32[]{:S(2)}, u32[]{:S(2)}) collective-permute-start(bf16[2,128,256]{2,1,0:T(8,128)(2,1)S(1)} %get-tuple-element.28), channel_id=1, source_target_pairs={{0,16},{1,5},{2,18},{3,7},{4,20},{5,1},{6,22},{7,3},{8,24},{9,13},... | collective-permute-start | bytes 393224 | tf_op jit(solution)/shard_map/ppermute | solution.py:30
  64.9 2.5 %collective-permute-start.22 = (bf16[2,128,256]{2,1,0:T(8,128)(2,1)S(1)}, bf16[2,128,256]{2,1,0:T(8,128)(2,1)S(1)}, u32[]{:S(2)}, u32[]{:S(2)}) collective-permute-start(bf16[2,128,256]{2,1,0:T(8,128)(2,1)S(1)} %get-tuple-element.28), channel_id=1, source_target_pairs={{0,24},{1,7},{2,26},{3,5},{4,28},{5,3},{6,30},{7,1},{8,16},{9,15},... | collective-permute-start | bytes 393224 | tf_op jit(solution)/shard_map/ppermute | solution.py:30
  68.2 1.0 %collective-permute-done.21 = bf16[2,128,256]{2,1,0:T(8,128)(2,1)S(1)} collective-permute-done((bf16[2,128,256]{2,1,0:T(8,128)(2,1)S(1)}, bf16[2,128,256]{2,1,0:T(8,128)(2,1)S(1)}, u32[]{:S(2)}, u32[]{:S(2)}) %collective-permute-start.21) | collective-permute-done | bytes 131104 | tf_op jit(solution)/shard_map/ppermute | solution.py:30
  69.2 1.4 %collective-permute-done.22 = bf16[2,128,256]{2,1,0:T(8,128)(2,1)S(1)} collective-permute-done((bf16[2,128,256]{2,1,0:T(8,128)(2,1)S(1)}, bf16[2,128,256]{2,1,0:T(8,128)(2,1)S(1)}, u32[]{:S(2)}, u32[]{:S(2)}) %collective-permute-start.22) | collective-permute-done | bytes 131104 | tf_op jit(solution)/shard_map/ppermute | solution.py:30
  70.7 2.3 %collective-permute-done.15 = bf16[2,128,256]{2,1,0:T(8,128)(2,1)S(1)} collective-permute-done((bf16[2,128,256]{2,1,0:T(8,128)(2,1)S(1)}, bf16[2,128,256]{2,1,0:T(8,128)(2,1)S(1)}, u32[]{:S(2)}, u32[]{:S(2)}) %collective-permute-start.15) | collective-permute-done | bytes 131104 | tf_op jit(solution)/shard_map/ppermute | solution.py:30
  73.9 3.1 %collective-permute-start.24 = (bf16[128,1024]{1,0:T(8,128)(2,1)S(1)}, bf16[128,1024]{1,0:T(8,128)(2,1)S(1)}, u32[]{:S(2)}, u32[]{:S(2)}) collective-permute-start(bf16[128,1024]{1,0:T(8,128)(2,1)S(1)} %get-tuple-element.15), channel_id=1, source_target_pairs={{0,4},{1,17},{2,6},{3,19},{4,0},{5,21},{6,2},{7,23},{8,12},{9,25},... | collective-permute-start | bytes 786440 | tf_op jit(solution)/shard_map/ppermute | solution.py:30
  77.8 1.6 %collective-permute-done.23 = bf16[128,1024]{1,0:T(8,128)(2,1)S(1)} collective-permute-done((bf16[128,1024]{1,0:T(8,128)(2,1)S(1)}, bf16[128,1024]{1,0:T(8,128)(2,1)S(1)}, u32[]{:S(2)}, u32[]{:S(2)}) %collective-permute-start.23) | collective-permute-done | bytes 262176 | tf_op jit(solution)/shard_map/ppermute | solution.py:30
  79.5 2.3 %collective-permute-start.26 = (bf16[2,64,1024]{2,1,0:T(8,128)(2,1)S(1)}, bf16[2,64,1024]{2,1,0:T(8,128)(2,1)S(1)}, u32[]{:S(2)}, u32[]{:S(2)}) collective-permute-start(bf16[2,64,1024]{2,1,0:T(8,128)(2,1)S(1)} %pad_maximum_fusion.3), channel_id=1, source_target_pairs={{0,1},{1,0},{2,3},{3,2},{4,5},{5,4},{6,7},{7,6},{8,9},{9,8},{10,11... | collective-permute-start | bytes 786440 | tf_op jit(solution)/shard_map/ppermute | solution.py:30
  81.8 2.1 %collective-permute-done.24 = bf16[128,1024]{1,0:T(8,128)(2,1)S(1)} collective-permute-done((bf16[128,1024]{1,0:T(8,128)(2,1)S(1)}, bf16[128,1024]{1,0:T(8,128)(2,1)S(1)}, u32[]{:S(2)}, u32[]{:S(2)}) %collective-permute-start.24) | collective-permute-done | bytes 262176 | tf_op jit(solution)/shard_map/ppermute | solution.py:30
  84.7 1.9 %collective-permute-done.25 = bf16[128,1024]{1,0:T(8,128)(2,1)S(1)} collective-permute-done((bf16[128,1024]{1,0:T(8,128)(2,1)S(1)}, bf16[128,1024]{1,0:T(8,128)(2,1)S(1)}, u32[]{:S(2)}, u32[]{:S(2)}) %collective-permute-start.25) | collective-permute-done | bytes 262176 | tf_op jit(solution)/shard_map/ppermute | solution.py:30
  88.4 2.1 %assemble.1 = f32[64,8192]{1,0:T(8,128)} custom-call(s32[4]{0:T(128)S(1)} %pad_add_fusion.where, bf16[64,1024]{1,0:T(8,128)(2,1)S(1)} %get-tuple-element.24.refs_0_, bf16[64,1024]{1,0:T(8,128)(2,1)S(1)} %get-tuple-element.26.refs_1_, bf16[64,1024]{1,0:T(8,128)(2,1)S(1)} %get-tuple-element.20.refs_2_, bf16[64,1024]{1,0:T(8,128)(2,1)S(1)} %get-tuple-element.18.refs_3_, ...), custom_call_target="tpu_custom_call" | custom-call | tf_op jit(solution)/shard_map/assemble/pallas_call | solution.py:203
  (51 shorter events, 11.2 us)
Async XLA Ops:
  0.7 4.1 %collective-permute-start = (bf16[64,128]{1,0:T(8,128)(2,1)S(1)}, bf16[64,128]{1,0:T(8,128)(2,1)S(1)}, u32[]{:S(2)}, u32[]{:S(2)}) collective-permute-start(bf16[64,128]{1,0:T(8,128)(2,1)S(1)} %get-tuple-element.12), channel_id=1, source_target_pairs={{0,1},{1,0},{2,3},{3,2},{4,5},{5,4},{6,7},{7,6},{8,9},{9,8},{10,11... | collective-permute-start | bytes 49160 | tf_op jit(solution)/shard_map/ppermute | solution.py:30
  4.8 4.8 %collective-permute-start.1 = (bf16[128,128]{1,0:T(8,128)(2,1)S(1)}, bf16[128,128]{1,0:T(8,128)(2,1)S(1)}, u32[]{:S(2)}, u32[]{:S(2)}) collective-permute-start(bf16[128,128]{1,0:T(8,128)(2,1)S(1)} %get-tuple-element.36), channel_id=1, source_target_pairs={{0,32},{1,33},{2,34},{3,35},{4,36},{5,37},{6,38},{7,39},{8,40},{9,... | collective-permute-start | bytes 98312 | tf_op jit(solution)/shard_map/ppermute | solution.py:30
  4.9 4.7 %collective-permute-start.2 = (bf16[128,128]{1,0:T(8,128)(2,1)S(1)}, bf16[128,128]{1,0:T(8,128)(2,1)S(1)}, u32[]{:S(2)}, u32[]{:S(2)}) collective-permute-start(bf16[128,128]{1,0:T(8,128)(2,1)S(1)} %get-tuple-element.36), channel_id=1, source_target_pairs={{0,64},{1,65},{2,66},{3,67},{4,68},{5,69},{6,70},{7,71},{8,72},{9,... | collective-permute-start | bytes 98312 | tf_op jit(solution)/shard_map/ppermute | solution.py:30
  7.8 4.6 %collective-permute-start.3 = (bf16[128,128]{1,0:T(8,128)(2,1)S(1)}, bf16[128,128]{1,0:T(8,128)(2,1)S(1)}, u32[]{:S(2)}, u32[]{:S(2)}) collective-permute-start(bf16[128,128]{1,0:T(8,128)(2,1)S(1)} %get-tuple-element.36), channel_id=1, source_target_pairs={{0,96},{1,97},{2,98},{3,99},{4,100},{5,101},{6,102},{7,103},{8,104... | collective-permute-start | bytes 98312 | tf_op jit(solution)/shard_map/ppermute | solution.py:30
  8.5 18.3 %collective-permute-start.10 = (bf16[64,8192]{1,0:T(8,128)(2,1)}, bf16[64,8192]{1,0:T(8,128)(2,1)S(1)}, u32[]{:S(2)}, u32[]{:S(2)}) collective-permute-start(bf16[64,8192]{1,0:T(8,128)(2,1)} %param.6), channel_id=1, source_target_pairs={{0,1},{1,0},{2,3},{3,2},{4,5},{5,4},{6,7},{7,6},{8,9},{9,8},{10,11... | collective-permute-start | bytes 3145736 | tf_op jit(solution)/shard_map/ppermute | solution.py:30
  9.7 17.1 %collective-permute-start.11 = (bf16[64,8192]{1,0:T(8,128)(2,1)}, bf16[64,8192]{1,0:T(8,128)(2,1)S(1)}, u32[]{:S(2)}, u32[]{:S(2)}) collective-permute-start(bf16[64,8192]{1,0:T(8,128)(2,1)} %param.7), channel_id=1, source_target_pairs={{0,1},{1,0},{2,3},{3,2},{4,5},{5,4},{6,7},{7,6},{8,9},{9,8},{10,11... | collective-permute-start | bytes 3145736 | tf_op jit(solution)/shard_map/ppermute | solution.py:30
  12.4 5.4 %collective-permute-start.4 = (bf16[4,128,128]{2,1,0:T(8,128)(2,1)S(1)}, bf16[4,128,128]{2,1,0:T(8,128)(2,1)S(1)}, u32[]{:S(2)}, u32[]{:S(2)}) collective-permute-start(bf16[4,128,128]{2,1,0:T(8,128)(2,1)S(1)} %get-tuple-element.30), channel_id=1, source_target_pairs={{0,8},{1,3},{2,10},{3,1},{4,12},{5,7},{6,14},{7,5},{8,0},{9,11},{1... | collective-permute-start | bytes 393224 | tf_op jit(solution)/shard_map/ppermute | solution.py:30
  13.7 6.3 %collective-permute-start.5 = (bf16[4,128,128]{2,1,0:T(8,128)(2,1)S(1)}, bf16[4,128,128]{2,1,0:T(8,128)(2,1)}, u32[]{:S(2)}, u32[]{:S(2)}) collective-permute-start(bf16[4,128,128]{2,1,0:T(8,128)(2,1)S(1)} %get-tuple-element.30), channel_id=1, source_target_pairs={{0,16},{1,5},{2,18},{3,7},{4,20},{5,1},{6,22},{7,3},{8,24},{9,13},... | collective-permute-start | bytes 393224 | tf_op jit(solution)/shard_map/ppermute | solution.py:30
  16.2 5.6 %collective-permute-start.6 = (bf16[4,128,128]{2,1,0:T(8,128)(2,1)S(1)}, bf16[4,128,128]{2,1,0:T(8,128)(2,1)}, u32[]{:S(2)}, u32[]{:S(2)}) collective-permute-start(bf16[4,128,128]{2,1,0:T(8,128)(2,1)S(1)} %get-tuple-element.30), channel_id=1, source_target_pairs={{0,24},{1,7},{2,26},{3,5},{4,28},{5,3},{6,30},{7,1},{8,16},{9,15},... | collective-permute-start | bytes 393224 | tf_op jit(solution)/shard_map/ppermute | solution.py:30
  22.8 8.4 %collective-permute-start.7 = (bf16[4,4,128,128]{3,2,1,0:T(8,128)(2,1)S(1)}, bf16[4,4,128,128]{3,2,1,0:T(8,128)(2,1)S(1)}, u32[]{:S(2)}, u32[]{:S(2)}) collective-permute-start(bf16[4,4,128,128]{3,2,1,0:T(8,128)(2,1)S(1)} %pad_maximum_fusion.p0), channel_id=1, source_target_pairs={{0,2},{1,9},{2,0},{3,11},{4,6},{5,13},{6,4},{7,15},{8,10},{9,1},{1... | collective-permute-start | bytes 1572872 | tf_op jit(solution)/shard_map/ppermute | solution.py:30
  24.0 15.3 %collective-permute-start.8 = (bf16[4,4,128,128]{3,2,1,0:T(8,128)(2,1)S(1)}, bf16[4,4,128,128]{3,2,1,0:T(8,128)(2,1)S(1)}, u32[]{:S(2)}, u32[]{:S(2)}) collective-permute-start(bf16[4,4,128,128]{3,2,1,0:T(8,128)(2,1)S(1)} %pad_maximum_fusion.p0), channel_id=1, source_target_pairs={{0,4},{1,17},{2,6},{3,19},{4,0},{5,21},{6,2},{7,23},{8,12},{9,25},... | collective-permute-start | bytes 1572872 | tf_op jit(solution)/shard_map/ppermute | solution.py:30
  26.8 15.2 %collective-permute-start.9 = (bf16[4,4,128,128]{3,2,1,0:T(8,128)(2,1)S(1)}, bf16[4,4,128,128]{3,2,1,0:T(8,128)(2,1)S(1)}, u32[]{:S(2)}, u32[]{:S(2)}) collective-permute-start(bf16[4,4,128,128]{3,2,1,0:T(8,128)(2,1)S(1)} %pad_maximum_fusion.p0), channel_id=1, source_target_pairs={{0,6},{1,25},{2,4},{3,27},{4,2},{5,29},{6,0},{7,31},{8,14},{9,17},... | collective-permute-start | bytes 1572872 | tf_op jit(solution)/shard_map/ppermute | solution.py:30
  43.3 5.7 %collective-permute-start.12 = (bf16[128,128]{1,0:T(8,128)(2,1)S(1)}, bf16[128,128]{1,0:T(8,128)(2,1)S(1)}, u32[]{:S(2)}, u32[]{:S(2)}) collective-permute-start(bf16[128,128]{1,0:T(8,128)(2,1)S(1)} %precondition.1), channel_id=1, source_target_pairs={{0,1},{1,0},{2,3},{3,2},{4,5},{5,4},{6,7},{7,6},{8,9},{9,8},{10,11... | collective-permute-start | bytes 98312 | tf_op jit(solution)/shard_map/ppermute | solution.py:30
  49.0 11.3 %collective-permute-start.13 = (bf16[128,128]{1,0:T(8,128)(2,1)S(1)}, bf16[128,128]{1,0:T(8,128)(2,1)S(1)}, u32[]{:S(2)}, u32[]{:S(2)}) collective-permute-start(bf16[128,128]{1,0:T(8,128)(2,1)S(1)} %get-tuple-element.32), channel_id=1, source_target_pairs={{0,128},{1,129},{2,130},{3,131},{4,132},{5,133},{6,134},{7,135},{8... | collective-permute-start | bytes 98312 | tf_op jit(solution)/shard_map/ppermute | solution.py:30
  53.3 7.2 %collective-permute-start.16 = (bf16[128,128]{1,0:T(8,128)(2,1)S(1)}, bf16[128,128]{1,0:T(8,128)(2,1)S(1)}, u32[]{:S(2)}, u32[]{:S(2)}) collective-permute-start(bf16[128,128]{1,0:T(8,128)(2,1)S(1)} %get-tuple-element.31), channel_id=1, source_target_pairs={{0,0},{1,32},{2,2},{3,34},{4,4},{5,36},{6,6},{7,38},{8,8},{9,40},{... | collective-permute-start | bytes 98312 | tf_op jit(solution)/shard_map/ppermute | solution.py:30
  55.2 6.0 %collective-permute-start.17 = (bf16[128,128]{1,0:T(8,128)(2,1)S(1)}, bf16[128,128]{1,0:T(8,128)(2,1)S(1)}, u32[]{:S(2)}, u32[]{:S(2)}) collective-permute-start(bf16[128,128]{1,0:T(8,128)(2,1)S(1)} %get-tuple-element.31), channel_id=1, source_target_pairs={{0,128},{1,160},{2,130},{3,162},{4,132},{5,164},{6,134},{7,166},{8... | collective-permute-start | bytes 98312 | tf_op jit(solution)/shard_map/ppermute | solution.py:30
  55.3 5.9 %collective-permute-start.18 = (bf16[128,128]{1,0:T(8,128)(2,1)S(1)}, bf16[128,128]{1,0:T(8,128)(2,1)S(1)}, u32[]{:S(2)}, u32[]{:S(2)}) collective-permute-start(bf16[128,128]{1,0:T(8,128)(2,1)S(1)} %get-tuple-element.31), channel_id=1, source_target_pairs={{0,64},{1,96},{2,66},{3,98},{4,68},{5,100},{6,70},{7,102},{8,72},{... | collective-permute-start | bytes 98312 | tf_op jit(solution)/shard_map/ppermute | solution.py:30
  57.5 5.7 %collective-permute-start.19 = (bf16[128,128]{1,0:T(8,128)(2,1)S(1)}, bf16[128,128]{1,0:T(8,128)(2,1)S(1)}, u32[]{:S(2)}, u32[]{:S(2)}) collective-permute-start(bf16[128,128]{1,0:T(8,128)(2,1)S(1)} %get-tuple-element.31), channel_id=1, source_target_pairs={{0,192},{1,224},{2,194},{3,226},{4,196},{5,228},{6,198},{7,230},{8... | collective-permute-start | bytes 98312 | tf_op jit(solution)/shard_map/ppermute | solution.py:30
  60.3 7.1 %collective-permute-start.14 = (bf16[128,256]{1,0:T(8,128)(2,1)S(1)}, bf16[128,256]{1,0:T(8,128)(2,1)S(1)}, u32[]{:S(2)}, u32[]{:S(2)}) collective-permute-start(bf16[128,256]{1,0:T(8,128)(2,1)S(1)} %get-tuple-element.34), channel_id=1, source_target_pairs={{0,2},{1,9},{2,0},{3,11},{4,6},{5,13},{6,4},{7,15},{8,10},{9,1},{1... | collective-permute-start | bytes 196616 | tf_op jit(solution)/shard_map/ppermute | solution.py:30
  63.2 4.9 %collective-permute-start.20 = (bf16[2,128,256]{2,1,0:T(8,128)(2,1)S(1)}, bf16[2,128,256]{2,1,0:T(8,128)(2,1)S(1)}, u32[]{:S(2)}, u32[]{:S(2)}) collective-permute-start(bf16[2,128,256]{2,1,0:T(8,128)(2,1)S(1)} %get-tuple-element.28), channel_id=1, source_target_pairs={{0,8},{1,3},{2,10},{3,1},{4,12},{5,7},{6,14},{7,5},{8,0},{9,11},{1... | collective-permute-start | bytes 393224 | tf_op jit(solution)/shard_map/ppermute | solution.py:30
  63.5 5.7 %collective-permute-start.21 = (bf16[2,128,256]{2,1,0:T(8,128)(2,1)S(1)}, bf16[2,128,256]{2,1,0:T(8,128)(2,1)S(1)}, u32[]{:S(2)}, u32[]{:S(2)}) collective-permute-start(bf16[2,128,256]{2,1,0:T(8,128)(2,1)S(1)} %get-tuple-element.28), channel_id=1, source_target_pairs={{0,16},{1,5},{2,18},{3,7},{4,20},{5,1},{6,22},{7,3},{8,24},{9,13},... | collective-permute-start | bytes 393224 | tf_op jit(solution)/shard_map/ppermute | solution.py:30
  64.9 5.7 %collective-permute-start.22 = (bf16[2,128,256]{2,1,0:T(8,128)(2,1)S(1)}, bf16[2,128,256]{2,1,0:T(8,128)(2,1)S(1)}, u32[]{:S(2)}, u32[]{:S(2)}) collective-permute-start(bf16[2,128,256]{2,1,0:T(8,128)(2,1)S(1)} %get-tuple-element.28), channel_id=1, source_target_pairs={{0,24},{1,7},{2,26},{3,5},{4,28},{5,3},{6,30},{7,1},{8,16},{9,15},... | collective-permute-start | bytes 393224 | tf_op jit(solution)/shard_map/ppermute | solution.py:30
  67.4 5.6 %collective-permute-start.15 = (bf16[2,128,256]{2,1,0:T(8,128)(2,1)S(1)}, bf16[2,128,256]{2,1,0:T(8,128)(2,1)S(1)}, u32[]{:S(2)}, u32[]{:S(2)}) collective-permute-start(bf16[2,128,256]{2,1,0:T(8,128)(2,1)S(1)} %pad_maximum_fusion.5), channel_id=1, source_target_pairs={{0,6},{1,25},{2,4},{3,27},{4,2},{5,29},{6,0},{7,31},{8,14},{9,17},... | collective-permute-start | bytes 393224 | tf_op jit(solution)/shard_map/ppermute | solution.py:30
  73.8 5.6 %collective-permute-start.23 = (bf16[128,1024]{1,0:T(8,128)(2,1)S(1)}, bf16[128,1024]{1,0:T(8,128)(2,1)S(1)}, u32[]{:S(2)}, u32[]{:S(2)}) collective-permute-start(bf16[128,1024]{1,0:T(8,128)(2,1)S(1)} %get-tuple-element.14), channel_id=1, source_target_pairs={{0,2},{1,9},{2,0},{3,11},{4,6},{5,13},{6,4},{7,15},{8,10},{9,1},{1... | collective-permute-start | bytes 786440 | tf_op jit(solution)/shard_map/ppermute | solution.py:30
  73.9 10.0 %collective-permute-start.24 = (bf16[128,1024]{1,0:T(8,128)(2,1)S(1)}, bf16[128,1024]{1,0:T(8,128)(2,1)S(1)}, u32[]{:S(2)}, u32[]{:S(2)}) collective-permute-start(bf16[128,1024]{1,0:T(8,128)(2,1)S(1)} %get-tuple-element.15), channel_id=1, source_target_pairs={{0,4},{1,17},{2,6},{3,19},{4,0},{5,21},{6,2},{7,23},{8,12},{9,25},... | collective-permute-start | bytes 786440 | tf_op jit(solution)/shard_map/ppermute | solution.py:30
  77.0 9.5 %collective-permute-start.25 = (bf16[128,1024]{1,0:T(8,128)(2,1)S(1)}, bf16[128,1024]{1,0:T(8,128)(2,1)S(1)}, u32[]{:S(2)}, u32[]{:S(2)}) collective-permute-start(bf16[128,1024]{1,0:T(8,128)(2,1)S(1)} %get-tuple-element.16), channel_id=1, source_target_pairs={{0,6},{1,25},{2,4},{3,27},{4,2},{5,29},{6,0},{7,31},{8,14},{9,17},... | collective-permute-start | bytes 786440 | tf_op jit(solution)/shard_map/ppermute | solution.py:30
  79.5 7.9 %collective-permute-start.26 = (bf16[2,64,1024]{2,1,0:T(8,128)(2,1)S(1)}, bf16[2,64,1024]{2,1,0:T(8,128)(2,1)S(1)}, u32[]{:S(2)}, u32[]{:S(2)}) collective-permute-start(bf16[2,64,1024]{2,1,0:T(8,128)(2,1)S(1)} %pad_maximum_fusion.3), channel_id=1, source_target_pairs={{0,1},{1,0},{2,3},{3,2},{4,5},{5,4},{6,7},{7,6},{8,9},{9,8},{10,11... | collective-permute-start | bytes 786440 | tf_op jit(solution)/shard_map/ppermute | solution.py:30
  83.9 3.5 %collective-permute-start.27 = (bf16[64,1024]{1,0:T(8,128)(2,1)S(1)}, bf16[64,1024]{1,0:T(8,128)(2,1)S(1)}, u32[]{:S(2)}, u32[]{:S(2)}) collective-permute-start(bf16[64,1024]{1,0:T(8,128)(2,1)S(1)} %get-tuple-element.19), channel_id=1, source_target_pairs={{0,1},{1,0},{2,3},{3,2},{4,5},{5,4},{6,7},{7,6},{8,9},{9,8},{10,11... | collective-permute-start | bytes 393224 | tf_op jit(solution)/shard_map/ppermute | solution.py:30
  86.6 1.8 %collective-permute-start.28 = (bf16[64,1024]{1,0:T(8,128)(2,1)S(1)}, bf16[64,1024]{1,0:T(8,128)(2,1)S(1)}, u32[]{:S(2)}, u32[]{:S(2)}) collective-permute-start(bf16[64,1024]{1,0:T(8,128)(2,1)S(1)} %get-tuple-element.17), channel_id=1, source_target_pairs={{0,1},{1,0},{2,3},{3,2},{4,5},{5,4},{6,7},{7,6},{8,9},{9,8},{10,11... | collective-permute-start | bytes 393224 | tf_op jit(solution)/shard_map/ppermute | solution.py:30

commit v8 on v7

--- a/solution.py
+++ b/solution.py
@@ -74,8 +74,9 @@
     return pl.multiple_of(((z * 4 + y) * 4 + x) * 128, 128)
 
 
-def precondition(where, p0, p1, p2, p3, mine, theirs, pre):
+def precondition(where, p0, p1, p2, p3, low, high, pre):
     total = jnp.zeros((128, 128), jnp.float32)
+    none = jnp.zeros((64, 128), jnp.bfloat16)
     for k3, piece in enumerate((p0, p1, p2, p3)):
         for k2 in range(4):
             at = [
@@ -85,17 +86,21 @@
             rows = jnp.concatenate(
                 [
                     jnp.concatenate([side[:, part] for part in at], axis=1)
-                    for side in (mine, theirs)
+                    for side in (low, high)
                 ],
                 axis=0,
             )
+            held = []
+            for kz in range(4):
+                block = piece[k2, kz]
+                held.append(jnp.where(where[3] == 0, block, none))
+                held.append(jnp.where(where[3] == 0, none, block))
             total += jnp.dot(
                 rows,
-                piece[k2].reshape(512, 128),
+                jnp.concatenate(held, axis=0),
                 preferred_element_type=jnp.float32,
             )
-    crossed = jnp.concatenate([total[64:], total[:64]], axis=0)
-    pre[...] = jnp.where(where[3] == 0, total, crossed).astype(pre.dtype)
+    pre[...] = total
 
 
 def tiles(g, plane, *made):
@@ -161,26 +166,28 @@
     ).astype(jnp.int32)
     first = c == 0
 
-    acts_t, grads_t = acts.T, grads_out.T
-    kept, given = lax.optimization_barrier(
-        (jnp.where(first, acts_t, grads_t), jnp.where(first, grads_t, acts_t))
-    )
-    got = swap_cores(given)
-    block = jnp.concatenate(
-        [jnp.where(first, kept, got), jnp.where(first, got, kept)], axis=0
-    )
-    mine = jnp.where(first, act_inverse, grad_inverse)
-    theirs = jnp.where(first, swap_cores(act_inverse), swap_cores(grad_inverse))
+    block = jnp.stack([acts.T, grads_out.T])
     line = jnp.stack(turned(along_line, [block] * 4))
-    plane = jnp.stack(turned(first_turn, [line] * 4))
-    pieces = turned(second_turn, [plane] * 4)
-    pre = call(
-        precondition, "precondition", shape((128, 128), bf16), [SMEM] + [VMEM] * 6
-    )(where, *pieces, mine, theirs)
-
-    near = swap_cores(pre)
-    act = jnp.where(first, pre, near)
-    grad = jnp.where(first, near, pre)
+    held = turned(first_turn, [line] * 4)
+    act_plane = jnp.stack([part[:, 0] for part in held])
+    grad_plane = jnp.stack([part[:, 1] for part in held])
+
+    def factor(rows):
+        theirs = swap_cores(rows)
+        return jnp.where(first, rows, theirs), jnp.where(first, theirs, rows)
+
+    def partial(pieces, rows):
+        return call(
+            precondition, "precondition", shape((128, 128), f32), [SMEM] + [VMEM] * 6
+        )(where, *pieces, *rows)
+
+    act_rows, grad_rows = factor(act_inverse), factor(grad_inverse)
+    part = partial(turned(second_turn, [act_plane] * 4), act_rows)
+    part, grad_plane = lax.optimization_barrier((part, grad_plane))
+    act = (part + swap_cores(part)).astype(bf16)
+    part = partial(turned(second_turn, [grad_plane] * 4), grad_rows)
+    grad = (part + swap_cores(part)).astype(bf16)
+
     here = [to_parity(act, j, 0) for j in (0, 1)]
     there = [to_parity(act, j, 1) for j in (0, 1)]
     pair = jnp.stack([jnp.concatenate(p, axis=1) for p in zip(here, there)])

time: 90.9 us -> 89.7 us (0.987)
  waiting for transfers between devices: 37.4 us -> 26.9 us
  starting transfers between devices: 45 us -> 54.7 us
  other arithmetic: 3.63 us -> 1.7 us
  Pallas kernels: 4.25 us -> 5.75 us
    ppermute x29 -> x32, waiting for transfers between devices: 37.4 us -> 26.9 us  [send(): return lax.ppermute(value, AXES, pairs)]
    ppermute x29 -> x32, starting transfers between devices: 45 us -> 54.7 us  [send(): return lax.ppermute(value, AXES, pairs)]
    select_n x5 -> x2, other arithmetic: 2.21 us -> 0.41 us  [factor(): return (jnp.where(first, rows, theirs), jnp.where(first, theirs, rows))]
    pallas_call x1 -> x2, Pallas kernels: 1.33 us -> 2.83 us  [partial(): call(precondition, 'precondition', shape((128, 128), f32), [SMEM] + [VMEM...]
    another operation x2, other arithmetic: 1.06 us -> 0.07 us  [the longest x1 0.04 us: on_device(): act_plane = jnp.stack([part[:, 0] for part in held])]
  transfers between devices with their start and end apart: 29 -> 32, of which waited for: 17 -> 16; matrix products, arithmetic and copies ran while one was open for 3% -> 1% of each run, Pallas kernels for 0% -> 3%
where the time goes in v8:
time: 89.7 us; the launch traced here: 89.5 us
  starting transfers between devices  54.7 us (61%)
  waiting for transfers between devices  26.9 us (30%)
  Pallas kernels  5.75 us (6%)
  other arithmetic  1.7 us (2%)
    ppermute x32, starting transfers between devices, send(): return lax.ppermute(value, AXES, pairs)  54.7 us
    ppermute x32, waiting for transfers between devices, send(): return lax.ppermute(value, AXES, pairs)  26.9 us
    pallas_call x2, Pallas kernels, partial(): call(precondition, 'precondition', shape((128, 128), f32), [SMEM] + [VMEM...  2.83 us
    pallas_call x1, Pallas kernels, on_device(): pl.pallas_call(assemble, out_shape=shape((64, 8192), f32), in_specs=[SMEM...  2.1 us
  transfers between devices with their start and end apart: 32, of which 16 were waited for; matrix products, arithmetic and copies ran while one was open for 1% of the time, Pallas kernels for 3%

profile of v8, /device:TPU:1, one launch (start us, length us, event | category | flops | bytes accessed | tf_op | source)
XLA Modules:
  0.0 89.5 jit_solution(1217437644376423220)
XLA Ops:
  0.8 5.2 %collective-permute-start.2 = (bf16[2,64,128]{2,1,0:T(8,128)(2,1)S(1)}, bf16[2,64,128]{2,1,0:T(8,128)(2,1)S(1)}, u32[]{:S(2)}, u32[]{:S(2)}) collective-permute-start(bf16[2,64,128]{2,1,0:T(8,128)(2,1)S(1)} %get-tuple-element.44), channel_id=1, source_target_pairs={{0,96},{1,97},{2,98},{3,99},{4,100},{5,101},{6,102},{7,103},{8,104... | collective-permute-start | bytes 98312 | tf_op jit(solution)/shard_map/ppermute | solution.py:30
  6.4 2.1 %collective-permute-start.9 = (bf16[64,8192]{1,0:T(8,128)(2,1)}, bf16[64,8192]{1,0:T(8,128)(2,1)S(1)}, u32[]{:S(2)}, u32[]{:S(2)}) collective-permute-start(bf16[64,8192]{1,0:T(8,128)(2,1)} %param.6), channel_id=1, source_target_pairs={{0,1},{1,0},{2,3},{3,2},{4,5},{5,4},{6,7},{7,6},{8,9},{9,8},{10,11... | collective-permute-start | bytes 3145736 | tf_op jit(solution)/shard_map/ppermute | solution.py:30
  8.5 1.5 %collective-permute-done.1 = bf16[2,64,128]{2,1,0:T(8,128)(2,1)S(1)} collective-permute-done((bf16[2,64,128]{2,1,0:T(8,128)(2,1)S(1)}, bf16[2,64,128]{2,1,0:T(8,128)(2,1)S(1)}, u32[]{:S(2)}, u32[]{:S(2)}) %collective-permute-start.1) | collective-permute-done | bytes 32800 | tf_op jit(solution)/shard_map/ppermute | solution.py:30
  10.1 2.6 %collective-permute-start.5 = (bf16[4,2,64,128]{3,2,0,1:T(8,128)(2,1)S(1)}, bf16[4,2,64,128]{3,2,0,1:T(8,128)(2,1)S(1)}, u32[]{:S(2)}, u32[]{:S(2)}) collective-permute-start(bf16[4,2,64,128]{3,2,0,1:T(8,128)(2,1)S(1)} %pad_maximum_fusion.5), channel_id=1, source_target_pairs={{0,24},{1,7},{2,26},{3,5},{4,28},{5,3},{6,30},{7,1},{8,16},{9,15},... | collective-permute-start | bytes 393224 | tf_op jit(solution)/shard_map/ppermute | solution.py:30
  13.4 2.5 %collective-permute-done.5 = bf16[4,2,64,128]{3,2,0,1:T(8,128)(2,1)S(1)} collective-permute-done((bf16[4,2,64,128]{3,2,0,1:T(8,128)(2,1)S(1)}, bf16[4,2,64,128]{3,2,0,1:T(8,128)(2,1)S(1)}, u32[]{:S(2)}, u32[]{:S(2)}) %collective-permute-start.5) | collective-permute-done | bytes 131104 | tf_op jit(solution)/shard_map/ppermute | solution.py:30
  16.0 2.0 %collective-permute-done.4 = bf16[4,2,64,128]{3,2,0,1:T(8,128)(2,1)S(1)} collective-permute-done((bf16[4,2,64,128]{3,2,0,1:T(8,128)(2,1)S(1)}, bf16[4,2,64,128]{3,2,0,1:T(8,128)(2,1)S(1)}, u32[]{:S(2)}, u32[]{:S(2)}) %collective-permute-start.4) | collective-permute-done | bytes 131104 | tf_op jit(solution)/shard_map/ppermute | solution.py:30
  18.0 1.4 %collective-permute-start.6 = (bf16[4,4,64,128]{3,2,1,0:T(8,128)(2,1)S(1)}, bf16[4,4,64,128]{3,2,1,0:T(8,128)(2,1)S(1)}, u32[]{:S(2)}, u32[]{:S(2)}) collective-permute-start(bf16[4,4,64,128]{3,2,1,0:T(8,128)(2,1)S(1)} %pad_maximum_fusion.1.p0), channel_id=1, source_target_pairs={{0,2},{1,9},{2,0},{3,11},{4,6},{5,13},{6,4},{7,15},{8,10},{9,1},{1... | collective-permute-start | bytes 786440 | tf_op jit(solution)/shard_map/ppermute | solution.py:30
  19.4 2.9 %collective-permute-start.7 = (bf16[4,4,64,128]{3,2,1,0:T(8,128)(2,1)S(1)}, bf16[4,4,64,128]{3,2,1,0:T(8,128)(2,1)S(1)}, u32[]{:S(2)}, u32[]{:S(2)}) collective-permute-start(bf16[4,4,64,128]{3,2,1,0:T(8,128)(2,1)S(1)} %pad_maximum_fusion.1.p0), channel_id=1, source_target_pairs={{0,4},{1,17},{2,6},{3,19},{4,0},{5,21},{6,2},{7,23},{8,12},{9,25},... | collective-permute-start | bytes 786440 | tf_op jit(solution)/shard_map/ppermute | solution.py:30
  23.4 5.6 %collective-permute-done.7.p2 = bf16[4,4,64,128]{3,2,1,0:T(8,128)(2,1)S(1)} collective-permute-done((bf16[4,4,64,128]{3,2,1,0:T(8,128)(2,1)S(1)}, bf16[4,4,64,128]{3,2,1,0:T(8,128)(2,1)S(1)}, u32[]{:S(2)}, u32[]{:S(2)}) %collective-permute-start.7) | collective-permute-done | bytes 262176 | tf_op jit(solution)/shard_map/ppermute | solution.py:30
  29.0 2.9 %collective-permute-done.8.p3 = bf16[4,4,64,128]{3,2,1,0:T(8,128)(2,1)S(1)} collective-permute-done((bf16[4,4,64,128]{3,2,1,0:T(8,128)(2,1)S(1)}, bf16[4,4,64,128]{3,2,1,0:T(8,128)(2,1)S(1)}, u32[]{:S(2)}, u32[]{:S(2)}) %collective-permute-start.8) | collective-permute-done | bytes 262176 | tf_op jit(solution)/shard_map/ppermute | solution.py:30
  31.9 1.4 %precondition.2 = f32[128,128]{1,0:T(8,128)S(1)} custom-call(s32[4]{0:T(128)S(1)} %pad_add_fusion.where, bf16[4,4,64,128]{3,2,1,0:T(8,128)(2,1)S(1)} %pad_maximum_fusion.1.p0, bf16[4,4,64,128]{3,2,1,0:T(8,128)(2,1)S(1)} %collective-permute-done.6.p1, bf16[4,4,64,128]{3,2,1,0:T(8,128)(2,1)S(1)} %collective-permute-done.7.p2, ...), custom_call_target="tpu_custom_call" | custom-call | tf_op jit(solution)/shard_map/precondition/pallas_call | solution.py:180
  33.3 3.9 %collective-permute-start.18 = (f32[128,128]{1,0:T(8,128)S(1)}, f32[128,128]{1,0:T(8,128)S(1)}, u32[]{:S(2)}, u32[]{:S(2)}) collective-permute-start(f32[128,128]{1,0:T(8,128)S(1)} %precondition.2), channel_id=1, source_target_pairs={{0,1},{1,0},{2,3},{3,2},{4,5},{5,4},{6,7},{7,6},{8,9},{9,8},{10,11... | collective-permute-start | bytes 196616 | tf_op jit(solution)/shard_map/ppermute | solution.py:30
  37.5 2.6 %collective-permute-start.11 = (bf16[4,4,64,128]{3,2,1,0:T(8,128)(2,1)S(1)}, bf16[4,4,64,128]{3,2,1,0:T(8,128)(2,1)S(1)}, u32[]{:S(2)}, u32[]{:S(2)}) collective-permute-start(bf16[4,4,64,128]{3,2,1,0:T(8,128)(2,1)S(1)} %pad_maximum_fusion.2.p0), channel_id=1, source_target_pairs={{0,4},{1,17},{2,6},{3,19},{4,0},{5,21},{6,2},{7,23},{8,12},{9,25},... | collective-permute-start | bytes 786440 | tf_op jit(solution)/shard_map/ppermute | solution.py:30
  40.1 1.0 %collective-permute-start.12 = (bf16[4,4,64,128]{3,2,1,0:T(8,128)(2,1)S(1)}, bf16[4,4,64,128]{3,2,1,0:T(8,128)(2,1)S(1)}, u32[]{:S(2)}, u32[]{:S(2)}) collective-permute-start(bf16[4,4,64,128]{3,2,1,0:T(8,128)(2,1)S(1)} %pad_maximum_fusion.2.p0), channel_id=1, source_target_pairs={{0,6},{1,25},{2,4},{3,27},{4,2},{5,29},{6,0},{7,31},{8,14},{9,17},... | collective-permute-start | bytes 786440 | tf_op jit(solution)/shard_map/ppermute | solution.py:30
  41.1 3.8 %collective-permute-start.22 = (bf16[128,128]{1,0:T(8,128)(2,1)S(1)}, bf16[128,128]{1,0:T(8,128)(2,1)S(1)}, u32[]{:S(2)}, u32[]{:S(2)}) collective-permute-start(bf16[128,128]{1,0:T(8,128)(2,1)S(1)} %add_convert_fusion), channel_id=1, source_target_pairs={{0,192},{1,224},{2,194},{3,226},{4,196},{5,228},{6,198},{7,230},{8... | collective-permute-start | bytes 98312 | tf_op jit(solution)/shard_map/ppermute | solution.py:30
  44.9 2.1 %collective-permute-start.21 = (bf16[128,128]{1,0:T(8,128)(2,1)S(1)}, bf16[128,128]{1,0:T(8,128)(2,1)S(1)}, u32[]{:S(2)}, u32[]{:S(2)}) collective-permute-start(bf16[128,128]{1,0:T(8,128)(2,1)S(1)} %add_convert_fusion), channel_id=1, source_target_pairs={{0,64},{1,96},{2,66},{3,98},{4,68},{5,100},{6,70},{7,102},{8,72},{... | collective-permute-start | bytes 98312 | tf_op jit(solution)/shard_map/ppermute | solution.py:30
  47.9 2.7 %collective-permute-start.19 = (bf16[128,128]{1,0:T(8,128)(2,1)S(1)}, bf16[128,128]{1,0:T(8,128)(2,1)S(1)}, u32[]{:S(2)}, u32[]{:S(2)}) collective-permute-start(bf16[128,128]{1,0:T(8,128)(2,1)S(1)} %add_convert_fusion), channel_id=1, source_target_pairs={{0,0},{1,32},{2,2},{3,34},{4,4},{5,36},{6,6},{7,38},{8,8},{9,40},{... | collective-permute-start | bytes 98312 | tf_op jit(solution)/shard_map/ppermute | solution.py:30
  50.6 1.4 %precondition.3 = f32[128,128]{1,0:T(8,128)S(1)} custom-call(s32[4]{0:T(128)S(1)} %pad_add_fusion.where, bf16[4,4,64,128]{3,2,1,0:T(8,128)(2,1)S(1)} %pad_maximum_fusion.2.p0, bf16[4,4,64,128]{3,2,1,0:T(8,128)(2,1)S(1)} %collective-permute-done.10.p1, bf16[4,4,64,128]{3,2,1,0:T(8,128)(2,1)S(1)} %collective-permute-done.11.p2, ...), custom_call_target="tpu_custom_call" | custom-call | tf_op jit(solution)/shard_map/precondition/pallas_call | solution.py:180
  52.2 1.2 %collective-permute-done.14 = f32[128,128]{1,0:T(8,128)S(1)} collective-permute-done((f32[128,128]{1,0:T(8,128)S(1)}, f32[128,128]{1,0:T(8,128)S(1)}, u32[]{:S(2)}, u32[]{:S(2)}) %collective-permute-start.14) | collective-permute-done | bytes 65568 | tf_op jit(solution)/shard_map/ppermute | solution.py:30
  53.4 5.4 %collective-permute-start.15 = (bf16[128,128]{1,0:T(8,128)(2,1)S(1)}, bf16[128,128]{1,0:T(8,128)(2,1)S(1)}, u32[]{:S(2)}, u32[]{:S(2)}) collective-permute-start(bf16[128,128]{1,0:T(8,128)(2,1)S(1)} %add_convert_fusion.1), channel_id=1, source_target_pairs={{0,128},{1,129},{2,130},{3,131},{4,132},{5,133},{6,134},{7,135},{8... | collective-permute-start | bytes 98312 | tf_op jit(solution)/shard_map/ppermute | solution.py:30
  58.8 1.5 %collective-permute-done.15 = bf16[128,128]{1,0:T(8,128)(2,1)S(1)} collective-permute-done((bf16[128,128]{1,0:T(8,128)(2,1)S(1)}, bf16[128,128]{1,0:T(8,128)(2,1)S(1)}, u32[]{:S(2)}, u32[]{:S(2)}) %collective-permute-start.15) | collective-permute-done | bytes 32800 | tf_op jit(solution)/shard_map/ppermute | solution.py:30
  61.6 2.4 %collective-permute-start.23 = (bf16[2,128,256]{2,1,0:T(8,128)(2,1)S(1)}, bf16[2,128,256]{2,1,0:T(8,128)(2,1)S(1)}, u32[]{:S(2)}, u32[]{:S(2)}) collective-permute-start(bf16[2,128,256]{2,1,0:T(8,128)(2,1)S(1)} %get-tuple-element.32), channel_id=1, source_target_pairs={{0,8},{1,3},{2,10},{3,1},{4,12},{5,7},{6,14},{7,5},{8,0},{9,11},{1... | collective-permute-start | bytes 393224 | tf_op jit(solution)/shard_map/ppermute | solution.py:30
  64.0 2.0 %collective-permute-start.17 = (bf16[2,128,256]{2,1,0:T(8,128)(2,1)S(1)}, bf16[2,128,256]{2,1,0:T(8,128)(2,1)S(1)}, u32[]{:S(2)}, u32[]{:S(2)}) collective-permute-start(bf16[2,128,256]{2,1,0:T(8,128)(2,1)S(1)} %pad_maximum_fusion.6), channel_id=1, source_target_pairs={{0,6},{1,25},{2,4},{3,27},{4,2},{5,29},{6,0},{7,31},{8,14},{9,17},... | collective-permute-start | bytes 393224 | tf_op jit(solution)/shard_map/ppermute | solution.py:30
  68.0 2.8 %collective-permute-done.17 = bf16[2,128,256]{2,1,0:T(8,128)(2,1)S(1)} collective-permute-done((bf16[2,128,256]{2,1,0:T(8,128)(2,1)S(1)}, bf16[2,128,256]{2,1,0:T(8,128)(2,1)S(1)}, u32[]{:S(2)}, u32[]{:S(2)}) %collective-permute-start.17) | collective-permute-done | bytes 131104 | tf_op jit(solution)/shard_map/ppermute | solution.py:30
  71.8 2.5 %collective-permute-start.27 = (bf16[128,1024]{1,0:T(8,128)(2,1)S(1)}, bf16[128,1024]{1,0:T(8,128)(2,1)S(1)}, u32[]{:S(2)}, u32[]{:S(2)}) collective-permute-start(bf16[128,1024]{1,0:T(8,128)(2,1)S(1)} %get-tuple-element.15), channel_id=1, source_target_pairs={{0,4},{1,17},{2,6},{3,19},{4,0},{5,21},{6,2},{7,23},{8,12},{9,25},... | collective-permute-start | bytes 786440 | tf_op jit(solution)/shard_map/ppermute | solution.py:30
  74.3 1.4 %collective-permute-start.28 = (bf16[128,1024]{1,0:T(8,128)(2,1)S(1)}, bf16[128,1024]{1,0:T(8,128)(2,1)S(1)}, u32[]{:S(2)}, u32[]{:S(2)}) collective-permute-start(bf16[128,1024]{1,0:T(8,128)(2,1)S(1)} %get-tuple-element.16), channel_id=1, source_target_pairs={{0,6},{1,25},{2,4},{3,27},{4,2},{5,29},{6,0},{7,31},{8,14},{9,17},... | collective-permute-start | bytes 786440 | tf_op jit(solution)/shard_map/ppermute | solution.py:30
  75.6 1.6 %collective-permute-done.26 = bf16[128,1024]{1,0:T(8,128)(2,1)S(1)} collective-permute-done((bf16[128,1024]{1,0:T(8,128)(2,1)S(1)}, bf16[128,1024]{1,0:T(8,128)(2,1)S(1)}, u32[]{:S(2)}, u32[]{:S(2)}) %collective-permute-start.26) | collective-permute-done | bytes 262176 | tf_op jit(solution)/shard_map/ppermute | solution.py:30
  77.3 2.5 %collective-permute-start.29 = (bf16[2,64,1024]{2,1,0:T(8,128)(2,1)S(1)}, bf16[2,64,1024]{2,1,0:T(8,128)(2,1)S(1)}, u32[]{:S(2)}, u32[]{:S(2)}) collective-permute-start(bf16[2,64,1024]{2,1,0:T(8,128)(2,1)S(1)} %pad_maximum_fusion.4), channel_id=1, source_target_pairs={{0,1},{1,0},{2,3},{3,2},{4,5},{5,4},{6,7},{7,6},{8,9},{9,8},{10,11... | collective-permute-start | bytes 786440 | tf_op jit(solution)/shard_map/ppermute | solution.py:30
  79.9 1.3 %collective-permute-done.27 = bf16[128,1024]{1,0:T(8,128)(2,1)S(1)} collective-permute-done((bf16[128,1024]{1,0:T(8,128)(2,1)S(1)}, bf16[128,1024]{1,0:T(8,128)(2,1)S(1)}, u32[]{:S(2)}, u32[]{:S(2)}) %collective-permute-start.27) | collective-permute-done | bytes 262176 | tf_op jit(solution)/shard_map/ppermute | solution.py:30
  81.2 2.4 %collective-permute-start.30 = (bf16[64,1024]{1,0:T(8,128)(2,1)S(1)}, bf16[64,1024]{1,0:T(8,128)(2,1)S(1)}, u32[]{:S(2)}, u32[]{:S(2)}) collective-permute-start(bf16[64,1024]{1,0:T(8,128)(2,1)S(1)} %get-tuple-element.23), channel_id=1, source_target_pairs={{0,1},{1,0},{2,3},{3,2},{4,5},{5,4},{6,7},{7,6},{8,9},{9,8},{10,11... | collective-permute-start | bytes 393224 | tf_op jit(solution)/shard_map/ppermute | solution.py:30
  83.8 2.5 %collective-permute-start.31 = (bf16[64,1024]{1,0:T(8,128)(2,1)S(1)}, bf16[64,1024]{1,0:T(8,128)(2,1)S(1)}, u32[]{:S(2)}, u32[]{:S(2)}) collective-permute-start(bf16[64,1024]{1,0:T(8,128)(2,1)S(1)} %get-tuple-element.21), channel_id=1, source_target_pairs={{0,1},{1,0},{2,3},{3,2},{4,5},{5,4},{6,7},{7,6},{8,9},{9,8},{10,11... | collective-permute-start | bytes 393224 | tf_op jit(solution)/shard_map/ppermute | solution.py:30
  87.3 2.1 %assemble.1 = f32[64,8192]{1,0:T(8,128)} custom-call(s32[4]{0:T(128)S(1)} %pad_add_fusion.where, bf16[64,1024]{1,0:T(8,128)(2,1)S(1)} %get-tuple-element.28.refs_0_, bf16[64,1024]{1,0:T(8,128)(2,1)S(1)} %get-tuple-element.30.refs_1_, bf16[64,1024]{1,0:T(8,128)(2,1)S(1)} %get-tuple-element.24.refs_2_, bf16[64,1024]{1,0:T(8,128)(2,1)S(1)} %get-tuple-element.22.refs_3_, ...), custom_call_target="tpu_custom_call" | custom-call | tf_op jit(solution)/shard_map/assemble/pallas_call | solution.py:210
  (66 shorter events, 10.1 us)
Async XLA Ops:
  0.8 7.7 %collective-permute-start.2 = (bf16[2,64,128]{2,1,0:T(8,128)(2,1)S(1)}, bf16[2,64,128]{2,1,0:T(8,128)(2,1)S(1)}, u32[]{:S(2)}, u32[]{:S(2)}) collective-permute-start(bf16[2,64,128]{2,1,0:T(8,128)(2,1)S(1)} %get-tuple-element.44), channel_id=1, source_target_pairs={{0,96},{1,97},{2,98},{3,99},{4,100},{5,101},{6,102},{7,103},{8,104... | collective-permute-start | bytes 98312 | tf_op jit(solution)/shard_map/ppermute | solution.py:30
  6.0 4.0 %collective-permute-start.1 = (bf16[2,64,128]{2,1,0:T(8,128)(2,1)S(1)}, bf16[2,64,128]{2,1,0:T(8,128)(2,1)S(1)}, u32[]{:S(2)}, u32[]{:S(2)}) collective-permute-start(bf16[2,64,128]{2,1,0:T(8,128)(2,1)S(1)} %get-tuple-element.44), channel_id=1, source_target_pairs={{0,64},{1,65},{2,66},{3,67},{4,68},{5,69},{6,70},{7,71},{8,72},{9,... | collective-permute-start | bytes 98312 | tf_op jit(solution)/shard_map/ppermute | solution.py:30
  6.0 4.0 %collective-permute-start = (bf16[2,64,128]{2,1,0:T(8,128)(2,1)S(1)}, bf16[2,64,128]{2,1,0:T(8,128)(2,1)S(1)}, u32[]{:S(2)}, u32[]{:S(2)}) collective-permute-start(bf16[2,64,128]{2,1,0:T(8,128)(2,1)S(1)} %get-tuple-element.44), channel_id=1, source_target_pairs={{0,32},{1,33},{2,34},{3,35},{4,36},{5,37},{6,38},{7,39},{8,40},{9,... | collective-permute-start | bytes 98312 | tf_op jit(solution)/shard_map/ppermute | solution.py:30
  6.4 16.0 %collective-permute-start.9 = (bf16[64,8192]{1,0:T(8,128)(2,1)}, bf16[64,8192]{1,0:T(8,128)(2,1)S(1)}, u32[]{:S(2)}, u32[]{:S(2)}) collective-permute-start(bf16[64,8192]{1,0:T(8,128)(2,1)} %param.6), channel_id=1, source_target_pairs={{0,1},{1,0},{2,3},{3,2},{4,5},{5,4},{6,7},{7,6},{8,9},{9,8},{10,11... | collective-permute-start | bytes 3145736 | tf_op jit(solution)/shard_map/ppermute | solution.py:30
  8.5 36.4 %collective-permute-start.13 = (bf16[64,8192]{1,0:T(8,128)(2,1)}, bf16[64,8192]{1,0:T(8,128)(2,1)S(1)}, u32[]{:S(2)}, u32[]{:S(2)}) collective-permute-start(bf16[64,8192]{1,0:T(8,128)(2,1)} %param.7), channel_id=1, source_target_pairs={{0,1},{1,0},{2,3},{3,2},{4,5},{5,4},{6,7},{7,6},{8,9},{9,8},{10,11... | collective-permute-start | bytes 3145736 | tf_op jit(solution)/shard_map/ppermute | solution.py:30
  10.1 5.9 %collective-permute-start.5 = (bf16[4,2,64,128]{3,2,0,1:T(8,128)(2,1)S(1)}, bf16[4,2,64,128]{3,2,0,1:T(8,128)(2,1)S(1)}, u32[]{:S(2)}, u32[]{:S(2)}) collective-permute-start(bf16[4,2,64,128]{3,2,0,1:T(8,128)(2,1)S(1)} %pad_maximum_fusion.5), channel_id=1, source_target_pairs={{0,24},{1,7},{2,26},{3,5},{4,28},{5,3},{6,30},{7,1},{8,16},{9,15},... | collective-permute-start | bytes 393224 | tf_op jit(solution)/shard_map/ppermute | solution.py:30
  12.6 5.3 %collective-permute-start.4 = (bf16[4,2,64,128]{3,2,0,1:T(8,128)(2,1)S(1)}, bf16[4,2,64,128]{3,2,0,1:T(8,128)(2,1)S(1)}, u32[]{:S(2)}, u32[]{:S(2)}) collective-permute-start(bf16[4,2,64,128]{3,2,0,1:T(8,128)(2,1)S(1)} %pad_maximum_fusion.5), channel_id=1, source_target_pairs={{0,16},{1,5},{2,18},{3,7},{4,20},{5,1},{6,22},{7,3},{8,24},{9,13},... | collective-permute-start | bytes 393224 | tf_op jit(solution)/shard_map/ppermute | solution.py:30
  13.2 4.8 %collective-permute-start.3 = (bf16[4,2,64,128]{3,2,0,1:T(8,128)(2,1)S(1)}, bf16[4,2,64,128]{3,2,0,1:T(8,128)(2,1)S(1)}, u32[]{:S(2)}, u32[]{:S(2)}) collective-permute-start(bf16[4,2,64,128]{3,2,0,1:T(8,128)(2,1)S(1)} %pad_maximum_fusion.5), channel_id=1, source_target_pairs={{0,8},{1,3},{2,10},{3,1},{4,12},{5,7},{6,14},{7,5},{8,0},{9,11},{1... | collective-permute-start | bytes 393224 | tf_op jit(solution)/shard_map/ppermute | solution.py:30
  18.0 5.3 %collective-permute-start.6 = (bf16[4,4,64,128]{3,2,1,0:T(8,128)(2,1)S(1)}, bf16[4,4,64,128]{3,2,1,0:T(8,128)(2,1)S(1)}, u32[]{:S(2)}, u32[]{:S(2)}) collective-permute-start(bf16[4,4,64,128]{3,2,1,0:T(8,128)(2,1)S(1)} %pad_maximum_fusion.1.p0), channel_id=1, source_target_pairs={{0,2},{1,9},{2,0},{3,11},{4,6},{5,13},{6,4},{7,15},{8,10},{9,1},{1... | collective-permute-start | bytes 786440 | tf_op jit(solution)/shard_map/ppermute | solution.py:30
  19.4 9.6 %collective-permute-start.7 = (bf16[4,4,64,128]{3,2,1,0:T(8,128)(2,1)S(1)}, bf16[4,4,64,128]{3,2,1,0:T(8,128)(2,1)S(1)}, u32[]{:S(2)}, u32[]{:S(2)}) collective-permute-start(bf16[4,4,64,128]{3,2,1,0:T(8,128)(2,1)S(1)} %pad_maximum_fusion.1.p0), channel_id=1, source_target_pairs={{0,4},{1,17},{2,6},{3,19},{4,0},{5,21},{6,2},{7,23},{8,12},{9,25},... | collective-permute-start | bytes 786440 | tf_op jit(solution)/shard_map/ppermute | solution.py:30
  22.3 9.5 %collective-permute-start.8 = (bf16[4,4,64,128]{3,2,1,0:T(8,128)(2,1)S(1)}, bf16[4,4,64,128]{3,2,1,0:T(8,128)(2,1)S(1)}, u32[]{:S(2)}, u32[]{:S(2)}) collective-permute-start(bf16[4,4,64,128]{3,2,1,0:T(8,128)(2,1)S(1)} %pad_maximum_fusion.1.p0), channel_id=1, source_target_pairs={{0,6},{1,25},{2,4},{3,27},{4,2},{5,29},{6,0},{7,31},{8,14},{9,17},... | collective-permute-start | bytes 786440 | tf_op jit(solution)/shard_map/ppermute | solution.py:30
  33.3 7.8 %collective-permute-start.18 = (f32[128,128]{1,0:T(8,128)S(1)}, f32[128,128]{1,0:T(8,128)S(1)}, u32[]{:S(2)}, u32[]{:S(2)}) collective-permute-start(f32[128,128]{1,0:T(8,128)S(1)} %precondition.2), channel_id=1, source_target_pairs={{0,1},{1,0},{2,3},{3,2},{4,5},{5,4},{6,7},{7,6},{8,9},{9,8},{10,11... | collective-permute-start | bytes 196616 | tf_op jit(solution)/shard_map/ppermute | solution.py:30
  37.2 10.0 %collective-permute-start.10 = (bf16[4,4,64,128]{3,2,1,0:T(8,128)(2,1)S(1)}, bf16[4,4,64,128]{3,2,1,0:T(8,128)(2,1)S(1)}, u32[]{:S(2)}, u32[]{:S(2)}) collective-permute-start(bf16[4,4,64,128]{3,2,1,0:T(8,128)(2,1)S(1)} %pad_maximum_fusion.2.p0), channel_id=1, source_target_pairs={{0,2},{1,9},{2,0},{3,11},{4,6},{5,13},{6,4},{7,15},{8,10},{9,1},{1... | collective-permute-start | bytes 786440 | tf_op jit(solution)/shard_map/ppermute | solution.py:30
  37.5 10.4 %collective-permute-start.11 = (bf16[4,4,64,128]{3,2,1,0:T(8,128)(2,1)S(1)}, bf16[4,4,64,128]{3,2,1,0:T(8,128)(2,1)S(1)}, u32[]{:S(2)}, u32[]{:S(2)}) collective-permute-start(bf16[4,4,64,128]{3,2,1,0:T(8,128)(2,1)S(1)} %pad_maximum_fusion.2.p0), channel_id=1, source_target_pairs={{0,4},{1,17},{2,6},{3,19},{4,0},{5,21},{6,2},{7,23},{8,12},{9,25},... | collective-permute-start | bytes 786440 | tf_op jit(solution)/shard_map/ppermute | solution.py:30
  40.1 10.5 %collective-permute-start.12 = (bf16[4,4,64,128]{3,2,1,0:T(8,128)(2,1)S(1)}, bf16[4,4,64,128]{3,2,1,0:T(8,128)(2,1)S(1)}, u32[]{:S(2)}, u32[]{:S(2)}) collective-permute-start(bf16[4,4,64,128]{3,2,1,0:T(8,128)(2,1)S(1)} %pad_maximum_fusion.2.p0), channel_id=1, source_target_pairs={{0,6},{1,25},{2,4},{3,27},{4,2},{5,29},{6,0},{7,31},{8,14},{9,17},... | collective-permute-start | bytes 786440 | tf_op jit(solution)/shard_map/ppermute | solution.py:30
  41.1 11.0 %collective-permute-start.22 = (bf16[128,128]{1,0:T(8,128)(2,1)S(1)}, bf16[128,128]{1,0:T(8,128)(2,1)S(1)}, u32[]{:S(2)}, u32[]{:S(2)}) collective-permute-start(bf16[128,128]{1,0:T(8,128)(2,1)S(1)} %add_convert_fusion), channel_id=1, source_target_pairs={{0,192},{1,224},{2,194},{3,226},{4,196},{5,228},{6,198},{7,230},{8... | collective-permute-start | bytes 98312 | tf_op jit(solution)/shard_map/ppermute | solution.py:30
  44.9 7.3 %collective-permute-start.21 = (bf16[128,128]{1,0:T(8,128)(2,1)S(1)}, bf16[128,128]{1,0:T(8,128)(2,1)S(1)}, u32[]{:S(2)}, u32[]{:S(2)}) collective-permute-start(bf16[128,128]{1,0:T(8,128)(2,1)S(1)} %add_convert_fusion), channel_id=1, source_target_pairs={{0,64},{1,96},{2,66},{3,98},{4,68},{5,100},{6,70},{7,102},{8,72},{... | collective-permute-start | bytes 98312 | tf_op jit(solution)/shard_map/ppermute | solution.py:30
  47.3 11.5 %collective-permute-start.20 = (bf16[128,128]{1,0:T(8,128)(2,1)S(1)}, bf16[128,128]{1,0:T(8,128)(2,1)S(1)}, u32[]{:S(2)}, u32[]{:S(2)}) collective-permute-start(bf16[128,128]{1,0:T(8,128)(2,1)S(1)} %add_convert_fusion), channel_id=1, source_target_pairs={{0,128},{1,160},{2,130},{3,162},{4,132},{5,164},{6,134},{7,166},{8... | collective-permute-start | bytes 98312 | tf_op jit(solution)/shard_map/ppermute | solution.py:30
  47.9 10.9 %collective-permute-start.19 = (bf16[128,128]{1,0:T(8,128)(2,1)S(1)}, bf16[128,128]{1,0:T(8,128)(2,1)S(1)}, u32[]{:S(2)}, u32[]{:S(2)}) collective-permute-start(bf16[128,128]{1,0:T(8,128)(2,1)S(1)} %add_convert_fusion), channel_id=1, source_target_pairs={{0,0},{1,32},{2,2},{3,34},{4,4},{5,36},{6,6},{7,38},{8,8},{9,40},{... | collective-permute-start | bytes 98312 | tf_op jit(solution)/shard_map/ppermute | solution.py:30
  52.0 1.3 %collective-permute-start.14 = (f32[128,128]{1,0:T(8,128)S(1)}, f32[128,128]{1,0:T(8,128)S(1)}, u32[]{:S(2)}, u32[]{:S(2)}) collective-permute-start(f32[128,128]{1,0:T(8,128)S(1)} %precondition.3), channel_id=1, source_target_pairs={{0,1},{1,0},{2,3},{3,2},{4,5},{5,4},{6,7},{7,6},{8,9},{9,8},{10,11... | collective-permute-start | bytes 196616 | tf_op jit(solution)/shard_map/ppermute | solution.py:30
  53.4 6.9 %collective-permute-start.15 = (bf16[128,128]{1,0:T(8,128)(2,1)S(1)}, bf16[128,128]{1,0:T(8,128)(2,1)S(1)}, u32[]{:S(2)}, u32[]{:S(2)}) collective-permute-start(bf16[128,128]{1,0:T(8,128)(2,1)S(1)} %add_convert_fusion.1), channel_id=1, source_target_pairs={{0,128},{1,129},{2,130},{3,131},{4,132},{5,133},{6,134},{7,135},{8... | collective-permute-start | bytes 98312 | tf_op jit(solution)/shard_map/ppermute | solution.py:30
  60.3 3.7 %collective-permute-start.16 = (bf16[128,256]{1,0:T(8,128)(2,1)S(1)}, bf16[128,256]{1,0:T(8,128)(2,1)S(1)}, u32[]{:S(2)}, u32[]{:S(2)}) collective-permute-start(bf16[128,256]{1,0:T(8,128)(2,1)S(1)} %get-tuple-element.42), channel_id=1, source_target_pairs={{0,2},{1,9},{2,0},{3,11},{4,6},{5,13},{6,4},{7,15},{8,10},{9,1},{1... | collective-permute-start | bytes 196616 | tf_op jit(solution)/shard_map/ppermute | solution.py:30
  60.6 5.8 %collective-permute-start.25 = (bf16[2,128,256]{2,1,0:T(8,128)(2,1)S(1)}, bf16[2,128,256]{2,1,0:T(8,128)(2,1)S(1)}, u32[]{:S(2)}, u32[]{:S(2)}) collective-permute-start(bf16[2,128,256]{2,1,0:T(8,128)(2,1)S(1)} %get-tuple-element.32), channel_id=1, source_target_pairs={{0,24},{1,7},{2,26},{3,5},{4,28},{5,3},{6,30},{7,1},{8,16},{9,15},... | collective-permute-start | bytes 393224 | tf_op jit(solution)/shard_map/ppermute | solution.py:30
  61.4 5.8 %collective-permute-start.24 = (bf16[2,128,256]{2,1,0:T(8,128)(2,1)S(1)}, bf16[2,128,256]{2,1,0:T(8,128)(2,1)S(1)}, u32[]{:S(2)}, u32[]{:S(2)}) collective-permute-start(bf16[2,128,256]{2,1,0:T(8,128)(2,1)S(1)} %get-tuple-element.32), channel_id=1, source_target_pairs={{0,16},{1,5},{2,18},{3,7},{4,20},{5,1},{6,22},{7,3},{8,24},{9,13},... | collective-permute-start | bytes 393224 | tf_op jit(solution)/shard_map/ppermute | solution.py:30
  61.6 6.4 %collective-permute-start.23 = (bf16[2,128,256]{2,1,0:T(8,128)(2,1)S(1)}, bf16[2,128,256]{2,1,0:T(8,128)(2,1)S(1)}, u32[]{:S(2)}, u32[]{:S(2)}) collective-permute-start(bf16[2,128,256]{2,1,0:T(8,128)(2,1)S(1)} %get-tuple-element.32), channel_id=1, source_target_pairs={{0,8},{1,3},{2,10},{3,1},{4,12},{5,7},{6,14},{7,5},{8,0},{9,11},{1... | collective-permute-start | bytes 393224 | tf_op jit(solution)/shard_map/ppermute | solution.py:30
  64.0 6.8 %collective-permute-start.17 = (bf16[2,128,256]{2,1,0:T(8,128)(2,1)S(1)}, bf16[2,128,256]{2,1,0:T(8,128)(2,1)S(1)}, u32[]{:S(2)}, u32[]{:S(2)}) collective-permute-start(bf16[2,128,256]{2,1,0:T(8,128)(2,1)S(1)} %pad_maximum_fusion.6), channel_id=1, source_target_pairs={{0,6},{1,25},{2,4},{3,27},{4,2},{5,29},{6,0},{7,31},{8,14},{9,17},... | collective-permute-start | bytes 393224 | tf_op jit(solution)/shard_map/ppermute | solution.py:30
  71.7 5.6 %collective-permute-start.26 = (bf16[128,1024]{1,0:T(8,128)(2,1)S(1)}, bf16[128,1024]{1,0:T(8,128)(2,1)S(1)}, u32[]{:S(2)}, u32[]{:S(2)}) collective-permute-start(bf16[128,1024]{1,0:T(8,128)(2,1)S(1)} %get-tuple-element.14), channel_id=1, source_target_pairs={{0,2},{1,9},{2,0},{3,11},{4,6},{5,13},{6,4},{7,15},{8,10},{9,1},{1... | collective-permute-start | bytes 786440 | tf_op jit(solution)/shard_map/ppermute | solution.py:30
  71.8 9.4 %collective-permute-start.27 = (bf16[128,1024]{1,0:T(8,128)(2,1)S(1)}, bf16[128,1024]{1,0:T(8,128)(2,1)S(1)}, u32[]{:S(2)}, u32[]{:S(2)}) collective-permute-start(bf16[128,1024]{1,0:T(8,128)(2,1)S(1)} %get-tuple-element.15), channel_id=1, source_target_pairs={{0,4},{1,17},{2,6},{3,19},{4,0},{5,21},{6,2},{7,23},{8,12},{9,25},... | collective-permute-start | bytes 786440 | tf_op jit(solution)/shard_map/ppermute | solution.py:30
  74.3 9.5 %collective-permute-start.28 = (bf16[128,1024]{1,0:T(8,128)(2,1)S(1)}, bf16[128,1024]{1,0:T(8,128)(2,1)S(1)}, u32[]{:S(2)}, u32[]{:S(2)}) collective-permute-start(bf16[128,1024]{1,0:T(8,128)(2,1)S(1)} %get-tuple-element.16), channel_id=1, source_target_pairs={{0,6},{1,25},{2,4},{3,27},{4,2},{5,29},{6,0},{7,31},{8,14},{9,17},... | collective-permute-start | bytes 786440 | tf_op jit(solution)/shard_map/ppermute | solution.py:30
  77.3 8.9 %collective-permute-start.29 = (bf16[2,64,1024]{2,1,0:T(8,128)(2,1)S(1)}, bf16[2,64,1024]{2,1,0:T(8,128)(2,1)S(1)}, u32[]{:S(2)}, u32[]{:S(2)}) collective-permute-start(bf16[2,64,1024]{2,1,0:T(8,128)(2,1)S(1)} %pad_maximum_fusion.4), channel_id=1, source_target_pairs={{0,1},{1,0},{2,3},{3,2},{4,5},{5,4},{6,7},{7,6},{8,9},{9,8},{10,11... | collective-permute-start | bytes 786440 | tf_op jit(solution)/shard_map/ppermute | solution.py:30
  81.2 5.1 %collective-permute-start.30 = (bf16[64,1024]{1,0:T(8,128)(2,1)S(1)}, bf16[64,1024]{1,0:T(8,128)(2,1)S(1)}, u32[]{:S(2)}, u32[]{:S(2)}) collective-permute-start(bf16[64,1024]{1,0:T(8,128)(2,1)S(1)} %get-tuple-element.23), channel_id=1, source_target_pairs={{0,1},{1,0},{2,3},{3,2},{4,5},{5,4},{6,7},{7,6},{8,9},{9,8},{10,11... | collective-permute-start | bytes 393224 | tf_op jit(solution)/shard_map/ppermute | solution.py:30
  83.8 3.4 %collective-permute-start.31 = (bf16[64,1024]{1,0:T(8,128)(2,1)S(1)}, bf16[64,1024]{1,0:T(8,128)(2,1)S(1)}, u32[]{:S(2)}, u32[]{:S(2)}) collective-permute-start(bf16[64,1024]{1,0:T(8,128)(2,1)S(1)} %get-tuple-element.21), channel_id=1, source_target_pairs={{0,1},{1,0},{2,3},{3,2},{4,5},{5,4},{6,7},{7,6},{8,9},{9,8},{10,11... | collective-permute-start | bytes 393224 | tf_op jit(solution)/shard_map/ppermute | solution.py:30
  (2 other events, 46.8 us)

commit v9 on v8

--- a/solution.py
+++ b/solution.py
@@ -103,19 +103,16 @@
     pre[...] = total
 
 
-def tiles(g, plane, *made):
-    x = plane[...].reshape(1024, 256)
-    for k, e in enumerate(made):
-        part = lax.dot_general(
-            g[k ^ (k >> 1)],
-            x,
-            (((1,), (1,)), ((), ())),
-            preferred_element_type=jnp.float32,
-        )
-        e[...] = (part * (1.0 / TOKENS)).astype(e.dtype)
-
-
-FIRST = 1
+def tile(where, g, piece, keep, give):
+    part = lax.dot_general(
+        g[...],
+        piece[...].reshape(1024, 256),
+        (((1,), (1,)), ((), ())),
+        preferred_element_type=jnp.float32,
+    ) * (1.0 / TOKENS)
+    low, high = part[:64], part[64:]
+    keep[...] = jnp.where(where[3] == 0, low, high)
+    give[...] = jnp.where(where[3] == 0, high, low)
 
 
 def assemble(where, *refs):
@@ -134,7 +131,7 @@
     for i in range(4):
         rows = slice(i * 16, i * 16 + 16)
         for piece, b, at in places:
-            wide[rows, pl.ds(at, 128)] = piece[rows, b : b + 128].astype(jnp.float32)
+            wide[rows, pl.ds(at, 128)] = piece[rows, b : b + 128]
         copies.append(pltpu.make_async_copy(wide.at[rows], out.at[rows], sems.at[i]))
         copies[-1].start()
     for copy in copies:
@@ -185,28 +182,25 @@
     part = partial(turned(second_turn, [act_plane] * 4), act_rows)
     part, grad_plane = lax.optimization_barrier((part, grad_plane))
     act = (part + swap_cores(part)).astype(bf16)
-    part = partial(turned(second_turn, [grad_plane] * 4), grad_rows)
-    grad = (part + swap_cores(part)).astype(bf16)
+    grad_pieces = turned(second_turn, [grad_plane] * 4)
 
     here = [to_parity(act, j, 0) for j in (0, 1)]
     there = [to_parity(act, j, 1) for j in (0, 1)]
     pair = jnp.stack([jnp.concatenate(p, axis=1) for p in zip(here, there)])
+    pair, *grad_pieces = lax.optimization_barrier((pair, *grad_pieces))
+    part = partial(grad_pieces, grad_rows)
+    grad = (part + swap_cores(part)).astype(bf16)
     grad = jnp.concatenate([grad, swap_reps(grad)], axis=1)
 
-    grads = jnp.stack([grad, second_turn(grad, 1)])
     plane = jnp.stack(turned(first_turn, [pair] * 4))
-    grads = jnp.concatenate([grads, second_turn(grads, 3)], axis=0)
-    made = call(tiles, "tiles", [shape((128, 1024), bf16)] * 4, [VMEM] * 2)(
-        grads, plane
-    )
-    whole = turned(second_turn, made)
-    own = [jnp.where(first, e[:64], e[64:]) for e in whole]
-    give = [jnp.where(first, e[64:], e[:64]) for e in whole]
-    one = swap_cores(jnp.stack([give[0], give[FIRST]]))
-    sibling = {0: one[0], FIRST: one[1]}
-    for k in (1, 2, 3):
-        if k != FIRST:
-            sibling[k] = swap_cores(give[k])
+    made = [
+        call(tile, "tile", [shape((64, 1024), f32)] * 2, [SMEM, VMEM, VMEM])(
+            where, grad, piece
+        )
+        for piece in turned(second_turn, [plane] * 4)
+    ]
+    own = [keep for keep, _ in made]
+    sibling = [swap_cores(give) for _, give in made]
     return pl.pallas_call(
         assemble,
         out_shape=shape((64, 8192), f32),
@@ -215,7 +209,7 @@
         scratch_shapes=[pltpu.VMEM((64, 8192), f32), pltpu.SemaphoreType.DMA((4,))],
         compiler_params=PARAMS,
         name="assemble",
-    )(where, *own, *(sibling[k] for k in range(4)))
+    )(where, *own, *sibling)
 
 
 def solution(mesh):

time: 89.7 us -> 90.8 us (1.012)
  starting transfers between devices: 54.7 us -> 49.4 us
  waiting for transfers between devices: 26.9 us -> 30.9 us
  Pallas kernels: 5.75 us -> 8.34 us
    ppermute x32 -> x31, starting transfers between devices: 54.7 us -> 49.4 us  [send(): return lax.ppermute(value, AXES, pairs)]
    ppermute x32 -> x31, waiting for transfers between devices: 26.9 us -> 30.9 us  [send(): return lax.ppermute(value, AXES, pairs)]
    pallas_call x1 -> x4, Pallas kernels: 0.81 us -> 3.39 us  [on_device(): call(tile, 'tile', [shape((64, 1024), f32)] * 2, [SMEM, VMEM, VMEM])]
  transfers between devices with their start and end apart: 32 -> 31, of which waited for: 16 -> 15; matrix products, arithmetic and copies ran while one was open for 1% -> 1% of each run, Pallas kernels for 3% -> 7%
where the time goes in v9:
time: 90.8 us; the launch traced here: 90.6 us
  starting transfers between devices  49.4 us (54%)
  waiting for transfers between devices  30.9 us (34%)
  Pallas kernels  8.34 us (9%)
  other arithmetic  1.54 us (2%)
    ppermute x31, starting transfers between devices, send(): return lax.ppermute(value, AXES, pairs)  49.4 us
    ppermute x31, waiting for transfers between devices, send(): return lax.ppermute(value, AXES, pairs)  30.9 us
    pallas_call x4, Pallas kernels, on_device(): call(tile, 'tile', [shape((64, 1024), f32)] * 2, [SMEM, VMEM, VMEM])  3.39 us
    pallas_call x2, Pallas kernels, partial(): call(precondition, 'precondition', shape((128, 128), f32), [SMEM] + [VMEM...  2.84 us
    pallas_call x1, Pallas kernels, on_device(): pl.pallas_call(assemble, out_shape=shape((64, 8192), f32), in_specs=[SMEM...  2.1 us
  transfers between devices with their start and end apart: 31, of which 15 were waited for; matrix products, arithmetic and copies ran while one was open for 1% of the time, Pallas kernels for 7%

profile of v9, /device:TPU:1, one launch (start us, length us, event | category | flops | bytes accessed | tf_op | source)
XLA Modules:
  0.0 90.6 jit_solution(4239000037401604668)
XLA Ops:
  0.8 5.2 %collective-permute-start.2 = (bf16[2,64,128]{2,1,0:T(8,128)(2,1)S(1)}, bf16[2,64,128]{2,1,0:T(8,128)(2,1)S(1)}, u32[]{:S(2)}, u32[]{:S(2)}) collective-permute-start(bf16[2,64,128]{2,1,0:T(8,128)(2,1)S(1)} %get-tuple-element.48), channel_id=1, source_target_pairs={{0,96},{1,97},{2,98},{3,99},{4,100},{5,101},{6,102},{7,103},{8,104... | collective-permute-start | bytes 98312 | tf_op jit(solution)/shard_map/ppermute | solution.py:30
  6.4 2.1 %collective-permute-start.9 = (bf16[64,8192]{1,0:T(8,128)(2,1)}, bf16[64,8192]{1,0:T(8,128)(2,1)S(1)}, u32[]{:S(2)}, u32[]{:S(2)}) collective-permute-start(bf16[64,8192]{1,0:T(8,128)(2,1)} %param.6), channel_id=1, source_target_pairs={{0,1},{1,0},{2,3},{3,2},{4,5},{5,4},{6,7},{7,6},{8,9},{9,8},{10,11... | collective-permute-start | bytes 3145736 | tf_op jit(solution)/shard_map/ppermute | solution.py:30
  8.5 1.5 %collective-permute-done.1 = bf16[2,64,128]{2,1,0:T(8,128)(2,1)S(1)} collective-permute-done((bf16[2,64,128]{2,1,0:T(8,128)(2,1)S(1)}, bf16[2,64,128]{2,1,0:T(8,128)(2,1)S(1)}, u32[]{:S(2)}, u32[]{:S(2)}) %collective-permute-start.1) | collective-permute-done | bytes 32800 | tf_op jit(solution)/shard_map/ppermute | solution.py:30
  10.1 2.6 %collective-permute-start.5 = (bf16[4,2,64,128]{3,2,0,1:T(8,128)(2,1)S(1)}, bf16[4,2,64,128]{3,2,0,1:T(8,128)(2,1)S(1)}, u32[]{:S(2)}, u32[]{:S(2)}) collective-permute-start(bf16[4,2,64,128]{3,2,0,1:T(8,128)(2,1)S(1)} %pad_maximum_fusion.3), channel_id=1, source_target_pairs={{0,24},{1,7},{2,26},{3,5},{4,28},{5,3},{6,30},{7,1},{8,16},{9,15},... | collective-permute-start | bytes 393224 | tf_op jit(solution)/shard_map/ppermute | solution.py:30
  13.4 2.5 %collective-permute-done.5 = bf16[4,2,64,128]{3,2,0,1:T(8,128)(2,1)S(1)} collective-permute-done((bf16[4,2,64,128]{3,2,0,1:T(8,128)(2,1)S(1)}, bf16[4,2,64,128]{3,2,0,1:T(8,128)(2,1)S(1)}, u32[]{:S(2)}, u32[]{:S(2)}) %collective-permute-start.5) | collective-permute-done | bytes 131104 | tf_op jit(solution)/shard_map/ppermute | solution.py:30
  16.0 2.0 %collective-permute-done.4 = bf16[4,2,64,128]{3,2,0,1:T(8,128)(2,1)S(1)} collective-permute-done((bf16[4,2,64,128]{3,2,0,1:T(8,128)(2,1)S(1)}, bf16[4,2,64,128]{3,2,0,1:T(8,128)(2,1)S(1)}, u32[]{:S(2)}, u32[]{:S(2)}) %collective-permute-start.4) | collective-permute-done | bytes 131104 | tf_op jit(solution)/shard_map/ppermute | solution.py:30
  18.0 1.4 %collective-permute-start.6 = (bf16[4,4,64,128]{3,2,1,0:T(8,128)(2,1)S(1)}, bf16[4,4,64,128]{3,2,1,0:T(8,128)(2,1)S(1)}, u32[]{:S(2)}, u32[]{:S(2)}) collective-permute-start(bf16[4,4,64,128]{3,2,1,0:T(8,128)(2,1)S(1)} %pad_maximum_fusion.1.p0), channel_id=1, source_target_pairs={{0,2},{1,9},{2,0},{3,11},{4,6},{5,13},{6,4},{7,15},{8,10},{9,1},{1... | collective-permute-start | bytes 786440 | tf_op jit(solution)/shard_map/ppermute | solution.py:30
  19.4 2.9 %collective-permute-start.7 = (bf16[4,4,64,128]{3,2,1,0:T(8,128)(2,1)S(1)}, bf16[4,4,64,128]{3,2,1,0:T(8,128)(2,1)S(1)}, u32[]{:S(2)}, u32[]{:S(2)}) collective-permute-start(bf16[4,4,64,128]{3,2,1,0:T(8,128)(2,1)S(1)} %pad_maximum_fusion.1.p0), channel_id=1, source_target_pairs={{0,4},{1,17},{2,6},{3,19},{4,0},{5,21},{6,2},{7,23},{8,12},{9,25},... | collective-permute-start | bytes 786440 | tf_op jit(solution)/shard_map/ppermute | solution.py:30
  23.4 5.6 %collective-permute-done.7.p2 = bf16[4,4,64,128]{3,2,1,0:T(8,128)(2,1)S(1)} collective-permute-done((bf16[4,4,64,128]{3,2,1,0:T(8,128)(2,1)S(1)}, bf16[4,4,64,128]{3,2,1,0:T(8,128)(2,1)S(1)}, u32[]{:S(2)}, u32[]{:S(2)}) %collective-permute-start.7) | collective-permute-done | bytes 262176 | tf_op jit(solution)/shard_map/ppermute | solution.py:30
  29.0 2.9 %collective-permute-done.8.p3 = bf16[4,4,64,128]{3,2,1,0:T(8,128)(2,1)S(1)} collective-permute-done((bf16[4,4,64,128]{3,2,1,0:T(8,128)(2,1)S(1)}, bf16[4,4,64,128]{3,2,1,0:T(8,128)(2,1)S(1)}, u32[]{:S(2)}, u32[]{:S(2)}) %collective-permute-start.8) | collective-permute-done | bytes 262176 | tf_op jit(solution)/shard_map/ppermute | solution.py:30
  31.9 1.4 %precondition.2 = f32[128,128]{1,0:T(8,128)S(1)} custom-call(s32[4]{0:T(128)S(1)} %pad_add_fusion.where, bf16[4,4,64,128]{3,2,1,0:T(8,128)(2,1)S(1)} %pad_maximum_fusion.1.p0, bf16[4,4,64,128]{3,2,1,0:T(8,128)(2,1)S(1)} %collective-permute-done.6.p1, bf16[4,4,64,128]{3,2,1,0:T(8,128)(2,1)S(1)} %collective-permute-done.7.p2, ...), custom_call_target="tpu_custom_call" | custom-call | tf_op jit(solution)/shard_map/precondition/pallas_call | solution.py:177
  33.3 3.9 %collective-permute-start.10 = (f32[128,128]{1,0:T(8,128)S(1)}, f32[128,128]{1,0:T(8,128)S(1)}, u32[]{:S(2)}, u32[]{:S(2)}) collective-permute-start(f32[128,128]{1,0:T(8,128)S(1)} %precondition.2), channel_id=1, source_target_pairs={{0,1},{1,0},{2,3},{3,2},{4,5},{5,4},{6,7},{7,6},{8,9},{9,8},{10,11... | collective-permute-start | bytes 196616 | tf_op jit(solution)/shard_map/ppermute | solution.py:30
  37.2 0.9 collective-permute-done.10
  38.2 3.2 %collective-permute-start.14 = (bf16[128,128]{1,0:T(8,128)(2,1)S(1)}, bf16[128,128]{1,0:T(8,128)(2,1)S(1)}, u32[]{:S(2)}, u32[]{:S(2)}) collective-permute-start(bf16[128,128]{1,0:T(8,128)(2,1)S(1)} %add_convert_fusion.1), channel_id=1, source_target_pairs={{0,192},{1,224},{2,194},{3,226},{4,196},{5,228},{6,198},{7,230},{8... | collective-permute-start | bytes 98312 | tf_op jit(solution)/shard_map/ppermute | solution.py:30
  41.3 2.7 %collective-permute-start.13 = (bf16[128,128]{1,0:T(8,128)(2,1)S(1)}, bf16[128,128]{1,0:T(8,128)(2,1)S(1)}, u32[]{:S(2)}, u32[]{:S(2)}) collective-permute-start(bf16[128,128]{1,0:T(8,128)(2,1)S(1)} %add_convert_fusion.1), channel_id=1, source_target_pairs={{0,64},{1,96},{2,66},{3,98},{4,68},{5,100},{6,70},{7,102},{8,72},{... | collective-permute-start | bytes 98312 | tf_op jit(solution)/shard_map/ppermute | solution.py:30
  44.3 2.6 %collective-permute-start.16 = (bf16[4,4,64,128]{3,2,1,0:T(8,128)(2,1)S(1)}, bf16[4,4,64,128]{3,2,1,0:T(8,128)(2,1)S(1)}, u32[]{:S(2)}, u32[]{:S(2)}) collective-permute-start(bf16[4,4,64,128]{3,2,1,0:T(8,128)(2,1)S(1)} %pad_maximum_fusion.2.p0), channel_id=1, source_target_pairs={{0,4},{1,17},{2,6},{3,19},{4,0},{5,21},{6,2},{7,23},{8,12},{9,25},... | collective-permute-start | bytes 786440 | tf_op jit(solution)/shard_map/ppermute | solution.py:30
  46.9 1.2 %collective-permute-start.17 = (bf16[4,4,64,128]{3,2,1,0:T(8,128)(2,1)S(1)}, bf16[4,4,64,128]{3,2,1,0:T(8,128)(2,1)S(1)}, u32[]{:S(2)}, u32[]{:S(2)}) collective-permute-start(bf16[4,4,64,128]{3,2,1,0:T(8,128)(2,1)S(1)} %pad_maximum_fusion.2.p0), channel_id=1, source_target_pairs={{0,6},{1,25},{2,4},{3,27},{4,2},{5,29},{6,0},{7,31},{8,14},{9,17},... | collective-permute-start | bytes 786440 | tf_op jit(solution)/shard_map/ppermute | solution.py:30
  48.0 1.8 %collective-permute-done.12 = bf16[128,128]{1,0:T(8,128)(2,1)S(1)} collective-permute-done((bf16[128,128]{1,0:T(8,128)(2,1)S(1)}, bf16[128,128]{1,0:T(8,128)(2,1)S(1)}, u32[]{:S(2)}, u32[]{:S(2)}) %collective-permute-start.12) | collective-permute-done | bytes 32800 | tf_op jit(solution)/shard_map/ppermute | solution.py:30
  49.8 1.9 %collective-permute-start.11 = (bf16[128,128]{1,0:T(8,128)(2,1)S(1)}, bf16[128,128]{1,0:T(8,128)(2,1)S(1)}, u32[]{:S(2)}, u32[]{:S(2)}) collective-permute-start(bf16[128,128]{1,0:T(8,128)(2,1)S(1)} %add_convert_fusion.1), channel_id=1, source_target_pairs={{0,0},{1,32},{2,2},{3,34},{4,4},{5,36},{6,6},{7,38},{8,8},{9,40},{... | collective-permute-start | bytes 98312 | tf_op jit(solution)/shard_map/ppermute | solution.py:30
  51.7 3.9 %collective-permute-done.11 = bf16[128,128]{1,0:T(8,128)(2,1)S(1)} collective-permute-done((bf16[128,128]{1,0:T(8,128)(2,1)S(1)}, bf16[128,128]{1,0:T(8,128)(2,1)S(1)}, u32[]{:S(2)}, u32[]{:S(2)}) %collective-permute-start.11) | collective-permute-done | bytes 32800 | tf_op jit(solution)/shard_map/ppermute | solution.py:30
  57.1 2.6 %collective-permute-start.21 = (bf16[2,128,256]{2,1,0:T(8,128)(2,1)S(1)}, bf16[2,128,256]{2,1,0:T(8,128)(2,1)S(1)}, u32[]{:S(2)}, u32[]{:S(2)}) collective-permute-start(bf16[2,128,256]{2,1,0:T(8,128)(2,1)S(1)} %pad_maximum_fusion.4), channel_id=1, source_target_pairs={{0,8},{1,3},{2,10},{3,1},{4,12},{5,7},{6,14},{7,5},{8,0},{9,11},{1... | collective-permute-start | bytes 393224 | tf_op jit(solution)/shard_map/ppermute | solution.py:30
  59.7 3.2 %collective-permute-done.23 = bf16[2,128,256]{2,1,0:T(8,128)(2,1)S(1)} collective-permute-done((bf16[2,128,256]{2,1,0:T(8,128)(2,1)S(1)}, bf16[2,128,256]{2,1,0:T(8,128)(2,1)S(1)}, u32[]{:S(2)}, u32[]{:S(2)}) %collective-permute-start.23) | collective-permute-done | bytes 131104 | tf_op jit(solution)/shard_map/ppermute | solution.py:30
  63.9 2.4 %collective-permute-start.25 = (bf16[4,2,128,256]{3,2,1,0:T(8,128)(2,1)S(1)}, bf16[4,2,128,256]{3,2,1,0:T(8,128)(2,1)S(1)}, u32[]{:S(2)}, u32[]{:S(2)}) collective-permute-start(bf16[4,2,128,256]{3,2,1,0:T(8,128)(2,1)S(1)} %pad_maximum_fusion.piece), channel_id=1, source_target_pairs={{0,4},{1,17},{2,6},{3,19},{4,0},{5,21},{6,2},{7,23},{8,12},{9,25},... | collective-permute-start | bytes 1572872 | tf_op jit(solution)/shard_map/ppermute | solution.py:30
  66.3 1.5 %collective-permute-start.26 = (bf16[4,2,128,256]{3,2,1,0:T(8,128)(2,1)S(1)}, bf16[4,2,128,256]{3,2,1,0:T(8,128)(2,1)S(1)}, u32[]{:S(2)}, u32[]{:S(2)}) collective-permute-start(bf16[4,2,128,256]{3,2,1,0:T(8,128)(2,1)S(1)} %pad_maximum_fusion.piece), channel_id=1, source_target_pairs={{0,6},{1,25},{2,4},{3,27},{4,2},{5,29},{6,0},{7,31},{8,14},{9,17},... | collective-permute-start | bytes 1572872 | tf_op jit(solution)/shard_map/ppermute | solution.py:30
  68.0 1.4 %precondition.3 = f32[128,128]{1,0:T(8,128)S(1)} custom-call(s32[4]{0:T(128)S(1)} %pad_add_fusion.where, bf16[4,4,64,128]{3,2,1,0:T(8,128)(2,1)S(1)} %pad_maximum_fusion.2.p0, bf16[4,4,64,128]{3,2,1,0:T(8,128)(2,1)S(1)} %collective-permute-done.15.p1, bf16[4,4,64,128]{3,2,1,0:T(8,128)(2,1)S(1)} %collective-permute-done.16.p2, ...), custom_call_target="tpu_custom_call" | custom-call | tf_op jit(solution)/shard_map/precondition/pallas_call | solution.py:177
  69.4 2.7 %collective-permute-start.19 = (f32[128,128]{1,0:T(8,128)S(1)}, f32[128,128]{1,0:T(8,128)S(1)}, u32[]{:S(2)}, u32[]{:S(2)}) collective-permute-start(f32[128,128]{1,0:T(8,128)S(1)} %precondition.3), channel_id=1, source_target_pairs={{0,1},{1,0},{2,3},{3,2},{4,5},{5,4},{6,7},{7,6},{8,9},{9,8},{10,11... | collective-permute-start | bytes 196616 | tf_op jit(solution)/shard_map/ppermute | solution.py:30
  73.1 4.7 %collective-permute-start.20 = (bf16[128,128]{1,0:T(8,128)(2,1)S(1)}, bf16[128,128]{1,0:T(8,128)(2,1)S(1)}, u32[]{:S(2)}, u32[]{:S(2)}) collective-permute-start(bf16[128,128]{1,0:T(8,128)(2,1)S(1)} %add_convert_fusion), channel_id=1, source_target_pairs={{0,128},{1,129},{2,130},{3,131},{4,132},{5,133},{6,134},{7,135},{8... | collective-permute-start | bytes 98312 | tf_op jit(solution)/shard_map/ppermute | solution.py:30
  77.7 2.1 %collective-permute-done.20 = bf16[128,128]{1,0:T(8,128)(2,1)S(1)} collective-permute-done((bf16[128,128]{1,0:T(8,128)(2,1)S(1)}, bf16[128,128]{1,0:T(8,128)(2,1)S(1)}, u32[]{:S(2)}, u32[]{:S(2)}) %collective-permute-start.20) | collective-permute-done | bytes 32800 | tf_op jit(solution)/shard_map/ppermute | solution.py:30
  80.7 1.6 %collective-permute-start.27 = (f32[64,1024]{1,0:T(8,128)S(1)}, f32[64,1024]{1,0:T(8,128)S(1)}, u32[]{:S(2)}, u32[]{:S(2)}) collective-permute-start(f32[64,1024]{1,0:T(8,128)S(1)} %get-tuple-element.31), channel_id=1, source_target_pairs={{0,1},{1,0},{2,3},{3,2},{4,5},{5,4},{6,7},{7,6},{8,9},{9,8},{10,11... | collective-permute-start | bytes 786440 | tf_op jit(solution)/shard_map/ppermute | solution.py:30
  85.6 1.6 %collective-permute-start.30 = (f32[64,1024]{1,0:T(8,128)S(1)}, f32[64,1024]{1,0:T(8,128)S(1)}, u32[]{:S(2)}, u32[]{:S(2)}) collective-permute-start(f32[64,1024]{1,0:T(8,128)S(1)} %get-tuple-element.34), channel_id=1, source_target_pairs={{0,1},{1,0},{2,3},{3,2},{4,5},{5,4},{6,7},{7,6},{8,9},{9,8},{10,11... | collective-permute-start | bytes 786440 | tf_op jit(solution)/shard_map/ppermute | solution.py:30
  87.1 1.1 %collective-permute-done.30.refs_7_ = f32[64,1024]{1,0:T(8,128)S(1)} collective-permute-done((f32[64,1024]{1,0:T(8,128)S(1)}, f32[64,1024]{1,0:T(8,128)S(1)}, u32[]{:S(2)}, u32[]{:S(2)}) %collective-permute-start.30) | collective-permute-done | bytes 262176 | tf_op jit(solution)/shard_map/ppermute | solution.py:30
  88.3 2.1 %assemble.1 = f32[64,8192]{1,0:T(8,128)} custom-call(s32[4]{0:T(128)S(1)} %pad_add_fusion.where, f32[64,1024]{1,0:T(8,128)S(1)} %get-tuple-element.27.refs_0_, f32[64,1024]{1,0:T(8,128)S(1)} %get-tuple-element.28.refs_1_, f32[64,1024]{1,0:T(8,128)S(1)} %get-tuple-element.29.refs_2_, f32[64,1024]{1,0:T(8,128)S(1)} %get-tuple-element.30.refs_3_, ...), custom_call_target="tpu_custom_call" | custom-call | tf_op jit(solution)/shard_map/assemble/pallas_call | solution.py:204
  (59 shorter events, 11.2 us)
Async XLA Ops:
  0.8 7.7 %collective-permute-start.2 = (bf16[2,64,128]{2,1,0:T(8,128)(2,1)S(1)}, bf16[2,64,128]{2,1,0:T(8,128)(2,1)S(1)}, u32[]{:S(2)}, u32[]{:S(2)}) collective-permute-start(bf16[2,64,128]{2,1,0:T(8,128)(2,1)S(1)} %get-tuple-element.48), channel_id=1, source_target_pairs={{0,96},{1,97},{2,98},{3,99},{4,100},{5,101},{6,102},{7,103},{8,104... | collective-permute-start | bytes 98312 | tf_op jit(solution)/shard_map/ppermute | solution.py:30
  6.0 4.0 %collective-permute-start.1 = (bf16[2,64,128]{2,1,0:T(8,128)(2,1)S(1)}, bf16[2,64,128]{2,1,0:T(8,128)(2,1)S(1)}, u32[]{:S(2)}, u32[]{:S(2)}) collective-permute-start(bf16[2,64,128]{2,1,0:T(8,128)(2,1)S(1)} %get-tuple-element.48), channel_id=1, source_target_pairs={{0,64},{1,65},{2,66},{3,67},{4,68},{5,69},{6,70},{7,71},{8,72},{9,... | collective-permute-start | bytes 98312 | tf_op jit(solution)/shard_map/ppermute | solution.py:30
  6.0 4.0 %collective-permute-start = (bf16[2,64,128]{2,1,0:T(8,128)(2,1)S(1)}, bf16[2,64,128]{2,1,0:T(8,128)(2,1)S(1)}, u32[]{:S(2)}, u32[]{:S(2)}) collective-permute-start(bf16[2,64,128]{2,1,0:T(8,128)(2,1)S(1)} %get-tuple-element.48), channel_id=1, source_target_pairs={{0,32},{1,33},{2,34},{3,35},{4,36},{5,37},{6,38},{7,39},{8,40},{9,... | collective-permute-start | bytes 98312 | tf_op jit(solution)/shard_map/ppermute | solution.py:30
  6.4 16.0 %collective-permute-start.9 = (bf16[64,8192]{1,0:T(8,128)(2,1)}, bf16[64,8192]{1,0:T(8,128)(2,1)S(1)}, u32[]{:S(2)}, u32[]{:S(2)}) collective-permute-start(bf16[64,8192]{1,0:T(8,128)(2,1)} %param.6), channel_id=1, source_target_pairs={{0,1},{1,0},{2,3},{3,2},{4,5},{5,4},{6,7},{7,6},{8,9},{9,8},{10,11... | collective-permute-start | bytes 3145736 | tf_op jit(solution)/shard_map/ppermute | solution.py:30
  8.5 59.3 %collective-permute-start.18 = (bf16[64,8192]{1,0:T(8,128)(2,1)}, bf16[64,8192]{1,0:T(8,128)(2,1)S(1)}, u32[]{:S(2)}, u32[]{:S(2)}) collective-permute-start(bf16[64,8192]{1,0:T(8,128)(2,1)} %param.7), channel_id=1, source_target_pairs={{0,1},{1,0},{2,3},{3,2},{4,5},{5,4},{6,7},{7,6},{8,9},{9,8},{10,11... | collective-permute-start | bytes 3145736 | tf_op jit(solution)/shard_map/ppermute | solution.py:30
  10.1 5.9 %collective-permute-start.5 = (bf16[4,2,64,128]{3,2,0,1:T(8,128)(2,1)S(1)}, bf16[4,2,64,128]{3,2,0,1:T(8,128)(2,1)S(1)}, u32[]{:S(2)}, u32[]{:S(2)}) collective-permute-start(bf16[4,2,64,128]{3,2,0,1:T(8,128)(2,1)S(1)} %pad_maximum_fusion.3), channel_id=1, source_target_pairs={{0,24},{1,7},{2,26},{3,5},{4,28},{5,3},{6,30},{7,1},{8,16},{9,15},... | collective-permute-start | bytes 393224 | tf_op jit(solution)/shard_map/ppermute | solution.py:30
  12.6 5.3 %collective-permute-start.4 = (bf16[4,2,64,128]{3,2,0,1:T(8,128)(2,1)S(1)}, bf16[4,2,64,128]{3,2,0,1:T(8,128)(2,1)S(1)}, u32[]{:S(2)}, u32[]{:S(2)}) collective-permute-start(bf16[4,2,64,128]{3,2,0,1:T(8,128)(2,1)S(1)} %pad_maximum_fusion.3), channel_id=1, source_target_pairs={{0,16},{1,5},{2,18},{3,7},{4,20},{5,1},{6,22},{7,3},{8,24},{9,13},... | collective-permute-start | bytes 393224 | tf_op jit(solution)/shard_map/ppermute | solution.py:30
  13.2 4.8 %collective-permute-start.3 = (bf16[4,2,64,128]{3,2,0,1:T(8,128)(2,1)S(1)}, bf16[4,2,64,128]{3,2,0,1:T(8,128)(2,1)S(1)}, u32[]{:S(2)}, u32[]{:S(2)}) collective-permute-start(bf16[4,2,64,128]{3,2,0,1:T(8,128)(2,1)S(1)} %pad_maximum_fusion.3), channel_id=1, source_target_pairs={{0,8},{1,3},{2,10},{3,1},{4,12},{5,7},{6,14},{7,5},{8,0},{9,11},{1... | collective-permute-start | bytes 393224 | tf_op jit(solution)/shard_map/ppermute | solution.py:30
  18.0 5.3 %collective-permute-start.6 = (bf16[4,4,64,128]{3,2,1,0:T(8,128)(2,1)S(1)}, bf16[4,4,64,128]{3,2,1,0:T(8,128)(2,1)S(1)}, u32[]{:S(2)}, u32[]{:S(2)}) collective-permute-start(bf16[4,4,64,128]{3,2,1,0:T(8,128)(2,1)S(1)} %pad_maximum_fusion.1.p0), channel_id=1, source_target_pairs={{0,2},{1,9},{2,0},{3,11},{4,6},{5,13},{6,4},{7,15},{8,10},{9,1},{1... | collective-permute-start | bytes 786440 | tf_op jit(solution)/shard_map/ppermute | solution.py:30
  19.4 9.6 %collective-permute-start.7 = (bf16[4,4,64,128]{3,2,1,0:T(8,128)(2,1)S(1)}, bf16[4,4,64,128]{3,2,1,0:T(8,128)(2,1)S(1)}, u32[]{:S(2)}, u32[]{:S(2)}) collective-permute-start(bf16[4,4,64,128]{3,2,1,0:T(8,128)(2,1)S(1)} %pad_maximum_fusion.1.p0), channel_id=1, source_target_pairs={{0,4},{1,17},{2,6},{3,19},{4,0},{5,21},{6,2},{7,23},{8,12},{9,25},... | collective-permute-start | bytes 786440 | tf_op jit(solution)/shard_map/ppermute | solution.py:30
  22.3 9.5 %collective-permute-start.8 = (bf16[4,4,64,128]{3,2,1,0:T(8,128)(2,1)S(1)}, bf16[4,4,64,128]{3,2,1,0:T(8,128)(2,1)S(1)}, u32[]{:S(2)}, u32[]{:S(2)}) collective-permute-start(bf16[4,4,64,128]{3,2,1,0:T(8,128)(2,1)S(1)} %pad_maximum_fusion.1.p0), channel_id=1, source_target_pairs={{0,6},{1,25},{2,4},{3,27},{4,2},{5,29},{6,0},{7,31},{8,14},{9,17},... | collective-permute-start | bytes 786440 | tf_op jit(solution)/shard_map/ppermute | solution.py:30
  31.9 35.9 %copy-start.1 = (bf16[64,8192]{1,0:T(8,128)(2,1)S(1)}, bf16[64,8192]{1,0:T(8,128)(2,1)}, u32[]{:S(2)}) copy-start(bf16[64,8192]{1,0:T(8,128)(2,1)} %param.7) | copy-start | bytes 3145732
  33.3 4.8 %collective-permute-start.10 = (f32[128,128]{1,0:T(8,128)S(1)}, f32[128,128]{1,0:T(8,128)S(1)}, u32[]{:S(2)}, u32[]{:S(2)}) collective-permute-start(f32[128,128]{1,0:T(8,128)S(1)} %precondition.2), channel_id=1, source_target_pairs={{0,1},{1,0},{2,3},{3,2},{4,5},{5,4},{6,7},{7,6},{8,9},{9,8},{10,11... | collective-permute-start | bytes 196616 | tf_op jit(solution)/shard_map/ppermute | solution.py:30
  38.2 6.2 %collective-permute-start.14 = (bf16[128,128]{1,0:T(8,128)(2,1)S(1)}, bf16[128,128]{1,0:T(8,128)(2,1)S(1)}, u32[]{:S(2)}, u32[]{:S(2)}) collective-permute-start(bf16[128,128]{1,0:T(8,128)(2,1)S(1)} %add_convert_fusion.1), channel_id=1, source_target_pairs={{0,192},{1,224},{2,194},{3,226},{4,196},{5,228},{6,198},{7,230},{8... | collective-permute-start | bytes 98312 | tf_op jit(solution)/shard_map/ppermute | solution.py:30
  41.3 5.5 %collective-permute-start.13 = (bf16[128,128]{1,0:T(8,128)(2,1)S(1)}, bf16[128,128]{1,0:T(8,128)(2,1)S(1)}, u32[]{:S(2)}, u32[]{:S(2)}) collective-permute-start(bf16[128,128]{1,0:T(8,128)(2,1)S(1)} %add_convert_fusion.1), channel_id=1, source_target_pairs={{0,64},{1,96},{2,66},{3,98},{4,68},{5,100},{6,70},{7,102},{8,72},{... | collective-permute-start | bytes 98312 | tf_op jit(solution)/shard_map/ppermute | solution.py:30
  44.0 5.8 %collective-permute-start.12 = (bf16[128,128]{1,0:T(8,128)(2,1)S(1)}, bf16[128,128]{1,0:T(8,128)(2,1)S(1)}, u32[]{:S(2)}, u32[]{:S(2)}) collective-permute-start(bf16[128,128]{1,0:T(8,128)(2,1)S(1)} %add_convert_fusion.1), channel_id=1, source_target_pairs={{0,128},{1,160},{2,130},{3,162},{4,132},{5,164},{6,134},{7,166},{8... | collective-permute-start | bytes 98312 | tf_op jit(solution)/shard_map/ppermute | solution.py:30
  44.0 11.6 %collective-permute-start.15 = (bf16[4,4,64,128]{3,2,1,0:T(8,128)(2,1)S(1)}, bf16[4,4,64,128]{3,2,1,0:T(8,128)(2,1)S(1)}, u32[]{:S(2)}, u32[]{:S(2)}) collective-permute-start(bf16[4,4,64,128]{3,2,1,0:T(8,128)(2,1)S(1)} %pad_maximum_fusion.2.p0), channel_id=1, source_target_pairs={{0,2},{1,9},{2,0},{3,11},{4,6},{5,13},{6,4},{7,15},{8,10},{9,1},{1... | collective-permute-start | bytes 786440 | tf_op jit(solution)/shard_map/ppermute | solution.py:30
  44.3 11.4 %collective-permute-start.16 = (bf16[4,4,64,128]{3,2,1,0:T(8,128)(2,1)S(1)}, bf16[4,4,64,128]{3,2,1,0:T(8,128)(2,1)S(1)}, u32[]{:S(2)}, u32[]{:S(2)}) collective-permute-start(bf16[4,4,64,128]{3,2,1,0:T(8,128)(2,1)S(1)} %pad_maximum_fusion.2.p0), channel_id=1, source_target_pairs={{0,4},{1,17},{2,6},{3,19},{4,0},{5,21},{6,2},{7,23},{8,12},{9,25},... | collective-permute-start | bytes 786440 | tf_op jit(solution)/shard_map/ppermute | solution.py:30
  46.9 9.5 %collective-permute-start.17 = (bf16[4,4,64,128]{3,2,1,0:T(8,128)(2,1)S(1)}, bf16[4,4,64,128]{3,2,1,0:T(8,128)(2,1)S(1)}, u32[]{:S(2)}, u32[]{:S(2)}) collective-permute-start(bf16[4,4,64,128]{3,2,1,0:T(8,128)(2,1)S(1)} %pad_maximum_fusion.2.p0), channel_id=1, source_target_pairs={{0,6},{1,25},{2,4},{3,27},{4,2},{5,29},{6,0},{7,31},{8,14},{9,17},... | collective-permute-start | bytes 786440 | tf_op jit(solution)/shard_map/ppermute | solution.py:30
  49.8 5.8 %collective-permute-start.11 = (bf16[128,128]{1,0:T(8,128)(2,1)S(1)}, bf16[128,128]{1,0:T(8,128)(2,1)S(1)}, u32[]{:S(2)}, u32[]{:S(2)}) collective-permute-start(bf16[128,128]{1,0:T(8,128)(2,1)S(1)} %add_convert_fusion.1), channel_id=1, source_target_pairs={{0,0},{1,32},{2,2},{3,34},{4,4},{5,36},{6,6},{7,38},{8,8},{9,40},{... | collective-permute-start | bytes 98312 | tf_op jit(solution)/shard_map/ppermute | solution.py:30
  56.4 6.5 %collective-permute-start.23 = (bf16[2,128,256]{2,1,0:T(8,128)(2,1)S(1)}, bf16[2,128,256]{2,1,0:T(8,128)(2,1)S(1)}, u32[]{:S(2)}, u32[]{:S(2)}) collective-permute-start(bf16[2,128,256]{2,1,0:T(8,128)(2,1)S(1)} %pad_maximum_fusion.4), channel_id=1, source_target_pairs={{0,24},{1,7},{2,26},{3,5},{4,28},{5,3},{6,30},{7,1},{8,16},{9,15},... | collective-permute-start | bytes 393224 | tf_op jit(solution)/shard_map/ppermute | solution.py:30
  56.6 6.3 %collective-permute-start.22 = (bf16[2,128,256]{2,1,0:T(8,128)(2,1)S(1)}, bf16[2,128,256]{2,1,0:T(8,128)(2,1)S(1)}, u32[]{:S(2)}, u32[]{:S(2)}) collective-permute-start(bf16[2,128,256]{2,1,0:T(8,128)(2,1)S(1)} %pad_maximum_fusion.4), channel_id=1, source_target_pairs={{0,16},{1,5},{2,18},{3,7},{4,20},{5,1},{6,22},{7,3},{8,24},{9,13},... | collective-permute-start | bytes 393224 | tf_op jit(solution)/shard_map/ppermute | solution.py:30
  57.1 6.6 %collective-permute-start.21 = (bf16[2,128,256]{2,1,0:T(8,128)(2,1)S(1)}, bf16[2,128,256]{2,1,0:T(8,128)(2,1)S(1)}, u32[]{:S(2)}, u32[]{:S(2)}) collective-permute-start(bf16[2,128,256]{2,1,0:T(8,128)(2,1)S(1)} %pad_maximum_fusion.4), channel_id=1, source_target_pairs={{0,8},{1,3},{2,10},{3,1},{4,12},{5,7},{6,14},{7,5},{8,0},{9,11},{1... | collective-permute-start | bytes 393224 | tf_op jit(solution)/shard_map/ppermute | solution.py:30
  63.8 18.5 %collective-permute-start.24 = (bf16[4,2,128,256]{3,2,1,0:T(8,128)(2,1)S(1)}, bf16[4,2,128,256]{3,2,1,0:T(8,128)(2,1)S(1)}, u32[]{:S(2)}, u32[]{:S(2)}) collective-permute-start(bf16[4,2,128,256]{3,2,1,0:T(8,128)(2,1)S(1)} %pad_maximum_fusion.piece), channel_id=1, source_target_pairs={{0,2},{1,9},{2,0},{3,11},{4,6},{5,13},{6,4},{7,15},{8,10},{9,1},{1... | collective-permute-start | bytes 1572872 | tf_op jit(solution)/shard_map/ppermute | solution.py:30
  63.9 19.4 %collective-permute-start.25 = (bf16[4,2,128,256]{3,2,1,0:T(8,128)(2,1)S(1)}, bf16[4,2,128,256]{3,2,1,0:T(8,128)(2,1)S(1)}, u32[]{:S(2)}, u32[]{:S(2)}) collective-permute-start(bf16[4,2,128,256]{3,2,1,0:T(8,128)(2,1)S(1)} %pad_maximum_fusion.piece), channel_id=1, source_target_pairs={{0,4},{1,17},{2,6},{3,19},{4,0},{5,21},{6,2},{7,23},{8,12},{9,25},... | collective-permute-start | bytes 1572872 | tf_op jit(solution)/shard_map/ppermute | solution.py:30
  66.3 18.5 %collective-permute-start.26 = (bf16[4,2,128,256]{3,2,1,0:T(8,128)(2,1)S(1)}, bf16[4,2,128,256]{3,2,1,0:T(8,128)(2,1)S(1)}, u32[]{:S(2)}, u32[]{:S(2)}) collective-permute-start(bf16[4,2,128,256]{3,2,1,0:T(8,128)(2,1)S(1)} %pad_maximum_fusion.piece), channel_id=1, source_target_pairs={{0,6},{1,25},{2,4},{3,27},{4,2},{5,29},{6,0},{7,31},{8,14},{9,17},... | collective-permute-start | bytes 1572872 | tf_op jit(solution)/shard_map/ppermute | solution.py:30
  69.4 3.6 %collective-permute-start.19 = (f32[128,128]{1,0:T(8,128)S(1)}, f32[128,128]{1,0:T(8,128)S(1)}, u32[]{:S(2)}, u32[]{:S(2)}) collective-permute-start(f32[128,128]{1,0:T(8,128)S(1)} %precondition.3), channel_id=1, source_target_pairs={{0,1},{1,0},{2,3},{3,2},{4,5},{5,4},{6,7},{7,6},{8,9},{9,8},{10,11... | collective-permute-start | bytes 196616 | tf_op jit(solution)/shard_map/ppermute | solution.py:30
  73.1 6.8 %collective-permute-start.20 = (bf16[128,128]{1,0:T(8,128)(2,1)S(1)}, bf16[128,128]{1,0:T(8,128)(2,1)S(1)}, u32[]{:S(2)}, u32[]{:S(2)}) collective-permute-start(bf16[128,128]{1,0:T(8,128)(2,1)S(1)} %add_convert_fusion), channel_id=1, source_target_pairs={{0,128},{1,129},{2,130},{3,131},{4,132},{5,133},{6,134},{7,135},{8... | collective-permute-start | bytes 98312 | tf_op jit(solution)/shard_map/ppermute | solution.py:30
  80.7 6.4 %collective-permute-start.27 = (f32[64,1024]{1,0:T(8,128)S(1)}, f32[64,1024]{1,0:T(8,128)S(1)}, u32[]{:S(2)}, u32[]{:S(2)}) collective-permute-start(f32[64,1024]{1,0:T(8,128)S(1)} %get-tuple-element.31), channel_id=1, source_target_pairs={{0,1},{1,0},{2,3},{3,2},{4,5},{5,4},{6,7},{7,6},{8,9},{9,8},{10,11... | collective-permute-start | bytes 786440 | tf_op jit(solution)/shard_map/ppermute | solution.py:30
  83.2 4.0 %collective-permute-start.28 = (f32[64,1024]{1,0:T(8,128)S(1)}, f32[64,1024]{1,0:T(8,128)S(1)}, u32[]{:S(2)}, u32[]{:S(2)}) collective-permute-start(f32[64,1024]{1,0:T(8,128)S(1)} %get-tuple-element.32), channel_id=1, source_target_pairs={{0,1},{1,0},{2,3},{3,2},{4,5},{5,4},{6,7},{7,6},{8,9},{9,8},{10,11... | collective-permute-start | bytes 786440 | tf_op jit(solution)/shard_map/ppermute | solution.py:30
  84.1 3.0 %collective-permute-start.29 = (f32[64,1024]{1,0:T(8,128)S(1)}, f32[64,1024]{1,0:T(8,128)S(1)}, u32[]{:S(2)}, u32[]{:S(2)}) collective-permute-start(f32[64,1024]{1,0:T(8,128)S(1)} %get-tuple-element.33), channel_id=1, source_target_pairs={{0,1},{1,0},{2,3},{3,2},{4,5},{5,4},{6,7},{7,6},{8,9},{9,8},{10,11... | collective-permute-start | bytes 786440 | tf_op jit(solution)/shard_map/ppermute | solution.py:30
  85.6 2.7 %collective-permute-start.30 = (f32[64,1024]{1,0:T(8,128)S(1)}, f32[64,1024]{1,0:T(8,128)S(1)}, u32[]{:S(2)}, u32[]{:S(2)}) collective-permute-start(f32[64,1024]{1,0:T(8,128)S(1)} %get-tuple-element.34), channel_id=1, source_target_pairs={{0,1},{1,0},{2,3},{3,2},{4,5},{5,4},{6,7},{7,6},{8,9},{9,8},{10,11... | collective-permute-start | bytes 786440 | tf_op jit(solution)/shard_map/ppermute | solution.py:30
  (1 other events, 22.4 us)

commit v10 on v9

--- a/solution.py
+++ b/solution.py
@@ -187,12 +187,13 @@
     here = [to_parity(act, j, 0) for j in (0, 1)]
     there = [to_parity(act, j, 1) for j in (0, 1)]
     pair = jnp.stack([jnp.concatenate(p, axis=1) for p in zip(here, there)])
-    pair, *grad_pieces = lax.optimization_barrier((pair, *grad_pieces))
     part = partial(grad_pieces, grad_rows)
+    pair, part = lax.optimization_barrier((pair, part))
     grad = (part + swap_cores(part)).astype(bf16)
+    plane = jnp.stack(turned(first_turn, [pair] * 4))
+    plane, grad = lax.optimization_barrier((plane, grad))
     grad = jnp.concatenate([grad, swap_reps(grad)], axis=1)
 
-    plane = jnp.stack(turned(first_turn, [pair] * 4))
     made = [
         call(tile, "tile", [shape((64, 1024), f32)] * 2, [SMEM, VMEM, VMEM])(
             where, grad, piece

time: 90.8 us -> 87.2 us (0.960)
  waiting for transfers between devices: 30.9 us -> 27.2 us
    ppermute x31, waiting for transfers between devices: 30.9 us -> 27.2 us  [send(): return lax.ppermute(value, AXES, pairs)]
  transfers between devices with their start and end apart: 31 -> 31, of which waited for: 15 -> 14; matrix products, arithmetic and copies ran while one was open for 1% -> 1% of each run, Pallas kernels for 7% -> 6%
where the time goes in v10:
time: 87.2 us; the launch traced here: 87 us
  starting transfers between devices  49.5 us (57%)
  waiting for transfers between devices  27.2 us (31%)
  Pallas kernels  8.32 us (10%)
  other arithmetic  1.53 us (2%)
    ppermute x31, starting transfers between devices, send(): return lax.ppermute(value, AXES, pairs)  49.5 us
    ppermute x31, waiting for transfers between devices, send(): return lax.ppermute(value, AXES, pairs)  27.2 us
    pallas_call x4, Pallas kernels, on_device(): call(tile, 'tile', [shape((64, 1024), f32)] * 2, [SMEM, VMEM, VMEM])  3.38 us
    pallas_call x2, Pallas kernels, partial(): call(precondition, 'precondition', shape((128, 128), f32), [SMEM] + [VMEM...  2.84 us
    pallas_call x1, Pallas kernels, on_device(): pl.pallas_call(assemble, out_shape=shape((64, 8192), f32), in_specs=[SMEM...  2.1 us
  transfers between devices with their start and end apart: 31, of which 14 were waited for; matrix products, arithmetic and copies ran while one was open for 1% of the time, Pallas kernels for 6%

profile of v10, /device:TPU:1, one launch (start us, length us, event | category | flops | bytes accessed | tf_op | source)
XLA Modules:
  0.0 87.0 jit_solution(7123568619953949477)
XLA Ops:
  0.8 3.8 %collective-permute-start.1 = (bf16[2,64,128]{2,1,0:T(8,128)(2,1)S(1)}, bf16[2,64,128]{2,1,0:T(8,128)(2,1)S(1)}, u32[]{:S(2)}, u32[]{:S(2)}) collective-permute-start(bf16[2,64,128]{2,1,0:T(8,128)(2,1)S(1)} %get-tuple-element.46), channel_id=1, source_target_pairs={{0,64},{1,65},{2,66},{3,67},{4,68},{5,69},{6,70},{7,71},{8,72},{9,... | collective-permute-start | bytes 98312 | tf_op jit(solution)/shard_map/ppermute | solution.py:30
  4.7 1.6 %collective-permute-start = (bf16[2,64,128]{2,1,0:T(8,128)(2,1)S(1)}, bf16[2,64,128]{2,1,0:T(8,128)(2,1)S(1)}, u32[]{:S(2)}, u32[]{:S(2)}) collective-permute-start(bf16[2,64,128]{2,1,0:T(8,128)(2,1)S(1)} %get-tuple-element.46), channel_id=1, source_target_pairs={{0,32},{1,33},{2,34},{3,35},{4,36},{5,37},{6,38},{7,39},{8,40},{9,... | collective-permute-start | bytes 98312 | tf_op jit(solution)/shard_map/ppermute | solution.py:30
  6.3 2.2 %collective-permute-start.9 = (bf16[64,8192]{1,0:T(8,128)(2,1)}, bf16[64,8192]{1,0:T(8,128)(2,1)S(1)}, u32[]{:S(2)}, u32[]{:S(2)}) collective-permute-start(bf16[64,8192]{1,0:T(8,128)(2,1)} %param.6), channel_id=1, source_target_pairs={{0,1},{1,0},{2,3},{3,2},{4,5},{5,4},{6,7},{7,6},{8,9},{9,8},{10,11... | collective-permute-start | bytes 3145736 | tf_op jit(solution)/shard_map/ppermute | solution.py:30
  8.5 2.3 %collective-permute-done.2 = bf16[2,64,128]{2,1,0:T(8,128)(2,1)S(1)} collective-permute-done((bf16[2,64,128]{2,1,0:T(8,128)(2,1)S(1)}, bf16[2,64,128]{2,1,0:T(8,128)(2,1)S(1)}, u32[]{:S(2)}, u32[]{:S(2)}) %collective-permute-start.2) | collective-permute-done | bytes 32800 | tf_op jit(solution)/shard_map/ppermute | solution.py:30
  10.9 2.6 %collective-permute-start.5 = (bf16[4,2,64,128]{3,2,0,1:T(8,128)(2,1)S(1)}, bf16[4,2,64,128]{3,2,0,1:T(8,128)(2,1)S(1)}, u32[]{:S(2)}, u32[]{:S(2)}) collective-permute-start(bf16[4,2,64,128]{3,2,0,1:T(8,128)(2,1)S(1)} %pad_maximum_fusion.3), channel_id=1, source_target_pairs={{0,24},{1,7},{2,26},{3,5},{4,28},{5,3},{6,30},{7,1},{8,16},{9,15},... | collective-permute-start | bytes 393224 | tf_op jit(solution)/shard_map/ppermute | solution.py:30
  14.2 2.5 %collective-permute-done.5 = bf16[4,2,64,128]{3,2,0,1:T(8,128)(2,1)S(1)} collective-permute-done((bf16[4,2,64,128]{3,2,0,1:T(8,128)(2,1)S(1)}, bf16[4,2,64,128]{3,2,0,1:T(8,128)(2,1)S(1)}, u32[]{:S(2)}, u32[]{:S(2)}) %collective-permute-start.5) | collective-permute-done | bytes 131104 | tf_op jit(solution)/shard_map/ppermute | solution.py:30
  16.8 2.0 %collective-permute-done.4 = bf16[4,2,64,128]{3,2,0,1:T(8,128)(2,1)S(1)} collective-permute-done((bf16[4,2,64,128]{3,2,0,1:T(8,128)(2,1)S(1)}, bf16[4,2,64,128]{3,2,0,1:T(8,128)(2,1)S(1)}, u32[]{:S(2)}, u32[]{:S(2)}) %collective-permute-start.4) | collective-permute-done | bytes 131104 | tf_op jit(solution)/shard_map/ppermute | solution.py:30
  18.9 3.1 %collective-permute-start.8 = (bf16[4,4,64,128]{3,2,1,0:T(8,128)(2,1)S(1)}, bf16[4,4,64,128]{3,2,1,0:T(8,128)(2,1)S(1)}, u32[]{:S(2)}, u32[]{:S(2)}) collective-permute-start(bf16[4,4,64,128]{3,2,1,0:T(8,128)(2,1)S(1)} %pad_maximum_fusion.1.p0), channel_id=1, source_target_pairs={{0,6},{1,25},{2,4},{3,27},{4,2},{5,29},{6,0},{7,31},{8,14},{9,17},... | collective-permute-start | bytes 786440 | tf_op jit(solution)/shard_map/ppermute | solution.py:30
  22.9 5.2 %collective-permute-done.8.p3 = bf16[4,4,64,128]{3,2,1,0:T(8,128)(2,1)S(1)} collective-permute-done((bf16[4,4,64,128]{3,2,1,0:T(8,128)(2,1)S(1)}, bf16[4,4,64,128]{3,2,1,0:T(8,128)(2,1)S(1)}, u32[]{:S(2)}, u32[]{:S(2)}) %collective-permute-start.8) | collective-permute-done | bytes 262176 | tf_op jit(solution)/shard_map/ppermute | solution.py:30
  28.7 0.9 collective-permute-done.6.p1
  29.6 1.4 %precondition.2 = f32[128,128]{1,0:T(8,128)S(1)} custom-call(s32[4]{0:T(128)S(1)} %pad_add_fusion.where, bf16[4,4,64,128]{3,2,1,0:T(8,128)(2,1)S(1)} %pad_maximum_fusion.1.p0, bf16[4,4,64,128]{3,2,1,0:T(8,128)(2,1)S(1)} %collective-permute-done.6.p1, bf16[4,4,64,128]{3,2,1,0:T(8,128)(2,1)S(1)} %collective-permute-done.7.p2, ...), custom_call_target="tpu_custom_call" | custom-call | tf_op jit(solution)/shard_map/precondition/pallas_call | solution.py:177
  31.0 4.8 %collective-permute-start.10 = (f32[128,128]{1,0:T(8,128)S(1)}, f32[128,128]{1,0:T(8,128)S(1)}, u32[]{:S(2)}, u32[]{:S(2)}) collective-permute-start(f32[128,128]{1,0:T(8,128)S(1)} %precondition.2), channel_id=1, source_target_pairs={{0,1},{1,0},{2,3},{3,2},{4,5},{5,4},{6,7},{7,6},{8,9},{9,8},{10,11... | collective-permute-start | bytes 196616 | tf_op jit(solution)/shard_map/ppermute | solution.py:30
  35.8 1.7 %collective-permute-start.17 = (bf16[4,4,64,128]{3,2,1,0:T(8,128)(2,1)S(1)}, bf16[4,4,64,128]{3,2,1,0:T(8,128)(2,1)S(1)}, u32[]{:S(2)}, u32[]{:S(2)}) collective-permute-start(bf16[4,4,64,128]{3,2,1,0:T(8,128)(2,1)S(1)} %pad_maximum_fusion.2.p0), channel_id=1, source_target_pairs={{0,6},{1,25},{2,4},{3,27},{4,2},{5,29},{6,0},{7,31},{8,14},{9,17},... | collective-permute-start | bytes 786440 | tf_op jit(solution)/shard_map/ppermute | solution.py:30
  37.8 1.2 %collective-permute-start.15 = (bf16[4,4,64,128]{3,2,1,0:T(8,128)(2,1)S(1)}, bf16[4,4,64,128]{3,2,1,0:T(8,128)(2,1)S(1)}, u32[]{:S(2)}, u32[]{:S(2)}) collective-permute-start(bf16[4,4,64,128]{3,2,1,0:T(8,128)(2,1)S(1)} %pad_maximum_fusion.2.p0), channel_id=1, source_target_pairs={{0,2},{1,9},{2,0},{3,11},{4,6},{5,13},{6,4},{7,15},{8,10},{9,1},{1... | collective-permute-start | bytes 786440 | tf_op jit(solution)/shard_map/ppermute | solution.py:30
  39.1 3.8 %collective-permute-start.14 = (bf16[128,128]{1,0:T(8,128)(2,1)S(1)}, bf16[128,128]{1,0:T(8,128)(2,1)S(1)}, u32[]{:S(2)}, u32[]{:S(2)}) collective-permute-start(bf16[128,128]{1,0:T(8,128)(2,1)S(1)} %add_convert_fusion.1), channel_id=1, source_target_pairs={{0,192},{1,224},{2,194},{3,226},{4,196},{5,228},{6,198},{7,230},{8... | collective-permute-start | bytes 98312 | tf_op jit(solution)/shard_map/ppermute | solution.py:30
  43.9 4.6 %collective-permute-start.12 = (bf16[128,128]{1,0:T(8,128)(2,1)S(1)}, bf16[128,128]{1,0:T(8,128)(2,1)S(1)}, u32[]{:S(2)}, u32[]{:S(2)}) collective-permute-start(bf16[128,128]{1,0:T(8,128)(2,1)S(1)} %add_convert_fusion.1), channel_id=1, source_target_pairs={{0,128},{1,160},{2,130},{3,162},{4,132},{5,164},{6,134},{7,166},{8... | collective-permute-start | bytes 98312 | tf_op jit(solution)/shard_map/ppermute | solution.py:30
  48.4 2.1 %collective-permute-start.11 = (bf16[128,128]{1,0:T(8,128)(2,1)S(1)}, bf16[128,128]{1,0:T(8,128)(2,1)S(1)}, u32[]{:S(2)}, u32[]{:S(2)}) collective-permute-start(bf16[128,128]{1,0:T(8,128)(2,1)S(1)} %add_convert_fusion.1), channel_id=1, source_target_pairs={{0,0},{1,32},{2,2},{3,34},{4,4},{5,36},{6,6},{7,38},{8,8},{9,40},{... | collective-permute-start | bytes 98312 | tf_op jit(solution)/shard_map/ppermute | solution.py:30
  50.6 3.0 %collective-permute-done.11 = bf16[128,128]{1,0:T(8,128)(2,1)S(1)} collective-permute-done((bf16[128,128]{1,0:T(8,128)(2,1)S(1)}, bf16[128,128]{1,0:T(8,128)(2,1)S(1)}, u32[]{:S(2)}, u32[]{:S(2)}) %collective-permute-start.11) | collective-permute-done | bytes 32800 | tf_op jit(solution)/shard_map/ppermute | solution.py:30
  53.6 1.4 %precondition.3 = f32[128,128]{1,0:T(8,128)S(1)} custom-call(s32[4]{0:T(128)S(1)} %pad_add_fusion.where, bf16[4,4,64,128]{3,2,1,0:T(8,128)(2,1)S(1)} %pad_maximum_fusion.2.p0, bf16[4,4,64,128]{3,2,1,0:T(8,128)(2,1)S(1)} %collective-permute-done.15.p1, bf16[4,4,64,128]{3,2,1,0:T(8,128)(2,1)S(1)} %collective-permute-done.16.p2, ...), custom_call_target="tpu_custom_call" | custom-call | tf_op jit(solution)/shard_map/precondition/pallas_call | solution.py:177
  55.5 2.4 %collective-permute-start.21 = (bf16[2,128,256]{2,1,0:T(8,128)(2,1)S(1)}, bf16[2,128,256]{2,1,0:T(8,128)(2,1)S(1)}, u32[]{:S(2)}, u32[]{:S(2)}) collective-permute-start(bf16[2,128,256]{2,1,0:T(8,128)(2,1)S(1)} %pad_maximum_fusion.4), channel_id=1, source_target_pairs={{0,24},{1,7},{2,26},{3,5},{4,28},{5,3},{6,30},{7,1},{8,16},{9,15},... | collective-permute-start | bytes 393224 | tf_op jit(solution)/shard_map/ppermute | solution.py:30
  58.8 2.5 %collective-permute-done.21 = bf16[2,128,256]{2,1,0:T(8,128)(2,1)S(1)} collective-permute-done((bf16[2,128,256]{2,1,0:T(8,128)(2,1)S(1)}, bf16[2,128,256]{2,1,0:T(8,128)(2,1)S(1)}, u32[]{:S(2)}, u32[]{:S(2)}) %collective-permute-start.21) | collective-permute-done | bytes 131104 | tf_op jit(solution)/shard_map/ppermute | solution.py:30
  61.3 2.3 %collective-permute-done.20 = bf16[2,128,256]{2,1,0:T(8,128)(2,1)S(1)} collective-permute-done((bf16[2,128,256]{2,1,0:T(8,128)(2,1)S(1)}, bf16[2,128,256]{2,1,0:T(8,128)(2,1)S(1)}, u32[]{:S(2)}, u32[]{:S(2)}) %collective-permute-start.20) | collective-permute-done | bytes 131104 | tf_op jit(solution)/shard_map/ppermute | solution.py:30
  63.6 1.4 %collective-permute-start.26 = (bf16[4,2,128,256]{3,2,1,0:T(8,128)(2,1)S(1)}, bf16[4,2,128,256]{3,2,1,0:T(8,128)(2,1)S(1)}, u32[]{:S(2)}, u32[]{:S(2)}) collective-permute-start(bf16[4,2,128,256]{3,2,1,0:T(8,128)(2,1)S(1)} %pad_maximum_fusion.piece), channel_id=1, source_target_pairs={{0,6},{1,25},{2,4},{3,27},{4,2},{5,29},{6,0},{7,31},{8,14},{9,17},... | collective-permute-start | bytes 1572872 | tf_op jit(solution)/shard_map/ppermute | solution.py:30
  65.4 1.5 %collective-permute-start.24 = (bf16[4,2,128,256]{3,2,1,0:T(8,128)(2,1)S(1)}, bf16[4,2,128,256]{3,2,1,0:T(8,128)(2,1)S(1)}, u32[]{:S(2)}, u32[]{:S(2)}) collective-permute-start(bf16[4,2,128,256]{3,2,1,0:T(8,128)(2,1)S(1)} %pad_maximum_fusion.piece), channel_id=1, source_target_pairs={{0,2},{1,9},{2,0},{3,11},{4,6},{5,13},{6,4},{7,15},{8,10},{9,1},{1... | collective-permute-start | bytes 1572872 | tf_op jit(solution)/shard_map/ppermute | solution.py:30
  67.0 4.5 %collective-permute-start.23 = (bf16[128,128]{1,0:T(8,128)(2,1)S(1)}, bf16[128,128]{1,0:T(8,128)(2,1)S(1)}, u32[]{:S(2)}, u32[]{:S(2)}) collective-permute-start(bf16[128,128]{1,0:T(8,128)(2,1)S(1)} %add_convert_fusion), channel_id=1, source_target_pairs={{0,128},{1,129},{2,130},{3,131},{4,132},{5,133},{6,134},{7,135},{8... | collective-permute-start | bytes 98312 | tf_op jit(solution)/shard_map/ppermute | solution.py:30
  71.5 2.2 %collective-permute-done.23 = bf16[128,128]{1,0:T(8,128)(2,1)S(1)} collective-permute-done((bf16[128,128]{1,0:T(8,128)(2,1)S(1)}, bf16[128,128]{1,0:T(8,128)(2,1)S(1)}, u32[]{:S(2)}, u32[]{:S(2)}) %collective-permute-start.23) | collective-permute-done | bytes 32800 | tf_op jit(solution)/shard_map/ppermute | solution.py:30
  73.7 0.8 tile.4
  74.5 2.6 %collective-permute-start.27 = (f32[64,1024]{1,0:T(8,128)S(1)}, f32[64,1024]{1,0:T(8,128)S(1)}, u32[]{:S(2)}, u32[]{:S(2)}) collective-permute-start(f32[64,1024]{1,0:T(8,128)S(1)} %get-tuple-element.29), channel_id=1, source_target_pairs={{0,1},{1,0},{2,3},{3,2},{4,5},{5,4},{6,7},{7,6},{8,9},{9,8},{10,11... | collective-permute-start | bytes 786440 | tf_op jit(solution)/shard_map/ppermute | solution.py:30
  77.1 1.8 %collective-permute-done.26.piece = bf16[4,2,128,256]{3,2,1,0:T(8,128)(2,1)S(1)} collective-permute-done((bf16[4,2,128,256]{3,2,1,0:T(8,128)(2,1)S(1)}, bf16[4,2,128,256]{3,2,1,0:T(8,128)(2,1)S(1)}, u32[]{:S(2)}, u32[]{:S(2)}) %collective-permute-start.26) | collective-permute-done | bytes 524320 | tf_op jit(solution)/shard_map/ppermute | solution.py:30
  79.7 1.4 %collective-permute-start.30 = (f32[64,1024]{1,0:T(8,128)S(1)}, f32[64,1024]{1,0:T(8,128)S(1)}, u32[]{:S(2)}, u32[]{:S(2)}) collective-permute-start(f32[64,1024]{1,0:T(8,128)S(1)} %get-tuple-element.32), channel_id=1, source_target_pairs={{0,1},{1,0},{2,3},{3,2},{4,5},{5,4},{6,7},{7,6},{8,9},{9,8},{10,11... | collective-permute-start | bytes 786440 | tf_op jit(solution)/shard_map/ppermute | solution.py:30
  83.7 1.1 %collective-permute-done.28.refs_5_ = f32[64,1024]{1,0:T(8,128)S(1)} collective-permute-done((f32[64,1024]{1,0:T(8,128)S(1)}, f32[64,1024]{1,0:T(8,128)S(1)}, u32[]{:S(2)}, u32[]{:S(2)}) %collective-permute-start.28) | collective-permute-done | bytes 262176 | tf_op jit(solution)/shard_map/ppermute | solution.py:30
  84.8 2.1 %assemble.1 = f32[64,8192]{1,0:T(8,128)} custom-call(s32[4]{0:T(128)S(1)} %pad_add_fusion.where, f32[64,1024]{1,0:T(8,128)S(1)} %get-tuple-element.25.refs_0_, f32[64,1024]{1,0:T(8,128)S(1)} %get-tuple-element.26.refs_1_, f32[64,1024]{1,0:T(8,128)S(1)} %get-tuple-element.27.refs_2_, f32[64,1024]{1,0:T(8,128)S(1)} %get-tuple-element.28.refs_3_, ...), custom_call_target="tpu_custom_call" | custom-call | tf_op jit(solution)/shard_map/assemble/pallas_call | solution.py:205
  (60 shorter events, 9.7 us)
Async XLA Ops:
  0.0 22.7 %copy-start = (bf16[64,8192]{1,0:T(8,128)(2,1)S(1)}, bf16[64,8192]{1,0:T(8,128)(2,1)}, u32[]{:S(2)}) copy-start(bf16[64,8192]{1,0:T(8,128)(2,1)} %param.6) | copy-start | bytes 3145732
  0.8 7.7 %collective-permute-start.1 = (bf16[2,64,128]{2,1,0:T(8,128)(2,1)S(1)}, bf16[2,64,128]{2,1,0:T(8,128)(2,1)S(1)}, u32[]{:S(2)}, u32[]{:S(2)}) collective-permute-start(bf16[2,64,128]{2,1,0:T(8,128)(2,1)S(1)} %get-tuple-element.46), channel_id=1, source_target_pairs={{0,64},{1,65},{2,66},{3,67},{4,68},{5,69},{6,70},{7,71},{8,72},{9,... | collective-permute-start | bytes 98312 | tf_op jit(solution)/shard_map/ppermute | solution.py:30
  4.7 3.9 %collective-permute-start = (bf16[2,64,128]{2,1,0:T(8,128)(2,1)S(1)}, bf16[2,64,128]{2,1,0:T(8,128)(2,1)S(1)}, u32[]{:S(2)}, u32[]{:S(2)}) collective-permute-start(bf16[2,64,128]{2,1,0:T(8,128)(2,1)S(1)} %get-tuple-element.46), channel_id=1, source_target_pairs={{0,32},{1,33},{2,34},{3,35},{4,36},{5,37},{6,38},{7,39},{8,40},{9,... | collective-permute-start | bytes 98312 | tf_op jit(solution)/shard_map/ppermute | solution.py:30
  6.3 4.6 %collective-permute-start.2 = (bf16[2,64,128]{2,1,0:T(8,128)(2,1)S(1)}, bf16[2,64,128]{2,1,0:T(8,128)(2,1)S(1)}, u32[]{:S(2)}, u32[]{:S(2)}) collective-permute-start(bf16[2,64,128]{2,1,0:T(8,128)(2,1)S(1)} %get-tuple-element.46), channel_id=1, source_target_pairs={{0,96},{1,97},{2,98},{3,99},{4,100},{5,101},{6,102},{7,103},{8,104... | collective-permute-start | bytes 98312 | tf_op jit(solution)/shard_map/ppermute | solution.py:30
  6.3 16.4 %collective-permute-start.9 = (bf16[64,8192]{1,0:T(8,128)(2,1)}, bf16[64,8192]{1,0:T(8,128)(2,1)S(1)}, u32[]{:S(2)}, u32[]{:S(2)}) collective-permute-start(bf16[64,8192]{1,0:T(8,128)(2,1)} %param.6), channel_id=1, source_target_pairs={{0,1},{1,0},{2,3},{3,2},{4,5},{5,4},{6,7},{7,6},{8,9},{9,8},{10,11... | collective-permute-start | bytes 3145736 | tf_op jit(solution)/shard_map/ppermute | solution.py:30
  8.5 34.4 %collective-permute-start.18 = (bf16[64,8192]{1,0:T(8,128)(2,1)}, bf16[64,8192]{1,0:T(8,128)(2,1)S(1)}, u32[]{:S(2)}, u32[]{:S(2)}) collective-permute-start(bf16[64,8192]{1,0:T(8,128)(2,1)} %param.7), channel_id=1, source_target_pairs={{0,1},{1,0},{2,3},{3,2},{4,5},{5,4},{6,7},{7,6},{8,9},{9,8},{10,11... | collective-permute-start | bytes 3145736 | tf_op jit(solution)/shard_map/ppermute | solution.py:30
  10.9 5.9 %collective-permute-start.5 = (bf16[4,2,64,128]{3,2,0,1:T(8,128)(2,1)S(1)}, bf16[4,2,64,128]{3,2,0,1:T(8,128)(2,1)S(1)}, u32[]{:S(2)}, u32[]{:S(2)}) collective-permute-start(bf16[4,2,64,128]{3,2,0,1:T(8,128)(2,1)S(1)} %pad_maximum_fusion.3), channel_id=1, source_target_pairs={{0,24},{1,7},{2,26},{3,5},{4,28},{5,3},{6,30},{7,1},{8,16},{9,15},... | collective-permute-start | bytes 393224 | tf_op jit(solution)/shard_map/ppermute | solution.py:30
  13.4 5.3 %collective-permute-start.4 = (bf16[4,2,64,128]{3,2,0,1:T(8,128)(2,1)S(1)}, bf16[4,2,64,128]{3,2,0,1:T(8,128)(2,1)S(1)}, u32[]{:S(2)}, u32[]{:S(2)}) collective-permute-start(bf16[4,2,64,128]{3,2,0,1:T(8,128)(2,1)S(1)} %pad_maximum_fusion.3), channel_id=1, source_target_pairs={{0,16},{1,5},{2,18},{3,7},{4,20},{5,1},{6,22},{7,3},{8,24},{9,13},... | collective-permute-start | bytes 393224 | tf_op jit(solution)/shard_map/ppermute | solution.py:30
  14.0 4.8 %collective-permute-start.3 = (bf16[4,2,64,128]{3,2,0,1:T(8,128)(2,1)S(1)}, bf16[4,2,64,128]{3,2,0,1:T(8,128)(2,1)S(1)}, u32[]{:S(2)}, u32[]{:S(2)}) collective-permute-start(bf16[4,2,64,128]{3,2,0,1:T(8,128)(2,1)S(1)} %pad_maximum_fusion.3), channel_id=1, source_target_pairs={{0,8},{1,3},{2,10},{3,1},{4,12},{5,7},{6,14},{7,5},{8,0},{9,11},{1... | collective-permute-start | bytes 393224 | tf_op jit(solution)/shard_map/ppermute | solution.py:30
  18.9 9.2 %collective-permute-start.8 = (bf16[4,4,64,128]{3,2,1,0:T(8,128)(2,1)S(1)}, bf16[4,4,64,128]{3,2,1,0:T(8,128)(2,1)S(1)}, u32[]{:S(2)}, u32[]{:S(2)}) collective-permute-start(bf16[4,4,64,128]{3,2,1,0:T(8,128)(2,1)S(1)} %pad_maximum_fusion.1.p0), channel_id=1, source_target_pairs={{0,6},{1,25},{2,4},{3,27},{4,2},{5,29},{6,0},{7,31},{8,14},{9,17},... | collective-permute-start | bytes 786440 | tf_op jit(solution)/shard_map/ppermute | solution.py:30
  22.0 6.7 %collective-permute-start.7 = (bf16[4,4,64,128]{3,2,1,0:T(8,128)(2,1)S(1)}, bf16[4,4,64,128]{3,2,1,0:T(8,128)(2,1)S(1)}, u32[]{:S(2)}, u32[]{:S(2)}) collective-permute-start(bf16[4,4,64,128]{3,2,1,0:T(8,128)(2,1)S(1)} %pad_maximum_fusion.1.p0), channel_id=1, source_target_pairs={{0,4},{1,17},{2,6},{3,19},{4,0},{5,21},{6,2},{7,23},{8,12},{9,25},... | collective-permute-start | bytes 786440 | tf_op jit(solution)/shard_map/ppermute | solution.py:30
  22.0 7.5 %collective-permute-start.6 = (bf16[4,4,64,128]{3,2,1,0:T(8,128)(2,1)S(1)}, bf16[4,4,64,128]{3,2,1,0:T(8,128)(2,1)S(1)}, u32[]{:S(2)}, u32[]{:S(2)}) collective-permute-start(bf16[4,4,64,128]{3,2,1,0:T(8,128)(2,1)S(1)} %pad_maximum_fusion.1.p0), channel_id=1, source_target_pairs={{0,2},{1,9},{2,0},{3,11},{4,6},{5,13},{6,4},{7,15},{8,10},{9,1},{1... | collective-permute-start | bytes 786440 | tf_op jit(solution)/shard_map/ppermute | solution.py:30
  31.0 8.1 %collective-permute-start.10 = (f32[128,128]{1,0:T(8,128)S(1)}, f32[128,128]{1,0:T(8,128)S(1)}, u32[]{:S(2)}, u32[]{:S(2)}) collective-permute-start(f32[128,128]{1,0:T(8,128)S(1)} %precondition.2), channel_id=1, source_target_pairs={{0,1},{1,0},{2,3},{3,2},{4,5},{5,4},{6,7},{7,6},{8,9},{9,8},{10,11... | collective-permute-start | bytes 196616 | tf_op jit(solution)/shard_map/ppermute | solution.py:30
  35.8 17.8 %collective-permute-start.17 = (bf16[4,4,64,128]{3,2,1,0:T(8,128)(2,1)S(1)}, bf16[4,4,64,128]{3,2,1,0:T(8,128)(2,1)S(1)}, u32[]{:S(2)}, u32[]{:S(2)}) collective-permute-start(bf16[4,4,64,128]{3,2,1,0:T(8,128)(2,1)S(1)} %pad_maximum_fusion.2.p0), channel_id=1, source_target_pairs={{0,6},{1,25},{2,4},{3,27},{4,2},{5,29},{6,0},{7,31},{8,14},{9,17},... | collective-permute-start | bytes 786440 | tf_op jit(solution)/shard_map/ppermute | solution.py:30
  37.5 16.1 %collective-permute-start.16 = (bf16[4,4,64,128]{3,2,1,0:T(8,128)(2,1)S(1)}, bf16[4,4,64,128]{3,2,1,0:T(8,128)(2,1)S(1)}, u32[]{:S(2)}, u32[]{:S(2)}) collective-permute-start(bf16[4,4,64,128]{3,2,1,0:T(8,128)(2,1)S(1)} %pad_maximum_fusion.2.p0), channel_id=1, source_target_pairs={{0,4},{1,17},{2,6},{3,19},{4,0},{5,21},{6,2},{7,23},{8,12},{9,25},... | collective-permute-start | bytes 786440 | tf_op jit(solution)/shard_map/ppermute | solution.py:30
  37.8 15.8 %collective-permute-start.15 = (bf16[4,4,64,128]{3,2,1,0:T(8,128)(2,1)S(1)}, bf16[4,4,64,128]{3,2,1,0:T(8,128)(2,1)S(1)}, u32[]{:S(2)}, u32[]{:S(2)}) collective-permute-start(bf16[4,4,64,128]{3,2,1,0:T(8,128)(2,1)S(1)} %pad_maximum_fusion.2.p0), channel_id=1, source_target_pairs={{0,2},{1,9},{2,0},{3,11},{4,6},{5,13},{6,4},{7,15},{8,10},{9,1},{1... | collective-permute-start | bytes 786440 | tf_op jit(solution)/shard_map/ppermute | solution.py:30
  39.1 4.8 %collective-permute-start.14 = (bf16[128,128]{1,0:T(8,128)(2,1)S(1)}, bf16[128,128]{1,0:T(8,128)(2,1)S(1)}, u32[]{:S(2)}, u32[]{:S(2)}) collective-permute-start(bf16[128,128]{1,0:T(8,128)(2,1)S(1)} %add_convert_fusion.1), channel_id=1, source_target_pairs={{0,192},{1,224},{2,194},{3,226},{4,196},{5,228},{6,198},{7,230},{8... | collective-permute-start | bytes 98312 | tf_op jit(solution)/shard_map/ppermute | solution.py:30
  42.8 5.6 %collective-permute-start.13 = (bf16[128,128]{1,0:T(8,128)(2,1)S(1)}, bf16[128,128]{1,0:T(8,128)(2,1)S(1)}, u32[]{:S(2)}, u32[]{:S(2)}) collective-permute-start(bf16[128,128]{1,0:T(8,128)(2,1)S(1)} %add_convert_fusion.1), channel_id=1, source_target_pairs={{0,64},{1,96},{2,66},{3,98},{4,68},{5,100},{6,70},{7,102},{8,72},{... | collective-permute-start | bytes 98312 | tf_op jit(solution)/shard_map/ppermute | solution.py:30
  43.9 6.7 %collective-permute-start.12 = (bf16[128,128]{1,0:T(8,128)(2,1)S(1)}, bf16[128,128]{1,0:T(8,128)(2,1)S(1)}, u32[]{:S(2)}, u32[]{:S(2)}) collective-permute-start(bf16[128,128]{1,0:T(8,128)(2,1)S(1)} %add_convert_fusion.1), channel_id=1, source_target_pairs={{0,128},{1,160},{2,130},{3,162},{4,132},{5,164},{6,134},{7,166},{8... | collective-permute-start | bytes 98312 | tf_op jit(solution)/shard_map/ppermute | solution.py:30
  48.4 5.1 %collective-permute-start.11 = (bf16[128,128]{1,0:T(8,128)(2,1)S(1)}, bf16[128,128]{1,0:T(8,128)(2,1)S(1)}, u32[]{:S(2)}, u32[]{:S(2)}) collective-permute-start(bf16[128,128]{1,0:T(8,128)(2,1)S(1)} %add_convert_fusion.1), channel_id=1, source_target_pairs={{0,0},{1,32},{2,2},{3,34},{4,4},{5,36},{6,6},{7,38},{8,8},{9,40},{... | collective-permute-start | bytes 98312 | tf_op jit(solution)/shard_map/ppermute | solution.py:30
  55.0 3.7 %collective-permute-start.22 = (f32[128,128]{1,0:T(8,128)S(1)}, f32[128,128]{1,0:T(8,128)S(1)}, u32[]{:S(2)}, u32[]{:S(2)}) collective-permute-start(f32[128,128]{1,0:T(8,128)S(1)} %precondition.3), channel_id=1, source_target_pairs={{0,1},{1,0},{2,3},{3,2},{4,5},{5,4},{6,7},{7,6},{8,9},{9,8},{10,11... | collective-permute-start | bytes 196616 | tf_op jit(solution)/shard_map/ppermute | solution.py:30
  55.5 5.8 %collective-permute-start.21 = (bf16[2,128,256]{2,1,0:T(8,128)(2,1)S(1)}, bf16[2,128,256]{2,1,0:T(8,128)(2,1)S(1)}, u32[]{:S(2)}, u32[]{:S(2)}) collective-permute-start(bf16[2,128,256]{2,1,0:T(8,128)(2,1)S(1)} %pad_maximum_fusion.4), channel_id=1, source_target_pairs={{0,24},{1,7},{2,26},{3,5},{4,28},{5,3},{6,30},{7,1},{8,16},{9,15},... | collective-permute-start | bytes 393224 | tf_op jit(solution)/shard_map/ppermute | solution.py:30
  58.0 5.6 %collective-permute-start.20 = (bf16[2,128,256]{2,1,0:T(8,128)(2,1)S(1)}, bf16[2,128,256]{2,1,0:T(8,128)(2,1)S(1)}, u32[]{:S(2)}, u32[]{:S(2)}) collective-permute-start(bf16[2,128,256]{2,1,0:T(8,128)(2,1)S(1)} %pad_maximum_fusion.4), channel_id=1, source_target_pairs={{0,16},{1,5},{2,18},{3,7},{4,20},{5,1},{6,22},{7,3},{8,24},{9,13},... | collective-permute-start | bytes 393224 | tf_op jit(solution)/shard_map/ppermute | solution.py:30
  58.5 5.1 %collective-permute-start.19 = (bf16[2,128,256]{2,1,0:T(8,128)(2,1)S(1)}, bf16[2,128,256]{2,1,0:T(8,128)(2,1)S(1)}, u32[]{:S(2)}, u32[]{:S(2)}) collective-permute-start(bf16[2,128,256]{2,1,0:T(8,128)(2,1)S(1)} %pad_maximum_fusion.4), channel_id=1, source_target_pairs={{0,8},{1,3},{2,10},{3,1},{4,12},{5,7},{6,14},{7,5},{8,0},{9,11},{1... | collective-permute-start | bytes 393224 | tf_op jit(solution)/shard_map/ppermute | solution.py:30
  63.6 15.2 %collective-permute-start.26 = (bf16[4,2,128,256]{3,2,1,0:T(8,128)(2,1)S(1)}, bf16[4,2,128,256]{3,2,1,0:T(8,128)(2,1)S(1)}, u32[]{:S(2)}, u32[]{:S(2)}) collective-permute-start(bf16[4,2,128,256]{3,2,1,0:T(8,128)(2,1)S(1)} %pad_maximum_fusion.piece), channel_id=1, source_target_pairs={{0,6},{1,25},{2,4},{3,27},{4,2},{5,29},{6,0},{7,31},{8,14},{9,17},... | collective-permute-start | bytes 1572872 | tf_op jit(solution)/shard_map/ppermute | solution.py:30
  65.1 16.1 %collective-permute-start.25 = (bf16[4,2,128,256]{3,2,1,0:T(8,128)(2,1)S(1)}, bf16[4,2,128,256]{3,2,1,0:T(8,128)(2,1)S(1)}, u32[]{:S(2)}, u32[]{:S(2)}) collective-permute-start(bf16[4,2,128,256]{3,2,1,0:T(8,128)(2,1)S(1)} %pad_maximum_fusion.piece), channel_id=1, source_target_pairs={{0,4},{1,17},{2,6},{3,19},{4,0},{5,21},{6,2},{7,23},{8,12},{9,25},... | collective-permute-start | bytes 1572872 | tf_op jit(solution)/shard_map/ppermute | solution.py:30
  65.4 16.7 %collective-permute-start.24 = (bf16[4,2,128,256]{3,2,1,0:T(8,128)(2,1)S(1)}, bf16[4,2,128,256]{3,2,1,0:T(8,128)(2,1)S(1)}, u32[]{:S(2)}, u32[]{:S(2)}) collective-permute-start(bf16[4,2,128,256]{3,2,1,0:T(8,128)(2,1)S(1)} %pad_maximum_fusion.piece), channel_id=1, source_target_pairs={{0,2},{1,9},{2,0},{3,11},{4,6},{5,13},{6,4},{7,15},{8,10},{9,1},{1... | collective-permute-start | bytes 1572872 | tf_op jit(solution)/shard_map/ppermute | solution.py:30
  67.0 6.7 %collective-permute-start.23 = (bf16[128,128]{1,0:T(8,128)(2,1)S(1)}, bf16[128,128]{1,0:T(8,128)(2,1)S(1)}, u32[]{:S(2)}, u32[]{:S(2)}) collective-permute-start(bf16[128,128]{1,0:T(8,128)(2,1)S(1)} %add_convert_fusion), channel_id=1, source_target_pairs={{0,128},{1,129},{2,130},{3,131},{4,132},{5,133},{6,134},{7,135},{8... | collective-permute-start | bytes 98312 | tf_op jit(solution)/shard_map/ppermute | solution.py:30
  74.5 9.1 %collective-permute-start.27 = (f32[64,1024]{1,0:T(8,128)S(1)}, f32[64,1024]{1,0:T(8,128)S(1)}, u32[]{:S(2)}, u32[]{:S(2)}) collective-permute-start(f32[64,1024]{1,0:T(8,128)S(1)} %get-tuple-element.29), channel_id=1, source_target_pairs={{0,1},{1,0},{2,3},{3,2},{4,5},{5,4},{6,7},{7,6},{8,9},{9,8},{10,11... | collective-permute-start | bytes 786440 | tf_op jit(solution)/shard_map/ppermute | solution.py:30
  79.7 3.9 %collective-permute-start.30 = (f32[64,1024]{1,0:T(8,128)S(1)}, f32[64,1024]{1,0:T(8,128)S(1)}, u32[]{:S(2)}, u32[]{:S(2)}) collective-permute-start(f32[64,1024]{1,0:T(8,128)S(1)} %get-tuple-element.32), channel_id=1, source_target_pairs={{0,1},{1,0},{2,3},{3,2},{4,5},{5,4},{6,7},{7,6},{8,9},{9,8},{10,11... | collective-permute-start | bytes 786440 | tf_op jit(solution)/shard_map/ppermute | solution.py:30
  82.0 1.6 %collective-permute-start.29 = (f32[64,1024]{1,0:T(8,128)S(1)}, f32[64,1024]{1,0:T(8,128)S(1)}, u32[]{:S(2)}, u32[]{:S(2)}) collective-permute-start(f32[64,1024]{1,0:T(8,128)S(1)} %get-tuple-element.31), channel_id=1, source_target_pairs={{0,1},{1,0},{2,3},{3,2},{4,5},{5,4},{6,7},{7,6},{8,9},{9,8},{10,11... | collective-permute-start | bytes 786440 | tf_op jit(solution)/shard_map/ppermute | solution.py:30
  83.0 1.7 %collective-permute-start.28 = (f32[64,1024]{1,0:T(8,128)S(1)}, f32[64,1024]{1,0:T(8,128)S(1)}, u32[]{:S(2)}, u32[]{:S(2)}) collective-permute-start(f32[64,1024]{1,0:T(8,128)S(1)} %get-tuple-element.30), channel_id=1, source_target_pairs={{0,1},{1,0},{2,3},{3,2},{4,5},{5,4},{6,7},{7,6},{8,9},{9,8},{10,11... | collective-permute-start | bytes 786440 | tf_op jit(solution)/shard_map/ppermute | solution.py:30
  (1 other events, 20.0 us)

commit v11 on v10

--- a/solution.py
+++ b/solution.py
@@ -1,3 +1,5 @@
+import functools
+
 import jax
 import jax.numpy as jnp
 from jax import lax
@@ -74,7 +76,7 @@
     return pl.multiple_of(((z * 4 + y) * 4 + x) * 128, 128)
 
 
-def precondition(where, p0, p1, p2, p3, low, high, pre):
+def precondition(flip, where, p0, p1, p2, p3, low, high, pre):
     total = jnp.zeros((128, 128), jnp.float32)
     none = jnp.zeros((64, 128), jnp.bfloat16)
     for k3, piece in enumerate((p0, p1, p2, p3)):
@@ -100,14 +102,14 @@
                 jnp.concatenate(held, axis=0),
                 preferred_element_type=jnp.float32,
             )
-    pre[...] = total
+    pre[...] = total.T if flip else total
 
 
 def tile(where, g, piece, keep, give):
-    part = lax.dot_general(
+    blocks = [piece[k2, j] for k2 in range(4) for j in range(2)]
+    part = jnp.dot(
         g[...],
-        piece[...].reshape(1024, 256),
-        (((1,), (1,)), ((), ())),
+        jnp.concatenate(blocks, axis=1),
         preferred_element_type=jnp.float32,
     ) * (1.0 / TOKENS)
     low, high = part[:64], part[64:]
@@ -173,21 +175,26 @@
         theirs = swap_cores(rows)
         return jnp.where(first, rows, theirs), jnp.where(first, theirs, rows)
 
-    def partial(pieces, rows):
+    def partial(pieces, rows, flip):
         return call(
-            precondition, "precondition", shape((128, 128), f32), [SMEM] + [VMEM] * 6
+            functools.partial(precondition, flip),
+            "precondition",
+            shape((128, 128), f32),
+            [SMEM] + [VMEM] * 6,
         )(where, *pieces, *rows)
 
     act_rows, grad_rows = factor(act_inverse), factor(grad_inverse)
-    part = partial(turned(second_turn, [act_plane] * 4), act_rows)
+    part = partial(turned(second_turn, [act_plane] * 4), act_rows, True)
     part, grad_plane = lax.optimization_barrier((part, grad_plane))
     act = (part + swap_cores(part)).astype(bf16)
-    grad_pieces = turned(second_turn, [grad_plane] * 4)
+    half = jnp.stack([grad_plane, second_turn(grad_plane, 1)])
+    rest = second_turn(half, 3)
+    grad_pieces = half[0], half[1], rest[1], rest[0]
 
     here = [to_parity(act, j, 0) for j in (0, 1)]
     there = [to_parity(act, j, 1) for j in (0, 1)]
-    pair = jnp.stack([jnp.concatenate(p, axis=1) for p in zip(here, there)])
-    part = partial(grad_pieces, grad_rows)
+    pair = jnp.stack([jnp.concatenate(p, axis=0) for p in zip(here, there)])
+    part = partial(grad_pieces, grad_rows, False)
     pair, part = lax.optimization_barrier((pair, part))
     grad = (part + swap_cores(part)).astype(bf16)
     plane = jnp.stack(turned(first_turn, [pair] * 4))

time: 87.2 us -> 86.8 us (level)
    ppermute x31 -> x30, waiting for transfers between devices: 27.2 us -> 26.9 us  [send(): return lax.ppermute(value, AXES, pairs)]
    ppermute x31 -> x30, starting transfers between devices: 49.5 us -> 49.5 us  [send(): return lax.ppermute(value, AXES, pairs)]
  transfers between devices with their start and end apart: 31 -> 30, of which waited for: 14 -> 16; matrix products, arithmetic and copies ran while one was open for 1% -> 1% of each run, Pallas kernels for 6% -> 5%
where the time goes in v11:
time: 86.8 us; the launch traced here: 86.5 us
  starting transfers between devices  49.5 us (57%)
  waiting for transfers between devices  26.9 us (31%)
  Pallas kernels  8.11 us (9%)
  other arithmetic  1.57 us (2%)
    ppermute x30, starting transfers between devices, send(): return lax.ppermute(value, AXES, pairs)  49.5 us
    ppermute x30, waiting for transfers between devices, send(): return lax.ppermute(value, AXES, pairs)  26.9 us
    pallas_call x4, Pallas kernels, on_device(): call(tile, 'tile', [shape((64, 1024), f32)] * 2, [SMEM, VMEM, VMEM])  3.1 us
    pallas_call x2, Pallas kernels, partial(): call(functools.partial(precondition, flip), 'precondition', shape((128, 1...  2.91 us
    pallas_call x1, Pallas kernels, on_device(): pl.pallas_call(assemble, out_shape=shape((64, 8192), f32), in_specs=[SMEM...  2.1 us
  transfers between devices with their start and end apart: 30, of which 16 were waited for; matrix products, arithmetic and copies ran while one was open for 1% of the time, Pallas kernels for 5%

profile of v11, /device:TPU:1, one launch (start us, length us, event | category | flops | bytes accessed | tf_op | source)
XLA Modules:
  0.0 86.5 jit_solution(15823629702163220433)
XLA Ops:
  0.8 3.8 %collective-permute-start.1 = (bf16[2,64,128]{2,1,0:T(8,128)(2,1)S(1)}, bf16[2,64,128]{2,1,0:T(8,128)(2,1)S(1)}, u32[]{:S(2)}, u32[]{:S(2)}) collective-permute-start(bf16[2,64,128]{2,1,0:T(8,128)(2,1)S(1)} %get-tuple-element.48), channel_id=1, source_target_pairs={{0,64},{1,65},{2,66},{3,67},{4,68},{5,69},{6,70},{7,71},{8,72},{9,... | collective-permute-start | bytes 98312 | tf_op jit(solution)/shard_map/ppermute | solution.py:32
  4.7 1.6 %collective-permute-start = (bf16[2,64,128]{2,1,0:T(8,128)(2,1)S(1)}, bf16[2,64,128]{2,1,0:T(8,128)(2,1)S(1)}, u32[]{:S(2)}, u32[]{:S(2)}) collective-permute-start(bf16[2,64,128]{2,1,0:T(8,128)(2,1)S(1)} %get-tuple-element.48), channel_id=1, source_target_pairs={{0,32},{1,33},{2,34},{3,35},{4,36},{5,37},{6,38},{7,39},{8,40},{9,... | collective-permute-start | bytes 98312 | tf_op jit(solution)/shard_map/ppermute | solution.py:32
  6.3 2.2 %collective-permute-start.9 = (bf16[64,8192]{1,0:T(8,128)(2,1)}, bf16[64,8192]{1,0:T(8,128)(2,1)S(1)}, u32[]{:S(2)}, u32[]{:S(2)}) collective-permute-start(bf16[64,8192]{1,0:T(8,128)(2,1)} %param.6), channel_id=1, source_target_pairs={{0,1},{1,0},{2,3},{3,2},{4,5},{5,4},{6,7},{7,6},{8,9},{9,8},{10,11... | collective-permute-start | bytes 3145736 | tf_op jit(solution)/shard_map/ppermute | solution.py:32
  8.5 2.3 %collective-permute-done.2 = bf16[2,64,128]{2,1,0:T(8,128)(2,1)S(1)} collective-permute-done((bf16[2,64,128]{2,1,0:T(8,128)(2,1)S(1)}, bf16[2,64,128]{2,1,0:T(8,128)(2,1)S(1)}, u32[]{:S(2)}, u32[]{:S(2)}) %collective-permute-start.2) | collective-permute-done | bytes 32800 | tf_op jit(solution)/shard_map/ppermute | solution.py:32
  10.9 2.6 %collective-permute-start.5 = (bf16[4,2,64,128]{3,2,0,1:T(8,128)(2,1)S(1)}, bf16[4,2,64,128]{3,2,0,1:T(8,128)(2,1)S(1)}, u32[]{:S(2)}, u32[]{:S(2)}) collective-permute-start(bf16[4,2,64,128]{3,2,0,1:T(8,128)(2,1)S(1)} %pad_maximum_fusion.4), channel_id=1, source_target_pairs={{0,24},{1,7},{2,26},{3,5},{4,28},{5,3},{6,30},{7,1},{8,16},{9,15},... | collective-permute-start | bytes 393224 | tf_op jit(solution)/shard_map/ppermute | solution.py:32
  14.2 2.5 %collective-permute-done.5 = bf16[4,2,64,128]{3,2,0,1:T(8,128)(2,1)S(1)} collective-permute-done((bf16[4,2,64,128]{3,2,0,1:T(8,128)(2,1)S(1)}, bf16[4,2,64,128]{3,2,0,1:T(8,128)(2,1)S(1)}, u32[]{:S(2)}, u32[]{:S(2)}) %collective-permute-start.5) | collective-permute-done | bytes 131104 | tf_op jit(solution)/shard_map/ppermute | solution.py:32
  16.8 2.0 %collective-permute-done.4 = bf16[4,2,64,128]{3,2,0,1:T(8,128)(2,1)S(1)} collective-permute-done((bf16[4,2,64,128]{3,2,0,1:T(8,128)(2,1)S(1)}, bf16[4,2,64,128]{3,2,0,1:T(8,128)(2,1)S(1)}, u32[]{:S(2)}, u32[]{:S(2)}) %collective-permute-start.4) | collective-permute-done | bytes 131104 | tf_op jit(solution)/shard_map/ppermute | solution.py:32
  18.9 3.1 %collective-permute-start.8 = (bf16[4,4,64,128]{3,2,1,0:T(8,128)(2,1)S(1)}, bf16[4,4,64,128]{3,2,1,0:T(8,128)(2,1)S(1)}, u32[]{:S(2)}, u32[]{:S(2)}) collective-permute-start(bf16[4,4,64,128]{3,2,1,0:T(8,128)(2,1)S(1)} %pad_maximum_fusion.2.p0), channel_id=1, source_target_pairs={{0,6},{1,25},{2,4},{3,27},{4,2},{5,29},{6,0},{7,31},{8,14},{9,17},... | collective-permute-start | bytes 786440 | tf_op jit(solution)/shard_map/ppermute | solution.py:32
  22.9 5.2 %collective-permute-done.8.p3 = bf16[4,4,64,128]{3,2,1,0:T(8,128)(2,1)S(1)} collective-permute-done((bf16[4,4,64,128]{3,2,1,0:T(8,128)(2,1)S(1)}, bf16[4,4,64,128]{3,2,1,0:T(8,128)(2,1)S(1)}, u32[]{:S(2)}, u32[]{:S(2)}) %collective-permute-start.8) | collective-permute-done | bytes 262176 | tf_op jit(solution)/shard_map/ppermute | solution.py:32
  29.6 1.5 %precondition.2 = f32[128,128]{1,0:T(8,128)S(1)} custom-call(s32[4]{0:T(128)S(1)} %pad_add_fusion.where, bf16[4,4,64,128]{3,2,1,0:T(8,128)(2,1)S(1)} %pad_maximum_fusion.2.p0, bf16[4,4,64,128]{3,2,1,0:T(8,128)(2,1)S(1)} %collective-permute-done.6.p1, bf16[4,4,64,128]{3,2,1,0:T(8,128)(2,1)S(1)} %collective-permute-done.7.p2, ...), custom_call_target="tpu_custom_call" | custom-call | tf_op jit(solution)/shard_map/precondition/pallas_call | solution.py:179
  31.0 4.8 %collective-permute-start.10 = (f32[128,128]{1,0:T(8,128)S(1)}, f32[128,128]{1,0:T(8,128)S(1)}, u32[]{:S(2)}, u32[]{:S(2)}) collective-permute-start(f32[128,128]{1,0:T(8,128)S(1)} %precondition.2), channel_id=1, source_target_pairs={{0,1},{1,0},{2,3},{3,2},{4,5},{5,4},{6,7},{7,6},{8,9},{9,8},{10,11... | collective-permute-start | bytes 196616 | tf_op jit(solution)/shard_map/ppermute | solution.py:32
  36.8 3.5 %collective-permute-start.14 = (bf16[128,128]{1,0:T(8,128)(2,1)S(1)}, bf16[128,128]{1,0:T(8,128)(2,1)S(1)}, u32[]{:S(2)}, u32[]{:S(2)}) collective-permute-start(bf16[128,128]{1,0:T(8,128)(2,1)S(1)} %add_convert_fusion.1), channel_id=1, source_target_pairs={{0,192},{1,224},{2,194},{3,226},{4,196},{5,228},{6,198},{7,230},{8... | collective-permute-start | bytes 98312 | tf_op jit(solution)/shard_map/ppermute | solution.py:32
  40.4 1.0 %collective-permute-done.15.p1 = bf16[4,4,64,128]{3,2,1,0:T(8,128)(2,1)S(1)} collective-permute-done((bf16[4,4,64,128]{3,2,1,0:T(8,128)(2,1)S(1)}, bf16[4,4,64,128]{3,2,1,0:T(8,128)(2,1)S(1)}, u32[]{:S(2)}, u32[]{:S(2)}) %collective-permute-start.15) | collective-permute-done | bytes 262176 | tf_op jit(solution)/shard_map/ppermute | solution.py:32
  41.4 1.7 %collective-permute-start.16 = (bf16[2,4,4,64,128]{4,3,2,1,0:T(8,128)(2,1)S(1)}, bf16[2,4,4,64,128]{4,3,2,1,0:T(8,128)(2,1)S(1)}, u32[]{:S(2)}, u32[]{:S(2)}) collective-permute-start(bf16[2,4,4,64,128]{4,3,2,1,0:T(8,128)(2,1)S(1)} %pad_maximum_fusion), channel_id=1, source_target_pairs={{0,6},{1,25},{2,4},{3,27},{4,2},{5,29},{6,0},{7,31},{8,14},{9,17},... | collective-permute-start | bytes 1572872 | tf_op jit(solution)/shard_map/ppermute | solution.py:32
  43.5 4.1 %collective-permute-start.12 = (bf16[128,128]{1,0:T(8,128)(2,1)S(1)}, bf16[128,128]{1,0:T(8,128)(2,1)S(1)}, u32[]{:S(2)}, u32[]{:S(2)}) collective-permute-start(bf16[128,128]{1,0:T(8,128)(2,1)S(1)} %add_convert_fusion.1), channel_id=1, source_target_pairs={{0,128},{1,160},{2,130},{3,162},{4,132},{5,164},{6,134},{7,166},{8... | collective-permute-start | bytes 98312 | tf_op jit(solution)/shard_map/ppermute | solution.py:32
  47.5 2.1 %collective-permute-start.11 = (bf16[128,128]{1,0:T(8,128)(2,1)S(1)}, bf16[128,128]{1,0:T(8,128)(2,1)S(1)}, u32[]{:S(2)}, u32[]{:S(2)}) collective-permute-start(bf16[128,128]{1,0:T(8,128)(2,1)S(1)} %add_convert_fusion.1), channel_id=1, source_target_pairs={{0,0},{1,32},{2,2},{3,34},{4,4},{5,36},{6,6},{7,38},{8,8},{9,40},{... | collective-permute-start | bytes 98312 | tf_op jit(solution)/shard_map/ppermute | solution.py:32
  49.7 2.8 %collective-permute-done.11 = bf16[128,128]{1,0:T(8,128)(2,1)S(1)} collective-permute-done((bf16[128,128]{1,0:T(8,128)(2,1)S(1)}, bf16[128,128]{1,0:T(8,128)(2,1)S(1)}, u32[]{:S(2)}, u32[]{:S(2)}) %collective-permute-start.11) | collective-permute-done | bytes 32800 | tf_op jit(solution)/shard_map/ppermute | solution.py:32
  52.5 1.4 %precondition.3 = f32[128,128]{1,0:T(8,128)S(1)} custom-call(s32[4]{0:T(128)S(1)} %pad_add_fusion.where, bf16[4,4,64,128]{3,2,1,0:T(8,128)(2,1)S(1)} %pad_maximum_fusion.3.p0, bf16[4,4,64,128]{3,2,1,0:T(8,128)(2,1)S(1)} %collective-permute-done.15.p1, bf16[4,4,64,128]{3,2,1,0:T(8,128)(2,1)S(1)} %get-tuple-element.38.p2, ...), custom_call_target="tpu_custom_call" | custom-call | tf_op jit(solution)/shard_map/precondition/pallas_call | solution.py:179
  54.0 1.3 %collective-permute-start.21 = (f32[128,128]{1,0:T(8,128)S(1)}, f32[128,128]{1,0:T(8,128)S(1)}, u32[]{:S(2)}, u32[]{:S(2)}) collective-permute-start(f32[128,128]{1,0:T(8,128)S(1)} %precondition.3), channel_id=1, source_target_pairs={{0,1},{1,0},{2,3},{3,2},{4,5},{5,4},{6,7},{7,6},{8,9},{9,8},{10,11... | collective-permute-start | bytes 196616 | tf_op jit(solution)/shard_map/ppermute | solution.py:32
  55.3 1.6 %collective-permute-start.20 = (bf16[2,256,128]{2,1,0:T(8,128)(2,1)S(1)}, bf16[2,256,128]{2,1,0:T(8,128)(2,1)S(1)}, u32[]{:S(2)}, u32[]{:S(2)}) collective-permute-start(bf16[2,256,128]{2,1,0:T(8,128)(2,1)S(1)} %pad_maximum_fusion.5), channel_id=1, source_target_pairs={{0,24},{1,7},{2,26},{3,5},{4,28},{5,3},{6,30},{7,1},{8,16},{9,15},... | collective-permute-start | bytes 393224 | tf_op jit(solution)/shard_map/ppermute | solution.py:32
  56.9 1.7 %collective-permute-start.18 = (bf16[2,256,128]{2,1,0:T(8,128)(2,1)S(1)}, bf16[2,256,128]{2,1,0:T(8,128)(2,1)S(1)}, u32[]{:S(2)}, u32[]{:S(2)}) collective-permute-start(bf16[2,256,128]{2,1,0:T(8,128)(2,1)S(1)} %pad_maximum_fusion.5), channel_id=1, source_target_pairs={{0,8},{1,3},{2,10},{3,1},{4,12},{5,7},{6,14},{7,5},{8,0},{9,11},{1... | collective-permute-start | bytes 393224 | tf_op jit(solution)/shard_map/ppermute | solution.py:32
  58.5 2.1 %collective-permute-done.20 = bf16[2,256,128]{2,1,0:T(8,128)(2,1)S(1)} collective-permute-done((bf16[2,256,128]{2,1,0:T(8,128)(2,1)S(1)}, bf16[2,256,128]{2,1,0:T(8,128)(2,1)S(1)}, u32[]{:S(2)}, u32[]{:S(2)}) %collective-permute-start.20) | collective-permute-done | bytes 131104 | tf_op jit(solution)/shard_map/ppermute | solution.py:32
  60.6 1.9 %collective-permute-done.19 = bf16[2,256,128]{2,1,0:T(8,128)(2,1)S(1)} collective-permute-done((bf16[2,256,128]{2,1,0:T(8,128)(2,1)S(1)}, bf16[2,256,128]{2,1,0:T(8,128)(2,1)S(1)}, u32[]{:S(2)}, u32[]{:S(2)}) %collective-permute-start.19) | collective-permute-done | bytes 131104 | tf_op jit(solution)/shard_map/ppermute | solution.py:32
  62.7 1.7 %collective-permute-start.25 = (bf16[4,2,256,128]{3,2,1,0:T(8,128)(2,1)S(1)}, bf16[4,2,256,128]{3,2,1,0:T(8,128)(2,1)S(1)}, u32[]{:S(2)}, u32[]{:S(2)}) collective-permute-start(bf16[4,2,256,128]{3,2,1,0:T(8,128)(2,1)S(1)} %pad_maximum_fusion.1.piece), channel_id=1, source_target_pairs={{0,6},{1,25},{2,4},{3,27},{4,2},{5,29},{6,0},{7,31},{8,14},{9,17},... | collective-permute-start | bytes 1572872 | tf_op jit(solution)/shard_map/ppermute | solution.py:32
  64.7 1.3 %collective-permute-start.23 = (bf16[4,2,256,128]{3,2,1,0:T(8,128)(2,1)S(1)}, bf16[4,2,256,128]{3,2,1,0:T(8,128)(2,1)S(1)}, u32[]{:S(2)}, u32[]{:S(2)}) collective-permute-start(bf16[4,2,256,128]{3,2,1,0:T(8,128)(2,1)S(1)} %pad_maximum_fusion.1.piece), channel_id=1, source_target_pairs={{0,2},{1,9},{2,0},{3,11},{4,6},{5,13},{6,4},{7,15},{8,10},{9,1},{1... | collective-permute-start | bytes 1572872 | tf_op jit(solution)/shard_map/ppermute | solution.py:32
  66.0 4.1 %collective-permute-start.22 = (bf16[128,128]{1,0:T(8,128)(2,1)S(1)}, bf16[128,128]{1,0:T(8,128)(2,1)S(1)}, u32[]{:S(2)}, u32[]{:S(2)}) collective-permute-start(bf16[128,128]{1,0:T(8,128)(2,1)S(1)} %add_convert_fusion), channel_id=1, source_target_pairs={{0,128},{1,129},{2,130},{3,131},{4,132},{5,133},{6,134},{7,135},{8... | collective-permute-start | bytes 98312 | tf_op jit(solution)/shard_map/ppermute | solution.py:32
  70.1 2.6 %collective-permute-done.22 = bf16[128,128]{1,0:T(8,128)(2,1)S(1)} collective-permute-done((bf16[128,128]{1,0:T(8,128)(2,1)S(1)}, bf16[128,128]{1,0:T(8,128)(2,1)S(1)}, u32[]{:S(2)}, u32[]{:S(2)}) %collective-permute-start.22) | collective-permute-done | bytes 32800 | tf_op jit(solution)/shard_map/ppermute | solution.py:32
  73.5 3.3 %collective-permute-start.26 = (f32[64,1024]{1,0:T(8,128)S(1)}, f32[64,1024]{1,0:T(8,128)S(1)}, u32[]{:S(2)}, u32[]{:S(2)}) collective-permute-start(f32[64,1024]{1,0:T(8,128)S(1)} %get-tuple-element.29), channel_id=1, source_target_pairs={{0,1},{1,0},{2,3},{3,2},{4,5},{5,4},{6,7},{7,6},{8,9},{9,8},{10,11... | collective-permute-start | bytes 786440 | tf_op jit(solution)/shard_map/ppermute | solution.py:32
  76.8 1.1 %collective-permute-done.25.piece = bf16[4,2,256,128]{3,2,1,0:T(8,128)(2,1)S(1)} collective-permute-done((bf16[4,2,256,128]{3,2,1,0:T(8,128)(2,1)S(1)}, bf16[4,2,256,128]{3,2,1,0:T(8,128)(2,1)S(1)}, u32[]{:S(2)}, u32[]{:S(2)}) %collective-permute-start.25) | collective-permute-done | bytes 524320 | tf_op jit(solution)/shard_map/ppermute | solution.py:32
  78.7 2.2 %collective-permute-start.29 = (f32[64,1024]{1,0:T(8,128)S(1)}, f32[64,1024]{1,0:T(8,128)S(1)}, u32[]{:S(2)}, u32[]{:S(2)}) collective-permute-start(f32[64,1024]{1,0:T(8,128)S(1)} %get-tuple-element.32), channel_id=1, source_target_pairs={{0,1},{1,0},{2,3},{3,2},{4,5},{5,4},{6,7},{7,6},{8,9},{9,8},{10,11... | collective-permute-start | bytes 786440 | tf_op jit(solution)/shard_map/ppermute | solution.py:32
  83.3 1.0 %collective-permute-done.27.refs_5_ = f32[64,1024]{1,0:T(8,128)S(1)} collective-permute-done((f32[64,1024]{1,0:T(8,128)S(1)}, f32[64,1024]{1,0:T(8,128)S(1)}, u32[]{:S(2)}, u32[]{:S(2)}) %collective-permute-start.27) | collective-permute-done | bytes 262176 | tf_op jit(solution)/shard_map/ppermute | solution.py:32
  84.3 2.1 %assemble.1 = f32[64,8192]{1,0:T(8,128)} custom-call(s32[4]{0:T(128)S(1)} %pad_add_fusion.where, f32[64,1024]{1,0:T(8,128)S(1)} %get-tuple-element.25.refs_0_, f32[64,1024]{1,0:T(8,128)S(1)} %get-tuple-element.26.refs_1_, f32[64,1024]{1,0:T(8,128)S(1)} %get-tuple-element.27.refs_2_, f32[64,1024]{1,0:T(8,128)S(1)} %get-tuple-element.28.refs_3_, ...), custom_call_target="tpu_custom_call" | custom-call | tf_op jit(solution)/shard_map/assemble/pallas_call | solution.py:212
  (60 shorter events, 10.0 us)
Async XLA Ops:
  0.0 22.7 %copy-start = (bf16[64,8192]{1,0:T(8,128)(2,1)S(1)}, bf16[64,8192]{1,0:T(8,128)(2,1)}, u32[]{:S(2)}) copy-start(bf16[64,8192]{1,0:T(8,128)(2,1)} %param.6) | copy-start | bytes 3145732
  0.8 7.7 %collective-permute-start.1 = (bf16[2,64,128]{2,1,0:T(8,128)(2,1)S(1)}, bf16[2,64,128]{2,1,0:T(8,128)(2,1)S(1)}, u32[]{:S(2)}, u32[]{:S(2)}) collective-permute-start(bf16[2,64,128]{2,1,0:T(8,128)(2,1)S(1)} %get-tuple-element.48), channel_id=1, source_target_pairs={{0,64},{1,65},{2,66},{3,67},{4,68},{5,69},{6,70},{7,71},{8,72},{9,... | collective-permute-start | bytes 98312 | tf_op jit(solution)/shard_map/ppermute | solution.py:32
  4.7 3.9 %collective-permute-start = (bf16[2,64,128]{2,1,0:T(8,128)(2,1)S(1)}, bf16[2,64,128]{2,1,0:T(8,128)(2,1)S(1)}, u32[]{:S(2)}, u32[]{:S(2)}) collective-permute-start(bf16[2,64,128]{2,1,0:T(8,128)(2,1)S(1)} %get-tuple-element.48), channel_id=1, source_target_pairs={{0,32},{1,33},{2,34},{3,35},{4,36},{5,37},{6,38},{7,39},{8,40},{9,... | collective-permute-start | bytes 98312 | tf_op jit(solution)/shard_map/ppermute | solution.py:32
  6.3 4.6 %collective-permute-start.2 = (bf16[2,64,128]{2,1,0:T(8,128)(2,1)S(1)}, bf16[2,64,128]{2,1,0:T(8,128)(2,1)S(1)}, u32[]{:S(2)}, u32[]{:S(2)}) collective-permute-start(bf16[2,64,128]{2,1,0:T(8,128)(2,1)S(1)} %get-tuple-element.48), channel_id=1, source_target_pairs={{0,96},{1,97},{2,98},{3,99},{4,100},{5,101},{6,102},{7,103},{8,104... | collective-permute-start | bytes 98312 | tf_op jit(solution)/shard_map/ppermute | solution.py:32
  6.3 16.4 %collective-permute-start.9 = (bf16[64,8192]{1,0:T(8,128)(2,1)}, bf16[64,8192]{1,0:T(8,128)(2,1)S(1)}, u32[]{:S(2)}, u32[]{:S(2)}) collective-permute-start(bf16[64,8192]{1,0:T(8,128)(2,1)} %param.6), channel_id=1, source_target_pairs={{0,1},{1,0},{2,3},{3,2},{4,5},{5,4},{6,7},{7,6},{8,9},{9,8},{10,11... | collective-permute-start | bytes 3145736 | tf_op jit(solution)/shard_map/ppermute | solution.py:32
  8.5 34.7 %collective-permute-start.17 = (bf16[64,8192]{1,0:T(8,128)(2,1)}, bf16[64,8192]{1,0:T(8,128)(2,1)S(1)}, u32[]{:S(2)}, u32[]{:S(2)}) collective-permute-start(bf16[64,8192]{1,0:T(8,128)(2,1)} %param.7), channel_id=1, source_target_pairs={{0,1},{1,0},{2,3},{3,2},{4,5},{5,4},{6,7},{7,6},{8,9},{9,8},{10,11... | collective-permute-start | bytes 3145736 | tf_op jit(solution)/shard_map/ppermute | solution.py:32
  10.9 5.9 %collective-permute-start.5 = (bf16[4,2,64,128]{3,2,0,1:T(8,128)(2,1)S(1)}, bf16[4,2,64,128]{3,2,0,1:T(8,128)(2,1)S(1)}, u32[]{:S(2)}, u32[]{:S(2)}) collective-permute-start(bf16[4,2,64,128]{3,2,0,1:T(8,128)(2,1)S(1)} %pad_maximum_fusion.4), channel_id=1, source_target_pairs={{0,24},{1,7},{2,26},{3,5},{4,28},{5,3},{6,30},{7,1},{8,16},{9,15},... | collective-permute-start | bytes 393224 | tf_op jit(solution)/shard_map/ppermute | solution.py:32
  13.4 5.3 %collective-permute-start.4 = (bf16[4,2,64,128]{3,2,0,1:T(8,128)(2,1)S(1)}, bf16[4,2,64,128]{3,2,0,1:T(8,128)(2,1)S(1)}, u32[]{:S(2)}, u32[]{:S(2)}) collective-permute-start(bf16[4,2,64,128]{3,2,0,1:T(8,128)(2,1)S(1)} %pad_maximum_fusion.4), channel_id=1, source_target_pairs={{0,16},{1,5},{2,18},{3,7},{4,20},{5,1},{6,22},{7,3},{8,24},{9,13},... | collective-permute-start | bytes 393224 | tf_op jit(solution)/shard_map/ppermute | solution.py:32
  14.0 4.8 %collective-permute-start.3 = (bf16[4,2,64,128]{3,2,0,1:T(8,128)(2,1)S(1)}, bf16[4,2,64,128]{3,2,0,1:T(8,128)(2,1)S(1)}, u32[]{:S(2)}, u32[]{:S(2)}) collective-permute-start(bf16[4,2,64,128]{3,2,0,1:T(8,128)(2,1)S(1)} %pad_maximum_fusion.4), channel_id=1, source_target_pairs={{0,8},{1,3},{2,10},{3,1},{4,12},{5,7},{6,14},{7,5},{8,0},{9,11},{1... | collective-permute-start | bytes 393224 | tf_op jit(solution)/shard_map/ppermute | solution.py:32
  18.9 9.2 %collective-permute-start.8 = (bf16[4,4,64,128]{3,2,1,0:T(8,128)(2,1)S(1)}, bf16[4,4,64,128]{3,2,1,0:T(8,128)(2,1)S(1)}, u32[]{:S(2)}, u32[]{:S(2)}) collective-permute-start(bf16[4,4,64,128]{3,2,1,0:T(8,128)(2,1)S(1)} %pad_maximum_fusion.2.p0), channel_id=1, source_target_pairs={{0,6},{1,25},{2,4},{3,27},{4,2},{5,29},{6,0},{7,31},{8,14},{9,17},... | collective-permute-start | bytes 786440 | tf_op jit(solution)/shard_map/ppermute | solution.py:32
  22.0 6.7 %collective-permute-start.7 = (bf16[4,4,64,128]{3,2,1,0:T(8,128)(2,1)S(1)}, bf16[4,4,64,128]{3,2,1,0:T(8,128)(2,1)S(1)}, u32[]{:S(2)}, u32[]{:S(2)}) collective-permute-start(bf16[4,4,64,128]{3,2,1,0:T(8,128)(2,1)S(1)} %pad_maximum_fusion.2.p0), channel_id=1, source_target_pairs={{0,4},{1,17},{2,6},{3,19},{4,0},{5,21},{6,2},{7,23},{8,12},{9,25},... | collective-permute-start | bytes 786440 | tf_op jit(solution)/shard_map/ppermute | solution.py:32
  22.0 7.5 %collective-permute-start.6 = (bf16[4,4,64,128]{3,2,1,0:T(8,128)(2,1)S(1)}, bf16[4,4,64,128]{3,2,1,0:T(8,128)(2,1)S(1)}, u32[]{:S(2)}, u32[]{:S(2)}) collective-permute-start(bf16[4,4,64,128]{3,2,1,0:T(8,128)(2,1)S(1)} %pad_maximum_fusion.2.p0), channel_id=1, source_target_pairs={{0,2},{1,9},{2,0},{3,11},{4,6},{5,13},{6,4},{7,15},{8,10},{9,1},{1... | collective-permute-start | bytes 786440 | tf_op jit(solution)/shard_map/ppermute | solution.py:32
  29.6 13.6 %copy-start.1 = (bf16[64,8192]{1,0:T(8,128)(2,1)S(1)}, bf16[64,8192]{1,0:T(8,128)(2,1)}, u32[]{:S(2)}) copy-start(bf16[64,8192]{1,0:T(8,128)(2,1)} %param.7) | copy-start | bytes 3145732
  31.0 5.7 %collective-permute-start.10 = (f32[128,128]{1,0:T(8,128)S(1)}, f32[128,128]{1,0:T(8,128)S(1)}, u32[]{:S(2)}, u32[]{:S(2)}) collective-permute-start(f32[128,128]{1,0:T(8,128)S(1)} %precondition.2), channel_id=1, source_target_pairs={{0,1},{1,0},{2,3},{3,2},{4,5},{5,4},{6,7},{7,6},{8,9},{9,8},{10,11... | collective-permute-start | bytes 196616 | tf_op jit(solution)/shard_map/ppermute | solution.py:32
  35.9 5.5 %collective-permute-start.15 = (bf16[4,4,64,128]{3,2,1,0:T(8,128)(2,1)S(1)}, bf16[4,4,64,128]{3,2,1,0:T(8,128)(2,1)S(1)}, u32[]{:S(2)}, u32[]{:S(2)}) collective-permute-start(bf16[4,4,64,128]{3,2,1,0:T(8,128)(2,1)S(1)} %pad_maximum_fusion.3.p0), channel_id=1, source_target_pairs={{0,2},{1,9},{2,0},{3,11},{4,6},{5,13},{6,4},{7,15},{8,10},{9,1},{1... | collective-permute-start | bytes 786440 | tf_op jit(solution)/shard_map/ppermute | solution.py:32
  36.8 12.8 %collective-permute-start.14 = (bf16[128,128]{1,0:T(8,128)(2,1)S(1)}, bf16[128,128]{1,0:T(8,128)(2,1)S(1)}, u32[]{:S(2)}, u32[]{:S(2)}) collective-permute-start(bf16[128,128]{1,0:T(8,128)(2,1)S(1)} %add_convert_fusion.1), channel_id=1, source_target_pairs={{0,192},{1,224},{2,194},{3,226},{4,196},{5,228},{6,198},{7,230},{8... | collective-permute-start | bytes 98312 | tf_op jit(solution)/shard_map/ppermute | solution.py:32
  40.3 9.3 %collective-permute-start.13 = (bf16[128,128]{1,0:T(8,128)(2,1)S(1)}, bf16[128,128]{1,0:T(8,128)(2,1)S(1)}, u32[]{:S(2)}, u32[]{:S(2)}) collective-permute-start(bf16[128,128]{1,0:T(8,128)(2,1)S(1)} %add_convert_fusion.1), channel_id=1, source_target_pairs={{0,64},{1,96},{2,66},{3,98},{4,68},{5,100},{6,70},{7,102},{8,72},{... | collective-permute-start | bytes 98312 | tf_op jit(solution)/shard_map/ppermute | solution.py:32
  41.4 11.1 %collective-permute-start.16 = (bf16[2,4,4,64,128]{4,3,2,1,0:T(8,128)(2,1)S(1)}, bf16[2,4,4,64,128]{4,3,2,1,0:T(8,128)(2,1)S(1)}, u32[]{:S(2)}, u32[]{:S(2)}) collective-permute-start(bf16[2,4,4,64,128]{4,3,2,1,0:T(8,128)(2,1)S(1)} %pad_maximum_fusion), channel_id=1, source_target_pairs={{0,6},{1,25},{2,4},{3,27},{4,2},{5,29},{6,0},{7,31},{8,14},{9,17},... | collective-permute-start | bytes 1572872 | tf_op jit(solution)/shard_map/ppermute | solution.py:32
  43.5 6.2 %collective-permute-start.12 = (bf16[128,128]{1,0:T(8,128)(2,1)S(1)}, bf16[128,128]{1,0:T(8,128)(2,1)S(1)}, u32[]{:S(2)}, u32[]{:S(2)}) collective-permute-start(bf16[128,128]{1,0:T(8,128)(2,1)S(1)} %add_convert_fusion.1), channel_id=1, source_target_pairs={{0,128},{1,160},{2,130},{3,162},{4,132},{5,164},{6,134},{7,166},{8... | collective-permute-start | bytes 98312 | tf_op jit(solution)/shard_map/ppermute | solution.py:32
  47.5 4.9 %collective-permute-start.11 = (bf16[128,128]{1,0:T(8,128)(2,1)S(1)}, bf16[128,128]{1,0:T(8,128)(2,1)S(1)}, u32[]{:S(2)}, u32[]{:S(2)}) collective-permute-start(bf16[128,128]{1,0:T(8,128)(2,1)S(1)} %add_convert_fusion.1), channel_id=1, source_target_pairs={{0,0},{1,32},{2,2},{3,34},{4,4},{5,36},{6,6},{7,38},{8,8},{9,40},{... | collective-permute-start | bytes 98312 | tf_op jit(solution)/shard_map/ppermute | solution.py:32
  54.0 4.6 %collective-permute-start.21 = (f32[128,128]{1,0:T(8,128)S(1)}, f32[128,128]{1,0:T(8,128)S(1)}, u32[]{:S(2)}, u32[]{:S(2)}) collective-permute-start(f32[128,128]{1,0:T(8,128)S(1)} %precondition.3), channel_id=1, source_target_pairs={{0,1},{1,0},{2,3},{3,2},{4,5},{5,4},{6,7},{7,6},{8,9},{9,8},{10,11... | collective-permute-start | bytes 196616 | tf_op jit(solution)/shard_map/ppermute | solution.py:32
  55.3 5.3 %collective-permute-start.20 = (bf16[2,256,128]{2,1,0:T(8,128)(2,1)S(1)}, bf16[2,256,128]{2,1,0:T(8,128)(2,1)S(1)}, u32[]{:S(2)}, u32[]{:S(2)}) collective-permute-start(bf16[2,256,128]{2,1,0:T(8,128)(2,1)S(1)} %pad_maximum_fusion.5), channel_id=1, source_target_pairs={{0,24},{1,7},{2,26},{3,5},{4,28},{5,3},{6,30},{7,1},{8,16},{9,15},... | collective-permute-start | bytes 393224 | tf_op jit(solution)/shard_map/ppermute | solution.py:32
  56.9 5.6 %collective-permute-start.19 = (bf16[2,256,128]{2,1,0:T(8,128)(2,1)S(1)}, bf16[2,256,128]{2,1,0:T(8,128)(2,1)S(1)}, u32[]{:S(2)}, u32[]{:S(2)}) collective-permute-start(bf16[2,256,128]{2,1,0:T(8,128)(2,1)S(1)} %pad_maximum_fusion.5), channel_id=1, source_target_pairs={{0,16},{1,5},{2,18},{3,7},{4,20},{5,1},{6,22},{7,3},{8,24},{9,13},... | collective-permute-start | bytes 393224 | tf_op jit(solution)/shard_map/ppermute | solution.py:32
  56.9 5.7 %collective-permute-start.18 = (bf16[2,256,128]{2,1,0:T(8,128)(2,1)S(1)}, bf16[2,256,128]{2,1,0:T(8,128)(2,1)S(1)}, u32[]{:S(2)}, u32[]{:S(2)}) collective-permute-start(bf16[2,256,128]{2,1,0:T(8,128)(2,1)S(1)} %pad_maximum_fusion.5), channel_id=1, source_target_pairs={{0,8},{1,3},{2,10},{3,1},{4,12},{5,7},{6,14},{7,5},{8,0},{9,11},{1... | collective-permute-start | bytes 393224 | tf_op jit(solution)/shard_map/ppermute | solution.py:32
  62.7 15.2 %collective-permute-start.25 = (bf16[4,2,256,128]{3,2,1,0:T(8,128)(2,1)S(1)}, bf16[4,2,256,128]{3,2,1,0:T(8,128)(2,1)S(1)}, u32[]{:S(2)}, u32[]{:S(2)}) collective-permute-start(bf16[4,2,256,128]{3,2,1,0:T(8,128)(2,1)S(1)} %pad_maximum_fusion.1.piece), channel_id=1, source_target_pairs={{0,6},{1,25},{2,4},{3,27},{4,2},{5,29},{6,0},{7,31},{8,14},{9,17},... | collective-permute-start | bytes 1572872 | tf_op jit(solution)/shard_map/ppermute | solution.py:32
  64.4 16.5 %collective-permute-start.24 = (bf16[4,2,256,128]{3,2,1,0:T(8,128)(2,1)S(1)}, bf16[4,2,256,128]{3,2,1,0:T(8,128)(2,1)S(1)}, u32[]{:S(2)}, u32[]{:S(2)}) collective-permute-start(bf16[4,2,256,128]{3,2,1,0:T(8,128)(2,1)S(1)} %pad_maximum_fusion.1.piece), channel_id=1, source_target_pairs={{0,4},{1,17},{2,6},{3,19},{4,0},{5,21},{6,2},{7,23},{8,12},{9,25},... | collective-permute-start | bytes 1572872 | tf_op jit(solution)/shard_map/ppermute | solution.py:32
  64.7 17.0 %collective-permute-start.23 = (bf16[4,2,256,128]{3,2,1,0:T(8,128)(2,1)S(1)}, bf16[4,2,256,128]{3,2,1,0:T(8,128)(2,1)S(1)}, u32[]{:S(2)}, u32[]{:S(2)}) collective-permute-start(bf16[4,2,256,128]{3,2,1,0:T(8,128)(2,1)S(1)} %pad_maximum_fusion.1.piece), channel_id=1, source_target_pairs={{0,2},{1,9},{2,0},{3,11},{4,6},{5,13},{6,4},{7,15},{8,10},{9,1},{1... | collective-permute-start | bytes 1572872 | tf_op jit(solution)/shard_map/ppermute | solution.py:32
  66.0 6.7 %collective-permute-start.22 = (bf16[128,128]{1,0:T(8,128)(2,1)S(1)}, bf16[128,128]{1,0:T(8,128)(2,1)S(1)}, u32[]{:S(2)}, u32[]{:S(2)}) collective-permute-start(bf16[128,128]{1,0:T(8,128)(2,1)S(1)} %add_convert_fusion), channel_id=1, source_target_pairs={{0,128},{1,129},{2,130},{3,131},{4,132},{5,133},{6,134},{7,135},{8... | collective-permute-start | bytes 98312 | tf_op jit(solution)/shard_map/ppermute | solution.py:32
  73.5 9.6 %collective-permute-start.26 = (f32[64,1024]{1,0:T(8,128)S(1)}, f32[64,1024]{1,0:T(8,128)S(1)}, u32[]{:S(2)}, u32[]{:S(2)}) collective-permute-start(f32[64,1024]{1,0:T(8,128)S(1)} %get-tuple-element.29), channel_id=1, source_target_pairs={{0,1},{1,0},{2,3},{3,2},{4,5},{5,4},{6,7},{7,6},{8,9},{9,8},{10,11... | collective-permute-start | bytes 786440 | tf_op jit(solution)/shard_map/ppermute | solution.py:32
  78.7 4.4 %collective-permute-start.29 = (f32[64,1024]{1,0:T(8,128)S(1)}, f32[64,1024]{1,0:T(8,128)S(1)}, u32[]{:S(2)}, u32[]{:S(2)}) collective-permute-start(f32[64,1024]{1,0:T(8,128)S(1)} %get-tuple-element.32), channel_id=1, source_target_pairs={{0,1},{1,0},{2,3},{3,2},{4,5},{5,4},{6,7},{7,6},{8,9},{9,8},{10,11... | collective-permute-start | bytes 786440 | tf_op jit(solution)/shard_map/ppermute | solution.py:32
  81.6 1.6 %collective-permute-start.28 = (f32[64,1024]{1,0:T(8,128)S(1)}, f32[64,1024]{1,0:T(8,128)S(1)}, u32[]{:S(2)}, u32[]{:S(2)}) collective-permute-start(f32[64,1024]{1,0:T(8,128)S(1)} %get-tuple-element.31), channel_id=1, source_target_pairs={{0,1},{1,0},{2,3},{3,2},{4,5},{5,4},{6,7},{7,6},{8,9},{9,8},{10,11... | collective-permute-start | bytes 786440 | tf_op jit(solution)/shard_map/ppermute | solution.py:32
  82.5 1.7 %collective-permute-start.27 = (f32[64,1024]{1,0:T(8,128)S(1)}, f32[64,1024]{1,0:T(8,128)S(1)}, u32[]{:S(2)}, u32[]{:S(2)}) collective-permute-start(f32[64,1024]{1,0:T(8,128)S(1)} %get-tuple-element.30), channel_id=1, source_target_pairs={{0,1},{1,0},{2,3},{3,2},{4,5},{5,4},{6,7},{7,6},{8,9},{9,8},{10,11... | collective-permute-start | bytes 786440 | tf_op jit(solution)/shard_map/ppermute | solution.py:32

commit v12 on v11

--- a/solution.py
+++ b/solution.py
@@ -76,10 +76,12 @@
     return pl.multiple_of(((z * 4 + y) * 4 + x) * 128, 128)
 
 
-def precondition(flip, where, p0, p1, p2, p3, low, high, pre):
-    total = jnp.zeros((128, 128), jnp.float32)
+def precondition(turns, flip, where, *refs):
+    pieces, (low, high), pre = refs[: len(turns)], refs[-3:-1], refs[-1]
+    rest = refs[len(turns) : -3]
+    total = rest[0][...] if rest else jnp.zeros((128, 128), jnp.float32)
     none = jnp.zeros((64, 128), jnp.bfloat16)
-    for k3, piece in enumerate((p0, p1, p2, p3)):
+    for k3, piece in zip(turns, pieces):
         for k2 in range(4):
             at = [
                 pl.ds(column(where, where[3], k3, k2, where[0] ^ kz), 128)
@@ -175,27 +177,30 @@
         theirs = swap_cores(rows)
         return jnp.where(first, rows, theirs), jnp.where(first, theirs, rows)
 
-    def partial(pieces, rows, flip):
+    def partial(turns, pieces, rest, rows, flip):
+        ins = [pieces[k] for k in turns] + rest + list(rows)
         return call(
-            functools.partial(precondition, flip),
+            functools.partial(precondition, turns, flip),
             "precondition",
             shape((128, 128), f32),
-            [SMEM] + [VMEM] * 6,
-        )(where, *pieces, *rows)
+            [SMEM] + [VMEM] * len(ins),
+        )(where, *ins)
 
     act_rows, grad_rows = factor(act_inverse), factor(grad_inverse)
-    part = partial(turned(second_turn, [act_plane] * 4), act_rows, True)
+    pieces = turned(second_turn, [act_plane] * 4)
+    part = partial((0, 3, 2), pieces, [], act_rows, False)
+    part = partial((1,), pieces, [part], act_rows, True)
     part, grad_plane = lax.optimization_barrier((part, grad_plane))
     act = (part + swap_cores(part)).astype(bf16)
     half = jnp.stack([grad_plane, second_turn(grad_plane, 1)])
+
+    here = [to_parity(act, j, 0) for j in (0, 1)]
+    there = [to_parity(act, j, 1) for j in (0, 1)]
+    half, here[0] = lax.optimization_barrier((half, here[0]))
     rest = second_turn(half, 3)
     grad_pieces = half[0], half[1], rest[1], rest[0]
-
-    here = [to_parity(act, j, 0) for j in (0, 1)]
-    there = [to_parity(act, j, 1) for j in (0, 1)]
     pair = jnp.stack([jnp.concatenate(p, axis=0) for p in zip(here, there)])
-    part = partial(grad_pieces, grad_rows, False)
-    pair, part = lax.optimization_barrier((pair, part))
+    part = partial((0, 1, 2, 3), grad_pieces, [], grad_rows, False)
     grad = (part + swap_cores(part)).astype(bf16)
     plane = jnp.stack(turned(first_turn, [pair] * 4))
     plane, grad = lax.optimization_barrier((plane, grad))

time: 86.8 us -> 85.4 us (0.984)
  starting transfers between devices: 49.5 us -> 47.2 us
    ppermute x30, starting transfers between devices: 49.5 us -> 47.2 us  [send(): return lax.ppermute(value, AXES, pairs)]
    pallas_call x2 -> x3, Pallas kernels: 2.91 us -> 3.55 us  [partial(): call(functools.partial(precondition, turns, flip), 'precondition', shape(...]
  transfers between devices with their start and end apart: 30 -> 30, of which waited for: 16 -> 15; matrix products, arithmetic and copies ran while one was open for 1% -> 1% of each run, Pallas kernels for 5% -> 8%
where the time goes in v12:
time: 85.4 us; the launch traced here: 85.2 us
  starting transfers between devices  47.2 us (55%)
  waiting for transfers between devices  27.1 us (32%)
  Pallas kernels  8.75 us (10%)
  other arithmetic  1.58 us (2%)
    ppermute x30, starting transfers between devices, send(): return lax.ppermute(value, AXES, pairs)  47.2 us
    ppermute x30, waiting for transfers between devices, send(): return lax.ppermute(value, AXES, pairs)  27.1 us
    pallas_call x3, Pallas kernels, partial(): call(functools.partial(precondition, turns, flip), 'precondition', shape(...  3.55 us
    pallas_call x4, Pallas kernels, on_device(): call(tile, 'tile', [shape((64, 1024), f32)] * 2, [SMEM, VMEM, VMEM])  3.1 us
    pallas_call x1, Pallas kernels, on_device(): pl.pallas_call(assemble, out_shape=shape((64, 8192), f32), in_specs=[SMEM...  2.1 us
  transfers between devices with their start and end apart: 30, of which 15 were waited for; matrix products, arithmetic and copies ran while one was open for 1% of the time, Pallas kernels for 8%

profile of v12, /device:TPU:1, one launch (start us, length us, event | category | flops | bytes accessed | tf_op | source)
XLA Modules:
  0.0 85.2 jit_solution(6677011483626955560)
XLA Ops:
  0.0 0.8 fusion
  0.8 2.5 %collective-permute-start = (bf16[2,64,128]{2,1,0:T(8,128)(2,1)S(1)}, bf16[2,64,128]{2,1,0:T(8,128)(2,1)S(1)}, u32[]{:S(2)}, u32[]{:S(2)}) collective-permute-start(bf16[2,64,128]{2,1,0:T(8,128)(2,1)S(1)} %get-tuple-element.52), channel_id=1, source_target_pairs={{0,32},{1,33},{2,34},{3,35},{4,36},{5,37},{6,38},{7,39},{8,40},{9,... | collective-permute-start | bytes 98312 | tf_op jit(solution)/shard_map/ppermute | solution.py:32
  3.3 3.0 %collective-permute-start.1 = (bf16[2,64,128]{2,1,0:T(8,128)(2,1)S(1)}, bf16[2,64,128]{2,1,0:T(8,128)(2,1)S(1)}, u32[]{:S(2)}, u32[]{:S(2)}) collective-permute-start(bf16[2,64,128]{2,1,0:T(8,128)(2,1)S(1)} %get-tuple-element.52), channel_id=1, source_target_pairs={{0,64},{1,65},{2,66},{3,67},{4,68},{5,69},{6,70},{7,71},{8,72},{9,... | collective-permute-start | bytes 98312 | tf_op jit(solution)/shard_map/ppermute | solution.py:32
  6.3 2.2 %collective-permute-start.9 = (bf16[64,8192]{1,0:T(8,128)(2,1)}, bf16[64,8192]{1,0:T(8,128)(2,1)S(1)}, u32[]{:S(2)}, u32[]{:S(2)}) collective-permute-start(bf16[64,8192]{1,0:T(8,128)(2,1)} %param.6), channel_id=1, source_target_pairs={{0,1},{1,0},{2,3},{3,2},{4,5},{5,4},{6,7},{7,6},{8,9},{9,8},{10,11... | collective-permute-start | bytes 3145736 | tf_op jit(solution)/shard_map/ppermute | solution.py:32
  8.5 2.3 %collective-permute-done.2 = bf16[2,64,128]{2,1,0:T(8,128)(2,1)S(1)} collective-permute-done((bf16[2,64,128]{2,1,0:T(8,128)(2,1)S(1)}, bf16[2,64,128]{2,1,0:T(8,128)(2,1)S(1)}, u32[]{:S(2)}, u32[]{:S(2)}) %collective-permute-start.2) | collective-permute-done | bytes 32800 | tf_op jit(solution)/shard_map/ppermute | solution.py:32
  10.9 1.3 %collective-permute-start.3 = (bf16[4,2,64,128]{3,2,0,1:T(8,128)(2,1)S(1)}, bf16[4,2,64,128]{3,2,0,1:T(8,128)(2,1)S(1)}, u32[]{:S(2)}, u32[]{:S(2)}) collective-permute-start(bf16[4,2,64,128]{3,2,0,1:T(8,128)(2,1)S(1)} %pad_maximum_fusion.4), channel_id=1, source_target_pairs={{0,8},{1,3},{2,10},{3,1},{4,12},{5,7},{6,14},{7,5},{8,0},{9,11},{1... | collective-permute-start | bytes 393224 | tf_op jit(solution)/shard_map/ppermute | solution.py:32
  12.2 2.5 %collective-permute-start.4 = (bf16[4,2,64,128]{3,2,0,1:T(8,128)(2,1)S(1)}, bf16[4,2,64,128]{3,2,0,1:T(8,128)(2,1)S(1)}, u32[]{:S(2)}, u32[]{:S(2)}) collective-permute-start(bf16[4,2,64,128]{3,2,0,1:T(8,128)(2,1)S(1)} %pad_maximum_fusion.4), channel_id=1, source_target_pairs={{0,16},{1,5},{2,18},{3,7},{4,20},{5,1},{6,22},{7,3},{8,24},{9,13},... | collective-permute-start | bytes 393224 | tf_op jit(solution)/shard_map/ppermute | solution.py:32
  14.9 3.5 %collective-permute-done.4 = bf16[4,2,64,128]{3,2,0,1:T(8,128)(2,1)S(1)} collective-permute-done((bf16[4,2,64,128]{3,2,0,1:T(8,128)(2,1)S(1)}, bf16[4,2,64,128]{3,2,0,1:T(8,128)(2,1)S(1)}, u32[]{:S(2)}, u32[]{:S(2)}) %collective-permute-start.4) | collective-permute-done | bytes 131104 | tf_op jit(solution)/shard_map/ppermute | solution.py:32
  18.4 1.4 %collective-permute-done.5 = bf16[4,2,64,128]{3,2,0,1:T(8,128)(2,1)S(1)} collective-permute-done((bf16[4,2,64,128]{3,2,0,1:T(8,128)(2,1)S(1)}, bf16[4,2,64,128]{3,2,0,1:T(8,128)(2,1)S(1)}, u32[]{:S(2)}, u32[]{:S(2)}) %collective-permute-start.5) | collective-permute-done | bytes 131104 | tf_op jit(solution)/shard_map/ppermute | solution.py:32
  19.8 3.1 %collective-permute-start.7 = (bf16[4,4,64,128]{3,2,1,0:T(8,128)(2,1)S(1)}, bf16[4,4,64,128]{3,2,1,0:T(8,128)(2,1)S(1)}, u32[]{:S(2)}, u32[]{:S(2)}) collective-permute-start(bf16[4,4,64,128]{3,2,1,0:T(8,128)(2,1)S(1)} %pad_maximum_fusion.2.refs_0_), channel_id=1, source_target_pairs={{0,6},{1,25},{2,4},{3,27},{4,2},{5,29},{6,0},{7,31},{8,14},{9,17},... | collective-permute-start | bytes 786440 | tf_op jit(solution)/shard_map/ppermute | solution.py:32
  23.8 5.2 %collective-permute-done.7.refs_1_ = bf16[4,4,64,128]{3,2,1,0:T(8,128)(2,1)S(1)} collective-permute-done((bf16[4,4,64,128]{3,2,1,0:T(8,128)(2,1)S(1)}, bf16[4,4,64,128]{3,2,1,0:T(8,128)(2,1)S(1)}, u32[]{:S(2)}, u32[]{:S(2)}) %collective-permute-start.7) | collective-permute-done | bytes 262176 | tf_op jit(solution)/shard_map/ppermute | solution.py:32
  29.7 1.2 %precondition.3.refs_1_ = f32[128,128]{1,0:T(8,128)S(1)} custom-call(s32[4]{0:T(128)S(1)} %pad_add_fusion.where, bf16[4,4,64,128]{3,2,1,0:T(8,128)(2,1)S(1)} %pad_maximum_fusion.2.refs_0_, bf16[4,4,64,128]{3,2,1,0:T(8,128)(2,1)S(1)} %collective-permute-done.7.refs_1_, bf16[4,4,64,128]{3,2,1,0:T(8,128)(2,1)S(1)} %collective-permute-done.8.refs_2_, ...), custom_call_target="tpu_custom_call" | custom-call | tf_op jit(solution)/shard_map/precondition/pallas_call | solution.py:182
  30.9 0.9 %precondition.4 = f32[128,128]{1,0:T(8,128)S(1)} custom-call(s32[4]{0:T(128)S(1)} %pad_add_fusion.where, bf16[4,4,64,128]{3,2,1,0:T(8,128)(2,1)S(1)} %collective-permute-done.6.refs_0_, f32[128,128]{1,0:T(8,128)S(1)} %precondition.3.refs_1_, bf16[64,8192]{1,0:T(8,128)(2,1)S(1)} %get-tuple-element.36.refs_3_.refs_2_, ...), custom_call_target="tpu_custom_call" | custom-call | tf_op jit(solution)/shard_map/precondition/pallas_call | solution.py:182
  32.2 6.7 %collective-permute-start.11 = (f32[128,128]{1,0:T(8,128)S(1)}, f32[128,128]{1,0:T(8,128)S(1)}, u32[]{:S(2)}, u32[]{:S(2)}) collective-permute-start(f32[128,128]{1,0:T(8,128)S(1)} %precondition.4), channel_id=1, source_target_pairs={{0,1},{1,0},{2,3},{3,2},{4,5},{5,4},{6,7},{7,6},{8,9},{9,8},{10,11... | collective-permute-start | bytes 196616 | tf_op jit(solution)/shard_map/ppermute | solution.py:32
  39.8 1.9 %collective-permute-start.12 = (bf16[128,128]{1,0:T(8,128)(2,1)S(1)}, bf16[128,128]{1,0:T(8,128)(2,1)S(1)}, u32[]{:S(2)}, u32[]{:S(2)}) collective-permute-start(bf16[128,128]{1,0:T(8,128)(2,1)S(1)} %add_convert_fusion.1), channel_id=1, source_target_pairs={{0,0},{1,32},{2,2},{3,34},{4,4},{5,36},{6,6},{7,38},{8,8},{9,40},{... | collective-permute-start | bytes 98312 | tf_op jit(solution)/shard_map/ppermute | solution.py:32
  41.7 2.6 %collective-permute-start.13 = (bf16[128,128]{1,0:T(8,128)(2,1)S(1)}, bf16[128,128]{1,0:T(8,128)(2,1)S(1)}, u32[]{:S(2)}, u32[]{:S(2)}) collective-permute-start(bf16[128,128]{1,0:T(8,128)(2,1)S(1)} %add_convert_fusion.1), channel_id=1, source_target_pairs={{0,128},{1,160},{2,130},{3,162},{4,132},{5,164},{6,134},{7,166},{8... | collective-permute-start | bytes 98312 | tf_op jit(solution)/shard_map/ppermute | solution.py:32
  44.3 3.6 %collective-permute-start.14 = (bf16[128,128]{1,0:T(8,128)(2,1)S(1)}, bf16[128,128]{1,0:T(8,128)(2,1)S(1)}, u32[]{:S(2)}, u32[]{:S(2)}) collective-permute-start(bf16[128,128]{1,0:T(8,128)(2,1)S(1)} %add_convert_fusion.1), channel_id=1, source_target_pairs={{0,64},{1,96},{2,66},{3,98},{4,68},{5,100},{6,70},{7,102},{8,72},{... | collective-permute-start | bytes 98312 | tf_op jit(solution)/shard_map/ppermute | solution.py:32
  48.1 1.8 %collective-permute-done.14 = bf16[128,128]{1,0:T(8,128)(2,1)S(1)} collective-permute-done((bf16[128,128]{1,0:T(8,128)(2,1)S(1)}, bf16[128,128]{1,0:T(8,128)(2,1)S(1)}, u32[]{:S(2)}, u32[]{:S(2)}) %collective-permute-start.14) | collective-permute-done | bytes 32800 | tf_op jit(solution)/shard_map/ppermute | solution.py:32
  49.9 2.4 %collective-permute-done.15 = bf16[128,128]{1,0:T(8,128)(2,1)S(1)} collective-permute-done((bf16[128,128]{1,0:T(8,128)(2,1)S(1)}, bf16[128,128]{1,0:T(8,128)(2,1)S(1)}, u32[]{:S(2)}, u32[]{:S(2)}) %collective-permute-start.15) | collective-permute-done | bytes 32800 | tf_op jit(solution)/shard_map/ppermute | solution.py:32
  52.4 0.9 %collective-permute-start.16 = (bf16[2,256,128]{2,1,0:T(8,128)(2,1)S(1)}, bf16[2,256,128]{2,1,0:T(8,128)(2,1)S(1)}, u32[]{:S(2)}, u32[]{:S(2)}) collective-permute-start(bf16[2,256,128]{2,1,0:T(8,128)(2,1)S(1)} %get-tuple-element.42), channel_id=1, source_target_pairs={{0,8},{1,3},{2,10},{3,1},{4,12},{5,7},{6,14},{7,5},{8,0},{9,11},{1... | collective-permute-start | bytes 393224 | tf_op jit(solution)/shard_map/ppermute | solution.py:32
  53.3 2.7 %collective-permute-start.17 = (bf16[2,256,128]{2,1,0:T(8,128)(2,1)S(1)}, bf16[2,256,128]{2,1,0:T(8,128)(2,1)S(1)}, u32[]{:S(2)}, u32[]{:S(2)}) collective-permute-start(bf16[2,256,128]{2,1,0:T(8,128)(2,1)S(1)} %get-tuple-element.42), channel_id=1, source_target_pairs={{0,16},{1,5},{2,18},{3,7},{4,20},{5,1},{6,22},{7,3},{8,24},{9,13},... | collective-permute-start | bytes 393224 | tf_op jit(solution)/shard_map/ppermute | solution.py:32
  56.6 3.0 %collective-permute-done.19 = bf16[2,4,4,64,128]{4,3,2,1,0:T(8,128)(2,1)S(1)} collective-permute-done((bf16[2,4,4,64,128]{4,3,2,1,0:T(8,128)(2,1)S(1)}, bf16[2,4,4,64,128]{4,3,2,1,0:T(8,128)(2,1)S(1)}, u32[]{:S(2)}, u32[]{:S(2)}) %collective-permute-start.19) | collective-permute-done | bytes 524320 | tf_op jit(solution)/shard_map/ppermute | solution.py:32
  59.6 1.4 %precondition.5 = f32[128,128]{1,0:T(8,128)S(1)} custom-call(s32[4]{0:T(128)S(1)} %pad_add_fusion.where, bf16[4,4,64,128]{3,2,1,0:T(8,128)(2,1)S(1)} %get-tuple-element.40.refs_0_, bf16[4,4,64,128]{3,2,1,0:T(8,128)(2,1)S(1)} %get-tuple-element.39.refs_1_, bf16[4,4,64,128]{3,2,1,0:T(8,128)(2,1)S(1)} %get-tuple-element.38.refs_2_, ...), custom_call_target="tpu_custom_call" | custom-call | tf_op jit(solution)/shard_map/precondition/pallas_call | solution.py:182
  61.3 1.1 %collective-permute-done.21 = f32[128,128]{1,0:T(8,128)S(1)} collective-permute-done((f32[128,128]{1,0:T(8,128)S(1)}, f32[128,128]{1,0:T(8,128)S(1)}, u32[]{:S(2)}, u32[]{:S(2)}) %collective-permute-start.21) | collective-permute-done | bytes 65568 | tf_op jit(solution)/shard_map/ppermute | solution.py:32
  62.6 3.1 %collective-permute-start.23 = (bf16[4,2,256,128]{3,2,1,0:T(8,128)(2,1)S(1)}, bf16[4,2,256,128]{3,2,1,0:T(8,128)(2,1)S(1)}, u32[]{:S(2)}, u32[]{:S(2)}) collective-permute-start(bf16[4,2,256,128]{3,2,1,0:T(8,128)(2,1)S(1)} %pad_maximum_fusion.1.piece), channel_id=1, source_target_pairs={{0,2},{1,9},{2,0},{3,11},{4,6},{5,13},{6,4},{7,15},{8,10},{9,1},{1... | collective-permute-start | bytes 1572872 | tf_op jit(solution)/shard_map/ppermute | solution.py:32
  65.7 5.0 %collective-permute-start.22 = (bf16[128,128]{1,0:T(8,128)(2,1)S(1)}, bf16[128,128]{1,0:T(8,128)(2,1)S(1)}, u32[]{:S(2)}, u32[]{:S(2)}) collective-permute-start(bf16[128,128]{1,0:T(8,128)(2,1)S(1)} %add_convert_fusion), channel_id=1, source_target_pairs={{0,128},{1,129},{2,130},{3,131},{4,132},{5,133},{6,134},{7,135},{8... | collective-permute-start | bytes 98312 | tf_op jit(solution)/shard_map/ppermute | solution.py:32
  70.7 1.7 %collective-permute-done.22 = bf16[128,128]{1,0:T(8,128)(2,1)S(1)} collective-permute-done((bf16[128,128]{1,0:T(8,128)(2,1)S(1)}, bf16[128,128]{1,0:T(8,128)(2,1)S(1)}, u32[]{:S(2)}, u32[]{:S(2)}) %collective-permute-start.22) | collective-permute-done | bytes 32800 | tf_op jit(solution)/shard_map/ppermute | solution.py:32
  73.2 2.2 %collective-permute-start.26 = (f32[64,1024]{1,0:T(8,128)S(1)}, f32[64,1024]{1,0:T(8,128)S(1)}, u32[]{:S(2)}, u32[]{:S(2)}) collective-permute-start(f32[64,1024]{1,0:T(8,128)S(1)} %get-tuple-element.29), channel_id=1, source_target_pairs={{0,1},{1,0},{2,3},{3,2},{4,5},{5,4},{6,7},{7,6},{8,9},{9,8},{10,11... | collective-permute-start | bytes 786440 | tf_op jit(solution)/shard_map/ppermute | solution.py:32
  75.4 2.2 %collective-permute-done.25.piece = bf16[4,2,256,128]{3,2,1,0:T(8,128)(2,1)S(1)} collective-permute-done((bf16[4,2,256,128]{3,2,1,0:T(8,128)(2,1)S(1)}, bf16[4,2,256,128]{3,2,1,0:T(8,128)(2,1)S(1)}, u32[]{:S(2)}, u32[]{:S(2)}) %collective-permute-start.25) | collective-permute-done | bytes 524320 | tf_op jit(solution)/shard_map/ppermute | solution.py:32
  78.4 1.1 %collective-permute-start.29 = (f32[64,1024]{1,0:T(8,128)S(1)}, f32[64,1024]{1,0:T(8,128)S(1)}, u32[]{:S(2)}, u32[]{:S(2)}) collective-permute-start(f32[64,1024]{1,0:T(8,128)S(1)} %get-tuple-element.32), channel_id=1, source_target_pairs={{0,1},{1,0},{2,3},{3,2},{4,5},{5,4},{6,7},{7,6},{8,9},{9,8},{10,11... | collective-permute-start | bytes 786440 | tf_op jit(solution)/shard_map/ppermute | solution.py:32
  81.9 1.0 %collective-permute-done.27.refs_5_ = f32[64,1024]{1,0:T(8,128)S(1)} collective-permute-done((f32[64,1024]{1,0:T(8,128)S(1)}, f32[64,1024]{1,0:T(8,128)S(1)}, u32[]{:S(2)}, u32[]{:S(2)}) %collective-permute-start.27) | collective-permute-done | bytes 262176 | tf_op jit(solution)/shard_map/ppermute | solution.py:32
  82.9 2.1 %assemble.1 = f32[64,8192]{1,0:T(8,128)} custom-call(s32[4]{0:T(128)S(1)} %pad_add_fusion.where, f32[64,1024]{1,0:T(8,128)S(1)} %get-tuple-element.25.refs_0_, f32[64,1024]{1,0:T(8,128)S(1)} %get-tuple-element.26.refs_1_, f32[64,1024]{1,0:T(8,128)S(1)} %get-tuple-element.27.refs_2_, f32[64,1024]{1,0:T(8,128)S(1)} %get-tuple-element.28.refs_3_, ...), custom_call_target="tpu_custom_call" | custom-call | tf_op jit(solution)/shard_map/assemble/pallas_call | solution.py:217
  (62 shorter events, 8.2 us)
Async XLA Ops:
  0.0 23.7 %copy-start = (bf16[64,8192]{1,0:T(8,128)(2,1)S(1)}, bf16[64,8192]{1,0:T(8,128)(2,1)}, u32[]{:S(2)}) copy-start(bf16[64,8192]{1,0:T(8,128)(2,1)} %param.6) | copy-start | bytes 3145732
  0.8 7.7 %collective-permute-start = (bf16[2,64,128]{2,1,0:T(8,128)(2,1)S(1)}, bf16[2,64,128]{2,1,0:T(8,128)(2,1)S(1)}, u32[]{:S(2)}, u32[]{:S(2)}) collective-permute-start(bf16[2,64,128]{2,1,0:T(8,128)(2,1)S(1)} %get-tuple-element.52), channel_id=1, source_target_pairs={{0,32},{1,33},{2,34},{3,35},{4,36},{5,37},{6,38},{7,39},{8,40},{9,... | collective-permute-start | bytes 98312 | tf_op jit(solution)/shard_map/ppermute | solution.py:32
  3.3 5.2 %collective-permute-start.1 = (bf16[2,64,128]{2,1,0:T(8,128)(2,1)S(1)}, bf16[2,64,128]{2,1,0:T(8,128)(2,1)S(1)}, u32[]{:S(2)}, u32[]{:S(2)}) collective-permute-start(bf16[2,64,128]{2,1,0:T(8,128)(2,1)S(1)} %get-tuple-element.52), channel_id=1, source_target_pairs={{0,64},{1,65},{2,66},{3,67},{4,68},{5,69},{6,70},{7,71},{8,72},{9,... | collective-permute-start | bytes 98312 | tf_op jit(solution)/shard_map/ppermute | solution.py:32
  6.3 4.6 %collective-permute-start.2 = (bf16[2,64,128]{2,1,0:T(8,128)(2,1)S(1)}, bf16[2,64,128]{2,1,0:T(8,128)(2,1)S(1)}, u32[]{:S(2)}, u32[]{:S(2)}) collective-permute-start(bf16[2,64,128]{2,1,0:T(8,128)(2,1)S(1)} %get-tuple-element.52), channel_id=1, source_target_pairs={{0,96},{1,97},{2,98},{3,99},{4,100},{5,101},{6,102},{7,103},{8,104... | collective-permute-start | bytes 98312 | tf_op jit(solution)/shard_map/ppermute | solution.py:32
  6.3 17.4 %collective-permute-start.9 = (bf16[64,8192]{1,0:T(8,128)(2,1)}, bf16[64,8192]{1,0:T(8,128)(2,1)S(1)}, u32[]{:S(2)}, u32[]{:S(2)}) collective-permute-start(bf16[64,8192]{1,0:T(8,128)(2,1)} %param.6), channel_id=1, source_target_pairs={{0,1},{1,0},{2,3},{3,2},{4,5},{5,4},{6,7},{7,6},{8,9},{9,8},{10,11... | collective-permute-start | bytes 3145736 | tf_op jit(solution)/shard_map/ppermute | solution.py:32
  8.5 30.4 %collective-permute-start.20 = (bf16[64,8192]{1,0:T(8,128)(2,1)}, bf16[64,8192]{1,0:T(8,128)(2,1)S(1)}, u32[]{:S(2)}, u32[]{:S(2)}) collective-permute-start(bf16[64,8192]{1,0:T(8,128)(2,1)} %param.7), channel_id=1, source_target_pairs={{0,1},{1,0},{2,3},{3,2},{4,5},{5,4},{6,7},{7,6},{8,9},{9,8},{10,11... | collective-permute-start | bytes 3145736 | tf_op jit(solution)/shard_map/ppermute | solution.py:32
  10.9 4.0 %collective-permute-start.3 = (bf16[4,2,64,128]{3,2,0,1:T(8,128)(2,1)S(1)}, bf16[4,2,64,128]{3,2,0,1:T(8,128)(2,1)S(1)}, u32[]{:S(2)}, u32[]{:S(2)}) collective-permute-start(bf16[4,2,64,128]{3,2,0,1:T(8,128)(2,1)S(1)} %pad_maximum_fusion.4), channel_id=1, source_target_pairs={{0,8},{1,3},{2,10},{3,1},{4,12},{5,7},{6,14},{7,5},{8,0},{9,11},{1... | collective-permute-start | bytes 393224 | tf_op jit(solution)/shard_map/ppermute | solution.py:32
  12.2 6.2 %collective-permute-start.4 = (bf16[4,2,64,128]{3,2,0,1:T(8,128)(2,1)S(1)}, bf16[4,2,64,128]{3,2,0,1:T(8,128)(2,1)S(1)}, u32[]{:S(2)}, u32[]{:S(2)}) collective-permute-start(bf16[4,2,64,128]{3,2,0,1:T(8,128)(2,1)S(1)} %pad_maximum_fusion.4), channel_id=1, source_target_pairs={{0,16},{1,5},{2,18},{3,7},{4,20},{5,1},{6,22},{7,3},{8,24},{9,13},... | collective-permute-start | bytes 393224 | tf_op jit(solution)/shard_map/ppermute | solution.py:32
  14.6 5.2 %collective-permute-start.5 = (bf16[4,2,64,128]{3,2,0,1:T(8,128)(2,1)S(1)}, bf16[4,2,64,128]{3,2,0,1:T(8,128)(2,1)S(1)}, u32[]{:S(2)}, u32[]{:S(2)}) collective-permute-start(bf16[4,2,64,128]{3,2,0,1:T(8,128)(2,1)S(1)} %pad_maximum_fusion.4), channel_id=1, source_target_pairs={{0,24},{1,7},{2,26},{3,5},{4,28},{5,3},{6,30},{7,1},{8,16},{9,15},... | collective-permute-start | bytes 393224 | tf_op jit(solution)/shard_map/ppermute | solution.py:32
  19.8 9.2 %collective-permute-start.7 = (bf16[4,4,64,128]{3,2,1,0:T(8,128)(2,1)S(1)}, bf16[4,4,64,128]{3,2,1,0:T(8,128)(2,1)S(1)}, u32[]{:S(2)}, u32[]{:S(2)}) collective-permute-start(bf16[4,4,64,128]{3,2,1,0:T(8,128)(2,1)S(1)} %pad_maximum_fusion.2.refs_0_), channel_id=1, source_target_pairs={{0,6},{1,25},{2,4},{3,27},{4,2},{5,29},{6,0},{7,31},{8,14},{9,17},... | collective-permute-start | bytes 786440 | tf_op jit(solution)/shard_map/ppermute | solution.py:32
  23.0 6.7 %collective-permute-start.8 = (bf16[4,4,64,128]{3,2,1,0:T(8,128)(2,1)S(1)}, bf16[4,4,64,128]{3,2,1,0:T(8,128)(2,1)S(1)}, u32[]{:S(2)}, u32[]{:S(2)}) collective-permute-start(bf16[4,4,64,128]{3,2,1,0:T(8,128)(2,1)S(1)} %pad_maximum_fusion.2.refs_0_), channel_id=1, source_target_pairs={{0,4},{1,17},{2,6},{3,19},{4,0},{5,21},{6,2},{7,23},{8,12},{9,25},... | collective-permute-start | bytes 786440 | tf_op jit(solution)/shard_map/ppermute | solution.py:32
  23.2 7.8 %collective-permute-start.6 = (bf16[4,4,64,128]{3,2,1,0:T(8,128)(2,1)S(1)}, bf16[4,4,64,128]{3,2,1,0:T(8,128)(2,1)S(1)}, u32[]{:S(2)}, u32[]{:S(2)}) collective-permute-start(bf16[4,4,64,128]{3,2,1,0:T(8,128)(2,1)S(1)} %pad_maximum_fusion.2.refs_0_), channel_id=1, source_target_pairs={{0,2},{1,9},{2,0},{3,11},{4,6},{5,13},{6,4},{7,15},{8,10},{9,1},{1... | collective-permute-start | bytes 786440 | tf_op jit(solution)/shard_map/ppermute | solution.py:32
  29.7 9.2 %copy-start.1 = (bf16[64,8192]{1,0:T(8,128)(2,1)S(1)}, bf16[64,8192]{1,0:T(8,128)(2,1)}, u32[]{:S(2)}) copy-start(bf16[64,8192]{1,0:T(8,128)(2,1)} %param.7) | copy-start | bytes 3145732
  31.8 16.1 %collective-permute-start.10 = (bf16[4,4,64,128]{3,2,1,0:T(8,128)(2,1)S(1)}, bf16[4,4,64,128]{3,2,1,0:T(8,128)(2,1)S(1)}, u32[]{:S(2)}, u32[]{:S(2)}) collective-permute-start(bf16[4,4,64,128]{3,2,1,0:T(8,128)(2,1)S(1)} %pad_maximum_fusion.3), channel_id=1, source_target_pairs={{0,2},{1,9},{2,0},{3,11},{4,6},{5,13},{6,4},{7,15},{8,10},{9,1},{1... | collective-permute-start | bytes 786440 | tf_op jit(solution)/shard_map/ppermute | solution.py:32
  32.2 7.6 %collective-permute-start.11 = (f32[128,128]{1,0:T(8,128)S(1)}, f32[128,128]{1,0:T(8,128)S(1)}, u32[]{:S(2)}, u32[]{:S(2)}) collective-permute-start(f32[128,128]{1,0:T(8,128)S(1)} %precondition.4), channel_id=1, source_target_pairs={{0,1},{1,0},{2,3},{3,2},{4,5},{5,4},{6,7},{7,6},{8,9},{9,8},{10,11... | collective-permute-start | bytes 196616 | tf_op jit(solution)/shard_map/ppermute | solution.py:32
  39.8 8.2 %collective-permute-start.12 = (bf16[128,128]{1,0:T(8,128)(2,1)S(1)}, bf16[128,128]{1,0:T(8,128)(2,1)S(1)}, u32[]{:S(2)}, u32[]{:S(2)}) collective-permute-start(bf16[128,128]{1,0:T(8,128)(2,1)S(1)} %add_convert_fusion.1), channel_id=1, source_target_pairs={{0,0},{1,32},{2,2},{3,34},{4,4},{5,36},{6,6},{7,38},{8,8},{9,40},{... | collective-permute-start | bytes 98312 | tf_op jit(solution)/shard_map/ppermute | solution.py:32
  41.7 10.6 %collective-permute-start.13 = (bf16[128,128]{1,0:T(8,128)(2,1)S(1)}, bf16[128,128]{1,0:T(8,128)(2,1)S(1)}, u32[]{:S(2)}, u32[]{:S(2)}) collective-permute-start(bf16[128,128]{1,0:T(8,128)(2,1)S(1)} %add_convert_fusion.1), channel_id=1, source_target_pairs={{0,128},{1,160},{2,130},{3,162},{4,132},{5,164},{6,134},{7,166},{8... | collective-permute-start | bytes 98312 | tf_op jit(solution)/shard_map/ppermute | solution.py:32
  44.3 5.6 %collective-permute-start.14 = (bf16[128,128]{1,0:T(8,128)(2,1)S(1)}, bf16[128,128]{1,0:T(8,128)(2,1)S(1)}, u32[]{:S(2)}, u32[]{:S(2)}) collective-permute-start(bf16[128,128]{1,0:T(8,128)(2,1)S(1)} %add_convert_fusion.1), channel_id=1, source_target_pairs={{0,64},{1,96},{2,66},{3,98},{4,68},{5,100},{6,70},{7,102},{8,72},{... | collective-permute-start | bytes 98312 | tf_op jit(solution)/shard_map/ppermute | solution.py:32
  47.9 4.4 %collective-permute-start.15 = (bf16[128,128]{1,0:T(8,128)(2,1)S(1)}, bf16[128,128]{1,0:T(8,128)(2,1)S(1)}, u32[]{:S(2)}, u32[]{:S(2)}) collective-permute-start(bf16[128,128]{1,0:T(8,128)(2,1)S(1)} %add_convert_fusion.1), channel_id=1, source_target_pairs={{0,192},{1,224},{2,194},{3,226},{4,196},{5,228},{6,198},{7,230},{8... | collective-permute-start | bytes 98312 | tf_op jit(solution)/shard_map/ppermute | solution.py:32
  48.0 11.6 %collective-permute-start.19 = (bf16[2,4,4,64,128]{4,3,2,1,0:T(8,128)(2,1)S(1)}, bf16[2,4,4,64,128]{4,3,2,1,0:T(8,128)(2,1)S(1)}, u32[]{:S(2)}, u32[]{:S(2)}) collective-permute-start(bf16[2,4,4,64,128]{4,3,2,1,0:T(8,128)(2,1)S(1)} %pad_maximum_fusion), channel_id=1, source_target_pairs={{0,6},{1,25},{2,4},{3,27},{4,2},{5,29},{6,0},{7,31},{8,14},{9,17},... | collective-permute-start | bytes 1572872 | tf_op jit(solution)/shard_map/ppermute | solution.py:32
  52.4 8.7 %collective-permute-start.16 = (bf16[2,256,128]{2,1,0:T(8,128)(2,1)S(1)}, bf16[2,256,128]{2,1,0:T(8,128)(2,1)S(1)}, u32[]{:S(2)}, u32[]{:S(2)}) collective-permute-start(bf16[2,256,128]{2,1,0:T(8,128)(2,1)S(1)} %get-tuple-element.42), channel_id=1, source_target_pairs={{0,8},{1,3},{2,10},{3,1},{4,12},{5,7},{6,14},{7,5},{8,0},{9,11},{1... | collective-permute-start | bytes 393224 | tf_op jit(solution)/shard_map/ppermute | solution.py:32
  53.3 7.8 %collective-permute-start.17 = (bf16[2,256,128]{2,1,0:T(8,128)(2,1)S(1)}, bf16[2,256,128]{2,1,0:T(8,128)(2,1)S(1)}, u32[]{:S(2)}, u32[]{:S(2)}) collective-permute-start(bf16[2,256,128]{2,1,0:T(8,128)(2,1)S(1)} %get-tuple-element.42), channel_id=1, source_target_pairs={{0,16},{1,5},{2,18},{3,7},{4,20},{5,1},{6,22},{7,3},{8,24},{9,13},... | collective-permute-start | bytes 393224 | tf_op jit(solution)/shard_map/ppermute | solution.py:32
  56.0 5.2 %collective-permute-start.18 = (bf16[2,256,128]{2,1,0:T(8,128)(2,1)S(1)}, bf16[2,256,128]{2,1,0:T(8,128)(2,1)S(1)}, u32[]{:S(2)}, u32[]{:S(2)}) collective-permute-start(bf16[2,256,128]{2,1,0:T(8,128)(2,1)S(1)} %get-tuple-element.42), channel_id=1, source_target_pairs={{0,24},{1,7},{2,26},{3,5},{4,28},{5,3},{6,30},{7,1},{8,16},{9,15},... | collective-permute-start | bytes 393224 | tf_op jit(solution)/shard_map/ppermute | solution.py:32
  61.0 1.3 %collective-permute-start.21 = (f32[128,128]{1,0:T(8,128)S(1)}, f32[128,128]{1,0:T(8,128)S(1)}, u32[]{:S(2)}, u32[]{:S(2)}) collective-permute-start(f32[128,128]{1,0:T(8,128)S(1)} %precondition.5), channel_id=1, source_target_pairs={{0,1},{1,0},{2,3},{3,2},{4,5},{5,4},{6,7},{7,6},{8,9},{9,8},{10,11... | collective-permute-start | bytes 196616 | tf_op jit(solution)/shard_map/ppermute | solution.py:32
  62.4 15.2 %collective-permute-start.25 = (bf16[4,2,256,128]{3,2,1,0:T(8,128)(2,1)S(1)}, bf16[4,2,256,128]{3,2,1,0:T(8,128)(2,1)S(1)}, u32[]{:S(2)}, u32[]{:S(2)}) collective-permute-start(bf16[4,2,256,128]{3,2,1,0:T(8,128)(2,1)S(1)} %pad_maximum_fusion.1.piece), channel_id=1, source_target_pairs={{0,6},{1,25},{2,4},{3,27},{4,2},{5,29},{6,0},{7,31},{8,14},{9,17},... | collective-permute-start | bytes 1572872 | tf_op jit(solution)/shard_map/ppermute | solution.py:32
  62.5 17.0 %collective-permute-start.24 = (bf16[4,2,256,128]{3,2,1,0:T(8,128)(2,1)S(1)}, bf16[4,2,256,128]{3,2,1,0:T(8,128)(2,1)S(1)}, u32[]{:S(2)}, u32[]{:S(2)}) collective-permute-start(bf16[4,2,256,128]{3,2,1,0:T(8,128)(2,1)S(1)} %pad_maximum_fusion.1.piece), channel_id=1, source_target_pairs={{0,4},{1,17},{2,6},{3,19},{4,0},{5,21},{6,2},{7,23},{8,12},{9,25},... | collective-permute-start | bytes 1572872 | tf_op jit(solution)/shard_map/ppermute | solution.py:32
  62.6 17.8 %collective-permute-start.23 = (bf16[4,2,256,128]{3,2,1,0:T(8,128)(2,1)S(1)}, bf16[4,2,256,128]{3,2,1,0:T(8,128)(2,1)S(1)}, u32[]{:S(2)}, u32[]{:S(2)}) collective-permute-start(bf16[4,2,256,128]{3,2,1,0:T(8,128)(2,1)S(1)} %pad_maximum_fusion.1.piece), channel_id=1, source_target_pairs={{0,2},{1,9},{2,0},{3,11},{4,6},{5,13},{6,4},{7,15},{8,10},{9,1},{1... | collective-permute-start | bytes 1572872 | tf_op jit(solution)/shard_map/ppermute | solution.py:32
  65.7 6.7 %collective-permute-start.22 = (bf16[128,128]{1,0:T(8,128)(2,1)S(1)}, bf16[128,128]{1,0:T(8,128)(2,1)S(1)}, u32[]{:S(2)}, u32[]{:S(2)}) collective-permute-start(bf16[128,128]{1,0:T(8,128)(2,1)S(1)} %add_convert_fusion), channel_id=1, source_target_pairs={{0,128},{1,129},{2,130},{3,131},{4,132},{5,133},{6,134},{7,135},{8... | collective-permute-start | bytes 98312 | tf_op jit(solution)/shard_map/ppermute | solution.py:32
  73.2 8.6 %collective-permute-start.26 = (f32[64,1024]{1,0:T(8,128)S(1)}, f32[64,1024]{1,0:T(8,128)S(1)}, u32[]{:S(2)}, u32[]{:S(2)}) collective-permute-start(f32[64,1024]{1,0:T(8,128)S(1)} %get-tuple-element.29), channel_id=1, source_target_pairs={{0,1},{1,0},{2,3},{3,2},{4,5},{5,4},{6,7},{7,6},{8,9},{9,8},{10,11... | collective-permute-start | bytes 786440 | tf_op jit(solution)/shard_map/ppermute | solution.py:32
  78.4 3.4 %collective-permute-start.29 = (f32[64,1024]{1,0:T(8,128)S(1)}, f32[64,1024]{1,0:T(8,128)S(1)}, u32[]{:S(2)}, u32[]{:S(2)}) collective-permute-start(f32[64,1024]{1,0:T(8,128)S(1)} %get-tuple-element.32), channel_id=1, source_target_pairs={{0,1},{1,0},{2,3},{3,2},{4,5},{5,4},{6,7},{7,6},{8,9},{9,8},{10,11... | collective-permute-start | bytes 786440 | tf_op jit(solution)/shard_map/ppermute | solution.py:32
  80.3 1.6 %collective-permute-start.28 = (f32[64,1024]{1,0:T(8,128)S(1)}, f32[64,1024]{1,0:T(8,128)S(1)}, u32[]{:S(2)}, u32[]{:S(2)}) collective-permute-start(f32[64,1024]{1,0:T(8,128)S(1)} %get-tuple-element.31), channel_id=1, source_target_pairs={{0,1},{1,0},{2,3},{3,2},{4,5},{5,4},{6,7},{7,6},{8,9},{9,8},{10,11... | collective-permute-start | bytes 786440 | tf_op jit(solution)/shard_map/ppermute | solution.py:32
  81.2 1.7 %collective-permute-start.27 = (f32[64,1024]{1,0:T(8,128)S(1)}, f32[64,1024]{1,0:T(8,128)S(1)}, u32[]{:S(2)}, u32[]{:S(2)}) collective-permute-start(f32[64,1024]{1,0:T(8,128)S(1)} %get-tuple-element.30), channel_id=1, source_target_pairs={{0,1},{1,0},{2,3},{3,2},{4,5},{5,4},{6,7},{7,6},{8,9},{9,8},{10,11... | collective-permute-start | bytes 786440 | tf_op jit(solution)/shard_map/ppermute | solution.py:32

commit v13 on v12

--- a/solution.py
+++ b/solution.py
@@ -107,16 +107,15 @@
     pre[...] = total.T if flip else total
 
 
-def tile(where, g, piece, keep, give):
+def tile(g, piece, keep, give):
     blocks = [piece[k2, j] for k2 in range(4) for j in range(2)]
     part = jnp.dot(
         g[...],
         jnp.concatenate(blocks, axis=1),
         preferred_element_type=jnp.float32,
     ) * (1.0 / TOKENS)
-    low, high = part[:64], part[64:]
-    keep[...] = jnp.where(where[3] == 0, low, high)
-    give[...] = jnp.where(where[3] == 0, high, low)
+    keep[...] = part[:64]
+    give[...] = part[64:]
 
 
 def assemble(where, *refs):
@@ -194,22 +193,22 @@
     act = (part + swap_cores(part)).astype(bf16)
     half = jnp.stack([grad_plane, second_turn(grad_plane, 1)])
 
+    there = [to_parity(act, j, 1) for j in (0, 1)]
     here = [to_parity(act, j, 0) for j in (0, 1)]
-    there = [to_parity(act, j, 1) for j in (0, 1)]
     half, here[0] = lax.optimization_barrier((half, here[0]))
     rest = second_turn(half, 3)
     grad_pieces = half[0], half[1], rest[1], rest[0]
-    pair = jnp.stack([jnp.concatenate(p, axis=0) for p in zip(here, there)])
+    pair = jnp.stack([*there, *here]).reshape(2, 2, 128, 128)
+    pair = jnp.swapaxes(pair, 0, 1).reshape(2, 256, 128)
     part = partial((0, 1, 2, 3), grad_pieces, [], grad_rows, False)
     grad = (part + swap_cores(part)).astype(bf16)
     plane = jnp.stack(turned(first_turn, [pair] * 4))
+    grad = jnp.where(first, grad, jnp.concatenate([grad[64:], grad[:64]], axis=0))
     plane, grad = lax.optimization_barrier((plane, grad))
-    grad = jnp.concatenate([grad, swap_reps(grad)], axis=1)
+    grad = jnp.concatenate([swap_reps(grad), grad], axis=1)
 
     made = [
-        call(tile, "tile", [shape((64, 1024), f32)] * 2, [SMEM, VMEM, VMEM])(
-            where, grad, piece
-        )
+        call(tile, "tile", [shape((64, 1024), f32)] * 2, [VMEM] * 2)(grad, piece)
         for piece in turned(second_turn, [plane] * 4)
     ]
     own = [keep for keep, _ in made]

time: 85.4 us -> 83.5 us (0.978)
  Pallas kernels: 8.75 us -> 6.59 us
  waiting for transfers between devices: 27.1 us -> 28.2 us
  starting transfers between devices: 47.2 us -> 46.3 us
    pallas_call x4, Pallas kernels: 3.1 us -> 0.93 us  [on_device(): call(tile, 'tile', [shape((64, 1024), f32)] * 2, [VMEM] * 2)(grad, piece)]
    ppermute x30, waiting for transfers between devices: 27.1 us -> 28.2 us  [send(): return lax.ppermute(value, AXES, pairs)]
    ppermute x30, starting transfers between devices: 47.2 us -> 46.3 us  [send(): return lax.ppermute(value, AXES, pairs)]
  transfers between devices with their start and end apart: 30 -> 30, of which waited for: 15 -> 14; matrix products, arithmetic and copies ran while one was open for 1% -> 1% of each run, Pallas kernels for 8% -> 5%
where the time goes in v13:
time: 83.5 us; the launch traced here: 83.3 us
  starting transfers between devices  46.3 us (55%)
  waiting for transfers between devices  28.2 us (34%)
  Pallas kernels  6.59 us (8%)
  other arithmetic  1.58 us (2%)
    ppermute x30, starting transfers between devices, send(): return lax.ppermute(value, AXES, pairs)  46.3 us
    ppermute x30, waiting for transfers between devices, send(): return lax.ppermute(value, AXES, pairs)  28.2 us
    pallas_call x3, Pallas kernels, partial(): call(functools.partial(precondition, turns, flip), 'precondition', shape(...  3.55 us
    pallas_call x1, Pallas kernels, on_device(): pl.pallas_call(assemble, out_shape=shape((64, 8192), f32), in_specs=[SMEM...  2.1 us
  transfers between devices with their start and end apart: 30, of which 14 were waited for; matrix products, arithmetic and copies ran while one was open for 1% of the time, Pallas kernels for 5%

profile of v13, /device:TPU:1, one launch (start us, length us, event | category | flops | bytes accessed | tf_op | source)
XLA Modules:
  0.0 83.3 jit_solution(973921600257136477)
XLA Ops:
  0.0 0.8 fusion
  0.8 2.5 %collective-permute-start = (bf16[2,64,128]{2,1,0:T(8,128)(2,1)S(1)}, bf16[2,64,128]{2,1,0:T(8,128)(2,1)S(1)}, u32[]{:S(2)}, u32[]{:S(2)}) collective-permute-start(bf16[2,64,128]{2,1,0:T(8,128)(2,1)S(1)} %get-tuple-element.52), channel_id=1, source_target_pairs={{0,32},{1,33},{2,34},{3,35},{4,36},{5,37},{6,38},{7,39},{8,40},{9,... | collective-permute-start | bytes 98312 | tf_op jit(solution)/shard_map/ppermute | solution.py:32
  3.3 3.0 %collective-permute-start.1 = (bf16[2,64,128]{2,1,0:T(8,128)(2,1)S(1)}, bf16[2,64,128]{2,1,0:T(8,128)(2,1)S(1)}, u32[]{:S(2)}, u32[]{:S(2)}) collective-permute-start(bf16[2,64,128]{2,1,0:T(8,128)(2,1)S(1)} %get-tuple-element.52), channel_id=1, source_target_pairs={{0,64},{1,65},{2,66},{3,67},{4,68},{5,69},{6,70},{7,71},{8,72},{9,... | collective-permute-start | bytes 98312 | tf_op jit(solution)/shard_map/ppermute | solution.py:32
  6.3 2.2 %collective-permute-start.9 = (bf16[64,8192]{1,0:T(8,128)(2,1)}, bf16[64,8192]{1,0:T(8,128)(2,1)S(1)}, u32[]{:S(2)}, u32[]{:S(2)}) collective-permute-start(bf16[64,8192]{1,0:T(8,128)(2,1)} %param.6), channel_id=1, source_target_pairs={{0,1},{1,0},{2,3},{3,2},{4,5},{5,4},{6,7},{7,6},{8,9},{9,8},{10,11... | collective-permute-start | bytes 3145736 | tf_op jit(solution)/shard_map/ppermute | solution.py:32
  8.5 2.3 %collective-permute-done.2 = bf16[2,64,128]{2,1,0:T(8,128)(2,1)S(1)} collective-permute-done((bf16[2,64,128]{2,1,0:T(8,128)(2,1)S(1)}, bf16[2,64,128]{2,1,0:T(8,128)(2,1)S(1)}, u32[]{:S(2)}, u32[]{:S(2)}) %collective-permute-start.2) | collective-permute-done | bytes 32800 | tf_op jit(solution)/shard_map/ppermute | solution.py:32
  10.9 1.3 %collective-permute-start.3 = (bf16[4,2,64,128]{3,2,0,1:T(8,128)(2,1)S(1)}, bf16[4,2,64,128]{3,2,0,1:T(8,128)(2,1)S(1)}, u32[]{:S(2)}, u32[]{:S(2)}) collective-permute-start(bf16[4,2,64,128]{3,2,0,1:T(8,128)(2,1)S(1)} %pad_maximum_fusion.4), channel_id=1, source_target_pairs={{0,8},{1,3},{2,10},{3,1},{4,12},{5,7},{6,14},{7,5},{8,0},{9,11},{1... | collective-permute-start | bytes 393224 | tf_op jit(solution)/shard_map/ppermute | solution.py:32
  12.2 2.5 %collective-permute-start.4 = (bf16[4,2,64,128]{3,2,0,1:T(8,128)(2,1)S(1)}, bf16[4,2,64,128]{3,2,0,1:T(8,128)(2,1)S(1)}, u32[]{:S(2)}, u32[]{:S(2)}) collective-permute-start(bf16[4,2,64,128]{3,2,0,1:T(8,128)(2,1)S(1)} %pad_maximum_fusion.4), channel_id=1, source_target_pairs={{0,16},{1,5},{2,18},{3,7},{4,20},{5,1},{6,22},{7,3},{8,24},{9,13},... | collective-permute-start | bytes 393224 | tf_op jit(solution)/shard_map/ppermute | solution.py:32
  14.9 3.5 %collective-permute-done.4 = bf16[4,2,64,128]{3,2,0,1:T(8,128)(2,1)S(1)} collective-permute-done((bf16[4,2,64,128]{3,2,0,1:T(8,128)(2,1)S(1)}, bf16[4,2,64,128]{3,2,0,1:T(8,128)(2,1)S(1)}, u32[]{:S(2)}, u32[]{:S(2)}) %collective-permute-start.4) | collective-permute-done | bytes 131104 | tf_op jit(solution)/shard_map/ppermute | solution.py:32
  18.4 1.4 %collective-permute-done.5 = bf16[4,2,64,128]{3,2,0,1:T(8,128)(2,1)S(1)} collective-permute-done((bf16[4,2,64,128]{3,2,0,1:T(8,128)(2,1)S(1)}, bf16[4,2,64,128]{3,2,0,1:T(8,128)(2,1)S(1)}, u32[]{:S(2)}, u32[]{:S(2)}) %collective-permute-start.5) | collective-permute-done | bytes 131104 | tf_op jit(solution)/shard_map/ppermute | solution.py:32
  19.8 3.1 %collective-permute-start.7 = (bf16[4,4,64,128]{3,2,1,0:T(8,128)(2,1)S(1)}, bf16[4,4,64,128]{3,2,1,0:T(8,128)(2,1)S(1)}, u32[]{:S(2)}, u32[]{:S(2)}) collective-permute-start(bf16[4,4,64,128]{3,2,1,0:T(8,128)(2,1)S(1)} %pad_maximum_fusion.2.refs_0_), channel_id=1, source_target_pairs={{0,6},{1,25},{2,4},{3,27},{4,2},{5,29},{6,0},{7,31},{8,14},{9,17},... | collective-permute-start | bytes 786440 | tf_op jit(solution)/shard_map/ppermute | solution.py:32
  23.8 5.2 %collective-permute-done.7.refs_1_ = bf16[4,4,64,128]{3,2,1,0:T(8,128)(2,1)S(1)} collective-permute-done((bf16[4,4,64,128]{3,2,1,0:T(8,128)(2,1)S(1)}, bf16[4,4,64,128]{3,2,1,0:T(8,128)(2,1)S(1)}, u32[]{:S(2)}, u32[]{:S(2)}) %collective-permute-start.7) | collective-permute-done | bytes 262176 | tf_op jit(solution)/shard_map/ppermute | solution.py:32
  29.7 1.2 %precondition.3.refs_1_ = f32[128,128]{1,0:T(8,128)S(1)} custom-call(s32[4]{0:T(128)S(1)} %pad_add_fusion.where, bf16[4,4,64,128]{3,2,1,0:T(8,128)(2,1)S(1)} %pad_maximum_fusion.2.refs_0_, bf16[4,4,64,128]{3,2,1,0:T(8,128)(2,1)S(1)} %collective-permute-done.7.refs_1_, bf16[4,4,64,128]{3,2,1,0:T(8,128)(2,1)S(1)} %collective-permute-done.8.refs_2_, ...), custom_call_target="tpu_custom_call" | custom-call | tf_op jit(solution)/shard_map/precondition/pallas_call | solution.py:181
  30.9 0.9 %precondition.4 = f32[128,128]{1,0:T(8,128)S(1)} custom-call(s32[4]{0:T(128)S(1)} %pad_add_fusion.where, bf16[4,4,64,128]{3,2,1,0:T(8,128)(2,1)S(1)} %collective-permute-done.6.refs_0_, f32[128,128]{1,0:T(8,128)S(1)} %precondition.3.refs_1_, bf16[64,8192]{1,0:T(8,128)(2,1)S(1)} %get-tuple-element.36.refs_3_.refs_2_, ...), custom_call_target="tpu_custom_call" | custom-call | tf_op jit(solution)/shard_map/precondition/pallas_call | solution.py:181
  31.9 6.4 %collective-permute-start.10 = (f32[128,128]{1,0:T(8,128)S(1)}, f32[128,128]{1,0:T(8,128)S(1)}, u32[]{:S(2)}, u32[]{:S(2)}) collective-permute-start(f32[128,128]{1,0:T(8,128)S(1)} %precondition.4), channel_id=1, source_target_pairs={{0,1},{1,0},{2,3},{3,2},{4,5},{5,4},{6,7},{7,6},{8,9},{9,8},{10,11... | collective-permute-start | bytes 196616 | tf_op jit(solution)/shard_map/ppermute | solution.py:32
  38.3 0.9 %collective-permute-done.10 = f32[128,128]{1,0:T(8,128)S(1)} collective-permute-done((f32[128,128]{1,0:T(8,128)S(1)}, f32[128,128]{1,0:T(8,128)S(1)}, u32[]{:S(2)}, u32[]{:S(2)}) %collective-permute-start.10) | collective-permute-done | bytes 65568 | tf_op jit(solution)/shard_map/ppermute | solution.py:32
  39.2 1.9 %collective-permute-start.14 = (bf16[128,128]{1,0:T(8,128)(2,1)S(1)}, bf16[128,128]{1,0:T(8,128)(2,1)S(1)}, u32[]{:S(2)}, u32[]{:S(2)}) collective-permute-start(bf16[128,128]{1,0:T(8,128)(2,1)S(1)} %add_convert_fusion.1), channel_id=1, source_target_pairs={{0,0},{1,32},{2,2},{3,34},{4,4},{5,36},{6,6},{7,38},{8,8},{9,40},{... | collective-permute-start | bytes 98312 | tf_op jit(solution)/shard_map/ppermute | solution.py:32
  41.1 2.5 %collective-permute-start.11 = (bf16[128,128]{1,0:T(8,128)(2,1)S(1)}, bf16[128,128]{1,0:T(8,128)(2,1)S(1)}, u32[]{:S(2)}, u32[]{:S(2)}) collective-permute-start(bf16[128,128]{1,0:T(8,128)(2,1)S(1)} %add_convert_fusion.1), channel_id=1, source_target_pairs={{0,128},{1,160},{2,130},{3,162},{4,132},{5,164},{6,134},{7,166},{8... | collective-permute-start | bytes 98312 | tf_op jit(solution)/shard_map/ppermute | solution.py:32
  43.6 0.8 collective-permute-start.12
  44.4 2.8 %collective-permute-start.15 = (bf16[128,128]{1,0:T(8,128)(2,1)S(1)}, bf16[128,128]{1,0:T(8,128)(2,1)S(1)}, u32[]{:S(2)}, u32[]{:S(2)}) collective-permute-start(bf16[128,128]{1,0:T(8,128)(2,1)S(1)} %add_convert_fusion.1), channel_id=1, source_target_pairs={{0,64},{1,96},{2,66},{3,98},{4,68},{5,100},{6,70},{7,102},{8,72},{... | collective-permute-start | bytes 98312 | tf_op jit(solution)/shard_map/ppermute | solution.py:32
  47.8 2.3 %collective-permute-done.15 = bf16[128,128]{1,0:T(8,128)(2,1)S(1)} collective-permute-done((bf16[128,128]{1,0:T(8,128)(2,1)S(1)}, bf16[128,128]{1,0:T(8,128)(2,1)S(1)}, u32[]{:S(2)}, u32[]{:S(2)}) %collective-permute-start.15) | collective-permute-done | bytes 32800 | tf_op jit(solution)/shard_map/ppermute | solution.py:32
  50.4 3.4 %collective-permute-start.17 = (bf16[2,256,128]{2,1,0:T(8,128)(2,1)S(1)}, bf16[2,256,128]{2,1,0:T(8,128)(2,1)S(1)}, u32[]{:S(2)}, u32[]{:S(2)}) collective-permute-start(bf16[2,256,128]{2,1,0:T(8,128)(2,1)S(1)} %bitcast.63), channel_id=1, source_target_pairs={{0,16},{1,5},{2,18},{3,7},{4,20},{5,1},{6,22},{7,3},{8,24},{9,13},... | collective-permute-start | bytes 393224 | tf_op jit(solution)/shard_map/ppermute | solution.py:32
  54.3 4.8 %collective-permute-done.19 = bf16[2,4,4,64,128]{4,3,2,1,0:T(8,128)(2,1)S(1)} collective-permute-done((bf16[2,4,4,64,128]{4,3,2,1,0:T(8,128)(2,1)S(1)}, bf16[2,4,4,64,128]{4,3,2,1,0:T(8,128)(2,1)S(1)}, u32[]{:S(2)}, u32[]{:S(2)}) %collective-permute-start.19) | collective-permute-done | bytes 524320 | tf_op jit(solution)/shard_map/ppermute | solution.py:32
  59.1 1.4 %precondition.5 = f32[128,128]{1,0:T(8,128)S(1)} custom-call(s32[4]{0:T(128)S(1)} %pad_add_fusion.where, bf16[4,4,64,128]{3,2,1,0:T(8,128)(2,1)S(1)} %get-tuple-element.40.refs_0_, bf16[4,4,64,128]{3,2,1,0:T(8,128)(2,1)S(1)} %get-tuple-element.39.refs_1_, bf16[4,4,64,128]{3,2,1,0:T(8,128)(2,1)S(1)} %get-tuple-element.38.refs_2_, ...), custom_call_target="tpu_custom_call" | custom-call | tf_op jit(solution)/shard_map/precondition/pallas_call | solution.py:181
  60.7 1.1 %collective-permute-done.21 = f32[128,128]{1,0:T(8,128)S(1)} collective-permute-done((f32[128,128]{1,0:T(8,128)S(1)}, f32[128,128]{1,0:T(8,128)S(1)}, u32[]{:S(2)}, u32[]{:S(2)}) %collective-permute-start.21) | collective-permute-done | bytes 65568 | tf_op jit(solution)/shard_map/ppermute | solution.py:32
  62.1 3.1 %collective-permute-start.23 = (bf16[4,2,256,128]{3,2,1,0:T(8,128)(2,1)S(1)}, bf16[4,2,256,128]{3,2,1,0:T(8,128)(2,1)S(1)}, u32[]{:S(2)}, u32[]{:S(2)}) collective-permute-start(bf16[4,2,256,128]{3,2,1,0:T(8,128)(2,1)S(1)} %pad_maximum_fusion.1.piece), channel_id=1, source_target_pairs={{0,2},{1,9},{2,0},{3,11},{4,6},{5,13},{6,4},{7,15},{8,10},{9,1},{1... | collective-permute-start | bytes 1572872 | tf_op jit(solution)/shard_map/ppermute | solution.py:32
  65.3 4.4 %collective-permute-start.22 = (bf16[128,128]{1,0:T(8,128)(2,1)S(1)}, bf16[128,128]{1,0:T(8,128)(2,1)S(1)}, u32[]{:S(2)}, u32[]{:S(2)}) collective-permute-start(bf16[128,128]{1,0:T(8,128)(2,1)S(1)} %maximum_select_fusion), channel_id=1, source_target_pairs={{0,128},{1,129},{2,130},{3,131},{4,132},{5,133},{6,134},{7,135},{8... | collective-permute-start | bytes 98312 | tf_op jit(solution)/shard_map/ppermute | solution.py:32
  69.6 2.3 %collective-permute-done.22 = bf16[128,128]{1,0:T(8,128)(2,1)S(1)} collective-permute-done((bf16[128,128]{1,0:T(8,128)(2,1)S(1)}, bf16[128,128]{1,0:T(8,128)(2,1)S(1)}, u32[]{:S(2)}, u32[]{:S(2)}) %collective-permute-start.22) | collective-permute-done | bytes 32800 | tf_op jit(solution)/shard_map/ppermute | solution.py:32
  72.2 2.5 %collective-permute-start.26 = (f32[64,1024]{1,0:T(8,128)S(1)}, f32[64,1024]{1,0:T(8,128)S(1)}, u32[]{:S(2)}, u32[]{:S(2)}) collective-permute-start(f32[64,1024]{1,0:T(8,128)S(1)} %get-tuple-element.29), channel_id=1, source_target_pairs={{0,1},{1,0},{2,3},{3,2},{4,5},{5,4},{6,7},{7,6},{8,9},{9,8},{10,11... | collective-permute-start | bytes 786440 | tf_op jit(solution)/shard_map/ppermute | solution.py:32
  74.7 2.4 %collective-permute-done.25.piece = bf16[4,2,256,128]{3,2,1,0:T(8,128)(2,1)S(1)} collective-permute-done((bf16[4,2,256,128]{3,2,1,0:T(8,128)(2,1)S(1)}, bf16[4,2,256,128]{3,2,1,0:T(8,128)(2,1)S(1)}, u32[]{:S(2)}, u32[]{:S(2)}) %collective-permute-start.25) | collective-permute-done | bytes 524320 | tf_op jit(solution)/shard_map/ppermute | solution.py:32
  77.4 1.3 %collective-permute-start.29 = (f32[64,1024]{1,0:T(8,128)S(1)}, f32[64,1024]{1,0:T(8,128)S(1)}, u32[]{:S(2)}, u32[]{:S(2)}) collective-permute-start(f32[64,1024]{1,0:T(8,128)S(1)} %get-tuple-element.32), channel_id=1, source_target_pairs={{0,1},{1,0},{2,3},{3,2},{4,5},{5,4},{6,7},{7,6},{8,9},{9,8},{10,11... | collective-permute-start | bytes 786440 | tf_op jit(solution)/shard_map/ppermute | solution.py:32
  79.9 0.7 collective-permute-done.28.refs_6_
  81.0 2.1 %assemble.1 = f32[64,8192]{1,0:T(8,128)} custom-call(s32[4]{0:T(128)S(1)} %pad_add_fusion.where, f32[64,1024]{1,0:T(8,128)S(1)} %get-tuple-element.25.refs_0_, f32[64,1024]{1,0:T(8,128)S(1)} %get-tuple-element.26.refs_1_, f32[64,1024]{1,0:T(8,128)S(1)} %get-tuple-element.27.refs_2_, f32[64,1024]{1,0:T(8,128)S(1)} %get-tuple-element.28.refs_3_, ...), custom_call_target="tpu_custom_call" | custom-call | tf_op jit(solution)/shard_map/assemble/pallas_call | solution.py:216
  (63 shorter events, 5.8 us)
Async XLA Ops:
  0.0 23.7 %copy-start = (bf16[64,8192]{1,0:T(8,128)(2,1)S(1)}, bf16[64,8192]{1,0:T(8,128)(2,1)}, u32[]{:S(2)}) copy-start(bf16[64,8192]{1,0:T(8,128)(2,1)} %param.6) | copy-start | bytes 3145732
  0.8 7.7 %collective-permute-start = (bf16[2,64,128]{2,1,0:T(8,128)(2,1)S(1)}, bf16[2,64,128]{2,1,0:T(8,128)(2,1)S(1)}, u32[]{:S(2)}, u32[]{:S(2)}) collective-permute-start(bf16[2,64,128]{2,1,0:T(8,128)(2,1)S(1)} %get-tuple-element.52), channel_id=1, source_target_pairs={{0,32},{1,33},{2,34},{3,35},{4,36},{5,37},{6,38},{7,39},{8,40},{9,... | collective-permute-start | bytes 98312 | tf_op jit(solution)/shard_map/ppermute | solution.py:32
  3.3 5.2 %collective-permute-start.1 = (bf16[2,64,128]{2,1,0:T(8,128)(2,1)S(1)}, bf16[2,64,128]{2,1,0:T(8,128)(2,1)S(1)}, u32[]{:S(2)}, u32[]{:S(2)}) collective-permute-start(bf16[2,64,128]{2,1,0:T(8,128)(2,1)S(1)} %get-tuple-element.52), channel_id=1, source_target_pairs={{0,64},{1,65},{2,66},{3,67},{4,68},{5,69},{6,70},{7,71},{8,72},{9,... | collective-permute-start | bytes 98312 | tf_op jit(solution)/shard_map/ppermute | solution.py:32
  6.3 4.6 %collective-permute-start.2 = (bf16[2,64,128]{2,1,0:T(8,128)(2,1)S(1)}, bf16[2,64,128]{2,1,0:T(8,128)(2,1)S(1)}, u32[]{:S(2)}, u32[]{:S(2)}) collective-permute-start(bf16[2,64,128]{2,1,0:T(8,128)(2,1)S(1)} %get-tuple-element.52), channel_id=1, source_target_pairs={{0,96},{1,97},{2,98},{3,99},{4,100},{5,101},{6,102},{7,103},{8,104... | collective-permute-start | bytes 98312 | tf_op jit(solution)/shard_map/ppermute | solution.py:32
  6.3 17.4 %collective-permute-start.9 = (bf16[64,8192]{1,0:T(8,128)(2,1)}, bf16[64,8192]{1,0:T(8,128)(2,1)S(1)}, u32[]{:S(2)}, u32[]{:S(2)}) collective-permute-start(bf16[64,8192]{1,0:T(8,128)(2,1)} %param.6), channel_id=1, source_target_pairs={{0,1},{1,0},{2,3},{3,2},{4,5},{5,4},{6,7},{7,6},{8,9},{9,8},{10,11... | collective-permute-start | bytes 3145736 | tf_op jit(solution)/shard_map/ppermute | solution.py:32
  8.5 38.9 %collective-permute-start.20 = (bf16[64,8192]{1,0:T(8,128)(2,1)}, bf16[64,8192]{1,0:T(8,128)(2,1)S(1)}, u32[]{:S(2)}, u32[]{:S(2)}) collective-permute-start(bf16[64,8192]{1,0:T(8,128)(2,1)} %param.7), channel_id=1, source_target_pairs={{0,1},{1,0},{2,3},{3,2},{4,5},{5,4},{6,7},{7,6},{8,9},{9,8},{10,11... | collective-permute-start | bytes 3145736 | tf_op jit(solution)/shard_map/ppermute | solution.py:32
  10.9 4.0 %collective-permute-start.3 = (bf16[4,2,64,128]{3,2,0,1:T(8,128)(2,1)S(1)}, bf16[4,2,64,128]{3,2,0,1:T(8,128)(2,1)S(1)}, u32[]{:S(2)}, u32[]{:S(2)}) collective-permute-start(bf16[4,2,64,128]{3,2,0,1:T(8,128)(2,1)S(1)} %pad_maximum_fusion.4), channel_id=1, source_target_pairs={{0,8},{1,3},{2,10},{3,1},{4,12},{5,7},{6,14},{7,5},{8,0},{9,11},{1... | collective-permute-start | bytes 393224 | tf_op jit(solution)/shard_map/ppermute | solution.py:32
  12.2 6.2 %collective-permute-start.4 = (bf16[4,2,64,128]{3,2,0,1:T(8,128)(2,1)S(1)}, bf16[4,2,64,128]{3,2,0,1:T(8,128)(2,1)S(1)}, u32[]{:S(2)}, u32[]{:S(2)}) collective-permute-start(bf16[4,2,64,128]{3,2,0,1:T(8,128)(2,1)S(1)} %pad_maximum_fusion.4), channel_id=1, source_target_pairs={{0,16},{1,5},{2,18},{3,7},{4,20},{5,1},{6,22},{7,3},{8,24},{9,13},... | collective-permute-start | bytes 393224 | tf_op jit(solution)/shard_map/ppermute | solution.py:32
  14.6 5.2 %collective-permute-start.5 = (bf16[4,2,64,128]{3,2,0,1:T(8,128)(2,1)S(1)}, bf16[4,2,64,128]{3,2,0,1:T(8,128)(2,1)S(1)}, u32[]{:S(2)}, u32[]{:S(2)}) collective-permute-start(bf16[4,2,64,128]{3,2,0,1:T(8,128)(2,1)S(1)} %pad_maximum_fusion.4), channel_id=1, source_target_pairs={{0,24},{1,7},{2,26},{3,5},{4,28},{5,3},{6,30},{7,1},{8,16},{9,15},... | collective-permute-start | bytes 393224 | tf_op jit(solution)/shard_map/ppermute | solution.py:32
  19.8 9.2 %collective-permute-start.7 = (bf16[4,4,64,128]{3,2,1,0:T(8,128)(2,1)S(1)}, bf16[4,4,64,128]{3,2,1,0:T(8,128)(2,1)S(1)}, u32[]{:S(2)}, u32[]{:S(2)}) collective-permute-start(bf16[4,4,64,128]{3,2,1,0:T(8,128)(2,1)S(1)} %pad_maximum_fusion.2.refs_0_), channel_id=1, source_target_pairs={{0,6},{1,25},{2,4},{3,27},{4,2},{5,29},{6,0},{7,31},{8,14},{9,17},... | collective-permute-start | bytes 786440 | tf_op jit(solution)/shard_map/ppermute | solution.py:32
  23.0 6.7 %collective-permute-start.8 = (bf16[4,4,64,128]{3,2,1,0:T(8,128)(2,1)S(1)}, bf16[4,4,64,128]{3,2,1,0:T(8,128)(2,1)S(1)}, u32[]{:S(2)}, u32[]{:S(2)}) collective-permute-start(bf16[4,4,64,128]{3,2,1,0:T(8,128)(2,1)S(1)} %pad_maximum_fusion.2.refs_0_), channel_id=1, source_target_pairs={{0,4},{1,17},{2,6},{3,19},{4,0},{5,21},{6,2},{7,23},{8,12},{9,25},... | collective-permute-start | bytes 786440 | tf_op jit(solution)/shard_map/ppermute | solution.py:32
  23.2 7.8 %collective-permute-start.6 = (bf16[4,4,64,128]{3,2,1,0:T(8,128)(2,1)S(1)}, bf16[4,4,64,128]{3,2,1,0:T(8,128)(2,1)S(1)}, u32[]{:S(2)}, u32[]{:S(2)}) collective-permute-start(bf16[4,4,64,128]{3,2,1,0:T(8,128)(2,1)S(1)} %pad_maximum_fusion.2.refs_0_), channel_id=1, source_target_pairs={{0,2},{1,9},{2,0},{3,11},{4,6},{5,13},{6,4},{7,15},{8,10},{9,1},{1... | collective-permute-start | bytes 786440 | tf_op jit(solution)/shard_map/ppermute | solution.py:32
  30.9 16.4 %copy-start.1 = (bf16[64,8192]{1,0:T(8,128)(2,1)S(1)}, bf16[64,8192]{1,0:T(8,128)(2,1)}, u32[]{:S(2)}) copy-start(bf16[64,8192]{1,0:T(8,128)(2,1)} %param.7) | copy-start | bytes 3145732
  31.9 7.3 %collective-permute-start.10 = (f32[128,128]{1,0:T(8,128)S(1)}, f32[128,128]{1,0:T(8,128)S(1)}, u32[]{:S(2)}, u32[]{:S(2)}) collective-permute-start(f32[128,128]{1,0:T(8,128)S(1)} %precondition.4), channel_id=1, source_target_pairs={{0,1},{1,0},{2,3},{3,2},{4,5},{5,4},{6,7},{7,6},{8,9},{9,8},{10,11... | collective-permute-start | bytes 196616 | tf_op jit(solution)/shard_map/ppermute | solution.py:32
  38.3 6.1 %collective-permute-start.13 = (bf16[4,4,64,128]{3,2,1,0:T(8,128)(2,1)S(1)}, bf16[4,4,64,128]{3,2,1,0:T(8,128)(2,1)S(1)}, u32[]{:S(2)}, u32[]{:S(2)}) collective-permute-start(bf16[4,4,64,128]{3,2,1,0:T(8,128)(2,1)S(1)} %pad_maximum_fusion.3), channel_id=1, source_target_pairs={{0,2},{1,9},{2,0},{3,11},{4,6},{5,13},{6,4},{7,15},{8,10},{9,1},{1... | collective-permute-start | bytes 786440 | tf_op jit(solution)/shard_map/ppermute | solution.py:32
  39.2 8.0 %collective-permute-start.14 = (bf16[128,128]{1,0:T(8,128)(2,1)S(1)}, bf16[128,128]{1,0:T(8,128)(2,1)S(1)}, u32[]{:S(2)}, u32[]{:S(2)}) collective-permute-start(bf16[128,128]{1,0:T(8,128)(2,1)S(1)} %add_convert_fusion.1), channel_id=1, source_target_pairs={{0,0},{1,32},{2,2},{3,34},{4,4},{5,36},{6,6},{7,38},{8,8},{9,40},{... | collective-permute-start | bytes 98312 | tf_op jit(solution)/shard_map/ppermute | solution.py:32
  41.1 6.5 %collective-permute-start.11 = (bf16[128,128]{1,0:T(8,128)(2,1)S(1)}, bf16[128,128]{1,0:T(8,128)(2,1)S(1)}, u32[]{:S(2)}, u32[]{:S(2)}) collective-permute-start(bf16[128,128]{1,0:T(8,128)(2,1)S(1)} %add_convert_fusion.1), channel_id=1, source_target_pairs={{0,128},{1,160},{2,130},{3,162},{4,132},{5,164},{6,134},{7,166},{8... | collective-permute-start | bytes 98312 | tf_op jit(solution)/shard_map/ppermute | solution.py:32
  43.6 4.2 %collective-permute-start.12 = (bf16[128,128]{1,0:T(8,128)(2,1)S(1)}, bf16[128,128]{1,0:T(8,128)(2,1)S(1)}, u32[]{:S(2)}, u32[]{:S(2)}) collective-permute-start(bf16[128,128]{1,0:T(8,128)(2,1)S(1)} %add_convert_fusion.1), channel_id=1, source_target_pairs={{0,192},{1,224},{2,194},{3,226},{4,196},{5,228},{6,198},{7,230},{8... | collective-permute-start | bytes 98312 | tf_op jit(solution)/shard_map/ppermute | solution.py:32
  44.4 5.7 %collective-permute-start.15 = (bf16[128,128]{1,0:T(8,128)(2,1)S(1)}, bf16[128,128]{1,0:T(8,128)(2,1)S(1)}, u32[]{:S(2)}, u32[]{:S(2)}) collective-permute-start(bf16[128,128]{1,0:T(8,128)(2,1)S(1)} %add_convert_fusion.1), channel_id=1, source_target_pairs={{0,64},{1,96},{2,66},{3,98},{4,68},{5,100},{6,70},{7,102},{8,72},{... | collective-permute-start | bytes 98312 | tf_op jit(solution)/shard_map/ppermute | solution.py:32
  47.2 11.8 %collective-permute-start.19 = (bf16[2,4,4,64,128]{4,3,2,1,0:T(8,128)(2,1)S(1)}, bf16[2,4,4,64,128]{4,3,2,1,0:T(8,128)(2,1)S(1)}, u32[]{:S(2)}, u32[]{:S(2)}) collective-permute-start(bf16[2,4,4,64,128]{4,3,2,1,0:T(8,128)(2,1)S(1)} %pad_maximum_fusion), channel_id=1, source_target_pairs={{0,6},{1,25},{2,4},{3,27},{4,2},{5,29},{6,0},{7,31},{8,14},{9,17},... | collective-permute-start | bytes 1572872 | tf_op jit(solution)/shard_map/ppermute | solution.py:32
  50.1 10.5 %collective-permute-start.16 = (bf16[2,256,128]{2,1,0:T(8,128)(2,1)S(1)}, bf16[2,256,128]{2,1,0:T(8,128)(2,1)S(1)}, u32[]{:S(2)}, u32[]{:S(2)}) collective-permute-start(bf16[2,256,128]{2,1,0:T(8,128)(2,1)S(1)} %bitcast.62), channel_id=1, source_target_pairs={{0,8},{1,3},{2,10},{3,1},{4,12},{5,7},{6,14},{7,5},{8,0},{9,11},{1... | collective-permute-start | bytes 393224 | tf_op jit(solution)/shard_map/ppermute | solution.py:32
  50.4 10.2 %collective-permute-start.17 = (bf16[2,256,128]{2,1,0:T(8,128)(2,1)S(1)}, bf16[2,256,128]{2,1,0:T(8,128)(2,1)S(1)}, u32[]{:S(2)}, u32[]{:S(2)}) collective-permute-start(bf16[2,256,128]{2,1,0:T(8,128)(2,1)S(1)} %bitcast.63), channel_id=1, source_target_pairs={{0,16},{1,5},{2,18},{3,7},{4,20},{5,1},{6,22},{7,3},{8,24},{9,13},... | collective-permute-start | bytes 393224 | tf_op jit(solution)/shard_map/ppermute | solution.py:32
  53.8 6.8 %collective-permute-start.18 = (bf16[2,256,128]{2,1,0:T(8,128)(2,1)S(1)}, bf16[2,256,128]{2,1,0:T(8,128)(2,1)S(1)}, u32[]{:S(2)}, u32[]{:S(2)}) collective-permute-start(bf16[2,256,128]{2,1,0:T(8,128)(2,1)S(1)} %bitcast.64), channel_id=1, source_target_pairs={{0,24},{1,7},{2,26},{3,5},{4,28},{5,3},{6,30},{7,1},{8,16},{9,15},... | collective-permute-start | bytes 393224 | tf_op jit(solution)/shard_map/ppermute | solution.py:32
  60.5 1.3 %collective-permute-start.21 = (f32[128,128]{1,0:T(8,128)S(1)}, f32[128,128]{1,0:T(8,128)S(1)}, u32[]{:S(2)}, u32[]{:S(2)}) collective-permute-start(f32[128,128]{1,0:T(8,128)S(1)} %precondition.5), channel_id=1, source_target_pairs={{0,1},{1,0},{2,3},{3,2},{4,5},{5,4},{6,7},{7,6},{8,9},{9,8},{10,11... | collective-permute-start | bytes 196616 | tf_op jit(solution)/shard_map/ppermute | solution.py:32
  61.9 15.2 %collective-permute-start.25 = (bf16[4,2,256,128]{3,2,1,0:T(8,128)(2,1)S(1)}, bf16[4,2,256,128]{3,2,1,0:T(8,128)(2,1)S(1)}, u32[]{:S(2)}, u32[]{:S(2)}) collective-permute-start(bf16[4,2,256,128]{3,2,1,0:T(8,128)(2,1)S(1)} %pad_maximum_fusion.1.piece), channel_id=1, source_target_pairs={{0,6},{1,25},{2,4},{3,27},{4,2},{5,29},{6,0},{7,31},{8,14},{9,17},... | collective-permute-start | bytes 1572872 | tf_op jit(solution)/shard_map/ppermute | solution.py:32
  62.0 16.7 %collective-permute-start.24 = (bf16[4,2,256,128]{3,2,1,0:T(8,128)(2,1)S(1)}, bf16[4,2,256,128]{3,2,1,0:T(8,128)(2,1)S(1)}, u32[]{:S(2)}, u32[]{:S(2)}) collective-permute-start(bf16[4,2,256,128]{3,2,1,0:T(8,128)(2,1)S(1)} %pad_maximum_fusion.1.piece), channel_id=1, source_target_pairs={{0,4},{1,17},{2,6},{3,19},{4,0},{5,21},{6,2},{7,23},{8,12},{9,25},... | collective-permute-start | bytes 1572872 | tf_op jit(solution)/shard_map/ppermute | solution.py:32
  62.1 16.9 %collective-permute-start.23 = (bf16[4,2,256,128]{3,2,1,0:T(8,128)(2,1)S(1)}, bf16[4,2,256,128]{3,2,1,0:T(8,128)(2,1)S(1)}, u32[]{:S(2)}, u32[]{:S(2)}) collective-permute-start(bf16[4,2,256,128]{3,2,1,0:T(8,128)(2,1)S(1)} %pad_maximum_fusion.1.piece), channel_id=1, source_target_pairs={{0,2},{1,9},{2,0},{3,11},{4,6},{5,13},{6,4},{7,15},{8,10},{9,1},{1... | collective-permute-start | bytes 1572872 | tf_op jit(solution)/shard_map/ppermute | solution.py:32
  65.3 6.7 %collective-permute-start.22 = (bf16[128,128]{1,0:T(8,128)(2,1)S(1)}, bf16[128,128]{1,0:T(8,128)(2,1)S(1)}, u32[]{:S(2)}, u32[]{:S(2)}) collective-permute-start(bf16[128,128]{1,0:T(8,128)(2,1)S(1)} %maximum_select_fusion), channel_id=1, source_target_pairs={{0,128},{1,129},{2,130},{3,131},{4,132},{5,133},{6,134},{7,135},{8... | collective-permute-start | bytes 98312 | tf_op jit(solution)/shard_map/ppermute | solution.py:32
  72.2 7.7 %collective-permute-start.26 = (f32[64,1024]{1,0:T(8,128)S(1)}, f32[64,1024]{1,0:T(8,128)S(1)}, u32[]{:S(2)}, u32[]{:S(2)}) collective-permute-start(f32[64,1024]{1,0:T(8,128)S(1)} %get-tuple-element.29), channel_id=1, source_target_pairs={{0,1},{1,0},{2,3},{3,2},{4,5},{5,4},{6,7},{7,6},{8,9},{9,8},{10,11... | collective-permute-start | bytes 786440 | tf_op jit(solution)/shard_map/ppermute | solution.py:32
  77.4 2.5 %collective-permute-start.29 = (f32[64,1024]{1,0:T(8,128)S(1)}, f32[64,1024]{1,0:T(8,128)S(1)}, u32[]{:S(2)}, u32[]{:S(2)}) collective-permute-start(f32[64,1024]{1,0:T(8,128)S(1)} %get-tuple-element.32), channel_id=1, source_target_pairs={{0,1},{1,0},{2,3},{3,2},{4,5},{5,4},{6,7},{7,6},{8,9},{9,8},{10,11... | collective-permute-start | bytes 786440 | tf_op jit(solution)/shard_map/ppermute | solution.py:32
  79.0 1.6 %collective-permute-start.28 = (f32[64,1024]{1,0:T(8,128)S(1)}, f32[64,1024]{1,0:T(8,128)S(1)}, u32[]{:S(2)}, u32[]{:S(2)}) collective-permute-start(f32[64,1024]{1,0:T(8,128)S(1)} %get-tuple-element.31), channel_id=1, source_target_pairs={{0,1},{1,0},{2,3},{3,2},{4,5},{5,4},{6,7},{7,6},{8,9},{9,8},{10,11... | collective-permute-start | bytes 786440 | tf_op jit(solution)/shard_map/ppermute | solution.py:32
  79.3 1.7 %collective-permute-start.27 = (f32[64,1024]{1,0:T(8,128)S(1)}, f32[64,1024]{1,0:T(8,128)S(1)}, u32[]{:S(2)}, u32[]{:S(2)}) collective-permute-start(f32[64,1024]{1,0:T(8,128)S(1)} %get-tuple-element.30), channel_id=1, source_target_pairs={{0,1},{1,0},{2,3},{3,2},{4,5},{5,4},{6,7},{7,6},{8,9},{9,8},{10,11... | collective-permute-start | bytes 786440 | tf_op jit(solution)/shard_map/ppermute | solution.py:32

commit v14 on v13

--- a/solution.py
+++ b/solution.py
@@ -70,13 +70,18 @@
     return [values[0]] + [got[k] for k in (1, 2, 3)]
 
 
+def here_is():
+    return [lax.axis_index(name) for name in ("zl", "y", "x", "c")]
+
+
 def column(where, core, k3, k2, z):
     y = where[1] ^ jnp.where(core == 0, k2, k3)
     x = where[2] ^ jnp.where(core == 0, k3, k2)
     return pl.multiple_of(((z * 4 + y) * 4 + x) * 128, 128)
 
 
-def precondition(turns, flip, where, *refs):
+def precondition(turns, flip, *refs):
+    where = here_is()
     pieces, (low, high), pre = refs[: len(turns)], refs[-3:-1], refs[-1]
     rest = refs[len(turns) : -3]
     total = rest[0][...] if rest else jnp.zeros((128, 128), jnp.float32)
@@ -118,7 +123,8 @@
     give[...] = part[64:]
 
 
-def assemble(where, *refs):
+def assemble(*refs):
+    where = here_is()
     pieces, (out, wide, sems) = refs[:8], refs[8:]
     core = where[3]
     places = []
@@ -142,7 +148,6 @@
 
 
 VMEM = pl.BlockSpec(memory_space=pltpu.VMEM)
-SMEM = pl.BlockSpec(memory_space=pltpu.SMEM)
 PARAMS = pltpu.CompilerParams(vmem_limit_bytes=12 * 1024 * 1024)
 
 
@@ -161,9 +166,6 @@
     bf16, f32 = jnp.bfloat16, jnp.float32
     shape = jax.ShapeDtypeStruct
     c = lax.axis_index("c")
-    where = jnp.stack(
-        [lax.axis_index("zl"), lax.axis_index("y"), lax.axis_index("x"), c]
-    ).astype(jnp.int32)
     first = c == 0
 
     block = jnp.stack([acts.T, grads_out.T])
@@ -182,8 +184,8 @@
             functools.partial(precondition, turns, flip),
             "precondition",
             shape((128, 128), f32),
-            [SMEM] + [VMEM] * len(ins),
-        )(where, *ins)
+            [VMEM] * len(ins),
+        )(*ins)
 
     act_rows, grad_rows = factor(act_inverse), factor(grad_inverse)
     pieces = turned(second_turn, [act_plane] * 4)
@@ -201,8 +203,8 @@
     pair = jnp.stack([*there, *here]).reshape(2, 2, 128, 128)
     pair = jnp.swapaxes(pair, 0, 1).reshape(2, 256, 128)
     part = partial((0, 1, 2, 3), grad_pieces, [], grad_rows, False)
+    plane = jnp.stack(turned(first_turn, [pair] * 4))
     grad = (part + swap_cores(part)).astype(bf16)
-    plane = jnp.stack(turned(first_turn, [pair] * 4))
     grad = jnp.where(first, grad, jnp.concatenate([grad[64:], grad[:64]], axis=0))
     plane, grad = lax.optimization_barrier((plane, grad))
     grad = jnp.concatenate([swap_reps(grad), grad], axis=1)
@@ -216,12 +218,12 @@
     return pl.pallas_call(
         assemble,
         out_shape=shape((64, 8192), f32),
-        in_specs=[SMEM] + [VMEM] * 8,
+        in_specs=[VMEM] * 8,
         out_specs=pl.BlockSpec(memory_space=pltpu.HBM),
         scratch_shapes=[pltpu.VMEM((64, 8192), f32), pltpu.SemaphoreType.DMA((4,))],
         compiler_params=PARAMS,
         name="assemble",
-    )(where, *own, *sibling)
+    )(*own, *sibling)
 
 
 def solution(mesh):

time: 83.5 us -> 81.8 us (0.980)
  Pallas kernels: 6.59 us -> 4.28 us
  starting transfers between devices: 46.3 us -> 47.2 us
    pallas_call x3, Pallas kernels: 3.55 us -> 1.93 us  [partial(): call(functools.partial(precondition, turns, flip), 'precondition', shape(...]
    ppermute x30, starting transfers between devices: 46.3 us -> 47.2 us  [send(): return lax.ppermute(value, AXES, pairs)]
  transfers between devices with their start and end apart: 30 -> 30, of which waited for: 14 -> 16; matrix products, arithmetic and copies ran while one was open for 1% -> 1% of each run, Pallas kernels for 5% -> 4%
where the time goes in v14:
time: 81.8 us; the launch traced here: 81.6 us
  starting transfers between devices  47.2 us (58%)
  waiting for transfers between devices  28.2 us (34%)
  Pallas kernels  4.28 us (5%)
  other arithmetic  1.38 us (2%)
    ppermute x30, starting transfers between devices, send(): return lax.ppermute(value, AXES, pairs)  47.2 us
    ppermute x30, waiting for transfers between devices, send(): return lax.ppermute(value, AXES, pairs)  28.2 us
    pallas_call x3, Pallas kernels, partial(): call(functools.partial(precondition, turns, flip), 'precondition', shape(...  1.93 us
  transfers between devices with their start and end apart: 30, of which 16 were waited for; matrix products, arithmetic and copies ran while one was open for 1% of the time, Pallas kernels for 4%

profile of v14, /device:TPU:1, one launch (start us, length us, event | category | flops | bytes accessed | tf_op | source)
XLA Modules:
  0.0 81.6 jit_solution(2219741312323521071)
XLA Ops:
  0.0 0.8 %fusion = (bf16[1,2,64,128]{3,2,0,1:T(8,128)(2,1)S(1)}, bf16[2,64,128]{2,1,0:T(8,128)(2,1)S(1)}) fusion(bf16[1,64,128]{2,1,0:T(8,128)(2,1)} %bitcast.73, bf16[1,64,128]{2,1,0:T(8,128)(2,1)} %bitcast.74), kind=kLoop, calls=%fused_computation.28 | loop fusion | flops 16384 | bytes 98304 | tf_op jit(solution)/shard_map/stack | solution.py:172
  0.8 5.2 %collective-permute-start.2 = (bf16[2,64,128]{2,1,0:T(8,128)(2,1)S(1)}, bf16[2,64,128]{2,1,0:T(8,128)(2,1)S(1)}, u32[]{:S(2)}, u32[]{:S(2)}) collective-permute-start(bf16[2,64,128]{2,1,0:T(8,128)(2,1)S(1)} %get-tuple-element.52), channel_id=1, source_target_pairs={{0,96},{1,97},{2,98},{3,99},{4,100},{5,101},{6,102},{7,103},{8,104... | collective-permute-start | bytes 98312 | tf_op jit(solution)/shard_map/ppermute | solution.py:32
  6.4 2.1 %collective-permute-start.9 = (bf16[64,8192]{1,0:T(8,128)(2,1)}, bf16[64,8192]{1,0:T(8,128)(2,1)S(1)}, u32[]{:S(2)}, u32[]{:S(2)}) collective-permute-start(bf16[64,8192]{1,0:T(8,128)(2,1)} %param.6), channel_id=1, source_target_pairs={{0,1},{1,0},{2,3},{3,2},{4,5},{5,4},{6,7},{7,6},{8,9},{9,8},{10,11... | collective-permute-start | bytes 3145736 | tf_op jit(solution)/shard_map/ppermute | solution.py:32
  8.5 0.6 collective-permute-done
  9.7 1.3 %collective-permute-start.3 = (bf16[4,2,64,128]{3,2,0,1:T(8,128)(2,1)S(1)}, bf16[4,2,64,128]{3,2,0,1:T(8,128)(2,1)S(1)}, u32[]{:S(2)}, u32[]{:S(2)}) collective-permute-start(bf16[4,2,64,128]{3,2,0,1:T(8,128)(2,1)S(1)} %pad_maximum_fusion.4), channel_id=1, source_target_pairs={{0,8},{1,3},{2,10},{3,1},{4,12},{5,7},{6,14},{7,5},{8,0},{9,11},{1... | collective-permute-start | bytes 393224 | tf_op jit(solution)/shard_map/ppermute | solution.py:32
  11.0 2.5 %collective-permute-start.4 = (bf16[4,2,64,128]{3,2,0,1:T(8,128)(2,1)S(1)}, bf16[4,2,64,128]{3,2,0,1:T(8,128)(2,1)S(1)}, u32[]{:S(2)}, u32[]{:S(2)}) collective-permute-start(bf16[4,2,64,128]{3,2,0,1:T(8,128)(2,1)S(1)} %pad_maximum_fusion.4), channel_id=1, source_target_pairs={{0,16},{1,5},{2,18},{3,7},{4,20},{5,1},{6,22},{7,3},{8,24},{9,13},... | collective-permute-start | bytes 393224 | tf_op jit(solution)/shard_map/ppermute | solution.py:32
  13.7 3.5 %collective-permute-done.4 = bf16[4,2,64,128]{3,2,0,1:T(8,128)(2,1)S(1)} collective-permute-done((bf16[4,2,64,128]{3,2,0,1:T(8,128)(2,1)S(1)}, bf16[4,2,64,128]{3,2,0,1:T(8,128)(2,1)S(1)}, u32[]{:S(2)}, u32[]{:S(2)}) %collective-permute-start.4) | collective-permute-done | bytes 131104 | tf_op jit(solution)/shard_map/ppermute | solution.py:32
  17.2 1.4 %collective-permute-done.5 = bf16[4,2,64,128]{3,2,0,1:T(8,128)(2,1)S(1)} collective-permute-done((bf16[4,2,64,128]{3,2,0,1:T(8,128)(2,1)S(1)}, bf16[4,2,64,128]{3,2,0,1:T(8,128)(2,1)S(1)}, u32[]{:S(2)}, u32[]{:S(2)}) %collective-permute-start.5) | collective-permute-done | bytes 131104 | tf_op jit(solution)/shard_map/ppermute | solution.py:32
  18.7 3.1 %collective-permute-start.7 = (bf16[4,4,64,128]{3,2,1,0:T(8,128)(2,1)S(1)}, bf16[4,4,64,128]{3,2,1,0:T(8,128)(2,1)S(1)}, u32[]{:S(2)}, u32[]{:S(2)}) collective-permute-start(bf16[4,4,64,128]{3,2,1,0:T(8,128)(2,1)S(1)} %pad_maximum_fusion.2.refs_0_), channel_id=1, source_target_pairs={{0,6},{1,25},{2,4},{3,27},{4,2},{5,29},{6,0},{7,31},{8,14},{9,17},... | collective-permute-start | bytes 786440 | tf_op jit(solution)/shard_map/ppermute | solution.py:32
  22.7 5.2 %collective-permute-done.7.refs_1_ = bf16[4,4,64,128]{3,2,1,0:T(8,128)(2,1)S(1)} collective-permute-done((bf16[4,4,64,128]{3,2,1,0:T(8,128)(2,1)S(1)}, bf16[4,4,64,128]{3,2,1,0:T(8,128)(2,1)S(1)}, u32[]{:S(2)}, u32[]{:S(2)}) %collective-permute-start.7) | collective-permute-done | bytes 262176 | tf_op jit(solution)/shard_map/ppermute | solution.py:32
  27.9 0.6 collective-permute-done.8.refs_2_
  28.5 0.7 precondition.3.refs_1_
  29.7 6.0 %collective-permute-start.10 = (f32[128,128]{1,0:T(8,128)S(1)}, f32[128,128]{1,0:T(8,128)S(1)}, u32[]{:S(2)}, u32[]{:S(2)}) collective-permute-start(f32[128,128]{1,0:T(8,128)S(1)} %precondition.4), channel_id=1, source_target_pairs={{0,1},{1,0},{2,3},{3,2},{4,5},{5,4},{6,7},{7,6},{8,9},{9,8},{10,11... | collective-permute-start | bytes 196616 | tf_op jit(solution)/shard_map/ppermute | solution.py:32
  35.7 0.9 %collective-permute-done.10 = f32[128,128]{1,0:T(8,128)S(1)} collective-permute-done((f32[128,128]{1,0:T(8,128)S(1)}, f32[128,128]{1,0:T(8,128)S(1)}, u32[]{:S(2)}, u32[]{:S(2)}) %collective-permute-start.10) | collective-permute-done | bytes 65568 | tf_op jit(solution)/shard_map/ppermute | solution.py:32
  36.6 4.0 %collective-permute-start.14 = (bf16[128,128]{1,0:T(8,128)(2,1)S(1)}, bf16[128,128]{1,0:T(8,128)(2,1)S(1)}, u32[]{:S(2)}, u32[]{:S(2)}) collective-permute-start(bf16[128,128]{1,0:T(8,128)(2,1)S(1)} %add_convert_fusion.1), channel_id=1, source_target_pairs={{0,0},{1,32},{2,2},{3,34},{4,4},{5,36},{6,6},{7,38},{8,8},{9,40},{... | collective-permute-start | bytes 98312 | tf_op jit(solution)/shard_map/ppermute | solution.py:32
  40.6 3.3 %collective-permute-start.11 = (bf16[128,128]{1,0:T(8,128)(2,1)S(1)}, bf16[128,128]{1,0:T(8,128)(2,1)S(1)}, u32[]{:S(2)}, u32[]{:S(2)}) collective-permute-start(bf16[128,128]{1,0:T(8,128)(2,1)S(1)} %add_convert_fusion.1), channel_id=1, source_target_pairs={{0,128},{1,160},{2,130},{3,162},{4,132},{5,164},{6,134},{7,166},{8... | collective-permute-start | bytes 98312 | tf_op jit(solution)/shard_map/ppermute | solution.py:32
  43.8 2.8 %collective-permute-start.15 = (bf16[128,128]{1,0:T(8,128)(2,1)S(1)}, bf16[128,128]{1,0:T(8,128)(2,1)S(1)}, u32[]{:S(2)}, u32[]{:S(2)}) collective-permute-start(bf16[128,128]{1,0:T(8,128)(2,1)S(1)} %add_convert_fusion.1), channel_id=1, source_target_pairs={{0,64},{1,96},{2,66},{3,98},{4,68},{5,100},{6,70},{7,102},{8,72},{... | collective-permute-start | bytes 98312 | tf_op jit(solution)/shard_map/ppermute | solution.py:32
  46.9 1.1 %collective-permute-done.12 = bf16[128,128]{1,0:T(8,128)(2,1)S(1)} collective-permute-done((bf16[128,128]{1,0:T(8,128)(2,1)S(1)}, bf16[128,128]{1,0:T(8,128)(2,1)S(1)}, u32[]{:S(2)}, u32[]{:S(2)}) %collective-permute-start.12) | collective-permute-done | bytes 32800 | tf_op jit(solution)/shard_map/ppermute | solution.py:32
  48.5 1.1 %collective-permute-start.16 = (bf16[2,256,128]{2,1,0:T(8,128)(2,1)S(1)}, bf16[2,256,128]{2,1,0:T(8,128)(2,1)S(1)}, u32[]{:S(2)}, u32[]{:S(2)}) collective-permute-start(bf16[2,256,128]{2,1,0:T(8,128)(2,1)S(1)} %bitcast.58), channel_id=1, source_target_pairs={{0,8},{1,3},{2,10},{3,1},{4,12},{5,7},{6,14},{7,5},{8,0},{9,11},{1... | collective-permute-start | bytes 393224 | tf_op jit(solution)/shard_map/ppermute | solution.py:32
  49.6 2.7 %collective-permute-start.17 = (bf16[2,256,128]{2,1,0:T(8,128)(2,1)S(1)}, bf16[2,256,128]{2,1,0:T(8,128)(2,1)S(1)}, u32[]{:S(2)}, u32[]{:S(2)}) collective-permute-start(bf16[2,256,128]{2,1,0:T(8,128)(2,1)S(1)} %bitcast.59), channel_id=1, source_target_pairs={{0,16},{1,5},{2,18},{3,7},{4,20},{5,1},{6,22},{7,3},{8,24},{9,13},... | collective-permute-start | bytes 393224 | tf_op jit(solution)/shard_map/ppermute | solution.py:32
  52.7 6.1 %collective-permute-done.19 = bf16[2,4,4,64,128]{4,3,2,1,0:T(8,128)(2,1)S(1)} collective-permute-done((bf16[2,4,4,64,128]{4,3,2,1,0:T(8,128)(2,1)S(1)}, bf16[2,4,4,64,128]{4,3,2,1,0:T(8,128)(2,1)S(1)}, u32[]{:S(2)}, u32[]{:S(2)}) %collective-permute-start.19) | collective-permute-done | bytes 524320 | tf_op jit(solution)/shard_map/ppermute | solution.py:32
  58.8 0.9 %precondition.5 = f32[128,128]{1,0:T(8,128)S(1)} custom-call(bf16[4,4,64,128]{3,2,1,0:T(8,128)(2,1)S(1)} %get-tuple-element.40.refs_0_, bf16[4,4,64,128]{3,2,1,0:T(8,128)(2,1)S(1)} %get-tuple-element.39.refs_1_, bf16[4,4,64,128]{3,2,1,0:T(8,128)(2,1)S(1)} %get-tuple-element.38.refs_2_, bf16[4,4,64,128]{3,2,1,0:T(8,128)(2,1)S(1)} %get-tuple-element.37.refs_3_, ...), custom_call_target="tpu_custom_call" | custom-call | tf_op jit(solution)/shard_map/precondition/pallas_call | solution.py:183
  59.9 1.1 %collective-permute-done.21 = f32[128,128]{1,0:T(8,128)S(1)} collective-permute-done((f32[128,128]{1,0:T(8,128)S(1)}, f32[128,128]{1,0:T(8,128)S(1)}, u32[]{:S(2)}, u32[]{:S(2)}) %collective-permute-start.21) | collective-permute-done | bytes 65568 | tf_op jit(solution)/shard_map/ppermute | solution.py:32
  61.2 1.1 %collective-permute-start.24 = (bf16[4,2,256,128]{3,2,1,0:T(8,128)(2,1)S(1)}, bf16[4,2,256,128]{3,2,1,0:T(8,128)(2,1)S(1)}, u32[]{:S(2)}, u32[]{:S(2)}) collective-permute-start(bf16[4,2,256,128]{3,2,1,0:T(8,128)(2,1)S(1)} %pad_maximum_fusion.1.piece), channel_id=1, source_target_pairs={{0,4},{1,17},{2,6},{3,19},{4,0},{5,21},{6,2},{7,23},{8,12},{9,25},... | collective-permute-start | bytes 1572872 | tf_op jit(solution)/shard_map/ppermute | solution.py:32
  62.3 2.2 %collective-permute-start.23 = (bf16[4,2,256,128]{3,2,1,0:T(8,128)(2,1)S(1)}, bf16[4,2,256,128]{3,2,1,0:T(8,128)(2,1)S(1)}, u32[]{:S(2)}, u32[]{:S(2)}) collective-permute-start(bf16[4,2,256,128]{3,2,1,0:T(8,128)(2,1)S(1)} %pad_maximum_fusion.1.piece), channel_id=1, source_target_pairs={{0,2},{1,9},{2,0},{3,11},{4,6},{5,13},{6,4},{7,15},{8,10},{9,1},{1... | collective-permute-start | bytes 1572872 | tf_op jit(solution)/shard_map/ppermute | solution.py:32
  64.4 4.2 %collective-permute-start.22 = (bf16[128,128]{1,0:T(8,128)(2,1)S(1)}, bf16[128,128]{1,0:T(8,128)(2,1)S(1)}, u32[]{:S(2)}, u32[]{:S(2)}) collective-permute-start(bf16[128,128]{1,0:T(8,128)(2,1)S(1)} %maximum_select_fusion), channel_id=1, source_target_pairs={{0,128},{1,129},{2,130},{3,131},{4,132},{5,133},{6,134},{7,135},{8... | collective-permute-start | bytes 98312 | tf_op jit(solution)/shard_map/ppermute | solution.py:32
  68.6 2.5 %collective-permute-done.22 = bf16[128,128]{1,0:T(8,128)(2,1)S(1)} collective-permute-done((bf16[128,128]{1,0:T(8,128)(2,1)S(1)}, bf16[128,128]{1,0:T(8,128)(2,1)S(1)}, u32[]{:S(2)}, u32[]{:S(2)}) %collective-permute-start.22) | collective-permute-done | bytes 32800 | tf_op jit(solution)/shard_map/ppermute | solution.py:32
  71.4 2.2 %collective-permute-start.26 = (f32[64,1024]{1,0:T(8,128)S(1)}, f32[64,1024]{1,0:T(8,128)S(1)}, u32[]{:S(2)}, u32[]{:S(2)}) collective-permute-start(f32[64,1024]{1,0:T(8,128)S(1)} %get-tuple-element.29), channel_id=1, source_target_pairs={{0,1},{1,0},{2,3},{3,2},{4,5},{5,4},{6,7},{7,6},{8,9},{9,8},{10,11... | collective-permute-start | bytes 786440 | tf_op jit(solution)/shard_map/ppermute | solution.py:32
  73.6 2.7 %collective-permute-done.25.piece = bf16[4,2,256,128]{3,2,1,0:T(8,128)(2,1)S(1)} collective-permute-done((bf16[4,2,256,128]{3,2,1,0:T(8,128)(2,1)S(1)}, bf16[4,2,256,128]{3,2,1,0:T(8,128)(2,1)S(1)}, u32[]{:S(2)}, u32[]{:S(2)}) %collective-permute-start.25) | collective-permute-done | bytes 524320 | tf_op jit(solution)/shard_map/ppermute | solution.py:32
  76.6 1.1 %collective-permute-start.29 = (f32[64,1024]{1,0:T(8,128)S(1)}, f32[64,1024]{1,0:T(8,128)S(1)}, u32[]{:S(2)}, u32[]{:S(2)}) collective-permute-start(f32[64,1024]{1,0:T(8,128)S(1)} %get-tuple-element.32), channel_id=1, source_target_pairs={{0,1},{1,0},{2,3},{3,2},{4,5},{5,4},{6,7},{7,6},{8,9},{9,8},{10,11... | collective-permute-start | bytes 786440 | tf_op jit(solution)/shard_map/ppermute | solution.py:32
  78.8 0.7 collective-permute-done.28.refs_6_
  80.0 1.4 %assemble.1 = f32[64,8192]{1,0:T(8,128)} custom-call(f32[64,1024]{1,0:T(8,128)S(1)} %get-tuple-element.25.refs_0_, f32[64,1024]{1,0:T(8,128)S(1)} %get-tuple-element.26.refs_1_, f32[64,1024]{1,0:T(8,128)S(1)} %get-tuple-element.27.refs_2_, f32[64,1024]{1,0:T(8,128)S(1)} %get-tuple-element.28.refs_3_, f32[64,1024]{1,0:T(8,128)S(1)} %collective-permute-done.26.refs_4_, ...), custom_call_target="tpu_custom_call" | custom-call | tf_op jit(solution)/shard_map/assemble/pallas_call | solution.py:218
  (62 shorter events, 6.2 us)
Async XLA Ops:
  0.0 22.5 %copy-start = (bf16[64,8192]{1,0:T(8,128)(2,1)S(1)}, bf16[64,8192]{1,0:T(8,128)(2,1)}, u32[]{:S(2)}) copy-start(bf16[64,8192]{1,0:T(8,128)(2,1)} %param.6) | copy-start | bytes 3145732
  0.8 7.6 %collective-permute-start.2 = (bf16[2,64,128]{2,1,0:T(8,128)(2,1)S(1)}, bf16[2,64,128]{2,1,0:T(8,128)(2,1)S(1)}, u32[]{:S(2)}, u32[]{:S(2)}) collective-permute-start(bf16[2,64,128]{2,1,0:T(8,128)(2,1)S(1)} %get-tuple-element.52), channel_id=1, source_target_pairs={{0,96},{1,97},{2,98},{3,99},{4,100},{5,101},{6,102},{7,103},{8,104... | collective-permute-start | bytes 98312 | tf_op jit(solution)/shard_map/ppermute | solution.py:32
  6.0 3.1 %collective-permute-start = (bf16[2,64,128]{2,1,0:T(8,128)(2,1)S(1)}, bf16[2,64,128]{2,1,0:T(8,128)(2,1)S(1)}, u32[]{:S(2)}, u32[]{:S(2)}) collective-permute-start(bf16[2,64,128]{2,1,0:T(8,128)(2,1)S(1)} %get-tuple-element.52), channel_id=1, source_target_pairs={{0,32},{1,33},{2,34},{3,35},{4,36},{5,37},{6,38},{7,39},{8,40},{9,... | collective-permute-start | bytes 98312 | tf_op jit(solution)/shard_map/ppermute | solution.py:32
  6.0 3.7 %collective-permute-start.1 = (bf16[2,64,128]{2,1,0:T(8,128)(2,1)S(1)}, bf16[2,64,128]{2,1,0:T(8,128)(2,1)S(1)}, u32[]{:S(2)}, u32[]{:S(2)}) collective-permute-start(bf16[2,64,128]{2,1,0:T(8,128)(2,1)S(1)} %get-tuple-element.52), channel_id=1, source_target_pairs={{0,64},{1,65},{2,66},{3,67},{4,68},{5,69},{6,70},{7,71},{8,72},{9,... | collective-permute-start | bytes 98312 | tf_op jit(solution)/shard_map/ppermute | solution.py:32
  6.4 16.1 %collective-permute-start.9 = (bf16[64,8192]{1,0:T(8,128)(2,1)}, bf16[64,8192]{1,0:T(8,128)(2,1)S(1)}, u32[]{:S(2)}, u32[]{:S(2)}) collective-permute-start(bf16[64,8192]{1,0:T(8,128)(2,1)} %param.6), channel_id=1, source_target_pairs={{0,1},{1,0},{2,3},{3,2},{4,5},{5,4},{6,7},{7,6},{8,9},{9,8},{10,11... | collective-permute-start | bytes 3145736 | tf_op jit(solution)/shard_map/ppermute | solution.py:32
  8.5 38.3 %collective-permute-start.20 = (bf16[64,8192]{1,0:T(8,128)(2,1)}, bf16[64,8192]{1,0:T(8,128)(2,1)S(1)}, u32[]{:S(2)}, u32[]{:S(2)}) collective-permute-start(bf16[64,8192]{1,0:T(8,128)(2,1)} %param.7), channel_id=1, source_target_pairs={{0,1},{1,0},{2,3},{3,2},{4,5},{5,4},{6,7},{7,6},{8,9},{9,8},{10,11... | collective-permute-start | bytes 3145736 | tf_op jit(solution)/shard_map/ppermute | solution.py:32
  9.7 4.0 %collective-permute-start.3 = (bf16[4,2,64,128]{3,2,0,1:T(8,128)(2,1)S(1)}, bf16[4,2,64,128]{3,2,0,1:T(8,128)(2,1)S(1)}, u32[]{:S(2)}, u32[]{:S(2)}) collective-permute-start(bf16[4,2,64,128]{3,2,0,1:T(8,128)(2,1)S(1)} %pad_maximum_fusion.4), channel_id=1, source_target_pairs={{0,8},{1,3},{2,10},{3,1},{4,12},{5,7},{6,14},{7,5},{8,0},{9,11},{1... | collective-permute-start | bytes 393224 | tf_op jit(solution)/shard_map/ppermute | solution.py:32
  11.0 6.2 %collective-permute-start.4 = (bf16[4,2,64,128]{3,2,0,1:T(8,128)(2,1)S(1)}, bf16[4,2,64,128]{3,2,0,1:T(8,128)(2,1)S(1)}, u32[]{:S(2)}, u32[]{:S(2)}) collective-permute-start(bf16[4,2,64,128]{3,2,0,1:T(8,128)(2,1)S(1)} %pad_maximum_fusion.4), channel_id=1, source_target_pairs={{0,16},{1,5},{2,18},{3,7},{4,20},{5,1},{6,22},{7,3},{8,24},{9,13},... | collective-permute-start | bytes 393224 | tf_op jit(solution)/shard_map/ppermute | solution.py:32
  13.4 5.2 %collective-permute-start.5 = (bf16[4,2,64,128]{3,2,0,1:T(8,128)(2,1)S(1)}, bf16[4,2,64,128]{3,2,0,1:T(8,128)(2,1)S(1)}, u32[]{:S(2)}, u32[]{:S(2)}) collective-permute-start(bf16[4,2,64,128]{3,2,0,1:T(8,128)(2,1)S(1)} %pad_maximum_fusion.4), channel_id=1, source_target_pairs={{0,24},{1,7},{2,26},{3,5},{4,28},{5,3},{6,30},{7,1},{8,16},{9,15},... | collective-permute-start | bytes 393224 | tf_op jit(solution)/shard_map/ppermute | solution.py:32
  18.7 9.2 %collective-permute-start.7 = (bf16[4,4,64,128]{3,2,1,0:T(8,128)(2,1)S(1)}, bf16[4,4,64,128]{3,2,1,0:T(8,128)(2,1)S(1)}, u32[]{:S(2)}, u32[]{:S(2)}) collective-permute-start(bf16[4,4,64,128]{3,2,1,0:T(8,128)(2,1)S(1)} %pad_maximum_fusion.2.refs_0_), channel_id=1, source_target_pairs={{0,6},{1,25},{2,4},{3,27},{4,2},{5,29},{6,0},{7,31},{8,14},{9,17},... | collective-permute-start | bytes 786440 | tf_op jit(solution)/shard_map/ppermute | solution.py:32
  21.8 6.7 %collective-permute-start.8 = (bf16[4,4,64,128]{3,2,1,0:T(8,128)(2,1)S(1)}, bf16[4,4,64,128]{3,2,1,0:T(8,128)(2,1)S(1)}, u32[]{:S(2)}, u32[]{:S(2)}) collective-permute-start(bf16[4,4,64,128]{3,2,1,0:T(8,128)(2,1)S(1)} %pad_maximum_fusion.2.refs_0_), channel_id=1, source_target_pairs={{0,4},{1,17},{2,6},{3,19},{4,0},{5,21},{6,2},{7,23},{8,12},{9,25},... | collective-permute-start | bytes 786440 | tf_op jit(solution)/shard_map/ppermute | solution.py:32
  22.0 7.4 %collective-permute-start.6 = (bf16[4,4,64,128]{3,2,1,0:T(8,128)(2,1)S(1)}, bf16[4,4,64,128]{3,2,1,0:T(8,128)(2,1)S(1)}, u32[]{:S(2)}, u32[]{:S(2)}) collective-permute-start(bf16[4,4,64,128]{3,2,1,0:T(8,128)(2,1)S(1)} %pad_maximum_fusion.2.refs_0_), channel_id=1, source_target_pairs={{0,2},{1,9},{2,0},{3,11},{4,6},{5,13},{6,4},{7,15},{8,10},{9,1},{1... | collective-permute-start | bytes 786440 | tf_op jit(solution)/shard_map/ppermute | solution.py:32
  29.2 17.6 %copy-start.1 = (bf16[64,8192]{1,0:T(8,128)(2,1)S(1)}, bf16[64,8192]{1,0:T(8,128)(2,1)}, u32[]{:S(2)}) copy-start(bf16[64,8192]{1,0:T(8,128)(2,1)} %param.7) | copy-start | bytes 3145732
  29.7 6.9 %collective-permute-start.10 = (f32[128,128]{1,0:T(8,128)S(1)}, f32[128,128]{1,0:T(8,128)S(1)}, u32[]{:S(2)}, u32[]{:S(2)}) collective-permute-start(f32[128,128]{1,0:T(8,128)S(1)} %precondition.4), channel_id=1, source_target_pairs={{0,1},{1,0},{2,3},{3,2},{4,5},{5,4},{6,7},{7,6},{8,9},{9,8},{10,11... | collective-permute-start | bytes 196616 | tf_op jit(solution)/shard_map/ppermute | solution.py:32
  35.7 8.1 %collective-permute-start.13 = (bf16[4,4,64,128]{3,2,1,0:T(8,128)(2,1)S(1)}, bf16[4,4,64,128]{3,2,1,0:T(8,128)(2,1)S(1)}, u32[]{:S(2)}, u32[]{:S(2)}) collective-permute-start(bf16[4,4,64,128]{3,2,1,0:T(8,128)(2,1)S(1)} %pad_maximum_fusion.3), channel_id=1, source_target_pairs={{0,2},{1,9},{2,0},{3,11},{4,6},{5,13},{6,4},{7,15},{8,10},{9,1},{1... | collective-permute-start | bytes 786440 | tf_op jit(solution)/shard_map/ppermute | solution.py:32
  36.6 10.0 %collective-permute-start.14 = (bf16[128,128]{1,0:T(8,128)(2,1)S(1)}, bf16[128,128]{1,0:T(8,128)(2,1)S(1)}, u32[]{:S(2)}, u32[]{:S(2)}) collective-permute-start(bf16[128,128]{1,0:T(8,128)(2,1)S(1)} %add_convert_fusion.1), channel_id=1, source_target_pairs={{0,0},{1,32},{2,2},{3,34},{4,4},{5,36},{6,6},{7,38},{8,8},{9,40},{... | collective-permute-start | bytes 98312 | tf_op jit(solution)/shard_map/ppermute | solution.py:32
  40.6 6.4 %collective-permute-start.11 = (bf16[128,128]{1,0:T(8,128)(2,1)S(1)}, bf16[128,128]{1,0:T(8,128)(2,1)S(1)}, u32[]{:S(2)}, u32[]{:S(2)}) collective-permute-start(bf16[128,128]{1,0:T(8,128)(2,1)S(1)} %add_convert_fusion.1), channel_id=1, source_target_pairs={{0,128},{1,160},{2,130},{3,162},{4,132},{5,164},{6,134},{7,166},{8... | collective-permute-start | bytes 98312 | tf_op jit(solution)/shard_map/ppermute | solution.py:32
  43.8 4.2 %collective-permute-start.12 = (bf16[128,128]{1,0:T(8,128)(2,1)S(1)}, bf16[128,128]{1,0:T(8,128)(2,1)S(1)}, u32[]{:S(2)}, u32[]{:S(2)}) collective-permute-start(bf16[128,128]{1,0:T(8,128)(2,1)S(1)} %add_convert_fusion.1), channel_id=1, source_target_pairs={{0,192},{1,224},{2,194},{3,226},{4,196},{5,228},{6,198},{7,230},{8... | collective-permute-start | bytes 98312 | tf_op jit(solution)/shard_map/ppermute | solution.py:32
  43.8 4.6 %collective-permute-start.15 = (bf16[128,128]{1,0:T(8,128)(2,1)S(1)}, bf16[128,128]{1,0:T(8,128)(2,1)S(1)}, u32[]{:S(2)}, u32[]{:S(2)}) collective-permute-start(bf16[128,128]{1,0:T(8,128)(2,1)S(1)} %add_convert_fusion.1), channel_id=1, source_target_pairs={{0,64},{1,96},{2,66},{3,98},{4,68},{5,100},{6,70},{7,102},{8,72},{... | collective-permute-start | bytes 98312 | tf_op jit(solution)/shard_map/ppermute | solution.py:32
  46.6 12.1 %collective-permute-start.19 = (bf16[2,4,4,64,128]{4,3,2,1,0:T(8,128)(2,1)S(1)}, bf16[2,4,4,64,128]{4,3,2,1,0:T(8,128)(2,1)S(1)}, u32[]{:S(2)}, u32[]{:S(2)}) collective-permute-start(bf16[2,4,4,64,128]{4,3,2,1,0:T(8,128)(2,1)S(1)} %pad_maximum_fusion), channel_id=1, source_target_pairs={{0,6},{1,25},{2,4},{3,27},{4,2},{5,29},{6,0},{7,31},{8,14},{9,17},... | collective-permute-start | bytes 1572872 | tf_op jit(solution)/shard_map/ppermute | solution.py:32
  48.5 11.3 %collective-permute-start.16 = (bf16[2,256,128]{2,1,0:T(8,128)(2,1)S(1)}, bf16[2,256,128]{2,1,0:T(8,128)(2,1)S(1)}, u32[]{:S(2)}, u32[]{:S(2)}) collective-permute-start(bf16[2,256,128]{2,1,0:T(8,128)(2,1)S(1)} %bitcast.58), channel_id=1, source_target_pairs={{0,8},{1,3},{2,10},{3,1},{4,12},{5,7},{6,14},{7,5},{8,0},{9,11},{1... | collective-permute-start | bytes 393224 | tf_op jit(solution)/shard_map/ppermute | solution.py:32
  49.6 10.2 %collective-permute-start.17 = (bf16[2,256,128]{2,1,0:T(8,128)(2,1)S(1)}, bf16[2,256,128]{2,1,0:T(8,128)(2,1)S(1)}, u32[]{:S(2)}, u32[]{:S(2)}) collective-permute-start(bf16[2,256,128]{2,1,0:T(8,128)(2,1)S(1)} %bitcast.59), channel_id=1, source_target_pairs={{0,16},{1,5},{2,18},{3,7},{4,20},{5,1},{6,22},{7,3},{8,24},{9,13},... | collective-permute-start | bytes 393224 | tf_op jit(solution)/shard_map/ppermute | solution.py:32
  52.3 7.5 %collective-permute-start.18 = (bf16[2,256,128]{2,1,0:T(8,128)(2,1)S(1)}, bf16[2,256,128]{2,1,0:T(8,128)(2,1)S(1)}, u32[]{:S(2)}, u32[]{:S(2)}) collective-permute-start(bf16[2,256,128]{2,1,0:T(8,128)(2,1)S(1)} %bitcast.60), channel_id=1, source_target_pairs={{0,24},{1,7},{2,26},{3,5},{4,28},{5,3},{6,30},{7,1},{8,16},{9,15},... | collective-permute-start | bytes 393224 | tf_op jit(solution)/shard_map/ppermute | solution.py:32
  59.7 1.3 %collective-permute-start.21 = (f32[128,128]{1,0:T(8,128)S(1)}, f32[128,128]{1,0:T(8,128)S(1)}, u32[]{:S(2)}, u32[]{:S(2)}) collective-permute-start(f32[128,128]{1,0:T(8,128)S(1)} %precondition.5), channel_id=1, source_target_pairs={{0,1},{1,0},{2,3},{3,2},{4,5},{5,4},{6,7},{7,6},{8,9},{9,8},{10,11... | collective-permute-start | bytes 196616 | tf_op jit(solution)/shard_map/ppermute | solution.py:32
  61.1 15.2 %collective-permute-start.25 = (bf16[4,2,256,128]{3,2,1,0:T(8,128)(2,1)S(1)}, bf16[4,2,256,128]{3,2,1,0:T(8,128)(2,1)S(1)}, u32[]{:S(2)}, u32[]{:S(2)}) collective-permute-start(bf16[4,2,256,128]{3,2,1,0:T(8,128)(2,1)S(1)} %pad_maximum_fusion.1.piece), channel_id=1, source_target_pairs={{0,6},{1,25},{2,4},{3,27},{4,2},{5,29},{6,0},{7,31},{8,14},{9,17},... | collective-permute-start | bytes 1572872 | tf_op jit(solution)/shard_map/ppermute | solution.py:32
  61.2 16.5 %collective-permute-start.24 = (bf16[4,2,256,128]{3,2,1,0:T(8,128)(2,1)S(1)}, bf16[4,2,256,128]{3,2,1,0:T(8,128)(2,1)S(1)}, u32[]{:S(2)}, u32[]{:S(2)}) collective-permute-start(bf16[4,2,256,128]{3,2,1,0:T(8,128)(2,1)S(1)} %pad_maximum_fusion.1.piece), channel_id=1, source_target_pairs={{0,4},{1,17},{2,6},{3,19},{4,0},{5,21},{6,2},{7,23},{8,12},{9,25},... | collective-permute-start | bytes 1572872 | tf_op jit(solution)/shard_map/ppermute | solution.py:32
  62.3 15.8 %collective-permute-start.23 = (bf16[4,2,256,128]{3,2,1,0:T(8,128)(2,1)S(1)}, bf16[4,2,256,128]{3,2,1,0:T(8,128)(2,1)S(1)}, u32[]{:S(2)}, u32[]{:S(2)}) collective-permute-start(bf16[4,2,256,128]{3,2,1,0:T(8,128)(2,1)S(1)} %pad_maximum_fusion.1.piece), channel_id=1, source_target_pairs={{0,2},{1,9},{2,0},{3,11},{4,6},{5,13},{6,4},{7,15},{8,10},{9,1},{1... | collective-permute-start | bytes 1572872 | tf_op jit(solution)/shard_map/ppermute | solution.py:32
  64.4 6.7 %collective-permute-start.22 = (bf16[128,128]{1,0:T(8,128)(2,1)S(1)}, bf16[128,128]{1,0:T(8,128)(2,1)S(1)}, u32[]{:S(2)}, u32[]{:S(2)}) collective-permute-start(bf16[128,128]{1,0:T(8,128)(2,1)S(1)} %maximum_select_fusion), channel_id=1, source_target_pairs={{0,128},{1,129},{2,130},{3,131},{4,132},{5,133},{6,134},{7,135},{8... | collective-permute-start | bytes 98312 | tf_op jit(solution)/shard_map/ppermute | solution.py:32
  71.4 7.5 %collective-permute-start.26 = (f32[64,1024]{1,0:T(8,128)S(1)}, f32[64,1024]{1,0:T(8,128)S(1)}, u32[]{:S(2)}, u32[]{:S(2)}) collective-permute-start(f32[64,1024]{1,0:T(8,128)S(1)} %get-tuple-element.29), channel_id=1, source_target_pairs={{0,1},{1,0},{2,3},{3,2},{4,5},{5,4},{6,7},{7,6},{8,9},{9,8},{10,11... | collective-permute-start | bytes 786440 | tf_op jit(solution)/shard_map/ppermute | solution.py:32
  76.6 2.3 %collective-permute-start.29 = (f32[64,1024]{1,0:T(8,128)S(1)}, f32[64,1024]{1,0:T(8,128)S(1)}, u32[]{:S(2)}, u32[]{:S(2)}) collective-permute-start(f32[64,1024]{1,0:T(8,128)S(1)} %get-tuple-element.32), channel_id=1, source_target_pairs={{0,1},{1,0},{2,3},{3,2},{4,5},{5,4},{6,7},{7,6},{8,9},{9,8},{10,11... | collective-permute-start | bytes 786440 | tf_op jit(solution)/shard_map/ppermute | solution.py:32
  77.9 1.6 %collective-permute-start.28 = (f32[64,1024]{1,0:T(8,128)S(1)}, f32[64,1024]{1,0:T(8,128)S(1)}, u32[]{:S(2)}, u32[]{:S(2)}) collective-permute-start(f32[64,1024]{1,0:T(8,128)S(1)} %get-tuple-element.31), channel_id=1, source_target_pairs={{0,1},{1,0},{2,3},{3,2},{4,5},{5,4},{6,7},{7,6},{8,9},{9,8},{10,11... | collective-permute-start | bytes 786440 | tf_op jit(solution)/shard_map/ppermute | solution.py:32
  78.3 1.7 %collective-permute-start.27 = (f32[64,1024]{1,0:T(8,128)S(1)}, f32[64,1024]{1,0:T(8,128)S(1)}, u32[]{:S(2)}, u32[]{:S(2)}) collective-permute-start(f32[64,1024]{1,0:T(8,128)S(1)} %get-tuple-element.30), channel_id=1, source_target_pairs={{0,1},{1,0},{2,3},{3,2},{4,5},{5,4},{6,7},{7,6},{8,9},{9,8},{10,11... | collective-permute-start | bytes 786440 | tf_op jit(solution)/shard_map/ppermute | solution.py:32

commit v15 on v14

--- a/solution.py
+++ b/solution.py
@@ -58,6 +58,11 @@
     )
 
 
+def stacked(turn, value, order):
+    got = turned(turn, [value] * 4)
+    return jnp.stack([got[k] for k in order])
+
+
 def to_parity(value, j, other_rep):
     def target(r, zl, y, x, c):
         return r ^ other_rep, zl ^ (2 * j + c), y, x, zl % 2
@@ -68,6 +73,10 @@
 def turned(turn, values):
     got = {k: turn(values[k], k) for k in (1, 3, 2)}
     return [values[0]] + [got[k] for k in (1, 2, 3)]
+
+
+ORDER_F = (0, 1, 3, 2)
+ORDER_Z, ORDER_2, ORDER_B = (0, 2, 1, 3), (0, 2, 1, 3), (0, 2, 1, 3)
 
 
 def here_is():
@@ -87,10 +96,10 @@
     total = rest[0][...] if rest else jnp.zeros((128, 128), jnp.float32)
     none = jnp.zeros((64, 128), jnp.bfloat16)
     for k3, piece in zip(turns, pieces):
-        for k2 in range(4):
+        for n, k2 in enumerate(ORDER_2):
             at = [
                 pl.ds(column(where, where[3], k3, k2, where[0] ^ kz), 128)
-                for kz in range(4)
+                for kz in ORDER_Z
             ]
             rows = jnp.concatenate(
                 [
@@ -100,8 +109,8 @@
                 axis=0,
             )
             held = []
-            for kz in range(4):
-                block = piece[k2, kz]
+            for m in range(4):
+                block = piece[n, m]
                 held.append(jnp.where(where[3] == 0, block, none))
                 held.append(jnp.where(where[3] == 0, none, block))
             total += jnp.dot(
@@ -130,12 +139,12 @@
     places = []
     for side in range(2):
         held_by = core if side == 0 else 1 - core
-        for k3 in range(4):
-            for k2 in range(4):
+        for m, k3 in enumerate(ORDER_F):
+            for n, k2 in enumerate(ORDER_B):
                 for j in range(2):
                     z = where[0] ^ (2 * j + lax.rem(where[0] + held_by, 2))
                     at = column(where, held_by, k3, k2, z)
-                    places.append((pieces[side * 4 + k3], (k2 * 2 + j) * 128, at))
+                    places.append((pieces[side * 4 + m], (n * 2 + j) * 128, at))
     copies = []
     for i in range(4):
         rows = slice(i * 16, i * 16 + 16)
@@ -169,8 +178,9 @@
     first = c == 0
 
     block = jnp.stack([acts.T, grads_out.T])
-    line = jnp.stack(turned(along_line, [block] * 4))
+    line = stacked(along_line, block, ORDER_Z)
     held = turned(first_turn, [line] * 4)
+    held = [held[k] for k in ORDER_2]
     act_plane = jnp.stack([part[:, 0] for part in held])
     grad_plane = jnp.stack([part[:, 1] for part in held])
 
@@ -189,7 +199,7 @@
 
     act_rows, grad_rows = factor(act_inverse), factor(grad_inverse)
     pieces = turned(second_turn, [act_plane] * 4)
-    part = partial((0, 3, 2), pieces, [], act_rows, False)
+    part = partial((0, 2, 3), pieces, [], act_rows, False)
     part = partial((1,), pieces, [part], act_rows, True)
     part, grad_plane = lax.optimization_barrier((part, grad_plane))
     act = (part + swap_cores(part)).astype(bf16)
@@ -197,13 +207,13 @@
 
     there = [to_parity(act, j, 1) for j in (0, 1)]
     here = [to_parity(act, j, 0) for j in (0, 1)]
-    half, here[0] = lax.optimization_barrier((half, here[0]))
+    half, there[0] = lax.optimization_barrier((half, there[0]))
     rest = second_turn(half, 3)
     grad_pieces = half[0], half[1], rest[1], rest[0]
     pair = jnp.stack([*there, *here]).reshape(2, 2, 128, 128)
     pair = jnp.swapaxes(pair, 0, 1).reshape(2, 256, 128)
     part = partial((0, 1, 2, 3), grad_pieces, [], grad_rows, False)
-    plane = jnp.stack(turned(first_turn, [pair] * 4))
+    plane = stacked(first_turn, pair, ORDER_B)
     grad = (part + swap_cores(part)).astype(bf16)
     grad = jnp.where(first, grad, jnp.concatenate([grad[64:], grad[:64]], axis=0))
     plane, grad = lax.optimization_barrier((plane, grad))
@@ -213,8 +223,8 @@
         call(tile, "tile", [shape((64, 1024), f32)] * 2, [VMEM] * 2)(grad, piece)
         for piece in turned(second_turn, [plane] * 4)
     ]
-    own = [keep for keep, _ in made]
-    sibling = [swap_cores(give) for _, give in made]
+    own = [made[k][0] for k in ORDER_F]
+    sibling = [swap_cores(made[k][1]) for k in ORDER_F]
     return pl.pallas_call(
         assemble,
         out_shape=shape((64, 8192), f32),

time: 81.8 us -> 81.3 us (level)
  waiting for transfers between devices: 28.2 us -> 27 us
    ppermute x30, waiting for transfers between devices: 28.2 us -> 27 us  [send(): return lax.ppermute(value, AXES, pairs)]
where the time goes in v15:
time: 81.3 us; the launch traced here: 80.7 us
  starting transfers between devices  47.5 us (58%)
  waiting for transfers between devices  27 us (33%)
  Pallas kernels  4.27 us (5%)
  other arithmetic  1.38 us (2%)
    ppermute x30, starting transfers between devices, send(): return lax.ppermute(value, AXES, pairs)  47.5 us
    ppermute x30, waiting for transfers between devices, send(): return lax.ppermute(value, AXES, pairs)  27 us
    pallas_call x3, Pallas kernels, partial(): call(functools.partial(precondition, turns, flip), 'precondition', shape(...  1.91 us
  transfers between devices with their start and end apart: 30, of which 16 were waited for; matrix products, arithmetic and copies ran while one was open for 1% of the time, Pallas kernels for 4%

profile of v15, /device:TPU:1, one launch (start us, length us, event | category | flops | bytes accessed | tf_op | source)
XLA Modules:
  0.0 80.7 jit_solution(10130812647048743001)
XLA Ops:
  0.0 0.8 %fusion = (bf16[1,2,64,128]{3,2,0,1:T(8,128)(2,1)S(1)}, bf16[2,64,128]{2,1,0:T(8,128)(2,1)S(1)}) fusion(bf16[1,64,128]{2,1,0:T(8,128)(2,1)} %bitcast.73, bf16[1,64,128]{2,1,0:T(8,128)(2,1)} %bitcast.74), kind=kLoop, calls=%fused_computation.28 | loop fusion | flops 16384 | bytes 98304 | tf_op jit(solution)/shard_map/stack | solution.py:63
  0.8 5.2 %collective-permute-start.2 = (bf16[2,64,128]{2,1,0:T(8,128)(2,1)S(1)}, bf16[2,64,128]{2,1,0:T(8,128)(2,1)S(1)}, u32[]{:S(2)}, u32[]{:S(2)}) collective-permute-start(bf16[2,64,128]{2,1,0:T(8,128)(2,1)S(1)} %get-tuple-element.52), channel_id=1, source_target_pairs={{0,96},{1,97},{2,98},{3,99},{4,100},{5,101},{6,102},{7,103},{8,104... | collective-permute-start | bytes 98312 | tf_op jit(solution)/shard_map/ppermute | solution.py:32
  6.4 2.1 %collective-permute-start.9 = (bf16[64,8192]{1,0:T(8,128)(2,1)}, bf16[64,8192]{1,0:T(8,128)(2,1)S(1)}, u32[]{:S(2)}, u32[]{:S(2)}) collective-permute-start(bf16[64,8192]{1,0:T(8,128)(2,1)} %param.6), channel_id=1, source_target_pairs={{0,1},{1,0},{2,3},{3,2},{4,5},{5,4},{6,7},{7,6},{8,9},{9,8},{10,11... | collective-permute-start | bytes 3145736 | tf_op jit(solution)/shard_map/ppermute | solution.py:32
  8.5 1.6 %collective-permute-done = bf16[2,64,128]{2,1,0:T(8,128)(2,1)S(1)} collective-permute-done((bf16[2,64,128]{2,1,0:T(8,128)(2,1)S(1)}, bf16[2,64,128]{2,1,0:T(8,128)(2,1)S(1)}, u32[]{:S(2)}, u32[]{:S(2)}) %collective-permute-start) | collective-permute-done | bytes 32800 | tf_op jit(solution)/shard_map/ppermute | solution.py:32
  10.1 2.8 %collective-permute-start.3 = (bf16[4,2,64,128]{3,2,0,1:T(8,128)(2,1)S(1)}, bf16[4,2,64,128]{3,2,0,1:T(8,128)(2,1)S(1)}, u32[]{:S(2)}, u32[]{:S(2)}) collective-permute-start(bf16[4,2,64,128]{3,2,0,1:T(8,128)(2,1)S(1)} %pad_maximum_fusion.4), channel_id=1, source_target_pairs={{0,16},{1,5},{2,18},{3,7},{4,20},{5,1},{6,22},{7,3},{8,24},{9,13},... | collective-permute-start | bytes 393224 | tf_op jit(solution)/shard_map/ppermute | solution.py:32
  13.8 1.7 %collective-permute-done.3 = bf16[4,2,64,128]{3,2,0,1:T(8,128)(2,1)S(1)} collective-permute-done((bf16[4,2,64,128]{3,2,0,1:T(8,128)(2,1)S(1)}, bf16[4,2,64,128]{3,2,0,1:T(8,128)(2,1)S(1)}, u32[]{:S(2)}, u32[]{:S(2)}) %collective-permute-start.3) | collective-permute-done | bytes 131104 | tf_op jit(solution)/shard_map/ppermute | solution.py:32
  15.5 1.8 %collective-permute-done.4 = bf16[4,2,64,128]{3,2,0,1:T(8,128)(2,1)S(1)} collective-permute-done((bf16[4,2,64,128]{3,2,0,1:T(8,128)(2,1)S(1)}, bf16[4,2,64,128]{3,2,0,1:T(8,128)(2,1)S(1)}, u32[]{:S(2)}, u32[]{:S(2)}) %collective-permute-start.4) | collective-permute-done | bytes 131104 | tf_op jit(solution)/shard_map/ppermute | solution.py:32
  17.3 1.0 %collective-permute-done.5 = bf16[4,2,64,128]{3,2,0,1:T(8,128)(2,1)S(1)} collective-permute-done((bf16[4,2,64,128]{3,2,0,1:T(8,128)(2,1)S(1)}, bf16[4,2,64,128]{3,2,0,1:T(8,128)(2,1)S(1)}, u32[]{:S(2)}, u32[]{:S(2)}) %collective-permute-start.5) | collective-permute-done | bytes 131104 | tf_op jit(solution)/shard_map/ppermute | solution.py:32
  18.3 3.0 %collective-permute-start.7 = (bf16[4,4,64,128]{3,2,1,0:T(8,128)(2,1)S(1)}, bf16[4,4,64,128]{3,2,1,0:T(8,128)(2,1)S(1)}, u32[]{:S(2)}, u32[]{:S(2)}) collective-permute-start(bf16[4,4,64,128]{3,2,1,0:T(8,128)(2,1)S(1)} %pad_maximum_fusion.2.refs_0_), channel_id=1, source_target_pairs={{0,4},{1,17},{2,6},{3,19},{4,0},{5,21},{6,2},{7,23},{8,12},{9,25},... | collective-permute-start | bytes 786440 | tf_op jit(solution)/shard_map/ppermute | solution.py:32
  21.3 0.8 collective-permute-start.8
  22.3 2.8 %collective-permute-done.7.refs_1_ = bf16[4,4,64,128]{3,2,1,0:T(8,128)(2,1)S(1)} collective-permute-done((bf16[4,4,64,128]{3,2,1,0:T(8,128)(2,1)S(1)}, bf16[4,4,64,128]{3,2,1,0:T(8,128)(2,1)S(1)}, u32[]{:S(2)}, u32[]{:S(2)}) %collective-permute-start.7) | collective-permute-done | bytes 262176 | tf_op jit(solution)/shard_map/ppermute | solution.py:32
  25.1 3.1 %collective-permute-done.8.refs_2_ = bf16[4,4,64,128]{3,2,1,0:T(8,128)(2,1)S(1)} collective-permute-done((bf16[4,4,64,128]{3,2,1,0:T(8,128)(2,1)S(1)}, bf16[4,4,64,128]{3,2,1,0:T(8,128)(2,1)S(1)}, u32[]{:S(2)}, u32[]{:S(2)}) %collective-permute-start.8) | collective-permute-done | bytes 262176 | tf_op jit(solution)/shard_map/ppermute | solution.py:32
  28.2 0.7 precondition.3.refs_1_
  29.3 4.7 %collective-permute-start.11 = (f32[128,128]{1,0:T(8,128)S(1)}, f32[128,128]{1,0:T(8,128)S(1)}, u32[]{:S(2)}, u32[]{:S(2)}) collective-permute-start(f32[128,128]{1,0:T(8,128)S(1)} %precondition.4), channel_id=1, source_target_pairs={{0,1},{1,0},{2,3},{3,2},{4,5},{5,4},{6,7},{7,6},{8,9},{9,8},{10,11... | collective-permute-start | bytes 196616 | tf_op jit(solution)/shard_map/ppermute | solution.py:32
  34.0 0.9 %collective-permute-done.11 = f32[128,128]{1,0:T(8,128)S(1)} collective-permute-done((f32[128,128]{1,0:T(8,128)S(1)}, f32[128,128]{1,0:T(8,128)S(1)}, u32[]{:S(2)}, u32[]{:S(2)}) %collective-permute-start.11) | collective-permute-done | bytes 65568 | tf_op jit(solution)/shard_map/ppermute | solution.py:32
  34.9 7.8 %collective-permute-start.12 = (bf16[128,128]{1,0:T(8,128)(2,1)S(1)}, bf16[128,128]{1,0:T(8,128)(2,1)S(1)}, u32[]{:S(2)}, u32[]{:S(2)}) collective-permute-start(bf16[128,128]{1,0:T(8,128)(2,1)S(1)} %add_convert_fusion.1), channel_id=1, source_target_pairs={{0,128},{1,160},{2,130},{3,162},{4,132},{5,164},{6,134},{7,166},{8... | collective-permute-start | bytes 98312 | tf_op jit(solution)/shard_map/ppermute | solution.py:32
  42.6 2.8 %collective-permute-start.14 = (bf16[128,128]{1,0:T(8,128)(2,1)S(1)}, bf16[128,128]{1,0:T(8,128)(2,1)S(1)}, u32[]{:S(2)}, u32[]{:S(2)}) collective-permute-start(bf16[128,128]{1,0:T(8,128)(2,1)S(1)} %add_convert_fusion.1), channel_id=1, source_target_pairs={{0,0},{1,32},{2,2},{3,34},{4,4},{5,36},{6,6},{7,38},{8,8},{9,40},{... | collective-permute-start | bytes 98312 | tf_op jit(solution)/shard_map/ppermute | solution.py:32
  46.6 0.7 collective-permute-done.14
  47.3 3.1 %collective-permute-done.15 = bf16[128,128]{1,0:T(8,128)(2,1)S(1)} collective-permute-done((bf16[128,128]{1,0:T(8,128)(2,1)S(1)}, bf16[128,128]{1,0:T(8,128)(2,1)S(1)}, u32[]{:S(2)}, u32[]{:S(2)}) %collective-permute-start.15) | collective-permute-done | bytes 32800 | tf_op jit(solution)/shard_map/ppermute | solution.py:32
  50.5 2.2 %collective-permute-start.16 = (bf16[2,256,128]{2,1,0:T(8,128)(2,1)S(1)}, bf16[2,256,128]{2,1,0:T(8,128)(2,1)S(1)}, u32[]{:S(2)}, u32[]{:S(2)}) collective-permute-start(bf16[2,256,128]{2,1,0:T(8,128)(2,1)S(1)} %bitcast.58), channel_id=1, source_target_pairs={{0,16},{1,5},{2,18},{3,7},{4,20},{5,1},{6,22},{7,3},{8,24},{9,13},... | collective-permute-start | bytes 393224 | tf_op jit(solution)/shard_map/ppermute | solution.py:32
  52.7 0.8 %collective-permute-start.17 = (bf16[2,256,128]{2,1,0:T(8,128)(2,1)S(1)}, bf16[2,256,128]{2,1,0:T(8,128)(2,1)S(1)}, u32[]{:S(2)}, u32[]{:S(2)}) collective-permute-start(bf16[2,256,128]{2,1,0:T(8,128)(2,1)S(1)} %bitcast.59), channel_id=1, source_target_pairs={{0,8},{1,3},{2,10},{3,1},{4,12},{5,7},{6,14},{7,5},{8,0},{9,11},{1... | collective-permute-start | bytes 393224 | tf_op jit(solution)/shard_map/ppermute | solution.py:32
  54.0 4.1 %collective-permute-done.19 = bf16[2,4,4,64,128]{4,3,2,1,0:T(8,128)(2,1)S(1)} collective-permute-done((bf16[2,4,4,64,128]{4,3,2,1,0:T(8,128)(2,1)S(1)}, bf16[2,4,4,64,128]{4,3,2,1,0:T(8,128)(2,1)S(1)}, u32[]{:S(2)}, u32[]{:S(2)}) %collective-permute-start.19) | collective-permute-done | bytes 524320 | tf_op jit(solution)/shard_map/ppermute | solution.py:32
  58.2 0.9 %precondition.5 = f32[128,128]{1,0:T(8,128)S(1)} custom-call(bf16[4,4,64,128]{3,2,1,0:T(8,128)(2,1)S(1)} %get-tuple-element.40.refs_0_, bf16[4,4,64,128]{3,2,1,0:T(8,128)(2,1)S(1)} %get-tuple-element.39.refs_1_, bf16[4,4,64,128]{3,2,1,0:T(8,128)(2,1)S(1)} %get-tuple-element.38.refs_2_, bf16[4,4,64,128]{3,2,1,0:T(8,128)(2,1)S(1)} %get-tuple-element.37.refs_3_, ...), custom_call_target="tpu_custom_call" | custom-call | tf_op jit(solution)/shard_map/precondition/pallas_call | solution.py:193
  59.2 1.1 %collective-permute-done.21 = f32[128,128]{1,0:T(8,128)S(1)} collective-permute-done((f32[128,128]{1,0:T(8,128)S(1)}, f32[128,128]{1,0:T(8,128)S(1)}, u32[]{:S(2)}, u32[]{:S(2)}) %collective-permute-start.21) | collective-permute-done | bytes 65568 | tf_op jit(solution)/shard_map/ppermute | solution.py:32
  60.5 2.2 %collective-permute-start.24 = (bf16[4,2,256,128]{3,2,1,0:T(8,128)(2,1)S(1)}, bf16[4,2,256,128]{3,2,1,0:T(8,128)(2,1)S(1)}, u32[]{:S(2)}, u32[]{:S(2)}) collective-permute-start(bf16[4,2,256,128]{3,2,1,0:T(8,128)(2,1)S(1)} %pad_maximum_fusion.1.piece), channel_id=1, source_target_pairs={{0,6},{1,25},{2,4},{3,27},{4,2},{5,29},{6,0},{7,31},{8,14},{9,17},... | collective-permute-start | bytes 1572872 | tf_op jit(solution)/shard_map/ppermute | solution.py:32
  63.1 5.1 %collective-permute-start.22 = (bf16[128,128]{1,0:T(8,128)(2,1)S(1)}, bf16[128,128]{1,0:T(8,128)(2,1)S(1)}, u32[]{:S(2)}, u32[]{:S(2)}) collective-permute-start(bf16[128,128]{1,0:T(8,128)(2,1)S(1)} %maximum_select_fusion), channel_id=1, source_target_pairs={{0,128},{1,129},{2,130},{3,131},{4,132},{5,133},{6,134},{7,135},{8... | collective-permute-start | bytes 98312 | tf_op jit(solution)/shard_map/ppermute | solution.py:32
  68.2 1.6 %collective-permute-done.22 = bf16[128,128]{1,0:T(8,128)(2,1)S(1)} collective-permute-done((bf16[128,128]{1,0:T(8,128)(2,1)S(1)}, bf16[128,128]{1,0:T(8,128)(2,1)S(1)}, u32[]{:S(2)}, u32[]{:S(2)}) %collective-permute-start.22) | collective-permute-done | bytes 32800 | tf_op jit(solution)/shard_map/ppermute | solution.py:32
  70.1 3.4 %collective-permute-start.26 = (f32[64,1024]{1,0:T(8,128)S(1)}, f32[64,1024]{1,0:T(8,128)S(1)}, u32[]{:S(2)}, u32[]{:S(2)}) collective-permute-start(f32[64,1024]{1,0:T(8,128)S(1)} %get-tuple-element.29), channel_id=1, source_target_pairs={{0,1},{1,0},{2,3},{3,2},{4,5},{5,4},{6,7},{7,6},{8,9},{9,8},{10,11... | collective-permute-start | bytes 786440 | tf_op jit(solution)/shard_map/ppermute | solution.py:32
  73.8 1.9 %collective-permute-done.24.piece = bf16[4,2,256,128]{3,2,1,0:T(8,128)(2,1)S(1)} collective-permute-done((bf16[4,2,256,128]{3,2,1,0:T(8,128)(2,1)S(1)}, bf16[4,2,256,128]{3,2,1,0:T(8,128)(2,1)S(1)}, u32[]{:S(2)}, u32[]{:S(2)}) %collective-permute-start.24) | collective-permute-done | bytes 524320 | tf_op jit(solution)/shard_map/ppermute | solution.py:32
  76.0 1.3 %collective-permute-start.28 = (f32[64,1024]{1,0:T(8,128)S(1)}, f32[64,1024]{1,0:T(8,128)S(1)}, u32[]{:S(2)}, u32[]{:S(2)}) collective-permute-start(f32[64,1024]{1,0:T(8,128)S(1)} %get-tuple-element.31), channel_id=1, source_target_pairs={{0,1},{1,0},{2,3},{3,2},{4,5},{5,4},{6,7},{7,6},{8,9},{9,8},{10,11... | collective-permute-start | bytes 786440 | tf_op jit(solution)/shard_map/ppermute | solution.py:32
  78.5 0.7 collective-permute-done.27.refs_5_
  79.2 1.4 %assemble.1 = f32[64,8192]{1,0:T(8,128)} custom-call(f32[64,1024]{1,0:T(8,128)S(1)} %get-tuple-element.25.refs_0_, f32[64,1024]{1,0:T(8,128)S(1)} %get-tuple-element.26.refs_1_, f32[64,1024]{1,0:T(8,128)S(1)} %get-tuple-element.27.refs_2_, f32[64,1024]{1,0:T(8,128)S(1)} %get-tuple-element.28.refs_3_, f32[64,1024]{1,0:T(8,128)S(1)} %collective-permute-done.26.refs_4_, ...), custom_call_target="tpu_custom_call" | custom-call | tf_op jit(solution)/shard_map/assemble/pallas_call | solution.py:228
  (62 shorter events, 6.4 us)
Async XLA Ops:
  0.0 22.1 %copy-start = (bf16[64,8192]{1,0:T(8,128)(2,1)S(1)}, bf16[64,8192]{1,0:T(8,128)(2,1)}, u32[]{:S(2)}) copy-start(bf16[64,8192]{1,0:T(8,128)(2,1)} %param.6) | copy-start | bytes 3145732
  0.8 7.6 %collective-permute-start.2 = (bf16[2,64,128]{2,1,0:T(8,128)(2,1)S(1)}, bf16[2,64,128]{2,1,0:T(8,128)(2,1)S(1)}, u32[]{:S(2)}, u32[]{:S(2)}) collective-permute-start(bf16[2,64,128]{2,1,0:T(8,128)(2,1)S(1)} %get-tuple-element.52), channel_id=1, source_target_pairs={{0,96},{1,97},{2,98},{3,99},{4,100},{5,101},{6,102},{7,103},{8,104... | collective-permute-start | bytes 98312 | tf_op jit(solution)/shard_map/ppermute | solution.py:32
  6.0 4.0 %collective-permute-start = (bf16[2,64,128]{2,1,0:T(8,128)(2,1)S(1)}, bf16[2,64,128]{2,1,0:T(8,128)(2,1)S(1)}, u32[]{:S(2)}, u32[]{:S(2)}) collective-permute-start(bf16[2,64,128]{2,1,0:T(8,128)(2,1)S(1)} %get-tuple-element.52), channel_id=1, source_target_pairs={{0,64},{1,65},{2,66},{3,67},{4,68},{5,69},{6,70},{7,71},{8,72},{9,... | collective-permute-start | bytes 98312 | tf_op jit(solution)/shard_map/ppermute | solution.py:32
  6.0 4.0 %collective-permute-start.1 = (bf16[2,64,128]{2,1,0:T(8,128)(2,1)S(1)}, bf16[2,64,128]{2,1,0:T(8,128)(2,1)S(1)}, u32[]{:S(2)}, u32[]{:S(2)}) collective-permute-start(bf16[2,64,128]{2,1,0:T(8,128)(2,1)S(1)} %get-tuple-element.52), channel_id=1, source_target_pairs={{0,32},{1,33},{2,34},{3,35},{4,36},{5,37},{6,38},{7,39},{8,40},{9,... | collective-permute-start | bytes 98312 | tf_op jit(solution)/shard_map/ppermute | solution.py:32
  6.4 15.7 %collective-permute-start.9 = (bf16[64,8192]{1,0:T(8,128)(2,1)}, bf16[64,8192]{1,0:T(8,128)(2,1)S(1)}, u32[]{:S(2)}, u32[]{:S(2)}) collective-permute-start(bf16[64,8192]{1,0:T(8,128)(2,1)} %param.6), channel_id=1, source_target_pairs={{0,1},{1,0},{2,3},{3,2},{4,5},{5,4},{6,7},{7,6},{8,9},{9,8},{10,11... | collective-permute-start | bytes 3145736 | tf_op jit(solution)/shard_map/ppermute | solution.py:32
  8.5 37.8 %collective-permute-start.20 = (bf16[64,8192]{1,0:T(8,128)(2,1)}, bf16[64,8192]{1,0:T(8,128)(2,1)S(1)}, u32[]{:S(2)}, u32[]{:S(2)}) collective-permute-start(bf16[64,8192]{1,0:T(8,128)(2,1)} %param.7), channel_id=1, source_target_pairs={{0,1},{1,0},{2,3},{3,2},{4,5},{5,4},{6,7},{7,6},{8,9},{9,8},{10,11... | collective-permute-start | bytes 3145736 | tf_op jit(solution)/shard_map/ppermute | solution.py:32
  10.1 5.4 %collective-permute-start.3 = (bf16[4,2,64,128]{3,2,0,1:T(8,128)(2,1)S(1)}, bf16[4,2,64,128]{3,2,0,1:T(8,128)(2,1)S(1)}, u32[]{:S(2)}, u32[]{:S(2)}) collective-permute-start(bf16[4,2,64,128]{3,2,0,1:T(8,128)(2,1)S(1)} %pad_maximum_fusion.4), channel_id=1, source_target_pairs={{0,16},{1,5},{2,18},{3,7},{4,20},{5,1},{6,22},{7,3},{8,24},{9,13},... | collective-permute-start | bytes 393224 | tf_op jit(solution)/shard_map/ppermute | solution.py:32
  12.9 4.4 %collective-permute-start.4 = (bf16[4,2,64,128]{3,2,0,1:T(8,128)(2,1)S(1)}, bf16[4,2,64,128]{3,2,0,1:T(8,128)(2,1)S(1)}, u32[]{:S(2)}, u32[]{:S(2)}) collective-permute-start(bf16[4,2,64,128]{3,2,0,1:T(8,128)(2,1)S(1)} %pad_maximum_fusion.4), channel_id=1, source_target_pairs={{0,8},{1,3},{2,10},{3,1},{4,12},{5,7},{6,14},{7,5},{8,0},{9,11},{1... | collective-permute-start | bytes 393224 | tf_op jit(solution)/shard_map/ppermute | solution.py:32
  13.2 5.0 %collective-permute-start.5 = (bf16[4,2,64,128]{3,2,0,1:T(8,128)(2,1)S(1)}, bf16[4,2,64,128]{3,2,0,1:T(8,128)(2,1)S(1)}, u32[]{:S(2)}, u32[]{:S(2)}) collective-permute-start(bf16[4,2,64,128]{3,2,0,1:T(8,128)(2,1)S(1)} %pad_maximum_fusion.4), channel_id=1, source_target_pairs={{0,24},{1,7},{2,26},{3,5},{4,28},{5,3},{6,30},{7,1},{8,16},{9,15},... | collective-permute-start | bytes 393224 | tf_op jit(solution)/shard_map/ppermute | solution.py:32
  18.3 6.8 %collective-permute-start.7 = (bf16[4,4,64,128]{3,2,1,0:T(8,128)(2,1)S(1)}, bf16[4,4,64,128]{3,2,1,0:T(8,128)(2,1)S(1)}, u32[]{:S(2)}, u32[]{:S(2)}) collective-permute-start(bf16[4,4,64,128]{3,2,1,0:T(8,128)(2,1)S(1)} %pad_maximum_fusion.2.refs_0_), channel_id=1, source_target_pairs={{0,4},{1,17},{2,6},{3,19},{4,0},{5,21},{6,2},{7,23},{8,12},{9,25},... | collective-permute-start | bytes 786440 | tf_op jit(solution)/shard_map/ppermute | solution.py:32
  21.3 6.9 %collective-permute-start.8 = (bf16[4,4,64,128]{3,2,1,0:T(8,128)(2,1)S(1)}, bf16[4,4,64,128]{3,2,1,0:T(8,128)(2,1)S(1)}, u32[]{:S(2)}, u32[]{:S(2)}) collective-permute-start(bf16[4,4,64,128]{3,2,1,0:T(8,128)(2,1)S(1)} %pad_maximum_fusion.2.refs_0_), channel_id=1, source_target_pairs={{0,6},{1,25},{2,4},{3,27},{4,2},{5,29},{6,0},{7,31},{8,14},{9,17},... | collective-permute-start | bytes 786440 | tf_op jit(solution)/shard_map/ppermute | solution.py:32
  22.1 6.8 %collective-permute-start.6 = (bf16[4,4,64,128]{3,2,1,0:T(8,128)(2,1)S(1)}, bf16[4,4,64,128]{3,2,1,0:T(8,128)(2,1)S(1)}, u32[]{:S(2)}, u32[]{:S(2)}) collective-permute-start(bf16[4,4,64,128]{3,2,1,0:T(8,128)(2,1)S(1)} %pad_maximum_fusion.2.refs_0_), channel_id=1, source_target_pairs={{0,2},{1,9},{2,0},{3,11},{4,6},{5,13},{6,4},{7,15},{8,10},{9,1},{1... | collective-permute-start | bytes 786440 | tf_op jit(solution)/shard_map/ppermute | solution.py:32
  28.9 17.4 %copy-start.1 = (bf16[64,8192]{1,0:T(8,128)(2,1)S(1)}, bf16[64,8192]{1,0:T(8,128)(2,1)}, u32[]{:S(2)}) copy-start(bf16[64,8192]{1,0:T(8,128)(2,1)} %param.7) | copy-start | bytes 3145732
  29.3 5.6 %collective-permute-start.11 = (f32[128,128]{1,0:T(8,128)S(1)}, f32[128,128]{1,0:T(8,128)S(1)}, u32[]{:S(2)}, u32[]{:S(2)}) collective-permute-start(f32[128,128]{1,0:T(8,128)S(1)} %precondition.4), channel_id=1, source_target_pairs={{0,1},{1,0},{2,3},{3,2},{4,5},{5,4},{6,7},{7,6},{8,9},{9,8},{10,11... | collective-permute-start | bytes 196616 | tf_op jit(solution)/shard_map/ppermute | solution.py:32
  33.9 11.5 %collective-permute-start.10 = (bf16[4,4,64,128]{3,2,1,0:T(8,128)(2,1)S(1)}, bf16[4,4,64,128]{3,2,1,0:T(8,128)(2,1)S(1)}, u32[]{:S(2)}, u32[]{:S(2)}) collective-permute-start(bf16[4,4,64,128]{3,2,1,0:T(8,128)(2,1)S(1)} %pad_maximum_fusion.3), channel_id=1, source_target_pairs={{0,2},{1,9},{2,0},{3,11},{4,6},{5,13},{6,4},{7,15},{8,10},{9,1},{1... | collective-permute-start | bytes 786440 | tf_op jit(solution)/shard_map/ppermute | solution.py:32
  34.9 11.3 %collective-permute-start.12 = (bf16[128,128]{1,0:T(8,128)(2,1)S(1)}, bf16[128,128]{1,0:T(8,128)(2,1)S(1)}, u32[]{:S(2)}, u32[]{:S(2)}) collective-permute-start(bf16[128,128]{1,0:T(8,128)(2,1)S(1)} %add_convert_fusion.1), channel_id=1, source_target_pairs={{0,128},{1,160},{2,130},{3,162},{4,132},{5,164},{6,134},{7,166},{8... | collective-permute-start | bytes 98312 | tf_op jit(solution)/shard_map/ppermute | solution.py:32
  42.6 4.0 %collective-permute-start.13 = (bf16[128,128]{1,0:T(8,128)(2,1)S(1)}, bf16[128,128]{1,0:T(8,128)(2,1)S(1)}, u32[]{:S(2)}, u32[]{:S(2)}) collective-permute-start(bf16[128,128]{1,0:T(8,128)(2,1)S(1)} %add_convert_fusion.1), channel_id=1, source_target_pairs={{0,192},{1,224},{2,194},{3,226},{4,196},{5,228},{6,198},{7,230},{8... | collective-permute-start | bytes 98312 | tf_op jit(solution)/shard_map/ppermute | solution.py:32
  42.6 4.6 %collective-permute-start.14 = (bf16[128,128]{1,0:T(8,128)(2,1)S(1)}, bf16[128,128]{1,0:T(8,128)(2,1)S(1)}, u32[]{:S(2)}, u32[]{:S(2)}) collective-permute-start(bf16[128,128]{1,0:T(8,128)(2,1)S(1)} %add_convert_fusion.1), channel_id=1, source_target_pairs={{0,0},{1,32},{2,2},{3,34},{4,4},{5,36},{6,6},{7,38},{8,8},{9,40},{... | collective-permute-start | bytes 98312 | tf_op jit(solution)/shard_map/ppermute | solution.py:32
  45.4 5.0 %collective-permute-start.15 = (bf16[128,128]{1,0:T(8,128)(2,1)S(1)}, bf16[128,128]{1,0:T(8,128)(2,1)S(1)}, u32[]{:S(2)}, u32[]{:S(2)}) collective-permute-start(bf16[128,128]{1,0:T(8,128)(2,1)S(1)} %add_convert_fusion.1), channel_id=1, source_target_pairs={{0,64},{1,96},{2,66},{3,98},{4,68},{5,100},{6,70},{7,102},{8,72},{... | collective-permute-start | bytes 98312 | tf_op jit(solution)/shard_map/ppermute | solution.py:32
  46.2 12.0 %collective-permute-start.19 = (bf16[2,4,4,64,128]{4,3,2,1,0:T(8,128)(2,1)S(1)}, bf16[2,4,4,64,128]{4,3,2,1,0:T(8,128)(2,1)S(1)}, u32[]{:S(2)}, u32[]{:S(2)}) collective-permute-start(bf16[2,4,4,64,128]{4,3,2,1,0:T(8,128)(2,1)S(1)} %pad_maximum_fusion), channel_id=1, source_target_pairs={{0,6},{1,25},{2,4},{3,27},{4,2},{5,29},{6,0},{7,31},{8,14},{9,17},... | collective-permute-start | bytes 1572872 | tf_op jit(solution)/shard_map/ppermute | solution.py:32
  50.5 8.7 %collective-permute-start.16 = (bf16[2,256,128]{2,1,0:T(8,128)(2,1)S(1)}, bf16[2,256,128]{2,1,0:T(8,128)(2,1)S(1)}, u32[]{:S(2)}, u32[]{:S(2)}) collective-permute-start(bf16[2,256,128]{2,1,0:T(8,128)(2,1)S(1)} %bitcast.58), channel_id=1, source_target_pairs={{0,16},{1,5},{2,18},{3,7},{4,20},{5,1},{6,22},{7,3},{8,24},{9,13},... | collective-permute-start | bytes 393224 | tf_op jit(solution)/shard_map/ppermute | solution.py:32
  52.7 6.5 %collective-permute-start.17 = (bf16[2,256,128]{2,1,0:T(8,128)(2,1)S(1)}, bf16[2,256,128]{2,1,0:T(8,128)(2,1)S(1)}, u32[]{:S(2)}, u32[]{:S(2)}) collective-permute-start(bf16[2,256,128]{2,1,0:T(8,128)(2,1)S(1)} %bitcast.59), channel_id=1, source_target_pairs={{0,8},{1,3},{2,10},{3,1},{4,12},{5,7},{6,14},{7,5},{8,0},{9,11},{1... | collective-permute-start | bytes 393224 | tf_op jit(solution)/shard_map/ppermute | solution.py:32
  53.5 5.6 %collective-permute-start.18 = (bf16[2,256,128]{2,1,0:T(8,128)(2,1)S(1)}, bf16[2,256,128]{2,1,0:T(8,128)(2,1)S(1)}, u32[]{:S(2)}, u32[]{:S(2)}) collective-permute-start(bf16[2,256,128]{2,1,0:T(8,128)(2,1)S(1)} %bitcast.60), channel_id=1, source_target_pairs={{0,24},{1,7},{2,26},{3,5},{4,28},{5,3},{6,30},{7,1},{8,16},{9,15},... | collective-permute-start | bytes 393224 | tf_op jit(solution)/shard_map/ppermute | solution.py:32
  59.0 1.3 %collective-permute-start.21 = (f32[128,128]{1,0:T(8,128)S(1)}, f32[128,128]{1,0:T(8,128)S(1)}, u32[]{:S(2)}, u32[]{:S(2)}) collective-permute-start(f32[128,128]{1,0:T(8,128)S(1)} %precondition.5), channel_id=1, source_target_pairs={{0,1},{1,0},{2,3},{3,2},{4,5},{5,4},{6,7},{7,6},{8,9},{9,8},{10,11... | collective-permute-start | bytes 196616 | tf_op jit(solution)/shard_map/ppermute | solution.py:32
  60.4 13.0 %collective-permute-start.25 = (bf16[4,2,256,128]{3,2,1,0:T(8,128)(2,1)S(1)}, bf16[4,2,256,128]{3,2,1,0:T(8,128)(2,1)S(1)}, u32[]{:S(2)}, u32[]{:S(2)}) collective-permute-start(bf16[4,2,256,128]{3,2,1,0:T(8,128)(2,1)S(1)} %pad_maximum_fusion.1.piece), channel_id=1, source_target_pairs={{0,4},{1,17},{2,6},{3,19},{4,0},{5,21},{6,2},{7,23},{8,12},{9,25},... | collective-permute-start | bytes 1572872 | tf_op jit(solution)/shard_map/ppermute | solution.py:32
  60.5 15.2 %collective-permute-start.24 = (bf16[4,2,256,128]{3,2,1,0:T(8,128)(2,1)S(1)}, bf16[4,2,256,128]{3,2,1,0:T(8,128)(2,1)S(1)}, u32[]{:S(2)}, u32[]{:S(2)}) collective-permute-start(bf16[4,2,256,128]{3,2,1,0:T(8,128)(2,1)S(1)} %pad_maximum_fusion.1.piece), channel_id=1, source_target_pairs={{0,6},{1,25},{2,4},{3,27},{4,2},{5,29},{6,0},{7,31},{8,14},{9,17},... | collective-permute-start | bytes 1572872 | tf_op jit(solution)/shard_map/ppermute | solution.py:32
  62.7 14.6 %collective-permute-start.23 = (bf16[4,2,256,128]{3,2,1,0:T(8,128)(2,1)S(1)}, bf16[4,2,256,128]{3,2,1,0:T(8,128)(2,1)S(1)}, u32[]{:S(2)}, u32[]{:S(2)}) collective-permute-start(bf16[4,2,256,128]{3,2,1,0:T(8,128)(2,1)S(1)} %pad_maximum_fusion.1.piece), channel_id=1, source_target_pairs={{0,2},{1,9},{2,0},{3,11},{4,6},{5,13},{6,4},{7,15},{8,10},{9,1},{1... | collective-permute-start | bytes 1572872 | tf_op jit(solution)/shard_map/ppermute | solution.py:32
  63.1 6.7 %collective-permute-start.22 = (bf16[128,128]{1,0:T(8,128)(2,1)S(1)}, bf16[128,128]{1,0:T(8,128)(2,1)S(1)}, u32[]{:S(2)}, u32[]{:S(2)}) collective-permute-start(bf16[128,128]{1,0:T(8,128)(2,1)S(1)} %maximum_select_fusion), channel_id=1, source_target_pairs={{0,128},{1,129},{2,130},{3,131},{4,132},{5,133},{6,134},{7,135},{8... | collective-permute-start | bytes 98312 | tf_op jit(solution)/shard_map/ppermute | solution.py:32
  70.1 7.7 %collective-permute-start.26 = (f32[64,1024]{1,0:T(8,128)S(1)}, f32[64,1024]{1,0:T(8,128)S(1)}, u32[]{:S(2)}, u32[]{:S(2)}) collective-permute-start(f32[64,1024]{1,0:T(8,128)S(1)} %get-tuple-element.29), channel_id=1, source_target_pairs={{0,1},{1,0},{2,3},{3,2},{4,5},{5,4},{6,7},{7,6},{8,9},{9,8},{10,11... | collective-permute-start | bytes 786440 | tf_op jit(solution)/shard_map/ppermute | solution.py:32
  73.7 4.1 %collective-permute-start.29 = (f32[64,1024]{1,0:T(8,128)S(1)}, f32[64,1024]{1,0:T(8,128)S(1)}, u32[]{:S(2)}, u32[]{:S(2)}) collective-permute-start(f32[64,1024]{1,0:T(8,128)S(1)} %get-tuple-element.32), channel_id=1, source_target_pairs={{0,1},{1,0},{2,3},{3,2},{4,5},{5,4},{6,7},{7,6},{8,9},{9,8},{10,11... | collective-permute-start | bytes 786440 | tf_op jit(solution)/shard_map/ppermute | solution.py:32
  76.0 2.5 %collective-permute-start.28 = (f32[64,1024]{1,0:T(8,128)S(1)}, f32[64,1024]{1,0:T(8,128)S(1)}, u32[]{:S(2)}, u32[]{:S(2)}) collective-permute-start(f32[64,1024]{1,0:T(8,128)S(1)} %get-tuple-element.31), channel_id=1, source_target_pairs={{0,1},{1,0},{2,3},{3,2},{4,5},{5,4},{6,7},{7,6},{8,9},{9,8},{10,11... | collective-permute-start | bytes 786440 | tf_op jit(solution)/shard_map/ppermute | solution.py:32
  77.5 1.6 %collective-permute-start.27 = (f32[64,1024]{1,0:T(8,128)S(1)}, f32[64,1024]{1,0:T(8,128)S(1)}, u32[]{:S(2)}, u32[]{:S(2)}) collective-permute-start(f32[64,1024]{1,0:T(8,128)S(1)} %get-tuple-element.30), channel_id=1, source_target_pairs={{0,1},{1,0},{2,3},{3,2},{4,5},{5,4},{6,7},{7,6},{8,9},{9,8},{10,11... | collective-permute-start | bytes 786440 | tf_op jit(solution)/shard_map/ppermute | solution.py:32

commit v16 on v15

--- a/solution.py
+++ b/solution.py
@@ -75,8 +75,8 @@
     return [values[0]] + [got[k] for k in (1, 2, 3)]
 
 
-ORDER_F = (0, 1, 3, 2)
-ORDER_Z, ORDER_2, ORDER_B = (0, 2, 1, 3), (0, 2, 1, 3), (0, 2, 1, 3)
+ORDER_F = (0, 2, 1, 3)
+ORDER_Z, ORDER_2, ORDER_B = (0, 1, 2, 3), (0, 1, 3, 2), (0, 1, 3, 2)
 
 
 def here_is():
@@ -199,25 +199,24 @@
 
     act_rows, grad_rows = factor(act_inverse), factor(grad_inverse)
     pieces = turned(second_turn, [act_plane] * 4)
-    part = partial((0, 2, 3), pieces, [], act_rows, False)
-    part = partial((1,), pieces, [part], act_rows, True)
+    part = partial((0, 3, 1), pieces, [], act_rows, False)
+    part = partial((2,), pieces, [part], act_rows, True)
     part, grad_plane = lax.optimization_barrier((part, grad_plane))
     act = (part + swap_cores(part)).astype(bf16)
     half = jnp.stack([grad_plane, second_turn(grad_plane, 1)])
 
     there = [to_parity(act, j, 1) for j in (0, 1)]
     here = [to_parity(act, j, 0) for j in (0, 1)]
-    half, there[0] = lax.optimization_barrier((half, there[0]))
+    half, here[0] = lax.optimization_barrier((half, here[0]))
     rest = second_turn(half, 3)
     grad_pieces = half[0], half[1], rest[1], rest[0]
-    pair = jnp.stack([*there, *here]).reshape(2, 2, 128, 128)
+    pair = jnp.stack([*here, *there]).reshape(2, 2, 128, 128)
     pair = jnp.swapaxes(pair, 0, 1).reshape(2, 256, 128)
     part = partial((0, 1, 2, 3), grad_pieces, [], grad_rows, False)
     plane = stacked(first_turn, pair, ORDER_B)
     grad = (part + swap_cores(part)).astype(bf16)
     grad = jnp.where(first, grad, jnp.concatenate([grad[64:], grad[:64]], axis=0))
-    plane, grad = lax.optimization_barrier((plane, grad))
-    grad = jnp.concatenate([swap_reps(grad), grad], axis=1)
+    grad = jnp.concatenate([grad, swap_reps(grad)], axis=1)
 
     made = [
         call(tile, "tile", [shape((64, 1024), f32)] * 2, [VMEM] * 2)(grad, piece)

time: 81.3 us -> 77.3 us (0.951)
  waiting for transfers between devices: 27 us -> 23 us
    ppermute x30, waiting for transfers between devices: 27 us -> 23 us  [send(): return lax.ppermute(value, AXES, pairs)]
  transfers between devices with their start and end apart: 30 -> 30, of which waited for: 16 -> 12; matrix products, arithmetic and copies ran while one was open for 1% -> 1% of each run, Pallas kernels for 4% -> 4%
where the time goes in v16:
time: 77.3 us; the launch traced here: 77.1 us
  starting transfers between devices  47.9 us (62%)
  waiting for transfers between devices  23 us (30%)
  Pallas kernels  4.29 us (6%)
  other arithmetic  1.38 us (2%)
    ppermute x30, starting transfers between devices, send(): return lax.ppermute(value, AXES, pairs)  47.9 us
    ppermute x30, waiting for transfers between devices, send(): return lax.ppermute(value, AXES, pairs)  23 us
    pallas_call x3, Pallas kernels, partial(): call(functools.partial(precondition, turns, flip), 'precondition', shape(...  1.92 us
  transfers between devices with their start and end apart: 30, of which 12 were waited for; matrix products, arithmetic and copies ran while one was open for 1% of the time, Pallas kernels for 4%

profile of v16, /device:TPU:1, one launch (start us, length us, event | category | flops | bytes accessed | tf_op | source)
XLA Modules:
  0.0 77.1 jit_solution(5711439206892193503)
XLA Ops:
  0.0 0.8 %fusion = (bf16[1,2,64,128]{3,2,0,1:T(8,128)(2,1)S(1)}, bf16[2,64,128]{2,1,0:T(8,128)(2,1)S(1)}) fusion(bf16[1,64,128]{2,1,0:T(8,128)(2,1)} %bitcast.73, bf16[1,64,128]{2,1,0:T(8,128)(2,1)} %bitcast.74), kind=kLoop, calls=%fused_computation.27 | loop fusion | flops 16384 | bytes 98304 | tf_op jit(solution)/shard_map/stack | solution.py:63
  0.8 5.2 %collective-permute-start.2 = (bf16[2,64,128]{2,1,0:T(8,128)(2,1)S(1)}, bf16[2,64,128]{2,1,0:T(8,128)(2,1)S(1)}, u32[]{:S(2)}, u32[]{:S(2)}) collective-permute-start(bf16[2,64,128]{2,1,0:T(8,128)(2,1)S(1)} %get-tuple-element.48), channel_id=1, source_target_pairs={{0,96},{1,97},{2,98},{3,99},{4,100},{5,101},{6,102},{7,103},{8,104... | collective-permute-start | bytes 98312 | tf_op jit(solution)/shard_map/ppermute | solution.py:32
  6.4 2.1 %collective-permute-start.9 = (bf16[64,8192]{1,0:T(8,128)(2,1)}, bf16[64,8192]{1,0:T(8,128)(2,1)S(1)}, u32[]{:S(2)}, u32[]{:S(2)}) collective-permute-start(bf16[64,8192]{1,0:T(8,128)(2,1)} %param.6), channel_id=1, source_target_pairs={{0,1},{1,0},{2,3},{3,2},{4,5},{5,4},{6,7},{7,6},{8,9},{9,8},{10,11... | collective-permute-start | bytes 3145736 | tf_op jit(solution)/shard_map/ppermute | solution.py:32
  8.5 1.6 %collective-permute-done.1 = bf16[2,64,128]{2,1,0:T(8,128)(2,1)S(1)} collective-permute-done((bf16[2,64,128]{2,1,0:T(8,128)(2,1)S(1)}, bf16[2,64,128]{2,1,0:T(8,128)(2,1)S(1)}, u32[]{:S(2)}, u32[]{:S(2)}) %collective-permute-start.1) | collective-permute-done | bytes 32800 | tf_op jit(solution)/shard_map/ppermute | solution.py:32
  10.1 2.8 %collective-permute-start.5 = (bf16[4,2,64,128]{3,2,0,1:T(8,128)(2,1)S(1)}, bf16[4,2,64,128]{3,2,0,1:T(8,128)(2,1)S(1)}, u32[]{:S(2)}, u32[]{:S(2)}) collective-permute-start(bf16[4,2,64,128]{3,2,0,1:T(8,128)(2,1)S(1)} %pad_maximum_fusion.4), channel_id=1, source_target_pairs={{0,16},{1,5},{2,18},{3,7},{4,20},{5,1},{6,22},{7,3},{8,24},{9,13},... | collective-permute-start | bytes 393224 | tf_op jit(solution)/shard_map/ppermute | solution.py:32
  12.9 0.9 %collective-permute-start.4 = (bf16[4,2,64,128]{3,2,0,1:T(8,128)(2,1)S(1)}, bf16[4,2,64,128]{3,2,0,1:T(8,128)(2,1)S(1)}, u32[]{:S(2)}, u32[]{:S(2)}) collective-permute-start(bf16[4,2,64,128]{3,2,0,1:T(8,128)(2,1)S(1)} %pad_maximum_fusion.4), channel_id=1, source_target_pairs={{0,24},{1,7},{2,26},{3,5},{4,28},{5,3},{6,30},{7,1},{8,16},{9,15},... | collective-permute-start | bytes 393224 | tf_op jit(solution)/shard_map/ppermute | solution.py:32
  13.8 1.7 %collective-permute-done.5 = bf16[4,2,64,128]{3,2,0,1:T(8,128)(2,1)S(1)} collective-permute-done((bf16[4,2,64,128]{3,2,0,1:T(8,128)(2,1)S(1)}, bf16[4,2,64,128]{3,2,0,1:T(8,128)(2,1)S(1)}, u32[]{:S(2)}, u32[]{:S(2)}) %collective-permute-start.5) | collective-permute-done | bytes 131104 | tf_op jit(solution)/shard_map/ppermute | solution.py:32
  15.5 2.5 %collective-permute-done.4 = bf16[4,2,64,128]{3,2,0,1:T(8,128)(2,1)S(1)} collective-permute-done((bf16[4,2,64,128]{3,2,0,1:T(8,128)(2,1)S(1)}, bf16[4,2,64,128]{3,2,0,1:T(8,128)(2,1)S(1)}, u32[]{:S(2)}, u32[]{:S(2)}) %collective-permute-start.4) | collective-permute-done | bytes 131104 | tf_op jit(solution)/shard_map/ppermute | solution.py:32
  18.1 3.0 %collective-permute-start.6 = (bf16[4,4,64,128]{3,2,1,0:T(8,128)(2,1)S(1)}, bf16[4,4,64,128]{3,2,1,0:T(8,128)(2,1)S(1)}, u32[]{:S(2)}, u32[]{:S(2)}) collective-permute-start(bf16[4,4,64,128]{3,2,1,0:T(8,128)(2,1)S(1)} %pad_maximum_fusion.2.refs_0_), channel_id=1, source_target_pairs={{0,4},{1,17},{2,6},{3,19},{4,0},{5,21},{6,2},{7,23},{8,12},{9,25},... | collective-permute-start | bytes 786440 | tf_op jit(solution)/shard_map/ppermute | solution.py:32
  21.1 0.7 collective-permute-start.7
  22.0 5.9 %collective-permute-done.7.refs_1_ = bf16[4,4,64,128]{3,2,1,0:T(8,128)(2,1)S(1)} collective-permute-done((bf16[4,4,64,128]{3,2,1,0:T(8,128)(2,1)S(1)}, bf16[4,4,64,128]{3,2,1,0:T(8,128)(2,1)S(1)}, u32[]{:S(2)}, u32[]{:S(2)}) %collective-permute-start.7) | collective-permute-done | bytes 262176 | tf_op jit(solution)/shard_map/ppermute | solution.py:32
  28.0 0.6 collective-permute-done.8.refs_2_
  28.6 0.7 precondition.3.refs_1_
  29.7 3.7 %collective-permute-start.11 = (f32[128,128]{1,0:T(8,128)S(1)}, f32[128,128]{1,0:T(8,128)S(1)}, u32[]{:S(2)}, u32[]{:S(2)}) collective-permute-start(f32[128,128]{1,0:T(8,128)S(1)} %precondition.4), channel_id=1, source_target_pairs={{0,1},{1,0},{2,3},{3,2},{4,5},{5,4},{6,7},{7,6},{8,9},{9,8},{10,11... | collective-permute-start | bytes 196616 | tf_op jit(solution)/shard_map/ppermute | solution.py:32
  33.4 0.9 %collective-permute-done.11 = f32[128,128]{1,0:T(8,128)S(1)} collective-permute-done((f32[128,128]{1,0:T(8,128)S(1)}, f32[128,128]{1,0:T(8,128)S(1)}, u32[]{:S(2)}, u32[]{:S(2)}) %collective-permute-start.11) | collective-permute-done | bytes 65568 | tf_op jit(solution)/shard_map/ppermute | solution.py:32
  34.3 2.0 %collective-permute-start.12 = (bf16[128,128]{1,0:T(8,128)(2,1)S(1)}, bf16[128,128]{1,0:T(8,128)(2,1)S(1)}, u32[]{:S(2)}, u32[]{:S(2)}) collective-permute-start(bf16[128,128]{1,0:T(8,128)(2,1)S(1)} %add_convert_fusion.1), channel_id=1, source_target_pairs={{0,0},{1,32},{2,2},{3,34},{4,4},{5,36},{6,6},{7,38},{8,8},{9,40},{... | collective-permute-start | bytes 98312 | tf_op jit(solution)/shard_map/ppermute | solution.py:32
  36.3 3.5 %collective-permute-start.19 = (bf16[128,128]{1,0:T(8,128)(2,1)S(1)}, bf16[128,128]{1,0:T(8,128)(2,1)S(1)}, u32[]{:S(2)}, u32[]{:S(2)}) collective-permute-start(bf16[128,128]{1,0:T(8,128)(2,1)S(1)} %add_convert_fusion.1), channel_id=1, source_target_pairs={{0,192},{1,224},{2,194},{3,226},{4,196},{5,228},{6,198},{7,230},{8... | collective-permute-start | bytes 98312 | tf_op jit(solution)/shard_map/ppermute | solution.py:32
  39.8 2.5 %collective-permute-start.18 = (bf16[128,128]{1,0:T(8,128)(2,1)S(1)}, bf16[128,128]{1,0:T(8,128)(2,1)S(1)}, u32[]{:S(2)}, u32[]{:S(2)}) collective-permute-start(bf16[128,128]{1,0:T(8,128)(2,1)S(1)} %add_convert_fusion.1), channel_id=1, source_target_pairs={{0,128},{1,160},{2,130},{3,162},{4,132},{5,164},{6,134},{7,166},{8... | collective-permute-start | bytes 98312 | tf_op jit(solution)/shard_map/ppermute | solution.py:32
  42.3 1.7 %collective-permute-start.17 = (bf16[128,128]{1,0:T(8,128)(2,1)S(1)}, bf16[128,128]{1,0:T(8,128)(2,1)S(1)}, u32[]{:S(2)}, u32[]{:S(2)}) collective-permute-start(bf16[128,128]{1,0:T(8,128)(2,1)S(1)} %add_convert_fusion.1), channel_id=1, source_target_pairs={{0,64},{1,96},{2,66},{3,98},{4,68},{5,100},{6,70},{7,102},{8,72},{... | collective-permute-start | bytes 98312 | tf_op jit(solution)/shard_map/ppermute | solution.py:32
  44.0 2.9 %collective-permute-start.13 = (bf16[2,4,4,64,128]{4,3,2,1,0:T(8,128)(2,1)S(1)}, bf16[2,4,4,64,128]{4,3,2,1,0:T(8,128)(2,1)S(1)}, u32[]{:S(2)}, u32[]{:S(2)}) collective-permute-start(bf16[2,4,4,64,128]{4,3,2,1,0:T(8,128)(2,1)S(1)} %pad_maximum_fusion), channel_id=1, source_target_pairs={{0,6},{1,25},{2,4},{3,27},{4,2},{5,29},{6,0},{7,31},{8,14},{9,17},... | collective-permute-start | bytes 1572872 | tf_op jit(solution)/shard_map/ppermute | solution.py:32
  47.4 1.6 %collective-permute-start.22 = (bf16[2,256,128]{2,1,0:T(8,128)(2,1)S(1)}, bf16[2,256,128]{2,1,0:T(8,128)(2,1)S(1)}, u32[]{:S(2)}, u32[]{:S(2)}) collective-permute-start(bf16[2,256,128]{2,1,0:T(8,128)(2,1)S(1)} %bitcast.58), channel_id=1, source_target_pairs={{0,16},{1,5},{2,18},{3,7},{4,20},{5,1},{6,22},{7,3},{8,24},{9,13},... | collective-permute-start | bytes 393224 | tf_op jit(solution)/shard_map/ppermute | solution.py:32
  49.0 2.2 %collective-permute-start.21 = (bf16[2,256,128]{2,1,0:T(8,128)(2,1)S(1)}, bf16[2,256,128]{2,1,0:T(8,128)(2,1)S(1)}, u32[]{:S(2)}, u32[]{:S(2)}) collective-permute-start(bf16[2,256,128]{2,1,0:T(8,128)(2,1)S(1)} %bitcast.59), channel_id=1, source_target_pairs={{0,24},{1,7},{2,26},{3,5},{4,28},{5,3},{6,30},{7,1},{8,16},{9,15},... | collective-permute-start | bytes 393224 | tf_op jit(solution)/shard_map/ppermute | solution.py:32
  51.2 3.7 %collective-permute-done.13 = bf16[2,4,4,64,128]{4,3,2,1,0:T(8,128)(2,1)S(1)} collective-permute-done((bf16[2,4,4,64,128]{4,3,2,1,0:T(8,128)(2,1)S(1)}, bf16[2,4,4,64,128]{4,3,2,1,0:T(8,128)(2,1)S(1)}, u32[]{:S(2)}, u32[]{:S(2)}) %collective-permute-start.13) | collective-permute-done | bytes 524320 | tf_op jit(solution)/shard_map/ppermute | solution.py:32
  54.9 0.9 %precondition.5 = f32[128,128]{1,0:T(8,128)S(1)} custom-call(bf16[4,4,64,128]{3,2,1,0:T(8,128)(2,1)S(1)} %get-tuple-element.36.refs_0_, bf16[4,4,64,128]{3,2,1,0:T(8,128)(2,1)S(1)} %get-tuple-element.35.refs_1_, bf16[4,4,64,128]{3,2,1,0:T(8,128)(2,1)S(1)} %get-tuple-element.34.refs_2_, bf16[4,4,64,128]{3,2,1,0:T(8,128)(2,1)S(1)} %get-tuple-element.33.refs_3_, ...), custom_call_target="tpu_custom_call" | custom-call | tf_op jit(solution)/shard_map/precondition/pallas_call | solution.py:193
  56.4 1.7 %collective-permute-start.23 = (bf16[4,2,256,128]{3,2,1,0:T(8,128)(2,1)S(1)}, bf16[4,2,256,128]{3,2,1,0:T(8,128)(2,1)S(1)}, u32[]{:S(2)}, u32[]{:S(2)}) collective-permute-start(bf16[4,2,256,128]{3,2,1,0:T(8,128)(2,1)S(1)} %pad_maximum_fusion.1.piece), channel_id=1, source_target_pairs={{0,4},{1,17},{2,6},{3,19},{4,0},{5,21},{6,2},{7,23},{8,12},{9,25},... | collective-permute-start | bytes 1572872 | tf_op jit(solution)/shard_map/ppermute | solution.py:32
  58.0 2.5 %collective-permute-start.24 = (bf16[4,2,256,128]{3,2,1,0:T(8,128)(2,1)S(1)}, bf16[4,2,256,128]{3,2,1,0:T(8,128)(2,1)S(1)}, u32[]{:S(2)}, u32[]{:S(2)}) collective-permute-start(bf16[4,2,256,128]{3,2,1,0:T(8,128)(2,1)S(1)} %pad_maximum_fusion.1.piece), channel_id=1, source_target_pairs={{0,2},{1,9},{2,0},{3,11},{4,6},{5,13},{6,4},{7,15},{8,10},{9,1},{1... | collective-permute-start | bytes 1572872 | tf_op jit(solution)/shard_map/ppermute | solution.py:32
  60.6 4.9 %collective-permute-start.16 = (bf16[128,128]{1,0:T(8,128)(2,1)S(1)}, bf16[128,128]{1,0:T(8,128)(2,1)S(1)}, u32[]{:S(2)}, u32[]{:S(2)}) collective-permute-start(bf16[128,128]{1,0:T(8,128)(2,1)S(1)} %maximum_select_fusion), channel_id=1, source_target_pairs={{0,128},{1,129},{2,130},{3,131},{4,132},{5,133},{6,134},{7,135},{8... | collective-permute-start | bytes 98312 | tf_op jit(solution)/shard_map/ppermute | solution.py:32
  65.5 1.9 %collective-permute-done.16 = bf16[128,128]{1,0:T(8,128)(2,1)S(1)} collective-permute-done((bf16[128,128]{1,0:T(8,128)(2,1)S(1)}, bf16[128,128]{1,0:T(8,128)(2,1)S(1)}, u32[]{:S(2)}, u32[]{:S(2)}) %collective-permute-start.16) | collective-permute-done | bytes 32800 | tf_op jit(solution)/shard_map/ppermute | solution.py:32
  67.6 2.4 %collective-permute-start.26 = (f32[64,1024]{1,0:T(8,128)S(1)}, f32[64,1024]{1,0:T(8,128)S(1)}, u32[]{:S(2)}, u32[]{:S(2)}) collective-permute-start(f32[64,1024]{1,0:T(8,128)S(1)} %get-tuple-element.25), channel_id=1, source_target_pairs={{0,1},{1,0},{2,3},{3,2},{4,5},{5,4},{6,7},{7,6},{8,9},{9,8},{10,11... | collective-permute-start | bytes 786440 | tf_op jit(solution)/shard_map/ppermute | solution.py:32
  70.4 2.6 %collective-permute-done.24.piece = bf16[4,2,256,128]{3,2,1,0:T(8,128)(2,1)S(1)} collective-permute-done((bf16[4,2,256,128]{3,2,1,0:T(8,128)(2,1)S(1)}, bf16[4,2,256,128]{3,2,1,0:T(8,128)(2,1)S(1)}, u32[]{:S(2)}, u32[]{:S(2)}) %collective-permute-start.24) | collective-permute-done | bytes 524320 | tf_op jit(solution)/shard_map/ppermute | solution.py:32
  74.3 0.6 collective-permute-done.28.refs_6_
  75.5 1.4 %assemble.1 = f32[64,8192]{1,0:T(8,128)} custom-call(f32[64,1024]{1,0:T(8,128)S(1)} %get-tuple-element.21.refs_0_, f32[64,1024]{1,0:T(8,128)S(1)} %get-tuple-element.22.refs_1_, f32[64,1024]{1,0:T(8,128)S(1)} %get-tuple-element.23.refs_2_, f32[64,1024]{1,0:T(8,128)S(1)} %get-tuple-element.24.refs_3_, f32[64,1024]{1,0:T(8,128)S(1)} %collective-permute-done.26.refs_4_, ...), custom_call_target="tpu_custom_call" | custom-call | tf_op jit(solution)/shard_map/assemble/pallas_call | solution.py:227
  (61 shorter events, 4.6 us)
Async XLA Ops:
  0.0 21.9 %copy-start = (bf16[64,8192]{1,0:T(8,128)(2,1)S(1)}, bf16[64,8192]{1,0:T(8,128)(2,1)}, u32[]{:S(2)}) copy-start(bf16[64,8192]{1,0:T(8,128)(2,1)} %param.6) | copy-start | bytes 3145732
  0.8 7.6 %collective-permute-start.2 = (bf16[2,64,128]{2,1,0:T(8,128)(2,1)S(1)}, bf16[2,64,128]{2,1,0:T(8,128)(2,1)S(1)}, u32[]{:S(2)}, u32[]{:S(2)}) collective-permute-start(bf16[2,64,128]{2,1,0:T(8,128)(2,1)S(1)} %get-tuple-element.48), channel_id=1, source_target_pairs={{0,96},{1,97},{2,98},{3,99},{4,100},{5,101},{6,102},{7,103},{8,104... | collective-permute-start | bytes 98312 | tf_op jit(solution)/shard_map/ppermute | solution.py:32
  6.0 4.0 %collective-permute-start.1 = (bf16[2,64,128]{2,1,0:T(8,128)(2,1)S(1)}, bf16[2,64,128]{2,1,0:T(8,128)(2,1)S(1)}, u32[]{:S(2)}, u32[]{:S(2)}) collective-permute-start(bf16[2,64,128]{2,1,0:T(8,128)(2,1)S(1)} %get-tuple-element.48), channel_id=1, source_target_pairs={{0,64},{1,65},{2,66},{3,67},{4,68},{5,69},{6,70},{7,71},{8,72},{9,... | collective-permute-start | bytes 98312 | tf_op jit(solution)/shard_map/ppermute | solution.py:32
  6.0 4.0 %collective-permute-start = (bf16[2,64,128]{2,1,0:T(8,128)(2,1)S(1)}, bf16[2,64,128]{2,1,0:T(8,128)(2,1)S(1)}, u32[]{:S(2)}, u32[]{:S(2)}) collective-permute-start(bf16[2,64,128]{2,1,0:T(8,128)(2,1)S(1)} %get-tuple-element.48), channel_id=1, source_target_pairs={{0,32},{1,33},{2,34},{3,35},{4,36},{5,37},{6,38},{7,39},{8,40},{9,... | collective-permute-start | bytes 98312 | tf_op jit(solution)/shard_map/ppermute | solution.py:32
  6.4 15.5 %collective-permute-start.9 = (bf16[64,8192]{1,0:T(8,128)(2,1)}, bf16[64,8192]{1,0:T(8,128)(2,1)S(1)}, u32[]{:S(2)}, u32[]{:S(2)}) collective-permute-start(bf16[64,8192]{1,0:T(8,128)(2,1)} %param.6), channel_id=1, source_target_pairs={{0,1},{1,0},{2,3},{3,2},{4,5},{5,4},{6,7},{7,6},{8,9},{9,8},{10,11... | collective-permute-start | bytes 3145736 | tf_op jit(solution)/shard_map/ppermute | solution.py:32
  8.5 38.5 %collective-permute-start.14 = (bf16[64,8192]{1,0:T(8,128)(2,1)}, bf16[64,8192]{1,0:T(8,128)(2,1)S(1)}, u32[]{:S(2)}, u32[]{:S(2)}) collective-permute-start(bf16[64,8192]{1,0:T(8,128)(2,1)} %param.7), channel_id=1, source_target_pairs={{0,1},{1,0},{2,3},{3,2},{4,5},{5,4},{6,7},{7,6},{8,9},{9,8},{10,11... | collective-permute-start | bytes 3145736 | tf_op jit(solution)/shard_map/ppermute | solution.py:32
  10.1 5.4 %collective-permute-start.5 = (bf16[4,2,64,128]{3,2,0,1:T(8,128)(2,1)S(1)}, bf16[4,2,64,128]{3,2,0,1:T(8,128)(2,1)S(1)}, u32[]{:S(2)}, u32[]{:S(2)}) collective-permute-start(bf16[4,2,64,128]{3,2,0,1:T(8,128)(2,1)S(1)} %pad_maximum_fusion.4), channel_id=1, source_target_pairs={{0,16},{1,5},{2,18},{3,7},{4,20},{5,1},{6,22},{7,3},{8,24},{9,13},... | collective-permute-start | bytes 393224 | tf_op jit(solution)/shard_map/ppermute | solution.py:32
  12.9 5.1 %collective-permute-start.4 = (bf16[4,2,64,128]{3,2,0,1:T(8,128)(2,1)S(1)}, bf16[4,2,64,128]{3,2,0,1:T(8,128)(2,1)S(1)}, u32[]{:S(2)}, u32[]{:S(2)}) collective-permute-start(bf16[4,2,64,128]{3,2,0,1:T(8,128)(2,1)S(1)} %pad_maximum_fusion.4), channel_id=1, source_target_pairs={{0,24},{1,7},{2,26},{3,5},{4,28},{5,3},{6,30},{7,1},{8,16},{9,15},... | collective-permute-start | bytes 393224 | tf_op jit(solution)/shard_map/ppermute | solution.py:32
  13.8 4.2 %collective-permute-start.3 = (bf16[4,2,64,128]{3,2,0,1:T(8,128)(2,1)S(1)}, bf16[4,2,64,128]{3,2,0,1:T(8,128)(2,1)S(1)}, u32[]{:S(2)}, u32[]{:S(2)}) collective-permute-start(bf16[4,2,64,128]{3,2,0,1:T(8,128)(2,1)S(1)} %pad_maximum_fusion.4), channel_id=1, source_target_pairs={{0,8},{1,3},{2,10},{3,1},{4,12},{5,7},{6,14},{7,5},{8,0},{9,11},{1... | collective-permute-start | bytes 393224 | tf_op jit(solution)/shard_map/ppermute | solution.py:32
  18.1 11.3 %collective-permute-start.6 = (bf16[4,4,64,128]{3,2,1,0:T(8,128)(2,1)S(1)}, bf16[4,4,64,128]{3,2,1,0:T(8,128)(2,1)S(1)}, u32[]{:S(2)}, u32[]{:S(2)}) collective-permute-start(bf16[4,4,64,128]{3,2,1,0:T(8,128)(2,1)S(1)} %pad_maximum_fusion.2.refs_0_), channel_id=1, source_target_pairs={{0,4},{1,17},{2,6},{3,19},{4,0},{5,21},{6,2},{7,23},{8,12},{9,25},... | collective-permute-start | bytes 786440 | tf_op jit(solution)/shard_map/ppermute | solution.py:32
  21.1 6.9 %collective-permute-start.7 = (bf16[4,4,64,128]{3,2,1,0:T(8,128)(2,1)S(1)}, bf16[4,4,64,128]{3,2,1,0:T(8,128)(2,1)S(1)}, u32[]{:S(2)}, u32[]{:S(2)}) collective-permute-start(bf16[4,4,64,128]{3,2,1,0:T(8,128)(2,1)S(1)} %pad_maximum_fusion.2.refs_0_), channel_id=1, source_target_pairs={{0,6},{1,25},{2,4},{3,27},{4,2},{5,29},{6,0},{7,31},{8,14},{9,17},... | collective-permute-start | bytes 786440 | tf_op jit(solution)/shard_map/ppermute | solution.py:32
  21.8 6.8 %collective-permute-start.8 = (bf16[4,4,64,128]{3,2,1,0:T(8,128)(2,1)S(1)}, bf16[4,4,64,128]{3,2,1,0:T(8,128)(2,1)S(1)}, u32[]{:S(2)}, u32[]{:S(2)}) collective-permute-start(bf16[4,4,64,128]{3,2,1,0:T(8,128)(2,1)S(1)} %pad_maximum_fusion.2.refs_0_), channel_id=1, source_target_pairs={{0,2},{1,9},{2,0},{3,11},{4,6},{5,13},{6,4},{7,15},{8,10},{9,1},{1... | collective-permute-start | bytes 786440 | tf_op jit(solution)/shard_map/ppermute | solution.py:32
  29.3 17.6 %copy-start.1 = (bf16[64,8192]{1,0:T(8,128)(2,1)S(1)}, bf16[64,8192]{1,0:T(8,128)(2,1)}, u32[]{:S(2)}) copy-start(bf16[64,8192]{1,0:T(8,128)(2,1)} %param.7) | copy-start | bytes 3145732
  29.7 4.6 %collective-permute-start.11 = (f32[128,128]{1,0:T(8,128)S(1)}, f32[128,128]{1,0:T(8,128)S(1)}, u32[]{:S(2)}, u32[]{:S(2)}) collective-permute-start(f32[128,128]{1,0:T(8,128)S(1)} %precondition.4), channel_id=1, source_target_pairs={{0,1},{1,0},{2,3},{3,2},{4,5},{5,4},{6,7},{7,6},{8,9},{9,8},{10,11... | collective-permute-start | bytes 196616 | tf_op jit(solution)/shard_map/ppermute | solution.py:32
  33.4 8.9 %collective-permute-start.10 = (bf16[4,4,64,128]{3,2,1,0:T(8,128)(2,1)S(1)}, bf16[4,4,64,128]{3,2,1,0:T(8,128)(2,1)S(1)}, u32[]{:S(2)}, u32[]{:S(2)}) collective-permute-start(bf16[4,4,64,128]{3,2,1,0:T(8,128)(2,1)S(1)} %pad_maximum_fusion.3), channel_id=1, source_target_pairs={{0,2},{1,9},{2,0},{3,11},{4,6},{5,13},{6,4},{7,15},{8,10},{9,1},{1... | collective-permute-start | bytes 786440 | tf_op jit(solution)/shard_map/ppermute | solution.py:32
  34.3 9.7 %collective-permute-start.12 = (bf16[128,128]{1,0:T(8,128)(2,1)S(1)}, bf16[128,128]{1,0:T(8,128)(2,1)S(1)}, u32[]{:S(2)}, u32[]{:S(2)}) collective-permute-start(bf16[128,128]{1,0:T(8,128)(2,1)S(1)} %add_convert_fusion.1), channel_id=1, source_target_pairs={{0,0},{1,32},{2,2},{3,34},{4,4},{5,36},{6,6},{7,38},{8,8},{9,40},{... | collective-permute-start | bytes 98312 | tf_op jit(solution)/shard_map/ppermute | solution.py:32
  36.3 10.8 %collective-permute-start.19 = (bf16[128,128]{1,0:T(8,128)(2,1)S(1)}, bf16[128,128]{1,0:T(8,128)(2,1)S(1)}, u32[]{:S(2)}, u32[]{:S(2)}) collective-permute-start(bf16[128,128]{1,0:T(8,128)(2,1)S(1)} %add_convert_fusion.1), channel_id=1, source_target_pairs={{0,192},{1,224},{2,194},{3,226},{4,196},{5,228},{6,198},{7,230},{8... | collective-permute-start | bytes 98312 | tf_op jit(solution)/shard_map/ppermute | solution.py:32
  39.8 7.3 %collective-permute-start.18 = (bf16[128,128]{1,0:T(8,128)(2,1)S(1)}, bf16[128,128]{1,0:T(8,128)(2,1)S(1)}, u32[]{:S(2)}, u32[]{:S(2)}) collective-permute-start(bf16[128,128]{1,0:T(8,128)(2,1)S(1)} %add_convert_fusion.1), channel_id=1, source_target_pairs={{0,128},{1,160},{2,130},{3,162},{4,132},{5,164},{6,134},{7,166},{8... | collective-permute-start | bytes 98312 | tf_op jit(solution)/shard_map/ppermute | solution.py:32
  42.3 5.1 %collective-permute-start.17 = (bf16[128,128]{1,0:T(8,128)(2,1)S(1)}, bf16[128,128]{1,0:T(8,128)(2,1)S(1)}, u32[]{:S(2)}, u32[]{:S(2)}) collective-permute-start(bf16[128,128]{1,0:T(8,128)(2,1)S(1)} %add_convert_fusion.1), channel_id=1, source_target_pairs={{0,64},{1,96},{2,66},{3,98},{4,68},{5,100},{6,70},{7,102},{8,72},{... | collective-permute-start | bytes 98312 | tf_op jit(solution)/shard_map/ppermute | solution.py:32
  44.0 10.9 %collective-permute-start.13 = (bf16[2,4,4,64,128]{4,3,2,1,0:T(8,128)(2,1)S(1)}, bf16[2,4,4,64,128]{4,3,2,1,0:T(8,128)(2,1)S(1)}, u32[]{:S(2)}, u32[]{:S(2)}) collective-permute-start(bf16[2,4,4,64,128]{4,3,2,1,0:T(8,128)(2,1)S(1)} %pad_maximum_fusion), channel_id=1, source_target_pairs={{0,6},{1,25},{2,4},{3,27},{4,2},{5,29},{6,0},{7,31},{8,14},{9,17},... | collective-permute-start | bytes 1572872 | tf_op jit(solution)/shard_map/ppermute | solution.py:32
  47.4 8.8 %collective-permute-start.22 = (bf16[2,256,128]{2,1,0:T(8,128)(2,1)S(1)}, bf16[2,256,128]{2,1,0:T(8,128)(2,1)S(1)}, u32[]{:S(2)}, u32[]{:S(2)}) collective-permute-start(bf16[2,256,128]{2,1,0:T(8,128)(2,1)S(1)} %bitcast.58), channel_id=1, source_target_pairs={{0,16},{1,5},{2,18},{3,7},{4,20},{5,1},{6,22},{7,3},{8,24},{9,13},... | collective-permute-start | bytes 393224 | tf_op jit(solution)/shard_map/ppermute | solution.py:32
  49.0 7.2 %collective-permute-start.21 = (bf16[2,256,128]{2,1,0:T(8,128)(2,1)S(1)}, bf16[2,256,128]{2,1,0:T(8,128)(2,1)S(1)}, u32[]{:S(2)}, u32[]{:S(2)}) collective-permute-start(bf16[2,256,128]{2,1,0:T(8,128)(2,1)S(1)} %bitcast.59), channel_id=1, source_target_pairs={{0,24},{1,7},{2,26},{3,5},{4,28},{5,3},{6,30},{7,1},{8,16},{9,15},... | collective-permute-start | bytes 393224 | tf_op jit(solution)/shard_map/ppermute | solution.py:32
  51.2 5.1 %collective-permute-start.20 = (bf16[2,256,128]{2,1,0:T(8,128)(2,1)S(1)}, bf16[2,256,128]{2,1,0:T(8,128)(2,1)S(1)}, u32[]{:S(2)}, u32[]{:S(2)}) collective-permute-start(bf16[2,256,128]{2,1,0:T(8,128)(2,1)S(1)} %bitcast.60), channel_id=1, source_target_pairs={{0,8},{1,3},{2,10},{3,1},{4,12},{5,7},{6,14},{7,5},{8,0},{9,11},{1... | collective-permute-start | bytes 393224 | tf_op jit(solution)/shard_map/ppermute | solution.py:32
  55.8 4.7 %collective-permute-start.15 = (f32[128,128]{1,0:T(8,128)S(1)}, f32[128,128]{1,0:T(8,128)S(1)}, u32[]{:S(2)}, u32[]{:S(2)}) collective-permute-start(f32[128,128]{1,0:T(8,128)S(1)} %precondition.5), channel_id=1, source_target_pairs={{0,1},{1,0},{2,3},{3,2},{4,5},{5,4},{6,7},{7,6},{8,9},{9,8},{10,11... | collective-permute-start | bytes 196616 | tf_op jit(solution)/shard_map/ppermute | solution.py:32
  56.4 13.7 %collective-permute-start.23 = (bf16[4,2,256,128]{3,2,1,0:T(8,128)(2,1)S(1)}, bf16[4,2,256,128]{3,2,1,0:T(8,128)(2,1)S(1)}, u32[]{:S(2)}, u32[]{:S(2)}) collective-permute-start(bf16[4,2,256,128]{3,2,1,0:T(8,128)(2,1)S(1)} %pad_maximum_fusion.1.piece), channel_id=1, source_target_pairs={{0,4},{1,17},{2,6},{3,19},{4,0},{5,21},{6,2},{7,23},{8,12},{9,25},... | collective-permute-start | bytes 1572872 | tf_op jit(solution)/shard_map/ppermute | solution.py:32
  58.0 15.1 %collective-permute-start.24 = (bf16[4,2,256,128]{3,2,1,0:T(8,128)(2,1)S(1)}, bf16[4,2,256,128]{3,2,1,0:T(8,128)(2,1)S(1)}, u32[]{:S(2)}, u32[]{:S(2)}) collective-permute-start(bf16[4,2,256,128]{3,2,1,0:T(8,128)(2,1)S(1)} %pad_maximum_fusion.1.piece), channel_id=1, source_target_pairs={{0,2},{1,9},{2,0},{3,11},{4,6},{5,13},{6,4},{7,15},{8,10},{9,1},{1... | collective-permute-start | bytes 1572872 | tf_op jit(solution)/shard_map/ppermute | solution.py:32
  60.6 13.1 %collective-permute-start.25 = (bf16[4,2,256,128]{3,2,1,0:T(8,128)(2,1)S(1)}, bf16[4,2,256,128]{3,2,1,0:T(8,128)(2,1)S(1)}, u32[]{:S(2)}, u32[]{:S(2)}) collective-permute-start(bf16[4,2,256,128]{3,2,1,0:T(8,128)(2,1)S(1)} %pad_maximum_fusion.1.piece), channel_id=1, source_target_pairs={{0,6},{1,25},{2,4},{3,27},{4,2},{5,29},{6,0},{7,31},{8,14},{9,17},... | collective-permute-start | bytes 1572872 | tf_op jit(solution)/shard_map/ppermute | solution.py:32
  60.6 6.8 %collective-permute-start.16 = (bf16[128,128]{1,0:T(8,128)(2,1)S(1)}, bf16[128,128]{1,0:T(8,128)(2,1)S(1)}, u32[]{:S(2)}, u32[]{:S(2)}) collective-permute-start(bf16[128,128]{1,0:T(8,128)(2,1)S(1)} %maximum_select_fusion), channel_id=1, source_target_pairs={{0,128},{1,129},{2,130},{3,131},{4,132},{5,133},{6,134},{7,135},{8... | collective-permute-start | bytes 98312 | tf_op jit(solution)/shard_map/ppermute | solution.py:32
  67.6 6.7 %collective-permute-start.26 = (f32[64,1024]{1,0:T(8,128)S(1)}, f32[64,1024]{1,0:T(8,128)S(1)}, u32[]{:S(2)}, u32[]{:S(2)}) collective-permute-start(f32[64,1024]{1,0:T(8,128)S(1)} %get-tuple-element.25), channel_id=1, source_target_pairs={{0,1},{1,0},{2,3},{3,2},{4,5},{5,4},{6,7},{7,6},{8,9},{9,8},{10,11... | collective-permute-start | bytes 786440 | tf_op jit(solution)/shard_map/ppermute | solution.py:32
  70.3 4.0 %collective-permute-start.27 = (f32[64,1024]{1,0:T(8,128)S(1)}, f32[64,1024]{1,0:T(8,128)S(1)}, u32[]{:S(2)}, u32[]{:S(2)}) collective-permute-start(f32[64,1024]{1,0:T(8,128)S(1)} %get-tuple-element.26), channel_id=1, source_target_pairs={{0,1},{1,0},{2,3},{3,2},{4,5},{5,4},{6,7},{7,6},{8,9},{9,8},{10,11... | collective-permute-start | bytes 786440 | tf_op jit(solution)/shard_map/ppermute | solution.py:32
  73.3 1.6 %collective-permute-start.28 = (f32[64,1024]{1,0:T(8,128)S(1)}, f32[64,1024]{1,0:T(8,128)S(1)}, u32[]{:S(2)}, u32[]{:S(2)}) collective-permute-start(f32[64,1024]{1,0:T(8,128)S(1)} %get-tuple-element.27), channel_id=1, source_target_pairs={{0,1},{1,0},{2,3},{3,2},{4,5},{5,4},{6,7},{7,6},{8,9},{9,8},{10,11... | collective-permute-start | bytes 786440 | tf_op jit(solution)/shard_map/ppermute | solution.py:32
  73.9 1.6 %collective-permute-start.29 = (f32[64,1024]{1,0:T(8,128)S(1)}, f32[64,1024]{1,0:T(8,128)S(1)}, u32[]{:S(2)}, u32[]{:S(2)}) collective-permute-start(f32[64,1024]{1,0:T(8,128)S(1)} %get-tuple-element.28), channel_id=1, source_target_pairs={{0,1},{1,0},{2,3},{3,2},{4,5},{5,4},{6,7},{7,6},{8,9},{9,8},{10,11... | collective-permute-start | bytes 786440 | tf_op jit(solution)/shard_map/ppermute | solution.py:32

commit v17 on v15

--- a/solution.py
+++ b/solution.py
@@ -207,16 +207,16 @@
 
     there = [to_parity(act, j, 1) for j in (0, 1)]
     here = [to_parity(act, j, 0) for j in (0, 1)]
-    half, there[0] = lax.optimization_barrier((half, there[0]))
+    half, here[0] = lax.optimization_barrier((half, here[0]))
     rest = second_turn(half, 3)
-    grad_pieces = half[0], half[1], rest[1], rest[0]
     pair = jnp.stack([*there, *here]).reshape(2, 2, 128, 128)
     pair = jnp.swapaxes(pair, 0, 1).reshape(2, 256, 128)
+    plane = stacked(first_turn, pair, ORDER_B)
+    plane, rest = lax.optimization_barrier((plane, rest))
+    grad_pieces = half[0], half[1], rest[1], rest[0]
     part = partial((0, 1, 2, 3), grad_pieces, [], grad_rows, False)
-    plane = stacked(first_turn, pair, ORDER_B)
     grad = (part + swap_cores(part)).astype(bf16)
     grad = jnp.where(first, grad, jnp.concatenate([grad[64:], grad[:64]], axis=0))
-    plane, grad = lax.optimization_barrier((plane, grad))
     grad = jnp.concatenate([swap_reps(grad), grad], axis=1)
 
     made = [

time: 81.3 us -> 81.1 us (level)
  transfers between devices with their start and end apart: 30 -> 30, of which waited for: 16 -> 17; matrix products, arithmetic and copies ran while one was open for 1% -> 1% of each run, Pallas kernels for 4% -> 2%
where the time goes in v17:
time: 81.1 us; the launch traced here: 80.9 us
  starting transfers between devices  47.6 us (59%)
  waiting for transfers between devices  27 us (33%)
  Pallas kernels  4.27 us (5%)
  other arithmetic  1.38 us (2%)
    ppermute x30, starting transfers between devices, send(): return lax.ppermute(value, AXES, pairs)  47.6 us
    ppermute x30, waiting for transfers between devices, send(): return lax.ppermute(value, AXES, pairs)  27 us
    pallas_call x3, Pallas kernels, partial(): call(functools.partial(precondition, turns, flip), 'precondition', shape(...  1.91 us
  transfers between devices with their start and end apart: 30, of which 17 were waited for; matrix products, arithmetic and copies ran while one was open for 1% of the time, Pallas kernels for 2%

profile of v17, /device:TPU:1, one launch (start us, length us, event | category | flops | bytes accessed | tf_op | source)
XLA Modules:
  0.0 80.9 jit_solution(1069482949787268496)
XLA Ops:
  0.0 0.8 %fusion = (bf16[1,2,64,128]{3,2,0,1:T(8,128)(2,1)S(1)}, bf16[2,64,128]{2,1,0:T(8,128)(2,1)S(1)}) fusion(bf16[1,64,128]{2,1,0:T(8,128)(2,1)} %bitcast.73, bf16[1,64,128]{2,1,0:T(8,128)(2,1)} %bitcast.74), kind=kLoop, calls=%fused_computation.27 | loop fusion | flops 16384 | bytes 98304 | tf_op jit(solution)/shard_map/stack | solution.py:63
  0.8 5.2 %collective-permute-start.2 = (bf16[2,64,128]{2,1,0:T(8,128)(2,1)S(1)}, bf16[2,64,128]{2,1,0:T(8,128)(2,1)S(1)}, u32[]{:S(2)}, u32[]{:S(2)}) collective-permute-start(bf16[2,64,128]{2,1,0:T(8,128)(2,1)S(1)} %get-tuple-element.52), channel_id=1, source_target_pairs={{0,96},{1,97},{2,98},{3,99},{4,100},{5,101},{6,102},{7,103},{8,104... | collective-permute-start | bytes 98312 | tf_op jit(solution)/shard_map/ppermute | solution.py:32
  6.4 2.1 %collective-permute-start.9 = (bf16[64,8192]{1,0:T(8,128)(2,1)}, bf16[64,8192]{1,0:T(8,128)(2,1)S(1)}, u32[]{:S(2)}, u32[]{:S(2)}) collective-permute-start(bf16[64,8192]{1,0:T(8,128)(2,1)} %param.6), channel_id=1, source_target_pairs={{0,1},{1,0},{2,3},{3,2},{4,5},{5,4},{6,7},{7,6},{8,9},{9,8},{10,11... | collective-permute-start | bytes 3145736 | tf_op jit(solution)/shard_map/ppermute | solution.py:32
  8.5 1.6 %collective-permute-done = bf16[2,64,128]{2,1,0:T(8,128)(2,1)S(1)} collective-permute-done((bf16[2,64,128]{2,1,0:T(8,128)(2,1)S(1)}, bf16[2,64,128]{2,1,0:T(8,128)(2,1)S(1)}, u32[]{:S(2)}, u32[]{:S(2)}) %collective-permute-start) | collective-permute-done | bytes 32800 | tf_op jit(solution)/shard_map/ppermute | solution.py:32
  10.1 2.8 %collective-permute-start.3 = (bf16[4,2,64,128]{3,2,0,1:T(8,128)(2,1)S(1)}, bf16[4,2,64,128]{3,2,0,1:T(8,128)(2,1)S(1)}, u32[]{:S(2)}, u32[]{:S(2)}) collective-permute-start(bf16[4,2,64,128]{3,2,0,1:T(8,128)(2,1)S(1)} %pad_maximum_fusion.4), channel_id=1, source_target_pairs={{0,16},{1,5},{2,18},{3,7},{4,20},{5,1},{6,22},{7,3},{8,24},{9,13},... | collective-permute-start | bytes 393224 | tf_op jit(solution)/shard_map/ppermute | solution.py:32
  13.8 1.7 %collective-permute-done.3 = bf16[4,2,64,128]{3,2,0,1:T(8,128)(2,1)S(1)} collective-permute-done((bf16[4,2,64,128]{3,2,0,1:T(8,128)(2,1)S(1)}, bf16[4,2,64,128]{3,2,0,1:T(8,128)(2,1)S(1)}, u32[]{:S(2)}, u32[]{:S(2)}) %collective-permute-start.3) | collective-permute-done | bytes 131104 | tf_op jit(solution)/shard_map/ppermute | solution.py:32
  15.5 1.8 %collective-permute-done.4 = bf16[4,2,64,128]{3,2,0,1:T(8,128)(2,1)S(1)} collective-permute-done((bf16[4,2,64,128]{3,2,0,1:T(8,128)(2,1)S(1)}, bf16[4,2,64,128]{3,2,0,1:T(8,128)(2,1)S(1)}, u32[]{:S(2)}, u32[]{:S(2)}) %collective-permute-start.4) | collective-permute-done | bytes 131104 | tf_op jit(solution)/shard_map/ppermute | solution.py:32
  17.3 1.0 %collective-permute-done.5 = bf16[4,2,64,128]{3,2,0,1:T(8,128)(2,1)S(1)} collective-permute-done((bf16[4,2,64,128]{3,2,0,1:T(8,128)(2,1)S(1)}, bf16[4,2,64,128]{3,2,0,1:T(8,128)(2,1)S(1)}, u32[]{:S(2)}, u32[]{:S(2)}) %collective-permute-start.5) | collective-permute-done | bytes 131104 | tf_op jit(solution)/shard_map/ppermute | solution.py:32
  18.3 3.0 %collective-permute-start.7 = (bf16[4,4,64,128]{3,2,1,0:T(8,128)(2,1)S(1)}, bf16[4,4,64,128]{3,2,1,0:T(8,128)(2,1)S(1)}, u32[]{:S(2)}, u32[]{:S(2)}) collective-permute-start(bf16[4,4,64,128]{3,2,1,0:T(8,128)(2,1)S(1)} %pad_maximum_fusion.2.refs_0_), channel_id=1, source_target_pairs={{0,4},{1,17},{2,6},{3,19},{4,0},{5,21},{6,2},{7,23},{8,12},{9,25},... | collective-permute-start | bytes 786440 | tf_op jit(solution)/shard_map/ppermute | solution.py:32
  22.3 2.8 %collective-permute-done.7.refs_1_ = bf16[4,4,64,128]{3,2,1,0:T(8,128)(2,1)S(1)} collective-permute-done((bf16[4,4,64,128]{3,2,1,0:T(8,128)(2,1)S(1)}, bf16[4,4,64,128]{3,2,1,0:T(8,128)(2,1)S(1)}, u32[]{:S(2)}, u32[]{:S(2)}) %collective-permute-start.7) | collective-permute-done | bytes 262176 | tf_op jit(solution)/shard_map/ppermute | solution.py:32
  25.1 3.1 %collective-permute-done.8.refs_2_ = bf16[4,4,64,128]{3,2,1,0:T(8,128)(2,1)S(1)} collective-permute-done((bf16[4,4,64,128]{3,2,1,0:T(8,128)(2,1)S(1)}, bf16[4,4,64,128]{3,2,1,0:T(8,128)(2,1)S(1)}, u32[]{:S(2)}, u32[]{:S(2)}) %collective-permute-start.8) | collective-permute-done | bytes 262176 | tf_op jit(solution)/shard_map/ppermute | solution.py:32
  29.3 4.7 %collective-permute-start.11 = (f32[128,128]{1,0:T(8,128)S(1)}, f32[128,128]{1,0:T(8,128)S(1)}, u32[]{:S(2)}, u32[]{:S(2)}) collective-permute-start(f32[128,128]{1,0:T(8,128)S(1)} %precondition.4), channel_id=1, source_target_pairs={{0,1},{1,0},{2,3},{3,2},{4,5},{5,4},{6,7},{7,6},{8,9},{9,8},{10,11... | collective-permute-start | bytes 196616 | tf_op jit(solution)/shard_map/ppermute | solution.py:32
  34.0 0.9 %collective-permute-done.11 = f32[128,128]{1,0:T(8,128)S(1)} collective-permute-done((f32[128,128]{1,0:T(8,128)S(1)}, f32[128,128]{1,0:T(8,128)S(1)}, u32[]{:S(2)}, u32[]{:S(2)}) %collective-permute-start.11) | collective-permute-done | bytes 65568 | tf_op jit(solution)/shard_map/ppermute | solution.py:32
  34.9 2.0 %collective-permute-start.12 = (bf16[128,128]{1,0:T(8,128)(2,1)S(1)}, bf16[128,128]{1,0:T(8,128)(2,1)S(1)}, u32[]{:S(2)}, u32[]{:S(2)}) collective-permute-start(bf16[128,128]{1,0:T(8,128)(2,1)S(1)} %add_convert_fusion.1), channel_id=1, source_target_pairs={{0,0},{1,32},{2,2},{3,34},{4,4},{5,36},{6,6},{7,38},{8,8},{9,40},{... | collective-permute-start | bytes 98312 | tf_op jit(solution)/shard_map/ppermute | solution.py:32
  36.9 7.7 %collective-permute-start.13 = (bf16[128,128]{1,0:T(8,128)(2,1)S(1)}, bf16[128,128]{1,0:T(8,128)(2,1)S(1)}, u32[]{:S(2)}, u32[]{:S(2)}) collective-permute-start(bf16[128,128]{1,0:T(8,128)(2,1)S(1)} %add_convert_fusion.1), channel_id=1, source_target_pairs={{0,128},{1,160},{2,130},{3,162},{4,132},{5,164},{6,134},{7,166},{8... | collective-permute-start | bytes 98312 | tf_op jit(solution)/shard_map/ppermute | solution.py:32
  44.6 0.8 %collective-permute-start.14 = (bf16[128,128]{1,0:T(8,128)(2,1)S(1)}, bf16[128,128]{1,0:T(8,128)(2,1)S(1)}, u32[]{:S(2)}, u32[]{:S(2)}) collective-permute-start(bf16[128,128]{1,0:T(8,128)(2,1)S(1)} %add_convert_fusion.1), channel_id=1, source_target_pairs={{0,192},{1,224},{2,194},{3,226},{4,196},{5,228},{6,198},{7,230},{8... | collective-permute-start | bytes 98312 | tf_op jit(solution)/shard_map/ppermute | solution.py:32
  45.4 1.7 %collective-permute-start.15 = (bf16[128,128]{1,0:T(8,128)(2,1)S(1)}, bf16[128,128]{1,0:T(8,128)(2,1)S(1)}, u32[]{:S(2)}, u32[]{:S(2)}) collective-permute-start(bf16[128,128]{1,0:T(8,128)(2,1)S(1)} %add_convert_fusion.1), channel_id=1, source_target_pairs={{0,64},{1,96},{2,66},{3,98},{4,68},{5,100},{6,70},{7,102},{8,72},{... | collective-permute-start | bytes 98312 | tf_op jit(solution)/shard_map/ppermute | solution.py:32
  47.4 1.1 %collective-permute-done.14 = bf16[128,128]{1,0:T(8,128)(2,1)S(1)} collective-permute-done((bf16[128,128]{1,0:T(8,128)(2,1)S(1)}, bf16[128,128]{1,0:T(8,128)(2,1)S(1)}, u32[]{:S(2)}, u32[]{:S(2)}) %collective-permute-start.14) | collective-permute-done | bytes 32800 | tf_op jit(solution)/shard_map/ppermute | solution.py:32
  48.5 2.1 %collective-permute-done.15 = bf16[128,128]{1,0:T(8,128)(2,1)S(1)} collective-permute-done((bf16[128,128]{1,0:T(8,128)(2,1)S(1)}, bf16[128,128]{1,0:T(8,128)(2,1)S(1)}, u32[]{:S(2)}, u32[]{:S(2)}) %collective-permute-start.15) | collective-permute-done | bytes 32800 | tf_op jit(solution)/shard_map/ppermute | solution.py:32
  50.7 1.5 %collective-permute-start.16 = (bf16[2,256,128]{2,1,0:T(8,128)(2,1)S(1)}, bf16[2,256,128]{2,1,0:T(8,128)(2,1)S(1)}, u32[]{:S(2)}, u32[]{:S(2)}) collective-permute-start(bf16[2,256,128]{2,1,0:T(8,128)(2,1)S(1)} %bitcast.58), channel_id=1, source_target_pairs={{0,16},{1,5},{2,18},{3,7},{4,20},{5,1},{6,22},{7,3},{8,24},{9,13},... | collective-permute-start | bytes 393224 | tf_op jit(solution)/shard_map/ppermute | solution.py:32
  52.2 1.5 %collective-permute-start.17 = (bf16[2,256,128]{2,1,0:T(8,128)(2,1)S(1)}, bf16[2,256,128]{2,1,0:T(8,128)(2,1)S(1)}, u32[]{:S(2)}, u32[]{:S(2)}) collective-permute-start(bf16[2,256,128]{2,1,0:T(8,128)(2,1)S(1)} %bitcast.59), channel_id=1, source_target_pairs={{0,8},{1,3},{2,10},{3,1},{4,12},{5,7},{6,14},{7,5},{8,0},{9,11},{1... | collective-permute-start | bytes 393224 | tf_op jit(solution)/shard_map/ppermute | solution.py:32
  54.3 2.1 %collective-permute-done.16 = bf16[2,256,128]{2,1,0:T(8,128)(2,1)S(1)} collective-permute-done((bf16[2,256,128]{2,1,0:T(8,128)(2,1)S(1)}, bf16[2,256,128]{2,1,0:T(8,128)(2,1)S(1)}, u32[]{:S(2)}, u32[]{:S(2)}) %collective-permute-start.16) | collective-permute-done | bytes 131104 | tf_op jit(solution)/shard_map/ppermute | solution.py:32
  56.4 1.5 %collective-permute-done.17 = bf16[2,256,128]{2,1,0:T(8,128)(2,1)S(1)} collective-permute-done((bf16[2,256,128]{2,1,0:T(8,128)(2,1)S(1)}, bf16[2,256,128]{2,1,0:T(8,128)(2,1)S(1)}, u32[]{:S(2)}, u32[]{:S(2)}) %collective-permute-start.17) | collective-permute-done | bytes 131104 | tf_op jit(solution)/shard_map/ppermute | solution.py:32
  57.8 1.2 %collective-permute-done.18 = bf16[2,256,128]{2,1,0:T(8,128)(2,1)S(1)} collective-permute-done((bf16[2,256,128]{2,1,0:T(8,128)(2,1)S(1)}, bf16[2,256,128]{2,1,0:T(8,128)(2,1)S(1)}, u32[]{:S(2)}, u32[]{:S(2)}) %collective-permute-start.18) | collective-permute-done | bytes 131104 | tf_op jit(solution)/shard_map/ppermute | solution.py:32
  59.3 0.9 %precondition.5 = f32[128,128]{1,0:T(8,128)S(1)} custom-call(bf16[4,4,64,128]{3,2,1,0:T(8,128)(2,1)S(1)} %get-tuple-element.40.refs_0_, bf16[4,4,64,128]{3,2,1,0:T(8,128)(2,1)S(1)} %get-tuple-element.39.refs_1_, bf16[4,4,64,128]{3,2,1,0:T(8,128)(2,1)S(1)} %get-tuple-element.38.refs_2_, bf16[4,4,64,128]{3,2,1,0:T(8,128)(2,1)S(1)} %get-tuple-element.37.refs_3_, ...), custom_call_target="tpu_custom_call" | custom-call | tf_op jit(solution)/shard_map/precondition/pallas_call | solution.py:193
  60.8 1.8 %collective-permute-start.24 = (bf16[4,2,256,128]{3,2,1,0:T(8,128)(2,1)S(1)}, bf16[4,2,256,128]{3,2,1,0:T(8,128)(2,1)S(1)}, u32[]{:S(2)}, u32[]{:S(2)}) collective-permute-start(bf16[4,2,256,128]{3,2,1,0:T(8,128)(2,1)S(1)} %pad_maximum_fusion.1.piece), channel_id=1, source_target_pairs={{0,6},{1,25},{2,4},{3,27},{4,2},{5,29},{6,0},{7,31},{8,14},{9,17},... | collective-permute-start | bytes 1572872 | tf_op jit(solution)/shard_map/ppermute | solution.py:32
  63.3 4.5 %collective-permute-start.22 = (bf16[128,128]{1,0:T(8,128)(2,1)S(1)}, bf16[128,128]{1,0:T(8,128)(2,1)S(1)}, u32[]{:S(2)}, u32[]{:S(2)}) collective-permute-start(bf16[128,128]{1,0:T(8,128)(2,1)S(1)} %maximum_select_fusion), channel_id=1, source_target_pairs={{0,128},{1,129},{2,130},{3,131},{4,132},{5,133},{6,134},{7,135},{8... | collective-permute-start | bytes 98312 | tf_op jit(solution)/shard_map/ppermute | solution.py:32
  67.8 2.3 %collective-permute-done.22 = bf16[128,128]{1,0:T(8,128)(2,1)S(1)} collective-permute-done((bf16[128,128]{1,0:T(8,128)(2,1)S(1)}, bf16[128,128]{1,0:T(8,128)(2,1)S(1)}, u32[]{:S(2)}, u32[]{:S(2)}) %collective-permute-start.22) | collective-permute-done | bytes 32800 | tf_op jit(solution)/shard_map/ppermute | solution.py:32
  70.3 3.0 %collective-permute-start.26 = (f32[64,1024]{1,0:T(8,128)S(1)}, f32[64,1024]{1,0:T(8,128)S(1)}, u32[]{:S(2)}, u32[]{:S(2)}) collective-permute-start(f32[64,1024]{1,0:T(8,128)S(1)} %get-tuple-element.29), channel_id=1, source_target_pairs={{0,1},{1,0},{2,3},{3,2},{4,5},{5,4},{6,7},{7,6},{8,9},{9,8},{10,11... | collective-permute-start | bytes 786440 | tf_op jit(solution)/shard_map/ppermute | solution.py:32
  73.6 2.3 %collective-permute-done.24.piece = bf16[4,2,256,128]{3,2,1,0:T(8,128)(2,1)S(1)} collective-permute-done((bf16[4,2,256,128]{3,2,1,0:T(8,128)(2,1)S(1)}, bf16[4,2,256,128]{3,2,1,0:T(8,128)(2,1)S(1)}, u32[]{:S(2)}, u32[]{:S(2)}) %collective-permute-start.24) | collective-permute-done | bytes 524320 | tf_op jit(solution)/shard_map/ppermute | solution.py:32
  76.2 1.3 %collective-permute-start.28 = (f32[64,1024]{1,0:T(8,128)S(1)}, f32[64,1024]{1,0:T(8,128)S(1)}, u32[]{:S(2)}, u32[]{:S(2)}) collective-permute-start(f32[64,1024]{1,0:T(8,128)S(1)} %get-tuple-element.31), channel_id=1, source_target_pairs={{0,1},{1,0},{2,3},{3,2},{4,5},{5,4},{6,7},{7,6},{8,9},{9,8},{10,11... | collective-permute-start | bytes 786440 | tf_op jit(solution)/shard_map/ppermute | solution.py:32
  79.3 1.4 %assemble.1 = f32[64,8192]{1,0:T(8,128)} custom-call(f32[64,1024]{1,0:T(8,128)S(1)} %get-tuple-element.25.refs_0_, f32[64,1024]{1,0:T(8,128)S(1)} %get-tuple-element.26.refs_1_, f32[64,1024]{1,0:T(8,128)S(1)} %get-tuple-element.27.refs_2_, f32[64,1024]{1,0:T(8,128)S(1)} %get-tuple-element.28.refs_3_, f32[64,1024]{1,0:T(8,128)S(1)} %collective-permute-done.26.refs_4_, ...), custom_call_target="tpu_custom_call" | custom-call | tf_op jit(solution)/shard_map/assemble/pallas_call | solution.py:228
  (61 shorter events, 8.4 us)
Async XLA Ops:
  0.0 22.1 %copy-start = (bf16[64,8192]{1,0:T(8,128)(2,1)S(1)}, bf16[64,8192]{1,0:T(8,128)(2,1)}, u32[]{:S(2)}) copy-start(bf16[64,8192]{1,0:T(8,128)(2,1)} %param.6) | copy-start | bytes 3145732
  0.8 7.6 %collective-permute-start.2 = (bf16[2,64,128]{2,1,0:T(8,128)(2,1)S(1)}, bf16[2,64,128]{2,1,0:T(8,128)(2,1)S(1)}, u32[]{:S(2)}, u32[]{:S(2)}) collective-permute-start(bf16[2,64,128]{2,1,0:T(8,128)(2,1)S(1)} %get-tuple-element.52), channel_id=1, source_target_pairs={{0,96},{1,97},{2,98},{3,99},{4,100},{5,101},{6,102},{7,103},{8,104... | collective-permute-start | bytes 98312 | tf_op jit(solution)/shard_map/ppermute | solution.py:32
  6.0 4.0 %collective-permute-start = (bf16[2,64,128]{2,1,0:T(8,128)(2,1)S(1)}, bf16[2,64,128]{2,1,0:T(8,128)(2,1)S(1)}, u32[]{:S(2)}, u32[]{:S(2)}) collective-permute-start(bf16[2,64,128]{2,1,0:T(8,128)(2,1)S(1)} %get-tuple-element.52), channel_id=1, source_target_pairs={{0,64},{1,65},{2,66},{3,67},{4,68},{5,69},{6,70},{7,71},{8,72},{9,... | collective-permute-start | bytes 98312 | tf_op jit(solution)/shard_map/ppermute | solution.py:32
  6.0 4.0 %collective-permute-start.1 = (bf16[2,64,128]{2,1,0:T(8,128)(2,1)S(1)}, bf16[2,64,128]{2,1,0:T(8,128)(2,1)S(1)}, u32[]{:S(2)}, u32[]{:S(2)}) collective-permute-start(bf16[2,64,128]{2,1,0:T(8,128)(2,1)S(1)} %get-tuple-element.52), channel_id=1, source_target_pairs={{0,32},{1,33},{2,34},{3,35},{4,36},{5,37},{6,38},{7,39},{8,40},{9,... | collective-permute-start | bytes 98312 | tf_op jit(solution)/shard_map/ppermute | solution.py:32
  6.4 15.7 %collective-permute-start.9 = (bf16[64,8192]{1,0:T(8,128)(2,1)}, bf16[64,8192]{1,0:T(8,128)(2,1)S(1)}, u32[]{:S(2)}, u32[]{:S(2)}) collective-permute-start(bf16[64,8192]{1,0:T(8,128)(2,1)} %param.6), channel_id=1, source_target_pairs={{0,1},{1,0},{2,3},{3,2},{4,5},{5,4},{6,7},{7,6},{8,9},{9,8},{10,11... | collective-permute-start | bytes 3145736 | tf_op jit(solution)/shard_map/ppermute | solution.py:32
  8.5 38.8 %collective-permute-start.20 = (bf16[64,8192]{1,0:T(8,128)(2,1)}, bf16[64,8192]{1,0:T(8,128)(2,1)S(1)}, u32[]{:S(2)}, u32[]{:S(2)}) collective-permute-start(bf16[64,8192]{1,0:T(8,128)(2,1)} %param.7), channel_id=1, source_target_pairs={{0,1},{1,0},{2,3},{3,2},{4,5},{5,4},{6,7},{7,6},{8,9},{9,8},{10,11... | collective-permute-start | bytes 3145736 | tf_op jit(solution)/shard_map/ppermute | solution.py:32
  10.1 5.4 %collective-permute-start.3 = (bf16[4,2,64,128]{3,2,0,1:T(8,128)(2,1)S(1)}, bf16[4,2,64,128]{3,2,0,1:T(8,128)(2,1)S(1)}, u32[]{:S(2)}, u32[]{:S(2)}) collective-permute-start(bf16[4,2,64,128]{3,2,0,1:T(8,128)(2,1)S(1)} %pad_maximum_fusion.4), channel_id=1, source_target_pairs={{0,16},{1,5},{2,18},{3,7},{4,20},{5,1},{6,22},{7,3},{8,24},{9,13},... | collective-permute-start | bytes 393224 | tf_op jit(solution)/shard_map/ppermute | solution.py:32
  12.9 4.4 %collective-permute-start.4 = (bf16[4,2,64,128]{3,2,0,1:T(8,128)(2,1)S(1)}, bf16[4,2,64,128]{3,2,0,1:T(8,128)(2,1)S(1)}, u32[]{:S(2)}, u32[]{:S(2)}) collective-permute-start(bf16[4,2,64,128]{3,2,0,1:T(8,128)(2,1)S(1)} %pad_maximum_fusion.4), channel_id=1, source_target_pairs={{0,8},{1,3},{2,10},{3,1},{4,12},{5,7},{6,14},{7,5},{8,0},{9,11},{1... | collective-permute-start | bytes 393224 | tf_op jit(solution)/shard_map/ppermute | solution.py:32
  13.2 5.0 %collective-permute-start.5 = (bf16[4,2,64,128]{3,2,0,1:T(8,128)(2,1)S(1)}, bf16[4,2,64,128]{3,2,0,1:T(8,128)(2,1)S(1)}, u32[]{:S(2)}, u32[]{:S(2)}) collective-permute-start(bf16[4,2,64,128]{3,2,0,1:T(8,128)(2,1)S(1)} %pad_maximum_fusion.4), channel_id=1, source_target_pairs={{0,24},{1,7},{2,26},{3,5},{4,28},{5,3},{6,30},{7,1},{8,16},{9,15},... | collective-permute-start | bytes 393224 | tf_op jit(solution)/shard_map/ppermute | solution.py:32
  18.3 6.8 %collective-permute-start.7 = (bf16[4,4,64,128]{3,2,1,0:T(8,128)(2,1)S(1)}, bf16[4,4,64,128]{3,2,1,0:T(8,128)(2,1)S(1)}, u32[]{:S(2)}, u32[]{:S(2)}) collective-permute-start(bf16[4,4,64,128]{3,2,1,0:T(8,128)(2,1)S(1)} %pad_maximum_fusion.2.refs_0_), channel_id=1, source_target_pairs={{0,4},{1,17},{2,6},{3,19},{4,0},{5,21},{6,2},{7,23},{8,12},{9,25},... | collective-permute-start | bytes 786440 | tf_op jit(solution)/shard_map/ppermute | solution.py:32
  21.3 6.9 %collective-permute-start.8 = (bf16[4,4,64,128]{3,2,1,0:T(8,128)(2,1)S(1)}, bf16[4,4,64,128]{3,2,1,0:T(8,128)(2,1)S(1)}, u32[]{:S(2)}, u32[]{:S(2)}) collective-permute-start(bf16[4,4,64,128]{3,2,1,0:T(8,128)(2,1)S(1)} %pad_maximum_fusion.2.refs_0_), channel_id=1, source_target_pairs={{0,6},{1,25},{2,4},{3,27},{4,2},{5,29},{6,0},{7,31},{8,14},{9,17},... | collective-permute-start | bytes 786440 | tf_op jit(solution)/shard_map/ppermute | solution.py:32
  22.1 6.8 %collective-permute-start.6 = (bf16[4,4,64,128]{3,2,1,0:T(8,128)(2,1)S(1)}, bf16[4,4,64,128]{3,2,1,0:T(8,128)(2,1)S(1)}, u32[]{:S(2)}, u32[]{:S(2)}) collective-permute-start(bf16[4,4,64,128]{3,2,1,0:T(8,128)(2,1)S(1)} %pad_maximum_fusion.2.refs_0_), channel_id=1, source_target_pairs={{0,2},{1,9},{2,0},{3,11},{4,6},{5,13},{6,4},{7,15},{8,10},{9,1},{1... | collective-permute-start | bytes 786440 | tf_op jit(solution)/shard_map/ppermute | solution.py:32
  28.9 18.4 %copy-start.1 = (bf16[64,8192]{1,0:T(8,128)(2,1)S(1)}, bf16[64,8192]{1,0:T(8,128)(2,1)}, u32[]{:S(2)}) copy-start(bf16[64,8192]{1,0:T(8,128)(2,1)} %param.7) | copy-start | bytes 3145732
  29.3 5.6 %collective-permute-start.11 = (f32[128,128]{1,0:T(8,128)S(1)}, f32[128,128]{1,0:T(8,128)S(1)}, u32[]{:S(2)}, u32[]{:S(2)}) collective-permute-start(f32[128,128]{1,0:T(8,128)S(1)} %precondition.4), channel_id=1, source_target_pairs={{0,1},{1,0},{2,3},{3,2},{4,5},{5,4},{6,7},{7,6},{8,9},{9,8},{10,11... | collective-permute-start | bytes 196616 | tf_op jit(solution)/shard_map/ppermute | solution.py:32
  33.9 11.4 %collective-permute-start.10 = (bf16[4,4,64,128]{3,2,1,0:T(8,128)(2,1)S(1)}, bf16[4,4,64,128]{3,2,1,0:T(8,128)(2,1)S(1)}, u32[]{:S(2)}, u32[]{:S(2)}) collective-permute-start(bf16[4,4,64,128]{3,2,1,0:T(8,128)(2,1)S(1)} %pad_maximum_fusion.3), channel_id=1, source_target_pairs={{0,2},{1,9},{2,0},{3,11},{4,6},{5,13},{6,4},{7,15},{8,10},{9,1},{1... | collective-permute-start | bytes 786440 | tf_op jit(solution)/shard_map/ppermute | solution.py:32
  34.9 12.3 %collective-permute-start.12 = (bf16[128,128]{1,0:T(8,128)(2,1)S(1)}, bf16[128,128]{1,0:T(8,128)(2,1)S(1)}, u32[]{:S(2)}, u32[]{:S(2)}) collective-permute-start(bf16[128,128]{1,0:T(8,128)(2,1)S(1)} %add_convert_fusion.1), channel_id=1, source_target_pairs={{0,0},{1,32},{2,2},{3,34},{4,4},{5,36},{6,6},{7,38},{8,8},{9,40},{... | collective-permute-start | bytes 98312 | tf_op jit(solution)/shard_map/ppermute | solution.py:32
  36.9 10.5 %collective-permute-start.13 = (bf16[128,128]{1,0:T(8,128)(2,1)S(1)}, bf16[128,128]{1,0:T(8,128)(2,1)S(1)}, u32[]{:S(2)}, u32[]{:S(2)}) collective-permute-start(bf16[128,128]{1,0:T(8,128)(2,1)S(1)} %add_convert_fusion.1), channel_id=1, source_target_pairs={{0,128},{1,160},{2,130},{3,162},{4,132},{5,164},{6,134},{7,166},{8... | collective-permute-start | bytes 98312 | tf_op jit(solution)/shard_map/ppermute | solution.py:32
  44.6 4.0 %collective-permute-start.14 = (bf16[128,128]{1,0:T(8,128)(2,1)S(1)}, bf16[128,128]{1,0:T(8,128)(2,1)S(1)}, u32[]{:S(2)}, u32[]{:S(2)}) collective-permute-start(bf16[128,128]{1,0:T(8,128)(2,1)S(1)} %add_convert_fusion.1), channel_id=1, source_target_pairs={{0,192},{1,224},{2,194},{3,226},{4,196},{5,228},{6,198},{7,230},{8... | collective-permute-start | bytes 98312 | tf_op jit(solution)/shard_map/ppermute | solution.py:32
  45.4 5.2 %collective-permute-start.15 = (bf16[128,128]{1,0:T(8,128)(2,1)S(1)}, bf16[128,128]{1,0:T(8,128)(2,1)S(1)}, u32[]{:S(2)}, u32[]{:S(2)}) collective-permute-start(bf16[128,128]{1,0:T(8,128)(2,1)S(1)} %add_convert_fusion.1), channel_id=1, source_target_pairs={{0,64},{1,96},{2,66},{3,98},{4,68},{5,100},{6,70},{7,102},{8,72},{... | collective-permute-start | bytes 98312 | tf_op jit(solution)/shard_map/ppermute | solution.py:32
  47.2 12.1 %collective-permute-start.19 = (bf16[2,4,4,64,128]{4,3,2,1,0:T(8,128)(2,1)S(1)}, bf16[2,4,4,64,128]{4,3,2,1,0:T(8,128)(2,1)S(1)}, u32[]{:S(2)}, u32[]{:S(2)}) collective-permute-start(bf16[2,4,4,64,128]{4,3,2,1,0:T(8,128)(2,1)S(1)} %pad_maximum_fusion), channel_id=1, source_target_pairs={{0,6},{1,25},{2,4},{3,27},{4,2},{5,29},{6,0},{7,31},{8,14},{9,17},... | collective-permute-start | bytes 1572872 | tf_op jit(solution)/shard_map/ppermute | solution.py:32
  50.7 5.7 %collective-permute-start.16 = (bf16[2,256,128]{2,1,0:T(8,128)(2,1)S(1)}, bf16[2,256,128]{2,1,0:T(8,128)(2,1)S(1)}, u32[]{:S(2)}, u32[]{:S(2)}) collective-permute-start(bf16[2,256,128]{2,1,0:T(8,128)(2,1)S(1)} %bitcast.58), channel_id=1, source_target_pairs={{0,16},{1,5},{2,18},{3,7},{4,20},{5,1},{6,22},{7,3},{8,24},{9,13},... | collective-permute-start | bytes 393224 | tf_op jit(solution)/shard_map/ppermute | solution.py:32
  52.2 5.6 %collective-permute-start.17 = (bf16[2,256,128]{2,1,0:T(8,128)(2,1)S(1)}, bf16[2,256,128]{2,1,0:T(8,128)(2,1)S(1)}, u32[]{:S(2)}, u32[]{:S(2)}) collective-permute-start(bf16[2,256,128]{2,1,0:T(8,128)(2,1)S(1)} %bitcast.59), channel_id=1, source_target_pairs={{0,8},{1,3},{2,10},{3,1},{4,12},{5,7},{6,14},{7,5},{8,0},{9,11},{1... | collective-permute-start | bytes 393224 | tf_op jit(solution)/shard_map/ppermute | solution.py:32
  53.7 5.3 %collective-permute-start.18 = (bf16[2,256,128]{2,1,0:T(8,128)(2,1)S(1)}, bf16[2,256,128]{2,1,0:T(8,128)(2,1)S(1)}, u32[]{:S(2)}, u32[]{:S(2)}) collective-permute-start(bf16[2,256,128]{2,1,0:T(8,128)(2,1)S(1)} %bitcast.60), channel_id=1, source_target_pairs={{0,24},{1,7},{2,26},{3,5},{4,28},{5,3},{6,30},{7,1},{8,16},{9,15},... | collective-permute-start | bytes 393224 | tf_op jit(solution)/shard_map/ppermute | solution.py:32
  60.2 3.0 %collective-permute-start.21 = (f32[128,128]{1,0:T(8,128)S(1)}, f32[128,128]{1,0:T(8,128)S(1)}, u32[]{:S(2)}, u32[]{:S(2)}) collective-permute-start(f32[128,128]{1,0:T(8,128)S(1)} %precondition.5), channel_id=1, source_target_pairs={{0,1},{1,0},{2,3},{3,2},{4,5},{5,4},{6,7},{7,6},{8,9},{9,8},{10,11... | collective-permute-start | bytes 196616 | tf_op jit(solution)/shard_map/ppermute | solution.py:32
  60.6 12.7 %collective-permute-start.25 = (bf16[4,2,256,128]{3,2,1,0:T(8,128)(2,1)S(1)}, bf16[4,2,256,128]{3,2,1,0:T(8,128)(2,1)S(1)}, u32[]{:S(2)}, u32[]{:S(2)}) collective-permute-start(bf16[4,2,256,128]{3,2,1,0:T(8,128)(2,1)S(1)} %pad_maximum_fusion.1.piece), channel_id=1, source_target_pairs={{0,4},{1,17},{2,6},{3,19},{4,0},{5,21},{6,2},{7,23},{8,12},{9,25},... | collective-permute-start | bytes 1572872 | tf_op jit(solution)/shard_map/ppermute | solution.py:32
  60.8 15.2 %collective-permute-start.24 = (bf16[4,2,256,128]{3,2,1,0:T(8,128)(2,1)S(1)}, bf16[4,2,256,128]{3,2,1,0:T(8,128)(2,1)S(1)}, u32[]{:S(2)}, u32[]{:S(2)}) collective-permute-start(bf16[4,2,256,128]{3,2,1,0:T(8,128)(2,1)S(1)} %pad_maximum_fusion.1.piece), channel_id=1, source_target_pairs={{0,6},{1,25},{2,4},{3,27},{4,2},{5,29},{6,0},{7,31},{8,14},{9,17},... | collective-permute-start | bytes 1572872 | tf_op jit(solution)/shard_map/ppermute | solution.py:32
  62.6 14.9 %collective-permute-start.23 = (bf16[4,2,256,128]{3,2,1,0:T(8,128)(2,1)S(1)}, bf16[4,2,256,128]{3,2,1,0:T(8,128)(2,1)S(1)}, u32[]{:S(2)}, u32[]{:S(2)}) collective-permute-start(bf16[4,2,256,128]{3,2,1,0:T(8,128)(2,1)S(1)} %pad_maximum_fusion.1.piece), channel_id=1, source_target_pairs={{0,2},{1,9},{2,0},{3,11},{4,6},{5,13},{6,4},{7,15},{8,10},{9,1},{1... | collective-permute-start | bytes 1572872 | tf_op jit(solution)/shard_map/ppermute | solution.py:32
  63.3 6.8 %collective-permute-start.22 = (bf16[128,128]{1,0:T(8,128)(2,1)S(1)}, bf16[128,128]{1,0:T(8,128)(2,1)S(1)}, u32[]{:S(2)}, u32[]{:S(2)}) collective-permute-start(bf16[128,128]{1,0:T(8,128)(2,1)S(1)} %maximum_select_fusion), channel_id=1, source_target_pairs={{0,128},{1,129},{2,130},{3,131},{4,132},{5,133},{6,134},{7,135},{8... | collective-permute-start | bytes 98312 | tf_op jit(solution)/shard_map/ppermute | solution.py:32
  70.3 7.5 %collective-permute-start.26 = (f32[64,1024]{1,0:T(8,128)S(1)}, f32[64,1024]{1,0:T(8,128)S(1)}, u32[]{:S(2)}, u32[]{:S(2)}) collective-permute-start(f32[64,1024]{1,0:T(8,128)S(1)} %get-tuple-element.29), channel_id=1, source_target_pairs={{0,1},{1,0},{2,3},{3,2},{4,5},{5,4},{6,7},{7,6},{8,9},{9,8},{10,11... | collective-permute-start | bytes 786440 | tf_op jit(solution)/shard_map/ppermute | solution.py:32
  73.5 4.3 %collective-permute-start.29 = (f32[64,1024]{1,0:T(8,128)S(1)}, f32[64,1024]{1,0:T(8,128)S(1)}, u32[]{:S(2)}, u32[]{:S(2)}) collective-permute-start(f32[64,1024]{1,0:T(8,128)S(1)} %get-tuple-element.32), channel_id=1, source_target_pairs={{0,1},{1,0},{2,3},{3,2},{4,5},{5,4},{6,7},{7,6},{8,9},{9,8},{10,11... | collective-permute-start | bytes 786440 | tf_op jit(solution)/shard_map/ppermute | solution.py:32
  76.2 2.4 %collective-permute-start.28 = (f32[64,1024]{1,0:T(8,128)S(1)}, f32[64,1024]{1,0:T(8,128)S(1)}, u32[]{:S(2)}, u32[]{:S(2)}) collective-permute-start(f32[64,1024]{1,0:T(8,128)S(1)} %get-tuple-element.31), channel_id=1, source_target_pairs={{0,1},{1,0},{2,3},{3,2},{4,5},{5,4},{6,7},{7,6},{8,9},{9,8},{10,11... | collective-permute-start | bytes 786440 | tf_op jit(solution)/shard_map/ppermute | solution.py:32
  77.7 1.6 %collective-permute-start.27 = (f32[64,1024]{1,0:T(8,128)S(1)}, f32[64,1024]{1,0:T(8,128)S(1)}, u32[]{:S(2)}, u32[]{:S(2)}) collective-permute-start(f32[64,1024]{1,0:T(8,128)S(1)} %get-tuple-element.30), channel_id=1, source_target_pairs={{0,1},{1,0},{2,3},{3,2},{4,5},{5,4},{6,7},{7,6},{8,9},{9,8},{10,11... | collective-permute-start | bytes 786440 | tf_op jit(solution)/shard_map/ppermute | solution.py:32

commit v18 on v16

--- a/solution.py
+++ b/solution.py
@@ -207,7 +207,6 @@
 
     there = [to_parity(act, j, 1) for j in (0, 1)]
     here = [to_parity(act, j, 0) for j in (0, 1)]
-    half, here[0] = lax.optimization_barrier((half, here[0]))
     rest = second_turn(half, 3)
     grad_pieces = half[0], half[1], rest[1], rest[0]
     pair = jnp.stack([*here, *there]).reshape(2, 2, 128, 128)

time: 77.3 us -> 77.2 us (level)
  transfers between devices with their start and end apart: 30 -> 30, of which waited for: 12 -> 11; matrix products, arithmetic and copies ran while one was open for 1% -> 1% of each run, Pallas kernels for 4% -> 4%
where the time goes in v18:
time: 77.2 us; the launch traced here: 77 us
  starting transfers between devices  47.4 us (61%)
  waiting for transfers between devices  23.3 us (30%)
  Pallas kernels  4.3 us (6%)
  other arithmetic  1.39 us (2%)
    ppermute x30, starting transfers between devices, send(): return lax.ppermute(value, AXES, pairs)  47.4 us
    ppermute x30, waiting for transfers between devices, send(): return lax.ppermute(value, AXES, pairs)  23.3 us
    pallas_call x3, Pallas kernels, partial(): call(functools.partial(precondition, turns, flip), 'precondition', shape(...  1.94 us
  transfers between devices with their start and end apart: 30, of which 11 were waited for; matrix products, arithmetic and copies ran while one was open for 1% of the time, Pallas kernels for 4%

profile of v18, /device:TPU:1, one launch (start us, length us, event | category | flops | bytes accessed | tf_op | source)
XLA Modules:
  0.0 77.0 jit_solution(5466515720026325665)
XLA Ops:
  0.0 0.8 %fusion = (bf16[1,2,64,128]{3,2,0,1:T(8,128)(2,1)S(1)}, bf16[2,64,128]{2,1,0:T(8,128)(2,1)S(1)}) fusion(bf16[1,64,128]{2,1,0:T(8,128)(2,1)} %bitcast.69, bf16[1,64,128]{2,1,0:T(8,128)(2,1)} %bitcast.70), kind=kLoop, calls=%fused_computation.25 | loop fusion | flops 16384 | bytes 98304 | tf_op jit(solution)/shard_map/stack | solution.py:63
  0.8 5.2 %collective-permute-start.2 = (bf16[2,64,128]{2,1,0:T(8,128)(2,1)S(1)}, bf16[2,64,128]{2,1,0:T(8,128)(2,1)S(1)}, u32[]{:S(2)}, u32[]{:S(2)}) collective-permute-start(bf16[2,64,128]{2,1,0:T(8,128)(2,1)S(1)} %get-tuple-element.42), channel_id=1, source_target_pairs={{0,96},{1,97},{2,98},{3,99},{4,100},{5,101},{6,102},{7,103},{8,104... | collective-permute-start | bytes 98312 | tf_op jit(solution)/shard_map/ppermute | solution.py:32
  6.4 2.1 %collective-permute-start.9 = (bf16[64,8192]{1,0:T(8,128)(2,1)}, bf16[64,8192]{1,0:T(8,128)(2,1)S(1)}, u32[]{:S(2)}, u32[]{:S(2)}) collective-permute-start(bf16[64,8192]{1,0:T(8,128)(2,1)} %param.6), channel_id=1, source_target_pairs={{0,1},{1,0},{2,3},{3,2},{4,5},{5,4},{6,7},{7,6},{8,9},{9,8},{10,11... | collective-permute-start | bytes 3145736 | tf_op jit(solution)/shard_map/ppermute | solution.py:32
  8.5 1.6 %collective-permute-done.1 = bf16[2,64,128]{2,1,0:T(8,128)(2,1)S(1)} collective-permute-done((bf16[2,64,128]{2,1,0:T(8,128)(2,1)S(1)}, bf16[2,64,128]{2,1,0:T(8,128)(2,1)S(1)}, u32[]{:S(2)}, u32[]{:S(2)}) %collective-permute-start.1) | collective-permute-done | bytes 32800 | tf_op jit(solution)/shard_map/ppermute | solution.py:32
  10.1 2.8 %collective-permute-start.5 = (bf16[4,2,64,128]{3,2,0,1:T(8,128)(2,1)S(1)}, bf16[4,2,64,128]{3,2,0,1:T(8,128)(2,1)S(1)}, u32[]{:S(2)}, u32[]{:S(2)}) collective-permute-start(bf16[4,2,64,128]{3,2,0,1:T(8,128)(2,1)S(1)} %pad_maximum_fusion.4), channel_id=1, source_target_pairs={{0,16},{1,5},{2,18},{3,7},{4,20},{5,1},{6,22},{7,3},{8,24},{9,13},... | collective-permute-start | bytes 393224 | tf_op jit(solution)/shard_map/ppermute | solution.py:32
  12.9 0.9 %collective-permute-start.4 = (bf16[4,2,64,128]{3,2,0,1:T(8,128)(2,1)S(1)}, bf16[4,2,64,128]{3,2,0,1:T(8,128)(2,1)S(1)}, u32[]{:S(2)}, u32[]{:S(2)}) collective-permute-start(bf16[4,2,64,128]{3,2,0,1:T(8,128)(2,1)S(1)} %pad_maximum_fusion.4), channel_id=1, source_target_pairs={{0,24},{1,7},{2,26},{3,5},{4,28},{5,3},{6,30},{7,1},{8,16},{9,15},... | collective-permute-start | bytes 393224 | tf_op jit(solution)/shard_map/ppermute | solution.py:32
  13.8 1.7 %collective-permute-done.5 = bf16[4,2,64,128]{3,2,0,1:T(8,128)(2,1)S(1)} collective-permute-done((bf16[4,2,64,128]{3,2,0,1:T(8,128)(2,1)S(1)}, bf16[4,2,64,128]{3,2,0,1:T(8,128)(2,1)S(1)}, u32[]{:S(2)}, u32[]{:S(2)}) %collective-permute-start.5) | collective-permute-done | bytes 131104 | tf_op jit(solution)/shard_map/ppermute | solution.py:32
  15.5 2.5 %collective-permute-done.4 = bf16[4,2,64,128]{3,2,0,1:T(8,128)(2,1)S(1)} collective-permute-done((bf16[4,2,64,128]{3,2,0,1:T(8,128)(2,1)S(1)}, bf16[4,2,64,128]{3,2,0,1:T(8,128)(2,1)S(1)}, u32[]{:S(2)}, u32[]{:S(2)}) %collective-permute-start.4) | collective-permute-done | bytes 131104 | tf_op jit(solution)/shard_map/ppermute | solution.py:32
  18.1 3.0 %collective-permute-start.6 = (bf16[4,4,64,128]{3,2,1,0:T(8,128)(2,1)S(1)}, bf16[4,4,64,128]{3,2,1,0:T(8,128)(2,1)S(1)}, u32[]{:S(2)}, u32[]{:S(2)}) collective-permute-start(bf16[4,4,64,128]{3,2,1,0:T(8,128)(2,1)S(1)} %pad_maximum_fusion.2.refs_0_), channel_id=1, source_target_pairs={{0,4},{1,17},{2,6},{3,19},{4,0},{5,21},{6,2},{7,23},{8,12},{9,25},... | collective-permute-start | bytes 786440 | tf_op jit(solution)/shard_map/ppermute | solution.py:32
  21.1 0.7 collective-permute-start.7
  22.0 5.9 %collective-permute-done.7.refs_1_ = bf16[4,4,64,128]{3,2,1,0:T(8,128)(2,1)S(1)} collective-permute-done((bf16[4,4,64,128]{3,2,1,0:T(8,128)(2,1)S(1)}, bf16[4,4,64,128]{3,2,1,0:T(8,128)(2,1)S(1)}, u32[]{:S(2)}, u32[]{:S(2)}) %collective-permute-start.7) | collective-permute-done | bytes 262176 | tf_op jit(solution)/shard_map/ppermute | solution.py:32
  28.6 0.7 precondition.3.refs_1_
  29.7 3.7 %collective-permute-start.15 = (f32[128,128]{1,0:T(8,128)S(1)}, f32[128,128]{1,0:T(8,128)S(1)}, u32[]{:S(2)}, u32[]{:S(2)}) collective-permute-start(f32[128,128]{1,0:T(8,128)S(1)} %precondition.4), channel_id=1, source_target_pairs={{0,1},{1,0},{2,3},{3,2},{4,5},{5,4},{6,7},{7,6},{8,9},{9,8},{10,11... | collective-permute-start | bytes 196616 | tf_op jit(solution)/shard_map/ppermute | solution.py:32
  33.4 0.9 %collective-permute-done.15 = f32[128,128]{1,0:T(8,128)S(1)} collective-permute-done((f32[128,128]{1,0:T(8,128)S(1)}, f32[128,128]{1,0:T(8,128)S(1)}, u32[]{:S(2)}, u32[]{:S(2)}) %collective-permute-start.15) | collective-permute-done | bytes 65568 | tf_op jit(solution)/shard_map/ppermute | solution.py:32
  34.3 3.5 %collective-permute-start.19 = (bf16[128,128]{1,0:T(8,128)(2,1)S(1)}, bf16[128,128]{1,0:T(8,128)(2,1)S(1)}, u32[]{:S(2)}, u32[]{:S(2)}) collective-permute-start(bf16[128,128]{1,0:T(8,128)(2,1)S(1)} %add_convert_fusion), channel_id=1, source_target_pairs={{0,192},{1,224},{2,194},{3,226},{4,196},{5,228},{6,198},{7,230},{8... | collective-permute-start | bytes 98312 | tf_op jit(solution)/shard_map/ppermute | solution.py:32
  37.8 1.8 %collective-permute-start.18 = (bf16[128,128]{1,0:T(8,128)(2,1)S(1)}, bf16[128,128]{1,0:T(8,128)(2,1)S(1)}, u32[]{:S(2)}, u32[]{:S(2)}) collective-permute-start(bf16[128,128]{1,0:T(8,128)(2,1)S(1)} %add_convert_fusion), channel_id=1, source_target_pairs={{0,128},{1,160},{2,130},{3,162},{4,132},{5,164},{6,134},{7,166},{8... | collective-permute-start | bytes 98312 | tf_op jit(solution)/shard_map/ppermute | solution.py:32
  39.6 1.0 %collective-permute-start.17 = (bf16[128,128]{1,0:T(8,128)(2,1)S(1)}, bf16[128,128]{1,0:T(8,128)(2,1)S(1)}, u32[]{:S(2)}, u32[]{:S(2)}) collective-permute-start(bf16[128,128]{1,0:T(8,128)(2,1)S(1)} %add_convert_fusion), channel_id=1, source_target_pairs={{0,64},{1,96},{2,66},{3,98},{4,68},{5,100},{6,70},{7,102},{8,72},{... | collective-permute-start | bytes 98312 | tf_op jit(solution)/shard_map/ppermute | solution.py:32
  40.6 2.5 %collective-permute-start.16 = (bf16[128,128]{1,0:T(8,128)(2,1)S(1)}, bf16[128,128]{1,0:T(8,128)(2,1)S(1)}, u32[]{:S(2)}, u32[]{:S(2)}) collective-permute-start(bf16[128,128]{1,0:T(8,128)(2,1)S(1)} %add_convert_fusion), channel_id=1, source_target_pairs={{0,0},{1,32},{2,2},{3,34},{4,4},{5,36},{6,6},{7,38},{8,8},{9,40},{... | collective-permute-start | bytes 98312 | tf_op jit(solution)/shard_map/ppermute | solution.py:32
  43.2 2.8 %collective-permute-start.11 = (bf16[2,4,4,64,128]{4,3,2,1,0:T(8,128)(2,1)S(1)}, bf16[2,4,4,64,128]{4,3,2,1,0:T(8,128)(2,1)S(1)}, u32[]{:S(2)}, u32[]{:S(2)}) collective-permute-start(bf16[2,4,4,64,128]{4,3,2,1,0:T(8,128)(2,1)S(1)} %pad_maximum_fusion), channel_id=1, source_target_pairs={{0,6},{1,25},{2,4},{3,27},{4,2},{5,29},{6,0},{7,31},{8,14},{9,17},... | collective-permute-start | bytes 1572872 | tf_op jit(solution)/shard_map/ppermute | solution.py:32
  46.2 1.9 %collective-permute-start.22 = (bf16[2,256,128]{2,1,0:T(8,128)(2,1)S(1)}, bf16[2,256,128]{2,1,0:T(8,128)(2,1)S(1)}, u32[]{:S(2)}, u32[]{:S(2)}) collective-permute-start(bf16[2,256,128]{2,1,0:T(8,128)(2,1)S(1)} %bitcast.55), channel_id=1, source_target_pairs={{0,16},{1,5},{2,18},{3,7},{4,20},{5,1},{6,22},{7,3},{8,24},{9,13},... | collective-permute-start | bytes 393224 | tf_op jit(solution)/shard_map/ppermute | solution.py:32
  48.1 2.1 %collective-permute-start.21 = (bf16[2,256,128]{2,1,0:T(8,128)(2,1)S(1)}, bf16[2,256,128]{2,1,0:T(8,128)(2,1)S(1)}, u32[]{:S(2)}, u32[]{:S(2)}) collective-permute-start(bf16[2,256,128]{2,1,0:T(8,128)(2,1)S(1)} %bitcast.56), channel_id=1, source_target_pairs={{0,24},{1,7},{2,26},{3,5},{4,28},{5,3},{6,30},{7,1},{8,16},{9,15},... | collective-permute-start | bytes 393224 | tf_op jit(solution)/shard_map/ppermute | solution.py:32
  50.2 4.0 %collective-permute-done.11 = bf16[2,4,4,64,128]{4,3,2,1,0:T(8,128)(2,1)S(1)} collective-permute-done((bf16[2,4,4,64,128]{4,3,2,1,0:T(8,128)(2,1)S(1)}, bf16[2,4,4,64,128]{4,3,2,1,0:T(8,128)(2,1)S(1)}, u32[]{:S(2)}, u32[]{:S(2)}) %collective-permute-start.11) | collective-permute-done | bytes 524320 | tf_op jit(solution)/shard_map/ppermute | solution.py:32
  54.3 0.9 %precondition.5 = f32[128,128]{1,0:T(8,128)S(1)} custom-call(bf16[4,4,64,128]{3,2,1,0:T(8,128)(2,1)S(1)} %pad_maximum_fusion.3.refs_0_, bf16[4,4,64,128]{3,2,1,0:T(8,128)(2,1)S(1)} %collective-permute-done.10.refs_1_, bf16[4,4,64,128]{3,2,1,0:T(8,128)(2,1)S(1)} %get-tuple-element.30.refs_2_, bf16[4,4,64,128]{3,2,1,0:T(8,128)(2,1)S(1)} %get-tuple-element.29.refs_3_, ...), custom_call_target="tpu_custom_call" | custom-call | tf_op jit(solution)/shard_map/precondition/pallas_call | solution.py:193
  55.2 1.8 %collective-permute-start.13 = (f32[128,128]{1,0:T(8,128)S(1)}, f32[128,128]{1,0:T(8,128)S(1)}, u32[]{:S(2)}, u32[]{:S(2)}) collective-permute-start(f32[128,128]{1,0:T(8,128)S(1)} %precondition.5), channel_id=1, source_target_pairs={{0,1},{1,0},{2,3},{3,2},{4,5},{5,4},{6,7},{7,6},{8,9},{9,8},{10,11... | collective-permute-start | bytes 196616 | tf_op jit(solution)/shard_map/ppermute | solution.py:32
  57.1 1.9 %collective-permute-start.23 = (bf16[4,2,256,128]{3,2,1,0:T(8,128)(2,1)S(1)}, bf16[4,2,256,128]{3,2,1,0:T(8,128)(2,1)S(1)}, u32[]{:S(2)}, u32[]{:S(2)}) collective-permute-start(bf16[4,2,256,128]{3,2,1,0:T(8,128)(2,1)S(1)} %pad_maximum_fusion.1.piece), channel_id=1, source_target_pairs={{0,4},{1,17},{2,6},{3,19},{4,0},{5,21},{6,2},{7,23},{8,12},{9,25},... | collective-permute-start | bytes 1572872 | tf_op jit(solution)/shard_map/ppermute | solution.py:32
  59.0 1.6 %collective-permute-start.24 = (bf16[4,2,256,128]{3,2,1,0:T(8,128)(2,1)S(1)}, bf16[4,2,256,128]{3,2,1,0:T(8,128)(2,1)S(1)}, u32[]{:S(2)}, u32[]{:S(2)}) collective-permute-start(bf16[4,2,256,128]{3,2,1,0:T(8,128)(2,1)S(1)} %pad_maximum_fusion.1.piece), channel_id=1, source_target_pairs={{0,2},{1,9},{2,0},{3,11},{4,6},{5,13},{6,4},{7,15},{8,10},{9,1},{1... | collective-permute-start | bytes 1572872 | tf_op jit(solution)/shard_map/ppermute | solution.py:32
  60.6 4.9 %collective-permute-start.14 = (bf16[128,128]{1,0:T(8,128)(2,1)S(1)}, bf16[128,128]{1,0:T(8,128)(2,1)S(1)}, u32[]{:S(2)}, u32[]{:S(2)}) collective-permute-start(bf16[128,128]{1,0:T(8,128)(2,1)S(1)} %maximum_select_fusion), channel_id=1, source_target_pairs={{0,128},{1,129},{2,130},{3,131},{4,132},{5,133},{6,134},{7,135},{8... | collective-permute-start | bytes 98312 | tf_op jit(solution)/shard_map/ppermute | solution.py:32
  65.5 1.8 %collective-permute-done.14 = bf16[128,128]{1,0:T(8,128)(2,1)S(1)} collective-permute-done((bf16[128,128]{1,0:T(8,128)(2,1)S(1)}, bf16[128,128]{1,0:T(8,128)(2,1)S(1)}, u32[]{:S(2)}, u32[]{:S(2)}) %collective-permute-start.14) | collective-permute-done | bytes 32800 | tf_op jit(solution)/shard_map/ppermute | solution.py:32
  67.6 2.0 %collective-permute-start.26 = (f32[64,1024]{1,0:T(8,128)S(1)}, f32[64,1024]{1,0:T(8,128)S(1)}, u32[]{:S(2)}, u32[]{:S(2)}) collective-permute-start(f32[64,1024]{1,0:T(8,128)S(1)} %get-tuple-element.21), channel_id=1, source_target_pairs={{0,1},{1,0},{2,3},{3,2},{4,5},{5,4},{6,7},{7,6},{8,9},{9,8},{10,11... | collective-permute-start | bytes 786440 | tf_op jit(solution)/shard_map/ppermute | solution.py:32
  70.0 3.0 %collective-permute-done.24.piece = bf16[4,2,256,128]{3,2,1,0:T(8,128)(2,1)S(1)} collective-permute-done((bf16[4,2,256,128]{3,2,1,0:T(8,128)(2,1)S(1)}, bf16[4,2,256,128]{3,2,1,0:T(8,128)(2,1)S(1)}, u32[]{:S(2)}, u32[]{:S(2)}) %collective-permute-start.24) | collective-permute-done | bytes 524320 | tf_op jit(solution)/shard_map/ppermute | solution.py:32
  74.2 0.7 collective-permute-done.28.refs_6_
  75.4 1.4 %assemble.1 = f32[64,8192]{1,0:T(8,128)} custom-call(f32[64,1024]{1,0:T(8,128)S(1)} %get-tuple-element.17.refs_0_, f32[64,1024]{1,0:T(8,128)S(1)} %get-tuple-element.18.refs_1_, f32[64,1024]{1,0:T(8,128)S(1)} %get-tuple-element.19.refs_2_, f32[64,1024]{1,0:T(8,128)S(1)} %get-tuple-element.20.refs_3_, f32[64,1024]{1,0:T(8,128)S(1)} %collective-permute-done.26.refs_4_, ...), custom_call_target="tpu_custom_call" | custom-call | tf_op jit(solution)/shard_map/assemble/pallas_call | solution.py:226
  (60 shorter events, 4.3 us)
Async XLA Ops:
  0.0 21.9 %copy-start = (bf16[64,8192]{1,0:T(8,128)(2,1)S(1)}, bf16[64,8192]{1,0:T(8,128)(2,1)}, u32[]{:S(2)}) copy-start(bf16[64,8192]{1,0:T(8,128)(2,1)} %param.6) | copy-start | bytes 3145732
  0.8 7.6 %collective-permute-start.2 = (bf16[2,64,128]{2,1,0:T(8,128)(2,1)S(1)}, bf16[2,64,128]{2,1,0:T(8,128)(2,1)S(1)}, u32[]{:S(2)}, u32[]{:S(2)}) collective-permute-start(bf16[2,64,128]{2,1,0:T(8,128)(2,1)S(1)} %get-tuple-element.42), channel_id=1, source_target_pairs={{0,96},{1,97},{2,98},{3,99},{4,100},{5,101},{6,102},{7,103},{8,104... | collective-permute-start | bytes 98312 | tf_op jit(solution)/shard_map/ppermute | solution.py:32
  6.0 4.0 %collective-permute-start.1 = (bf16[2,64,128]{2,1,0:T(8,128)(2,1)S(1)}, bf16[2,64,128]{2,1,0:T(8,128)(2,1)S(1)}, u32[]{:S(2)}, u32[]{:S(2)}) collective-permute-start(bf16[2,64,128]{2,1,0:T(8,128)(2,1)S(1)} %get-tuple-element.42), channel_id=1, source_target_pairs={{0,64},{1,65},{2,66},{3,67},{4,68},{5,69},{6,70},{7,71},{8,72},{9,... | collective-permute-start | bytes 98312 | tf_op jit(solution)/shard_map/ppermute | solution.py:32
  6.0 4.0 %collective-permute-start = (bf16[2,64,128]{2,1,0:T(8,128)(2,1)S(1)}, bf16[2,64,128]{2,1,0:T(8,128)(2,1)S(1)}, u32[]{:S(2)}, u32[]{:S(2)}) collective-permute-start(bf16[2,64,128]{2,1,0:T(8,128)(2,1)S(1)} %get-tuple-element.42), channel_id=1, source_target_pairs={{0,32},{1,33},{2,34},{3,35},{4,36},{5,37},{6,38},{7,39},{8,40},{9,... | collective-permute-start | bytes 98312 | tf_op jit(solution)/shard_map/ppermute | solution.py:32
  6.4 15.5 %collective-permute-start.9 = (bf16[64,8192]{1,0:T(8,128)(2,1)}, bf16[64,8192]{1,0:T(8,128)(2,1)S(1)}, u32[]{:S(2)}, u32[]{:S(2)}) collective-permute-start(bf16[64,8192]{1,0:T(8,128)(2,1)} %param.6), channel_id=1, source_target_pairs={{0,1},{1,0},{2,3},{3,2},{4,5},{5,4},{6,7},{7,6},{8,9},{9,8},{10,11... | collective-permute-start | bytes 3145736 | tf_op jit(solution)/shard_map/ppermute | solution.py:32
  8.5 34.8 %collective-permute-start.12 = (bf16[64,8192]{1,0:T(8,128)(2,1)}, bf16[64,8192]{1,0:T(8,128)(2,1)S(1)}, u32[]{:S(2)}, u32[]{:S(2)}) collective-permute-start(bf16[64,8192]{1,0:T(8,128)(2,1)} %param.7), channel_id=1, source_target_pairs={{0,1},{1,0},{2,3},{3,2},{4,5},{5,4},{6,7},{7,6},{8,9},{9,8},{10,11... | collective-permute-start | bytes 3145736 | tf_op jit(solution)/shard_map/ppermute | solution.py:32
  10.1 5.4 %collective-permute-start.5 = (bf16[4,2,64,128]{3,2,0,1:T(8,128)(2,1)S(1)}, bf16[4,2,64,128]{3,2,0,1:T(8,128)(2,1)S(1)}, u32[]{:S(2)}, u32[]{:S(2)}) collective-permute-start(bf16[4,2,64,128]{3,2,0,1:T(8,128)(2,1)S(1)} %pad_maximum_fusion.4), channel_id=1, source_target_pairs={{0,16},{1,5},{2,18},{3,7},{4,20},{5,1},{6,22},{7,3},{8,24},{9,13},... | collective-permute-start | bytes 393224 | tf_op jit(solution)/shard_map/ppermute | solution.py:32
  12.9 5.1 %collective-permute-start.4 = (bf16[4,2,64,128]{3,2,0,1:T(8,128)(2,1)S(1)}, bf16[4,2,64,128]{3,2,0,1:T(8,128)(2,1)S(1)}, u32[]{:S(2)}, u32[]{:S(2)}) collective-permute-start(bf16[4,2,64,128]{3,2,0,1:T(8,128)(2,1)S(1)} %pad_maximum_fusion.4), channel_id=1, source_target_pairs={{0,24},{1,7},{2,26},{3,5},{4,28},{5,3},{6,30},{7,1},{8,16},{9,15},... | collective-permute-start | bytes 393224 | tf_op jit(solution)/shard_map/ppermute | solution.py:32
  13.8 4.2 %collective-permute-start.3 = (bf16[4,2,64,128]{3,2,0,1:T(8,128)(2,1)S(1)}, bf16[4,2,64,128]{3,2,0,1:T(8,128)(2,1)S(1)}, u32[]{:S(2)}, u32[]{:S(2)}) collective-permute-start(bf16[4,2,64,128]{3,2,0,1:T(8,128)(2,1)S(1)} %pad_maximum_fusion.4), channel_id=1, source_target_pairs={{0,8},{1,3},{2,10},{3,1},{4,12},{5,7},{6,14},{7,5},{8,0},{9,11},{1... | collective-permute-start | bytes 393224 | tf_op jit(solution)/shard_map/ppermute | solution.py:32
  18.1 11.3 %collective-permute-start.6 = (bf16[4,4,64,128]{3,2,1,0:T(8,128)(2,1)S(1)}, bf16[4,4,64,128]{3,2,1,0:T(8,128)(2,1)S(1)}, u32[]{:S(2)}, u32[]{:S(2)}) collective-permute-start(bf16[4,4,64,128]{3,2,1,0:T(8,128)(2,1)S(1)} %pad_maximum_fusion.2.refs_0_), channel_id=1, source_target_pairs={{0,4},{1,17},{2,6},{3,19},{4,0},{5,21},{6,2},{7,23},{8,12},{9,25},... | collective-permute-start | bytes 786440 | tf_op jit(solution)/shard_map/ppermute | solution.py:32
  21.1 6.9 %collective-permute-start.7 = (bf16[4,4,64,128]{3,2,1,0:T(8,128)(2,1)S(1)}, bf16[4,4,64,128]{3,2,1,0:T(8,128)(2,1)S(1)}, u32[]{:S(2)}, u32[]{:S(2)}) collective-permute-start(bf16[4,4,64,128]{3,2,1,0:T(8,128)(2,1)S(1)} %pad_maximum_fusion.2.refs_0_), channel_id=1, source_target_pairs={{0,6},{1,25},{2,4},{3,27},{4,2},{5,29},{6,0},{7,31},{8,14},{9,17},... | collective-permute-start | bytes 786440 | tf_op jit(solution)/shard_map/ppermute | solution.py:32
  21.8 6.8 %collective-permute-start.8 = (bf16[4,4,64,128]{3,2,1,0:T(8,128)(2,1)S(1)}, bf16[4,4,64,128]{3,2,1,0:T(8,128)(2,1)S(1)}, u32[]{:S(2)}, u32[]{:S(2)}) collective-permute-start(bf16[4,4,64,128]{3,2,1,0:T(8,128)(2,1)S(1)} %pad_maximum_fusion.2.refs_0_), channel_id=1, source_target_pairs={{0,2},{1,9},{2,0},{3,11},{4,6},{5,13},{6,4},{7,15},{8,10},{9,1},{1... | collective-permute-start | bytes 786440 | tf_op jit(solution)/shard_map/ppermute | solution.py:32
  29.3 16.7 %copy-start.1 = (bf16[64,8192]{1,0:T(8,128)(2,1)S(1)}, bf16[64,8192]{1,0:T(8,128)(2,1)}, u32[]{:S(2)}) copy-start(bf16[64,8192]{1,0:T(8,128)(2,1)} %param.7) | copy-start | bytes 3145732
  29.7 4.6 %collective-permute-start.15 = (f32[128,128]{1,0:T(8,128)S(1)}, f32[128,128]{1,0:T(8,128)S(1)}, u32[]{:S(2)}, u32[]{:S(2)}) collective-permute-start(f32[128,128]{1,0:T(8,128)S(1)} %precondition.4), channel_id=1, source_target_pairs={{0,1},{1,0},{2,3},{3,2},{4,5},{5,4},{6,7},{7,6},{8,9},{9,8},{10,11... | collective-permute-start | bytes 196616 | tf_op jit(solution)/shard_map/ppermute | solution.py:32
  33.4 7.2 %collective-permute-start.10 = (bf16[4,4,64,128]{3,2,1,0:T(8,128)(2,1)S(1)}, bf16[4,4,64,128]{3,2,1,0:T(8,128)(2,1)S(1)}, u32[]{:S(2)}, u32[]{:S(2)}) collective-permute-start(bf16[4,4,64,128]{3,2,1,0:T(8,128)(2,1)S(1)} %pad_maximum_fusion.3.refs_0_), channel_id=1, source_target_pairs={{0,2},{1,9},{2,0},{3,11},{4,6},{5,13},{6,4},{7,15},{8,10},{9,1},{1... | collective-permute-start | bytes 786440 | tf_op jit(solution)/shard_map/ppermute | solution.py:32
  34.3 11.8 %collective-permute-start.19 = (bf16[128,128]{1,0:T(8,128)(2,1)S(1)}, bf16[128,128]{1,0:T(8,128)(2,1)S(1)}, u32[]{:S(2)}, u32[]{:S(2)}) collective-permute-start(bf16[128,128]{1,0:T(8,128)(2,1)S(1)} %add_convert_fusion), channel_id=1, source_target_pairs={{0,192},{1,224},{2,194},{3,226},{4,196},{5,228},{6,198},{7,230},{8... | collective-permute-start | bytes 98312 | tf_op jit(solution)/shard_map/ppermute | solution.py:32
  37.8 8.3 %collective-permute-start.18 = (bf16[128,128]{1,0:T(8,128)(2,1)S(1)}, bf16[128,128]{1,0:T(8,128)(2,1)S(1)}, u32[]{:S(2)}, u32[]{:S(2)}) collective-permute-start(bf16[128,128]{1,0:T(8,128)(2,1)S(1)} %add_convert_fusion), channel_id=1, source_target_pairs={{0,128},{1,160},{2,130},{3,162},{4,132},{5,164},{6,134},{7,166},{8... | collective-permute-start | bytes 98312 | tf_op jit(solution)/shard_map/ppermute | solution.py:32
  39.6 6.5 %collective-permute-start.17 = (bf16[128,128]{1,0:T(8,128)(2,1)S(1)}, bf16[128,128]{1,0:T(8,128)(2,1)S(1)}, u32[]{:S(2)}, u32[]{:S(2)}) collective-permute-start(bf16[128,128]{1,0:T(8,128)(2,1)S(1)} %add_convert_fusion), channel_id=1, source_target_pairs={{0,64},{1,96},{2,66},{3,98},{4,68},{5,100},{6,70},{7,102},{8,72},{... | collective-permute-start | bytes 98312 | tf_op jit(solution)/shard_map/ppermute | solution.py:32
  40.6 5.5 %collective-permute-start.16 = (bf16[128,128]{1,0:T(8,128)(2,1)S(1)}, bf16[128,128]{1,0:T(8,128)(2,1)S(1)}, u32[]{:S(2)}, u32[]{:S(2)}) collective-permute-start(bf16[128,128]{1,0:T(8,128)(2,1)S(1)} %add_convert_fusion), channel_id=1, source_target_pairs={{0,0},{1,32},{2,2},{3,34},{4,4},{5,36},{6,6},{7,38},{8,8},{9,40},{... | collective-permute-start | bytes 98312 | tf_op jit(solution)/shard_map/ppermute | solution.py:32
  43.2 11.0 %collective-permute-start.11 = (bf16[2,4,4,64,128]{4,3,2,1,0:T(8,128)(2,1)S(1)}, bf16[2,4,4,64,128]{4,3,2,1,0:T(8,128)(2,1)S(1)}, u32[]{:S(2)}, u32[]{:S(2)}) collective-permute-start(bf16[2,4,4,64,128]{4,3,2,1,0:T(8,128)(2,1)S(1)} %pad_maximum_fusion), channel_id=1, source_target_pairs={{0,6},{1,25},{2,4},{3,27},{4,2},{5,29},{6,0},{7,31},{8,14},{9,17},... | collective-permute-start | bytes 1572872 | tf_op jit(solution)/shard_map/ppermute | solution.py:32
  46.2 10.8 %collective-permute-start.22 = (bf16[2,256,128]{2,1,0:T(8,128)(2,1)S(1)}, bf16[2,256,128]{2,1,0:T(8,128)(2,1)S(1)}, u32[]{:S(2)}, u32[]{:S(2)}) collective-permute-start(bf16[2,256,128]{2,1,0:T(8,128)(2,1)S(1)} %bitcast.55), channel_id=1, source_target_pairs={{0,16},{1,5},{2,18},{3,7},{4,20},{5,1},{6,22},{7,3},{8,24},{9,13},... | collective-permute-start | bytes 393224 | tf_op jit(solution)/shard_map/ppermute | solution.py:32
  48.1 8.9 %collective-permute-start.21 = (bf16[2,256,128]{2,1,0:T(8,128)(2,1)S(1)}, bf16[2,256,128]{2,1,0:T(8,128)(2,1)S(1)}, u32[]{:S(2)}, u32[]{:S(2)}) collective-permute-start(bf16[2,256,128]{2,1,0:T(8,128)(2,1)S(1)} %bitcast.56), channel_id=1, source_target_pairs={{0,24},{1,7},{2,26},{3,5},{4,28},{5,3},{6,30},{7,1},{8,16},{9,15},... | collective-permute-start | bytes 393224 | tf_op jit(solution)/shard_map/ppermute | solution.py:32
  50.2 6.7 %collective-permute-start.20 = (bf16[2,256,128]{2,1,0:T(8,128)(2,1)S(1)}, bf16[2,256,128]{2,1,0:T(8,128)(2,1)S(1)}, u32[]{:S(2)}, u32[]{:S(2)}) collective-permute-start(bf16[2,256,128]{2,1,0:T(8,128)(2,1)S(1)} %bitcast.57), channel_id=1, source_target_pairs={{0,8},{1,3},{2,10},{3,1},{4,12},{5,7},{6,14},{7,5},{8,0},{9,11},{1... | collective-permute-start | bytes 393224 | tf_op jit(solution)/shard_map/ppermute | solution.py:32
  55.2 5.4 %collective-permute-start.13 = (f32[128,128]{1,0:T(8,128)S(1)}, f32[128,128]{1,0:T(8,128)S(1)}, u32[]{:S(2)}, u32[]{:S(2)}) collective-permute-start(f32[128,128]{1,0:T(8,128)S(1)} %precondition.5), channel_id=1, source_target_pairs={{0,1},{1,0},{2,3},{3,2},{4,5},{5,4},{6,7},{7,6},{8,9},{9,8},{10,11... | collective-permute-start | bytes 196616 | tf_op jit(solution)/shard_map/ppermute | solution.py:32
  57.1 12.6 %collective-permute-start.23 = (bf16[4,2,256,128]{3,2,1,0:T(8,128)(2,1)S(1)}, bf16[4,2,256,128]{3,2,1,0:T(8,128)(2,1)S(1)}, u32[]{:S(2)}, u32[]{:S(2)}) collective-permute-start(bf16[4,2,256,128]{3,2,1,0:T(8,128)(2,1)S(1)} %pad_maximum_fusion.1.piece), channel_id=1, source_target_pairs={{0,4},{1,17},{2,6},{3,19},{4,0},{5,21},{6,2},{7,23},{8,12},{9,25},... | collective-permute-start | bytes 1572872 | tf_op jit(solution)/shard_map/ppermute | solution.py:32
  59.0 14.1 %collective-permute-start.24 = (bf16[4,2,256,128]{3,2,1,0:T(8,128)(2,1)S(1)}, bf16[4,2,256,128]{3,2,1,0:T(8,128)(2,1)S(1)}, u32[]{:S(2)}, u32[]{:S(2)}) collective-permute-start(bf16[4,2,256,128]{3,2,1,0:T(8,128)(2,1)S(1)} %pad_maximum_fusion.1.piece), channel_id=1, source_target_pairs={{0,2},{1,9},{2,0},{3,11},{4,6},{5,13},{6,4},{7,15},{8,10},{9,1},{1... | collective-permute-start | bytes 1572872 | tf_op jit(solution)/shard_map/ppermute | solution.py:32
  60.6 12.9 %collective-permute-start.25 = (bf16[4,2,256,128]{3,2,1,0:T(8,128)(2,1)S(1)}, bf16[4,2,256,128]{3,2,1,0:T(8,128)(2,1)S(1)}, u32[]{:S(2)}, u32[]{:S(2)}) collective-permute-start(bf16[4,2,256,128]{3,2,1,0:T(8,128)(2,1)S(1)} %pad_maximum_fusion.1.piece), channel_id=1, source_target_pairs={{0,6},{1,25},{2,4},{3,27},{4,2},{5,29},{6,0},{7,31},{8,14},{9,17},... | collective-permute-start | bytes 1572872 | tf_op jit(solution)/shard_map/ppermute | solution.py:32
  60.6 6.8 %collective-permute-start.14 = (bf16[128,128]{1,0:T(8,128)(2,1)S(1)}, bf16[128,128]{1,0:T(8,128)(2,1)S(1)}, u32[]{:S(2)}, u32[]{:S(2)}) collective-permute-start(bf16[128,128]{1,0:T(8,128)(2,1)S(1)} %maximum_select_fusion), channel_id=1, source_target_pairs={{0,128},{1,129},{2,130},{3,131},{4,132},{5,133},{6,134},{7,135},{8... | collective-permute-start | bytes 98312 | tf_op jit(solution)/shard_map/ppermute | solution.py:32
  67.6 6.6 %collective-permute-start.26 = (f32[64,1024]{1,0:T(8,128)S(1)}, f32[64,1024]{1,0:T(8,128)S(1)}, u32[]{:S(2)}, u32[]{:S(2)}) collective-permute-start(f32[64,1024]{1,0:T(8,128)S(1)} %get-tuple-element.21), channel_id=1, source_target_pairs={{0,1},{1,0},{2,3},{3,2},{4,5},{5,4},{6,7},{7,6},{8,9},{9,8},{10,11... | collective-permute-start | bytes 786440 | tf_op jit(solution)/shard_map/ppermute | solution.py:32
  69.9 4.3 %collective-permute-start.27 = (f32[64,1024]{1,0:T(8,128)S(1)}, f32[64,1024]{1,0:T(8,128)S(1)}, u32[]{:S(2)}, u32[]{:S(2)}) collective-permute-start(f32[64,1024]{1,0:T(8,128)S(1)} %get-tuple-element.22), channel_id=1, source_target_pairs={{0,1},{1,0},{2,3},{3,2},{4,5},{5,4},{6,7},{7,6},{8,9},{9,8},{10,11... | collective-permute-start | bytes 786440 | tf_op jit(solution)/shard_map/ppermute | solution.py:32
  73.3 1.6 %collective-permute-start.28 = (f32[64,1024]{1,0:T(8,128)S(1)}, f32[64,1024]{1,0:T(8,128)S(1)}, u32[]{:S(2)}, u32[]{:S(2)}) collective-permute-start(f32[64,1024]{1,0:T(8,128)S(1)} %get-tuple-element.23), channel_id=1, source_target_pairs={{0,1},{1,0},{2,3},{3,2},{4,5},{5,4},{6,7},{7,6},{8,9},{9,8},{10,11... | collective-permute-start | bytes 786440 | tf_op jit(solution)/shard_map/ppermute | solution.py:32
  73.7 1.7 %collective-permute-start.29 = (f32[64,1024]{1,0:T(8,128)S(1)}, f32[64,1024]{1,0:T(8,128)S(1)}, u32[]{:S(2)}, u32[]{:S(2)}) collective-permute-start(f32[64,1024]{1,0:T(8,128)S(1)} %get-tuple-element.24), channel_id=1, source_target_pairs={{0,1},{1,0},{2,3},{3,2},{4,5},{5,4},{6,7},{7,6},{8,9},{9,8},{10,11... | collective-permute-start | bytes 786440 | tf_op jit(solution)/shard_map/ppermute | solution.py:32
